TPU v7x, 32 devices: a whole 2x2x4 slice. The times are simulated.
32 devices in a mesh: dp: 8 (over y, x, core), fsdp: 4 (over z).
Axes of the slice: x: 2, y: 2, z: 4, core: 2. Of those that a mesh axis runs over, the one named last changes fastest.
Arguments:
- patches: bfloat16 [16384, 1024], P(('dp', 'fsdp')), may hold values from -6 to 6
- cotangent: bfloat16 [16384, 1024], P(('dp', 'fsdp')), may hold values from -6 to 6
- ln1_gain: bfloat16 [1024], P('fsdp'), may hold values from 0.5 to 1.5
- ln1_bias: bfloat16 [1024], P('fsdp'), may hold values from -1.75 to 1.75
- w_qkv: bfloat16 [1024, 3072], P('fsdp'), may hold values from -0.1875 to 0.1875
- w_out: bfloat16 [1024, 1024], P('fsdp'), may hold values from -0.5 to 0.5
- ln2_gain: bfloat16 [1024], P('fsdp'), may hold values from 0.5 to 1.5
- ln2_bias: bfloat16 [1024], P('fsdp'), may hold values from -1.75 to 1.75
- w_fc1: bfloat16 [1024, 4096], P('fsdp'), may hold values from -0.1875 to 0.1875
- fc1_bias: bfloat16 [4096], P('fsdp'), may hold values from -3 to 3
- w_fc2: bfloat16 [4096, 1024], P('fsdp'), may hold values from -0.09375 to 0.09375
- pos_table: bfloat16 [50, 1024], P(None, 'fsdp'), may hold values from -3 to 3
- pos_index: int32 [145, 4], replicated, may hold values from 0 to 49, as said below
- pos_weight: float32 [145, 4], replicated, may hold values from 0.1 to 0.6
Outputs:
- block_out: bfloat16 [16384, 1024], P(('dp', 'fsdp'))
- input_grad: bfloat16 [16384, 1024], P(('dp', 'fsdp'))
- ln1_gain_grad: float32 [1024], P('fsdp')
- ln1_bias_grad: float32 [1024], P('fsdp')
- qkv_grad: float32 [1024, 3072], P('fsdp')
- out_proj_grad: float32 [1024, 1024], P('fsdp')
- ln2_gain_grad: float32 [1024], P('fsdp')
- ln2_bias_grad: float32 [1024], P('fsdp')
- fc1_grad: float32 [1024, 4096], P('fsdp')
- fc1_bias_grad: float32 [4096], P('fsdp')
- fc2_grad: float32 [4096, 1024], P('fsdp')
- table_grad: float32 [50, 1024], P(None, 'fsdp')
Inputs may be any that keep to these rules, and one draw needn't show every extreme that they name: `pos_index`: row 0 names row 0 four times; every other row names rows 1 + 7i + j, 2 + 7i + j, 8 + 7i + j, 9 + 7i + j for some i, j in 0 to 5.
All inputs are finite; a program needn't handle non-finite values.
Results may differ from a plain program's by a relative error of at most 0.018.
Values may be sent and summed in bfloat16 or wider, within the bound.
No kernel may reach another device: no remote copies, remote signals or barrier semaphores. Data moves between devices by JAX's collectives and lax.ppermute only.
A program may use at most 192 MiB of HBM per device.

v0:
```python
import jax
import jax.numpy as jnp
from jax import lax
from jax.sharding import PartitionSpec as P

HEADS = 16
HDIM = 64
POS = 50
HIGH_LEN = 145


highest = lax.Precision.HIGHEST


def layer_norm(hidden, gain, shift):
    centre = hidden - jnp.mean(hidden, axis=-1, keepdims=True)
    spread = jnp.mean(centre * centre, axis=-1, keepdims=True)
    return centre * lax.rsqrt(spread + 1e-06) * gain + shift


def place_rows(rows, low_flag, pos_index, pos_weight):
    offsets = jnp.arange(rows, dtype=jnp.int32)
    table_ids = jnp.arange(POS, dtype=jnp.int32)
    high_ids = jnp.arange(HIGH_LEN, dtype=jnp.int32)
    picks = (pos_index[:, :, None] == table_ids[None, None, :]).astype(jnp.float32)
    interp = jnp.sum(pos_weight[:, :, None] * picks, axis=1)
    low_valid = offsets < rows // POS * POS
    high_valid = offsets < rows // HIGH_LEN * HIGH_LEN
    low_place = (((offsets % POS)[:, None] == table_ids[None, :]) & low_valid[:, None]).astype(
        jnp.float32
    )
    high_pick = (((offsets % HIGH_LEN)[:, None] == high_ids[None, :]) & high_valid[:, None]).astype(
        jnp.float32
    )
    high_place = jnp.dot(high_pick, interp, precision=highest)
    place = jnp.where(low_flag, low_place, high_place)
    valid = jnp.where(low_flag, low_valid, high_valid)
    segment = jnp.where(
        low_flag,
        jnp.where(low_valid, offsets // POS, -1),
        jnp.where(high_valid, offsets // HIGH_LEN, -1),
    )
    return (place, valid, segment[:, None] == segment[None, :])


def split_pairs(block):
    return block.reshape(block.shape[0], HEADS // 2, 2, HDIM).transpose(1, 0, 2, 3)


def join_pairs(block):
    return block.transpose(1, 0, 2, 3).reshape(block.shape[1], HEADS * HDIM)


def masked_scores(query_pair, key_pair, mask):
    scores = jnp.einsum(
        "qhd,khd->hqk", query_pair, key_pair, preferred_element_type=jnp.float32
    ) * HDIM ** (-0.5)
    return jnp.where(mask[None], scores, -1e30)


def forward(patches, params, place, mask):
    gain_one, bias_one, w_qkv, w_out, gain_two, bias_two, w_fc1, fc1_bias, w_fc2, pos_table = params
    width = w_out.shape[0]
    hidden_in = patches.astype(jnp.float32) + jnp.dot(
        place, pos_table.astype(jnp.float32), precision=highest
    )
    normed_one = layer_norm(
        hidden_in, gain_one.astype(jnp.float32), bias_one.astype(jnp.float32)
    ).astype(jnp.bfloat16)
    projected = jnp.dot(normed_one, w_qkv, preferred_element_type=jnp.float32).astype(jnp.bfloat16)
    queries = split_pairs(projected[:, :width])
    keys = split_pairs(projected[:, width : 2 * width])
    values = split_pairs(projected[:, 2 * width :])

    def attend(items):
        query_pair, key_pair, value_pair = items
        scores = masked_scores(query_pair, key_pair, mask)
        peak = jnp.max(scores, axis=-1, keepdims=True)
        expo = jnp.exp(scores - peak)
        total = jnp.sum(expo, axis=-1, keepdims=True)
        probs = (expo / total).astype(jnp.bfloat16)
        mixed = jnp.einsum("hqk,khd->qhd", probs, value_pair, preferred_element_type=jnp.float32)
        return (mixed.astype(jnp.bfloat16), (peak + jnp.log(total))[..., 0])

    attended, log_norm = lax.map(attend, (queries, keys, values))
    attn_rows = join_pairs(attended)
    hidden_mid = hidden_in + jnp.dot(attn_rows, w_out, preferred_element_type=jnp.float32)
    normed_two = layer_norm(
        hidden_mid, gain_two.astype(jnp.float32), bias_two.astype(jnp.float32)
    ).astype(jnp.bfloat16)
    pre_act = jnp.dot(normed_two, w_fc1, preferred_element_type=jnp.float32) + fc1_bias.astype(
        jnp.float32
    )
    activated = jax.nn.gelu(pre_act, approximate=False).astype(jnp.bfloat16)
    branch_out = jnp.dot(activated, w_fc2, preferred_element_type=jnp.float32)
    return (
        hidden_in,
        normed_one,
        projected,
        log_norm,
        attn_rows,
        hidden_mid,
        normed_two,
        pre_act,
        activated,
        branch_out,
    )


def backward(kept, params, place, mask, grad_out):
    gain_one, bias_one, w_qkv, w_out, gain_two, bias_two, w_fc1, fc1_bias, w_fc2, pos_table = params
    (
        hidden_in,
        normed_one,
        projected,
        log_norm,
        attn_rows,
        hidden_mid,
        normed_two,
        pre_act,
        activated,
        branch_out,
    ) = kept
    width = w_out.shape[0]
    grad_fc2 = jnp.einsum("rf,rd->fd", activated, grad_out, preferred_element_type=jnp.float32)
    grad_act = jnp.einsum("rd,fd->rf", grad_out, w_fc2, preferred_element_type=jnp.float32)
    _, pull_gelu = jax.vjp(lambda inner: jax.nn.gelu(inner, approximate=False), pre_act)
    grad_pre = pull_gelu(grad_act)[0].astype(jnp.bfloat16)
    grad_fc1_bias = jnp.sum(grad_pre.astype(jnp.float32), axis=0)
    grad_fc1 = jnp.einsum("rd,rf->df", normed_two, grad_pre, preferred_element_type=jnp.float32)
    grad_norm_two = jnp.einsum("rf,df->rd", grad_pre, w_fc1, preferred_element_type=jnp.float32)
    _, pull_two = jax.vjp(
        layer_norm, hidden_mid, gain_two.astype(jnp.float32), bias_two.astype(jnp.float32)
    )
    back_mid, grad_gain_two, grad_bias_two = pull_two(grad_norm_two)
    grad_mid = grad_out.astype(jnp.float32) + back_mid
    grad_branch = grad_mid.astype(jnp.bfloat16)
    grad_wout = jnp.einsum("rd,re->de", attn_rows, grad_branch, preferred_element_type=jnp.float32)
    grad_attn = jnp.einsum(
        "re,de->rd", grad_branch, w_out, preferred_element_type=jnp.float32
    ).astype(jnp.bfloat16)
    queries = split_pairs(projected[:, :width])
    keys = split_pairs(projected[:, width : 2 * width])
    values = split_pairs(projected[:, 2 * width :])
    grad_pairs = split_pairs(grad_attn)

    def attend_back(items):
        query_pair, key_pair, value_pair, grad_pair, log_pair = items
        scores = masked_scores(query_pair, key_pair, mask)
        probs = jnp.exp(scores - log_pair[..., None])
        probs_low = probs.astype(jnp.bfloat16)
        grad_probs = jnp.einsum(
            "qhd,khd->hqk", grad_pair, value_pair, preferred_element_type=jnp.float32
        )
        centre = jnp.sum(probs * grad_probs, axis=-1, keepdims=True)
        grad_scores = (probs * (grad_probs - centre)).astype(jnp.bfloat16)
        grad_query = jnp.einsum(
            "hqk,khd->qhd", grad_scores, key_pair, preferred_element_type=jnp.float32
        ) * HDIM ** (-0.5)
        grad_key = jnp.einsum(
            "hqk,qhd->khd", grad_scores, query_pair, preferred_element_type=jnp.float32
        ) * HDIM ** (-0.5)
        grad_value = jnp.einsum(
            "hqk,qhd->khd", probs_low, grad_pair, preferred_element_type=jnp.float32
        )
        return (grad_query, grad_key, grad_value)

    grad_query, grad_key, grad_value = lax.map(
        attend_back, (queries, keys, values, grad_pairs, log_norm)
    )
    grad_proj = jnp.concatenate(
        [join_pairs(grad_query), join_pairs(grad_key), join_pairs(grad_value)], axis=1
    ).astype(jnp.bfloat16)
    grad_qkv = jnp.einsum("rd,re->de", normed_one, grad_proj, preferred_element_type=jnp.float32)
    grad_norm_one = jnp.einsum("re,de->rd", grad_proj, w_qkv, preferred_element_type=jnp.float32)
    _, pull_one = jax.vjp(
        layer_norm, hidden_in, gain_one.astype(jnp.float32), bias_one.astype(jnp.float32)
    )
    back_in, grad_gain_one, grad_bias_one = pull_one(grad_norm_one)
    grad_in = grad_mid + back_in
    grad_table = jnp.dot(place.T, grad_in, precision=highest)
    grads = (
        grad_gain_one,
        grad_bias_one,
        grad_qkv,
        grad_wout,
        grad_gain_two,
        grad_bias_two,
        grad_fc1,
        grad_fc1_bias,
        grad_fc2,
        grad_table,
    )
    return (grad_in.astype(jnp.bfloat16), grads)


def per_device(
    patches,
    cotangent,
    ln1_gain,
    ln1_bias,
    w_qkv,
    w_out,
    ln2_gain,
    ln2_bias,
    w_fc1,
    fc1_bias,
    w_fc2,
    pos_table,
    pos_index,
    pos_weight,
):
    n_data = lax.axis_size("dp")
    low_flag = lax.axis_index("dp") < n_data * 7 // 16
    rows = patches.shape[0]
    place, valid, mask = place_rows(rows, low_flag, pos_index, pos_weight)
    gathered = (
        lax.all_gather(ln1_gain, "fsdp", axis=0, tiled=True),
        lax.all_gather(ln1_bias, "fsdp", axis=0, tiled=True),
        lax.all_gather(w_qkv, "fsdp", axis=0, tiled=True),
        lax.all_gather(w_out, "fsdp", axis=0, tiled=True),
        lax.all_gather(ln2_gain, "fsdp", axis=0, tiled=True),
        lax.all_gather(ln2_bias, "fsdp", axis=0, tiled=True),
        lax.all_gather(w_fc1, "fsdp", axis=0, tiled=True),
        lax.all_gather(fc1_bias, "fsdp", axis=0, tiled=True),
        lax.all_gather(w_fc2, "fsdp", axis=0, tiled=True),
        lax.all_gather(pos_table, "fsdp", axis=1, tiled=True),
    )
    kept = forward(patches, gathered, place, mask)
    block_out = jnp.where(valid[:, None], kept[5] + kept[9], 0.0).astype(jnp.bfloat16)
    regathered = (
        lax.all_gather(ln1_gain, "fsdp", axis=0, tiled=True),
        lax.all_gather(ln1_bias, "fsdp", axis=0, tiled=True),
        lax.all_gather(w_qkv, "fsdp", axis=0, tiled=True),
        lax.all_gather(w_out, "fsdp", axis=0, tiled=True),
        lax.all_gather(ln2_gain, "fsdp", axis=0, tiled=True),
        lax.all_gather(ln2_bias, "fsdp", axis=0, tiled=True),
        lax.all_gather(w_fc1, "fsdp", axis=0, tiled=True),
        lax.all_gather(fc1_bias, "fsdp", axis=0, tiled=True),
        lax.all_gather(w_fc2, "fsdp", axis=0, tiled=True),
        lax.all_gather(pos_table, "fsdp", axis=1, tiled=True),
    )
    rekept = forward(patches, regathered, place, mask)
    grad_out = jnp.where(valid[:, None], cotangent, jnp.zeros_like(cotangent))
    input_grad, grads = backward(rekept, regathered, place, mask, grad_out)
    shares = (
        lax.psum_scatter(
            grads[0].astype(jnp.bfloat16), "fsdp", scatter_dimension=0, tiled=True
        ).astype(jnp.float32),
        lax.psum_scatter(
            grads[1].astype(jnp.bfloat16), "fsdp", scatter_dimension=0, tiled=True
        ).astype(jnp.float32),
        lax.psum_scatter(
            grads[2].astype(jnp.bfloat16), "fsdp", scatter_dimension=0, tiled=True
        ).astype(jnp.float32),
        lax.psum_scatter(
            grads[3].astype(jnp.bfloat16), "fsdp", scatter_dimension=0, tiled=True
        ).astype(jnp.float32),
        lax.psum_scatter(
            grads[4].astype(jnp.bfloat16), "fsdp", scatter_dimension=0, tiled=True
        ).astype(jnp.float32),
        lax.psum_scatter(
            grads[5].astype(jnp.bfloat16), "fsdp", scatter_dimension=0, tiled=True
        ).astype(jnp.float32),
        lax.psum_scatter(
            grads[6].astype(jnp.bfloat16), "fsdp", scatter_dimension=0, tiled=True
        ).astype(jnp.float32),
        lax.psum_scatter(
            grads[7].astype(jnp.bfloat16), "fsdp", scatter_dimension=0, tiled=True
        ).astype(jnp.float32),
        lax.psum_scatter(
            grads[8].astype(jnp.bfloat16), "fsdp", scatter_dimension=0, tiled=True
        ).astype(jnp.float32),
        lax.psum_scatter(
            grads[9].astype(jnp.bfloat16), "fsdp", scatter_dimension=1, tiled=True
        ).astype(jnp.float32),
    )
    totals = (
        lax.psum(shares[0].astype(jnp.bfloat16), "dp").astype(jnp.float32),
        lax.psum(shares[1].astype(jnp.bfloat16), "dp").astype(jnp.float32),
        lax.psum(shares[2].astype(jnp.bfloat16), "dp").astype(jnp.float32),
        lax.psum(shares[3].astype(jnp.bfloat16), "dp").astype(jnp.float32),
        lax.psum(shares[4].astype(jnp.bfloat16), "dp").astype(jnp.float32),
        lax.psum(shares[5].astype(jnp.bfloat16), "dp").astype(jnp.float32),
        lax.psum(shares[6].astype(jnp.bfloat16), "dp").astype(jnp.float32),
        lax.psum(shares[7].astype(jnp.bfloat16), "dp").astype(jnp.float32),
        lax.psum(shares[8].astype(jnp.bfloat16), "dp").astype(jnp.float32),
        lax.psum(shares[9].astype(jnp.bfloat16), "dp").astype(jnp.float32),
    )
    return (
        block_out,
        input_grad,
        totals[0],
        totals[1],
        totals[2],
        totals[3],
        totals[4],
        totals[5],
        totals[6],
        totals[7],
        totals[8],
        totals[9],
    )


def solution(mesh):
    return jax.shard_map(
        per_device,
        mesh=mesh,
        in_specs=(
            P(("dp", "fsdp"), None),
            P(("dp", "fsdp"), None),
            P("fsdp"),
            P("fsdp"),
            P("fsdp", None),
            P("fsdp", None),
            P("fsdp"),
            P("fsdp"),
            P("fsdp", None),
            P("fsdp"),
            P("fsdp", None),
            P(None, "fsdp"),
            P(),
            P(),
        ),
        out_specs=(
            P(("dp", "fsdp"), None),
            P(("dp", "fsdp"), None),
            P("fsdp"),
            P("fsdp"),
            P("fsdp", None),
            P("fsdp", None),
            P("fsdp"),
            P("fsdp"),
            P("fsdp", None),
            P("fsdp"),
            P("fsdp", None),
            P(None, "fsdp"),
        ),
        check_vma=False,
    )
```

profile of v0, /device:TPU:0, one launch (start us, length us, event | category | flops | bytes accessed | tf_op | source)
XLA Modules:
  0.0 1141.8 jit_solution(14354497924452631395)
XLA Ops:
  10.2 15.1 %all_gather.40 = bf16[50,1024]{1,0:T(8,128)(2,1)S(1)} all-gather(bf16[50,256]{1,0:T(8,128)(2,1)S(1)} %copy-done.16), channel_id=1, replica_groups=mesh['dp'=8,'fsdp'=4] {'fsdp'}, dimensions={1}, use_global_device_ids=true | all-gather | bytes 128000 | tf_op jit(solution)/shard_map/all_gather | solution.py:227
  27.7 12.1 %all-gather = bf16[4,1,256]{2,1,0:T(2,128)(2,1)S(1)} all-gather(bf16[1,1,256]{2,1,0:T(2,128)(2,1)S(1)} %reshape.257), channel_id=1, replica_groups=mesh['dp'=8,'fsdp'=4] {'fsdp'}, dimensions={0}, use_global_device_ids=true | all-gather | bytes 2560 | tf_op jit(solution)/shard_map/all_gather | solution.py:218
  39.8 8.5 all-gather.1
  48.3 14.1 %all-gather.2 = bf16[4,1,256]{2,1,0:T(2,128)(2,1)S(1)} all-gather(bf16[1,1,256]{2,1,0:T(2,128)(2,1)S(1)} %reshape.261), channel_id=1, replica_groups=mesh['dp'=8,'fsdp'=4] {'fsdp'}, dimensions={0}, use_global_device_ids=true | all-gather | bytes 2560 | tf_op jit(solution)/shard_map/all_gather | solution.py:222
  62.4 17.2 %all_gather.48 = bf16[4096]{0:T(1024)(128)(2,1)S(1)} all-gather(bf16[1024]{0:T(1024)(128)(2,1)S(1)} %copy-done.22), channel_id=1, replica_groups=mesh['dp'=8,'fsdp'=4] {'fsdp'}, dimensions={0}, use_global_device_ids=true | all-gather | bytes 10240 | tf_op jit(solution)/shard_map/all_gather | solution.py:225
  79.7 8.2 all-gather.3
  87.9 40.0 %all-gather.9.cloned.1.call-done = bf16[1024,3072]{1,0:T(8,128)(2,1)} async-done(((bf16[256,3072]{1,0:T(8,128)(2,1)}), bf16[1024,3072]{1,0:T(8,128)(2,1)}) %all-gather.9.cloned.1.call-update) | async-done | bytes 6291472 | tf_op jit(solution)/shard_map/all_gather | solution.py:220
  128.0 6.6 convolution_convert_fusion.5
  139.1 2.3 copy.66
  142.4 36.8 %while.40 = (s32[]{:T(128)}, bf16[8,512,2,64]{1,3,2,0:T(8,128)(2,1)}, f32[8,2,512]{2,1,0:T(2,128)S(1)}, bf16[8,512,2,64]{1,3,2,0:T(8,128)(2,1)}, bf16[8,512,2,64...) while((s32[]{:T(128)}, ...), condition=%wide.region_12.13_spmd.clone, body=%wide.region_9.12_spmd.clone.sunk | while | flops 140835840 | bytes 7901273 | solution.py:85
  144.7 2.3 fusion.277
  149.3 2.3 fusion.277
  153.9 2.3 fusion.277
  158.5 2.3 fusion.277
  163.1 2.3 fusion.277
  167.7 2.3 fusion.277
  172.3 2.3 fusion.277
  176.9 2.3 fusion.277
  179.2 4.0 fusion.218
  184.9 138.7 %all-gather.13.cloned.1.call-done = bf16[1024,4096]{1,0:T(8,128)(2,1)} async-done(((bf16[256,4096]{1,0:T(8,128)(2,1)}), bf16[1024,4096]{1,0:T(8,128)(2,1)}) %all-gather.13.cloned.1.call-update) | async-done | bytes 8388624 | tf_op jit(solution)/shard_map/all_gather | solution.py:224
  323.6 28.0 %fusion.98 = (f32[512,4096]{1,0:T(8,128)}, f32[512,4096]{1,0:T(8,128)}) fusion(f32[4096]{0:T(1024)S(1)} %convert_element_type.184, bf16[1024,4096]{1,0:T(8,128)(2,1)} %all-gather.13.cloned.1.call-done, f32[512,1024]{1,0:T(8,128)} %copy-done.2, f32[512]{0:T(512)S(1)} %fusion.171, f32[512]{0:T(512)S(1)} %broadcast_multiply_fusion, f32[1024]{0:T(1024)S(1)} %bitcast.216, ...), kind=kOutput, calls=%fused_computation.96 | convolution fusion | flops 4429709312 | bytes 27291648 | tf_op jit(solution)/shard_map/dot_general | solution.py:91
  351.6 121.2 %all-gather.15.cloned.1.call-done = bf16[4096,1024]{1,0:T(8,128)(2,1)} async-done(((bf16[1024,1024]{1,0:T(8,128)(2,1)}), bf16[4096,1024]{1,0:T(8,128)(2,1)}) %all-gather.15.cloned.1.call-update) | async-done | bytes 8388624 | tf_op jit(solution)/shard_map/all_gather | solution.py:226
  472.8 15.7 %fusion.219 = (bf16[4096]{0:T(1024)(128)(2,1)}, bf16[512,4096]{1,0:T(8,128)(2,1)}) fusion(f32[512,4096]{1,0:T(8,128)} %get-tuple-element.283, bf16[4096,1024]{1,0:T(8,128)(2,1)} %all-gather.15.cloned.1.call-done, bf16[512,1024]{1,0:T(8,128)(2,1)S(1)} %copy-done.5, pred[512]{0:T(512)(128)(4,1)S(1)} %broadcast_select_fusion.1, ...), kind=kOutput, calls=%fused_computation.279 | convolution fusion | flops 4329041920 | bytes 30433792 | tf_op jit(solution)/shard_map/rd,fd->rf/dot_general | solution.py:126
  488.6 9.3 multiply_reduce_fusion.1
  501.3 3.8 convolution_convert_fusion.6
  505.2 4.2 convolution_convert_fusion.7
  511.1 72.4 %while.41 = (s32[]{:T(128)}, bf16[8,512,2,64]{1,3,2,0:T(8,128)(2,1)}, bf16[8,512,2,64]{1,3,2,0:T(8,128)(2,1)}, bf16[8,512,2,64]{1,3,2,0:T(8,128)(2,1)}, bf16[8,5...) while((s32[]{:T(128)}, ...), condition=%wide.region_19.20_spmd.clone, body=%wide.region_17.19_spmd.clone.sunk | while | flops 340655104 | bytes 17984624 | solution.py:168
  515.2 2.0 fusion.288
  524.2 2.0 fusion.288
  533.3 2.0 fusion.288
  542.3 2.0 fusion.288
  551.4 2.0 fusion.288
  560.4 2.0 fusion.288
  569.5 2.0 fusion.288
  578.5 2.0 fusion.288
  583.5 8.3 convolution_convert_fusion.4
  593.0 15.1 %convolution_convert_fusion.2 = bf16[4096,1024]{1,0:T(8,128)(2,1)} fusion(f32[512,4096]{1,0:T(8,128)} %get-tuple-element.283, f32[512,4096]{1,0:T(8,128)} %get-tuple-element.284, f32[4096]{0:T(1024)S(1)} %convert_element_type.184, bf16[512,1024]{1,0:T(8,128)(2,1)S(1)} %copy-done.6, pred[512]{0:T(512)(128)(4,1)S(1)} %broadcast_select_fusion.1), kind=kOutput, calls=%fused_computation.127 | convolution fusion | flops 4308074496 | bytes 26231296 | tf_op jit(solution)/shard_map/rf,rd->fd/dot_general | solution.py:125
  608.2 10.8 convolution_convert_fusion.3
  622.6 40.7 %while.39 = (s32[]{:T(128)}, bf16[8,512,2,64]{1,3,2,0:T(8,128)(2,1)}, bf16[8,512,2,64]{1,3,2,0:T(8,128)(2,1)}, bf16[8,512,2,64]{1,3,2,0:T(8,128)(2,1)}, bf16[8,5...) while((s32[]{:T(128)}, bf16[8,512,2,64]{1,3,2,0:T(8,128)(2,1)}, ...), condition=%wide.region_6.7_spmd.clone, body=%wide.region_3.6_spmd.clone.sunk | while | flops 206374912 | bytes 1586253 | solution.py:85
  624.8 2.9 fusion.273
  629.9 2.9 fusion.273
  635.0 2.9 fusion.273
  638.1 2.0 fusion.272
  640.0 2.9 fusion.273
  643.2 2.0 fusion.272
  645.1 2.9 fusion.273
  648.2 2.0 fusion.272
  650.2 2.9 fusion.273
  653.3 2.0 fusion.272
  655.3 2.9 fusion.273
  660.4 2.9 fusion.273
  663.3 3.5 fusion.217
  668.4 7.3 multiply_reduce_fusion.2
  678.9 2.0 convolution_convert_fusion.8
  681.0 19.9 %reduce-scatter.6.cloned.1.call-done = bf16[256,3072]{1,0:T(8,128)(2,1)} async-done(((bf16[1024,3072]{1,0:T(8,128)(2,1)}), bf16[256,3072]{1,0:T(8,128)(2,1)}) %reduce-scatter.6.cloned.1.call-update) | async-done | bytes 1572880 | tf_op jit(solution)/shard_map/reduce_scatter | solution.py:253
  700.9 147.5 %reduce-scatter.12.cloned.1.call-done = bf16[1024,1024]{1,0:T(8,128)(2,1)} async-done(((bf16[4096,1024]{1,0:T(8,128)(2,1)}), bf16[1024,1024]{1,0:T(8,128)(2,1)}) %reduce-scatter.12.cloned.1.call-update) | async-done | bytes 2097168 | tf_op jit(solution)/shard_map/reduce_scatter | solution.py:271
  848.5 147.6 %reduce-scatter.10.cloned.1.call-done = bf16[256,4096]{1,0:T(8,128)(2,1)} async-done(((bf16[1024,4096]{1,0:T(8,128)(2,1)}), bf16[256,4096]{1,0:T(8,128)(2,1)}) %reduce-scatter.10.cloned.1.call-update) | async-done | bytes 2097168 | tf_op jit(solution)/shard_map/reduce_scatter | solution.py:265
  996.1 32.4 %select_convert_fusion = bf16[512,1024]{1,0:T(8,128)(2,1)} fusion(f32[512,1024]{1,0:T(8,128)S(1)} %copy-done.9, bf16[4096,1024]{1,0:T(8,128)(2,1)} %all-gather.15.cloned.1.call-done, bf16[1024,4096]{1,0:T(8,128)(2,1)} %all-gather.13.cloned.1.call-done, f32[4096]{0:T(1024)S(1)} %convert_element_type.184, f32[1024]{0:T(1024)S(1)} %bitcast.218, ...), kind=kOutput, calls=%fused_computation.176 | convolution fusion | flops 8732540928 | bytes 19952128 | tf_op jit(solution)/shard_map/dot_general | solution.py:95
  1028.6 18.1 %all-reduce.7 = (bf16[1024]{0:T(1024)(128)(2,1)S(1)}, bf16[1024]{0:T(1024)(128)(2,1)S(1)}, bf16[1024]{0:T(1024)(128)(2,1)S(1)}, bf16[1024]{0:T(1024)(128)(2,1)S(1)}, bf16[4096]{0:T(1024)(128)(2,1)S(1)}) all-reduce(bf16[1024]{0:T(1024)(128)(2,1)S(1)} %get-tuple-element.199, ...), channel_id=2, replica_groups=mesh['dp'=8,'fsdp'=4] {'fsdp'}, use_global_device_ids=true, to_apply=%region_23.24.clone | all-reduce | flops 8192 | bytes 32768
  1047.0 23.9 %all-reduce.5 = (bf16[256]{0:T(256)(128)(2,1)S(1)}, bf16[256]{0:T(256)(128)(2,1)S(1)}, bf16[256]{0:T(256)(128)(2,1)S(1)}, bf16[256]{0:T(256)(128)(2,1)S(1)}, bf1...) all-reduce(bf16[256]{0:T(256)(128)(2,1)S(1)} %dynamic-slice.1, ...), channel_id=1, replica_groups=mesh['dp'=8,'fsdp'=4] {'dp'}, use_global_device_ids=true, to_apply=%region_24.25 | all-reduce | flops 14848 | bytes 59392 | tf_op jit(solution)/shard_map/psum | solution.py:279
  1074.4 50.6 %all-reduce.10.cloned.1.call-done = (bf16[256,3072]{1,0:T(8,128)(2,1)}, bf16[256,1024]{1,0:T(8,128)(2,1)}, bf16[256,4096]{1,0:T(8,128)(2,1)}, bf16[1024,1024]{1,0:T(8,128)(2,1)}) async-done(((bf16[256,3072]{1,0:T(8,128)(2,1)}, bf16[256,1024]{1,0:T(8,128)(2,1)}, bf16[256,4096]{1,0:T(8,128)(2,1)}, bf16[1024,1024]{1,0:T(8,128)(2,1)}), (bf16[256,3072]{1,0:T(8,128)(2,1)}, bf16[256,1024]{1,0:T(8,128)(2,1)}, ...) | async-done | bytes 6291472 | tf_op jit(solution)/shard_map/psum | solution.py:281
  1124.9 4.2 convert_element_type.206
  1129.2 2.5 convert_element_type.210
  1131.7 2.0 convert_element_type.198
  (243 shorter events, 114.4 us)
Async XLA Ops:
  7.2 3.0 copy-start.16
  7.2 18.2 %copy-start.21 = (s32[145,4]{0,1:T(4,128)S(1)}, s32[145,4]{0,1:T(4,128)}, u32[]{:S(2)}) copy-start(s32[145,4]{0,1:T(4,128)} %param.32) | copy-start | bytes 6964
  7.2 18.1 %copy-start.20 = (f32[145,4]{0,1:T(4,128)S(1)}, f32[145,4]{0,1:T(4,128)}, u32[]{:S(2)}) copy-start(f32[145,4]{0,1:T(4,128)} %param.33) | copy-start | bytes 6964
  7.2 18.8 %copy-start.11 = (bf16[512,1024]{1,0:T(8,128)(2,1)S(1)}, bf16[512,1024]{1,0:T(8,128)(2,1)}, u32[]{:S(2)}) copy-start(bf16[512,1024]{1,0:T(8,128)(2,1)} %param.20) | copy-start | bytes 3145732
  7.2 120.7 %all-gather.9.cloned.1.call-start = ((), (), s32[]{:S(2)}) async-start(), calls=%async_computation.5 | async-start | bytes 7864320 | tf_op jit(solution)/shard_map/all_gather | solution.py:220
  8.0 171.3 %all-gather.11.cloned.1.call-start = ((), (), s32[]{:S(2)}) async-start(), calls=%async_computation.6 | async-start | bytes 2621440 | tf_op jit(solution)/shard_map/all_gather | solution.py:221
  8.7 314.9 %all-gather.13.cloned.1.call-start = ((), (), s32[]{:S(2)}) async-start(), calls=%async_computation.7 | async-start | bytes 10485760 | tf_op jit(solution)/shard_map/all_gather | solution.py:224
  9.4 18.2 %copy-start.27 = (bf16[256]{0:T(256)(128)(2,1)S(1)}, bf16[256]{0:T(256)(128)(2,1)}, u32[]{:S(2)}) copy-start(bf16[256]{0:T(256)(128)(2,1)} %param.22) | copy-start | bytes 1540
  9.4 30.3 %copy-start.28 = (bf16[256]{0:T(256)(128)(2,1)S(1)}, bf16[256]{0:T(256)(128)(2,1)}, u32[]{:S(2)}) copy-start(bf16[256]{0:T(256)(128)(2,1)} %param.23) | copy-start | bytes 1540
  9.5 38.8 %copy-start.29 = (bf16[256]{0:T(256)(128)(2,1)S(1)}, bf16[256]{0:T(256)(128)(2,1)}, u32[]{:S(2)}) copy-start(bf16[256]{0:T(256)(128)(2,1)} %param.26) | copy-start | bytes 1540
  9.5 53.0 %copy-start.22 = (bf16[1024]{0:T(1024)(128)(2,1)S(1)}, bf16[1024]{0:T(1024)(128)(2,1)}, u32[]{:S(2)}) copy-start(bf16[1024]{0:T(1024)(128)(2,1)} %param.29) | copy-start | bytes 6148
  9.5 70.2 %copy-start.30 = (bf16[256]{0:T(256)(128)(2,1)S(1)}, bf16[256]{0:T(256)(128)(2,1)}, u32[]{:S(2)}) copy-start(bf16[256]{0:T(256)(128)(2,1)} %param.27) | copy-start | bytes 1540
  9.5 463.3 %all-gather.15.cloned.1.call-start = ((), (), s32[]{:S(2)}) async-start(), calls=%async_computation.8 | async-start | bytes 10485760 | tf_op jit(solution)/shard_map/all_gather | solution.py:226
  10.1 670.9 %reduce-scatter.8.cloned.1.call-start = ((), (), s32[]{:S(2)}) async-start(), calls=%async_computation.10 | async-start | bytes 2621440 | tf_op jit(solution)/shard_map/reduce_scatter | solution.py:256
  26.0 108.6 %copy-start.14 = (f32[512,50]{0,1:T(8,128)}, f32[512,50]{0,1:T(8,128)S(1)}, u32[]{:S(2)}) copy-start(f32[512,50]{0,1:T(8,128)S(1)} %convolution_select_fusion) | copy-start | bytes 307204
  27.6 34.8 %copy-start.17 = (f32[512]{0:T(512)}, f32[512]{0:T(512)S(1)}, u32[]{:S(2)}) copy-start(f32[512]{0:T(512)S(1)} %multiply_reduce_fusion.7) | copy-start | bytes 6148
  179.2 5.7 copy-start.4
  183.2 1.3 copy-start.2
  323.6 149.3 %copy-start.5 = (bf16[512,1024]{1,0:T(8,128)(2,1)S(1)}, bf16[512,1024]{1,0:T(8,128)(2,1)}, u32[]{:S(2)}) copy-start(bf16[512,1024]{1,0:T(8,128)(2,1)} %param.21) | copy-start | bytes 3145732
  472.8 15.7 %copy-start.3 = (f32[512,1024]{1,0:T(8,128)S(1)}, f32[512,1024]{1,0:T(8,128)}, u32[]{:S(2)}) copy-start(f32[512,1024]{1,0:T(8,128)} %copy-done.2) | copy-start | bytes 6291460
  498.6 1.3 copy-start
  500.3 1.0 copy-start.12
  505.1 195.8 %reduce-scatter.6.cloned.1.call-start = ((), (), s32[]{:S(2)}) async-start(), calls=%async_computation.9 | async-start | bytes 7864320 | tf_op jit(solution)/shard_map/reduce_scatter | solution.py:253
  591.8 1.2 copy-start.6
  591.8 256.6 %reduce-scatter.12.cloned.1.call-start = ((), (), s32[]{:S(2)}) async-start(), calls=%async_computation.12 | async-start | bytes 10485760 | tf_op jit(solution)/shard_map/reduce_scatter | solution.py:271
  608.1 388.0 %reduce-scatter.10.cloned.1.call-start = ((), (), s32[]{:S(2)}) async-start(), calls=%async_computation.11 | async-start | bytes 10485760 | tf_op jit(solution)/shard_map/reduce_scatter | solution.py:265
  619.0 0.7 copy-start.31
  619.0 428.0 %reduce-scatter.14.cloned.1.call-start = ((), (), s32[]{:S(2)}) async-start(), calls=%async_computation.13 | async-start | bytes 143360 | tf_op jit(solution)/shard_map/reduce_scatter | solution.py:274
  663.3 5.2 copy-start.25
  663.3 5.2 copy-start.26
  666.8 1.3 copy-start.8
  668.4 7.3 copy-start.18
  675.7 1.6 copy-start.1
  677.3 1.5 copy-start.15
  678.9 317.2 %copy-start.9 = (f32[512,1024]{1,0:T(8,128)S(1)}, f32[512,1024]{1,0:T(8,128)}, u32[]{:S(2)}) copy-start(f32[512,1024]{1,0:T(8,128)} %copy-done.8) | copy-start | bytes 6291460
  680.9 444.0 %all-reduce.10.cloned.1.call-start = ((), (), s32[]{:S(2)}) async-start(), calls=%async_computation.14 | async-start | bytes 12582912 | tf_op jit(solution)/shard_map/psum | solution.py:281
  996.1 32.5 %copy-start.19 = (bf16[4096]{0:T(1024)(128)(2,1)S(1)}, bf16[4096]{0:T(1024)(128)(2,1)}, u32[]{:S(2)}) copy-start(bf16[4096]{0:T(1024)(128)(2,1)} %get-tuple-element.287) | copy-start | bytes 24580
  996.1 32.5 %copy-start.23 = (bf16[1024]{0:T(1024)(128)(2,1)S(1)}, bf16[1024]{0:T(1024)(128)(2,1)}, u32[]{:S(2)}) copy-start(bf16[1024]{0:T(1024)(128)(2,1)} %get-tuple-element.197) | copy-start | bytes 6148
  996.1 32.5 %copy-start.24 = (bf16[1024]{0:T(1024)(128)(2,1)S(1)}, bf16[1024]{0:T(1024)(128)(2,1)}, u32[]{:S(2)}) copy-start(bf16[1024]{0:T(1024)(128)(2,1)} %get-tuple-element.201) | copy-start | bytes 6148
  1124.9 4.3 copy-start.7
  1129.2 2.5 copy-start.10
  1129.2 4.5 copy-start.13
Sparse Core Ops, SparseCore 0:
  9.6 118.3 all-gather.8
  129.5 43.9 all-gather.10
  175.0 148.4 all-gather.12
  325.0 147.7 all-gather.14
  505.3 41.7 reduce-scatter.7
  591.9 108.9 reduce-scatter.5
  703.3 145.1 reduce-scatter.11
  850.8 145.2 reduce-scatter.9
  998.9 20.0 reduce-scatter.13
  1022.4 102.4 all-reduce.9
where the time goes:
time: 1150 us; the launch traced here: 1140 us
  waiting for transfers between devices  668 us (58%)
  matrix products  288 us (25%)
  blocking collectives  117 us (10%)
  other arithmetic  31.7 us (3%)
  local copies, waits for them, and re-layouts  18.6 us (2%)
  between operations  16.1 us (1%)
    reduce_scatter x1, waiting for transfers between devices, per_device(): lax.psum_scatter(grads[6].astype(jnp.bfloat16), 'fsdp', scatter_dimension...  148 us
    reduce_scatter x1, waiting for transfers between devices, per_device(): lax.psum_scatter(grads[8].astype(jnp.bfloat16), 'fsdp', scatter_dimension...  148 us
    all_gather x1, waiting for transfers between devices, per_device(): lax.all_gather(w_fc1, 'fsdp', axis=0, tiled=True)  139 us
    all_gather x1, waiting for transfers between devices, per_device(): lax.all_gather(w_fc2, 'fsdp', axis=0, tiled=True)  121 us
    psum x1, waiting for transfers between devices, per_device(): lax.psum(shares[2].astype(jnp.bfloat16), 'dp').astype(jnp.float32)  50.6 us
    dot_general x16, matrix products, attend(): jnp.einsum('hqk,khd->qhd', probs, value_pair, preferred_element_type=jnp....  41.9 us
    all_gather x1, waiting for transfers between devices, per_device(): lax.all_gather(w_qkv, 'fsdp', axis=0, tiled=True)  40 us
    dot_general x1, matrix products, forward(): branch_out = jnp.dot(activated, w_fc2, preferred_element_type=jnp.float32)  32.4 us
  transfers between devices with their start and end apart: 10, of which 7 were waited for; matrix products, arithmetic and copies ran while one was open for 26% of the time, Pallas kernels for 0%

commit v1 on v0

--- a/solution.py
+++ b/solution.py
@@ -194,6 +194,87 @@
     return (grad_in.astype(jnp.bfloat16), grads)
 
 
+def hop_bit(core, stage, bits):
+    return 1 + stage if core == 0 else bits - stage
+
+
+def hop_pairs(n_dp, stage):
+    bits = n_dp.bit_length() - 2
+    return [(i, i ^ (1 << hop_bit(i % 2, stage, bits))) for i in range(n_dp)]
+
+
+def swap_core(block, n_dp):
+    return lax.ppermute(block, "dp", [(i, i ^ 1) for i in range(n_dp)])
+
+
+def ahead(block, n_line, step):
+    return lax.ppermute(block, "fsdp", [(i, (i + step) % n_line) for i in range(n_line)])
+
+
+def line_gather(unit, n_line):
+    if n_line <= 4:
+        return jnp.stack([ahead(unit, n_line, step) for step in range(1, n_line)])
+    every = lax.all_gather(unit, "fsdp", axis=0)
+    order = (lax.axis_index("fsdp") - jnp.arange(1, n_line)) % n_line
+    return jnp.take(every, order, axis=0)
+
+
+def spread(parts, n_dp):
+    for stage in range(n_dp.bit_length() - 2):
+        send = jnp.concatenate(parts) if len(parts) > 1 else parts[0]
+        parts = parts + [lax.ppermute(send, "dp", hop_pairs(n_dp, stage))]
+    return parts + [swap_core(jnp.concatenate(parts), n_dp)]
+
+
+def add_up(terms):
+    total = terms[0].astype(jnp.float32)
+    for term in terms[1:]:
+        total = total + term.astype(jnp.float32)
+    return total
+
+
+def reduce_units(away, keep, n_dp, n_line):
+    terms = [keep, swap_core(away, n_dp)]
+    half = keep.shape[0] // 2
+    for stage in range(n_dp.bit_length() - 2):
+        send = add_up([term[half:] for term in terms]).astype(jnp.bfloat16)
+        terms = [term[:half] for term in terms] + [lax.ppermute(send, "dp", hop_pairs(n_dp, stage))]
+        half //= 2
+    terms = [term[0] for term in terms]
+    if n_line <= 4:
+        arrived = [
+            ahead(add_up([term[step] for term in terms]).astype(jnp.bfloat16), n_line, step)
+            for step in range(1, n_line)
+        ]
+        total = add_up([term[0] for term in terms] + arrived)
+    else:
+        order = (jnp.arange(n_line) - lax.axis_index("fsdp")) % n_line
+        line = jnp.take(add_up(terms).astype(jnp.bfloat16), order, axis=0)
+        total = lax.psum_scatter(line, "fsdp", scatter_dimension=0)
+    return jnp.concatenate(spread([total.astype(jnp.bfloat16)[None]], n_dp))
+
+
+def place_of(n_dp, me, flip):
+    bits = n_dp.bit_length() - 2
+    core = me % 2
+    halves = []
+    for other in range(2):
+        place = jnp.arange(1 << bits, dtype=jnp.int32)
+        owner = jnp.full((1 << bits,), me ^ other, jnp.int32)
+        for stage in range(bits):
+            at = bits - 1 - stage if flip else stage
+            low = 1 << hop_bit(0, stage, bits)
+            high = 1 << hop_bit(1, stage, bits)
+            mask = jnp.where((core ^ other) == 0, low, high)
+            owner = owner ^ (((place >> at) & 1) * mask)
+        halves.append(owner)
+    return jnp.concatenate(halves)
+
+
+def inverse(owner, n):
+    return jnp.argmax(owner[None, :] == jnp.arange(n)[:, None], axis=1)
+
+
 def per_device(
     patches,
     cotangent,
@@ -210,96 +291,156 @@
     pos_index,
     pos_weight,
 ):
-    n_data = lax.axis_size("dp")
-    low_flag = lax.axis_index("dp") < n_data * 7 // 16
+    bf16 = jnp.bfloat16
+    n_dp = lax.axis_size("dp")
+    n_line = lax.axis_size("fsdp")
+    dp = lax.axis_index("dp")
+    line = lax.axis_index("fsdp")
+    low_flag = dp < n_dp * 7 // 16
     rows = patches.shape[0]
+    width = patches.shape[1]
+    shard = width // n_line
     place, valid, mask = place_rows(rows, low_flag, pos_index, pos_weight)
-    gathered = (
-        lax.all_gather(ln1_gain, "fsdp", axis=0, tiled=True),
-        lax.all_gather(ln1_bias, "fsdp", axis=0, tiled=True),
-        lax.all_gather(w_qkv, "fsdp", axis=0, tiled=True),
-        lax.all_gather(w_out, "fsdp", axis=0, tiled=True),
-        lax.all_gather(ln2_gain, "fsdp", axis=0, tiled=True),
-        lax.all_gather(ln2_bias, "fsdp", axis=0, tiled=True),
-        lax.all_gather(w_fc1, "fsdp", axis=0, tiled=True),
-        lax.all_gather(fc1_bias, "fsdp", axis=0, tiled=True),
-        lax.all_gather(w_fc2, "fsdp", axis=0, tiled=True),
-        lax.all_gather(pos_table, "fsdp", axis=1, tiled=True),
-    )
-    kept = forward(patches, gathered, place, mask)
-    block_out = jnp.where(valid[:, None], kept[5] + kept[9], 0.0).astype(jnp.bfloat16)
-    regathered = (
-        lax.all_gather(ln1_gain, "fsdp", axis=0, tiled=True),
-        lax.all_gather(ln1_bias, "fsdp", axis=0, tiled=True),
-        lax.all_gather(w_qkv, "fsdp", axis=0, tiled=True),
-        lax.all_gather(w_out, "fsdp", axis=0, tiled=True),
-        lax.all_gather(ln2_gain, "fsdp", axis=0, tiled=True),
-        lax.all_gather(ln2_bias, "fsdp", axis=0, tiled=True),
-        lax.all_gather(w_fc1, "fsdp", axis=0, tiled=True),
-        lax.all_gather(fc1_bias, "fsdp", axis=0, tiled=True),
-        lax.all_gather(w_fc2, "fsdp", axis=0, tiled=True),
-        lax.all_gather(pos_table, "fsdp", axis=1, tiled=True),
-    )
-    rekept = forward(patches, regathered, place, mask)
+
+    def column_units(matrix):
+        return matrix.reshape(matrix.shape[0], n_dp, -1).transpose(1, 0, 2)
+
+    def row_units(matrix):
+        return matrix.reshape(n_dp, -1, matrix.shape[1])
+
+    own_one = jnp.concatenate([column_units(w_qkv), column_units(w_out)], axis=2)
+    own_two = column_units(w_fc1)
+    own_three = row_units(w_fc2)
+    deep, wide = own_one.shape[1:]
+    smalls = jnp.concatenate(
+        [
+            jnp.stack([ln1_gain, ln1_bias, ln2_gain, ln2_bias]),
+            fc1_bias.reshape(-1, shard),
+            pos_table,
+        ]
+    )
+    n_small = smalls.shape[0]
+    fold = wide // shard
+    small_rows = -(-n_small // (16 * fold)) * 16
+    smalls = jnp.pad(smalls, ((0, small_rows * fold - n_small), (0, 0)))
+    packed = lax.optimization_barrier(
+        jnp.concatenate([smalls[i * small_rows : (i + 1) * small_rows] for i in range(fold)], axis=1)
+    )
+
+    def pick(units):
+        return lax.dynamic_index_in_dim(units, dp, 0, keepdims=False)
+
+    first = line_gather(jnp.concatenate([pick(own_one), packed]), n_line)
+    got_one = spread([first[:, :deep][None]], n_dp)
+    got_two = spread([line_gather(pick(own_two), n_line)[None]], n_dp)
+    got_three = spread([line_gather(pick(own_three), n_line)[None]], n_dp)
+
+    unplace = inverse(place_of(n_dp, dp, False), n_dp)
+    unline = (line - jnp.arange(n_line)) % n_line
+
+    def whole(own, got):
+        every = jnp.concatenate([jnp.take(own, place_of(n_dp, dp, False), axis=0)[:, None], jnp.concatenate(got)], axis=1)
+        return jnp.take(jnp.take(every, unplace, axis=0), unline, axis=1)
+
+    def by_columns(units):
+        return units.transpose(1, 2, 0, 3).reshape(n_line * units.shape[2], -1)
+
+    full_one = whole(own_one, got_one)
+    cut = w_qkv.shape[1] // n_dp
+    full_qkv = by_columns(full_one[..., :cut])
+    full_out = by_columns(full_one[..., cut:])
+    full_fc1 = by_columns(whole(own_two, got_two))
+    full_fc2 = whole(own_three, got_three).transpose(1, 0, 2, 3).reshape(-1, width)
+    far = jnp.concatenate(
+        [first[:, deep:, i * shard : (i + 1) * shard] for i in range(fold)], axis=1
+    )
+    table = jnp.take(jnp.concatenate([smalls[None], far]), unline, axis=0)
+
+    def across(block):
+        return block.transpose(1, 0, 2).reshape(block.shape[1], width)
+
+    vectors = across(table[:, :4])
+    full_bias = table[:, 4 : 4 + fc1_bias.size // shard].reshape(-1)
+    full_table = across(table[:, 4 + fc1_bias.size // shard : n_small])
+    params = (
+        vectors[0],
+        vectors[1],
+        full_qkv,
+        full_out,
+        vectors[2],
+        vectors[3],
+        full_fc1,
+        full_bias,
+        full_fc2,
+        full_table,
+    )
+    kept = forward(patches, params, place, mask)
+    block_out = jnp.where(valid[:, None], kept[5] + kept[9], 0.0).astype(bf16)
     grad_out = jnp.where(valid[:, None], cotangent, jnp.zeros_like(cotangent))
-    input_grad, grads = backward(rekept, regathered, place, mask, grad_out)
-    shares = (
-        lax.psum_scatter(
-            grads[0].astype(jnp.bfloat16), "fsdp", scatter_dimension=0, tiled=True
-        ).astype(jnp.float32),
-        lax.psum_scatter(
-            grads[1].astype(jnp.bfloat16), "fsdp", scatter_dimension=0, tiled=True
-        ).astype(jnp.float32),
-        lax.psum_scatter(
-            grads[2].astype(jnp.bfloat16), "fsdp", scatter_dimension=0, tiled=True
-        ).astype(jnp.float32),
-        lax.psum_scatter(
-            grads[3].astype(jnp.bfloat16), "fsdp", scatter_dimension=0, tiled=True
-        ).astype(jnp.float32),
-        lax.psum_scatter(
-            grads[4].astype(jnp.bfloat16), "fsdp", scatter_dimension=0, tiled=True
-        ).astype(jnp.float32),
-        lax.psum_scatter(
-            grads[5].astype(jnp.bfloat16), "fsdp", scatter_dimension=0, tiled=True
-        ).astype(jnp.float32),
-        lax.psum_scatter(
-            grads[6].astype(jnp.bfloat16), "fsdp", scatter_dimension=0, tiled=True
-        ).astype(jnp.float32),
-        lax.psum_scatter(
-            grads[7].astype(jnp.bfloat16), "fsdp", scatter_dimension=0, tiled=True
-        ).astype(jnp.float32),
-        lax.psum_scatter(
-            grads[8].astype(jnp.bfloat16), "fsdp", scatter_dimension=0, tiled=True
-        ).astype(jnp.float32),
-        lax.psum_scatter(
-            grads[9].astype(jnp.bfloat16), "fsdp", scatter_dimension=1, tiled=True
-        ).astype(jnp.float32),
-    )
-    totals = (
-        lax.psum(shares[0].astype(jnp.bfloat16), "dp").astype(jnp.float32),
-        lax.psum(shares[1].astype(jnp.bfloat16), "dp").astype(jnp.float32),
-        lax.psum(shares[2].astype(jnp.bfloat16), "dp").astype(jnp.float32),
-        lax.psum(shares[3].astype(jnp.bfloat16), "dp").astype(jnp.float32),
-        lax.psum(shares[4].astype(jnp.bfloat16), "dp").astype(jnp.float32),
-        lax.psum(shares[5].astype(jnp.bfloat16), "dp").astype(jnp.float32),
-        lax.psum(shares[6].astype(jnp.bfloat16), "dp").astype(jnp.float32),
-        lax.psum(shares[7].astype(jnp.bfloat16), "dp").astype(jnp.float32),
-        lax.psum(shares[8].astype(jnp.bfloat16), "dp").astype(jnp.float32),
-        lax.psum(shares[9].astype(jnp.bfloat16), "dp").astype(jnp.float32),
-    )
+    input_grad, grads = backward(kept, params, place, mask, grad_out)
+
+    send_place = place_of(n_dp, dp, True)
+    send_line = (line + jnp.arange(n_line)) % n_line
+
+    def reduced(units):
+        units = jnp.take(jnp.take(units, send_place, axis=0), send_line, axis=1)
+        half = n_dp // 2
+        done = reduce_units(units[half:], units[:half], n_dp, n_line)
+        return jnp.take(done, unplace, axis=0)
+
+    def grad_columns(grad):
+        return grad.astype(bf16).reshape(n_line, -1, n_dp, grad.shape[1] // n_dp).transpose(2, 0, 1, 3)
+
+    sum_three = reduced(grads[8].astype(bf16).reshape(n_line, n_dp, -1, width).transpose(1, 0, 2, 3))
+    sum_two = reduced(grad_columns(grads[6]))
+
+    def split(block):
+        return block.reshape(-1, n_line, shard).transpose(1, 0, 2)
+
+    rows_small = jnp.concatenate(
+        [
+            split(jnp.stack([grads[0], grads[1], grads[4], grads[5]])),
+            grads[7].reshape(n_line, -1, shard),
+            split(grads[9]),
+        ],
+        axis=1,
+    ).astype(bf16)
+    per_dp = -(-n_small // n_dp)
+    rows_small = jnp.pad(rows_small, ((0, 0), (0, per_dp * n_dp - n_small), (0, 0)))
+    rows_small = rows_small.reshape(n_line, n_dp, per_dp, shard).transpose(1, 0, 2, 3)
+    extra = -(-per_dp // 16) * 16
+    rows_small = lax.optimization_barrier(
+        jnp.pad(rows_small, ((0, 0), (0, 0), (0, extra - per_dp), (0, wide - shard)))
+    )
+    sum_one = reduced(
+        jnp.concatenate(
+            [
+                jnp.concatenate([grad_columns(grads[2]), grad_columns(grads[3])], axis=3),
+                rows_small,
+            ],
+            axis=2,
+        )
+    )
+
+    def flat_columns(units):
+        return units.transpose(1, 0, 2).reshape(units.shape[1], -1).astype(jnp.float32)
+
+    small = sum_one[:, deep : deep + per_dp, :shard].reshape(-1, shard)[:n_small]
+    small = small.astype(jnp.float32)
+    n_bias = fc1_bias.size // shard
     return (
         block_out,
         input_grad,
-        totals[0],
-        totals[1],
-        totals[2],
-        totals[3],
-        totals[4],
-        totals[5],
-        totals[6],
-        totals[7],
-        totals[8],
-        totals[9],
+        small[0],
+        small[1],
+        flat_columns(sum_one[:, :deep, :cut]),
+        flat_columns(sum_one[:, :deep, cut:]),
+        small[2],
+        small[3],
+        flat_columns(sum_two),
+        small[4 : 4 + n_bias].reshape(-1),
+        sum_three.reshape(-1, width).astype(jnp.float32),
+        small[4 + n_bias :],
     )
 
 

time: 1150 us -> 943 us (0.82)
  waiting for transfers between devices: 668 us -> 132 us
  local copies, waits for them, and re-layouts: 18.6 us -> 305 us
  other arithmetic: 31.7 us -> 193 us
  blocking collectives: 117 us -> 0 us
  starting transfers between devices: 0.86 us -> 94.2 us
  matrix products: 288 us -> 205 us
  between operations: 16.1 us -> 2.37 us
    reduce_scatter x5 -> x0, waiting for transfers between devices: 315 us -> none  [the longest x1 148 us: per_device(): lax.psum_scatter(grads[6].astype(jnp.bfloat16), 'fsdp', scatter_dimension...]
    all_gather x4 -> x0, waiting for transfers between devices: 300 us -> none  [the longest x1 139 us: per_device(): lax.all_gather(w_fc1, 'fsdp', axis=0, tiled=True)]
    gather x0 -> x31, local copies, waits for them, and re-layouts: none -> 165 us  [the longest x12 76.4 us: reduced(): units = jnp.take(jnp.take(units, send_place, axis=0), send_line, axis=1)]
    ppermute x0 -> x45, waiting for transfers between devices: none -> 132 us  [the longest x6 80.2 us: reduce_units(): lax.ppermute(send, 'dp', hop_pairs(n_dp, stage))]
    ppermute x0 -> x45, starting transfers between devices: none -> 94.2 us  [the longest x18 69.2 us: ahead(): lax.ppermute(block, 'fsdp', [(i, (i + step) % n_line) for i in range(n_li...]
    all_gather x6 -> x0, blocking collectives: 75.3 us -> none  [the longest x1 17.2 us: per_device(): lax.all_gather(fc1_bias, 'fsdp', axis=0, tiled=True)]
    select_n x0 -> x18, other arithmetic: none -> 70.5 us  [the longest x9 40.9 us: reduced(): units = jnp.take(jnp.take(units, send_place, axis=0), send_line, axis=1)]
    unnamed x74 -> x183, local copies, waits for them, and re-layouts: 8 us -> 71.1 us
  transfers between devices with their start and end apart: 10 -> 45, of which waited for: 7 -> 14; matrix products, arithmetic and copies ran while one was open for 26% -> 21% of each run, Pallas kernels for 0% -> 0%
where the time goes in v1:
time: 943 us; the launch traced here: 931 us
  local copies, waits for them, and re-layouts  305 us (32%)
  matrix products  205 us (22%)
  other arithmetic  193 us (20%)
  waiting for transfers between devices  132 us (14%)
  starting transfers between devices  94.2 us (10%)
    ppermute x6, waiting for transfers between devices, reduce_units(): lax.ppermute(send, 'dp', hop_pairs(n_dp, stage))  80.2 us
    gather x12, local copies, waits for them, and re-layouts, reduced(): units = jnp.take(jnp.take(units, send_place, axis=0), send_line, axis=1)  76.4 us
    unnamed x183, local copies, waits for them, and re-layouts  71.1 us
    gather x12, local copies, waits for them, and re-layouts, whole(): return jnp.take(jnp.take(every, unplace, axis=0), unline, axis=1)  70 us
    ppermute x18, starting transfers between devices, ahead(): lax.ppermute(block, 'fsdp', [(i, (i + step) % n_line) for i in range(n_li...  69.2 us
    select_n x9, other arithmetic, reduced(): units = jnp.take(jnp.take(units, send_place, axis=0), send_line, axis=1)  40.9 us
    ppermute x12, waiting for transfers between devices, spread(): parts = parts + [lax.ppermute(send, 'dp', hop_pairs(n_dp, stage))]  34.1 us
    dot_general x1, matrix products, forward(): jnp.dot(normed_two, w_fc1, preferred_element_type=jnp.float32)  27.9 us
  transfers between devices with their start and end apart: 45, of which 14 were waited for; matrix products, arithmetic and copies ran while one was open for 21% of the time, Pallas kernels for 0%

profile of v1, /device:TPU:0, one launch (start us, length us, event | category | flops | bytes accessed | tf_op | source)
XLA Modules:
  0.0 931.2 jit_solution(12397433032499343952)
XLA Ops:
  3.0 5.1 collective-permute-start.14
  39.0 7.2 collective-permute-done.15
  51.6 13.6 %collective-permute-start.1 = (bf16[288,512]{1,0:T(8,128)(2,1)}, bf16[288,512]{1,0:T(8,128)(2,1)S(1)}, u32[]{:S(2)}, u32[]{:S(2)}) collective-permute-start(bf16[288,512]{1,0:T(8,128)(2,1)} %pad_maximum_fusion.22), channel_id=1, source_target_pairs={{0,2},{1,3},{2,0},{3,1},{4,6},{5,7},{6,4},{7,5},{8,10},{9,11},{10,... | collective-permute-start | bytes 884744 | tf_op jit(solution)/shard_map/ppermute | solution.py:211
  115.6 13.3 %collective-permute-done.4 = bf16[2,3,256,512]{3,2,1,0:T(8,128)(2,1)S(1)} collective-permute-done((bf16[2,3,256,512]{3,2,1,0:T(8,128)(2,1)S(1)}, bf16[2,3,256,512]{3,2,1,0:T(8,128)(2,1)S(1)}, u32[]{:S(2)}, u32[]{:S(2)}) %collective-permute-start.4) | collective-permute-done | bytes 1572896 | tf_op jit(solution)/shard_map/ppermute | solution.py:225
  131.1 6.4 maximum_maximum_fusion.2
  137.5 5.9 maximum_maximum_fusion.1
  143.4 8.2 gather_fusion.14
  151.5 8.1 gather_fusion.10
  159.6 7.6 broadcast_select_fusion.3
  167.2 6.0 fusion.152
  173.2 5.0 gather_fusion.15
  178.2 5.0 gather_fusion.16
  183.2 8.7 maximum_select_fusion.3
  192.0 5.8 maximum_maximum_fusion
  197.8 8.0 gather_fusion.6
  205.9 9.4 %broadcast_select_fusion.4 = (bf16[8,4,256,512]{3,2,1,0:T(8,128)(2,1)S(1)}, bf16[8,4,256,512]{3,2,1,0:T(8,128)(2,1)}) fusion(bf16[8,4,256,512]{3,2,1,0:T(8,128)(2,1)} %gather_fusion.10, pred[8]{0:T(512)(128)(4,1)S(1)} %compare_and_fusion, bf16[8,4,256,512]{3,2,1,0:T(8,128)(2,1)} %gather_fusion.6), kind=kLoop, calls=%fused_computation.115 | loop fusion | flops 8388608 | bytes 33554440 | tf_op jit(solution)/shard_map/jit(_take)/select_n | solution.py:343
  218.9 5.0 gather_fusion.11
  224.0 5.0 gather_fusion.12
  229.0 6.0 fusion.154
  235.0 5.0 gather_fusion.7
  240.0 5.0 gather_fusion.8
  245.0 11.1 %fusion.47 = (bf16[4,256,8,512]{3,1,2,0:T(8,128)(2,1)}, bf16[8,4,256,512]{3,2,0,1:T(8,128)(2,1)S(1)}) fusion(bf16[8,4,256,256]{3,2,0,1:T(8,128)(2,1)} %bitcast.471, bf16[8,4,256,256]{3,2,0,1:T(8,128)(2,1)} %bitcast.469, pred[4]{0:T(512)(128)(4,1)S(1)} %copy-done.53, bf16[8,4,256,256]{3,2,0,1:T(8,128)(2,1)} %bitcast.475, bf16[8,4,256,256]{3,2,0,1:T(8,128)(2,1)} %bitcast.472), kind=kLoop, calls=%fused_computation.92 | loop fusion | flops 41943040 | bytes 33554436 | tf_op jit(solution)/shard_map/transpose | solution.py:346
  260.0 11.5 %copy.214 = bf16[4,256,8,512]{3,2,1,0:T(8,128)(2,1)} copy(bf16[4,256,8,512]{3,1,2,0:T(8,128)(2,1)} %get-tuple-element.270) | data formatting | bytes 16777216 | tf_op jit(solution)/shard_map/transpose | solution.py:346
  271.5 12.5 %copy.288 = bf16[128,8,8,512]{3,1,2,0:T(8,128)(2,1)} copy(bf16[128,8,8,512]{3,2,1,0:T(8,128)(2,1)} %bitcast.462) | data formatting | bytes 16777216
  284.0 6.6 copy.205
  304.8 37.2 %while.28 = (s32[]{:T(128)}, bf16[8,512,2,64]{1,3,2,0:T(8,128)(2,1)}, f32[8,2,512]{2,1,0:T(2,128)S(1)}, bf16[8,512,2,64]{1,3,2,0:T(8,128)(2,1)}, bf16[8,512,2,64...) while((s32[]{:T(128)}, ...), condition=%wide.region_7.11_spmd.clone, body=%wide.region_4.10_spmd.clone.sunk | while | flops 140835840 | bytes 7901281 | solution.py:85
  346.8 27.9 %multiply_convert_fusion.1 = (bf16[512,4096]{1,0:T(8,128)(2,1)}, f32[512,4096]{1,0:T(8,128)}, f32[512,4096]{1,0:T(8,128)}) fusion(f32[4096]{0:T(1024)S(1)} %bitcast.524, bf16[1024,4096]{1,0:T(8,128)(2,1)} %bitcast.493, f32[512,1024]{1,0:T(8,128)S(1)} %get-tuple-element.279, f32[1024]{0:T(1024)S(1)} %bitcast.535, f32[1024]{0:T(1024)S(1)} %bitcast.530, ...), kind=kOutput, calls=%fused_computation.99 | convolution fusion | flops 4436000768 | bytes 31485952 | tf_op jit(solution)/shard_map/dot_general | solution.py:91
  374.7 12.6 %fusion.160 = (bf16[4096]{0:T(1024)(128)(2,1)S(1)}, bf16[512,4096]{1,0:T(8,128)(2,1)}) fusion(f32[512,4096]{1,0:T(8,128)} %get-tuple-element.230, bf16[4096,1024]{1,0:T(8,128)(2,1)S(1)} %bitcast.487, bf16[512,1024]{1,0:T(8,128)(2,1)} %param.31, pred[512]{0:T(512)(128)(4,1)S(1)} %copy-done.60, f32[512,4096]{1,0:T(8,128)} %get-tuple-element.280, ...), kind=kOutput, calls=%fused_computation.408 | convolution fusion | flops 4329041920 | bytes 30433792 | tf_op jit(solution)/shard_map/rd,fd->rf/dot_general | solution.py:126
  387.3 8.9 multiply_reduce_fusion.1
  405.5 72.4 %while.29 = (s32[]{:T(128)}, bf16[8,512,2,64]{1,3,2,0:T(8,128)(2,1)}, bf16[8,512,2,64]{1,3,2,0:T(8,128)(2,1)}, bf16[8,512,2,64]{1,3,2,0:T(8,128)(2,1)}, bf16[8,5...) while((s32[]{:T(128)}, ...), condition=%wide.region_14.21_spmd.clone, body=%wide.region_12.20_spmd.clone.sunk | while | flops 340655104 | bytes 17984632 | solution.py:168
  478.0 9.7 %multiply_reduce_fusion.2 = (bf16[1024]{0:T(1024)(128)(2,1)S(1)}, f32[512]{0:T(512)S(1)}, bf16[1024]{0:T(1024)(128)(2,1)S(1)}, f32[512,1024]{1,0:T(8,128)}) fusion(f32[512,1024]{1,0:T(8,128)} %copy-done.5, f32[512]{0:T(512)S(1)} %fusion.132, f32[512]{0:T(512)S(1)} %broadcast_multiply_fusion.1, f32[1024]{0:T(1024)S(1)} %bitcast.527, ...), kind=kOutput, calls=%fused_computation.156 | convolution fusion | flops 3234854400 | bytes 13645824 | tf_op jit(solution)/shard_map/re,de->rd/dot_general | solution.py:175
  487.7 8.7 convolution_convert_fusion.3
  496.5 7.5 convolution_convert_fusion.2
  523.7 9.0 gather_fusion.1
  532.7 7.8 broadcast_select_fusion
  540.5 7.9 fusion.149
  548.4 5.2 gather_fusion.3
  553.6 5.2 gather_fusion.4
  558.9 12.3 %copy.292 = bf16[128,8,8,512]{3,2,1,0:T(8,128)(2,1)} copy(bf16[128,8,8,512]{3,1,2,0:T(8,128)(2,1)} %bitcast.495) | data formatting | bytes 16777216
  571.2 9.6 %copy.316 = bf16[4,256,8,512]{3,1,0,2:T(8,128)(2,1)} copy(bf16[4,256,8,512]{3,2,1,0:T(8,128)(2,1)} %bitcast.463) | data formatting | bytes 16777216 | tf_op jit(solution)/shard_map/reshape | solution.py:392
  580.8 8.3 gather_fusion.17
  589.1 7.5 broadcast_select_fusion.2
  596.6 6.6 fusion.151
  603.4 7.2 convolution_convert_fusion.1
  610.6 8.2 gather_fusion.21
  618.8 7.5 broadcast_select_fusion.1
  626.3 6.0 fusion.150
  632.2 5.0 gather_fusion.18
  637.2 5.0 gather_fusion.22
  642.2 5.0 gather_fusion.23
  647.2 5.0 gather_fusion.19
  652.2 5.3 maximum_select_fusion.5
  674.8 9.4 %maximum_select_fusion = bf16[8,4,272,512]{3,2,0,1:T(8,128)(2,1)} fusion(bf16[8,4,272,256]{3,2,0,1:T(8,128)(2,1)} %bitcast.468, bf16[8,4,272,256]{3,2,0,1:T(8,128)(2,1)} %bitcast.467, pred[4]{0:T(512)(128)(4,1)S(1)} %copy-done.51), kind=kLoop, calls=%fused_computation.85 | loop fusion | flops 22282240 | bytes 17825796 | tf_op jit(solution)/shard_map/jit(_take)/select_n | solution.py:386
  701.4 18.3 %collective-permute-done.28 = bf16[2,4,256,512]{3,2,1,0:T(8,128)(2,1)S(1)} collective-permute-done((bf16[2,4,256,512]{3,2,1,0:T(8,128)(2,1)S(1)}, bf16[2,4,256,512]{3,2,1,0:T(8,128)(2,1)S(1)}, u32[]{:S(2)}, u32[]{:S(2)}) %collective-permute-start.28) | collective-permute-done | bytes 2097184 | tf_op jit(solution)/shard_map/ppermute | solution.py:241
  722.9 30.5 %collective-permute-done.37 = bf16[2,4,128,1024]{3,2,1,0:T(8,128)(2,1)S(1)} collective-permute-done((bf16[2,4,128,1024]{3,2,1,0:T(8,128)(2,1)S(1)}, bf16[2,4,128,1024]{3,2,1,0:T(8,128)(2,1)S(1)}, u32[]{:S(2)}, u32[]{:S(2)}) %collective-permute-start.37) | collective-permute-done | bytes 2097184 | tf_op jit(solution)/shard_map/ppermute | solution.py:241
  757.2 31.4 %collective-permute-done.19 = bf16[2,4,272,512]{3,2,1,0:T(8,128)(2,1)S(1)} collective-permute-done((bf16[2,4,272,512]{3,2,1,0:T(8,128)(2,1)S(1)}, bf16[2,4,272,512]{3,2,1,0:T(8,128)(2,1)S(1)}, u32[]{:S(2)}, u32[]{:S(2)}) %collective-permute-start.19) | collective-permute-done | bytes 2228256 | tf_op jit(solution)/shard_map/ppermute | solution.py:241
  791.7 5.6 collective-permute-start.30
  806.7 16.7 %collective-permute-start.39 = (bf16[128,1024]{1,0:T(8,128)(2,1)S(1)}, bf16[128,1024]{1,0:T(8,128)(2,1)S(1)}, u32[]{:S(2)}, u32[]{:S(2)}) collective-permute-start(bf16[128,1024]{1,0:T(8,128)(2,1)S(1)} %get-tuple-element.239), channel_id=1, source_target_pairs={{0,1},{1,2},{2,3},{3,0},{4,5},{5,6},{6,7},{7,4},{8,9},{9,10},{10,1... | collective-permute-start | bytes 786440 | tf_op jit(solution)/shard_map/ppermute | solution.py:211
  829.7 10.6 %collective-permute-start.21 = (bf16[272,512]{1,0:T(8,128)(2,1)S(1)}, bf16[272,512]{1,0:T(8,128)(2,1)S(1)}, u32[]{:S(2)}, u32[]{:S(2)}) collective-permute-start(bf16[272,512]{1,0:T(8,128)(2,1)S(1)} %fusion.88), channel_id=1, source_target_pairs={{0,1},{1,2},{2,3},{3,0},{4,5},{5,6},{6,7},{7,4},{8,9},{9,10},{10,1... | collective-permute-start | bytes 835592 | tf_op jit(solution)/shard_map/ppermute | solution.py:211
  843.2 10.9 %collective-permute-done.40 = bf16[128,1024]{1,0:T(8,128)(2,1)S(1)} collective-permute-done((bf16[128,1024]{1,0:T(8,128)(2,1)S(1)}, bf16[128,1024]{1,0:T(8,128)(2,1)S(1)}, u32[]{:S(2)}, u32[]{:S(2)}) %collective-permute-start.40) | collective-permute-done | bytes 262176 | tf_op jit(solution)/shard_map/ppermute | solution.py:211
  865.0 5.0 collective-permute-done.24
  874.7 7.8 select_convert_fusion
  890.5 5.5 copy.250
  895.9 5.6 copy.262
  (523 shorter events, 370.7 us)
Async XLA Ops:
  0.7 20.8 %copy-start.39 = (bf16[256,1024]{1,0:T(8,128)(2,1)S(1)}, bf16[256,1024]{1,0:T(8,128)(2,1)}, u32[]{:S(2)}) copy-start(bf16[256,1024]{1,0:T(8,128)(2,1)} %param.35) | copy-start | bytes 1572868
  3.0 26.1 %collective-permute-start.14 = (bf16[128,1024]{1,0:T(8,128)(2,1)}, bf16[128,1024]{1,0:T(8,128)(2,1)}, u32[]{:S(2)}, u32[]{:S(2)}) collective-permute-start(bf16[128,1024]{1,0:T(8,128)(2,1)} %dynamic-slice_bitcast_fusion.1), channel_id=1, source_target_pairs={{0,3},{1,0},{2,1},{3,2},{4,7},{5,4},{6,5},{7,6},{8,11},{9,8},{10,9... | collective-permute-start | bytes 786440 | tf_op jit(solution)/shard_map/ppermute | solution.py:211
  8.0 24.9 %collective-permute-start.13 = (bf16[128,1024]{1,0:T(8,128)(2,1)}, bf16[128,1024]{1,0:T(8,128)(2,1)}, u32[]{:S(2)}, u32[]{:S(2)}) collective-permute-start(bf16[128,1024]{1,0:T(8,128)(2,1)} %dynamic-slice_bitcast_fusion.1), channel_id=1, source_target_pairs={{0,2},{1,3},{2,0},{3,1},{4,6},{5,7},{6,4},{7,5},{8,10},{9,11},{10,... | collective-permute-start | bytes 786440 | tf_op jit(solution)/shard_map/ppermute | solution.py:211
  8.0 24.9 %collective-permute-start.12 = (bf16[128,1024]{1,0:T(8,128)(2,1)}, bf16[128,1024]{1,0:T(8,128)(2,1)}, u32[]{:S(2)}, u32[]{:S(2)}) collective-permute-start(bf16[128,1024]{1,0:T(8,128)(2,1)} %dynamic-slice_bitcast_fusion.1), channel_id=1, source_target_pairs={{0,1},{1,2},{2,3},{3,0},{4,5},{5,6},{6,7},{7,4},{8,9},{9,10},{10,1... | collective-permute-start | bytes 786440 | tf_op jit(solution)/shard_map/ppermute | solution.py:211
  14.9 36.7 %collective-permute-start.8 = (bf16[256,512]{1,0:T(8,128)(2,1)}, bf16[256,512]{1,0:T(8,128)(2,1)}, u32[]{:S(2)}, u32[]{:S(2)}) collective-permute-start(bf16[256,512]{1,0:T(8,128)(2,1)} %bitcast.35), channel_id=1, source_target_pairs={{0,3},{1,0},{2,1},{3,2},{4,7},{5,4},{6,5},{7,6},{8,11},{9,8},{10,9... | collective-permute-start | bytes 786440 | tf_op jit(solution)/shard_map/ppermute | solution.py:211
  17.8 47.5 %collective-permute-start.7 = (bf16[256,512]{1,0:T(8,128)(2,1)}, bf16[256,512]{1,0:T(8,128)(2,1)}, u32[]{:S(2)}, u32[]{:S(2)}) collective-permute-start(bf16[256,512]{1,0:T(8,128)(2,1)} %bitcast.35), channel_id=1, source_target_pairs={{0,2},{1,3},{2,0},{3,1},{4,6},{5,7},{6,4},{7,5},{8,10},{9,11},{10,... | collective-permute-start | bytes 786440 | tf_op jit(solution)/shard_map/ppermute | solution.py:211
  19.0 53.8 %copy-start.54 = (pred[8]{0:T(512)(128)(4,1)}, pred[8]{0:T(512)(128)(4,1)S(1)}, u32[]{:S(2)}) copy-start(pred[8]{0:T(512)(128)(4,1)S(1)} %get-tuple-element.231) | copy-start | bytes 28
  20.3 177.5 %copy-start.47 = (s32[1024]{0:T(1024)}, s32[1024]{0:T(1024)S(1)}, u32[]{:S(2)}) copy-start(s32[1024]{0:T(1024)S(1)} %pad_clamp_fusion.5) | copy-start | bytes 12292
  20.9 47.8 %copy-start.50 = (s32[1024]{0:T(1024)}, s32[1024]{0:T(1024)S(1)}, u32[]{:S(2)}) copy-start(s32[1024]{0:T(1024)S(1)} %pad_clamp_fusion.6) | copy-start | bytes 12292
  27.2 22.8 %copy-start.62 = (s32[4]{0:T(128)S(1)}, s32[4]{0:T(128)}, u32[]{:S(2)}) copy-start(s32[4]{0:T(128)} %get-tuple-element.292) | copy-start | bytes 52
  27.2 22.8 %copy-start.11 = (bf16[256,8,384]{2,0,1:T(8,128)(2,1)S(1)}, bf16[256,8,384]{2,0,1:T(8,128)(2,1)}, u32[]{:S(2)}) copy-start(bf16[256,8,384]{2,0,1:T(8,128)(2,1)} %copy.200) | copy-start | bytes 4718596
  29.0 36.2 %collective-permute-start.6 = (bf16[256,512]{1,0:T(8,128)(2,1)}, bf16[256,512]{1,0:T(8,128)(2,1)S(1)}, u32[]{:S(2)}, u32[]{:S(2)}) collective-permute-start(bf16[256,512]{1,0:T(8,128)(2,1)} %bitcast.35), channel_id=1, source_target_pairs={{0,1},{1,2},{2,3},{3,0},{4,5},{5,6},{6,7},{7,4},{8,9},{9,10},{10,1... | collective-permute-start | bytes 786440 | tf_op jit(solution)/shard_map/ppermute | solution.py:211
  33.0 53.7 %collective-permute-start.2 = (bf16[288,512]{1,0:T(8,128)(2,1)}, bf16[288,512]{1,0:T(8,128)(2,1)}, u32[]{:S(2)}, u32[]{:S(2)}) collective-permute-start(bf16[288,512]{1,0:T(8,128)(2,1)} %pad_maximum_fusion.22), channel_id=1, source_target_pairs={{0,3},{1,0},{2,1},{3,2},{4,7},{5,4},{6,5},{7,6},{8,11},{9,8},{10,9... | collective-permute-start | bytes 884744 | tf_op jit(solution)/shard_map/ppermute | solution.py:211
  34.2 12.1 %collective-permute-start.15 = (bf16[1,3,128,1024]{3,2,1,0:T(8,128)(2,1)S(1)}, bf16[1,3,128,1024]{3,2,1,0:T(8,128)(2,1)S(1)}, u32[]{:S(2)}, u32[]{:S(2)}) collective-permute-start(bf16[1,3,128,1024]{3,2,1,0:T(8,128)(2,1)S(1)} %maximum_bitcast_fusion.1), channel_id=1, source_target_pairs={{0,8},{4,20},{8,0},{12,28},{16,24},{20,4},{24,16},{28,12},{1,9},{5... | collective-permute-start | bytes 2359304 | tf_op jit(solution)/shard_map/ppermute | solution.py:225
  48.5 34.8 %collective-permute-start.16 = (bf16[2,3,128,1024]{3,2,1,0:T(8,128)(2,1)}, bf16[2,3,128,1024]{3,2,1,0:T(8,128)(2,1)}, u32[]{:S(2)}, u32[]{:S(2)}) collective-permute-start(bf16[2,3,128,1024]{3,2,1,0:T(8,128)(2,1)} %pad_maximum_fusion.11), channel_id=1, source_target_pairs={{0,16},{4,12},{8,24},{12,4},{16,0},{20,28},{24,8},{28,20},{1,17},{... | collective-permute-start | bytes 4718600 | tf_op jit(solution)/shard_map/ppermute | solution.py:225
  50.1 20.7 %copy-start.72 = (s32[8]{0:T(128)S(1)}, s32[8]{0:T(128)}, u32[]{:S(2)}) copy-start(s32[8]{0:T(128)} %copy-done.71) | copy-start | bytes 100
  51.6 35.1 %collective-permute-start.1 = (bf16[288,512]{1,0:T(8,128)(2,1)}, bf16[288,512]{1,0:T(8,128)(2,1)S(1)}, u32[]{:S(2)}, u32[]{:S(2)}) collective-permute-start(bf16[288,512]{1,0:T(8,128)(2,1)} %pad_maximum_fusion.22), channel_id=1, source_target_pairs={{0,2},{1,3},{2,0},{3,1},{4,6},{5,7},{6,4},{7,5},{8,10},{9,11},{10,... | collective-permute-start | bytes 884744 | tf_op jit(solution)/shard_map/ppermute | solution.py:211
  65.2 21.5 %collective-permute-start = (bf16[288,512]{1,0:T(8,128)(2,1)}, bf16[288,512]{1,0:T(8,128)(2,1)S(1)}, u32[]{:S(2)}, u32[]{:S(2)}) collective-permute-start(bf16[288,512]{1,0:T(8,128)(2,1)} %pad_maximum_fusion.22), channel_id=1, source_target_pairs={{0,1},{1,2},{2,3},{3,0},{4,5},{5,6},{6,7},{7,4},{8,9},{9,10},{10,1... | collective-permute-start | bytes 884744 | tf_op jit(solution)/shard_map/ppermute | solution.py:211
  67.2 12.3 %collective-permute-start.9 = (bf16[1,3,256,512]{3,2,1,0:T(8,128)(2,1)}, bf16[1,3,256,512]{3,2,1,0:T(8,128)(2,1)}, u32[]{:S(2)}, u32[]{:S(2)}) collective-permute-start(bf16[1,3,256,512]{3,2,1,0:T(8,128)(2,1)} %maximum_bitcast_fusion), channel_id=1, source_target_pairs={{0,8},{4,20},{8,0},{12,28},{16,24},{20,4},{24,16},{28,12},{1,9},{5... | collective-permute-start | bytes 2359304 | tf_op jit(solution)/shard_map/ppermute | solution.py:225
  70.7 135.2 %copy-start.45 = (pred[8]{0:T(512)(128)(4,1)}, pred[8]{0:T(512)(128)(4,1)S(1)}, u32[]{:S(2)}) copy-start(pred[8]{0:T(512)(128)(4,1)S(1)} %compare_and_fusion) | copy-start | bytes 28
  82.3 29.2 %collective-permute-start.10 = (bf16[2,3,256,512]{3,2,1,0:T(8,128)(2,1)}, bf16[2,3,256,512]{3,2,1,0:T(8,128)(2,1)}, u32[]{:S(2)}, u32[]{:S(2)}) collective-permute-start(bf16[2,3,256,512]{3,2,1,0:T(8,128)(2,1)} %pad_maximum_fusion.10), channel_id=1, source_target_pairs={{0,16},{4,12},{8,24},{12,4},{16,0},{20,28},{24,8},{28,20},{1,17},{... | collective-permute-start | bytes 4718600 | tf_op jit(solution)/shard_map/ppermute | solution.py:225
  83.3 24.5 %copy-start.52 = (pred[4]{0:T(512)(128)(4,1)}, pred[4]{0:T(512)(128)(4,1)S(1)}, u32[]{:S(2)}) copy-start(pred[4]{0:T(512)(128)(4,1)S(1)} %get-tuple-element.294) | copy-start | bytes 16
  86.7 44.4 %collective-permute-start.17 = (bf16[4,3,128,1024]{3,2,1,0:T(8,128)(2,1)}, bf16[4,3,128,1024]{3,2,1,0:T(8,128)(2,1)}, u32[]{:S(2)}, u32[]{:S(2)}) collective-permute-start(bf16[4,3,128,1024]{3,2,1,0:T(8,128)(2,1)} %pad_maximum_fusion.3), channel_id=1, source_target_pairs={{0,4},{4,0},{8,12},{12,8},{16,20},{20,16},{24,28},{28,24},{1,5},{5... | collective-permute-start | bytes 9437192 | tf_op jit(solution)/shard_map/ppermute | solution.py:207
  87.7 20.5 %copy-start.12 = (bf16[1,3,256,512]{3,2,1,0:T(8,128)(2,1)}, bf16[1,3,256,512]{3,2,1,0:T(8,128)(2,1)S(1)}, u32[]{:S(2)}) copy-start(bf16[1,3,256,512]{3,2,1,0:T(8,128)(2,1)S(1)} %fusion.69) | copy-start | bytes 2359300
  87.7 20.5 %collective-permute-start.3 = (bf16[1,3,256,512]{3,2,1,0:T(8,128)(2,1)S(1)}, bf16[1,3,256,512]{3,2,1,0:T(8,128)(2,1)S(1)}, u32[]{:S(2)}, u32[]{:S(2)}) collective-permute-start(bf16[1,3,256,512]{3,2,1,0:T(8,128)(2,1)S(1)} %fusion.69), channel_id=1, source_target_pairs={{0,8},{4,20},{8,0},{12,28},{16,24},{20,4},{24,16},{28,12},{1,9},{5... | collective-permute-start | bytes 2359304 | tf_op jit(solution)/shard_map/ppermute | solution.py:225
  108.4 20.5 %collective-permute-start.4 = (bf16[2,3,256,512]{3,2,1,0:T(8,128)(2,1)S(1)}, bf16[2,3,256,512]{3,2,1,0:T(8,128)(2,1)S(1)}, u32[]{:S(2)}, u32[]{:S(2)}) collective-permute-start(bf16[2,3,256,512]{3,2,1,0:T(8,128)(2,1)S(1)} %pad_maximum_fusion.9), channel_id=1, source_target_pairs={{0,16},{4,12},{8,24},{12,4},{16,0},{20,28},{24,8},{28,20},{1,17},{... | collective-permute-start | bytes 4718600 | tf_op jit(solution)/shard_map/ppermute | solution.py:225
  113.6 23.9 %collective-permute-start.11 = (bf16[4,3,256,512]{3,2,1,0:T(8,128)(2,1)S(1)}, bf16[4,3,256,512]{3,2,1,0:T(8,128)(2,1)S(1)}, u32[]{:S(2)}, u32[]{:S(2)}) collective-permute-start(bf16[4,3,256,512]{3,2,1,0:T(8,128)(2,1)S(1)} %pad_maximum_fusion.2), channel_id=1, source_target_pairs={{0,4},{4,0},{8,12},{12,8},{16,20},{20,16},{24,28},{28,24},{1,5},{5... | collective-permute-start | bytes 9437192 | tf_op jit(solution)/shard_map/ppermute | solution.py:207
  115.1 180.3 %copy-start.5 = (f32[512,1024]{1,0:T(8,128)}, f32[512,1024]{1,0:T(8,128)S(1)}, u32[]{:S(2)}) copy-start(f32[512,1024]{1,0:T(8,128)S(1)} %get-tuple-element.277) | copy-start | bytes 6291460
  115.5 22.0 %copy-start.43 = (f32[512]{0:T(512)}, f32[512]{0:T(512)S(1)}, u32[]{:S(2)}) copy-start(f32[512]{0:T(512)S(1)} %multiply_reduce_fusion.6) | copy-start | bytes 6148
  115.6 179.9 %copy-start.58 = (f32[1,4,256]{2,0,1:T(1,128)}, f32[1,4,256]{2,0,1:T(1,128)S(1)}, u32[]{:S(2)}) copy-start(f32[1,4,256]{2,0,1:T(1,128)S(1)} %get-tuple-element.268) | copy-start | bytes 12292
  131.1 60.9 %collective-permute-start.5 = (bf16[4,3,256,512]{3,2,1,0:T(8,128)(2,1)}, bf16[4,3,256,512]{3,2,1,0:T(8,128)(2,1)}, u32[]{:S(2)}, u32[]{:S(2)}) collective-permute-start(bf16[4,3,256,512]{3,2,1,0:T(8,128)(2,1)} %pad_maximum_fusion.1), channel_id=1, source_target_pairs={{0,4},{4,0},{8,12},{12,8},{16,20},{20,16},{24,28},{28,24},{1,5},{5... | collective-permute-start | bytes 9437192 | tf_op jit(solution)/shard_map/ppermute | solution.py:207
  342.1 32.6 %slice-start.4 = ((s8[8388608]{0:T(1024)(128)(4,1)}), s8[4194304]{0:T(1024)(128)(4,1)S(1)}, s32[]{:S(2)}) async-start(s8[8388608]{0:T(1024)(128)(4,1)} %bitcast.485), calls=%async_computation.4 | async-start | bytes 8388608
  346.4 40.9 %copy-start.16 = (f32[512,1024]{1,0:T(8,128)}, f32[512,1024]{1,0:T(8,128)S(1)}, u32[]{:S(2)}) copy-start(f32[512,1024]{1,0:T(8,128)S(1)} %get-tuple-element.279) | copy-start | bytes 6291460
  346.8 27.9 %slice-start.5 = ((s8[8388608]{0:T(1024)(128)(4,1)}), s8[4194304]{0:T(1024)(128)(4,1)S(1)}, s32[]{:S(2)}) async-start(s8[8388608]{0:T(1024)(128)(4,1)} %bitcast.485), calls=%async_computation.5 | async-start | bytes 8388608
  346.8 27.9 %copy-start.60 = (pred[512]{0:T(512)(128)(4,1)S(1)}, pred[512]{0:T(512)(128)(4,1)}, u32[]{:S(2)}) copy-start(pred[512]{0:T(512)(128)(4,1)} %broadcast_select_fusion.10) | copy-start | bytes 1540
  674.3 15.1 %collective-permute-start.27 = (bf16[4,4,256,512]{3,2,1,0:T(8,128)(2,1)}, bf16[4,4,256,512]{3,2,1,0:T(8,128)(2,1)}, u32[]{:S(2)}, u32[]{:S(2)}) collective-permute-start(bf16[4,4,256,512]{3,2,1,0:T(8,128)(2,1)} %copy.274), channel_id=1, source_target_pairs={{0,4},{4,0},{8,12},{12,8},{16,20},{20,16},{24,28},{28,24},{1,5},{5... | collective-permute-start | bytes 12582920 | tf_op jit(solution)/shard_map/ppermute | solution.py:207
  674.6 20.5 %collective-permute-start.36 = (bf16[4,4,128,1024]{3,2,1,0:T(8,128)(2,1)}, bf16[4,4,128,1024]{3,2,1,0:T(8,128)(2,1)}, u32[]{:S(2)}, u32[]{:S(2)}) collective-permute-start(bf16[4,4,128,1024]{3,2,1,0:T(8,128)(2,1)} %copy.280), channel_id=1, source_target_pairs={{0,4},{4,0},{8,12},{12,8},{16,20},{20,16},{24,28},{28,24},{1,5},{5... | collective-permute-start | bytes 12582920 | tf_op jit(solution)/shard_map/ppermute | solution.py:207
  689.0 10.0 %collective-permute-start.18 = (bf16[4,4,272,512]{3,2,1,0:T(8,128)(2,1)}, bf16[4,4,272,512]{3,2,1,0:T(8,128)(2,1)S(1)}, u32[]{:S(2)}, u32[]{:S(2)}) collective-permute-start(bf16[4,4,272,512]{3,2,1,0:T(8,128)(2,1)} %copy.268), channel_id=1, source_target_pairs={{0,4},{4,0},{8,12},{12,8},{16,20},{20,16},{24,28},{28,24},{1,5},{5... | collective-permute-start | bytes 13369352 | tf_op jit(solution)/shard_map/ppermute | solution.py:207
  693.6 26.1 %collective-permute-start.28 = (bf16[2,4,256,512]{3,2,1,0:T(8,128)(2,1)S(1)}, bf16[2,4,256,512]{3,2,1,0:T(8,128)(2,1)S(1)}, u32[]{:S(2)}, u32[]{:S(2)}) collective-permute-start(bf16[2,4,256,512]{3,2,1,0:T(8,128)(2,1)S(1)} %add_convert_fusion.3), channel_id=1, source_target_pairs={{0,8},{4,20},{8,0},{12,28},{16,24},{20,4},{24,16},{28,12},{1,9},{5... | collective-permute-start | bytes 6291464 | tf_op jit(solution)/shard_map/ppermute | solution.py:241
  698.4 55.0 %collective-permute-start.37 = (bf16[2,4,128,1024]{3,2,1,0:T(8,128)(2,1)S(1)}, bf16[2,4,128,1024]{3,2,1,0:T(8,128)(2,1)S(1)}, u32[]{:S(2)}, u32[]{:S(2)}) collective-permute-start(bf16[2,4,128,1024]{3,2,1,0:T(8,128)(2,1)S(1)} %add_convert_fusion.2), channel_id=1, source_target_pairs={{0,8},{4,20},{8,0},{12,28},{16,24},{20,4},{24,16},{28,12},{1,9},{5... | collective-permute-start | bytes 6291464 | tf_op jit(solution)/shard_map/ppermute | solution.py:241
  699.8 88.7 %collective-permute-start.19 = (bf16[2,4,272,512]{3,2,1,0:T(8,128)(2,1)S(1)}, bf16[2,4,272,512]{3,2,1,0:T(8,128)(2,1)S(1)}, u32[]{:S(2)}, u32[]{:S(2)}) collective-permute-start(bf16[2,4,272,512]{3,2,1,0:T(8,128)(2,1)S(1)} %add_convert_fusion.1), channel_id=1, source_target_pairs={{0,8},{4,20},{8,0},{12,28},{16,24},{20,4},{24,16},{28,12},{1,9},{5... | collective-permute-start | bytes 6684680 | tf_op jit(solution)/shard_map/ppermute | solution.py:241
  721.4 69.2 %collective-permute-start.29 = (bf16[1,4,256,512]{3,2,0,1:T(8,128)(2,1)S(1)}, bf16[1,4,256,512]{3,2,0,1:T(8,128)(2,1)S(1)}, u32[]{:S(2)}, u32[]{:S(2)}) collective-permute-start(bf16[1,4,256,512]{3,2,0,1:T(8,128)(2,1)S(1)} %fusion.68), channel_id=1, source_target_pairs={{0,16},{4,12},{8,24},{12,4},{16,0},{20,28},{24,8},{28,20},{1,17},{... | collective-permute-start | bytes 3145736 | tf_op jit(solution)/shard_map/ppermute | solution.py:241
  755.6 48.1 %collective-permute-start.38 = (bf16[1,4,128,1024]{3,2,1,0:T(8,128)(2,1)S(1)}, bf16[1,4,128,1024]{3,2,1,0:T(8,128)(2,1)S(1)}, u32[]{:S(2)}, u32[]{:S(2)}) collective-permute-start(bf16[1,4,128,1024]{3,2,1,0:T(8,128)(2,1)S(1)} %add_convert_fusion.5), channel_id=1, source_target_pairs={{0,16},{4,12},{8,24},{12,4},{16,0},{20,28},{24,8},{28,20},{1,17},{... | collective-permute-start | bytes 3145736 | tf_op jit(solution)/shard_map/ppermute | solution.py:241
  789.0 40.5 %collective-permute-start.20 = (bf16[1,4,272,512]{3,2,0,1:T(8,128)(2,1)S(1)}, bf16[1,4,272,512]{3,2,0,1:T(8,128)(2,1)S(1)}, u32[]{:S(2)}, u32[]{:S(2)}) collective-permute-start(bf16[1,4,272,512]{3,2,0,1:T(8,128)(2,1)S(1)} %fusion.67), channel_id=1, source_target_pairs={{0,16},{4,12},{8,24},{12,4},{16,0},{20,28},{24,8},{28,20},{1,17},{... | collective-permute-start | bytes 3342344 | tf_op jit(solution)/shard_map/ppermute | solution.py:241
  791.7 15.0 %collective-permute-start.30 = (bf16[256,512]{1,0:T(8,128)(2,1)S(1)}, bf16[256,512]{1,0:T(8,128)(2,1)S(1)}, u32[]{:S(2)}, u32[]{:S(2)}) collective-permute-start(bf16[256,512]{1,0:T(8,128)(2,1)S(1)} %fusion.93), channel_id=1, source_target_pairs={{0,1},{1,2},{2,3},{3,0},{4,5},{5,6},{6,7},{7,4},{8,9},{9,10},{10,1... | collective-permute-start | bytes 786440 | tf_op jit(solution)/shard_map/ppermute | solution.py:211
  798.6 24.9 %collective-permute-start.31 = (bf16[256,512]{1,0:T(8,128)(2,1)S(1)}, bf16[256,512]{1,0:T(8,128)(2,1)S(1)}, u32[]{:S(2)}, u32[]{:S(2)}) collective-permute-start(bf16[256,512]{1,0:T(8,128)(2,1)S(1)} %get-tuple-element.241), channel_id=1, source_target_pairs={{0,2},{1,3},{2,0},{3,1},{4,6},{5,7},{6,4},{7,5},{8,10},{9,11},{10,... | collective-permute-start | bytes 786440 | tf_op jit(solution)/shard_map/ppermute | solution.py:211
  800.8 27.5 %collective-permute-start.32 = (bf16[256,512]{1,0:T(8,128)(2,1)S(1)}, bf16[256,512]{1,0:T(8,128)(2,1)S(1)}, u32[]{:S(2)}, u32[]{:S(2)}) collective-permute-start(bf16[256,512]{1,0:T(8,128)(2,1)S(1)} %get-tuple-element.242), channel_id=1, source_target_pairs={{0,3},{1,0},{2,1},{3,2},{4,7},{5,4},{6,5},{7,6},{8,11},{9,8},{10,9... | collective-permute-start | bytes 786440 | tf_op jit(solution)/shard_map/ppermute | solution.py:211
  804.9 35.6 %collective-permute-start.41 = (bf16[128,1024]{1,0:T(8,128)(2,1)S(1)}, bf16[128,1024]{1,0:T(8,128)(2,1)S(1)}, u32[]{:S(2)}, u32[]{:S(2)}) collective-permute-start(bf16[128,1024]{1,0:T(8,128)(2,1)S(1)} %fusion.100), channel_id=1, source_target_pairs={{0,3},{1,0},{2,1},{3,2},{4,7},{5,4},{6,5},{7,6},{8,11},{9,8},{10,9... | collective-permute-start | bytes 786440 | tf_op jit(solution)/shard_map/ppermute | solution.py:211
  805.0 69.7 %slice-start.6 = ((s8[8388608]{0:T(1024)(128)(4,1)}), s8[4194304]{0:T(1024)(128)(4,1)S(1)}, s32[]{:S(2)}) async-start(s8[8388608]{0:T(1024)(128)(4,1)} %bitcast.488), calls=%async_computation.6 | async-start | bytes 8388608
  806.7 34.0 %collective-permute-start.39 = (bf16[128,1024]{1,0:T(8,128)(2,1)S(1)}, bf16[128,1024]{1,0:T(8,128)(2,1)S(1)}, u32[]{:S(2)}, u32[]{:S(2)}) collective-permute-start(bf16[128,1024]{1,0:T(8,128)(2,1)S(1)} %get-tuple-element.239), channel_id=1, source_target_pairs={{0,1},{1,2},{2,3},{3,0},{4,5},{5,6},{6,7},{7,4},{8,9},{9,10},{10,1... | collective-permute-start | bytes 786440 | tf_op jit(solution)/shard_map/ppermute | solution.py:211
  823.4 30.7 %collective-permute-start.40 = (bf16[128,1024]{1,0:T(8,128)(2,1)S(1)}, bf16[128,1024]{1,0:T(8,128)(2,1)S(1)}, u32[]{:S(2)}, u32[]{:S(2)}) collective-permute-start(bf16[128,1024]{1,0:T(8,128)(2,1)S(1)} %get-tuple-element.240), channel_id=1, source_target_pairs={{0,2},{1,3},{2,0},{3,1},{4,6},{5,7},{6,4},{7,5},{8,10},{9,11},{10,... | collective-permute-start | bytes 786440 | tf_op jit(solution)/shard_map/ppermute | solution.py:211
  829.5 27.5 %collective-permute-start.33 = (bf16[1,256,512]{2,1,0:T(8,128)(2,1)S(1)}, bf16[1,256,512]{2,1,0:T(8,128)(2,1)S(1)}, u32[]{:S(2)}, u32[]{:S(2)}) collective-permute-start(bf16[1,256,512]{2,1,0:T(8,128)(2,1)S(1)} %fusion.96), channel_id=1, source_target_pairs={{0,8},{4,20},{8,0},{12,28},{16,24},{20,4},{24,16},{28,12},{1,9},{5... | collective-permute-start | bytes 786440 | tf_op jit(solution)/shard_map/ppermute | solution.py:225
  829.7 28.0 %collective-permute-start.21 = (bf16[272,512]{1,0:T(8,128)(2,1)S(1)}, bf16[272,512]{1,0:T(8,128)(2,1)S(1)}, u32[]{:S(2)}, u32[]{:S(2)}) collective-permute-start(bf16[272,512]{1,0:T(8,128)(2,1)S(1)} %fusion.88), channel_id=1, source_target_pairs={{0,1},{1,2},{2,3},{3,0},{4,5},{5,6},{6,7},{7,4},{8,9},{9,10},{10,1... | collective-permute-start | bytes 835592 | tf_op jit(solution)/shard_map/ppermute | solution.py:211
  840.6 19.6 %collective-permute-start.22 = (bf16[272,512]{1,0:T(8,128)(2,1)S(1)}, bf16[272,512]{1,0:T(8,128)(2,1)S(1)}, u32[]{:S(2)}, u32[]{:S(2)}) collective-permute-start(bf16[272,512]{1,0:T(8,128)(2,1)S(1)} %get-tuple-element.237), channel_id=1, source_target_pairs={{0,2},{1,3},{2,0},{3,1},{4,6},{5,7},{6,4},{7,5},{8,10},{9,11},{10,... | collective-permute-start | bytes 835592 | tf_op jit(solution)/shard_map/ppermute | solution.py:211
  840.7 34.1 %slice-start.7 = ((s8[8388608]{0:T(1024)(128)(4,1)}), s8[4194304]{0:T(1024)(128)(4,1)S(1)}, s32[]{:S(2)}) async-start(s8[8388608]{0:T(1024)(128)(4,1)} %bitcast.488), calls=%async_computation.7 | async-start | bytes 8388608
  840.7 19.5 %collective-permute-start.23 = (bf16[272,512]{1,0:T(8,128)(2,1)S(1)}, bf16[272,512]{1,0:T(8,128)(2,1)S(1)}, u32[]{:S(2)}, u32[]{:S(2)}) collective-permute-start(bf16[272,512]{1,0:T(8,128)(2,1)S(1)} %get-tuple-element.238), channel_id=1, source_target_pairs={{0,3},{1,0},{2,1},{3,2},{4,7},{5,4},{6,5},{7,6},{8,11},{9,8},{10,9... | collective-permute-start | bytes 835592 | tf_op jit(solution)/shard_map/ppermute | solution.py:211
  855.5 7.4 collective-permute-start.42
  857.0 14.3 %collective-permute-start.34 = (bf16[2,256,512]{2,1,0:T(8,128)(2,1)S(1)}, bf16[2,256,512]{2,1,0:T(8,128)(2,1)S(1)}, u32[]{:S(2)}, u32[]{:S(2)}) collective-permute-start(bf16[2,256,512]{2,1,0:T(8,128)(2,1)S(1)} %pad_maximum_fusion.20), channel_id=1, source_target_pairs={{0,16},{4,12},{8,24},{12,4},{16,0},{20,28},{24,8},{28,20},{1,17},{... | collective-permute-start | bytes 1572872 | tf_op jit(solution)/shard_map/ppermute | solution.py:225
  860.4 9.6 %collective-permute-start.24 = (bf16[1,272,512]{2,1,0:T(8,128)(2,1)S(1)}, bf16[1,272,512]{2,1,0:T(8,128)(2,1)S(1)}, u32[]{:S(2)}, u32[]{:S(2)}) collective-permute-start(bf16[1,272,512]{2,1,0:T(8,128)(2,1)S(1)} %fusion.89), channel_id=1, source_target_pairs={{0,8},{4,20},{8,0},{12,28},{16,24},{20,4},{24,16},{28,12},{1,9},{5... | collective-permute-start | bytes 835592 | tf_op jit(solution)/shard_map/ppermute | solution.py:225
  863.0 10.6 %collective-permute-start.43 = (bf16[2,128,1024]{2,1,0:T(8,128)(2,1)S(1)}, bf16[2,128,1024]{2,1,0:T(8,128)(2,1)S(1)}, u32[]{:S(2)}, u32[]{:S(2)}) collective-permute-start(bf16[2,128,1024]{2,1,0:T(8,128)(2,1)S(1)} %pad_maximum_fusion.21), channel_id=1, source_target_pairs={{0,16},{4,12},{8,24},{12,4},{16,0},{20,28},{24,8},{28,20},{1,17},{... | collective-permute-start | bytes 1572872 | tf_op jit(solution)/shard_map/ppermute | solution.py:225
  870.0 12.5 %collective-permute-start.25 = (bf16[2,272,512]{2,1,0:T(8,128)(2,1)S(1)}, bf16[2,272,512]{2,1,0:T(8,128)(2,1)S(1)}, u32[]{:S(2)}, u32[]{:S(2)}) collective-permute-start(bf16[2,272,512]{2,1,0:T(8,128)(2,1)S(1)} %pad_maximum_fusion.19), channel_id=1, source_target_pairs={{0,16},{4,12},{8,24},{12,4},{16,0},{20,28},{24,8},{28,20},{1,17},{... | collective-permute-start | bytes 1671176 | tf_op jit(solution)/shard_map/ppermute | solution.py:225
  871.4 12.8 %collective-permute-start.35 = (bf16[4,256,512]{2,1,0:T(8,128)(2,1)S(1)}, bf16[4,256,512]{2,1,0:T(8,128)(2,1)S(1)}, u32[]{:S(2)}, u32[]{:S(2)}) collective-permute-start(bf16[4,256,512]{2,1,0:T(8,128)(2,1)S(1)} %pad_maximum_fusion.15), channel_id=1, source_target_pairs={{0,4},{4,0},{8,12},{12,8},{16,20},{20,16},{24,28},{28,24},{1,5},{5... | collective-permute-start | bytes 3145736 | tf_op jit(solution)/shard_map/ppermute | solution.py:207
  874.7 26.8 %collective-permute-start.44 = (bf16[4,128,1024]{2,1,0:T(8,128)(2,1)}, bf16[4,128,1024]{2,1,0:T(8,128)(2,1)}, u32[]{:S(2)}, u32[]{:S(2)}) collective-permute-start(bf16[4,128,1024]{2,1,0:T(8,128)(2,1)} %pad_maximum_fusion.16), channel_id=1, source_target_pairs={{0,4},{4,0},{8,12},{12,8},{16,20},{20,16},{24,28},{28,24},{1,5},{5... | collective-permute-start | bytes 3145736 | tf_op jit(solution)/shard_map/ppermute | solution.py:207
  883.7 26.0 %collective-permute-start.26 = (bf16[4,272,512]{2,1,0:T(8,128)(2,1)}, bf16[4,272,512]{2,1,0:T(8,128)(2,1)}, u32[]{:S(2)}, u32[]{:S(2)}) collective-permute-start(bf16[4,272,512]{2,1,0:T(8,128)(2,1)} %pad_maximum_fusion.14), channel_id=1, source_target_pairs={{0,4},{4,0},{8,12},{12,8},{16,20},{20,16},{24,28},{28,24},{1,5},{5... | collective-permute-start | bytes 3342344 | tf_op jit(solution)/shard_map/ppermute | solution.py:207
  (64 other events, 531.1 us)

commit v2 on v1

v2 whole, which is shorter than its diff:
```python
import jax
import jax.numpy as jnp
from jax import lax
from jax.experimental import pallas as pl
from jax.experimental.pallas import tpu as pltpu
from jax.sharding import PartitionSpec as P

HEADS = 16
HDIM = 64
POS = 50
HIGH_LEN = 145
TILE = 128


highest = lax.Precision.HIGHEST


def layer_norm(hidden, gain, shift):
    centre = hidden - jnp.mean(hidden, axis=-1, keepdims=True)
    spread = jnp.mean(centre * centre, axis=-1, keepdims=True)
    return centre * lax.rsqrt(spread + 1e-06) * gain + shift


def place_rows(rows, low_flag, pos_index, pos_weight):
    offsets = jnp.arange(rows, dtype=jnp.int32)
    table_ids = jnp.arange(POS, dtype=jnp.int32)
    high_ids = jnp.arange(HIGH_LEN, dtype=jnp.int32)
    picks = (pos_index[:, :, None] == table_ids[None, None, :]).astype(jnp.float32)
    interp = jnp.sum(pos_weight[:, :, None] * picks, axis=1)
    low_valid = offsets < rows // POS * POS
    high_valid = offsets < rows // HIGH_LEN * HIGH_LEN
    low_place = (((offsets % POS)[:, None] == table_ids[None, :]) & low_valid[:, None]).astype(
        jnp.float32
    )
    high_pick = (((offsets % HIGH_LEN)[:, None] == high_ids[None, :]) & high_valid[:, None]).astype(
        jnp.float32
    )
    high_place = jnp.dot(high_pick, interp, precision=highest)
    place = jnp.where(low_flag, low_place, high_place)
    valid = jnp.where(low_flag, low_valid, high_valid)
    segment = jnp.where(
        low_flag,
        jnp.where(low_valid, offsets // POS, -1),
        jnp.where(high_valid, offsets // HIGH_LEN, -1),
    )
    return (place, valid, segment)


def key_windows(rows):
    out = []
    for start in range(0, rows, TILE):
        least, most = rows, 0
        for size in (POS, HIGH_LEN):
            used = rows // size * size
            for row in (start, start + TILE - 1):
                image = row // size
                begin = image * size if row < used else used
                end = begin + size if row < used else rows
                least, most = min(least, begin), max(most, end)
        out.append((start, least // TILE * TILE, -(-most // TILE) * TILE))
    return out


def times_t(left, right):
    return lax.dot_general(left, right, (((1,), (1,)), ((), ())), preferred_element_type=jnp.float32)


def t_times(left, right):
    return lax.dot_general(left, right, (((0,), (0,)), ((), ())), preferred_element_type=jnp.float32)


def halves(block, scale=None):
    lane = lax.broadcasted_iota(jnp.int32, block.shape, 1)
    if scale is not None:
        block = block * jnp.asarray(scale, block.dtype)
    zero = jnp.zeros_like(block)
    return (jnp.where(lane < HDIM, block, zero), jnp.where(lane < HDIM, zero, block))


def soft(query, keys, same):
    scores = jnp.where(same, times_t(query, keys), -1e30)
    expo = jnp.exp(scores - jnp.max(scores, axis=-1, keepdims=True))
    return expo * (1.0 / jnp.sum(expo, axis=-1, keepdims=True))


def attend_body(windows, col_ref, row_ref, q_ref, k_ref, v_ref, out_ref):
    values = halves(v_ref[...])
    for start, lo, hi in windows:
        rows = slice(start, start + TILE)
        same = col_ref[rows, :] == row_ref[:, lo:hi]
        keys = k_ref[lo:hi, :]
        total = None
        for query, value in zip(halves(q_ref[rows, :], HDIM ** (-0.5)), values):
            probs = soft(query, keys, same).astype(jnp.bfloat16)
            part = jnp.dot(probs, value[lo:hi], preferred_element_type=jnp.float32)
            total = part if total is None else total + part
        out_ref[rows, :] = total.astype(jnp.bfloat16)


def attend_back_body(windows, col_ref, row_ref, q_ref, k_ref, v_ref, g_ref, out_ref, dk_ref, dv_ref):
    width = q_ref.shape[1]
    full = out_ref.shape[1] // 3
    at = pl.program_id(0) * width
    dk_ref[...] = jnp.zeros_like(dk_ref)
    dv_ref[...] = jnp.zeros_like(dv_ref)
    scaled = halves(k_ref[...], HDIM ** (-0.5))
    for start, lo, hi in windows:
        rows = slice(start, start + TILE)
        same = col_ref[rows, :] == row_ref[:, lo:hi]
        keys = k_ref[lo:hi, :]
        values = v_ref[lo:hi, :]
        total = None
        queries = halves(q_ref[rows, :], HDIM ** (-0.5))
        grads = halves(g_ref[rows, :])
        for query, grad, key in zip(queries, grads, scaled):
            probs = soft(query, keys, same)
            grad_probs = times_t(grad, values)
            centre = jnp.sum(probs * grad_probs, axis=-1, keepdims=True)
            grad_scores = (probs * (grad_probs - centre)).astype(jnp.bfloat16)
            part = jnp.dot(grad_scores, key[lo:hi], preferred_element_type=jnp.float32)
            total = part if total is None else total + part
            dk_ref[lo:hi, :] += t_times(grad_scores, query)
            dv_ref[lo:hi, :] += t_times(probs.astype(jnp.bfloat16), grad)
        out_ref[rows, pl.ds(pl.multiple_of(at, width), width)] = total.astype(jnp.bfloat16)
    out_ref[:, pl.ds(pl.multiple_of(full + at, width), width)] = dk_ref[...].astype(jnp.bfloat16)
    out_ref[:, pl.ds(pl.multiple_of(2 * full + at, width), width)] = dv_ref[...].astype(jnp.bfloat16)


def pair_specs(rows, pairs):
    pair = 2 * HDIM
    whole = [
        pl.BlockSpec((rows, 1), lambda i: (0, 0)),
        pl.BlockSpec((1, rows), lambda i: (0, 0)),
    ]
    return whole + [
        pl.BlockSpec((rows, pair), lambda i, j=j: (0, j * pairs + i)) for j in range(3)
    ]


def attend(projected, segment):
    rows = projected.shape[0]
    pairs = HEADS // 2
    windows = key_windows(rows)

    def body(*refs):
        attend_body(windows, *refs)

    return pl.pallas_call(
        body,
        grid=(pairs,),
        in_specs=pair_specs(rows, pairs),
        out_specs=pl.BlockSpec((rows, 2 * HDIM), lambda i: (0, i)),
        out_shape=jax.ShapeDtypeStruct((rows, HEADS * HDIM), jnp.bfloat16),
        name="attend",
    )(segment[:, None], segment[None, :], projected, projected, projected)


def attend_back(projected, grad_attn, segment):
    rows = projected.shape[0]
    pairs = HEADS // 2
    windows = key_windows(rows)

    def body(*refs):
        attend_back_body(windows, *refs)

    return pl.pallas_call(
        body,
        grid=(pairs,),
        in_specs=pair_specs(rows, pairs) + [pl.BlockSpec((rows, 2 * HDIM), lambda i: (0, i))],
        out_specs=pl.BlockSpec((rows, 3 * HEADS * HDIM), lambda i: (0, 0)),
        out_shape=jax.ShapeDtypeStruct((rows, 3 * HEADS * HDIM), jnp.bfloat16),
        scratch_shapes=[pltpu.VMEM((rows, 2 * HDIM), jnp.float32)] * 2,
        name="attend_back",
    )(segment[:, None], segment[None, :], projected, projected, projected, grad_attn)


def copies(pairs_of, sems):
    moves = [
        pltpu.make_async_copy(source, target, sems.at[i])
        for i, (source, target) in enumerate(pairs_of)
    ]
    for move in moves:
        move.start()
    for move in moves:
        move.wait()


def assemble(owns, parts, table, n_line, unit):
    n_places = sum(part.shape[0] for part in parts)
    n_own = len(owns)
    n_parts = len(parts)
    ends = []
    for own in owns:
        ends.append((ends[-1] if ends else 0) + own.shape[1])
    count = n_own * (1 + n_places * (n_line - 1))

    def body(table_ref, *refs):
        own_refs = refs[:n_own]
        part_refs = refs[n_own : n_own + n_parts]
        out_refs = refs[n_own + n_parts : 2 * n_own + n_parts]
        sems = refs[-1]
        todo = []
        for own_ref, out_ref, end in zip(own_refs, out_refs, ends):
            shard_rows = own_ref.shape[0]
            columns = pl.ds(end - own_ref.shape[1], own_ref.shape[1])
            first = pl.multiple_of(table_ref[n_places * n_line] * unit, unit)
            todo.append((own_ref, out_ref.at[pl.ds(first, shard_rows), :]))
            place = 0
            for part_ref in part_refs:
                for k in range(part_ref.shape[0]):
                    for step in range(1, n_line):
                        row = pl.multiple_of(table_ref[place * n_line + step] * unit, unit)
                        todo.append(
                            (
                                part_ref.at[k, step - 1, pl.ds(0, unit), columns],
                                out_ref.at[pl.ds(row, unit), :],
                            )
                        )
                    place += 1
        copies(todo, sems)

    anywhere = pl.BlockSpec(memory_space=pl.ANY)
    return pl.pallas_call(
        body,
        in_specs=[pl.BlockSpec(memory_space=pltpu.SMEM)] + [anywhere] * (n_own + n_parts),
        out_specs=[anywhere] * n_own,
        out_shape=[
            jax.ShapeDtypeStruct((own.shape[0] * n_line, own.shape[1]), own.dtype) for own in owns
        ],
        scratch_shapes=[pltpu.SemaphoreType.DMA((count,))],
        name="assemble",
    )(table, *owns, *parts)


def column_order(block, table, unit):
    count = block.shape[1] // unit

    def body(table_ref, in_ref, out_ref, sems):
        copies(
            [
                (
                    in_ref.at[:, pl.ds(pl.multiple_of(table_ref[i] * unit, unit), unit)],
                    out_ref.at[:, pl.ds(i * unit, unit)],
                )
                for i in range(count)
            ],
            sems,
        )

    anywhere = pl.BlockSpec(memory_space=pl.ANY)
    return pl.pallas_call(
        body,
        in_specs=[pl.BlockSpec(memory_space=pltpu.SMEM), anywhere],
        out_specs=anywhere,
        out_shape=jax.ShapeDtypeStruct(block.shape, block.dtype),
        scratch_shapes=[pltpu.SemaphoreType.DMA((count,))],
        name="column_order",
    )(table, block)


def finish(parts, owner, cuts):
    unit = parts[0].shape[1]
    n_places = sum(part.shape[0] for part in parts)

    def body(owner_ref, *refs):
        part_refs = refs[: len(parts)]
        out_refs = refs[len(parts) :]
        place = 0
        for part_ref in part_refs:
            for k in range(part_ref.shape[0]):
                row = pl.multiple_of(owner_ref[place] * unit, unit)
                at = 0
                for out_ref, cut in zip(out_refs, cuts):
                    out_ref[pl.ds(row, unit), :] = part_ref[k, :, at : at + cut].astype(jnp.float32)
                    at += cut
                place += 1

    return pl.pallas_call(
        body,
        in_specs=[pl.BlockSpec(memory_space=pltpu.SMEM)]
        + [pl.BlockSpec(memory_space=pltpu.VMEM)] * len(parts),
        out_specs=[pl.BlockSpec(memory_space=pltpu.VMEM)] * len(cuts),
        out_shape=[jax.ShapeDtypeStruct((n_places * unit, cut), jnp.float32) for cut in cuts],
        name="finish",
    )(owner, *parts)


def hop_bit(core, stage, bits):
    return 1 + stage if core == 0 else bits - stage


def hop_pairs(n_dp, stage):
    bits = n_dp.bit_length() - 2
    return [(i, i ^ (1 << hop_bit(i % 2, stage, bits))) for i in range(n_dp)]


def swap_core(block, n_dp):
    return lax.ppermute(block, "dp", [(i, i ^ 1) for i in range(n_dp)])


def ahead(block, n_line, step):
    return lax.ppermute(block, "fsdp", [(i, (i + step) % n_line) for i in range(n_line)])


def line_gather(unit, n_line):
    return jnp.stack([ahead(unit, n_line, step) for step in range(1, n_line)])


def spread(part, n_dp):
    parts = [part]
    for stage in range(n_dp.bit_length() - 2):
        parts = parts + [lax.ppermute(item, "dp", hop_pairs(n_dp, stage)) for item in parts]
    return parts + [swap_core(item, n_dp) for item in parts]


def add_up(terms):
    total = terms[0].astype(jnp.float32)
    for term in terms[1:]:
        total = total + term.astype(jnp.float32)
    return total


def reduce_units(away, keep, n_dp, n_line):
    terms = [keep, swap_core(away, n_dp)]
    half = keep.shape[0] // 2
    for stage in range(n_dp.bit_length() - 2):
        send = add_up([term[half:] for term in terms]).astype(jnp.bfloat16)
        terms = [term[:half] for term in terms] + [lax.ppermute(send, "dp", hop_pairs(n_dp, stage))]
        half //= 2
    terms = [term[0] for term in terms]
    arrived = [
        ahead(add_up([term[step] for term in terms]).astype(jnp.bfloat16), n_line, step)
        for step in range(1, n_line)
    ]
    total = add_up([term[0] for term in terms] + arrived)
    return spread(total.astype(jnp.bfloat16)[None], n_dp)


def place_of(n_dp, me, flip):
    bits = n_dp.bit_length() - 2
    core = me % 2
    halves = []
    for other in range(2):
        place = jnp.arange(1 << bits, dtype=jnp.int32)
        owner = jnp.full((1 << bits,), me ^ other, jnp.int32)
        for stage in range(bits):
            at = bits - 1 - stage if flip else stage
            low = 1 << hop_bit(0, stage, bits)
            high = 1 << hop_bit(1, stage, bits)
            mask = jnp.where((core ^ other) == 0, low, high)
            owner = owner ^ (((place >> at) & 1) * mask)
        halves.append(owner)
    return jnp.concatenate(halves)


class Wide:
    def __init__(self, shard):
        self.shard = shard

    def gather(self, w_qkv, w_out, w_fc1, w_fc2, smalls):
        def full(matrix):
            return lax.all_gather(matrix, "fsdp", axis=0, tiled=True)

        table = lax.all_gather(smalls, "fsdp", axis=0)
        return (table, full(w_qkv), full(w_out), full(w_fc1), full(w_fc2))

    def rows(self, block):
        return block

    def wide_columns(self, block):
        return block

    def total(self, terms):
        bf16 = jnp.bfloat16
        outs = []
        for left, right in terms:
            grad = t_times(left, right).astype(bf16)
            own = lax.psum_scatter(grad, "fsdp", scatter_dimension=0, tiled=True)
            outs.append(lax.psum(own, "dp").astype(jnp.float32))
        return outs

    def total_small(self, terms, smalls):
        own = lax.psum_scatter(
            smalls.astype(jnp.bfloat16), "fsdp", scatter_dimension=0, tiled=False
        )
        return self.total(terms) + [lax.psum(own, "dp").astype(jnp.float32)]


class Staged:
    def __init__(self, n_dp, n_line, dp, line, width):
        self.n_dp = n_dp
        self.n_line = n_line
        self.dp = dp
        self.line = line
        self.unit = width // n_line // n_dp
        steps = jnp.arange(n_line, dtype=jnp.int32)
        owner = place_of(n_dp, dp, False)
        self.owner = owner
        self.unline = (line - steps) % n_line
        first = line * n_dp
        got = self.unline[None, :] * n_dp + owner[:, None]
        self.got_table = jnp.concatenate([got.reshape(-1), first[None]]).astype(jnp.int32)
        send_line = (line + steps) % n_line
        send = send_line[None, :] * n_dp + place_of(n_dp, dp, True)[:, None]
        self.send_table = send.reshape(-1).astype(jnp.int32)
        natural = jnp.arange(width, dtype=jnp.int32)
        arranged = (
            self.send_table[:, None] * self.unit + jnp.arange(self.unit, dtype=jnp.int32)[None, :]
        ).reshape(-1)
        self.order = (natural[:, None] == arranged[None, :]).astype(jnp.bfloat16)

    def pick(self, shard):
        size = shard.shape[0] // self.n_dp
        return lax.dynamic_slice_in_dim(shard, self.dp * size, size, 0)

    def gather(self, w_qkv, w_out, w_fc1, w_fc2, smalls):
        n_dp = self.n_dp
        n_line = self.n_line
        shard = smalls.shape[1]
        wide = w_qkv.shape[1] + w_out.shape[1]
        fold = wide // shard
        small_rows = -(-smalls.shape[0] // (16 * fold)) * 16
        padded = jnp.pad(smalls, ((0, small_rows * fold - smalls.shape[0]), (0, 0)))
        packed = jnp.concatenate(
            [padded[i * small_rows : (i + 1) * small_rows] for i in range(fold)], axis=1
        )
        unit_one = jnp.concatenate(
            [jnp.concatenate([self.pick(w_qkv), self.pick(w_out)], axis=1), packed]
        )
        unit_two, unit_three = (self.pick(w_fc1), self.pick(w_fc2))
        first = line_gather(unit_one, n_line)
        first, unit_two = lax.optimization_barrier((first, unit_two))
        second = line_gather(unit_two, n_line)
        second, unit_three = lax.optimization_barrier((second, unit_three))
        third = line_gather(unit_three, n_line)
        size = self.unit
        got_one = spread(first[None, :, :size], n_dp)
        got_two = spread(second[None], n_dp)
        got_three = spread(third[None], n_dp)
        full_qkv, full_out = assemble([w_qkv, w_out], got_one, self.got_table, n_line, size)
        (full_fc1,) = assemble([w_fc1], got_two, self.got_table, n_line, size)
        (full_fc2,) = assemble([w_fc2], got_three, self.got_table, n_line, third.shape[1])
        far = jnp.concatenate(
            [first[:, size:, i * shard : (i + 1) * shard] for i in range(fold)], axis=1
        )
        table = jnp.take(jnp.concatenate([padded[None], far]), self.unline, axis=0)
        return (table, full_qkv, full_out, full_fc1, full_fc2)

    def rows(self, block):
        return jnp.dot(block, self.order, preferred_element_type=jnp.float32).astype(jnp.bfloat16)

    def wide_columns(self, block):
        return column_order(block, self.send_table, block.shape[1] // (self.n_dp * self.n_line))

    def total(self, terms, extra=None):
        n_dp = self.n_dp
        n_line = self.n_line
        sides = []
        for side in (1, 0):
            grads = []
            for left, right in terms:
                half = left.shape[1] // 2
                grad = t_times(left[:, side * half : (side + 1) * half], right).astype(jnp.bfloat16)
                grads.append(grad.reshape(n_dp // 2, n_line, -1, right.shape[1]))
            if extra is not None:
                half = n_dp // 2
                grads.append(extra[side * half : (side + 1) * half])
            sides.append(jnp.concatenate(grads, axis=3) if len(grads) > 1 else grads[0])
        done = reduce_units(sides[0], sides[1], n_dp, n_line)
        cuts = [right.shape[1] for left, right in terms]
        if extra is not None:
            cuts.append(extra.shape[3])
        return list(finish(done, self.owner.astype(jnp.int32), cuts))

    def total_small(self, terms, smalls):
        n_dp = self.n_dp
        n_line = self.n_line
        n_small, shard = smalls.shape[1:]
        per_dp = -(-n_small // n_dp)
        size = self.unit
        columns = -(-per_dp * shard // (size * TILE)) * TILE
        units = jnp.pad(smalls, ((0, 0), (0, per_dp * n_dp - n_small), (0, 0)))
        units = units.reshape(n_line * n_dp, per_dp * shard).astype(jnp.bfloat16)
        units = jnp.pad(units, ((0, 0), (0, size * columns - per_dp * shard)))
        ids = jnp.arange(n_line * n_dp, dtype=jnp.int32)
        choose = (self.send_table[:, None] == ids[None, :]).astype(jnp.bfloat16)
        units = jnp.dot(choose, units, preferred_element_type=jnp.float32).astype(jnp.bfloat16)
        outs = self.total(terms, units.reshape(n_dp, n_line, size, columns))
        small = outs[-1].reshape(n_dp, size * columns)[:, : per_dp * shard]
        return outs[:-1] + [small.reshape(-1, shard)[:n_small]]


def per_device(
    patches,
    cotangent,
    ln1_gain,
    ln1_bias,
    w_qkv,
    w_out,
    ln2_gain,
    ln2_bias,
    w_fc1,
    fc1_bias,
    w_fc2,
    pos_table,
    pos_index,
    pos_weight,
):
    bf16 = jnp.bfloat16
    f32 = jnp.float32
    n_dp = lax.axis_size("dp")
    n_line = lax.axis_size("fsdp")
    dp = lax.axis_index("dp")
    line = lax.axis_index("fsdp")
    low_flag = dp < n_dp * 7 // 16
    rows = patches.shape[0]
    width = patches.shape[1]
    shard = width // n_line
    place, valid, segment = place_rows(rows, low_flag, pos_index, pos_weight)
    if n_line <= 4 and shard % (16 * n_dp) == 0:
        plan = Staged(n_dp, n_line, dp, line, width)
    else:
        plan = Wide(shard)
    n_bias = fc1_bias.size // shard
    smalls = jnp.concatenate(
        [
            jnp.stack([ln1_gain, ln1_bias, ln2_gain, ln2_bias]),
            fc1_bias.reshape(-1, shard),
            pos_table,
        ]
    )
    n_small = smalls.shape[0]
    table, full_qkv, full_out, full_fc1, full_fc2 = plan.gather(w_qkv, w_out, w_fc1, w_fc2, smalls)

    def across(block):
        return block.transpose(1, 0, 2).reshape(block.shape[1], width).astype(f32)

    gain_one, bias_one, gain_two, bias_two = across(table[:, :4])
    full_bias = table[:, 4 : 4 + n_bias].reshape(-1).astype(f32)
    full_table = across(table[:, 4 + n_bias : n_small])

    hidden_in = patches.astype(f32) + jnp.dot(place, full_table, precision=highest)
    normed_one = layer_norm(hidden_in, gain_one, bias_one).astype(bf16)
    projected = jnp.dot(normed_one, full_qkv, preferred_element_type=f32).astype(bf16)
    attn_rows = attend(projected, segment)
    hidden_mid = hidden_in + jnp.dot(attn_rows, full_out, preferred_element_type=f32)
    normed_two = layer_norm(hidden_mid, gain_two, bias_two).astype(bf16)
    pre_act = jnp.dot(normed_two, full_fc1, preferred_element_type=f32) + full_bias
    share = 0.5 * (1.0 + lax.erf(pre_act * 0.5**0.5))
    bell = jnp.exp(-0.5 * pre_act * pre_act) * (0.5 / jnp.pi) ** 0.5
    activated = (pre_act * share).astype(bf16)
    slope = (share + pre_act * bell).astype(bf16)
    branch_out = jnp.dot(activated, full_fc2, preferred_element_type=f32)
    block_out = jnp.where(valid[:, None], hidden_mid + branch_out, 0.0).astype(bf16)
    grad_out = jnp.where(valid[:, None], cotangent, jnp.zeros_like(cotangent))

    (sum_fc2,) = plan.total([(plan.wide_columns(activated), grad_out)])
    grad_pre = (times_t(grad_out, full_fc2) * slope.astype(f32)).astype(bf16)
    grad_fc1_bias = jnp.sum(grad_pre.astype(f32), axis=0)
    (sum_fc1,) = plan.total([(plan.rows(normed_two), grad_pre)])
    grad_norm_two = times_t(grad_pre, full_fc1)
    _, pull_two = jax.vjp(layer_norm, hidden_mid, gain_two, bias_two)
    back_mid, grad_gain_two, grad_bias_two = pull_two(grad_norm_two)
    grad_mid = grad_out.astype(f32) + back_mid
    grad_branch = grad_mid.astype(bf16)
    (sum_out,) = plan.total([(plan.rows(attn_rows), grad_branch)])
    grad_attn = times_t(grad_branch, full_out).astype(bf16)
    grad_proj = attend_back(projected, grad_attn, segment)
    grad_norm_one = times_t(grad_proj, full_qkv)
    _, pull_one = jax.vjp(layer_norm, hidden_in, gain_one, bias_one)
    back_in, grad_gain_one, grad_bias_one = pull_one(grad_norm_one)
    grad_in = grad_mid + back_in
    grad_table = jnp.dot(place.T, grad_in, precision=highest)

    def split(block):
        return block.reshape(-1, n_line, shard).transpose(1, 0, 2)

    rows_small = jnp.concatenate(
        [
            split(jnp.stack([grad_gain_one, grad_bias_one, grad_gain_two, grad_bias_two])),
            grad_fc1_bias.reshape(n_line, -1, shard),
            split(grad_table),
        ],
        axis=1,
    )
    sum_qkv, small = plan.total_small([(plan.rows(normed_one), grad_proj)], rows_small)
    return (
        block_out,
        grad_in.astype(bf16),
        small[0],
        small[1],
        sum_qkv,
        sum_out,
        small[2],
        small[3],
        sum_fc1,
        small[4 : 4 + n_bias].reshape(-1),
        sum_fc2,
        small[4 + n_bias :],
    )


def solution(mesh):
    return jax.shard_map(
        per_device,
        mesh=mesh,
        in_specs=(
            P(("dp", "fsdp"), None),
            P(("dp", "fsdp"), None),
            P("fsdp"),
            P("fsdp"),
            P("fsdp", None),
            P("fsdp", None),
            P("fsdp"),
            P("fsdp"),
            P("fsdp", None),
            P("fsdp"),
            P("fsdp", None),
            P(None, "fsdp"),
            P(),
            P(),
        ),
        out_specs=(
            P(("dp", "fsdp"), None),
            P(("dp", "fsdp"), None),
            P("fsdp"),
            P("fsdp"),
            P("fsdp", None),
            P("fsdp", None),
            P("fsdp"),
            P("fsdp"),
            P("fsdp", None),
            P("fsdp"),
            P("fsdp", None),
            P(None, "fsdp"),
        ),
        check_vma=False,
    )
```

time: 943 us -> 1370 us (1.45)
  Pallas kernels: 0 us -> 963 us
  local copies, waits for them, and re-layouts: 305 us -> 31 us
  other arithmetic: 193 us -> 30.1 us
  matrix products: 205 us -> 91.7 us
  waiting for transfers between devices: 132 us -> 180 us
  starting transfers between devices: 94.2 us -> 63.8 us
    pallas_call x0 -> x10, Pallas kernels: none -> 963 us  [the longest x3 769 us: assemble(): pl.pallas_call(body, in_specs=[pl.BlockSpec(memory_space=pltpu.SMEM)] + [...]
    gather x31 -> x1, local copies, waits for them, and re-layouts: 165 us -> 0.58 us  [gather(): table = jnp.take(jnp.concatenate([padded[None], far]), self.unline, axis=0)]
    dot_general x70 -> x22, matrix products: 203 us -> 91.2 us  [the longest x4 33.6 us: times_t(): lax.dot_general(left, right, (((1,), (1,)), ((), ())), preferred_element_...]
    select_n x18 -> x2, other arithmetic: 70.5 us -> 0.13 us  [gather(): table = jnp.take(jnp.concatenate([padded[None], far]), self.unline, axis=0)]
    ppermute x18 -> x21, waiting for transfers between devices: 17.3 us -> 86.5 us  [ahead(): lax.ppermute(block, 'fsdp', [(i, (i + step) % n_line) for i in range(n_li...]
    unnamed x183 -> x172, local copies, waits for them, and re-layouts: 71.1 us -> 17.6 us
    concatenate x23 -> x7, other arithmetic: 45.5 us -> 1.12 us  [the longest x1 0.59 us: __init__(): jnp.concatenate([got.reshape(-1), first[None]]).astype(jnp.int32)]
    ppermute x18 -> x21, starting transfers between devices: 69.2 us -> 25.3 us  [ahead(): lax.ppermute(block, 'fsdp', [(i, (i + step) % n_line) for i in range(n_li...]
  transfers between devices with their start and end apart: 45 -> 82, of which waited for: 14 -> 21; matrix products, arithmetic and copies ran while one was open for 21% -> 6% of each run, Pallas kernels for 0% -> 49%
where the time goes in v2:
time: 1370 us; the launch traced here: 1360 us
  Pallas kernels  963 us (70%)
  waiting for transfers between devices  180 us (13%)
  matrix products  91.7 us (7%)
  starting transfers between devices  63.8 us (5%)
  local copies, waits for them, and re-layouts  31 us (2%)
  other arithmetic  30.1 us (2%)
    pallas_call x3, Pallas kernels, assemble(): pl.pallas_call(body, in_specs=[pl.BlockSpec(memory_space=pltpu.SMEM)] + [...  769 us
    pallas_call x1, Pallas kernels, column_order(): pl.pallas_call(body, in_specs=[pl.BlockSpec(memory_space=pltpu.SMEM), any...  129 us
    ppermute x21, waiting for transfers between devices, ahead(): lax.ppermute(block, 'fsdp', [(i, (i + step) % n_line) for i in range(n_li...  86.5 us
    ppermute x8, waiting for transfers between devices, reduce_units(): lax.ppermute(send, 'dp', hop_pairs(n_dp, stage))  56.4 us
    ppermute x21, waiting for transfers between devices, spread(): lax.ppermute(item, 'dp', hop_pairs(n_dp, stage))  36.8 us
    pallas_call x1, Pallas kernels, attend_back(): pl.pallas_call(body, grid=(pairs,), in_specs=pair_specs(rows, pairs) + [p...  35.8 us
    dot_general x4, matrix products, times_t(): lax.dot_general(left, right, (((1,), (1,)), ((), ())), preferred_element_...  33.6 us
  transfers between devices with their start and end apart: 82, of which 21 were waited for; matrix products, arithmetic and copies ran while one was open for 6% of the time, Pallas kernels for 49%

profile of v2, /device:TPU:0, one launch (start us, length us, event | category | flops | bytes accessed | tf_op | source)
XLA Modules:
  0.0 1361.3 jit_solution(5718859261945227480)
XLA Ops:
  8.1 5.1 collective-permute-start.2
  17.6 1.7 constant_dynamic-slice_fusion
  19.8 1.7 constant_dynamic-slice_fusion.1
  22.8 24.0 %collective-permute-done.1 = bf16[48,4096]{1,0:T(8,128)(2,1)S(1)} collective-permute-done((bf16[48,4096]{1,0:T(8,128)(2,1)S(1)}, bf16[48,4096]{1,0:T(8,128)(2,1)S(1)}, u32[]{:S(2)}, u32[]{:S(2)}) %collective-permute-start.1) | collective-permute-done | bytes 393248 | tf_op jit(solution)/shard_map/ppermute | solution.py:302
  47.0 2.9 collective-permute-start.11
  49.9 1.9 collective-permute-start.10
  58.4 12.6 collective-permute-done.3.refs_3_
  73.9 2.0 collective-permute-start.22
  76.9 5.7 collective-permute-done.22
  82.7 14.7 %collective-permute-done.21 = bf16[128,1024]{1,0:T(8,128)(2,1)S(1)} collective-permute-done((bf16[128,1024]{1,0:T(8,128)(2,1)S(1)}, bf16[128,1024]{1,0:T(8,128)(2,1)S(1)}, u32[]{:S(2)}, u32[]{:S(2)}) %collective-permute-start.21) | collective-permute-done | bytes 262176 | tf_op jit(solution)/shard_map/ppermute | solution.py:302
  97.3 1.7 collective-permute-start.13
  99.7 2.5 fusion.20
  103.6 5.8 collective-permute-done.13.refs_2_
  111.5 1.7 collective-permute-start.23
  115.7 256.3 %assemble.3 = (bf16[1024,3072]{1,0:T(8,128)(2,1)}, bf16[1024,1024]{1,0:T(8,128)(2,1)}) custom-call(s32[33]{0:T(128)} %pad_add_fusion.1.table_ref, bf16[256,3072]{1,0:T(8,128)(2,1)} %refs_0_.3, bf16[256,1024]{1,0:T(8,128)(2,1)} %refs_1_.1, bf16[1,3,32,4096]{3,2,1,0:T(8,128)(2,1)} %slice_bitcast_fusion.refs_2_, ...), custom_call_target="tpu_custom_call" | custom-call | tf_op jit(solution)/shard_map/assemble/pallas_call | solution.py:223
  372.0 8.3 convolution_convert_fusion.5.refs_2_.refs_3_.refs_4_
  380.3 15.8 %attend.1 = bf16[512,1024]{1,0:T(8,128)(2,1)} custom-call(s32[512,1]{1,0:T(8,128)} %fusion.54.refs_0_, s32[1,512]{1,0:T(1,128)} %broadcast_select_fusion.2.refs_1_, bf16[512,3072]{1,0:T(8,128)(2,1)} %convolution_convert_fusion.5.refs_2_.refs_3_.refs_4_, bf16[512,3072]{1,0:T(8,128)(2,1)} %convolution_convert_fusion.5.refs_2_.refs_3_.refs_4_, ...), custom_call_target="tpu_custom_call" | custom-call | tf_op jit(solution)/shard_map/attend/pallas_call | solution.py:148
  396.1 3.3 fusion.106
  401.0 2.5 fusion.22
  404.4 7.9 collective-permute-done.25.refs_4_
  412.3 256.1 %assemble.4 = bf16[1024,4096]{1,0:T(8,128)(2,1)} custom-call(s32[33]{0:T(128)} %pad_add_fusion.1.table_ref, bf16[256,4096]{1,0:T(8,128)(2,1)} %refs_0_.4, bf16[1,3,32,4096]{3,2,1,0:T(8,128)(2,1)} %bitcast.317, bf16[1,3,32,4096]{3,2,1,0:T(8,128)(2,1)} %collective-permute-done.13.refs_2_, bf16[1,3,32,4096]{3,2,1,0:T(8,128)(2,1)} %collective-permute-done.14.refs_3_, ...), custom_call_target="tpu_custom_call" | custom-call | tf_op jit(solution)/shard_map/assemble/pallas_call | solution.py:223
  668.4 10.5 multiply_convert_fusion.1
  678.9 129.1 %column_order.1 = bf16[512,4096]{1,0:T(8,128)(2,1)} custom-call(s32[32]{0:T(128)} %copy-done.59, bf16[512,4096]{1,0:T(8,128)(2,1)} %get-tuple-element.66.in_ref), custom_call_target="tpu_custom_call" | custom-call | tf_op jit(solution)/shard_map/column_order/pallas_call | solution.py:251
  808.1 256.2 %assemble.5 = bf16[4096,1024]{1,0:T(8,128)(2,1)} custom-call(s32[33]{0:T(128)} %pad_add_fusion.1.table_ref, bf16[1024,1024]{1,0:T(8,128)(2,1)} %refs_0_.5, bf16[1,3,128,1024]{3,2,1,0:T(8,128)(2,1)} %maximum_bitcast_fusion.refs_1_, bf16[1,3,128,1024]{3,2,1,0:T(8,128)(2,1)} %collective-permute-done.23.refs_2_, ...), custom_call_target="tpu_custom_call" | custom-call | tf_op jit(solution)/shard_map/assemble/pallas_call | solution.py:223
  1064.4 10.9 fusion.107
  1075.3 11.1 multiply_reduce_fusion
  1086.4 2.9 fusion.102
  1091.3 2.3 convolution_convert_fusion.8.refs_5_
  1093.5 35.8 %attend_back.1 = bf16[512,3072]{1,0:T(8,128)(2,1)} custom-call(s32[512,1]{1,0:T(8,128)} %fusion.54.refs_0_, s32[1,512]{1,0:T(1,128)} %broadcast_select_fusion.2.refs_1_, bf16[512,3072]{1,0:T(8,128)(2,1)} %convolution_convert_fusion.5.refs_2_.refs_3_.refs_4_, bf16[512,3072]{1,0:T(8,128)(2,1)} %convolution_convert_fusion.5.refs_2_.refs_3_.refs_4_, ...), custom_call_target="tpu_custom_call" | custom-call | tf_op jit(solution)/shard_map/attend_back/pallas_call | solution.py:166
  1129.3 9.4 multiply_reduce_fusion.1
  1138.8 2.9 fusion.101
  1143.0 1.9 convolution_convert_fusion.11
  1145.4 3.9 convolution_convert_fusion.3
  1151.5 4.4 convolution_convert_fusion.6
  1156.4 2.9 convolution_convert_fusion
  1160.8 2.4 convolution_convert_fusion.7
  1163.2 2.0 copy-done.9
  1166.6 1.8 convolution_convert_fusion.10
  1168.4 2.4 convolution_convert_fusion.1
  1170.9 2.1 copy-done.6
  1174.6 1.8 convolution_convert_fusion.4
  1177.6 2.0 add_convert_fusion
  1180.8 5.1 collective-permute-done.44
  1190.6 15.6 %collective-permute-done.31 = bf16[2,4,32,3200]{3,2,1,0:T(8,128)(2,1)S(1)} collective-permute-done((bf16[2,4,32,3200]{3,2,1,0:T(8,128)(2,1)S(1)}, bf16[2,4,32,3200]{3,2,1,0:T(8,128)(2,1)S(1)}, u32[]{:S(2)}, u32[]{:S(2)}) %collective-permute-start.31) | collective-permute-done | bytes 1638432 | tf_op jit(solution)/shard_map/ppermute | solution.py:328
  1206.2 1.6 add_convert_fusion.3
  1209.5 3.8 collective-permute-start.48
  1213.3 2.4 collective-permute-done.46
  1215.8 5.2 collective-permute-done.47
  1222.6 6.5 collective-permute-done.32
  1230.7 3.8 collective-permute-start.35
  1234.5 3.0 collective-permute-done.70
  1238.8 21.2 %collective-permute-done.57 = bf16[2,4,32,4096]{3,2,1,0:T(8,128)(2,1)S(1)} collective-permute-done((bf16[2,4,32,4096]{3,2,1,0:T(8,128)(2,1)S(1)}, bf16[2,4,32,4096]{3,2,1,0:T(8,128)(2,1)S(1)}, u32[]{:S(2)}, u32[]{:S(2)}) %collective-permute-start.57) | collective-permute-done | bytes 2097184 | tf_op jit(solution)/shard_map/ppermute | solution.py:328
  1265.0 10.5 collective-permute-done.50.refs_2_
  1276.0 1.7 fusion.34
  1277.8 3.8 collective-permute-start.74
  1281.6 5.1 collective-permute-done.58
  1288.8 6.0 collective-permute-done.74
  1294.9 14.2 %collective-permute-done.73 = bf16[128,1024]{1,0:T(8,128)(2,1)S(1)} collective-permute-done((bf16[128,1024]{1,0:T(8,128)(2,1)S(1)}, bf16[128,1024]{1,0:T(8,128)(2,1)S(1)}, u32[]{:S(2)}, u32[]{:S(2)}) %collective-permute-start.73) | collective-permute-done | bytes 262176 | tf_op jit(solution)/shard_map/ppermute | solution.py:302
  1312.8 12.4 collective-permute-done.60
  1331.2 5.5 select_convert_fusion
  1341.7 2.1 finish.5
  1343.8 3.4 finish.4
  1351.9 3.8 finish.7
  1357.3 3.8 finish.6
  (412 shorter events, 85.4 us)
Async XLA Ops:
  8.1 14.7 %collective-permute-start.2 = (bf16[48,4096]{1,0:T(8,128)(2,1)S(1)}, bf16[48,4096]{1,0:T(8,128)(2,1)S(1)}, u32[]{:S(2)}, u32[]{:S(2)}) collective-permute-start(bf16[48,4096]{1,0:T(8,128)(2,1)S(1)} %pad_maximum_fusion.4), channel_id=1, source_target_pairs={{0,3},{1,0},{2,1},{3,2},{4,7},{5,4},{6,5},{7,6},{8,11},{9,8},{10,9... | collective-permute-start | bytes 1179656 | tf_op jit(solution)/shard_map/ppermute | solution.py:302
  13.3 33.5 %collective-permute-start.1 = (bf16[48,4096]{1,0:T(8,128)(2,1)S(1)}, bf16[48,4096]{1,0:T(8,128)(2,1)S(1)}, u32[]{:S(2)}, u32[]{:S(2)}) collective-permute-start(bf16[48,4096]{1,0:T(8,128)(2,1)S(1)} %pad_maximum_fusion.4), channel_id=1, source_target_pairs={{0,2},{1,3},{2,0},{3,1},{4,6},{5,7},{6,4},{7,5},{8,10},{9,11},{10,... | collective-permute-start | bytes 1179656 | tf_op jit(solution)/shard_map/ppermute | solution.py:302
  13.3 33.5 %collective-permute-start = (bf16[48,4096]{1,0:T(8,128)(2,1)S(1)}, bf16[48,4096]{1,0:T(8,128)(2,1)S(1)}, u32[]{:S(2)}, u32[]{:S(2)}) collective-permute-start(bf16[48,4096]{1,0:T(8,128)(2,1)S(1)} %pad_maximum_fusion.4), channel_id=1, source_target_pairs={{0,1},{1,2},{2,3},{3,0},{4,5},{5,6},{6,7},{7,4},{8,9},{9,10},{10,1... | collective-permute-start | bytes 1179656 | tf_op jit(solution)/shard_map/ppermute | solution.py:302
  46.9 25.6 %collective-permute-start.12 = (bf16[32,4096]{1,0:T(8,128)(2,1)}, bf16[32,4096]{1,0:T(8,128)(2,1)}, u32[]{:S(2)}, u32[]{:S(2)}) collective-permute-start(bf16[32,4096]{1,0:T(8,128)(2,1)} %constant_dynamic-slice_fusion.1), channel_id=1, source_target_pairs={{0,3},{1,0},{2,1},{3,2},{4,7},{5,4},{6,5},{7,6},{8,11},{9,8},{10,9... | collective-permute-start | bytes 786440 | tf_op jit(solution)/shard_map/ppermute | solution.py:302
  47.0 25.7 %collective-permute-start.11 = (bf16[32,4096]{1,0:T(8,128)(2,1)}, bf16[32,4096]{1,0:T(8,128)(2,1)}, u32[]{:S(2)}, u32[]{:S(2)}) collective-permute-start(bf16[32,4096]{1,0:T(8,128)(2,1)} %constant_dynamic-slice_fusion.1), channel_id=1, source_target_pairs={{0,2},{1,3},{2,0},{3,1},{4,6},{5,7},{6,4},{7,5},{8,10},{9,11},{10,... | collective-permute-start | bytes 786440 | tf_op jit(solution)/shard_map/ppermute | solution.py:302
  49.9 22.9 %collective-permute-start.10 = (bf16[32,4096]{1,0:T(8,128)(2,1)}, bf16[32,4096]{1,0:T(8,128)(2,1)}, u32[]{:S(2)}, u32[]{:S(2)}) collective-permute-start(bf16[32,4096]{1,0:T(8,128)(2,1)} %constant_dynamic-slice_fusion.1), channel_id=1, source_target_pairs={{0,1},{1,2},{2,3},{3,0},{4,5},{5,6},{6,7},{7,4},{8,9},{9,10},{10,1... | collective-permute-start | bytes 786440 | tf_op jit(solution)/shard_map/ppermute | solution.py:302
  52.8 46.3 %collective-permute-start.4 = (bf16[1,3,32,4096]{3,2,1,0:T(8,128)(2,1)}, bf16[1,3,32,4096]{3,2,1,0:T(8,128)(2,1)}, u32[]{:S(2)}, u32[]{:S(2)}) collective-permute-start(bf16[1,3,32,4096]{3,2,1,0:T(8,128)(2,1)} %slice_bitcast_fusion.refs_2_), channel_id=1, source_target_pairs={{0,16},{4,12},{8,24},{12,4},{16,0},{20,28},{24,8},{28,20},{1,17},{... | collective-permute-start | bytes 2359304 | tf_op jit(solution)/shard_map/ppermute | solution.py:312
  54.3 16.7 %collective-permute-start.3 = (bf16[1,3,32,4096]{3,2,1,0:T(8,128)(2,1)}, bf16[1,3,32,4096]{3,2,1,0:T(8,128)(2,1)}, u32[]{:S(2)}, u32[]{:S(2)}) collective-permute-start(bf16[1,3,32,4096]{3,2,1,0:T(8,128)(2,1)} %slice_bitcast_fusion.refs_2_), channel_id=1, source_target_pairs={{0,8},{4,20},{8,0},{12,28},{16,24},{20,4},{24,16},{28,12},{1,9},{5... | collective-permute-start | bytes 2359304 | tf_op jit(solution)/shard_map/ppermute | solution.py:312
  71.0 28.6 %collective-permute-start.5 = (bf16[1,3,32,4096]{3,2,1,0:T(8,128)(2,1)}, bf16[1,3,32,4096]{3,2,1,0:T(8,128)(2,1)S(1)}, u32[]{:S(2)}, u32[]{:S(2)}) collective-permute-start(bf16[1,3,32,4096]{3,2,1,0:T(8,128)(2,1)} %collective-permute-done.3.refs_3_), channel_id=1, source_target_pairs={{0,16},{4,12},{8,24},{12,4},{16,0},{20,28},{24,8},{28,20},{1,17},{... | collective-permute-start | bytes 2359304 | tf_op jit(solution)/shard_map/ppermute | solution.py:312
  75.9 21.4 %collective-permute-start.21 = (bf16[128,1024]{1,0:T(8,128)(2,1)S(1)}, bf16[128,1024]{1,0:T(8,128)(2,1)S(1)}, u32[]{:S(2)}, u32[]{:S(2)}) collective-permute-start(bf16[128,1024]{1,0:T(8,128)(2,1)S(1)} %copy-done.42), channel_id=1, source_target_pairs={{0,2},{1,3},{2,0},{3,1},{4,6},{5,7},{6,4},{7,5},{8,10},{9,11},{10,... | collective-permute-start | bytes 786440 | tf_op jit(solution)/shard_map/ppermute | solution.py:302
  75.9 23.1 %collective-permute-start.20 = (bf16[128,1024]{1,0:T(8,128)(2,1)S(1)}, bf16[128,1024]{1,0:T(8,128)(2,1)S(1)}, u32[]{:S(2)}, u32[]{:S(2)}) collective-permute-start(bf16[128,1024]{1,0:T(8,128)(2,1)S(1)} %copy-done.42), channel_id=1, source_target_pairs={{0,1},{1,2},{2,3},{3,0},{4,5},{5,6},{6,7},{7,4},{8,9},{9,10},{10,1... | collective-permute-start | bytes 786440 | tf_op jit(solution)/shard_map/ppermute | solution.py:302
  82.7 20.5 %collective-permute-start.6 = (bf16[1,3,32,4096]{3,2,1,0:T(8,128)(2,1)}, bf16[1,3,32,4096]{3,2,1,0:T(8,128)(2,1)S(1)}, u32[]{:S(2)}, u32[]{:S(2)}) collective-permute-start(bf16[1,3,32,4096]{3,2,1,0:T(8,128)(2,1)} %slice_bitcast_fusion.refs_2_), channel_id=1, source_target_pairs={{0,4},{4,0},{8,12},{12,8},{16,20},{20,16},{24,28},{28,24},{1,5},{5... | collective-permute-start | bytes 2359304 | tf_op jit(solution)/shard_map/ppermute | solution.py:298
  97.3 12.1 collective-permute-start.13
  99.1 12.4 collective-permute-start.7
  99.1 11.9 collective-permute-start.8
  99.6 13.6 %collective-permute-start.9 = (bf16[1,3,32,4096]{3,2,1,0:T(8,128)(2,1)S(1)}, bf16[1,3,32,4096]{3,2,1,0:T(8,128)(2,1)S(1)}, u32[]{:S(2)}, u32[]{:S(2)}) collective-permute-start(bf16[1,3,32,4096]{3,2,1,0:T(8,128)(2,1)S(1)} %collective-permute-done.5.refs_5_), channel_id=1, source_target_pairs={{0,4},{4,0},{8,12},{12,8},{16,20},{20,16},{24,28},{28,24},{1,5},{5... | collective-permute-start | bytes 2359304 | tf_op jit(solution)/shard_map/ppermute | solution.py:298
  103.2 296.2 %collective-permute-start.16 = (bf16[1,3,32,4096]{3,2,1,0:T(8,128)(2,1)S(1)}, bf16[1,3,32,4096]{3,2,1,0:T(8,128)(2,1)}, u32[]{:S(2)}, u32[]{:S(2)}) collective-permute-start(bf16[1,3,32,4096]{3,2,1,0:T(8,128)(2,1)S(1)} %bitcast.315), channel_id=1, source_target_pairs={{0,4},{4,0},{8,12},{12,8},{16,20},{20,16},{24,28},{28,24},{1,5},{5... | collective-permute-start | bytes 2359304 | tf_op jit(solution)/shard_map/ppermute | solution.py:298
  109.4 290.0 %collective-permute-start.14 = (bf16[1,3,32,4096]{3,2,1,0:T(8,128)(2,1)S(1)}, bf16[1,3,32,4096]{3,2,1,0:T(8,128)(2,1)}, u32[]{:S(2)}, u32[]{:S(2)}) collective-permute-start(bf16[1,3,32,4096]{3,2,1,0:T(8,128)(2,1)S(1)} %bitcast.316), channel_id=1, source_target_pairs={{0,16},{4,12},{8,24},{12,4},{16,0},{20,28},{24,8},{28,20},{1,17},{... | collective-permute-start | bytes 2359304 | tf_op jit(solution)/shard_map/ppermute | solution.py:312
  111.0 292.5 %collective-permute-start.24 = (bf16[1,3,128,1024]{3,2,1,0:T(8,128)(2,1)}, bf16[1,3,128,1024]{3,2,1,0:T(8,128)(2,1)}, u32[]{:S(2)}, u32[]{:S(2)}) collective-permute-start(bf16[1,3,128,1024]{3,2,1,0:T(8,128)(2,1)} %maximum_bitcast_fusion.refs_1_), channel_id=1, source_target_pairs={{0,16},{4,12},{8,24},{12,4},{16,0},{20,28},{24,8},{28,20},{1,17},{... | collective-permute-start | bytes 2359304 | tf_op jit(solution)/shard_map/ppermute | solution.py:312
  111.5 288.5 %collective-permute-start.23 = (bf16[1,3,128,1024]{3,2,1,0:T(8,128)(2,1)}, bf16[1,3,128,1024]{3,2,1,0:T(8,128)(2,1)}, u32[]{:S(2)}, u32[]{:S(2)}) collective-permute-start(bf16[1,3,128,1024]{3,2,1,0:T(8,128)(2,1)} %maximum_bitcast_fusion.refs_1_), channel_id=1, source_target_pairs={{0,8},{4,20},{8,0},{12,28},{16,24},{20,4},{24,16},{28,12},{1,9},{5... | collective-permute-start | bytes 2359304 | tf_op jit(solution)/shard_map/ppermute | solution.py:312
  114.1 286.3 %collective-permute-start.15 = (bf16[1,3,32,4096]{3,2,1,0:T(8,128)(2,1)}, bf16[1,3,32,4096]{3,2,1,0:T(8,128)(2,1)}, u32[]{:S(2)}, u32[]{:S(2)}) collective-permute-start(bf16[1,3,32,4096]{3,2,1,0:T(8,128)(2,1)} %collective-permute-done.13.refs_2_), channel_id=1, source_target_pairs={{0,16},{4,12},{8,24},{12,4},{16,0},{20,28},{24,8},{28,20},{1,17},{... | collective-permute-start | bytes 2359304 | tf_op jit(solution)/shard_map/ppermute | solution.py:312
  399.9 12.3 collective-permute-start.25
  400.4 11.8 collective-permute-start.19
  403.4 404.6 %collective-permute-start.26 = (bf16[1,3,128,1024]{3,2,1,0:T(8,128)(2,1)}, bf16[1,3,128,1024]{3,2,1,0:T(8,128)(2,1)}, u32[]{:S(2)}, u32[]{:S(2)}) collective-permute-start(bf16[1,3,128,1024]{3,2,1,0:T(8,128)(2,1)} %maximum_bitcast_fusion.refs_1_), channel_id=1, source_target_pairs={{0,4},{4,0},{8,12},{12,8},{16,20},{20,16},{24,28},{28,24},{1,5},{5... | collective-permute-start | bytes 2359304 | tf_op jit(solution)/shard_map/ppermute | solution.py:298
  403.9 404.2 %collective-permute-start.27 = (bf16[1,3,128,1024]{3,2,1,0:T(8,128)(2,1)}, bf16[1,3,128,1024]{3,2,1,0:T(8,128)(2,1)}, u32[]{:S(2)}, u32[]{:S(2)}) collective-permute-start(bf16[1,3,128,1024]{3,2,1,0:T(8,128)(2,1)} %collective-permute-done.23.refs_2_), channel_id=1, source_target_pairs={{0,4},{4,0},{8,12},{12,8},{16,20},{20,16},{24,28},{28,24},{1,5},{5... | collective-permute-start | bytes 2359304 | tf_op jit(solution)/shard_map/ppermute | solution.py:298
  404.0 404.0 %collective-permute-start.28 = (bf16[1,3,128,1024]{3,2,1,0:T(8,128)(2,1)}, bf16[1,3,128,1024]{3,2,1,0:T(8,128)(2,1)}, u32[]{:S(2)}, u32[]{:S(2)}) collective-permute-start(bf16[1,3,128,1024]{3,2,1,0:T(8,128)(2,1)} %collective-permute-done.24.refs_3_), channel_id=1, source_target_pairs={{0,4},{4,0},{8,12},{12,8},{16,20},{20,16},{24,28},{28,24},{1,5},{5... | collective-permute-start | bytes 2359304 | tf_op jit(solution)/shard_map/ppermute | solution.py:298
  412.2 395.8 %collective-permute-start.29 = (bf16[1,3,128,1024]{3,2,1,0:T(8,128)(2,1)}, bf16[1,3,128,1024]{3,2,1,0:T(8,128)(2,1)}, u32[]{:S(2)}, u32[]{:S(2)}) collective-permute-start(bf16[1,3,128,1024]{3,2,1,0:T(8,128)(2,1)} %collective-permute-done.25.refs_4_), channel_id=1, source_target_pairs={{0,4},{4,0},{8,12},{12,8},{16,20},{20,16},{24,28},{28,24},{1,5},{5... | collective-permute-start | bytes 2359304 | tf_op jit(solution)/shard_map/ppermute | solution.py:298
  1149.6 27.9 %collective-permute-start.30 = (bf16[4,4,32,3200]{3,2,1,0:T(8,128)(2,1)S(1)}, bf16[4,4,32,3200]{3,2,1,0:T(8,128)(2,1)}, u32[]{:S(2)}, u32[]{:S(2)}) collective-permute-start(bf16[4,4,32,3200]{3,2,1,0:T(8,128)(2,1)S(1)} %pad_maximum_fusion), channel_id=1, source_target_pairs={{0,4},{4,0},{8,12},{12,8},{16,20},{20,16},{24,28},{28,24},{1,5},{5... | collective-permute-start | bytes 9830408 | tf_op jit(solution)/shard_map/ppermute | solution.py:298
  1155.9 30.7 %collective-permute-start.69 = (bf16[4,4,128,1024]{3,2,1,0:T(8,128)(2,1)}, bf16[4,4,128,1024]{3,2,1,0:T(8,128)(2,1)S(1)}, u32[]{:S(2)}, u32[]{:S(2)}) collective-permute-start(bf16[4,4,128,1024]{3,2,1,0:T(8,128)(2,1)} %bitcast.66), channel_id=1, source_target_pairs={{0,4},{4,0},{8,12},{12,8},{16,20},{20,16},{24,28},{28,24},{1,5},{5... | collective-permute-start | bytes 12582920 | tf_op jit(solution)/shard_map/ppermute | solution.py:298
  1159.3 29.2 %collective-permute-start.56 = (bf16[4,4,32,4096]{3,2,1,0:T(8,128)(2,1)S(1)}, bf16[4,4,32,4096]{3,2,1,0:T(8,128)(2,1)S(1)}, u32[]{:S(2)}, u32[]{:S(2)}) collective-permute-start(bf16[4,4,32,4096]{3,2,1,0:T(8,128)(2,1)S(1)} %bitcast.309), channel_id=1, source_target_pairs={{0,4},{4,0},{8,12},{12,8},{16,20},{20,16},{24,28},{28,24},{1,5},{5... | collective-permute-start | bytes 12582920 | tf_op jit(solution)/shard_map/ppermute | solution.py:298
  1166.0 10.4 collective-permute-start.43
  1179.6 26.7 %collective-permute-start.31 = (bf16[2,4,32,3200]{3,2,1,0:T(8,128)(2,1)S(1)}, bf16[2,4,32,3200]{3,2,1,0:T(8,128)(2,1)S(1)}, u32[]{:S(2)}, u32[]{:S(2)}) collective-permute-start(bf16[2,4,32,3200]{3,2,1,0:T(8,128)(2,1)S(1)} %add_convert_fusion), channel_id=1, source_target_pairs={{0,8},{4,20},{8,0},{12,28},{16,24},{20,4},{24,16},{28,12},{1,9},{5... | collective-permute-start | bytes 4915208 | tf_op jit(solution)/shard_map/ppermute | solution.py:328
  1186.0 22.4 %collective-permute-start.45 = (bf16[1,4,32,1024]{3,2,1,0:T(8,128)(2,1)S(1)}, bf16[1,4,32,1024]{3,2,1,0:T(8,128)(2,1)S(1)}, u32[]{:S(2)}, u32[]{:S(2)}) collective-permute-start(bf16[1,4,32,1024]{3,2,1,0:T(8,128)(2,1)S(1)} %fusion.47), channel_id=1, source_target_pairs={{0,16},{4,12},{8,24},{12,4},{16,0},{20,28},{24,8},{28,20},{1,17},{... | collective-permute-start | bytes 786440 | tf_op jit(solution)/shard_map/ppermute | solution.py:328
  1187.6 49.8 %collective-permute-start.70 = (bf16[2,4,128,1024]{3,2,1,0:T(8,128)(2,1)S(1)}, bf16[2,4,128,1024]{3,2,1,0:T(8,128)(2,1)S(1)}, u32[]{:S(2)}, u32[]{:S(2)}) collective-permute-start(bf16[2,4,128,1024]{3,2,1,0:T(8,128)(2,1)S(1)} %fusion.5), channel_id=1, source_target_pairs={{0,8},{4,20},{8,0},{12,28},{16,24},{20,4},{24,16},{28,12},{1,9},{5... | collective-permute-start | bytes 6291464 | tf_op jit(solution)/shard_map/ppermute | solution.py:328
  1189.3 70.6 %collective-permute-start.57 = (bf16[2,4,32,4096]{3,2,1,0:T(8,128)(2,1)S(1)}, bf16[2,4,32,4096]{3,2,1,0:T(8,128)(2,1)S(1)}, u32[]{:S(2)}, u32[]{:S(2)}) collective-permute-start(bf16[2,4,32,4096]{3,2,1,0:T(8,128)(2,1)S(1)} %fusion.6), channel_id=1, source_target_pairs={{0,8},{4,20},{8,0},{12,28},{16,24},{20,4},{24,16},{28,12},{1,9},{5... | collective-permute-start | bytes 6291464 | tf_op jit(solution)/shard_map/ppermute | solution.py:328
  1207.9 21.2 %collective-permute-start.32 = (bf16[1,4,32,3200]{3,2,1,0:T(8,128)(2,1)S(1)}, bf16[1,4,32,3200]{3,2,1,0:T(8,128)(2,1)S(1)}, u32[]{:S(2)}, u32[]{:S(2)}) collective-permute-start(bf16[1,4,32,3200]{3,2,1,0:T(8,128)(2,1)S(1)} %add_convert_fusion.3), channel_id=1, source_target_pairs={{0,16},{4,12},{8,24},{12,4},{16,0},{20,28},{24,8},{28,20},{1,17},{... | collective-permute-start | bytes 2457608 | tf_op jit(solution)/shard_map/ppermute | solution.py:328
  1221.9 39.1 %collective-permute-start.49 = (bf16[1,32,1024]{2,1,0:T(8,128)(2,1)S(1)}, bf16[1,32,1024]{2,1,0:T(8,128)(2,1)S(1)}, u32[]{:S(2)}, u32[]{:S(2)}) collective-permute-start(bf16[1,32,1024]{2,1,0:T(8,128)(2,1)S(1)} %fusion.83.refs_0_), channel_id=1, source_target_pairs={{0,8},{4,20},{8,0},{12,28},{16,24},{20,4},{24,16},{28,12},{1,9},{5... | collective-permute-start | bytes 196616 | tf_op jit(solution)/shard_map/ppermute | solution.py:312
  1230.7 30.4 %collective-permute-start.33 = (bf16[32,3200]{1,0:T(8,128)(2,1)S(1)}, bf16[32,3200]{1,0:T(8,128)(2,1)S(1)}, u32[]{:S(2)}, u32[]{:S(2)}) collective-permute-start(bf16[32,3200]{1,0:T(8,128)(2,1)S(1)} %get-tuple-element.44), channel_id=1, source_target_pairs={{0,1},{1,2},{2,3},{3,0},{4,5},{5,6},{6,7},{7,4},{8,9},{9,10},{10,1... | collective-permute-start | bytes 614408 | tf_op jit(solution)/shard_map/ppermute | solution.py:302
  1230.7 31.9 %collective-permute-start.35 = (bf16[32,3200]{1,0:T(8,128)(2,1)S(1)}, bf16[32,3200]{1,0:T(8,128)(2,1)S(1)}, u32[]{:S(2)}, u32[]{:S(2)}) collective-permute-start(bf16[32,3200]{1,0:T(8,128)(2,1)S(1)} %get-tuple-element.45), channel_id=1, source_target_pairs={{0,3},{1,0},{2,1},{3,2},{4,7},{5,4},{6,5},{7,6},{8,11},{9,8},{10,9... | collective-permute-start | bytes 614408 | tf_op jit(solution)/shard_map/ppermute | solution.py:302
  1237.5 25.2 %collective-permute-start.34 = (bf16[32,3200]{1,0:T(8,128)(2,1)S(1)}, bf16[32,3200]{1,0:T(8,128)(2,1)S(1)}, u32[]{:S(2)}, u32[]{:S(2)}) collective-permute-start(bf16[32,3200]{1,0:T(8,128)(2,1)S(1)} %get-tuple-element.46), channel_id=1, source_target_pairs={{0,2},{1,3},{2,0},{3,1},{4,6},{5,7},{6,4},{7,5},{8,10},{9,11},{10,... | collective-permute-start | bytes 614408 | tf_op jit(solution)/shard_map/ppermute | solution.py:302
  1260.0 16.0 %collective-permute-start.71 = (bf16[1,4,128,1024]{3,2,1,0:T(8,128)(2,1)S(1)}, bf16[1,4,128,1024]{3,2,1,0:T(8,128)(2,1)S(1)}, u32[]{:S(2)}, u32[]{:S(2)}) collective-permute-start(bf16[1,4,128,1024]{3,2,1,0:T(8,128)(2,1)S(1)} %fusion.13), channel_id=1, source_target_pairs={{0,16},{4,12},{8,24},{12,4},{16,0},{20,28},{24,8},{28,20},{1,17},{... | collective-permute-start | bytes 3145736 | tf_op jit(solution)/shard_map/ppermute | solution.py:328
  1261.0 16.8 %collective-permute-start.52 = (bf16[1,32,1024]{2,1,0:T(8,128)(2,1)S(1)}, bf16[1,32,1024]{2,1,0:T(8,128)(2,1)S(1)}, u32[]{:S(2)}, u32[]{:S(2)}) collective-permute-start(bf16[1,32,1024]{2,1,0:T(8,128)(2,1)S(1)} %fusion.83.refs_0_), channel_id=1, source_target_pairs={{0,4},{4,0},{8,12},{12,8},{16,20},{20,16},{24,28},{28,24},{1,5},{5... | collective-permute-start | bytes 196616 | tf_op jit(solution)/shard_map/ppermute | solution.py:298
  1261.1 14.4 %collective-permute-start.50 = (bf16[1,32,1024]{2,1,0:T(8,128)(2,1)S(1)}, bf16[1,32,1024]{2,1,0:T(8,128)(2,1)S(1)}, u32[]{:S(2)}, u32[]{:S(2)}) collective-permute-start(bf16[1,32,1024]{2,1,0:T(8,128)(2,1)S(1)} %fusion.83.refs_0_), channel_id=1, source_target_pairs={{0,16},{4,12},{8,24},{12,4},{16,0},{20,28},{24,8},{28,20},{1,17},{... | collective-permute-start | bytes 196616 | tf_op jit(solution)/shard_map/ppermute | solution.py:312
  1262.7 24.5 %collective-permute-start.53 = (bf16[1,32,1024]{2,1,0:T(8,128)(2,1)S(1)}, bf16[1,32,1024]{2,1,0:T(8,128)(2,1)S(1)}, u32[]{:S(2)}, u32[]{:S(2)}) collective-permute-start(bf16[1,32,1024]{2,1,0:T(8,128)(2,1)S(1)} %collective-permute-done.49.refs_1_), channel_id=1, source_target_pairs={{0,4},{4,0},{8,12},{12,8},{16,20},{20,16},{24,28},{28,24},{1,5},{5... | collective-permute-start | bytes 196616 | tf_op jit(solution)/shard_map/ppermute | solution.py:298
  1262.7 24.0 %collective-permute-start.58 = (bf16[1,4,32,4096]{3,2,1,0:T(8,128)(2,1)S(1)}, bf16[1,4,32,4096]{3,2,1,0:T(8,128)(2,1)S(1)}, u32[]{:S(2)}, u32[]{:S(2)}) collective-permute-start(bf16[1,4,32,4096]{3,2,1,0:T(8,128)(2,1)S(1)} %fusion.15), channel_id=1, source_target_pairs={{0,16},{4,12},{8,24},{12,4},{16,0},{20,28},{24,8},{28,20},{1,17},{... | collective-permute-start | bytes 3145736 | tf_op jit(solution)/shard_map/ppermute | solution.py:328
  1275.5 12.3 collective-permute-start.51
  1277.8 11.1 collective-permute-start.72
  1277.8 17.0 %collective-permute-start.74 = (bf16[128,1024]{1,0:T(8,128)(2,1)S(1)}, bf16[128,1024]{1,0:T(8,128)(2,1)S(1)}, u32[]{:S(2)}, u32[]{:S(2)}) collective-permute-start(bf16[128,1024]{1,0:T(8,128)(2,1)S(1)} %get-tuple-element.39), channel_id=1, source_target_pairs={{0,3},{1,0},{2,1},{3,2},{4,7},{5,4},{6,5},{7,6},{8,11},{9,8},{10,9... | collective-permute-start | bytes 786440 | tf_op jit(solution)/shard_map/ppermute | solution.py:302
  1286.7 22.4 %collective-permute-start.73 = (bf16[128,1024]{1,0:T(8,128)(2,1)S(1)}, bf16[128,1024]{1,0:T(8,128)(2,1)S(1)}, u32[]{:S(2)}, u32[]{:S(2)}) collective-permute-start(bf16[128,1024]{1,0:T(8,128)(2,1)S(1)} %get-tuple-element.40), channel_id=1, source_target_pairs={{0,2},{1,3},{2,0},{3,1},{4,6},{5,7},{6,4},{7,5},{8,10},{9,11},{10,... | collective-permute-start | bytes 786440 | tf_op jit(solution)/shard_map/ppermute | solution.py:302
  1287.2 23.3 %collective-permute-start.37 = (bf16[1,32,3200]{2,1,0:T(8,128)(2,1)S(1)}, bf16[1,32,3200]{2,1,0:T(8,128)(2,1)S(1)}, u32[]{:S(2)}, u32[]{:S(2)}) collective-permute-start(bf16[1,32,3200]{2,1,0:T(8,128)(2,1)S(1)} %fusion.70.refs_0_), channel_id=1, source_target_pairs={{0,16},{4,12},{8,24},{12,4},{16,0},{20,28},{24,8},{28,20},{1,17},{... | collective-permute-start | bytes 614408 | tf_op jit(solution)/shard_map/ppermute | solution.py:312
  1287.8 22.9 %collective-permute-start.36 = (bf16[1,32,3200]{2,1,0:T(8,128)(2,1)S(1)}, bf16[1,32,3200]{2,1,0:T(8,128)(2,1)S(1)}, u32[]{:S(2)}, u32[]{:S(2)}) collective-permute-start(bf16[1,32,3200]{2,1,0:T(8,128)(2,1)S(1)} %fusion.70.refs_0_), channel_id=1, source_target_pairs={{0,8},{4,20},{8,0},{12,28},{16,24},{20,4},{24,16},{28,12},{1,9},{5... | collective-permute-start | bytes 614408 | tf_op jit(solution)/shard_map/ppermute | solution.py:312
  1288.8 22.4 %collective-permute-start.59 = (bf16[32,4096]{1,0:T(8,128)(2,1)S(1)}, bf16[32,4096]{1,0:T(8,128)(2,1)S(1)}, u32[]{:S(2)}, u32[]{:S(2)}) collective-permute-start(bf16[32,4096]{1,0:T(8,128)(2,1)S(1)} %get-tuple-element.41), channel_id=1, source_target_pairs={{0,1},{1,2},{2,3},{3,0},{4,5},{5,6},{6,7},{7,4},{8,9},{9,10},{10,1... | collective-permute-start | bytes 786440 | tf_op jit(solution)/shard_map/ppermute | solution.py:302
  1294.9 16.4 %collective-permute-start.61 = (bf16[32,4096]{1,0:T(8,128)(2,1)S(1)}, bf16[32,4096]{1,0:T(8,128)(2,1)S(1)}, u32[]{:S(2)}, u32[]{:S(2)}) collective-permute-start(bf16[32,4096]{1,0:T(8,128)(2,1)S(1)} %get-tuple-element.42), channel_id=1, source_target_pairs={{0,3},{1,0},{2,1},{3,2},{4,7},{5,4},{6,5},{7,6},{8,11},{9,8},{10,9... | collective-permute-start | bytes 786440 | tf_op jit(solution)/shard_map/ppermute | solution.py:302
  1309.1 16.1 %collective-permute-start.60 = (bf16[32,4096]{1,0:T(8,128)(2,1)S(1)}, bf16[32,4096]{1,0:T(8,128)(2,1)S(1)}, u32[]{:S(2)}, u32[]{:S(2)}) collective-permute-start(bf16[32,4096]{1,0:T(8,128)(2,1)S(1)} %get-tuple-element.43), channel_id=1, source_target_pairs={{0,2},{1,3},{2,0},{3,1},{4,6},{5,7},{6,4},{7,5},{8,10},{9,11},{10,... | collective-permute-start | bytes 786440 | tf_op jit(solution)/shard_map/ppermute | solution.py:302
  1310.6 16.2 %collective-permute-start.55 = (bf16[1,32,1024]{2,1,0:T(8,128)(2,1)S(1)}, bf16[1,32,1024]{2,1,0:T(8,128)(2,1)S(1)}, u32[]{:S(2)}, u32[]{:S(2)}) collective-permute-start(bf16[1,32,1024]{2,1,0:T(8,128)(2,1)S(1)} %collective-permute-done.51.refs_3_), channel_id=1, source_target_pairs={{0,4},{4,0},{8,12},{12,8},{16,20},{20,16},{24,28},{28,24},{1,5},{5... | collective-permute-start | bytes 196616 | tf_op jit(solution)/shard_map/ppermute | solution.py:298
  1310.7 16.2 %collective-permute-start.39 = (bf16[1,32,3200]{2,1,0:T(8,128)(2,1)S(1)}, bf16[1,32,3200]{2,1,0:T(8,128)(2,1)S(1)}, u32[]{:S(2)}, u32[]{:S(2)}) collective-permute-start(bf16[1,32,3200]{2,1,0:T(8,128)(2,1)S(1)} %fusion.70.refs_0_), channel_id=1, source_target_pairs={{0,4},{4,0},{8,12},{12,8},{16,20},{20,16},{24,28},{28,24},{1,5},{5... | collective-permute-start | bytes 614408 | tf_op jit(solution)/shard_map/ppermute | solution.py:298
  1311.2 18.1 %collective-permute-start.40 = (bf16[1,32,3200]{2,1,0:T(8,128)(2,1)S(1)}, bf16[1,32,3200]{2,1,0:T(8,128)(2,1)S(1)}, u32[]{:S(2)}, u32[]{:S(2)}) collective-permute-start(bf16[1,32,3200]{2,1,0:T(8,128)(2,1)S(1)} %collective-permute-done.36.refs_1_), channel_id=1, source_target_pairs={{0,4},{4,0},{8,12},{12,8},{16,20},{20,16},{24,28},{28,24},{1,5},{5... | collective-permute-start | bytes 614408 | tf_op jit(solution)/shard_map/ppermute | solution.py:298
  1311.3 14.9 %collective-permute-start.38 = (bf16[1,32,3200]{2,1,0:T(8,128)(2,1)S(1)}, bf16[1,32,3200]{2,1,0:T(8,128)(2,1)S(1)}, u32[]{:S(2)}, u32[]{:S(2)}) collective-permute-start(bf16[1,32,3200]{2,1,0:T(8,128)(2,1)S(1)} %collective-permute-done.36.refs_1_), channel_id=1, source_target_pairs={{0,16},{4,12},{8,24},{12,4},{16,0},{20,28},{24,8},{28,20},{1,17},{... | collective-permute-start | bytes 614408 | tf_op jit(solution)/shard_map/ppermute | solution.py:312
  1326.2 10.6 collective-permute-start.42
  1326.8 10.6 collective-permute-start.78
  1326.9 12.1 collective-permute-start.76
  1336.8 11.4 collective-permute-start.63
  1337.4 11.4 collective-permute-start.79
  1337.4 11.5 collective-permute-start.77
  (91 other events, 1951.5 us)

commit v3 on v2

--- a/solution.py
+++ b/solution.py
@@ -223,7 +223,7 @@
     return pl.pallas_call(
         body,
         in_specs=[pl.BlockSpec(memory_space=pltpu.SMEM)] + [anywhere] * (n_own + n_parts),
-        out_specs=[anywhere] * n_own,
+        out_specs=[pl.BlockSpec(memory_space=pltpu.VMEM)] * n_own,
         out_shape=[
             jax.ShapeDtypeStruct((own.shape[0] * n_line, own.shape[1]), own.dtype) for own in owns
         ],
@@ -235,25 +235,19 @@
 def column_order(block, table, unit):
     count = block.shape[1] // unit
 
-    def body(table_ref, in_ref, out_ref, sems):
-        copies(
-            [
-                (
-                    in_ref.at[:, pl.ds(pl.multiple_of(table_ref[i] * unit, unit), unit)],
-                    out_ref.at[:, pl.ds(i * unit, unit)],
-                )
-                for i in range(count)
-            ],
-            sems,
-        )
-
-    anywhere = pl.BlockSpec(memory_space=pl.ANY)
+    def body(table_ref, in_ref, out_ref):
+        for i in range(count):
+            column = pl.multiple_of(table_ref[i] * unit, unit)
+            out_ref[:, i * unit : (i + 1) * unit] = in_ref[:, pl.ds(column, unit)]
+
     return pl.pallas_call(
         body,
-        in_specs=[pl.BlockSpec(memory_space=pltpu.SMEM), anywhere],
-        out_specs=anywhere,
+        in_specs=[
+            pl.BlockSpec(memory_space=pltpu.SMEM),
+            pl.BlockSpec(memory_space=pltpu.VMEM),
+        ],
+        out_specs=pl.BlockSpec(memory_space=pltpu.VMEM),
         out_shape=jax.ShapeDtypeStruct(block.shape, block.dtype),
-        scratch_shapes=[pltpu.SemaphoreType.DMA((count,))],
         name="column_order",
     )(table, block)
 
@@ -320,20 +314,74 @@
     return total
 
 
-def reduce_units(away, keep, n_dp, n_line):
-    terms = [keep, swap_core(away, n_dp)]
+def reduce_steps(away, keep, n_dp, n_line):
+    (away,) = yield [away]
+    (got,) = yield [swap_core(away, n_dp)]
+    terms = [keep, got]
     half = keep.shape[0] // 2
     for stage in range(n_dp.bit_length() - 2):
-        send = add_up([term[half:] for term in terms]).astype(jnp.bfloat16)
-        terms = [term[:half] for term in terms] + [lax.ppermute(send, "dp", hop_pairs(n_dp, stage))]
+        (send,) = yield [add_up([term[half:] for term in terms]).astype(jnp.bfloat16)]
+        (got,) = yield [lax.ppermute(send, "dp", hop_pairs(n_dp, stage))]
+        terms = [term[:half] for term in terms] + [got]
         half //= 2
     terms = [term[0] for term in terms]
-    arrived = [
-        ahead(add_up([term[step] for term in terms]).astype(jnp.bfloat16), n_line, step)
-        for step in range(1, n_line)
+    sends = yield [
+        add_up([term[step] for term in terms]).astype(jnp.bfloat16) for step in range(1, n_line)
     ]
-    total = add_up([term[0] for term in terms] + arrived)
-    return spread(total.astype(jnp.bfloat16)[None], n_dp)
+    arrived = yield [ahead(send, n_line, step + 1) for step, send in enumerate(sends)]
+    parts = [add_up([term[0] for term in terms] + arrived).astype(jnp.bfloat16)[None]]
+    for stage in range(n_dp.bit_length() - 2):
+        parts = yield parts
+        parts = parts + (yield [lax.ppermute(item, "dp", hop_pairs(n_dp, stage)) for item in parts])
+    parts = yield parts
+    return parts + (yield [swap_core(item, n_dp) for item in parts])
+
+
+class Reduction:
+    def __init__(self, steps, close):
+        self.steps = steps
+        self.close = close
+        self.parts = None
+        self.held = None
+        self.begin = next(steps)
+
+    def take(self, got):
+        try:
+            return self.steps.send(got)
+        except StopIteration as stop:
+            self.parts = stop.value
+            return []
+
+    def result(self):
+        if self.held is None:
+            self.held = self.steps.send(self.begin)
+        while self.parts is None:
+            sends = self.take(self.held)
+            if self.parts is None:
+                self.held = self.steps.send(sends)
+        return self.close(self.parts)
+
+
+class Ready:
+    def __init__(self, outs):
+        self.outs = outs
+
+    def result(self):
+        return self.outs
+
+
+def tick(value, running):
+    running = [item for item in running if isinstance(item, Reduction) and item.parts is None]
+    old = [item for item in running if item.held is not None]
+    value, gots = lax.optimization_barrier((value, [item.held for item in old]))
+    sends = [item.take(got) for item, got in zip(old, gots)]
+    new = [item for item in running if item.held is None]
+    sends = sends + [item.begin for item in new]
+    value, sends = lax.optimization_barrier((value, sends))
+    for item, send in zip(old + new, sends):
+        if item.parts is None:
+            item.held = item.steps.send(send)
+    return value
 
 
 def place_of(n_dp, me, flip):
@@ -377,13 +425,13 @@
             grad = t_times(left, right).astype(bf16)
             own = lax.psum_scatter(grad, "fsdp", scatter_dimension=0, tiled=True)
             outs.append(lax.psum(own, "dp").astype(jnp.float32))
-        return outs
-
-    def total_small(self, terms, smalls):
+        return Ready(outs)
+
+    def total_small(self, smalls):
         own = lax.psum_scatter(
             smalls.astype(jnp.bfloat16), "fsdp", scatter_dimension=0, tiled=False
         )
-        return self.total(terms) + [lax.psum(own, "dp").astype(jnp.float32)]
+        return Ready(lax.psum(own, "dp").astype(jnp.float32))
 
 
 class Staged:
@@ -452,7 +500,7 @@
     def wide_columns(self, block):
         return column_order(block, self.send_table, block.shape[1] // (self.n_dp * self.n_line))
 
-    def total(self, terms, extra=None):
+    def total(self, terms):
         n_dp = self.n_dp
         n_line = self.n_line
         sides = []
@@ -462,32 +510,34 @@
                 half = left.shape[1] // 2
                 grad = t_times(left[:, side * half : (side + 1) * half], right).astype(jnp.bfloat16)
                 grads.append(grad.reshape(n_dp // 2, n_line, -1, right.shape[1]))
-            if extra is not None:
-                half = n_dp // 2
-                grads.append(extra[side * half : (side + 1) * half])
             sides.append(jnp.concatenate(grads, axis=3) if len(grads) > 1 else grads[0])
-        done = reduce_units(sides[0], sides[1], n_dp, n_line)
         cuts = [right.shape[1] for left, right in terms]
-        if extra is not None:
-            cuts.append(extra.shape[3])
-        return list(finish(done, self.owner.astype(jnp.int32), cuts))
-
-    def total_small(self, terms, smalls):
+        owner = self.owner.astype(jnp.int32)
+        steps = reduce_steps(sides[0], sides[1], n_dp, n_line)
+        return Reduction(steps, lambda parts: list(finish(parts, owner, cuts)))
+
+    def total_small(self, smalls):
         n_dp = self.n_dp
         n_line = self.n_line
         n_small, shard = smalls.shape[1:]
         per_dp = -(-n_small // n_dp)
-        size = self.unit
-        columns = -(-per_dp * shard // (size * TILE)) * TILE
         units = jnp.pad(smalls, ((0, 0), (0, per_dp * n_dp - n_small), (0, 0)))
         units = units.reshape(n_line * n_dp, per_dp * shard).astype(jnp.bfloat16)
-        units = jnp.pad(units, ((0, 0), (0, size * columns - per_dp * shard)))
+        size = -(-per_dp * shard // (16 * TILE)) * 16
+        units = jnp.pad(units, ((0, 0), (0, size * TILE - per_dp * shard)))
         ids = jnp.arange(n_line * n_dp, dtype=jnp.int32)
         choose = (self.send_table[:, None] == ids[None, :]).astype(jnp.bfloat16)
         units = jnp.dot(choose, units, preferred_element_type=jnp.float32).astype(jnp.bfloat16)
-        outs = self.total(terms, units.reshape(n_dp, n_line, size, columns))
-        small = outs[-1].reshape(n_dp, size * columns)[:, : per_dp * shard]
-        return outs[:-1] + [small.reshape(-1, shard)[:n_small]]
+        units = units.reshape(n_dp, n_line, size, TILE)
+        owner = self.owner.astype(jnp.int32)
+
+        def close(parts):
+            (small,) = finish(parts, owner, [TILE])
+            small = small.reshape(n_dp, size * TILE)[:, : per_dp * shard]
+            return small.reshape(-1, shard)[:n_small]
+
+        half = n_dp // 2
+        return Reduction(reduce_steps(units[half:], units[:half], n_dp, n_line), close)
 
 
 def per_device(
@@ -554,22 +604,27 @@
     block_out = jnp.where(valid[:, None], hidden_mid + branch_out, 0.0).astype(bf16)
     grad_out = jnp.where(valid[:, None], cotangent, jnp.zeros_like(cotangent))
 
-    (sum_fc2,) = plan.total([(plan.wide_columns(activated), grad_out)])
+    run_fc2 = plan.total([(plan.wide_columns(activated), grad_out)])
+    grad_out = tick(grad_out, [run_fc2])
     grad_pre = (times_t(grad_out, full_fc2) * slope.astype(f32)).astype(bf16)
     grad_fc1_bias = jnp.sum(grad_pre.astype(f32), axis=0)
-    (sum_fc1,) = plan.total([(plan.rows(normed_two), grad_pre)])
+    run_fc1 = plan.total([(plan.rows(normed_two), grad_pre)])
+    grad_pre = tick(grad_pre, [run_fc2, run_fc1])
     grad_norm_two = times_t(grad_pre, full_fc1)
     _, pull_two = jax.vjp(layer_norm, hidden_mid, gain_two, bias_two)
     back_mid, grad_gain_two, grad_bias_two = pull_two(grad_norm_two)
     grad_mid = grad_out.astype(f32) + back_mid
-    grad_branch = grad_mid.astype(bf16)
-    (sum_out,) = plan.total([(plan.rows(attn_rows), grad_branch)])
+    grad_branch = tick(grad_mid.astype(bf16), [run_fc2, run_fc1])
+    run_out = plan.total([(plan.rows(attn_rows), grad_branch)])
     grad_attn = times_t(grad_branch, full_out).astype(bf16)
+    grad_attn = tick(grad_attn, [run_fc2, run_fc1, run_out])
     grad_proj = attend_back(projected, grad_attn, segment)
+    run_qkv = plan.total([(plan.rows(normed_one), grad_proj)])
+    grad_proj = tick(grad_proj, [run_fc2, run_fc1, run_out, run_qkv])
     grad_norm_one = times_t(grad_proj, full_qkv)
     _, pull_one = jax.vjp(layer_norm, hidden_in, gain_one, bias_one)
     back_in, grad_gain_one, grad_bias_one = pull_one(grad_norm_one)
-    grad_in = grad_mid + back_in
+    grad_in = tick(grad_mid + back_in, [run_fc2, run_fc1, run_out, run_qkv])
     grad_table = jnp.dot(place.T, grad_in, precision=highest)
 
     def split(block):
@@ -583,7 +638,12 @@
         ],
         axis=1,
     )
-    sum_qkv, small = plan.total_small([(plan.rows(normed_one), grad_proj)], rows_small)
+    run_small = plan.total_small(rows_small)
+    (sum_fc2,) = run_fc2.result()
+    (sum_fc1,) = run_fc1.result()
+    (sum_out,) = run_out.result()
+    (sum_qkv,) = run_qkv.result()
+    small = run_small.result()
     return (
         block_out,
         grad_in.astype(bf16),

time: 1370 us -> 556 us (0.41)
  Pallas kernels: 963 us -> 94.5 us
  other arithmetic: 30.1 us -> 48.6 us
  starting transfers between devices: 63.8 us -> 78.8 us
    pallas_call x3, Pallas kernels: 769 us -> 22.9 us  [assemble(): pl.pallas_call(body, in_specs=[pl.BlockSpec(memory_space=pltpu.SMEM)] + [...]
    pallas_call x1, Pallas kernels: 129 us -> 5.38 us  [column_order(): pl.pallas_call(body, in_specs=[pl.BlockSpec(memory_space=pltpu.SMEM), pl....]
    ppermute x8 -> x25, starting transfers between devices: 6.96 us -> 27.8 us  [the longest x15 17.8 us: reduce_steps(): lax.ppermute(item, 'dp', hop_pairs(n_dp, stage))]
    convert_element_type x12 -> x17, other arithmetic: 10.5 us -> 30.6 us  [the longest x10 20.8 us: reduce_steps(): add_up([term[half:] for term in terms]).astype(jnp.bfloat16)]
    ppermute x21 -> x9, waiting for transfers between devices: 36.8 us -> 20.2 us  [spread(): lax.ppermute(item, 'dp', hop_pairs(n_dp, stage))]
    ppermute x8 -> x25, waiting for transfers between devices: 56.4 us -> 72.8 us  [the longest x10 59.3 us: reduce_steps(): got, = (yield [lax.ppermute(send, 'dp', hop_pairs(n_dp, stage))])]
    ppermute x21 -> x9, starting transfers between devices: 24.7 us -> 8.77 us  [spread(): lax.ppermute(item, 'dp', hop_pairs(n_dp, stage))]
    ppermute x21 -> x24, waiting for transfers between devices: 86.5 us -> 97.5 us  [ahead(): lax.ppermute(block, 'fsdp', [(i, (i + step) % n_line) for i in range(n_li...]
  transfers between devices with their start and end apart: 82 -> 95, of which waited for: 21 -> 32; matrix products, arithmetic and copies ran while one was open for 6% -> 23% of each run, Pallas kernels for 49% -> 17%
where the time goes in v3:
time: 556 us; the launch traced here: 551 us
  waiting for transfers between devices  192 us (35%)
  matrix products  100 us (18%)
  Pallas kernels  94.5 us (17%)
  starting transfers between devices  78.8 us (14%)
  other arithmetic  48.6 us (9%)
  local copies, waits for them, and re-layouts  34.9 us (6%)
    ppermute x24, waiting for transfers between devices, ahead(): lax.ppermute(block, 'fsdp', [(i, (i + step) % n_line) for i in range(n_li...  97.5 us
    ppermute x10, waiting for transfers between devices, reduce_steps(): got, = (yield [lax.ppermute(send, 'dp', hop_pairs(n_dp, stage))])  59.3 us
    pallas_call x1, Pallas kernels, attend_back(): pl.pallas_call(body, grid=(pairs,), in_specs=pair_specs(rows, pairs) + [p...  35.9 us
    ppermute x24, starting transfers between devices, ahead(): lax.ppermute(block, 'fsdp', [(i, (i + step) % n_line) for i in range(n_li...  35.7 us
    dot_general x4, matrix products, times_t(): lax.dot_general(left, right, (((1,), (1,)), ((), ())), preferred_element_...  28.1 us
    dot_general x8, matrix products, t_times(): lax.dot_general(left, right, (((0,), (0,)), ((), ())), preferred_element_...  26.3 us
    pallas_call x3, Pallas kernels, assemble(): pl.pallas_call(body, in_specs=[pl.BlockSpec(memory_space=pltpu.SMEM)] + [...  22.9 us
    convert_element_type x10, other arithmetic, reduce_steps(): add_up([term[half:] for term in terms]).astype(jnp.bfloat16)  20.8 us
  transfers between devices with their start and end apart: 95, of which 32 were waited for; matrix products, arithmetic and copies ran while one was open for 23% of the time, Pallas kernels for 17%

profile of v3, /device:TPU:0, one launch (start us, length us, event | category | flops | bytes accessed | tf_op | source)
XLA Modules:
  0.0 551.2 jit_solution(14293164629826817330)
XLA Ops:
  8.9 5.1 collective-permute-start.2
  21.6 2.3 collective-permute-done.2
  23.9 23.9 %collective-permute-done.1 = bf16[48,4096]{1,0:T(8,128)(2,1)S(1)} collective-permute-done((bf16[48,4096]{1,0:T(8,128)(2,1)}, bf16[48,4096]{1,0:T(8,128)(2,1)S(1)}, u32[]{:S(2)}, u32[]{:S(2)}) %collective-permute-start.1) | collective-permute-done | bytes 393248 | tf_op jit(solution)/shard_map/ppermute | solution.py:296
  52.9 2.9 collective-permute-start.11
  60.0 17.9 %collective-permute-done.11 = bf16[32,4096]{1,0:T(8,128)(2,1)S(1)} collective-permute-done((bf16[32,4096]{1,0:T(8,128)(2,1)S(1)}, bf16[32,4096]{1,0:T(8,128)(2,1)S(1)}, u32[]{:S(2)}, u32[]{:S(2)}) %collective-permute-start.11) | collective-permute-done | bytes 262176 | tf_op jit(solution)/shard_map/ppermute | solution.py:296
  79.5 6.2 %collective-permute-done.22 = bf16[128,1024]{1,0:T(8,128)(2,1)S(1)} collective-permute-done((bf16[128,1024]{1,0:T(8,128)(2,1)S(1)}, bf16[128,1024]{1,0:T(8,128)(2,1)S(1)}, u32[]{:S(2)}, u32[]{:S(2)}) %collective-permute-start.22) | collective-permute-done | bytes 262176 | tf_op jit(solution)/shard_map/ppermute | solution.py:296
  87.1 9.2 %collective-permute-done.21 = bf16[128,1024]{1,0:T(8,128)(2,1)S(1)} collective-permute-done((bf16[128,1024]{1,0:T(8,128)(2,1)S(1)}, bf16[128,1024]{1,0:T(8,128)(2,1)S(1)}, u32[]{:S(2)}, u32[]{:S(2)}) %collective-permute-start.21) | collective-permute-done | bytes 262176 | tf_op jit(solution)/shard_map/ppermute | solution.py:296
  96.4 2.5 fusion.111
  98.9 6.9 %collective-permute-done.20 = bf16[128,1024]{1,0:T(8,128)(2,1)S(1)} collective-permute-done((bf16[128,1024]{1,0:T(8,128)(2,1)S(1)}, bf16[128,1024]{1,0:T(8,128)(2,1)S(1)}, u32[]{:S(2)}, u32[]{:S(2)}) %collective-permute-start.20) | collective-permute-done | bytes 262176 | tf_op jit(solution)/shard_map/ppermute | solution.py:296
  110.6 7.5 %collective-permute-done.14.refs_3_ = bf16[1,3,32,4096]{3,2,1,0:T(8,128)(2,1)} collective-permute-done((bf16[1,3,32,4096]{3,2,1,0:T(8,128)(2,1)}, bf16[1,3,32,4096]{3,2,1,0:T(8,128)(2,1)}, u32[]{:S(2)}, u32[]{:S(2)}) %collective-permute-start.14) | collective-permute-done | bytes 786464 | tf_op jit(solution)/shard_map/ppermute | solution.py:306
  118.9 12.7 %collective-permute-done.15.refs_4_ = bf16[1,3,32,4096]{3,2,1,0:T(8,128)(2,1)} collective-permute-done((bf16[1,3,32,4096]{3,2,1,0:T(8,128)(2,1)}, bf16[1,3,32,4096]{3,2,1,0:T(8,128)(2,1)}, u32[]{:S(2)}, u32[]{:S(2)}) %collective-permute-start.15) | collective-permute-done | bytes 786464 | tf_op jit(solution)/shard_map/ppermute | solution.py:306
  133.0 7.7 %assemble.3 = (bf16[1024,3072]{1,0:T(8,128)(2,1)}, bf16[1024,1024]{1,0:T(8,128)(2,1)}) custom-call(s32[33]{0:T(128)} %pad_add_fusion.1.table_ref, bf16[256,3072]{1,0:T(8,128)(2,1)} %refs_0_.3, bf16[256,1024]{1,0:T(8,128)(2,1)} %refs_1_.1, bf16[1,3,32,4096]{3,2,1,0:T(8,128)(2,1)} %slice_bitcast_fusion.refs_2_, ...), custom_call_target="tpu_custom_call" | custom-call | tf_op jit(solution)/shard_map/assemble/pallas_call | solution.py:223
  140.7 7.8 %convolution_convert_fusion.4.refs_2_.refs_3_.refs_4_ = bf16[512,3072]{1,0:T(8,128)(2,1)} fusion(bf16[1024,3072]{1,0:T(8,128)(2,1)} %get-tuple-element.67, f32[512,1024]{1,0:T(8,128)S(1)} %get-tuple-element.160, f32[1024]{0:T(1024)S(1)} %bitcast.393, f32[1024]{0:T(1024)S(1)} %bitcast.385, f32[512]{0:T(512)S(1)} %fusion.100, f32[512]{0:T(512)S(1)} %broadcast_multiply_fusion.1), kind=kOutput, calls=%fused_computation.14 | convolution fusion | flops 3225419776 | bytes 11546624 | tf_op jit(solution)/shard_map/dot_general | solution.py:594
  148.5 15.8 %attend.1 = bf16[512,1024]{1,0:T(8,128)(2,1)} custom-call(s32[512,1]{1,0:T(8,128)} %fusion.59.refs_0_, s32[1,512]{1,0:T(1,128)} %broadcast_select_fusion.2.refs_1_, bf16[512,3072]{1,0:T(8,128)(2,1)} %convolution_convert_fusion.4.refs_2_.refs_3_.refs_4_, bf16[512,3072]{1,0:T(8,128)(2,1)} %convolution_convert_fusion.4.refs_2_.refs_3_.refs_4_, ...), custom_call_target="tpu_custom_call" | custom-call | tf_op jit(solution)/shard_map/attend/pallas_call | solution.py:148
  164.3 3.3 fusion.112
  171.4 7.6 %assemble.4 = bf16[1024,4096]{1,0:T(8,128)(2,1)} custom-call(s32[33]{0:T(128)} %pad_add_fusion.1.table_ref, bf16[256,4096]{1,0:T(8,128)(2,1)} %refs_0_.4, bf16[1,3,32,4096]{3,2,1,0:T(8,128)(2,1)} %bitcast.16.refs_1_, bf16[1,3,32,4096]{3,2,1,0:T(8,128)(2,1)} %collective-permute-done.13.refs_2_, bf16[1,3,32,4096]{3,2,1,0:T(8,128)(2,1)} %collective-permute-done.14.refs_3_, ...), custom_call_target="tpu_custom_call" | custom-call | tf_op jit(solution)/shard_map/assemble/pallas_call | solution.py:223
  179.0 11.4 %multiply_convert_fusion.1 = (bf16[512,4096]{1,0:T(8,128)(2,1)}, f32[512,4096]{1,0:T(8,128)}) fusion(f32[4096]{0:T(1024)S(1)} %bitcast.383, bf16[1024,4096]{1,0:T(8,128)(2,1)} %assemble.4, f32[512,1024]{1,0:T(8,128)} %copy-done.15, f32[1024]{0:T(1024)S(1)} %bitcast.395, f32[1024]{0:T(1024)S(1)} %bitcast.389, f32[512]{0:T(512)S(1)} %fusion.101, ...), kind=kOutput, calls=%fused_computation.8 | convolution fusion | flops 4310171648 | bytes 23097344 | tf_op jit(solution)/shard_map/dot_general | solution.py:598
  190.3 5.4 column_order.1
  195.7 6.0 %convolution_convert_fusion.6 = bf16[2048,1024]{1,0:T(8,128)(2,1)} fusion(bf16[512,1024]{1,0:T(8,128)(2,1)S(1)} %broadcast_select_fusion, bf16[512,4096]{1,0:T(8,128)(2,1)} %column_order.1), kind=kOutput, calls=%fused_computation.24 | convolution fusion | flops 2149580800 | bytes 7340032 | tf_op jit(solution)/shard_map/dot_general | solution.py:69
  203.0 4.2 fusion.22
  207.1 2.4 convolution_convert_fusion.5
  214.2 7.6 %assemble.5 = bf16[4096,1024]{1,0:T(8,128)(2,1)} custom-call(s32[33]{0:T(128)} %pad_add_fusion.1.table_ref, bf16[1024,1024]{1,0:T(8,128)(2,1)} %refs_0_.5, bf16[1,3,128,1024]{3,2,1,0:T(8,128)(2,1)} %maximum_bitcast_fusion.refs_1_, bf16[1,3,128,1024]{3,2,1,0:T(8,128)(2,1)} %collective-permute-done.23.refs_2_, ...), custom_call_target="tpu_custom_call" | custom-call | tf_op jit(solution)/shard_map/assemble/pallas_call | solution.py:223
  221.8 11.2 %fusion.113 = (bf16[4096]{0:T(1024)(128)(2,1)S(1)}, bf16[512,4096]{1,0:T(8,128)(2,1)S(1)}) fusion(f32[512,4096]{1,0:T(8,128)} %get-tuple-element.164, f32[4096]{0:T(1024)S(1)} %bitcast.384, bf16[512,1024]{1,0:T(8,128)(2,1)S(1)} %broadcast_select_fusion, bf16[4096,1024]{1,0:T(8,128)(2,1)} %assemble.5), kind=kOutput, calls=%fused_computation.369 | convolution fusion | flops 4324323328 | bytes 22044672 | tf_op jit(solution)/shard_map/dot_general | solution.py:65
  233.1 4.5 convolution_convert_fusion.1
  237.6 3.9 fusion.6
  242.7 2.5 convolution_convert_fusion
  247.8 6.7 %multiply_reduce_fusion = (bf16[1024]{0:T(1024)(128)(2,1)S(1)}, f32[512]{0:T(512)S(1)}, bf16[1024]{0:T(1024)(128)(2,1)S(1)}, f32[512,1024]{1,0:T(8,128)S(1)}) fusion(f32[512,1024]{1,0:T(8,128)} %copy-done.15, f32[512]{0:T(512)S(1)} %fusion.101, f32[512]{0:T(512)S(1)} %broadcast_multiply_fusion, f32[1024]{0:T(1024)S(1)} %bitcast.391, ...), kind=kOutput, calls=%fused_computation.38 | convolution fusion | flops 4299159040 | bytes 16791552 | tf_op jit(solution)/shard_map/dot_general | solution.py:65
  256.6 17.0 %collective-permute-done.31 = bf16[2,4,128,1024]{3,2,1,0:T(8,128)(2,1)} collective-permute-done((bf16[2,4,128,1024]{3,2,1,0:T(8,128)(2,1)}, bf16[2,4,128,1024]{3,2,1,0:T(8,128)(2,1)}, u32[]{:S(2)}, u32[]{:S(2)}) %collective-permute-start.31) | collective-permute-done | bytes 2097184 | tf_op jit(solution)/shard_map/ppermute | solution.py:324
  273.6 2.3 fusion.16
  275.9 2.6 fusion.5
  282.7 2.3 convolution_convert_fusion.8.refs_5_
  285.0 20.2 %collective-permute-done.33 = bf16[1,4,128,1024]{3,2,1,0:T(8,128)(2,1)S(1)} collective-permute-done((bf16[1,4,128,1024]{3,2,1,0:T(8,128)(2,1)S(1)}, bf16[1,4,128,1024]{3,2,1,0:T(8,128)(2,1)S(1)}, u32[]{:S(2)}, u32[]{:S(2)}) %collective-permute-start.33) | collective-permute-done | bytes 1048608 | tf_op jit(solution)/shard_map/ppermute | solution.py:324
  305.2 9.5 %collective-permute-done.34 = bf16[2,4,32,4096]{3,2,1,0:T(8,128)(2,1)S(1)} collective-permute-done((bf16[2,4,32,4096]{3,2,1,0:T(8,128)(2,1)S(1)}, bf16[2,4,32,4096]{3,2,1,0:T(8,128)(2,1)S(1)}, u32[]{:S(2)}, u32[]{:S(2)}) %collective-permute-start.34) | collective-permute-done | bytes 2097184 | tf_op jit(solution)/shard_map/ppermute | solution.py:324
  314.7 3.5 fusion.46
  318.3 2.7 fusion.14
  322.5 2.5 fusion.24
  325.8 35.9 %attend_back.1 = bf16[512,3072]{1,0:T(8,128)(2,1)} custom-call(s32[512,1]{1,0:T(8,128)} %fusion.59.refs_0_, s32[1,512]{1,0:T(1,128)} %broadcast_select_fusion.2.refs_1_, bf16[512,3072]{1,0:T(8,128)(2,1)} %convolution_convert_fusion.4.refs_2_.refs_3_.refs_4_, bf16[512,3072]{1,0:T(8,128)(2,1)} %convolution_convert_fusion.4.refs_2_.refs_3_.refs_4_, ...), custom_call_target="tpu_custom_call" | custom-call | tf_op jit(solution)/shard_map/attend_back/pallas_call | solution.py:166
  363.4 2.4 collective-permute-start.37
  365.8 5.5 %convolution_convert_fusion.3 = bf16[512,3072]{1,0:T(8,128)(2,1)} fusion(bf16[512,3072]{1,0:T(8,128)(2,1)} %attend_back.1, bf16[512,1024]{1,0:T(8,128)(2,1)S(1)} %copy-done.30), kind=kOutput, calls=%fused_computation.13 | convolution fusion | flops 1612185600 | bytes 6815744 | tf_op jit(solution)/shard_map/dot_general | solution.py:69
  373.1 10.3 %collective-permute-done.36 = bf16[128,1024]{1,0:T(8,128)(2,1)S(1)} collective-permute-done((bf16[128,1024]{1,0:T(8,128)(2,1)}, bf16[128,1024]{1,0:T(8,128)(2,1)S(1)}, u32[]{:S(2)}, u32[]{:S(2)}) %collective-permute-start.36) | collective-permute-done | bytes 262176 | tf_op jit(solution)/shard_map/ppermute | solution.py:296
  383.4 3.1 fusion.39
  386.6 2.2 fusion.26
  390.3 2.9 convolution_convert_fusion.2
  395.4 5.7 %collective-permute-start.41 = (bf16[32,4096]{1,0:T(8,128)(2,1)}, bf16[32,4096]{1,0:T(8,128)(2,1)}, u32[]{:S(2)}, u32[]{:S(2)}) collective-permute-start(bf16[32,4096]{1,0:T(8,128)(2,1)} %get-tuple-element.102), channel_id=1, source_target_pairs={{0,1},{1,2},{2,3},{3,0},{4,5},{5,6},{6,7},{7,4},{8,9},{9,10},{10,1... | collective-permute-start | bytes 786440 | tf_op jit(solution)/shard_map/ppermute | solution.py:296
  402.6 7.9 %multiply_reduce_fusion.1 = (bf16[1024]{0:T(1024)(128)(2,1)S(1)}, f32[512]{0:T(512)S(1)}, bf16[1024]{0:T(1024)(128)(2,1)S(1)}, f32[512,1024]{1,0:T(8,128)}) fusion(f32[512,1024]{1,0:T(8,128)S(1)} %copy-done.4, f32[512]{0:T(512)S(1)} %fusion.100, f32[512]{0:T(512)S(1)} %broadcast_multiply_fusion.1, f32[1024]{0:T(1024)S(1)} %bitcast.387, ...), kind=kOutput, calls=%fused_computation.39 | convolution fusion | flops 3225417216 | bytes 13645824 | tf_op jit(solution)/shard_map/dot_general | solution.py:65
  410.6 3.0 fusion.108
  413.7 2.7 collective-permute-start.43
  417.8 5.4 collective-permute-done.43
  425.1 3.3 fusion.10
  438.5 12.6 %collective-permute-done.47 = bf16[2,4,16,128]{3,2,1,0:T(8,128)(2,1)S(1)} collective-permute-done((bf16[2,4,16,128]{3,2,1,0:T(8,128)(2,1)S(1)}, bf16[2,4,16,128]{3,2,1,0:T(8,128)(2,1)S(1)}, u32[]{:S(2)}, u32[]{:S(2)}) %collective-permute-start.47) | collective-permute-done | bytes 32800 | tf_op jit(solution)/shard_map/ppermute | solution.py:324
  456.3 3.5 collective-permute-start.51
  461.1 3.2 collective-permute-done.50
  477.6 3.5 collective-permute-done.82.refs_1_
  481.2 2.2 collective-permute-start.90
  488.4 2.7 collective-permute-start.63
  497.4 2.2 collective-permute-done.75.refs_1_
  501.7 2.2 collective-permute-done.77.refs_3_
  504.4 4.7 collective-permute-done.62
  513.6 10.1 %select_convert_fusion = bf16[512,1024]{1,0:T(8,128)(2,1)} fusion(f32[512,1024]{1,0:T(8,128)S(1)} %copy-done.17, bf16[512,4096]{1,0:T(8,128)(2,1)} %get-tuple-element.163.in_ref, bf16[4096,1024]{1,0:T(8,128)(2,1)} %assemble.5, pred[512]{0:T(512)(128)(4,1)S(1)} %copy-done.79), kind=kOutput, calls=%fused_computation.47 | convolution fusion | flops 4296540160 | bytes 15729152 | tf_op jit(solution)/shard_map/dot_general | solution.py:603
  532.2 2.1 collective-permute-done.66.refs_3_
  535.6 2.1 finish.7
  537.7 3.8 finish.9
  542.3 3.8 finish.8
  547.6 3.3 finish.6
  (480 shorter events, 128.8 us)
Async XLA Ops:
  8.9 14.9 %collective-permute-start.2 = (bf16[48,4096]{1,0:T(8,128)(2,1)}, bf16[48,4096]{1,0:T(8,128)(2,1)S(1)}, u32[]{:S(2)}, u32[]{:S(2)}) collective-permute-start(bf16[48,4096]{1,0:T(8,128)(2,1)} %pad_maximum_fusion.3), channel_id=1, source_target_pairs={{0,3},{1,0},{2,1},{3,2},{4,7},{5,4},{6,5},{7,6},{8,11},{9,8},{10,9... | collective-permute-start | bytes 1179656 | tf_op jit(solution)/shard_map/ppermute | solution.py:296
  14.0 33.8 %collective-permute-start.1 = (bf16[48,4096]{1,0:T(8,128)(2,1)}, bf16[48,4096]{1,0:T(8,128)(2,1)S(1)}, u32[]{:S(2)}, u32[]{:S(2)}) collective-permute-start(bf16[48,4096]{1,0:T(8,128)(2,1)} %pad_maximum_fusion.3), channel_id=1, source_target_pairs={{0,2},{1,3},{2,0},{3,1},{4,6},{5,7},{6,4},{7,5},{8,10},{9,11},{10,... | collective-permute-start | bytes 1179656 | tf_op jit(solution)/shard_map/ppermute | solution.py:296
  14.0 33.8 %collective-permute-start = (bf16[48,4096]{1,0:T(8,128)(2,1)}, bf16[48,4096]{1,0:T(8,128)(2,1)}, u32[]{:S(2)}, u32[]{:S(2)}) collective-permute-start(bf16[48,4096]{1,0:T(8,128)(2,1)} %pad_maximum_fusion.3), channel_id=1, source_target_pairs={{0,1},{1,2},{2,3},{3,0},{4,5},{5,6},{6,7},{7,4},{8,9},{9,10},{10,1... | collective-permute-start | bytes 1179656 | tf_op jit(solution)/shard_map/ppermute | solution.py:296
  49.9 36.4 %collective-permute-start.3 = (bf16[1,3,32,4096]{3,2,1,0:T(8,128)(2,1)}, bf16[1,3,32,4096]{3,2,1,0:T(8,128)(2,1)}, u32[]{:S(2)}, u32[]{:S(2)}) collective-permute-start(bf16[1,3,32,4096]{3,2,1,0:T(8,128)(2,1)} %slice_bitcast_fusion.refs_2_), channel_id=1, source_target_pairs={{0,8},{4,20},{8,0},{12,28},{16,24},{20,4},{24,16},{28,12},{1,9},{5... | collective-permute-start | bytes 2359304 | tf_op jit(solution)/shard_map/ppermute | solution.py:306
  51.4 55.0 %collective-permute-start.4 = (bf16[1,3,32,4096]{3,2,1,0:T(8,128)(2,1)}, bf16[1,3,32,4096]{3,2,1,0:T(8,128)(2,1)}, u32[]{:S(2)}, u32[]{:S(2)}) collective-permute-start(bf16[1,3,32,4096]{3,2,1,0:T(8,128)(2,1)} %slice_bitcast_fusion.refs_2_), channel_id=1, source_target_pairs={{0,16},{4,12},{8,24},{12,4},{16,0},{20,28},{24,8},{28,20},{1,17},{... | collective-permute-start | bytes 2359304 | tf_op jit(solution)/shard_map/ppermute | solution.py:306
  52.9 24.9 %collective-permute-start.11 = (bf16[32,4096]{1,0:T(8,128)(2,1)S(1)}, bf16[32,4096]{1,0:T(8,128)(2,1)S(1)}, u32[]{:S(2)}, u32[]{:S(2)}) collective-permute-start(bf16[32,4096]{1,0:T(8,128)(2,1)S(1)} %constant_dynamic-slice_fusion.1), channel_id=1, source_target_pairs={{0,2},{1,3},{2,0},{3,1},{4,6},{5,7},{6,4},{7,5},{8,10},{9,11},{10,... | collective-permute-start | bytes 786440 | tf_op jit(solution)/shard_map/ppermute | solution.py:296
  55.8 22.0 %collective-permute-start.10 = (bf16[32,4096]{1,0:T(8,128)(2,1)S(1)}, bf16[32,4096]{1,0:T(8,128)(2,1)S(1)}, u32[]{:S(2)}, u32[]{:S(2)}) collective-permute-start(bf16[32,4096]{1,0:T(8,128)(2,1)S(1)} %constant_dynamic-slice_fusion.1), channel_id=1, source_target_pairs={{0,1},{1,2},{2,3},{3,0},{4,5},{5,6},{6,7},{7,4},{8,9},{9,10},{10,1... | collective-permute-start | bytes 786440 | tf_op jit(solution)/shard_map/ppermute | solution.py:296
  60.0 46.4 %collective-permute-start.6 = (bf16[1,3,32,4096]{3,2,1,0:T(8,128)(2,1)}, bf16[1,3,32,4096]{3,2,1,0:T(8,128)(2,1)}, u32[]{:S(2)}, u32[]{:S(2)}) collective-permute-start(bf16[1,3,32,4096]{3,2,1,0:T(8,128)(2,1)} %slice_bitcast_fusion.refs_2_), channel_id=1, source_target_pairs={{0,4},{4,0},{8,12},{12,8},{16,20},{20,16},{24,28},{28,24},{1,5},{5... | collective-permute-start | bytes 2359304 | tf_op jit(solution)/shard_map/ppermute | solution.py:292
  79.4 16.8 %collective-permute-start.21 = (bf16[128,1024]{1,0:T(8,128)(2,1)S(1)}, bf16[128,1024]{1,0:T(8,128)(2,1)S(1)}, u32[]{:S(2)}, u32[]{:S(2)}) collective-permute-start(bf16[128,1024]{1,0:T(8,128)(2,1)S(1)} %constant_dynamic-slice_fusion), channel_id=1, source_target_pairs={{0,2},{1,3},{2,0},{3,1},{4,6},{5,7},{6,4},{7,5},{8,10},{9,11},{10,... | collective-permute-start | bytes 786440 | tf_op jit(solution)/shard_map/ppermute | solution.py:296
  85.7 21.1 %collective-permute-start.13 = (bf16[1,3,32,4096]{3,2,1,0:T(8,128)(2,1)}, bf16[1,3,32,4096]{3,2,1,0:T(8,128)(2,1)}, u32[]{:S(2)}, u32[]{:S(2)}) collective-permute-start(bf16[1,3,32,4096]{3,2,1,0:T(8,128)(2,1)} %bitcast.16.refs_1_), channel_id=1, source_target_pairs={{0,8},{4,20},{8,0},{12,28},{16,24},{20,4},{24,16},{28,12},{1,9},{5... | collective-permute-start | bytes 2359304 | tf_op jit(solution)/shard_map/ppermute | solution.py:306
  86.3 22.1 %collective-permute-start.5 = (bf16[1,3,32,4096]{3,2,1,0:T(8,128)(2,1)}, bf16[1,3,32,4096]{3,2,1,0:T(8,128)(2,1)S(1)}, u32[]{:S(2)}, u32[]{:S(2)}) collective-permute-start(bf16[1,3,32,4096]{3,2,1,0:T(8,128)(2,1)} %collective-permute-done.3.refs_3_), channel_id=1, source_target_pairs={{0,16},{4,12},{8,24},{12,4},{16,0},{20,28},{24,8},{28,20},{1,17},{... | collective-permute-start | bytes 2359304 | tf_op jit(solution)/shard_map/ppermute | solution.py:306
  96.2 9.6 %collective-permute-start.20 = (bf16[128,1024]{1,0:T(8,128)(2,1)S(1)}, bf16[128,1024]{1,0:T(8,128)(2,1)S(1)}, u32[]{:S(2)}, u32[]{:S(2)}) collective-permute-start(bf16[128,1024]{1,0:T(8,128)(2,1)S(1)} %constant_dynamic-slice_fusion), channel_id=1, source_target_pairs={{0,1},{1,2},{2,3},{3,0},{4,5},{5,6},{6,7},{7,4},{8,9},{9,10},{10,1... | collective-permute-start | bytes 786440 | tf_op jit(solution)/shard_map/ppermute | solution.py:296
  105.8 12.3 %collective-permute-start.14 = (bf16[1,3,32,4096]{3,2,1,0:T(8,128)(2,1)}, bf16[1,3,32,4096]{3,2,1,0:T(8,128)(2,1)}, u32[]{:S(2)}, u32[]{:S(2)}) collective-permute-start(bf16[1,3,32,4096]{3,2,1,0:T(8,128)(2,1)} %bitcast.16.refs_1_), channel_id=1, source_target_pairs={{0,16},{4,12},{8,24},{12,4},{16,0},{20,28},{24,8},{28,20},{1,17},{... | collective-permute-start | bytes 2359304 | tf_op jit(solution)/shard_map/ppermute | solution.py:306
  106.3 11.8 %collective-permute-start.7 = (bf16[1,3,32,4096]{3,2,1,0:T(8,128)(2,1)}, bf16[1,3,32,4096]{3,2,1,0:T(8,128)(2,1)S(1)}, u32[]{:S(2)}, u32[]{:S(2)}) collective-permute-start(bf16[1,3,32,4096]{3,2,1,0:T(8,128)(2,1)} %collective-permute-done.3.refs_3_), channel_id=1, source_target_pairs={{0,4},{4,0},{8,12},{12,8},{16,20},{20,16},{24,28},{28,24},{1,5},{5... | collective-permute-start | bytes 2359304 | tf_op jit(solution)/shard_map/ppermute | solution.py:292
  106.3 12.4 %collective-permute-start.8 = (bf16[1,3,32,4096]{3,2,1,0:T(8,128)(2,1)}, bf16[1,3,32,4096]{3,2,1,0:T(8,128)(2,1)S(1)}, u32[]{:S(2)}, u32[]{:S(2)}) collective-permute-start(bf16[1,3,32,4096]{3,2,1,0:T(8,128)(2,1)} %collective-permute-done.4.refs_4_), channel_id=1, source_target_pairs={{0,4},{4,0},{8,12},{12,8},{16,20},{20,16},{24,28},{28,24},{1,5},{5... | collective-permute-start | bytes 2359304 | tf_op jit(solution)/shard_map/ppermute | solution.py:292
  106.9 24.7 %collective-permute-start.15 = (bf16[1,3,32,4096]{3,2,1,0:T(8,128)(2,1)}, bf16[1,3,32,4096]{3,2,1,0:T(8,128)(2,1)}, u32[]{:S(2)}, u32[]{:S(2)}) collective-permute-start(bf16[1,3,32,4096]{3,2,1,0:T(8,128)(2,1)} %collective-permute-done.13.refs_2_), channel_id=1, source_target_pairs={{0,16},{4,12},{8,24},{12,4},{16,0},{20,28},{24,8},{28,20},{1,17},{... | collective-permute-start | bytes 2359304 | tf_op jit(solution)/shard_map/ppermute | solution.py:306
  109.3 22.3 %collective-permute-start.9 = (bf16[1,3,32,4096]{3,2,1,0:T(8,128)(2,1)S(1)}, bf16[1,3,32,4096]{3,2,1,0:T(8,128)(2,1)S(1)}, u32[]{:S(2)}, u32[]{:S(2)}) collective-permute-start(bf16[1,3,32,4096]{3,2,1,0:T(8,128)(2,1)S(1)} %collective-permute-done.5.refs_5_), channel_id=1, source_target_pairs={{0,4},{4,0},{8,12},{12,8},{16,20},{20,16},{24,28},{28,24},{1,5},{5... | collective-permute-start | bytes 2359304 | tf_op jit(solution)/shard_map/ppermute | solution.py:292
  118.1 51.1 %collective-permute-start.16 = (bf16[1,3,32,4096]{3,2,1,0:T(8,128)(2,1)}, bf16[1,3,32,4096]{3,2,1,0:T(8,128)(2,1)}, u32[]{:S(2)}, u32[]{:S(2)}) collective-permute-start(bf16[1,3,32,4096]{3,2,1,0:T(8,128)(2,1)} %bitcast.16.refs_1_), channel_id=1, source_target_pairs={{0,4},{4,0},{8,12},{12,8},{16,20},{20,16},{24,28},{28,24},{1,5},{5... | collective-permute-start | bytes 2359304 | tf_op jit(solution)/shard_map/ppermute | solution.py:292
  118.1 51.7 %collective-permute-start.23 = (bf16[1,3,128,1024]{3,2,1,0:T(8,128)(2,1)}, bf16[1,3,128,1024]{3,2,1,0:T(8,128)(2,1)}, u32[]{:S(2)}, u32[]{:S(2)}) collective-permute-start(bf16[1,3,128,1024]{3,2,1,0:T(8,128)(2,1)} %maximum_bitcast_fusion.refs_1_), channel_id=1, source_target_pairs={{0,8},{4,20},{8,0},{12,28},{16,24},{20,4},{24,16},{28,12},{1,9},{5... | collective-permute-start | bytes 2359304 | tf_op jit(solution)/shard_map/ppermute | solution.py:306
  118.7 52.6 %collective-permute-start.17 = (bf16[1,3,32,4096]{3,2,1,0:T(8,128)(2,1)}, bf16[1,3,32,4096]{3,2,1,0:T(8,128)(2,1)}, u32[]{:S(2)}, u32[]{:S(2)}) collective-permute-start(bf16[1,3,32,4096]{3,2,1,0:T(8,128)(2,1)} %collective-permute-done.13.refs_2_), channel_id=1, source_target_pairs={{0,4},{4,0},{8,12},{12,8},{16,20},{20,16},{24,28},{28,24},{1,5},{5... | collective-permute-start | bytes 2359304 | tf_op jit(solution)/shard_map/ppermute | solution.py:292
  131.6 39.8 %collective-permute-start.18 = (bf16[1,3,32,4096]{3,2,1,0:T(8,128)(2,1)}, bf16[1,3,32,4096]{3,2,1,0:T(8,128)(2,1)}, u32[]{:S(2)}, u32[]{:S(2)}) collective-permute-start(bf16[1,3,32,4096]{3,2,1,0:T(8,128)(2,1)} %collective-permute-done.14.refs_3_), channel_id=1, source_target_pairs={{0,4},{4,0},{8,12},{12,8},{16,20},{20,16},{24,28},{28,24},{1,5},{5... | collective-permute-start | bytes 2359304 | tf_op jit(solution)/shard_map/ppermute | solution.py:292
  132.5 38.9 %collective-permute-start.19 = (bf16[1,3,32,4096]{3,2,1,0:T(8,128)(2,1)}, bf16[1,3,32,4096]{3,2,1,0:T(8,128)(2,1)}, u32[]{:S(2)}, u32[]{:S(2)}) collective-permute-start(bf16[1,3,32,4096]{3,2,1,0:T(8,128)(2,1)} %collective-permute-done.15.refs_4_), channel_id=1, source_target_pairs={{0,4},{4,0},{8,12},{12,8},{16,20},{20,16},{24,28},{28,24},{1,5},{5... | collective-permute-start | bytes 2359304 | tf_op jit(solution)/shard_map/ppermute | solution.py:292
  169.3 33.2 %collective-permute-start.24 = (bf16[1,3,128,1024]{3,2,1,0:T(8,128)(2,1)}, bf16[1,3,128,1024]{3,2,1,0:T(8,128)(2,1)}, u32[]{:S(2)}, u32[]{:S(2)}) collective-permute-start(bf16[1,3,128,1024]{3,2,1,0:T(8,128)(2,1)} %maximum_bitcast_fusion.refs_1_), channel_id=1, source_target_pairs={{0,16},{4,12},{8,24},{12,4},{16,0},{20,28},{24,8},{28,20},{1,17},{... | collective-permute-start | bytes 2359304 | tf_op jit(solution)/shard_map/ppermute | solution.py:306
  169.8 33.0 %collective-permute-start.25 = (bf16[1,3,128,1024]{3,2,1,0:T(8,128)(2,1)}, bf16[1,3,128,1024]{3,2,1,0:T(8,128)(2,1)}, u32[]{:S(2)}, u32[]{:S(2)}) collective-permute-start(bf16[1,3,128,1024]{3,2,1,0:T(8,128)(2,1)} %collective-permute-done.23.refs_2_), channel_id=1, source_target_pairs={{0,16},{4,12},{8,24},{12,4},{16,0},{20,28},{24,8},{28,20},{1,17},{... | collective-permute-start | bytes 2359304 | tf_op jit(solution)/shard_map/ppermute | solution.py:306
  201.7 35.9 %collective-permute-start.30 = (bf16[4,4,128,1024]{3,2,1,0:T(8,128)(2,1)}, bf16[4,4,128,1024]{3,2,1,0:T(8,128)(2,1)}, u32[]{:S(2)}, u32[]{:S(2)}) collective-permute-start(bf16[4,4,128,1024]{3,2,1,0:T(8,128)(2,1)} %bitcast.21), channel_id=1, source_target_pairs={{0,4},{4,0},{8,12},{12,8},{16,20},{20,16},{24,28},{28,24},{1,5},{5... | collective-permute-start | bytes 12582920 | tf_op jit(solution)/shard_map/ppermute | solution.py:292
  201.9 9.7 %collective-permute-start.26 = (bf16[1,3,128,1024]{3,2,1,0:T(8,128)(2,1)}, bf16[1,3,128,1024]{3,2,1,0:T(8,128)(2,1)S(1)}, u32[]{:S(2)}, u32[]{:S(2)}) collective-permute-start(bf16[1,3,128,1024]{3,2,1,0:T(8,128)(2,1)} %maximum_bitcast_fusion.refs_1_), channel_id=1, source_target_pairs={{0,4},{4,0},{8,12},{12,8},{16,20},{20,16},{24,28},{28,24},{1,5},{5... | collective-permute-start | bytes 2359304 | tf_op jit(solution)/shard_map/ppermute | solution.py:292
  202.4 10.0 %collective-permute-start.27 = (bf16[1,3,128,1024]{3,2,1,0:T(8,128)(2,1)}, bf16[1,3,128,1024]{3,2,1,0:T(8,128)(2,1)S(1)}, u32[]{:S(2)}, u32[]{:S(2)}) collective-permute-start(bf16[1,3,128,1024]{3,2,1,0:T(8,128)(2,1)} %collective-permute-done.23.refs_2_), channel_id=1, source_target_pairs={{0,4},{4,0},{8,12},{12,8},{16,20},{20,16},{24,28},{28,24},{1,5},{5... | collective-permute-start | bytes 2359304 | tf_op jit(solution)/shard_map/ppermute | solution.py:292
  202.4 10.9 %collective-permute-start.28 = (bf16[1,3,128,1024]{3,2,1,0:T(8,128)(2,1)}, bf16[1,3,128,1024]{3,2,1,0:T(8,128)(2,1)S(1)}, u32[]{:S(2)}, u32[]{:S(2)}) collective-permute-start(bf16[1,3,128,1024]{3,2,1,0:T(8,128)(2,1)} %collective-permute-done.24.refs_3_), channel_id=1, source_target_pairs={{0,4},{4,0},{8,12},{12,8},{16,20},{20,16},{24,28},{28,24},{1,5},{5... | collective-permute-start | bytes 2359304 | tf_op jit(solution)/shard_map/ppermute | solution.py:292
  202.9 11.3 %collective-permute-start.29 = (bf16[1,3,128,1024]{3,2,1,0:T(8,128)(2,1)}, bf16[1,3,128,1024]{3,2,1,0:T(8,128)(2,1)}, u32[]{:S(2)}, u32[]{:S(2)}) collective-permute-start(bf16[1,3,128,1024]{3,2,1,0:T(8,128)(2,1)} %collective-permute-done.25.refs_4_), channel_id=1, source_target_pairs={{0,4},{4,0},{8,12},{12,8},{16,20},{20,16},{24,28},{28,24},{1,5},{5... | collective-permute-start | bytes 2359304 | tf_op jit(solution)/shard_map/ppermute | solution.py:292
  241.5 32.1 %collective-permute-start.32 = (bf16[4,4,32,4096]{3,2,1,0:T(8,128)(2,1)}, bf16[4,4,32,4096]{3,2,1,0:T(8,128)(2,1)}, u32[]{:S(2)}, u32[]{:S(2)}) collective-permute-start(bf16[4,4,32,4096]{3,2,1,0:T(8,128)(2,1)} %bitcast.23), channel_id=1, source_target_pairs={{0,4},{4,0},{8,12},{12,8},{16,20},{20,16},{24,28},{28,24},{1,5},{5... | collective-permute-start | bytes 12582920 | tf_op jit(solution)/shard_map/ppermute | solution.py:292
  247.2 26.4 %collective-permute-start.31 = (bf16[2,4,128,1024]{3,2,1,0:T(8,128)(2,1)}, bf16[2,4,128,1024]{3,2,1,0:T(8,128)(2,1)}, u32[]{:S(2)}, u32[]{:S(2)}) collective-permute-start(bf16[2,4,128,1024]{3,2,1,0:T(8,128)(2,1)} %fusion.6), channel_id=1, source_target_pairs={{0,8},{4,20},{8,0},{12,28},{16,24},{20,4},{24,16},{28,12},{1,9},{5... | collective-permute-start | bytes 6291464 | tf_op jit(solution)/shard_map/ppermute | solution.py:324
  278.5 36.2 %collective-permute-start.34 = (bf16[2,4,32,4096]{3,2,1,0:T(8,128)(2,1)S(1)}, bf16[2,4,32,4096]{3,2,1,0:T(8,128)(2,1)S(1)}, u32[]{:S(2)}, u32[]{:S(2)}) collective-permute-start(bf16[2,4,32,4096]{3,2,1,0:T(8,128)(2,1)S(1)} %fusion.5), channel_id=1, source_target_pairs={{0,8},{4,20},{8,0},{12,28},{16,24},{20,4},{24,16},{28,12},{1,9},{5... | collective-permute-start | bytes 6291464 | tf_op jit(solution)/shard_map/ppermute | solution.py:324
  279.2 26.0 %collective-permute-start.33 = (bf16[1,4,128,1024]{3,2,1,0:T(8,128)(2,1)S(1)}, bf16[1,4,128,1024]{3,2,1,0:T(8,128)(2,1)S(1)}, u32[]{:S(2)}, u32[]{:S(2)}) collective-permute-start(bf16[1,4,128,1024]{3,2,1,0:T(8,128)(2,1)S(1)} %fusion.16), channel_id=1, source_target_pairs={{0,16},{4,12},{8,24},{12,4},{16,0},{20,28},{24,8},{28,20},{1,17},{... | collective-permute-start | bytes 3145736 | tf_op jit(solution)/shard_map/ppermute | solution.py:324
  320.9 62.5 %collective-permute-start.38 = (bf16[1,4,32,4096]{3,2,1,0:T(8,128)(2,1)}, bf16[1,4,32,4096]{3,2,1,0:T(8,128)(2,1)}, u32[]{:S(2)}, u32[]{:S(2)}) collective-permute-start(bf16[1,4,32,4096]{3,2,1,0:T(8,128)(2,1)} %fusion.14), channel_id=1, source_target_pairs={{0,16},{4,12},{8,24},{12,4},{16,0},{20,28},{24,8},{28,20},{1,17},{... | collective-permute-start | bytes 3145736 | tf_op jit(solution)/shard_map/ppermute | solution.py:324
  322.5 60.9 %collective-permute-start.39 = (bf16[4,4,32,1024]{3,2,1,0:T(8,128)(2,1)}, bf16[4,4,32,1024]{3,2,1,0:T(8,128)(2,1)S(1)}, u32[]{:S(2)}, u32[]{:S(2)}) collective-permute-start(bf16[4,4,32,1024]{3,2,1,0:T(8,128)(2,1)} %bitcast.36), channel_id=1, source_target_pairs={{0,4},{4,0},{8,12},{12,8},{16,20},{20,16},{24,28},{28,24},{1,5},{5... | collective-permute-start | bytes 3145736 | tf_op jit(solution)/shard_map/ppermute | solution.py:292
  361.7 11.4 %collective-permute-start.35 = (bf16[128,1024]{1,0:T(8,128)(2,1)}, bf16[128,1024]{1,0:T(8,128)(2,1)S(1)}, u32[]{:S(2)}, u32[]{:S(2)}) collective-permute-start(bf16[128,1024]{1,0:T(8,128)(2,1)} %get-tuple-element.89), channel_id=1, source_target_pairs={{0,1},{1,2},{2,3},{3,0},{4,5},{5,6},{6,7},{7,4},{8,9},{9,10},{10,1... | collective-permute-start | bytes 786440 | tf_op jit(solution)/shard_map/ppermute | solution.py:296
  361.8 21.6 %collective-permute-start.36 = (bf16[128,1024]{1,0:T(8,128)(2,1)}, bf16[128,1024]{1,0:T(8,128)(2,1)S(1)}, u32[]{:S(2)}, u32[]{:S(2)}) collective-permute-start(bf16[128,1024]{1,0:T(8,128)(2,1)} %get-tuple-element.90), channel_id=1, source_target_pairs={{0,2},{1,3},{2,0},{3,1},{4,6},{5,7},{6,4},{7,5},{8,10},{9,11},{10,... | collective-permute-start | bytes 786440 | tf_op jit(solution)/shard_map/ppermute | solution.py:296
  363.4 20.1 %collective-permute-start.37 = (bf16[128,1024]{1,0:T(8,128)(2,1)S(1)}, bf16[128,1024]{1,0:T(8,128)(2,1)S(1)}, u32[]{:S(2)}, u32[]{:S(2)}) collective-permute-start(bf16[128,1024]{1,0:T(8,128)(2,1)S(1)} %get-tuple-element.91), channel_id=1, source_target_pairs={{0,3},{1,0},{2,1},{3,2},{4,7},{5,4},{6,5},{7,6},{8,11},{9,8},{10,9... | collective-permute-start | bytes 786440 | tf_op jit(solution)/shard_map/ppermute | solution.py:296
  390.2 33.1 %collective-permute-start.45 = (bf16[4,4,32,3072]{3,2,1,0:T(8,128)(2,1)}, bf16[4,4,32,3072]{3,2,1,0:T(8,128)(2,1)}, u32[]{:S(2)}, u32[]{:S(2)}) collective-permute-start(bf16[4,4,32,3072]{3,2,1,0:T(8,128)(2,1)} %bitcast.51), channel_id=1, source_target_pairs={{0,4},{4,0},{8,12},{12,8},{16,20},{20,16},{24,28},{28,24},{1,5},{5... | collective-permute-start | bytes 9437192 | tf_op jit(solution)/shard_map/ppermute | solution.py:292
  394.9 18.8 %collective-permute-start.40 = (bf16[1,128,1024]{2,1,0:T(8,128)(2,1)S(1)}, bf16[1,128,1024]{2,1,0:T(8,128)(2,1)}, u32[]{:S(2)}, u32[]{:S(2)}) collective-permute-start(bf16[1,128,1024]{2,1,0:T(8,128)(2,1)S(1)} %fusion.64.refs_0_), channel_id=1, source_target_pairs={{0,8},{4,20},{8,0},{12,28},{16,24},{20,4},{24,16},{28,12},{1,9},{5... | collective-permute-start | bytes 786440 | tf_op jit(solution)/shard_map/ppermute | solution.py:335
  395.4 21.5 %collective-permute-start.41 = (bf16[32,4096]{1,0:T(8,128)(2,1)}, bf16[32,4096]{1,0:T(8,128)(2,1)}, u32[]{:S(2)}, u32[]{:S(2)}) collective-permute-start(bf16[32,4096]{1,0:T(8,128)(2,1)} %get-tuple-element.102), channel_id=1, source_target_pairs={{0,1},{1,2},{2,3},{3,0},{4,5},{5,6},{6,7},{7,4},{8,9},{9,10},{10,1... | collective-permute-start | bytes 786440 | tf_op jit(solution)/shard_map/ppermute | solution.py:296
  401.1 16.7 %collective-permute-start.42 = (bf16[32,4096]{1,0:T(8,128)(2,1)}, bf16[32,4096]{1,0:T(8,128)(2,1)}, u32[]{:S(2)}, u32[]{:S(2)}) collective-permute-start(bf16[32,4096]{1,0:T(8,128)(2,1)} %get-tuple-element.103), channel_id=1, source_target_pairs={{0,2},{1,3},{2,0},{3,1},{4,6},{5,7},{6,4},{7,5},{8,10},{9,11},{10,... | collective-permute-start | bytes 786440 | tf_op jit(solution)/shard_map/ppermute | solution.py:296
  401.1 22.1 %collective-permute-start.44 = (bf16[2,4,32,1024]{3,2,1,0:T(8,128)(2,1)}, bf16[2,4,32,1024]{3,2,1,0:T(8,128)(2,1)}, u32[]{:S(2)}, u32[]{:S(2)}) collective-permute-start(bf16[2,4,32,1024]{3,2,1,0:T(8,128)(2,1)} %fusion.26), channel_id=1, source_target_pairs={{0,8},{4,20},{8,0},{12,28},{16,24},{20,4},{24,16},{28,12},{1,9},{5... | collective-permute-start | bytes 1572872 | tf_op jit(solution)/shard_map/ppermute | solution.py:324
  413.7 9.5 %collective-permute-start.43 = (bf16[32,4096]{1,0:T(8,128)(2,1)S(1)}, bf16[32,4096]{1,0:T(8,128)(2,1)S(1)}, u32[]{:S(2)}, u32[]{:S(2)}) collective-permute-start(bf16[32,4096]{1,0:T(8,128)(2,1)S(1)} %copy-done.52), channel_id=1, source_target_pairs={{0,3},{1,0},{2,1},{3,2},{4,7},{5,4},{6,5},{7,6},{8,11},{9,8},{10,9... | collective-permute-start | bytes 786440 | tf_op jit(solution)/shard_map/ppermute | solution.py:296
  430.0 22.2 %collective-permute-start.59 = (bf16[2,4,32,3072]{3,2,1,0:T(8,128)(2,1)}, bf16[2,4,32,3072]{3,2,1,0:T(8,128)(2,1)}, u32[]{:S(2)}, u32[]{:S(2)}) collective-permute-start(bf16[2,4,32,3072]{3,2,1,0:T(8,128)(2,1)} %fusion.10), channel_id=1, source_target_pairs={{0,8},{4,20},{8,0},{12,28},{16,24},{20,4},{24,16},{28,12},{1,9},{5... | collective-permute-start | bytes 4718600 | tf_op jit(solution)/shard_map/ppermute | solution.py:324
  437.0 14.1 %collective-permute-start.47 = (bf16[2,4,16,128]{3,2,1,0:T(8,128)(2,1)S(1)}, bf16[2,4,16,128]{3,2,1,0:T(8,128)(2,1)S(1)}, u32[]{:S(2)}, u32[]{:S(2)}) collective-permute-start(bf16[2,4,16,128]{3,2,1,0:T(8,128)(2,1)S(1)} %add_convert_fusion.2), channel_id=1, source_target_pairs={{0,8},{4,20},{8,0},{12,28},{16,24},{20,4},{24,16},{28,12},{1,9},{5... | collective-permute-start | bytes 98312 | tf_op jit(solution)/shard_map/ppermute | solution.py:324
  454.1 31.2 %collective-permute-start.60 = (bf16[1,4,32,3072]{3,2,1,0:T(8,128)(2,1)S(1)}, bf16[1,4,32,3072]{3,2,1,0:T(8,128)(2,1)S(1)}, u32[]{:S(2)}, u32[]{:S(2)}) collective-permute-start(bf16[1,4,32,3072]{3,2,1,0:T(8,128)(2,1)S(1)} %fusion.21), channel_id=1, source_target_pairs={{0,16},{4,12},{8,24},{12,4},{16,0},{20,28},{24,8},{28,20},{1,17},{... | collective-permute-start | bytes 2359304 | tf_op jit(solution)/shard_map/ppermute | solution.py:324
  455.2 19.6 %collective-permute-start.71 = (bf16[1,4,32,1024]{3,2,1,0:T(8,128)(2,1)S(1)}, bf16[1,4,32,1024]{3,2,1,0:T(8,128)(2,1)S(1)}, u32[]{:S(2)}, u32[]{:S(2)}) collective-permute-start(bf16[1,4,32,1024]{3,2,1,0:T(8,128)(2,1)S(1)} %copy-done.48), channel_id=1, source_target_pairs={{0,16},{4,12},{8,24},{12,4},{16,0},{20,28},{24,8},{28,20},{1,17},{... | collective-permute-start | bytes 786440 | tf_op jit(solution)/shard_map/ppermute | solution.py:324
  474.8 9.7 %collective-permute-start.89 = (bf16[1,128,1024]{2,1,0:T(8,128)(2,1)S(1)}, bf16[1,128,1024]{2,1,0:T(8,128)(2,1)}, u32[]{:S(2)}, u32[]{:S(2)}) collective-permute-start(bf16[1,128,1024]{2,1,0:T(8,128)(2,1)S(1)} %fusion.64.refs_0_), channel_id=1, source_target_pairs={{0,16},{4,12},{8,24},{12,4},{16,0},{20,28},{24,8},{28,20},{1,17},{... | collective-permute-start | bytes 786440 | tf_op jit(solution)/shard_map/ppermute | solution.py:335
  481.1 14.2 %collective-permute-start.91 = (bf16[1,128,1024]{2,1,0:T(8,128)(2,1)S(1)}, bf16[1,128,1024]{2,1,0:T(8,128)(2,1)S(1)}, u32[]{:S(2)}, u32[]{:S(2)}) collective-permute-start(bf16[1,128,1024]{2,1,0:T(8,128)(2,1)S(1)} %fusion.64.refs_0_), channel_id=1, source_target_pairs={{0,4},{4,0},{8,12},{12,8},{16,20},{20,16},{24,28},{28,24},{1,5},{5... | collective-permute-start | bytes 786440 | tf_op jit(solution)/shard_map/ppermute | solution.py:292
  488.4 15.5 %collective-permute-start.63 = (bf16[32,3072]{1,0:T(8,128)(2,1)S(1)}, bf16[32,3072]{1,0:T(8,128)(2,1)S(1)}, u32[]{:S(2)}, u32[]{:S(2)}) collective-permute-start(bf16[32,3072]{1,0:T(8,128)(2,1)S(1)} %get-tuple-element.137), channel_id=1, source_target_pairs={{0,3},{1,0},{2,1},{3,2},{4,7},{5,4},{6,5},{7,6},{8,11},{9,8},{10,9... | collective-permute-start | bytes 589832 | tf_op jit(solution)/shard_map/ppermute | solution.py:296
  492.3 16.9 %collective-permute-start.62 = (bf16[32,3072]{1,0:T(8,128)(2,1)S(1)}, bf16[32,3072]{1,0:T(8,128)(2,1)S(1)}, u32[]{:S(2)}, u32[]{:S(2)}) collective-permute-start(bf16[32,3072]{1,0:T(8,128)(2,1)S(1)} %get-tuple-element.138), channel_id=1, source_target_pairs={{0,2},{1,3},{2,0},{3,1},{4,6},{5,7},{6,4},{7,5},{8,10},{9,11},{10,... | collective-permute-start | bytes 589832 | tf_op jit(solution)/shard_map/ppermute | solution.py:296
  492.3 16.9 %collective-permute-start.61 = (bf16[32,3072]{1,0:T(8,128)(2,1)S(1)}, bf16[32,3072]{1,0:T(8,128)(2,1)S(1)}, u32[]{:S(2)}, u32[]{:S(2)}) collective-permute-start(bf16[32,3072]{1,0:T(8,128)(2,1)S(1)} %get-tuple-element.136), channel_id=1, source_target_pairs={{0,1},{1,2},{2,3},{3,0},{4,5},{5,6},{6,7},{7,4},{8,9},{9,10},{10,1... | collective-permute-start | bytes 589832 | tf_op jit(solution)/shard_map/ppermute | solution.py:296
  500.5 11.6 %collective-permute-start.84 = (bf16[1,32,4096]{2,1,0:T(8,128)(2,1)S(1)}, bf16[1,32,4096]{2,1,0:T(8,128)(2,1)S(1)}, u32[]{:S(2)}, u32[]{:S(2)}) collective-permute-start(bf16[1,32,4096]{2,1,0:T(8,128)(2,1)S(1)} %collective-permute-done.82.refs_1_), channel_id=1, source_target_pairs={{0,16},{4,12},{8,24},{12,4},{16,0},{20,28},{24,8},{28,20},{1,17},{... | collective-permute-start | bytes 786440 | tf_op jit(solution)/shard_map/ppermute | solution.py:335
  510.9 15.4 %collective-permute-start.86 = (bf16[1,32,4096]{2,1,0:T(8,128)(2,1)S(1)}, bf16[1,32,4096]{2,1,0:T(8,128)(2,1)}, u32[]{:S(2)}, u32[]{:S(2)}) collective-permute-start(bf16[1,32,4096]{2,1,0:T(8,128)(2,1)S(1)} %collective-permute-done.82.refs_1_), channel_id=1, source_target_pairs={{0,4},{4,0},{8,12},{12,8},{16,20},{20,16},{24,28},{28,24},{1,5},{5... | collective-permute-start | bytes 786440 | tf_op jit(solution)/shard_map/ppermute | solution.py:292
  511.0 15.4 %collective-permute-start.87 = (bf16[1,32,4096]{2,1,0:T(8,128)(2,1)S(1)}, bf16[1,32,4096]{2,1,0:T(8,128)(2,1)}, u32[]{:S(2)}, u32[]{:S(2)}) collective-permute-start(bf16[1,32,4096]{2,1,0:T(8,128)(2,1)S(1)} %collective-permute-done.83.refs_2_), channel_id=1, source_target_pairs={{0,4},{4,0},{8,12},{12,8},{16,20},{20,16},{24,28},{28,24},{1,5},{5... | collective-permute-start | bytes 786440 | tf_op jit(solution)/shard_map/ppermute | solution.py:292
  511.6 19.8 %collective-permute-start.93 = (bf16[1,128,1024]{2,1,0:T(8,128)(2,1)}, bf16[1,128,1024]{2,1,0:T(8,128)(2,1)}, u32[]{:S(2)}, u32[]{:S(2)}) collective-permute-start(bf16[1,128,1024]{2,1,0:T(8,128)(2,1)} %collective-permute-done.89.refs_2_), channel_id=1, source_target_pairs={{0,4},{4,0},{8,12},{12,8},{16,20},{20,16},{24,28},{28,24},{1,5},{5... | collective-permute-start | bytes 786440 | tf_op jit(solution)/shard_map/ppermute | solution.py:292
  511.7 19.8 %collective-permute-start.94 = (bf16[1,128,1024]{2,1,0:T(8,128)(2,1)}, bf16[1,128,1024]{2,1,0:T(8,128)(2,1)}, u32[]{:S(2)}, u32[]{:S(2)}) collective-permute-start(bf16[1,128,1024]{2,1,0:T(8,128)(2,1)} %collective-permute-done.90.refs_3_), channel_id=1, source_target_pairs={{0,4},{4,0},{8,12},{12,8},{16,20},{20,16},{24,28},{28,24},{1,5},{5... | collective-permute-start | bytes 786440 | tf_op jit(solution)/shard_map/ppermute | solution.py:292
  512.3 15.0 %collective-permute-start.64 = (bf16[1,32,3072]{2,1,0:T(8,128)(2,1)S(1)}, bf16[1,32,3072]{2,1,0:T(8,128)(2,1)}, u32[]{:S(2)}, u32[]{:S(2)}) collective-permute-start(bf16[1,32,3072]{2,1,0:T(8,128)(2,1)S(1)} %fusion.71.refs_0_), channel_id=1, source_target_pairs={{0,8},{4,20},{8,0},{12,28},{16,24},{20,4},{24,16},{28,12},{1,9},{5... | collective-permute-start | bytes 589832 | tf_op jit(solution)/shard_map/ppermute | solution.py:335
  526.4 15.2 %collective-permute-start.88 = (bf16[1,32,4096]{2,1,0:T(8,128)(2,1)S(1)}, bf16[1,32,4096]{2,1,0:T(8,128)(2,1)S(1)}, u32[]{:S(2)}, u32[]{:S(2)}) collective-permute-start(bf16[1,32,4096]{2,1,0:T(8,128)(2,1)S(1)} %collective-permute-done.84.refs_3_), channel_id=1, source_target_pairs={{0,4},{4,0},{8,12},{12,8},{16,20},{20,16},{24,28},{28,24},{1,5},{5... | collective-permute-start | bytes 786440 | tf_op jit(solution)/shard_map/ppermute | solution.py:292
  531.4 14.6 %collective-permute-start.67 = (bf16[1,32,3072]{2,1,0:T(8,128)(2,1)S(1)}, bf16[1,32,3072]{2,1,0:T(8,128)(2,1)S(1)}, u32[]{:S(2)}, u32[]{:S(2)}) collective-permute-start(bf16[1,32,3072]{2,1,0:T(8,128)(2,1)S(1)} %fusion.71.refs_0_), channel_id=1, source_target_pairs={{0,4},{4,0},{8,12},{12,8},{16,20},{20,16},{24,28},{28,24},{1,5},{5... | collective-permute-start | bytes 589832 | tf_op jit(solution)/shard_map/ppermute | solution.py:292
  531.4 14.6 %collective-permute-start.68 = (bf16[1,32,3072]{2,1,0:T(8,128)(2,1)}, bf16[1,32,3072]{2,1,0:T(8,128)(2,1)S(1)}, u32[]{:S(2)}, u32[]{:S(2)}) collective-permute-start(bf16[1,32,3072]{2,1,0:T(8,128)(2,1)} %collective-permute-done.64.refs_1_), channel_id=1, source_target_pairs={{0,4},{4,0},{8,12},{12,8},{16,20},{20,16},{24,28},{28,24},{1,5},{5... | collective-permute-start | bytes 589832 | tf_op jit(solution)/shard_map/ppermute | solution.py:292
  532.2 13.9 %collective-permute-start.69 = (bf16[1,32,3072]{2,1,0:T(8,128)(2,1)S(1)}, bf16[1,32,3072]{2,1,0:T(8,128)(2,1)S(1)}, u32[]{:S(2)}, u32[]{:S(2)}) collective-permute-start(bf16[1,32,3072]{2,1,0:T(8,128)(2,1)S(1)} %collective-permute-done.65.refs_2_), channel_id=1, source_target_pairs={{0,4},{4,0},{8,12},{12,8},{16,20},{20,16},{24,28},{28,24},{1,5},{5... | collective-permute-start | bytes 589832 | tf_op jit(solution)/shard_map/ppermute | solution.py:292
  534.3 11.8 %collective-permute-start.70 = (bf16[1,32,3072]{2,1,0:T(8,128)(2,1)S(1)}, bf16[1,32,3072]{2,1,0:T(8,128)(2,1)S(1)}, u32[]{:S(2)}, u32[]{:S(2)}) collective-permute-start(bf16[1,32,3072]{2,1,0:T(8,128)(2,1)S(1)} %collective-permute-done.66.refs_3_), channel_id=1, source_target_pairs={{0,4},{4,0},{8,12},{12,8},{16,20},{20,16},{24,28},{28,24},{1,5},{5... | collective-permute-start | bytes 589832 | tf_op jit(solution)/shard_map/ppermute | solution.py:292
  (122 other events, 1925.5 us)

commit v4 on v3

--- a/solution.py
+++ b/solution.py
@@ -126,14 +126,14 @@
     out_ref[:, pl.ds(pl.multiple_of(2 * full + at, width), width)] = dv_ref[...].astype(jnp.bfloat16)
 
 
-def pair_specs(rows, pairs):
+def pair_specs(rows, pairs, start=0):
     pair = 2 * HDIM
     whole = [
         pl.BlockSpec((rows, 1), lambda i: (0, 0)),
         pl.BlockSpec((1, rows), lambda i: (0, 0)),
     ]
     return whole + [
-        pl.BlockSpec((rows, pair), lambda i, j=j: (0, j * pairs + i)) for j in range(3)
+        pl.BlockSpec((rows, pair), lambda i, j=j: (0, j * pairs + start + i)) for j in range(3)
     ]
 
 
@@ -155,20 +155,22 @@
     )(segment[:, None], segment[None, :], projected, projected, projected)
 
 
-def attend_back(projected, grad_attn, segment):
+def attend_back(projected, grad_attn, segment, start, count):
     rows = projected.shape[0]
     pairs = HEADS // 2
     windows = key_windows(rows)
+    wide = 3 * count * 2 * HDIM
 
     def body(*refs):
         attend_back_body(windows, *refs)
 
     return pl.pallas_call(
         body,
-        grid=(pairs,),
-        in_specs=pair_specs(rows, pairs) + [pl.BlockSpec((rows, 2 * HDIM), lambda i: (0, i))],
-        out_specs=pl.BlockSpec((rows, 3 * HEADS * HDIM), lambda i: (0, 0)),
-        out_shape=jax.ShapeDtypeStruct((rows, 3 * HEADS * HDIM), jnp.bfloat16),
+        grid=(count,),
+        in_specs=pair_specs(rows, pairs, start)
+        + [pl.BlockSpec((rows, 2 * HDIM), lambda i: (0, start + i))],
+        out_specs=pl.BlockSpec((rows, wide), lambda i: (0, 0)),
+        out_shape=jax.ShapeDtypeStruct((rows, wide), jnp.bfloat16),
         scratch_shapes=[pltpu.VMEM((rows, 2 * HDIM), jnp.float32)] * 2,
         name="attend_back",
     )(segment[:, None], segment[None, :], projected, projected, projected, grad_attn)
@@ -296,17 +298,6 @@
     return lax.ppermute(block, "fsdp", [(i, (i + step) % n_line) for i in range(n_line)])
 
 
-def line_gather(unit, n_line):
-    return jnp.stack([ahead(unit, n_line, step) for step in range(1, n_line)])
-
-
-def spread(part, n_dp):
-    parts = [part]
-    for stage in range(n_dp.bit_length() - 2):
-        parts = parts + [lax.ppermute(item, "dp", hop_pairs(n_dp, stage)) for item in parts]
-    return parts + [swap_core(item, n_dp) for item in parts]
-
-
 def add_up(terms):
     total = terms[0].astype(jnp.float32)
     for term in terms[1:]:
@@ -331,10 +322,30 @@
     arrived = yield [ahead(send, n_line, step + 1) for step, send in enumerate(sends)]
     parts = [add_up([term[0] for term in terms] + arrived).astype(jnp.bfloat16)[None]]
     for stage in range(n_dp.bit_length() - 2):
-        parts = yield parts
-        parts = parts + (yield [lax.ppermute(item, "dp", hop_pairs(n_dp, stage)) for item in parts])
-    parts = yield parts
-    return parts + (yield [swap_core(item, n_dp) for item in parts])
+        (send,) = yield [jnp.concatenate(parts) if len(parts) > 1 else parts[0]]
+        (got,) = yield [lax.ppermute(send, "dp", hop_pairs(n_dp, stage))]
+        parts = parts + [got]
+    (send,) = yield [jnp.concatenate(parts)]
+    (got,) = yield [swap_core(send, n_dp)]
+    return [send, got]
+
+
+def small_steps(mine, n_dp, n_line):
+    (mine,) = yield [mine]
+    for bit in range(n_dp.bit_length() - 1):
+        pairs = [(i, i ^ (1 << bit)) for i in range(n_dp)]
+        (got,) = yield [lax.ppermute(mine, "dp", pairs)]
+        (mine,) = yield [mine + got]
+    line = lax.axis_index("fsdp")
+
+    def part(step):
+        return lax.dynamic_index_in_dim(mine, (line + step) % n_line, 0, keepdims=False)
+
+    arrived = yield [ahead(part(step), n_line, step) for step in range(1, n_line)]
+    total = part(0)
+    for item in arrived:
+        total = total + item
+    return [total]
 
 
 class Reduction:
@@ -409,8 +420,22 @@
         def full(matrix):
             return lax.all_gather(matrix, "fsdp", axis=0, tiled=True)
 
-        table = lax.all_gather(smalls, "fsdp", axis=0)
-        return (table, full(w_qkv), full(w_out), full(w_fc1), full(w_fc2))
+        self.full = [full(w_qkv), full(w_out), full(w_fc1), full(w_fc2)]
+        return lax.all_gather(smalls, "fsdp", axis=0)
+
+    def first(self):
+        return self.full[:2]
+
+    def second(self):
+        return self.full[2]
+
+    def third(self):
+        return self.full[3]
+
+    def pass_one(self, gate):
+        return gate
+
+    pass_two = pass_three = pass_four = pass_one
 
     def rows(self, block):
         return block
@@ -432,6 +457,35 @@
             smalls.astype(jnp.bfloat16), "fsdp", scatter_dimension=0, tiled=False
         )
         return Ready(lax.psum(own, "dp").astype(jnp.float32))
+
+
+class Gather:
+    def __init__(self, unit, n_dp, n_line):
+        self.n_dp = n_dp
+        self.line = [ahead(unit, n_line, step) for step in range(1, n_line)]
+
+    def hop(self, block, stage):
+        return lax.ppermute(block, "dp", hop_pairs(self.n_dp, stage))
+
+    def fan(self, gate, rows):
+        self.line, gate = lax.optimization_barrier((self.line, gate))
+        near = jnp.stack([item[:rows] for item in self.line])[None]
+        near, gate = lax.optimization_barrier((near, gate))
+        self.parts = [near, self.hop(near, 0), self.hop(near, 1)]
+        self.cores = [swap_core(near, self.n_dp)]
+        return gate
+
+    def forward(self, gate):
+        self.parts[1], gate = lax.optimization_barrier((self.parts[1], gate))
+        self.parts.append(self.hop(self.parts[1], 1))
+        self.cores.append(swap_core(self.parts[1], self.n_dp))
+        return gate
+
+    def close(self, gate):
+        late, gate = lax.optimization_barrier((self.parts[2:], gate))
+        self.cores += [swap_core(item, self.n_dp) for item in late]
+        self.parts = self.parts[:2] + late
+        return gate
 
 
 class Staged:
@@ -476,23 +530,44 @@
             [jnp.concatenate([self.pick(w_qkv), self.pick(w_out)], axis=1), packed]
         )
         unit_two, unit_three = (self.pick(w_fc1), self.pick(w_fc2))
-        first = line_gather(unit_one, n_line)
-        first, unit_two = lax.optimization_barrier((first, unit_two))
-        second = line_gather(unit_two, n_line)
-        second, unit_three = lax.optimization_barrier((second, unit_three))
-        third = line_gather(unit_three, n_line)
         size = self.unit
-        got_one = spread(first[None, :, :size], n_dp)
-        got_two = spread(second[None], n_dp)
-        got_three = spread(third[None], n_dp)
-        full_qkv, full_out = assemble([w_qkv, w_out], got_one, self.got_table, n_line, size)
-        (full_fc1,) = assemble([w_fc1], got_two, self.got_table, n_line, size)
-        (full_fc2,) = assemble([w_fc2], got_three, self.got_table, n_line, third.shape[1])
-        far = jnp.concatenate(
-            [first[:, size:, i * shard : (i + 1) * shard] for i in range(fold)], axis=1
-        )
-        table = jnp.take(jnp.concatenate([padded[None], far]), self.unline, axis=0)
-        return (table, full_qkv, full_out, full_fc1, full_fc2)
+        one = Gather(unit_one, n_dp, n_line)
+        unit_two = one.fan(unit_two, size)
+        far = jnp.stack([item[size:] for item in one.line])
+        two = Gather(unit_two, n_dp, n_line)
+        two.line = one.forward(two.line)
+        two.line = one.close(two.line)
+        table, unit_three = two.fan((self.got_table, unit_three), size)
+        three = Gather(unit_three, n_dp, n_line)
+        full_qkv, full_out = assemble([w_qkv, w_out], one.parts + one.cores, table, n_line, size)
+        self.one = (full_qkv, full_out)
+        self.two = (w_fc1, two)
+        self.three = (w_fc2, three, unit_three.shape[0])
+        far = jnp.concatenate([far[:, :, i * shard : (i + 1) * shard] for i in range(fold)], axis=1)
+        return jnp.take(jnp.concatenate([padded[None], far]), self.unline, axis=0)
+
+    def first(self):
+        return self.one
+
+    def pass_one(self, gate):
+        return self.two[1].forward(gate)
+
+    def pass_two(self, gate):
+        return self.three[1].fan(self.two[1].close(gate), self.three[2])
+
+    def pass_three(self, gate):
+        return self.three[1].forward(gate)
+
+    def pass_four(self, gate):
+        return self.three[1].close(gate)
+
+    def second(self):
+        own, got = self.two
+        return assemble([own], got.parts + got.cores, self.got_table, self.n_line, self.unit)[0]
+
+    def third(self):
+        own, got, unit = self.three
+        return assemble([own], got.parts + got.cores, self.got_table, self.n_line, unit)[0]
 
     def rows(self, block):
         return jnp.dot(block, self.order, preferred_element_type=jnp.float32).astype(jnp.bfloat16)
@@ -517,27 +592,11 @@
         return Reduction(steps, lambda parts: list(finish(parts, owner, cuts)))
 
     def total_small(self, smalls):
-        n_dp = self.n_dp
-        n_line = self.n_line
-        n_small, shard = smalls.shape[1:]
-        per_dp = -(-n_small // n_dp)
-        units = jnp.pad(smalls, ((0, 0), (0, per_dp * n_dp - n_small), (0, 0)))
-        units = units.reshape(n_line * n_dp, per_dp * shard).astype(jnp.bfloat16)
-        size = -(-per_dp * shard // (16 * TILE)) * 16
-        units = jnp.pad(units, ((0, 0), (0, size * TILE - per_dp * shard)))
-        ids = jnp.arange(n_line * n_dp, dtype=jnp.int32)
-        choose = (self.send_table[:, None] == ids[None, :]).astype(jnp.bfloat16)
-        units = jnp.dot(choose, units, preferred_element_type=jnp.float32).astype(jnp.bfloat16)
-        units = units.reshape(n_dp, n_line, size, TILE)
-        owner = self.owner.astype(jnp.int32)
-
-        def close(parts):
-            (small,) = finish(parts, owner, [TILE])
-            small = small.reshape(n_dp, size * TILE)[:, : per_dp * shard]
-            return small.reshape(-1, shard)[:n_small]
-
-        half = n_dp // 2
-        return Reduction(reduce_steps(units[half:], units[:half], n_dp, n_line), close)
+        n_small = smalls.shape[1]
+        padded = jnp.pad(smalls, ((0, 0), (0, -n_small % 8), (0, 0)))
+        return Reduction(
+            small_steps(padded, self.n_dp, self.n_line), lambda parts: parts[0][:n_small]
+        )
 
 
 def per_device(
@@ -567,7 +626,7 @@
     width = patches.shape[1]
     shard = width // n_line
     place, valid, segment = place_rows(rows, low_flag, pos_index, pos_weight)
-    if n_line <= 4 and shard % (16 * n_dp) == 0:
+    if n_dp == 8 and n_line <= 4 and shard % (16 * n_dp) == 0:
         plan = Staged(n_dp, n_line, dp, line, width)
     else:
         plan = Wide(shard)
@@ -580,7 +639,8 @@
         ]
     )
     n_small = smalls.shape[0]
-    table, full_qkv, full_out, full_fc1, full_fc2 = plan.gather(w_qkv, w_out, w_fc1, w_fc2, smalls)
+    table = plan.gather(w_qkv, w_out, w_fc1, w_fc2, smalls)
+    full_qkv, full_out = plan.first()
 
     def across(block):
         return block.transpose(1, 0, 2).reshape(block.shape[1], width).astype(f32)
@@ -592,39 +652,53 @@
     hidden_in = patches.astype(f32) + jnp.dot(place, full_table, precision=highest)
     normed_one = layer_norm(hidden_in, gain_one, bias_one).astype(bf16)
     projected = jnp.dot(normed_one, full_qkv, preferred_element_type=f32).astype(bf16)
-    attn_rows = attend(projected, segment)
+    projected = plan.pass_one(projected)
+    attn_rows = plan.pass_two(attend(projected, segment))
     hidden_mid = hidden_in + jnp.dot(attn_rows, full_out, preferred_element_type=f32)
     normed_two = layer_norm(hidden_mid, gain_two, bias_two).astype(bf16)
+    normed_two = plan.pass_three(normed_two)
+    full_fc1 = plan.second()
     pre_act = jnp.dot(normed_two, full_fc1, preferred_element_type=f32) + full_bias
     share = 0.5 * (1.0 + lax.erf(pre_act * 0.5**0.5))
     bell = jnp.exp(-0.5 * pre_act * pre_act) * (0.5 / jnp.pi) ** 0.5
     activated = (pre_act * share).astype(bf16)
     slope = (share + pre_act * bell).astype(bf16)
+    activated = plan.pass_four(activated)
+    grad_out = jnp.where(valid[:, None], cotangent, jnp.zeros_like(cotangent))
+    run_fc2 = plan.total([(plan.wide_columns(activated), grad_out)])
+    activated = tick(activated, [run_fc2])
+    full_fc2, activated = tick((plan.third(), activated), [run_fc2])
     branch_out = jnp.dot(activated, full_fc2, preferred_element_type=f32)
     block_out = jnp.where(valid[:, None], hidden_mid + branch_out, 0.0).astype(bf16)
-    grad_out = jnp.where(valid[:, None], cotangent, jnp.zeros_like(cotangent))
-
-    run_fc2 = plan.total([(plan.wide_columns(activated), grad_out)])
-    grad_out = tick(grad_out, [run_fc2])
+
     grad_pre = (times_t(grad_out, full_fc2) * slope.astype(f32)).astype(bf16)
     grad_fc1_bias = jnp.sum(grad_pre.astype(f32), axis=0)
     run_fc1 = plan.total([(plan.rows(normed_two), grad_pre)])
-    grad_pre = tick(grad_pre, [run_fc2, run_fc1])
+    grad_pre = tick(grad_pre, [run_fc1])
     grad_norm_two = times_t(grad_pre, full_fc1)
     _, pull_two = jax.vjp(layer_norm, hidden_mid, gain_two, bias_two)
     back_mid, grad_gain_two, grad_bias_two = pull_two(grad_norm_two)
     grad_mid = grad_out.astype(f32) + back_mid
-    grad_branch = tick(grad_mid.astype(bf16), [run_fc2, run_fc1])
+    grad_branch = tick(grad_mid.astype(bf16), [run_fc1])
     run_out = plan.total([(plan.rows(attn_rows), grad_branch)])
     grad_attn = times_t(grad_branch, full_out).astype(bf16)
-    grad_attn = tick(grad_attn, [run_fc2, run_fc1, run_out])
-    grad_proj = attend_back(projected, grad_attn, segment)
+    grad_attn = tick(grad_attn, [run_fc2, run_out])
+    half = HEADS // 4
+    back_a = attend_back(projected, grad_attn, segment, 0, half)
+    back_a, grad_attn = tick((back_a, grad_attn), [run_fc2, run_fc1, run_out])
+    back_b = attend_back(projected, grad_attn, segment, half, half)
+    back_a, back_b = tick((back_a, back_b), [run_fc2, run_fc1, run_out])
+    side = back_a.shape[1] // 3
+    grad_proj = jnp.concatenate(
+        [part[:, i * side : (i + 1) * side] for i in range(3) for part in (back_a, back_b)], axis=1
+    )
     run_qkv = plan.total([(plan.rows(normed_one), grad_proj)])
-    grad_proj = tick(grad_proj, [run_fc2, run_fc1, run_out, run_qkv])
+    grad_proj = tick(grad_proj, [run_qkv])
     grad_norm_one = times_t(grad_proj, full_qkv)
+    grad_norm_one = tick(grad_norm_one, [run_fc2, run_fc1, run_out, run_qkv])
     _, pull_one = jax.vjp(layer_norm, hidden_in, gain_one, bias_one)
     back_in, grad_gain_one, grad_bias_one = pull_one(grad_norm_one)
-    grad_in = tick(grad_mid + back_in, [run_fc2, run_fc1, run_out, run_qkv])
+    grad_in = grad_mid + back_in
     grad_table = jnp.dot(place.T, grad_in, precision=highest)
 
     def split(block):

time: 556 us -> 490 us (0.88)
  waiting for transfers between devices: 192 us -> 112 us
  starting transfers between devices: 78.8 us -> 89.1 us
  other arithmetic: 48.6 us -> 55.6 us
    ppermute x24, waiting for transfers between devices: 97.5 us -> 56.7 us  [ahead(): lax.ppermute(block, 'fsdp', [(i, (i + step) % n_line) for i in range(n_li...]
    ppermute x10 -> x16, waiting for transfers between devices: 59.3 us -> 29.8 us  [reduce_steps(): got, = (yield [lax.ppermute(send, 'dp', hop_pairs(n_dp, stage))])]
    ppermute x24, starting transfers between devices: 35.7 us -> 58.5 us  [ahead(): lax.ppermute(block, 'fsdp', [(i, (i + step) % n_line) for i in range(n_li...]
    ppermute x24 -> x12, starting transfers between devices: 26.5 us -> 8.69 us  [the longest x9 7.76 us: hop(): return lax.ppermute(block, 'dp', hop_pairs(self.n_dp, stage))]
    ppermute x24 -> x12, waiting for transfers between devices: 33.7 us -> 23.8 us  [the longest x9 17 us: hop(): return lax.ppermute(block, 'dp', hop_pairs(self.n_dp, stage))]
    ppermute x10 -> x16, starting transfers between devices: 10.1 us -> 17.6 us  [reduce_steps(): got, = (yield [lax.ppermute(send, 'dp', hop_pairs(n_dp, stage))])]
    pallas_call x1 -> x2, Pallas kernels: 35.9 us -> 37.7 us  [attend_back(): pl.pallas_call(body, grid=(count,), in_specs=pair_specs(rows, pairs, star...]
    pallas_call x5 -> x4, Pallas kernels: 14.5 us -> 13 us  [finish(): pl.pallas_call(body, in_specs=[pl.BlockSpec(memory_space=pltpu.SMEM)] + [...]
  transfers between devices with their start and end apart: 95 -> 72, of which waited for: 32 -> 20; matrix products, arithmetic and copies ran while one was open for 23% -> 23% of each run, Pallas kernels for 17% -> 18%
where the time goes in v4:
time: 490 us; the launch traced here: 484 us
  waiting for transfers between devices  112 us (23%)
  matrix products  95 us (19%)
  Pallas kernels  94.8 us (19%)
  starting transfers between devices  89.1 us (18%)
  other arithmetic  55.6 us (11%)
  local copies, waits for them, and re-layouts  35 us (7%)
    ppermute x24, starting transfers between devices, ahead(): lax.ppermute(block, 'fsdp', [(i, (i + step) % n_line) for i in range(n_li...  58.5 us
    ppermute x24, waiting for transfers between devices, ahead(): lax.ppermute(block, 'fsdp', [(i, (i + step) % n_line) for i in range(n_li...  56.7 us
    pallas_call x2, Pallas kernels, attend_back(): pl.pallas_call(body, grid=(count,), in_specs=pair_specs(rows, pairs, star...  37.7 us
    ppermute x16, waiting for transfers between devices, reduce_steps(): got, = (yield [lax.ppermute(send, 'dp', hop_pairs(n_dp, stage))])  29.8 us
    dot_general x4, matrix products, times_t(): lax.dot_general(left, right, (((1,), (1,)), ((), ())), preferred_element_...  28.3 us
    dot_general x8, matrix products, t_times(): lax.dot_general(left, right, (((0,), (0,)), ((), ())), preferred_element_...  25.6 us
    pallas_call x3, Pallas kernels, assemble(): pl.pallas_call(body, in_specs=[pl.BlockSpec(memory_space=pltpu.SMEM)] + [...  22.9 us
    convert_element_type x8, other arithmetic, reduce_steps(): add_up([term[half:] for term in terms]).astype(jnp.bfloat16)  21.8 us
  transfers between devices with their start and end apart: 72, of which 20 were waited for; matrix products, arithmetic and copies ran while one was open for 23% of the time, Pallas kernels for 18%

profile of v4, /device:TPU:0, one launch (start us, length us, event | category | flops | bytes accessed | tf_op | source)
XLA Modules:
  0.0 483.6 jit_solution(15543145020426732388)
XLA Ops:
  8.1 3.1 collective-permute-start
  11.2 2.6 collective-permute-start.1
  21.0 2.4 collective-permute-done
  23.3 16.0 %collective-permute-done.1 = bf16[48,4096]{1,0:T(8,128)(2,1)S(1)} collective-permute-done((bf16[48,4096]{1,0:T(8,128)(2,1)S(1)}, bf16[48,4096]{1,0:T(8,128)(2,1)S(1)}, u32[]{:S(2)}, u32[]{:S(2)}) %collective-permute-start.1) | collective-permute-done | bytes 393248 | tf_op jit(solution)/shard_map/ppermute | solution.py:298
  43.4 8.9 %collective-permute-start.5 = (bf16[32,4096]{1,0:T(8,128)(2,1)S(1)}, bf16[32,4096]{1,0:T(8,128)(2,1)S(1)}, u32[]{:S(2)}, u32[]{:S(2)}) collective-permute-start(bf16[32,4096]{1,0:T(8,128)(2,1)S(1)} %constant_dynamic-slice_fusion.5), channel_id=1, source_target_pairs={{0,1},{1,2},{2,3},{3,0},{4,5},{5,6},{6,7},{7,4},{8,9},{9,10},{10,1... | collective-permute-start | bytes 786440 | tf_op jit(solution)/shard_map/ppermute | solution.py:298
  55.9 4.7 collective-permute-done.5
  60.6 9.0 %collective-permute-done.6 = bf16[32,4096]{1,0:T(8,128)(2,1)S(1)} collective-permute-done((bf16[32,4096]{1,0:T(8,128)(2,1)S(1)}, bf16[32,4096]{1,0:T(8,128)(2,1)S(1)}, u32[]{:S(2)}, u32[]{:S(2)}) %collective-permute-start.6) | collective-permute-done | bytes 262176 | tf_op jit(solution)/shard_map/ppermute | solution.py:298
  72.1 9.8 %collective-permute-done.8.refs_5_ = bf16[1,3,32,4096]{3,2,1,0:T(8,128)(2,1)S(1)} collective-permute-done((bf16[1,3,32,4096]{3,2,1,0:T(8,128)(2,1)}, bf16[1,3,32,4096]{3,2,1,0:T(8,128)(2,1)S(1)}, u32[]{:S(2)}, u32[]{:S(2)}) %collective-permute-start.8) | collective-permute-done | bytes 786464 | tf_op jit(solution)/shard_map/ppermute | solution.py:468
  85.6 7.7 %assemble.3 = (bf16[1024,3072]{1,0:T(8,128)(2,1)}, bf16[1024,1024]{1,0:T(8,128)(2,1)}) custom-call(s32[33]{0:T(128)} %pad_add_fusion.1.table_ref, bf16[256,3072]{1,0:T(8,128)(2,1)} %refs_0_.3, bf16[256,1024]{1,0:T(8,128)(2,1)} %refs_1_.1, bf16[1,3,32,4096]{3,2,1,0:T(8,128)(2,1)} %maximum_bitcast_fusion.refs_2_, ...), custom_call_target="tpu_custom_call" | custom-call | tf_op jit(solution)/shard_map/assemble/pallas_call | solution.py:225
  93.3 7.8 %convolution_convert_fusion.4.refs_2_.refs_3_.refs_4_ = bf16[512,3072]{1,0:T(8,128)(2,1)} fusion(bf16[1024,3072]{1,0:T(8,128)(2,1)} %get-tuple-element.137, f32[512,1024]{1,0:T(8,128)S(1)} %get-tuple-element.255, f32[1024]{0:T(1024)S(1)} %bitcast.313, f32[1024]{0:T(1024)S(1)} %bitcast.305, f32[512]{0:T(512)S(1)} %fusion.86, f32[512]{0:T(512)S(1)} %broadcast_multiply_fusion.1), kind=kOutput, calls=%fused_computation.15 | convolution fusion | flops 3225419776 | bytes 11546624 | tf_op jit(solution)/shard_map/dot_general | solution.py:654
  104.0 6.0 %collective-permute-start.9 = (bf16[128,1024]{1,0:T(8,128)(2,1)S(1)}, bf16[128,1024]{1,0:T(8,128)(2,1)S(1)}, u32[]{:S(2)}, u32[]{:S(2)}) collective-permute-start(bf16[128,1024]{1,0:T(8,128)(2,1)S(1)} %copy-done.41), channel_id=1, source_target_pairs={{0,1},{1,2},{2,3},{3,0},{4,5},{5,6},{6,7},{7,4},{8,9},{9,10},{10,1... | collective-permute-start | bytes 786440 | tf_op jit(solution)/shard_map/ppermute | solution.py:298
  110.0 2.4 collective-permute-start.10
  116.8 15.8 %attend.1 = bf16[512,1024]{1,0:T(8,128)(2,1)} custom-call(s32[512,1]{1,0:T(8,128)} %fusion.59.refs_0_, s32[1,512]{1,0:T(1,128)} %broadcast_select_fusion.2.refs_1_, bf16[512,3072]{1,0:T(8,128)(2,1)} %convolution_convert_fusion.4.refs_2_.refs_3_.refs_4_, bf16[512,3072]{1,0:T(8,128)(2,1)} %convolution_convert_fusion.4.refs_2_.refs_3_.refs_4_, ...), custom_call_target="tpu_custom_call" | custom-call | tf_op jit(solution)/shard_map/attend/pallas_call | solution.py:148
  133.2 2.0 maximum_bitcast_fusion.2.refs_1_
  136.5 3.3 fusion.101
  141.8 5.6 %collective-permute-done.19.refs_2_ = bf16[1,3,128,1024]{3,2,1,0:T(8,128)(2,1)} collective-permute-done((bf16[1,3,128,1024]{3,2,1,0:T(8,128)(2,1)}, bf16[1,3,128,1024]{3,2,1,0:T(8,128)(2,1)}, u32[]{:S(2)}, u32[]{:S(2)}) %collective-permute-start.19) | collective-permute-done | bytes 786464 | tf_op jit(solution)/shard_map/ppermute | solution.py:468
  150.4 7.6 %assemble.4 = bf16[1024,4096]{1,0:T(8,128)(2,1)} custom-call(s32[33]{0:T(128)} %pad_add_fusion.1.table_ref, bf16[256,4096]{1,0:T(8,128)(2,1)} %refs_0_.4, bf16[1,3,32,4096]{3,2,1,0:T(8,128)(2,1)} %copy-done.21, bf16[1,3,32,4096]{3,2,1,0:T(8,128)(2,1)} %collective-permute-done.13.refs_2_, bf16[1,3,32,4096]{3,2,1,0:T(8,128)(2,1)} %collective-permute-done.12.refs_3_, ...), custom_call_target="tpu_custom_call" | custom-call | tf_op jit(solution)/shard_map/assemble/pallas_call | solution.py:225
  158.0 10.4 %multiply_convert_fusion.1 = (bf16[512,4096]{1,0:T(8,128)(2,1)}, f32[512,4096]{1,0:T(8,128)}) fusion(f32[4096]{0:T(1024)S(1)} %bitcast.310, bf16[512,1024]{1,0:T(8,128)(2,1)S(1)} %copy-done.29, bf16[1024,4096]{1,0:T(8,128)(2,1)} %assemble.4), kind=kOutput, calls=%fused_computation.9 | convolution fusion | flops 4307550208 | bytes 22036480 | tf_op jit(solution)/shard_map/dot_general | solution.py:661
  168.5 5.5 %column_order.1 = bf16[512,4096]{1,0:T(8,128)(2,1)} custom-call(s32[32]{0:T(128)} %add.550.table_ref, bf16[512,4096]{1,0:T(8,128)(2,1)} %get-tuple-element.160.in_ref), custom_call_target="tpu_custom_call" | custom-call | tf_op jit(solution)/shard_map/column_order/pallas_call | solution.py:245
  174.0 6.0 %convolution_convert_fusion.6 = bf16[2048,1024]{1,0:T(8,128)(2,1)} fusion(bf16[512,4096]{1,0:T(8,128)(2,1)} %column_order.1, bf16[512,1024]{1,0:T(8,128)(2,1)S(1)} %copy-done.19, pred[512]{0:T(512)(128)(4,1)S(1)} %copy-done.72), kind=kOutput, calls=%fused_computation.25 | convolution fusion | flops 2150105088 | bytes 7340544 | tf_op jit(solution)/shard_map/dot_general | solution.py:69
  181.2 3.7 fusion.22
  184.9 2.4 convolution_convert_fusion.5
  192.6 7.6 %assemble.5 = bf16[4096,1024]{1,0:T(8,128)(2,1)} custom-call(s32[33]{0:T(128)} %pad_add_fusion.1.table_ref, bf16[1024,1024]{1,0:T(8,128)(2,1)} %refs_0_.5, bf16[1,3,128,1024]{3,2,1,0:T(8,128)(2,1)} %maximum_bitcast_fusion.2.refs_1_, bf16[1,3,128,1024]{3,2,1,0:T(8,128)(2,1)} %collective-permute-done.19.refs_2_, ...), custom_call_target="tpu_custom_call" | custom-call | tf_op jit(solution)/shard_map/assemble/pallas_call | solution.py:225
  200.2 3.4 fusion.6
  203.6 11.7 %convert_reduce_fusion = (f32[4096]{0:T(1024)}, bf16[512,4096]{1,0:T(8,128)(2,1)S(1)}) fusion(f32[512,4096]{1,0:T(8,128)} %get-tuple-element.259, f32[4096]{0:T(1024)S(1)} %bitcast.311, bf16[4096,1024]{1,0:T(8,128)(2,1)} %assemble.5, bf16[512,1024]{1,0:T(8,128)(2,1)S(1)} %copy-done.19, pred[512]{0:T(512)(128)(4,1)S(1)} %copy-done.72), kind=kOutput, calls=%fused_computation.7 | convolution fusion | flops 4326944768 | bytes 22053376 | tf_op jit(solution)/shard_map/dot_general | solution.py:65
  215.3 5.7 %convolution_convert_fusion.1 = bf16[512,4096]{1,0:T(8,128)(2,1)} fusion(bf16[512,4096]{1,0:T(8,128)(2,1)S(1)} %get-tuple-element.162, bf16[512,1024]{1,0:T(8,128)(2,1)} %fusion.22), kind=kOutput, calls=%fused_computation.12 | convolution fusion | flops 2149580800 | bytes 8912896 | tf_op jit(solution)/shard_map/dot_general | solution.py:69
  222.0 6.8 %multiply_reduce_fusion = (f32[1024]{0:T(1024)}, f32[512]{0:T(512)S(1)}, f32[1024]{0:T(1024)}, f32[512,1024]{1,0:T(8,128)}) fusion(f32[512,1024]{1,0:T(8,128)S(1)} %copy-done.1, f32[512]{0:T(512)S(1)} %fusion.87, f32[512]{0:T(512)S(1)} %broadcast_multiply_fusion, f32[1024]{0:T(1024)S(1)} %bitcast.303, bf16[512,4096]{1,0:T(8,128)(2,1)S(1)} %get-tuple-element.162, ...), kind=kOutput, calls=%fused_computation.38 | convolution fusion | flops 4299159040 | bytes 16795648 | tf_op jit(solution)/shard_map/dot_general | solution.py:65
  228.9 2.4 fusion.97
  231.3 2.5 convolution_convert_fusion
  233.8 2.0 copy-done.5
  237.7 3.8 fusion.5
  246.4 2.7 convolution_convert_fusion.7.refs_5_
  250.8 3.2 fusion.16
  255.5 18.8 %attend_back.2 = bf16[512,1536]{1,0:T(8,128)(2,1)} custom-call(s32[512,1]{1,0:T(8,128)} %fusion.59.refs_0_, s32[1,512]{1,0:T(1,128)} %broadcast_select_fusion.2.refs_1_, bf16[512,3072]{1,0:T(8,128)(2,1)} %convolution_convert_fusion.4.refs_2_.refs_3_.refs_4_, bf16[512,3072]{1,0:T(8,128)(2,1)} %convolution_convert_fusion.4.refs_2_.refs_3_.refs_4_, ...), custom_call_target="tpu_custom_call" | custom-call | tf_op jit(solution)/shard_map/attend_back/pallas_call | solution.py:167
  276.1 4.2 collective-permute-done.33
  281.4 3.1 fusion.46
  284.5 3.1 fusion.14
  290.9 2.1 collective-permute-start.36
  295.4 2.5 fusion.24
  297.9 18.9 %attend_back.3 = bf16[512,1536]{1,0:T(8,128)(2,1)} custom-call(s32[512,1]{1,0:T(8,128)} %fusion.59.refs_0_, s32[1,512]{1,0:T(1,128)} %broadcast_select_fusion.2.refs_1_, bf16[512,3072]{1,0:T(8,128)(2,1)} %convolution_convert_fusion.4.refs_2_.refs_3_.refs_4_, bf16[512,3072]{1,0:T(8,128)(2,1)} %convolution_convert_fusion.4.refs_2_.refs_3_.refs_4_, ...), custom_call_target="tpu_custom_call" | custom-call | tf_op jit(solution)/shard_map/attend_back/pallas_call | solution.py:167
  316.8 3.2 fusion.39
  324.3 3.7 convolution_convert_fusion.3
  331.0 7.2 %fusion.102 = f32[512,1024]{1,0:T(8,128)S(1)} fusion(bf16[512,3072]{1,0:T(8,128)(2,1)} %copy-done.7, bf16[1024,3072]{1,0:T(8,128)(2,1)} %get-tuple-element.137), kind=kOutput, calls=%fused_computation.344 | convolution fusion | flops 3221225472 | bytes 11534336 | tf_op jit(solution)/shard_map/dot_general | solution.py:65
  338.6 2.2 collective-permute-start.43
  349.4 10.3 %collective-permute-done.43 = bf16[32,4096]{1,0:T(8,128)(2,1)S(1)} collective-permute-done((bf16[32,4096]{1,0:T(8,128)(2,1)S(1)}, bf16[32,4096]{1,0:T(8,128)(2,1)S(1)}, u32[]{:S(2)}, u32[]{:S(2)}) %collective-permute-start.43) | collective-permute-done | bytes 262176 | tf_op jit(solution)/shard_map/ppermute | solution.py:298
  362.3 3.3 fusion.10
  373.7 6.0 %collective-permute-start.63 = (bf16[32,1024]{1,0:T(8,128)(2,1)S(1)}, bf16[32,1024]{1,0:T(8,128)(2,1)S(1)}, u32[]{:S(2)}, u32[]{:S(2)}) collective-permute-start(bf16[32,1024]{1,0:T(8,128)(2,1)S(1)} %copy-done.55), channel_id=1, source_target_pairs={{0,3},{1,0},{2,1},{3,2},{4,7},{5,4},{6,5},{7,6},{8,11},{9,8},{10,9... | collective-permute-start | bytes 196616 | tf_op jit(solution)/shard_map/ppermute | solution.py:298
  381.3 7.3 %collective-permute-done.53 = bf16[2,4,32,3072]{3,2,1,0:T(8,128)(2,1)} collective-permute-done((bf16[2,4,32,3072]{3,2,1,0:T(8,128)(2,1)}, bf16[2,4,32,3072]{3,2,1,0:T(8,128)(2,1)}, u32[]{:S(2)}, u32[]{:S(2)}) %collective-permute-start.53) | collective-permute-done | bytes 1572896 | tf_op jit(solution)/shard_map/ppermute | solution.py:315
  388.6 2.6 fusion.21
  394.3 3.4 collective-permute-done.64
  401.2 6.6 %collective-permute-done.65 = bf16[2,32,1024]{2,1,0:T(8,128)(2,1)S(1)} collective-permute-done((bf16[2,32,1024]{2,1,0:T(8,128)(2,1)S(1)}, bf16[2,32,1024]{2,1,0:T(8,128)(2,1)S(1)}, u32[]{:S(2)}, u32[]{:S(2)}) %collective-permute-start.65) | collective-permute-done | bytes 131104 | tf_op jit(solution)/shard_map/ppermute | solution.py:326
  408.7 2.0 fusion.53
  410.8 5.8 %collective-permute-start.57 = (bf16[32,3072]{1,0:T(8,128)(2,1)S(1)}, bf16[32,3072]{1,0:T(8,128)(2,1)S(1)}, u32[]{:S(2)}, u32[]{:S(2)}) collective-permute-start(bf16[32,3072]{1,0:T(8,128)(2,1)S(1)} %get-tuple-element.235), channel_id=1, source_target_pairs={{0,3},{1,0},{2,1},{3,2},{4,7},{5,4},{6,5},{7,6},{8,11},{9,8},{10,9... | collective-permute-start | bytes 589832 | tf_op jit(solution)/shard_map/ppermute | solution.py:298
  418.4 4.3 collective-permute-done.57
  424.2 8.1 %collective-permute-done.56 = bf16[32,3072]{1,0:T(8,128)(2,1)S(1)} collective-permute-done((bf16[32,3072]{1,0:T(8,128)(2,1)S(1)}, bf16[32,3072]{1,0:T(8,128)(2,1)S(1)}, u32[]{:S(2)}, u32[]{:S(2)}) %collective-permute-start.56) | collective-permute-done | bytes 196640 | tf_op jit(solution)/shard_map/ppermute | solution.py:298
  434.3 6.7 %collective-permute-done.49 = f32[4,64,256]{2,0,1:T(4,128)S(1)} collective-permute-done((f32[4,64,256]{2,0,1:T(4,128)S(1)}, f32[4,64,256]{2,0,1:T(4,128)S(1)}, u32[]{:S(2)}, u32[]{:S(2)}) %collective-permute-start.49) | collective-permute-done | bytes 262176 | tf_op jit(solution)/shard_map/ppermute | solution.py:337
  444.4 3.5 collective-permute-start.51
  448.4 7.3 %collective-permute-done.59 = bf16[2,32,3072]{2,1,0:T(8,128)(2,1)S(1)} collective-permute-done((bf16[2,32,3072]{2,1,0:T(8,128)(2,1)S(1)}, bf16[2,32,3072]{2,1,0:T(8,128)(2,1)S(1)}, u32[]{:S(2)}, u32[]{:S(2)}) %collective-permute-start.59) | collective-permute-done | bytes 393248 | tf_op jit(solution)/shard_map/ppermute | solution.py:326
  455.7 2.2 collective-permute-start.50
  458.7 9.0 %select_convert_fusion = bf16[512,1024]{1,0:T(8,128)(2,1)} fusion(f32[512,1024]{1,0:T(8,128)S(1)} %copy-done.2, bf16[512,4096]{1,0:T(8,128)(2,1)S(1)} %copy-done.15, bf16[4096,1024]{1,0:T(8,128)(2,1)} %assemble.5, pred[512]{0:T(512)(128)(4,1)S(1)} %copy-done.74), kind=kOutput, calls=%fused_computation.47 | convolution fusion | flops 4296540160 | bytes 15729152 | tf_op jit(solution)/shard_map/dot_general | solution.py:671
  467.6 2.1 finish.5
  472.4 3.8 finish.7
  476.3 3.8 finish.6
  480.1 3.3 finish.4
  (442 shorter events, 116.4 us)
Async XLA Ops:
  8.1 15.2 %collective-permute-start = (bf16[48,4096]{1,0:T(8,128)(2,1)S(1)}, bf16[48,4096]{1,0:T(8,128)(2,1)S(1)}, u32[]{:S(2)}, u32[]{:S(2)}) collective-permute-start(bf16[48,4096]{1,0:T(8,128)(2,1)S(1)} %pad_maximum_fusion.6), channel_id=1, source_target_pairs={{0,1},{1,2},{2,3},{3,0},{4,5},{5,6},{6,7},{7,4},{8,9},{9,10},{10,1... | collective-permute-start | bytes 1179656 | tf_op jit(solution)/shard_map/ppermute | solution.py:298
  11.2 28.1 %collective-permute-start.1 = (bf16[48,4096]{1,0:T(8,128)(2,1)S(1)}, bf16[48,4096]{1,0:T(8,128)(2,1)S(1)}, u32[]{:S(2)}, u32[]{:S(2)}) collective-permute-start(bf16[48,4096]{1,0:T(8,128)(2,1)S(1)} %pad_maximum_fusion.6), channel_id=1, source_target_pairs={{0,2},{1,3},{2,0},{3,1},{4,6},{5,7},{6,4},{7,5},{8,10},{9,11},{10,... | collective-permute-start | bytes 1179656 | tf_op jit(solution)/shard_map/ppermute | solution.py:298
  13.8 25.5 %collective-permute-start.2 = (bf16[48,4096]{1,0:T(8,128)(2,1)S(1)}, bf16[48,4096]{1,0:T(8,128)(2,1)S(1)}, u32[]{:S(2)}, u32[]{:S(2)}) collective-permute-start(bf16[48,4096]{1,0:T(8,128)(2,1)S(1)} %pad_maximum_fusion.6), channel_id=1, source_target_pairs={{0,3},{1,0},{2,1},{3,2},{4,7},{5,4},{6,5},{7,6},{8,11},{9,8},{10,9... | collective-permute-start | bytes 1179656 | tf_op jit(solution)/shard_map/ppermute | solution.py:298
  40.4 31.7 %collective-permute-start.3 = (bf16[1,3,32,4096]{3,2,1,0:T(8,128)(2,1)}, bf16[1,3,32,4096]{3,2,1,0:T(8,128)(2,1)}, u32[]{:S(2)}, u32[]{:S(2)}) collective-permute-start(bf16[1,3,32,4096]{3,2,1,0:T(8,128)(2,1)} %maximum_bitcast_fusion.refs_2_), channel_id=1, source_target_pairs={{0,16},{4,12},{8,24},{12,4},{16,0},{20,28},{24,8},{28,20},{1,17},{... | collective-permute-start | bytes 2359304 | tf_op jit(solution)/shard_map/ppermute | solution.py:468
  41.9 27.7 %collective-permute-start.4 = (bf16[1,3,32,4096]{3,2,1,0:T(8,128)(2,1)}, bf16[1,3,32,4096]{3,2,1,0:T(8,128)(2,1)}, u32[]{:S(2)}, u32[]{:S(2)}) collective-permute-start(bf16[1,3,32,4096]{3,2,1,0:T(8,128)(2,1)} %maximum_bitcast_fusion.refs_2_), channel_id=1, source_target_pairs={{0,8},{4,20},{8,0},{12,28},{16,24},{20,4},{24,16},{28,12},{1,9},{5... | collective-permute-start | bytes 2359304 | tf_op jit(solution)/shard_map/ppermute | solution.py:468
  43.4 17.2 %collective-permute-start.5 = (bf16[32,4096]{1,0:T(8,128)(2,1)S(1)}, bf16[32,4096]{1,0:T(8,128)(2,1)S(1)}, u32[]{:S(2)}, u32[]{:S(2)}) collective-permute-start(bf16[32,4096]{1,0:T(8,128)(2,1)S(1)} %constant_dynamic-slice_fusion.5), channel_id=1, source_target_pairs={{0,1},{1,2},{2,3},{3,0},{4,5},{5,6},{6,7},{7,4},{8,9},{9,10},{10,1... | collective-permute-start | bytes 786440 | tf_op jit(solution)/shard_map/ppermute | solution.py:298
  52.3 17.3 %collective-permute-start.6 = (bf16[32,4096]{1,0:T(8,128)(2,1)S(1)}, bf16[32,4096]{1,0:T(8,128)(2,1)S(1)}, u32[]{:S(2)}, u32[]{:S(2)}) collective-permute-start(bf16[32,4096]{1,0:T(8,128)(2,1)S(1)} %constant_dynamic-slice_fusion.5), channel_id=1, source_target_pairs={{0,2},{1,3},{2,0},{3,1},{4,6},{5,7},{6,4},{7,5},{8,10},{9,11},{10,... | collective-permute-start | bytes 786440 | tf_op jit(solution)/shard_map/ppermute | solution.py:298
  53.9 15.7 %collective-permute-start.7 = (bf16[32,4096]{1,0:T(8,128)(2,1)S(1)}, bf16[32,4096]{1,0:T(8,128)(2,1)S(1)}, u32[]{:S(2)}, u32[]{:S(2)}) collective-permute-start(bf16[32,4096]{1,0:T(8,128)(2,1)S(1)} %constant_dynamic-slice_fusion.5), channel_id=1, source_target_pairs={{0,3},{1,0},{2,1},{3,2},{4,7},{5,4},{6,5},{7,6},{8,11},{9,8},{10,9... | collective-permute-start | bytes 786440 | tf_op jit(solution)/shard_map/ppermute | solution.py:298
  60.6 23.1 %collective-permute-start.14 = (bf16[1,3,32,4096]{3,2,1,0:T(8,128)(2,1)}, bf16[1,3,32,4096]{3,2,1,0:T(8,128)(2,1)}, u32[]{:S(2)}, u32[]{:S(2)}) collective-permute-start(bf16[1,3,32,4096]{3,2,1,0:T(8,128)(2,1)} %maximum_bitcast_fusion.refs_2_), channel_id=1, source_target_pairs={{0,4},{4,0},{8,12},{12,8},{16,20},{20,16},{24,28},{28,24},{1,5},{5... | collective-permute-start | bytes 2359304 | tf_op jit(solution)/shard_map/ppermute | solution.py:294
  69.6 12.3 %collective-permute-start.8 = (bf16[1,3,32,4096]{3,2,1,0:T(8,128)(2,1)}, bf16[1,3,32,4096]{3,2,1,0:T(8,128)(2,1)S(1)}, u32[]{:S(2)}, u32[]{:S(2)}) collective-permute-start(bf16[1,3,32,4096]{3,2,1,0:T(8,128)(2,1)} %collective-permute-done.4.refs_3_), channel_id=1, source_target_pairs={{0,16},{4,12},{8,24},{12,4},{16,0},{20,28},{24,8},{28,20},{1,17},{... | collective-permute-start | bytes 2359304 | tf_op jit(solution)/shard_map/ppermute | solution.py:468
  72.0 12.2 %collective-permute-start.15 = (bf16[1,3,32,4096]{3,2,1,0:T(8,128)(2,1)}, bf16[1,3,32,4096]{3,2,1,0:T(8,128)(2,1)}, u32[]{:S(2)}, u32[]{:S(2)}) collective-permute-start(bf16[1,3,32,4096]{3,2,1,0:T(8,128)(2,1)} %collective-permute-done.4.refs_3_), channel_id=1, source_target_pairs={{0,4},{4,0},{8,12},{12,8},{16,20},{20,16},{24,28},{28,24},{1,5},{5... | collective-permute-start | bytes 2359304 | tf_op jit(solution)/shard_map/ppermute | solution.py:294
  83.1 49.4 %collective-permute-start.12 = (bf16[1,3,32,4096]{3,2,1,0:T(8,128)(2,1)S(1)}, bf16[1,3,32,4096]{3,2,1,0:T(8,128)(2,1)}, u32[]{:S(2)}, u32[]{:S(2)}) collective-permute-start(bf16[1,3,32,4096]{3,2,1,0:T(8,128)(2,1)S(1)} %maximum_bitcast_fusion.1.refs_1_), channel_id=1, source_target_pairs={{0,16},{4,12},{8,24},{12,4},{16,0},{20,28},{24,8},{28,20},{1,17},{... | collective-permute-start | bytes 2359304 | tf_op jit(solution)/shard_map/ppermute | solution.py:468
  83.7 19.0 %collective-permute-start.13 = (bf16[1,3,32,4096]{3,2,1,0:T(8,128)(2,1)S(1)}, bf16[1,3,32,4096]{3,2,1,0:T(8,128)(2,1)}, u32[]{:S(2)}, u32[]{:S(2)}) collective-permute-start(bf16[1,3,32,4096]{3,2,1,0:T(8,128)(2,1)S(1)} %maximum_bitcast_fusion.1.refs_1_), channel_id=1, source_target_pairs={{0,8},{4,20},{8,0},{12,28},{16,24},{20,4},{24,16},{28,12},{1,9},{5... | collective-permute-start | bytes 2359304 | tf_op jit(solution)/shard_map/ppermute | solution.py:468
  102.8 29.9 %collective-permute-start.18 = (bf16[1,3,32,4096]{3,2,1,0:T(8,128)(2,1)}, bf16[1,3,32,4096]{3,2,1,0:T(8,128)(2,1)}, u32[]{:S(2)}, u32[]{:S(2)}) collective-permute-start(bf16[1,3,32,4096]{3,2,1,0:T(8,128)(2,1)} %collective-permute-done.13.refs_2_), channel_id=1, source_target_pairs={{0,16},{4,12},{8,24},{12,4},{16,0},{20,28},{24,8},{28,20},{1,17},{... | collective-permute-start | bytes 2359304 | tf_op jit(solution)/shard_map/ppermute | solution.py:468
  104.0 29.1 %collective-permute-start.9 = (bf16[128,1024]{1,0:T(8,128)(2,1)S(1)}, bf16[128,1024]{1,0:T(8,128)(2,1)S(1)}, u32[]{:S(2)}, u32[]{:S(2)}) collective-permute-start(bf16[128,1024]{1,0:T(8,128)(2,1)S(1)} %copy-done.41), channel_id=1, source_target_pairs={{0,1},{1,2},{2,3},{3,0},{4,5},{5,6},{6,7},{7,4},{8,9},{9,10},{10,1... | collective-permute-start | bytes 786440 | tf_op jit(solution)/shard_map/ppermute | solution.py:298
  110.0 23.1 %collective-permute-start.10 = (bf16[128,1024]{1,0:T(8,128)(2,1)S(1)}, bf16[128,1024]{1,0:T(8,128)(2,1)}, u32[]{:S(2)}, u32[]{:S(2)}) collective-permute-start(bf16[128,1024]{1,0:T(8,128)(2,1)S(1)} %copy-done.41), channel_id=1, source_target_pairs={{0,2},{1,3},{2,0},{3,1},{4,6},{5,7},{6,4},{7,5},{8,10},{9,11},{10,... | collective-permute-start | bytes 786440 | tf_op jit(solution)/shard_map/ppermute | solution.py:298
  112.5 20.7 %collective-permute-start.11 = (bf16[128,1024]{1,0:T(8,128)(2,1)S(1)}, bf16[128,1024]{1,0:T(8,128)(2,1)}, u32[]{:S(2)}, u32[]{:S(2)}) collective-permute-start(bf16[128,1024]{1,0:T(8,128)(2,1)S(1)} %copy-done.41), channel_id=1, source_target_pairs={{0,3},{1,0},{2,1},{3,2},{4,7},{5,4},{6,5},{7,6},{8,11},{9,8},{10,9... | collective-permute-start | bytes 786440 | tf_op jit(solution)/shard_map/ppermute | solution.py:298
  132.6 16.4 %collective-permute-start.22 = (bf16[1,3,32,4096]{3,2,1,0:T(8,128)(2,1)S(1)}, bf16[1,3,32,4096]{3,2,1,0:T(8,128)(2,1)S(1)}, u32[]{:S(2)}, u32[]{:S(2)}) collective-permute-start(bf16[1,3,32,4096]{3,2,1,0:T(8,128)(2,1)S(1)} %maximum_bitcast_fusion.1.refs_1_), channel_id=1, source_target_pairs={{0,4},{4,0},{8,12},{12,8},{16,20},{20,16},{24,28},{28,24},{1,5},{5... | collective-permute-start | bytes 2359304 | tf_op jit(solution)/shard_map/ppermute | solution.py:294
  132.7 17.7 %collective-permute-start.23 = (bf16[1,3,32,4096]{3,2,1,0:T(8,128)(2,1)}, bf16[1,3,32,4096]{3,2,1,0:T(8,128)(2,1)}, u32[]{:S(2)}, u32[]{:S(2)}) collective-permute-start(bf16[1,3,32,4096]{3,2,1,0:T(8,128)(2,1)} %collective-permute-done.13.refs_2_), channel_id=1, source_target_pairs={{0,4},{4,0},{8,12},{12,8},{16,20},{20,16},{24,28},{28,24},{1,5},{5... | collective-permute-start | bytes 2359304 | tf_op jit(solution)/shard_map/ppermute | solution.py:294
  135.2 12.3 %collective-permute-start.19 = (bf16[1,3,128,1024]{3,2,1,0:T(8,128)(2,1)}, bf16[1,3,128,1024]{3,2,1,0:T(8,128)(2,1)}, u32[]{:S(2)}, u32[]{:S(2)}) collective-permute-start(bf16[1,3,128,1024]{3,2,1,0:T(8,128)(2,1)} %maximum_bitcast_fusion.2.refs_1_), channel_id=1, source_target_pairs={{0,8},{4,20},{8,0},{12,28},{16,24},{20,4},{24,16},{28,12},{1,9},{5... | collective-permute-start | bytes 2359304 | tf_op jit(solution)/shard_map/ppermute | solution.py:468
  135.7 14.7 %collective-permute-start.24 = (bf16[1,3,32,4096]{3,2,1,0:T(8,128)(2,1)}, bf16[1,3,32,4096]{3,2,1,0:T(8,128)(2,1)}, u32[]{:S(2)}, u32[]{:S(2)}) collective-permute-start(bf16[1,3,32,4096]{3,2,1,0:T(8,128)(2,1)} %collective-permute-done.12.refs_3_), channel_id=1, source_target_pairs={{0,4},{4,0},{8,12},{12,8},{16,20},{20,16},{24,28},{28,24},{1,5},{5... | collective-permute-start | bytes 2359304 | tf_op jit(solution)/shard_map/ppermute | solution.py:294
  136.5 13.9 %collective-permute-start.25 = (bf16[1,3,32,4096]{3,2,1,0:T(8,128)(2,1)}, bf16[1,3,32,4096]{3,2,1,0:T(8,128)(2,1)}, u32[]{:S(2)}, u32[]{:S(2)}) collective-permute-start(bf16[1,3,32,4096]{3,2,1,0:T(8,128)(2,1)} %collective-permute-done.18.refs_4_), channel_id=1, source_target_pairs={{0,4},{4,0},{8,12},{12,8},{16,20},{20,16},{24,28},{28,24},{1,5},{5... | collective-permute-start | bytes 2359304 | tf_op jit(solution)/shard_map/ppermute | solution.py:294
  147.5 21.0 %collective-permute-start.20 = (bf16[1,3,128,1024]{3,2,1,0:T(8,128)(2,1)}, bf16[1,3,128,1024]{3,2,1,0:T(8,128)(2,1)}, u32[]{:S(2)}, u32[]{:S(2)}) collective-permute-start(bf16[1,3,128,1024]{3,2,1,0:T(8,128)(2,1)} %maximum_bitcast_fusion.2.refs_1_), channel_id=1, source_target_pairs={{0,16},{4,12},{8,24},{12,4},{16,0},{20,28},{24,8},{28,20},{1,17},{... | collective-permute-start | bytes 2359304 | tf_op jit(solution)/shard_map/ppermute | solution.py:468
  149.9 18.6 %collective-permute-start.21 = (bf16[1,3,128,1024]{3,2,1,0:T(8,128)(2,1)}, bf16[1,3,128,1024]{3,2,1,0:T(8,128)(2,1)}, u32[]{:S(2)}, u32[]{:S(2)}) collective-permute-start(bf16[1,3,128,1024]{3,2,1,0:T(8,128)(2,1)} %collective-permute-done.19.refs_2_), channel_id=1, source_target_pairs={{0,16},{4,12},{8,24},{12,4},{16,0},{20,28},{24,8},{28,20},{1,17},{... | collective-permute-start | bytes 2359304 | tf_op jit(solution)/shard_map/ppermute | solution.py:468
  179.9 20.3 %collective-permute-start.30 = (bf16[4,4,128,1024]{3,2,1,0:T(8,128)(2,1)}, bf16[4,4,128,1024]{3,2,1,0:T(8,128)(2,1)}, u32[]{:S(2)}, u32[]{:S(2)}) collective-permute-start(bf16[4,4,128,1024]{3,2,1,0:T(8,128)(2,1)} %bitcast.24), channel_id=1, source_target_pairs={{0,4},{4,0},{8,12},{12,8},{16,20},{20,16},{24,28},{28,24},{1,5},{5... | collective-permute-start | bytes 12582920 | tf_op jit(solution)/shard_map/ppermute | solution.py:294
  180.7 11.0 %collective-permute-start.28 = (bf16[1,3,128,1024]{3,2,1,0:T(8,128)(2,1)}, bf16[1,3,128,1024]{3,2,1,0:T(8,128)(2,1)S(1)}, u32[]{:S(2)}, u32[]{:S(2)}) collective-permute-start(bf16[1,3,128,1024]{3,2,1,0:T(8,128)(2,1)} %collective-permute-done.20.refs_3_), channel_id=1, source_target_pairs={{0,4},{4,0},{8,12},{12,8},{16,20},{20,16},{24,28},{28,24},{1,5},{5... | collective-permute-start | bytes 2359304 | tf_op jit(solution)/shard_map/ppermute | solution.py:294
  181.1 11.5 %collective-permute-start.29 = (bf16[1,3,128,1024]{3,2,1,0:T(8,128)(2,1)}, bf16[1,3,128,1024]{3,2,1,0:T(8,128)(2,1)}, u32[]{:S(2)}, u32[]{:S(2)}) collective-permute-start(bf16[1,3,128,1024]{3,2,1,0:T(8,128)(2,1)} %collective-permute-done.21.refs_4_), channel_id=1, source_target_pairs={{0,4},{4,0},{8,12},{12,8},{16,20},{20,16},{24,28},{28,24},{1,5},{5... | collective-permute-start | bytes 2359304 | tf_op jit(solution)/shard_map/ppermute | solution.py:294
  221.0 15.2 %collective-permute-start.31 = (bf16[4,4,32,4096]{3,2,1,0:T(8,128)(2,1)}, bf16[4,4,32,4096]{3,2,1,0:T(8,128)(2,1)}, u32[]{:S(2)}, u32[]{:S(2)}) collective-permute-start(bf16[4,4,32,4096]{3,2,1,0:T(8,128)(2,1)} %bitcast.26), channel_id=1, source_target_pairs={{0,4},{4,0},{8,12},{12,8},{16,20},{20,16},{24,28},{28,24},{1,5},{5... | collective-permute-start | bytes 12582920 | tf_op jit(solution)/shard_map/ppermute | solution.py:294
  221.5 27.6 %collective-permute-start.32 = (bf16[2,4,128,1024]{3,2,1,0:T(8,128)(2,1)S(1)}, bf16[2,4,128,1024]{3,2,1,0:T(8,128)(2,1)}, u32[]{:S(2)}, u32[]{:S(2)}) collective-permute-start(bf16[2,4,128,1024]{3,2,1,0:T(8,128)(2,1)S(1)} %fusion.6), channel_id=1, source_target_pairs={{0,8},{4,20},{8,0},{12,28},{16,24},{20,4},{24,16},{28,12},{1,9},{5... | collective-permute-start | bytes 6291464 | tf_op jit(solution)/shard_map/ppermute | solution.py:315
  241.6 39.8 %collective-permute-start.34 = (bf16[2,4,32,4096]{3,2,1,0:T(8,128)(2,1)}, bf16[2,4,32,4096]{3,2,1,0:T(8,128)(2,1)}, u32[]{:S(2)}, u32[]{:S(2)}) collective-permute-start(bf16[2,4,32,4096]{3,2,1,0:T(8,128)(2,1)} %fusion.5), channel_id=1, source_target_pairs={{0,8},{4,20},{8,0},{12,28},{16,24},{20,4},{24,16},{28,12},{1,9},{5... | collective-permute-start | bytes 6291464 | tf_op jit(solution)/shard_map/ppermute | solution.py:315
  254.0 26.3 %collective-permute-start.33 = (bf16[1,4,128,1024]{3,2,1,0:T(8,128)(2,1)}, bf16[1,4,128,1024]{3,2,1,0:T(8,128)(2,1)}, u32[]{:S(2)}, u32[]{:S(2)}) collective-permute-start(bf16[1,4,128,1024]{3,2,1,0:T(8,128)(2,1)} %fusion.16), channel_id=1, source_target_pairs={{0,16},{4,12},{8,24},{12,4},{16,0},{20,28},{24,8},{28,20},{1,17},{... | collective-permute-start | bytes 3145736 | tf_op jit(solution)/shard_map/ppermute | solution.py:315
  255.5 24.9 %collective-permute-start.35 = (bf16[4,4,32,1024]{3,2,1,0:T(8,128)(2,1)}, bf16[4,4,32,1024]{3,2,1,0:T(8,128)(2,1)}, u32[]{:S(2)}, u32[]{:S(2)}) collective-permute-start(bf16[4,4,32,1024]{3,2,1,0:T(8,128)(2,1)} %bitcast.29), channel_id=1, source_target_pairs={{0,4},{4,0},{8,12},{12,8},{16,20},{20,16},{24,28},{28,24},{1,5},{5... | collective-permute-start | bytes 3145736 | tf_op jit(solution)/shard_map/ppermute | solution.py:294
  288.9 27.9 %collective-permute-start.39 = (bf16[1,4,32,4096]{3,2,1,0:T(8,128)(2,1)}, bf16[1,4,32,4096]{3,2,1,0:T(8,128)(2,1)}, u32[]{:S(2)}, u32[]{:S(2)}) collective-permute-start(bf16[1,4,32,4096]{3,2,1,0:T(8,128)(2,1)} %fusion.14), channel_id=1, source_target_pairs={{0,16},{4,12},{8,24},{12,4},{16,0},{20,28},{24,8},{28,20},{1,17},{... | collective-permute-start | bytes 3145736 | tf_op jit(solution)/shard_map/ppermute | solution.py:315
  290.4 26.4 %collective-permute-start.40 = (bf16[2,4,32,1024]{3,2,1,0:T(8,128)(2,1)S(1)}, bf16[2,4,32,1024]{3,2,1,0:T(8,128)(2,1)S(1)}, u32[]{:S(2)}, u32[]{:S(2)}) collective-permute-start(bf16[2,4,32,1024]{3,2,1,0:T(8,128)(2,1)S(1)} %fusion.26), channel_id=1, source_target_pairs={{0,8},{4,20},{8,0},{12,28},{16,24},{20,4},{24,16},{28,12},{1,9},{5... | collective-permute-start | bytes 1572872 | tf_op jit(solution)/shard_map/ppermute | solution.py:315
  290.9 25.8 %collective-permute-start.36 = (bf16[128,1024]{1,0:T(8,128)(2,1)}, bf16[128,1024]{1,0:T(8,128)(2,1)}, u32[]{:S(2)}, u32[]{:S(2)}) collective-permute-start(bf16[128,1024]{1,0:T(8,128)(2,1)} %get-tuple-element.181), channel_id=1, source_target_pairs={{0,1},{1,2},{2,3},{3,0},{4,5},{5,6},{6,7},{7,4},{8,9},{9,10},{10,1... | collective-permute-start | bytes 786440 | tf_op jit(solution)/shard_map/ppermute | solution.py:298
  293.0 23.7 %collective-permute-start.37 = (bf16[128,1024]{1,0:T(8,128)(2,1)}, bf16[128,1024]{1,0:T(8,128)(2,1)}, u32[]{:S(2)}, u32[]{:S(2)}) collective-permute-start(bf16[128,1024]{1,0:T(8,128)(2,1)} %get-tuple-element.182), channel_id=1, source_target_pairs={{0,2},{1,3},{2,0},{3,1},{4,6},{5,7},{6,4},{7,5},{8,10},{9,11},{10,... | collective-permute-start | bytes 786440 | tf_op jit(solution)/shard_map/ppermute | solution.py:298
  293.5 23.2 %collective-permute-start.38 = (bf16[128,1024]{1,0:T(8,128)(2,1)}, bf16[128,1024]{1,0:T(8,128)(2,1)}, u32[]{:S(2)}, u32[]{:S(2)}) collective-permute-start(bf16[128,1024]{1,0:T(8,128)(2,1)} %get-tuple-element.183), channel_id=1, source_target_pairs={{0,3},{1,0},{2,1},{3,2},{4,7},{5,4},{6,5},{7,6},{8,11},{9,8},{10,9... | collective-permute-start | bytes 786440 | tf_op jit(solution)/shard_map/ppermute | solution.py:298
  328.0 31.8 %collective-permute-start.46 = (bf16[4,4,32,3072]{3,2,1,0:T(8,128)(2,1)}, bf16[4,4,32,3072]{3,2,1,0:T(8,128)(2,1)}, u32[]{:S(2)}, u32[]{:S(2)}) collective-permute-start(bf16[4,4,32,3072]{3,2,1,0:T(8,128)(2,1)} %bitcast.55), channel_id=1, source_target_pairs={{0,4},{4,0},{8,12},{12,8},{16,20},{20,16},{24,28},{28,24},{1,5},{5... | collective-permute-start | bytes 9437192 | tf_op jit(solution)/shard_map/ppermute | solution.py:294
  329.2 13.3 %collective-permute-start.41 = (bf16[1,128,1024]{2,1,0:T(8,128)(2,1)S(1)}, bf16[1,128,1024]{2,1,0:T(8,128)(2,1)S(1)}, u32[]{:S(2)}, u32[]{:S(2)}) collective-permute-start(bf16[1,128,1024]{2,1,0:T(8,128)(2,1)S(1)} %fusion.64), channel_id=1, source_target_pairs={{0,8},{4,20},{8,0},{12,28},{16,24},{20,4},{24,16},{28,12},{1,9},{5... | collective-permute-start | bytes 786440 | tf_op jit(solution)/shard_map/ppermute | solution.py:326
  338.2 11.2 %collective-permute-start.42 = (bf16[32,4096]{1,0:T(8,128)(2,1)S(1)}, bf16[32,4096]{1,0:T(8,128)(2,1)S(1)}, u32[]{:S(2)}, u32[]{:S(2)}) collective-permute-start(bf16[32,4096]{1,0:T(8,128)(2,1)S(1)} %copy-done.52), channel_id=1, source_target_pairs={{0,1},{1,2},{2,3},{3,0},{4,5},{5,6},{6,7},{7,4},{8,9},{9,10},{10,1... | collective-permute-start | bytes 786440 | tf_op jit(solution)/shard_map/ppermute | solution.py:298
  338.6 21.1 %collective-permute-start.43 = (bf16[32,4096]{1,0:T(8,128)(2,1)S(1)}, bf16[32,4096]{1,0:T(8,128)(2,1)S(1)}, u32[]{:S(2)}, u32[]{:S(2)}) collective-permute-start(bf16[32,4096]{1,0:T(8,128)(2,1)S(1)} %copy-done.51), channel_id=1, source_target_pairs={{0,2},{1,3},{2,0},{3,1},{4,6},{5,7},{6,4},{7,5},{8,10},{9,11},{10,... | collective-permute-start | bytes 786440 | tf_op jit(solution)/shard_map/ppermute | solution.py:298
  340.9 18.9 %collective-permute-start.44 = (bf16[32,4096]{1,0:T(8,128)(2,1)S(1)}, bf16[32,4096]{1,0:T(8,128)(2,1)S(1)}, u32[]{:S(2)}, u32[]{:S(2)}) collective-permute-start(bf16[32,4096]{1,0:T(8,128)(2,1)S(1)} %copy-done.50), channel_id=1, source_target_pairs={{0,3},{1,0},{2,1},{3,2},{4,7},{5,4},{6,5},{7,6},{8,11},{9,8},{10,9... | collective-permute-start | bytes 786440 | tf_op jit(solution)/shard_map/ppermute | solution.py:298
  342.5 17.2 %collective-permute-start.45 = (bf16[1,4,32,1024]{3,2,1,0:T(8,128)(2,1)S(1)}, bf16[1,4,32,1024]{3,2,1,0:T(8,128)(2,1)S(1)}, u32[]{:S(2)}, u32[]{:S(2)}) collective-permute-start(bf16[1,4,32,1024]{3,2,1,0:T(8,128)(2,1)S(1)} %fusion.38), channel_id=1, source_target_pairs={{0,16},{4,12},{8,24},{12,4},{16,0},{20,28},{24,8},{28,20},{1,17},{... | collective-permute-start | bytes 786440 | tf_op jit(solution)/shard_map/ppermute | solution.py:315
  367.8 20.8 %collective-permute-start.53 = (bf16[2,4,32,3072]{3,2,1,0:T(8,128)(2,1)}, bf16[2,4,32,3072]{3,2,1,0:T(8,128)(2,1)}, u32[]{:S(2)}, u32[]{:S(2)}) collective-permute-start(bf16[2,4,32,3072]{3,2,1,0:T(8,128)(2,1)} %fusion.10), channel_id=1, source_target_pairs={{0,8},{4,20},{8,0},{12,28},{16,24},{20,4},{24,16},{28,12},{1,9},{5... | collective-permute-start | bytes 4718600 | tf_op jit(solution)/shard_map/ppermute | solution.py:315
  373.7 17.9 %collective-permute-start.63 = (bf16[32,1024]{1,0:T(8,128)(2,1)S(1)}, bf16[32,1024]{1,0:T(8,128)(2,1)S(1)}, u32[]{:S(2)}, u32[]{:S(2)}) collective-permute-start(bf16[32,1024]{1,0:T(8,128)(2,1)S(1)} %copy-done.55), channel_id=1, source_target_pairs={{0,3},{1,0},{2,1},{3,2},{4,7},{5,4},{6,5},{7,6},{8,11},{9,8},{10,9... | collective-permute-start | bytes 196616 | tf_op jit(solution)/shard_map/ppermute | solution.py:298
  379.7 12.0 %collective-permute-start.62 = (bf16[32,1024]{1,0:T(8,128)(2,1)S(1)}, bf16[32,1024]{1,0:T(8,128)(2,1)S(1)}, u32[]{:S(2)}, u32[]{:S(2)}) collective-permute-start(bf16[32,1024]{1,0:T(8,128)(2,1)S(1)} %copy-done.54), channel_id=1, source_target_pairs={{0,2},{1,3},{2,0},{3,1},{4,6},{5,7},{6,4},{7,5},{8,10},{9,11},{10,... | collective-permute-start | bytes 196616 | tf_op jit(solution)/shard_map/ppermute | solution.py:298
  381.3 10.4 %collective-permute-start.61 = (bf16[32,1024]{1,0:T(8,128)(2,1)S(1)}, bf16[32,1024]{1,0:T(8,128)(2,1)S(1)}, u32[]{:S(2)}, u32[]{:S(2)}) collective-permute-start(bf16[32,1024]{1,0:T(8,128)(2,1)S(1)} %copy-done.53), channel_id=1, source_target_pairs={{0,1},{1,2},{2,3},{3,0},{4,5},{5,6},{6,7},{7,4},{8,9},{9,10},{10,1... | collective-permute-start | bytes 196616 | tf_op jit(solution)/shard_map/ppermute | solution.py:298
  391.2 17.5 %collective-permute-start.54 = (bf16[1,4,32,3072]{3,2,1,0:T(8,128)(2,1)}, bf16[1,4,32,3072]{3,2,1,0:T(8,128)(2,1)S(1)}, u32[]{:S(2)}, u32[]{:S(2)}) collective-permute-start(bf16[1,4,32,3072]{3,2,1,0:T(8,128)(2,1)} %fusion.21), channel_id=1, source_target_pairs={{0,16},{4,12},{8,24},{12,4},{16,0},{20,28},{24,8},{28,20},{1,17},{... | collective-permute-start | bytes 2359304 | tf_op jit(solution)/shard_map/ppermute | solution.py:315
  394.2 13.7 %collective-permute-start.47 = (f32[4,64,256]{2,0,1:T(4,128)S(1)}, f32[4,64,256]{2,0,1:T(4,128)S(1)}, u32[]{:S(2)}, u32[]{:S(2)}) collective-permute-start(f32[4,64,256]{2,0,1:T(4,128)S(1)} %select_maximum_fusion), channel_id=1, source_target_pairs={{0,4},{4,0},{8,12},{12,8},{16,20},{20,16},{24,28},{28,24},{1,5},{5... | collective-permute-start | bytes 786440 | tf_op jit(solution)/shard_map/ppermute | solution.py:337
  399.3 18.9 %collective-permute-start.67 = (bf16[1,32,4096]{2,1,0:T(8,128)(2,1)S(1)}, bf16[1,32,4096]{2,1,0:T(8,128)(2,1)S(1)}, u32[]{:S(2)}, u32[]{:S(2)}) collective-permute-start(bf16[1,32,4096]{2,1,0:T(8,128)(2,1)S(1)} %fusion.65), channel_id=1, source_target_pairs={{0,8},{4,20},{8,0},{12,28},{16,24},{20,4},{24,16},{28,12},{1,9},{5... | collective-permute-start | bytes 786440 | tf_op jit(solution)/shard_map/ppermute | solution.py:326
  400.2 33.9 %collective-permute-start.70 = (bf16[2,128,1024]{2,1,0:T(8,128)(2,1)}, bf16[2,128,1024]{2,1,0:T(8,128)(2,1)S(1)}, u32[]{:S(2)}, u32[]{:S(2)}) collective-permute-start(bf16[2,128,1024]{2,1,0:T(8,128)(2,1)} %pad_maximum_fusion.4), channel_id=1, source_target_pairs={{0,16},{4,12},{8,24},{12,4},{16,0},{20,28},{24,8},{28,20},{1,17},{... | collective-permute-start | bytes 1572872 | tf_op jit(solution)/shard_map/ppermute | solution.py:326
  408.0 10.3 %collective-permute-start.48 = (f32[4,64,256]{2,0,1:T(4,128)S(1)}, f32[4,64,256]{2,0,1:T(4,128)S(1)}, u32[]{:S(2)}, u32[]{:S(2)}) collective-permute-start(f32[4,64,256]{2,0,1:T(4,128)S(1)} %fusion.93), channel_id=1, source_target_pairs={{0,8},{4,12},{8,0},{12,4},{16,24},{20,28},{24,16},{28,20},{1,9},{5... | collective-permute-start | bytes 786440 | tf_op jit(solution)/shard_map/ppermute | solution.py:337
  410.8 11.9 %collective-permute-start.57 = (bf16[32,3072]{1,0:T(8,128)(2,1)S(1)}, bf16[32,3072]{1,0:T(8,128)(2,1)S(1)}, u32[]{:S(2)}, u32[]{:S(2)}) collective-permute-start(bf16[32,3072]{1,0:T(8,128)(2,1)S(1)} %get-tuple-element.235), channel_id=1, source_target_pairs={{0,3},{1,0},{2,1},{3,2},{4,7},{5,4},{6,5},{7,6},{8,11},{9,8},{10,9... | collective-permute-start | bytes 589832 | tf_op jit(solution)/shard_map/ppermute | solution.py:298
  416.6 15.7 %collective-permute-start.56 = (bf16[32,3072]{1,0:T(8,128)(2,1)S(1)}, bf16[32,3072]{1,0:T(8,128)(2,1)S(1)}, u32[]{:S(2)}, u32[]{:S(2)}) collective-permute-start(bf16[32,3072]{1,0:T(8,128)(2,1)S(1)} %get-tuple-element.236), channel_id=1, source_target_pairs={{0,2},{1,3},{2,0},{3,1},{4,6},{5,7},{6,4},{7,5},{8,10},{9,11},{10,... | collective-permute-start | bytes 589832 | tf_op jit(solution)/shard_map/ppermute | solution.py:298
  418.2 14.2 %collective-permute-start.55 = (bf16[32,3072]{1,0:T(8,128)(2,1)S(1)}, bf16[32,3072]{1,0:T(8,128)(2,1)S(1)}, u32[]{:S(2)}, u32[]{:S(2)}) collective-permute-start(bf16[32,3072]{1,0:T(8,128)(2,1)S(1)} %get-tuple-element.234), channel_id=1, source_target_pairs={{0,1},{1,2},{2,3},{3,0},{4,5},{5,6},{6,7},{7,4},{8,9},{9,10},{10,1... | collective-permute-start | bytes 589832 | tf_op jit(solution)/shard_map/ppermute | solution.py:298
  418.3 39.8 %collective-permute-start.66 = (bf16[4,32,1024]{2,1,0:T(8,128)(2,1)S(1)}, bf16[4,32,1024]{2,1,0:T(8,128)(2,1)S(1)}, u32[]{:S(2)}, u32[]{:S(2)}) collective-permute-start(bf16[4,32,1024]{2,1,0:T(8,128)(2,1)S(1)} %pad_maximum_fusion.9.refs_0_), channel_id=1, source_target_pairs={{0,4},{4,0},{8,12},{12,8},{16,20},{20,16},{24,28},{28,24},{1,5},{5... | collective-permute-start | bytes 786440 | tf_op jit(solution)/shard_map/ppermute | solution.py:294
  422.7 25.2 %collective-permute-start.68 = (bf16[2,32,4096]{2,1,0:T(8,128)(2,1)S(1)}, bf16[2,32,4096]{2,1,0:T(8,128)(2,1)S(1)}, u32[]{:S(2)}, u32[]{:S(2)}) collective-permute-start(bf16[2,32,4096]{2,1,0:T(8,128)(2,1)S(1)} %pad_maximum_fusion.5), channel_id=1, source_target_pairs={{0,16},{4,12},{8,24},{12,4},{16,0},{20,28},{24,8},{28,20},{1,17},{... | collective-permute-start | bytes 1572872 | tf_op jit(solution)/shard_map/ppermute | solution.py:326
  433.6 10.8 %collective-permute-start.58 = (bf16[1,32,3072]{2,1,0:T(8,128)(2,1)S(1)}, bf16[1,32,3072]{2,1,0:T(8,128)(2,1)S(1)}, u32[]{:S(2)}, u32[]{:S(2)}) collective-permute-start(bf16[1,32,3072]{2,1,0:T(8,128)(2,1)S(1)} %fusion.68), channel_id=1, source_target_pairs={{0,8},{4,20},{8,0},{12,28},{16,24},{20,4},{24,16},{28,12},{1,9},{5... | collective-permute-start | bytes 589832 | tf_op jit(solution)/shard_map/ppermute | solution.py:326
  434.2 38.2 %collective-permute-start.71 = (bf16[4,128,1024]{2,1,0:T(8,128)(2,1)S(1)}, bf16[4,128,1024]{2,1,0:T(8,128)(2,1)}, u32[]{:S(2)}, u32[]{:S(2)}) collective-permute-start(bf16[4,128,1024]{2,1,0:T(8,128)(2,1)S(1)} %pad_maximum_fusion.1.refs_0_), channel_id=1, source_target_pairs={{0,4},{4,0},{8,12},{12,8},{16,20},{20,16},{24,28},{28,24},{1,5},{5... | collective-permute-start | bytes 3145736 | tf_op jit(solution)/shard_map/ppermute | solution.py:294
  441.3 16.8 %collective-permute-start.52 = (f32[64,256]{1,0:T(8,128)S(1)}, f32[64,256]{1,0:T(8,128)S(1)}, u32[]{:S(2)}, u32[]{:S(2)}) collective-permute-start(f32[64,256]{1,0:T(8,128)S(1)} %bitcast.301), channel_id=1, source_target_pairs={{0,3},{1,0},{2,1},{3,2},{4,7},{5,4},{6,5},{7,6},{8,11},{9,8},{10,9... | collective-permute-start | bytes 196616 | tf_op jit(solution)/shard_map/ppermute | solution.py:298
  444.4 25.3 %collective-permute-start.51 = (f32[64,256]{1,0:T(8,128)}, f32[64,256]{1,0:T(8,128)}, u32[]{:S(2)}, u32[]{:S(2)}) collective-permute-start(f32[64,256]{1,0:T(8,128)} %bitcast.281), channel_id=1, source_target_pairs={{0,2},{1,3},{2,0},{3,1},{4,6},{5,7},{6,4},{7,5},{8,10},{9,11},{10,... | collective-permute-start | bytes 196616 | tf_op jit(solution)/shard_map/ppermute | solution.py:298
  455.7 14.0 %collective-permute-start.50 = (f32[64,256]{1,0:T(8,128)}, f32[64,256]{1,0:T(8,128)}, u32[]{:S(2)}, u32[]{:S(2)}) collective-permute-start(f32[64,256]{1,0:T(8,128)} %bitcast.282), channel_id=1, source_target_pairs={{0,1},{1,2},{2,3},{3,0},{4,5},{5,6},{6,7},{7,4},{8,9},{9,10},{10,1... | collective-permute-start | bytes 196616 | tf_op jit(solution)/shard_map/ppermute | solution.py:298
  458.1 18.2 %collective-permute-start.69 = (bf16[4,32,4096]{2,1,0:T(8,128)(2,1)S(1)}, bf16[4,32,4096]{2,1,0:T(8,128)(2,1)}, u32[]{:S(2)}, u32[]{:S(2)}) collective-permute-start(bf16[4,32,4096]{2,1,0:T(8,128)(2,1)S(1)} %pad_maximum_fusion.refs_0_), channel_id=1, source_target_pairs={{0,4},{4,0},{8,12},{12,8},{16,20},{20,16},{24,28},{28,24},{1,5},{5... | collective-permute-start | bytes 3145736 | tf_op jit(solution)/shard_map/ppermute | solution.py:294
  458.2 21.9 %collective-permute-start.60 = (bf16[4,32,3072]{2,1,0:T(8,128)(2,1)S(1)}, bf16[4,32,3072]{2,1,0:T(8,128)(2,1)}, u32[]{:S(2)}, u32[]{:S(2)}) collective-permute-start(bf16[4,32,3072]{2,1,0:T(8,128)(2,1)S(1)} %pad_maximum_fusion.2.refs_0_), channel_id=1, source_target_pairs={{0,4},{4,0},{8,12},{12,8},{16,20},{20,16},{24,28},{28,24},{1,5},{5... | collective-permute-start | bytes 2359304 | tf_op jit(solution)/shard_map/ppermute | solution.py:294
  (96 other events, 888.7 us)

commit v5 on v4

--- a/solution.py
+++ b/solution.py
@@ -305,22 +305,22 @@
     return total
 
 
-def reduce_steps(away, keep, n_dp, n_line):
-    (away,) = yield [away]
+def reduce_steps(grad, n_dp, n_line):
+    half = n_dp // 2
+    (away,) = yield [grad(half, n_dp).astype(jnp.bfloat16)]
     (got,) = yield [swap_core(away, n_dp)]
-    terms = [keep, got]
-    half = keep.shape[0] // 2
+    terms = [got]
+    half //= 2
     for stage in range(n_dp.bit_length() - 2):
-        (send,) = yield [add_up([term[half:] for term in terms]).astype(jnp.bfloat16)]
+        total = add_up([grad(half, 2 * half)] + [term[half:] for term in terms])
+        (send,) = yield [total.astype(jnp.bfloat16)]
         (got,) = yield [lax.ppermute(send, "dp", hop_pairs(n_dp, stage))]
         terms = [term[:half] for term in terms] + [got]
         half //= 2
-    terms = [term[0] for term in terms]
-    sends = yield [
-        add_up([term[step] for term in terms]).astype(jnp.bfloat16) for step in range(1, n_line)
-    ]
-    arrived = yield [ahead(send, n_line, step + 1) for step, send in enumerate(sends)]
-    parts = [add_up([term[0] for term in terms] + arrived).astype(jnp.bfloat16)[None]]
+    total = add_up([grad(0, 1)[0]] + [term[0] for term in terms]).astype(jnp.bfloat16)
+    sends = yield [total[step] for step in range(n_line)]
+    arrived = yield [ahead(sends[step], n_line, step) for step in range(1, n_line)]
+    parts = [add_up([sends[0]] + arrived).astype(jnp.bfloat16)[None]]
     for stage in range(n_dp.bit_length() - 2):
         (send,) = yield [jnp.concatenate(parts) if len(parts) > 1 else parts[0]]
         (got,) = yield [lax.ppermute(send, "dp", hop_pairs(n_dp, stage))]
@@ -424,10 +424,10 @@
         return lax.all_gather(smalls, "fsdp", axis=0)
 
     def first(self):
-        return self.full[:2]
+        return self.full[0]
 
     def second(self):
-        return self.full[2]
+        return self.full[1:3]
 
     def third(self):
         return self.full[3]
@@ -443,14 +443,10 @@
     def wide_columns(self, block):
         return block
 
-    def total(self, terms):
-        bf16 = jnp.bfloat16
-        outs = []
-        for left, right in terms:
-            grad = t_times(left, right).astype(bf16)
-            own = lax.psum_scatter(grad, "fsdp", scatter_dimension=0, tiled=True)
-            outs.append(lax.psum(own, "dp").astype(jnp.float32))
-        return Ready(outs)
+    def total(self, left, right):
+        grad = t_times(left, right).astype(jnp.bfloat16)
+        own = lax.psum_scatter(grad, "fsdp", scatter_dimension=0, tiled=True)
+        return Ready(lax.psum(own, "dp").astype(jnp.float32))
 
     def total_small(self, smalls):
         own = lax.psum_scatter(
@@ -467,9 +463,9 @@
     def hop(self, block, stage):
         return lax.ppermute(block, "dp", hop_pairs(self.n_dp, stage))
 
-    def fan(self, gate, rows):
+    def fan(self, gate, columns):
         self.line, gate = lax.optimization_barrier((self.line, gate))
-        near = jnp.stack([item[:rows] for item in self.line])[None]
+        near = jnp.stack([item[:, :columns] for item in self.line])[None]
         near, gate = lax.optimization_barrier((near, gate))
         self.parts = [near, self.hop(near, 0), self.hop(near, 1)]
         self.cores = [swap_core(near, self.n_dp)]
@@ -519,30 +515,26 @@
         n_dp = self.n_dp
         n_line = self.n_line
         shard = smalls.shape[1]
-        wide = w_qkv.shape[1] + w_out.shape[1]
-        fold = wide // shard
-        small_rows = -(-smalls.shape[0] // (16 * fold)) * 16
-        padded = jnp.pad(smalls, ((0, small_rows * fold - smalls.shape[0]), (0, 0)))
-        packed = jnp.concatenate(
-            [padded[i * small_rows : (i + 1) * small_rows] for i in range(fold)], axis=1
-        )
-        unit_one = jnp.concatenate(
-            [jnp.concatenate([self.pick(w_qkv), self.pick(w_out)], axis=1), packed]
-        )
-        unit_two, unit_three = (self.pick(w_fc1), self.pick(w_fc2))
         size = self.unit
+        wide = w_qkv.shape[1]
+        fold = -(-smalls.shape[0] // size)
+        padded = jnp.pad(smalls, ((0, size * fold - smalls.shape[0]), (0, 0)))
+        packed = [padded[i * size : (i + 1) * size] for i in range(fold)]
+        unit_one = jnp.concatenate([self.pick(w_qkv)] + packed, axis=1)
+        unit_two = jnp.concatenate([self.pick(w_out), self.pick(w_fc1)], axis=1)
+        unit_three = self.pick(w_fc2)
         one = Gather(unit_one, n_dp, n_line)
-        unit_two = one.fan(unit_two, size)
-        far = jnp.stack([item[size:] for item in one.line])
+        unit_two = one.fan(unit_two, wide)
+        far = jnp.stack([item[:, wide:] for item in one.line])
         two = Gather(unit_two, n_dp, n_line)
         two.line = one.forward(two.line)
         two.line = one.close(two.line)
-        table, unit_three = two.fan((self.got_table, unit_three), size)
+        table, unit_three = two.fan((self.got_table, unit_three), unit_two.shape[1])
         three = Gather(unit_three, n_dp, n_line)
-        full_qkv, full_out = assemble([w_qkv, w_out], one.parts + one.cores, table, n_line, size)
-        self.one = (full_qkv, full_out)
-        self.two = (w_fc1, two)
-        self.three = (w_fc2, three, unit_three.shape[0])
+        (full_qkv,) = assemble([w_qkv], one.parts + one.cores, table, n_line, size)
+        self.one = full_qkv
+        self.two = ([w_out, w_fc1], two)
+        self.three = (w_fc2, three, unit_three.shape)
         far = jnp.concatenate([far[:, :, i * shard : (i + 1) * shard] for i in range(fold)], axis=1)
         return jnp.take(jnp.concatenate([padded[None], far]), self.unline, axis=0)
 
@@ -553,7 +545,7 @@
         return self.two[1].forward(gate)
 
     def pass_two(self, gate):
-        return self.three[1].fan(self.two[1].close(gate), self.three[2])
+        return self.three[1].fan(self.two[1].close(gate), self.three[2][1])
 
     def pass_three(self, gate):
         return self.three[1].forward(gate)
@@ -562,12 +554,12 @@
         return self.three[1].close(gate)
 
     def second(self):
-        own, got = self.two
-        return assemble([own], got.parts + got.cores, self.got_table, self.n_line, self.unit)[0]
+        owns, got = self.two
+        return assemble(owns, got.parts + got.cores, self.got_table, self.n_line, self.unit)
 
     def third(self):
         own, got, unit = self.three
-        return assemble([own], got.parts + got.cores, self.got_table, self.n_line, unit)[0]
+        return assemble([own], got.parts + got.cores, self.got_table, self.n_line, unit[0])[0]
 
     def rows(self, block):
         return jnp.dot(block, self.order, preferred_element_type=jnp.float32).astype(jnp.bfloat16)
@@ -575,21 +567,17 @@
     def wide_columns(self, block):
         return column_order(block, self.send_table, block.shape[1] // (self.n_dp * self.n_line))
 
-    def total(self, terms):
+    def total(self, left, right):
         n_dp = self.n_dp
-        n_line = self.n_line
-        sides = []
-        for side in (1, 0):
-            grads = []
-            for left, right in terms:
-                half = left.shape[1] // 2
-                grad = t_times(left[:, side * half : (side + 1) * half], right).astype(jnp.bfloat16)
-                grads.append(grad.reshape(n_dp // 2, n_line, -1, right.shape[1]))
-            sides.append(jnp.concatenate(grads, axis=3) if len(grads) > 1 else grads[0])
-        cuts = [right.shape[1] for left, right in terms]
+        per = left.shape[1] // n_dp
         owner = self.owner.astype(jnp.int32)
-        steps = reduce_steps(sides[0], sides[1], n_dp, n_line)
-        return Reduction(steps, lambda parts: list(finish(parts, owner, cuts)))
+
+        def grad(first, last):
+            out = t_times(left[:, first * per : last * per], right)
+            return out.reshape(last - first, self.n_line, -1, right.shape[1])
+
+        steps = reduce_steps(grad, n_dp, self.n_line)
+        return Reduction(steps, lambda parts: finish(parts, owner, [right.shape[1]])[0])
 
     def total_small(self, smalls):
         n_small = smalls.shape[1]
@@ -640,7 +628,7 @@
     )
     n_small = smalls.shape[0]
     table = plan.gather(w_qkv, w_out, w_fc1, w_fc2, smalls)
-    full_qkv, full_out = plan.first()
+    full_qkv = plan.first()
 
     def across(block):
         return block.transpose(1, 0, 2).reshape(block.shape[1], width).astype(f32)
@@ -654,52 +642,54 @@
     projected = jnp.dot(normed_one, full_qkv, preferred_element_type=f32).astype(bf16)
     projected = plan.pass_one(projected)
     attn_rows = plan.pass_two(attend(projected, segment))
+    full_out, full_fc1 = plan.second()
     hidden_mid = hidden_in + jnp.dot(attn_rows, full_out, preferred_element_type=f32)
     normed_two = layer_norm(hidden_mid, gain_two, bias_two).astype(bf16)
-    normed_two = plan.pass_three(normed_two)
-    full_fc1 = plan.second()
     pre_act = jnp.dot(normed_two, full_fc1, preferred_element_type=f32) + full_bias
     share = 0.5 * (1.0 + lax.erf(pre_act * 0.5**0.5))
     bell = jnp.exp(-0.5 * pre_act * pre_act) * (0.5 / jnp.pi) ** 0.5
     activated = (pre_act * share).astype(bf16)
     slope = (share + pre_act * bell).astype(bf16)
-    activated = plan.pass_four(activated)
+    activated, slope = plan.pass_three((activated, slope))
     grad_out = jnp.where(valid[:, None], cotangent, jnp.zeros_like(cotangent))
-    run_fc2 = plan.total([(plan.wide_columns(activated), grad_out)])
-    activated = tick(activated, [run_fc2])
-    full_fc2, activated = tick((plan.third(), activated), [run_fc2])
+    run_fc2 = plan.total(plan.wide_columns(activated), grad_out)
+    activated, slope = tick((activated, slope), [run_fc2])
+    activated, slope = plan.pass_four((activated, slope))
+    full_fc2 = tick(plan.third(), [run_fc2])
     branch_out = jnp.dot(activated, full_fc2, preferred_element_type=f32)
     block_out = jnp.where(valid[:, None], hidden_mid + branch_out, 0.0).astype(bf16)
 
     grad_pre = (times_t(grad_out, full_fc2) * slope.astype(f32)).astype(bf16)
     grad_fc1_bias = jnp.sum(grad_pre.astype(f32), axis=0)
-    run_fc1 = plan.total([(plan.rows(normed_two), grad_pre)])
+    run_fc1 = plan.total(plan.rows(normed_two), grad_pre)
     grad_pre = tick(grad_pre, [run_fc1])
     grad_norm_two = times_t(grad_pre, full_fc1)
+    grad_norm_two = tick(grad_norm_two, [run_fc1, run_fc2])
     _, pull_two = jax.vjp(layer_norm, hidden_mid, gain_two, bias_two)
     back_mid, grad_gain_two, grad_bias_two = pull_two(grad_norm_two)
     grad_mid = grad_out.astype(f32) + back_mid
-    grad_branch = tick(grad_mid.astype(bf16), [run_fc1])
-    run_out = plan.total([(plan.rows(attn_rows), grad_branch)])
+    grad_branch = grad_mid.astype(bf16)
+    run_out = plan.total(plan.rows(attn_rows), grad_branch)
+    grad_branch = tick(grad_branch, [run_out])
     grad_attn = times_t(grad_branch, full_out).astype(bf16)
-    grad_attn = tick(grad_attn, [run_fc2, run_out])
+    grad_attn = tick(grad_attn, [run_out])
     half = HEADS // 4
     back_a = attend_back(projected, grad_attn, segment, 0, half)
     back_a, grad_attn = tick((back_a, grad_attn), [run_fc2, run_fc1, run_out])
     back_b = attend_back(projected, grad_attn, segment, half, half)
-    back_a, back_b = tick((back_a, back_b), [run_fc2, run_fc1, run_out])
     side = back_a.shape[1] // 3
     grad_proj = jnp.concatenate(
         [part[:, i * side : (i + 1) * side] for i in range(3) for part in (back_a, back_b)], axis=1
     )
-    run_qkv = plan.total([(plan.rows(normed_one), grad_proj)])
+    run_qkv = plan.total(plan.rows(normed_one), grad_proj)
     grad_proj = tick(grad_proj, [run_qkv])
-    grad_norm_one = times_t(grad_proj, full_qkv)
-    grad_norm_one = tick(grad_norm_one, [run_fc2, run_fc1, run_out, run_qkv])
+    grad_norm_one = tick(times_t(grad_proj, full_qkv), [run_qkv])
+    grad_norm_one = tick(grad_norm_one, [run_fc2, run_fc1, run_out])
     _, pull_one = jax.vjp(layer_norm, hidden_in, gain_one, bias_one)
     back_in, grad_gain_one, grad_bias_one = pull_one(grad_norm_one)
     grad_in = grad_mid + back_in
     grad_table = jnp.dot(place.T, grad_in, precision=highest)
+    grad_table, block_out = tick((grad_table, block_out), [run_qkv, run_fc1, run_fc2, run_out])
 
     def split(block):
         return block.reshape(-1, n_line, shard).transpose(1, 0, 2)
@@ -713,10 +703,10 @@
         axis=1,
     )
     run_small = plan.total_small(rows_small)
-    (sum_fc2,) = run_fc2.result()
-    (sum_fc1,) = run_fc1.result()
-    (sum_out,) = run_out.result()
-    (sum_qkv,) = run_qkv.result()
+    sum_fc2 = run_fc2.result()
+    sum_fc1 = run_fc1.result()
+    sum_out = run_out.result()
+    sum_qkv = run_qkv.result()
     small = run_small.result()
     return (
         block_out,

time: 490 us -> 520 us (1.061)
  waiting for transfers between devices: 112 us -> 131 us
  local copies, waits for them, and re-layouts: 35 us -> 23.7 us
  matrix products: 95 us -> 105 us
  starting transfers between devices: 89.1 us -> 99.1 us
    ppermute x9, waiting for transfers between devices: 17 us -> 33.5 us  [hop(): return lax.ppermute(block, 'dp', hop_pairs(self.n_dp, stage))]
    dot_general x8 -> x16, matrix products: 25.6 us -> 40.7 us  [t_times(): lax.dot_general(left, right, (((0,), (0,)), ((), ())), preferred_element_...]
    ppermute x16, waiting for transfers between devices: 29.8 us -> 39.5 us  [reduce_steps(): got, = (yield [lax.ppermute(send, 'dp', hop_pairs(n_dp, stage))])]
    unnamed x205 -> x133, local copies, waits for them, and re-layouts: 17.7 us -> 8.65 us
    ppermute x24, waiting for transfers between devices: 56.7 us -> 49.5 us  [ahead(): lax.ppermute(block, 'fsdp', [(i, (i + step) % n_line) for i in range(n_li...]
    dot_general x4, matrix products: 28.3 us -> 22.4 us  [times_t(): lax.dot_general(left, right, (((1,), (1,)), ((), ())), preferred_element_...]
    convert_element_type x14 -> x13, other arithmetic: 33.6 us -> 32.9 us  [the longest x8 23.8 us: reduce_steps(): send, = (yield [total.astype(jnp.bfloat16)])]
  transfers between devices with their start and end apart: 72 -> 72, of which waited for: 20 -> 28; matrix products, arithmetic and copies ran while one was open for 23% -> 22% of each run, Pallas kernels for 18% -> 13%
where the time goes in v5:
time: 520 us; the launch traced here: 512 us
  waiting for transfers between devices  131 us (25%)
  matrix products  105 us (20%)
  starting transfers between devices  99.1 us (19%)
  Pallas kernels  94.8 us (18%)
  other arithmetic  56 us (11%)
  local copies, waits for them, and re-layouts  23.7 us (5%)
    ppermute x24, starting transfers between devices, ahead(): lax.ppermute(block, 'fsdp', [(i, (i + step) % n_line) for i in range(n_li...  63 us
    ppermute x24, waiting for transfers between devices, ahead(): lax.ppermute(block, 'fsdp', [(i, (i + step) % n_line) for i in range(n_li...  49.5 us
    dot_general x16, matrix products, t_times(): lax.dot_general(left, right, (((0,), (0,)), ((), ())), preferred_element_...  40.7 us
    ppermute x16, waiting for transfers between devices, reduce_steps(): got, = (yield [lax.ppermute(send, 'dp', hop_pairs(n_dp, stage))])  39.5 us
    pallas_call x2, Pallas kernels, attend_back(): pl.pallas_call(body, grid=(count,), in_specs=pair_specs(rows, pairs, star...  37.8 us
    ppermute x9, waiting for transfers between devices, hop(): return lax.ppermute(block, 'dp', hop_pairs(self.n_dp, stage))  33.5 us
    convert_element_type x8, other arithmetic, reduce_steps(): send, = (yield [total.astype(jnp.bfloat16)])  23.8 us
    pallas_call x3, Pallas kernels, assemble(): pl.pallas_call(body, in_specs=[pl.BlockSpec(memory_space=pltpu.SMEM)] + [...  22.9 us
  transfers between devices with their start and end apart: 72, of which 28 were waited for; matrix products, arithmetic and copies ran while one was open for 22% of the time, Pallas kernels for 13%

profile of v5, /device:TPU:0, one launch (start us, length us, event | category | flops | bytes accessed | tf_op | source)
XLA Modules:
  0.0 512.0 jit_solution(2129289147900678633)
XLA Ops:
  5.8 3.1 collective-permute-start
  8.9 2.6 collective-permute-start.1
  18.5 7.9 %collective-permute-done.1 = bf16[32,3584]{1,0:T(8,128)(2,1)S(1)} collective-permute-done((bf16[32,3584]{1,0:T(8,128)(2,1)S(1)}, bf16[32,3584]{1,0:T(8,128)(2,1)S(1)}, u32[]{:S(2)}, u32[]{:S(2)}) %collective-permute-start.1) | collective-permute-done | bytes 229408 | tf_op jit(solution)/shard_map/ppermute | solution.py:298
  27.4 5.4 %collective-permute-start.5 = (bf16[32,5120]{1,0:T(8,128)(2,1)}, bf16[32,5120]{1,0:T(8,128)(2,1)}, u32[]{:S(2)}, u32[]{:S(2)}) collective-permute-start(bf16[32,5120]{1,0:T(8,128)(2,1)} %pad_maximum_fusion.6), channel_id=1, source_target_pairs={{0,1},{1,2},{2,3},{3,0},{4,5},{5,6},{6,7},{7,4},{8,9},{9,10},{10,1... | collective-permute-start | bytes 983048 | tf_op jit(solution)/shard_map/ppermute | solution.py:298
  40.3 2.6 collective-permute-done.5
  42.9 12.3 %collective-permute-done.6 = bf16[32,5120]{1,0:T(8,128)(2,1)} collective-permute-done((bf16[32,5120]{1,0:T(8,128)(2,1)}, bf16[32,5120]{1,0:T(8,128)(2,1)}, u32[]{:S(2)}, u32[]{:S(2)}) %collective-permute-start.6) | collective-permute-done | bytes 327712 | tf_op jit(solution)/shard_map/ppermute | solution.py:298
  57.2 8.1 %collective-permute-done.8.refs_4_ = bf16[1,3,32,3072]{3,2,1,0:T(8,128)(2,1)S(1)} collective-permute-done((bf16[1,3,32,3072]{3,2,1,0:T(8,128)(2,1)}, bf16[1,3,32,3072]{3,2,1,0:T(8,128)(2,1)S(1)}, u32[]{:S(2)}, u32[]{:S(2)}) %collective-permute-start.8) | collective-permute-done | bytes 589856 | tf_op jit(solution)/shard_map/ppermute | solution.py:464
  70.3 6.2 %assemble.3 = bf16[1024,3072]{1,0:T(8,128)(2,1)} custom-call(s32[33]{0:T(128)} %pad_add_fusion.1.table_ref, bf16[256,3072]{1,0:T(8,128)(2,1)} %refs_0_.3, bf16[1,3,32,3072]{3,2,1,0:T(8,128)(2,1)} %maximum_bitcast_fusion.2.refs_1_, bf16[1,3,32,3072]{3,2,1,0:T(8,128)(2,1)} %collective-permute-done.4.refs_2_, ...), custom_call_target="tpu_custom_call" | custom-call | tf_op jit(solution)/shard_map/assemble/pallas_call | solution.py:225
  76.5 7.8 %convolution_convert_fusion.2.refs_2_.refs_3_.refs_4_ = bf16[512,3072]{1,0:T(8,128)(2,1)} fusion(bf16[1024,3072]{1,0:T(8,128)(2,1)} %assemble.3, f32[512,1024]{1,0:T(8,128)S(1)} %get-tuple-element.296, f32[1024]{0:T(1024)S(1)} %bitcast.224, f32[1024]{0:T(1024)S(1)} %bitcast.214, f32[512]{0:T(512)S(1)} %fusion.73, f32[512]{0:T(512)S(1)} %broadcast_multiply_fusion.1), kind=kOutput, calls=%fused_computation.13 | convolution fusion | flops 3225419776 | bytes 11546624 | tf_op jit(solution)/shard_map/dot_general | solution.py:642
  84.3 7.2 %collective-permute-done.13.refs_3_ = bf16[1,3,32,5120]{3,2,1,0:T(8,128)(2,1)} collective-permute-done((bf16[1,3,32,5120]{3,2,1,0:T(8,128)(2,1)S(1)}, bf16[1,3,32,5120]{3,2,1,0:T(8,128)(2,1)}, u32[]{:S(2)}, u32[]{:S(2)}) %collective-permute-start.13) | collective-permute-done | bytes 983072 | tf_op jit(solution)/shard_map/ppermute | solution.py:464
  93.5 6.5 %collective-permute-start.10 = (bf16[128,1024]{1,0:T(8,128)(2,1)S(1)}, bf16[128,1024]{1,0:T(8,128)(2,1)}, u32[]{:S(2)}, u32[]{:S(2)}) collective-permute-start(bf16[128,1024]{1,0:T(8,128)(2,1)S(1)} %constant_dynamic-slice_fusion.4), channel_id=1, source_target_pairs={{0,2},{1,3},{2,0},{3,1},{4,6},{5,7},{6,4},{7,5},{8,10},{9,11},{10,... | collective-permute-start | bytes 786440 | tf_op jit(solution)/shard_map/ppermute | solution.py:298
  101.1 15.8 %attend.1 = bf16[512,1024]{1,0:T(8,128)(2,1)} custom-call(s32[512,1]{1,0:T(8,128)} %fusion.35.refs_0_, s32[1,512]{1,0:T(1,128)} %broadcast_select_fusion.2.refs_1_, bf16[512,3072]{1,0:T(8,128)(2,1)} %convolution_convert_fusion.2.refs_2_.refs_3_.refs_4_, bf16[512,3072]{1,0:T(8,128)(2,1)} %convolution_convert_fusion.2.refs_2_.refs_3_.refs_4_, ...), custom_call_target="tpu_custom_call" | custom-call | tf_op jit(solution)/shard_map/attend/pallas_call | solution.py:148
  117.5 3.4 collective-permute-start.11
  121.0 6.4 %collective-permute-done.11 = bf16[128,1024]{1,0:T(8,128)(2,1)S(1)} collective-permute-done((bf16[128,1024]{1,0:T(8,128)(2,1)S(1)}, bf16[128,1024]{1,0:T(8,128)(2,1)S(1)}, u32[]{:S(2)}, u32[]{:S(2)}) %collective-permute-start.11) | collective-permute-done | bytes 262176 | tf_op jit(solution)/shard_map/ppermute | solution.py:298
  129.8 7.2 %collective-permute-done.9 = bf16[128,1024]{1,0:T(8,128)(2,1)} collective-permute-done((bf16[128,1024]{1,0:T(8,128)(2,1)S(1)}, bf16[128,1024]{1,0:T(8,128)(2,1)}, u32[]{:S(2)}, u32[]{:S(2)}) %collective-permute-start.9) | collective-permute-done | bytes 262176 | tf_op jit(solution)/shard_map/ppermute | solution.py:298
  140.6 9.1 %assemble.4 = (bf16[1024,1024]{1,0:T(8,128)(2,1)}, bf16[1024,4096]{1,0:T(8,128)(2,1)}) custom-call(s32[33]{0:T(128)} %pad_add_fusion.1.table_ref, bf16[256,1024]{1,0:T(8,128)(2,1)} %refs_0_.4, bf16[256,4096]{1,0:T(8,128)(2,1)} %refs_1_.1, bf16[1,3,32,5120]{3,2,1,0:T(8,128)(2,1)} %copy-done.22, bf16[1,3,32,5120]{3,2,1,0:T(8,128)(2,1)} %collective-permute-done.13.refs_3_, ...), custom_call_target="tpu_custom_call" | custom-call | tf_op jit(solution)/shard_map/assemble/pallas_call | solution.py:225
  149.7 3.4 fusion.91
  154.0 11.4 %fusion.4 = (bf16[512,4096]{1,0:T(8,128)(2,1)}, bf16[512,4096]{1,0:T(8,128)(2,1)}) fusion(f32[4096]{0:T(1024)S(1)} %bitcast.222, bf16[1024,4096]{1,0:T(8,128)(2,1)S(1)} %copy-done.58, f32[512,1024]{1,0:T(8,128)S(1)} %get-tuple-element.298, f32[1024]{0:T(1024)S(1)} %bitcast.226, f32[1024]{0:T(1024)S(1)} %bitcast.218, f32[512]{0:T(512)S(1)} %fusion.74, ...), kind=kOutput, calls=%fused_computation.6 | convolution fusion | flops 4322754560 | bytes 18903040 | tf_op jit(solution)/shard_map/dot_general | solution.py:648
  165.4 5.4 %column_order.1 = bf16[512,4096]{1,0:T(8,128)(2,1)} custom-call(s32[32]{0:T(128)} %add.443.table_ref, bf16[512,4096]{1,0:T(8,128)(2,1)} %get-tuple-element.219.in_ref), custom_call_target="tpu_custom_call" | custom-call | tf_op jit(solution)/shard_map/column_order/pallas_call | solution.py:245
  170.8 6.1 %convolution_convert_fusion.3 = bf16[2048,1024]{1,0:T(8,128)(2,1)} fusion(bf16[512,4096]{1,0:T(8,128)(2,1)} %column_order.1, bf16[512,1024]{1,0:T(8,128)(2,1)S(1)} %copy-done.20, pred[512]{0:T(512)(128)(4,1)S(1)} %broadcast_select_fusion.3), kind=kOutput, calls=%fused_computation.20 | convolution fusion | flops 2150105088 | bytes 7340544 | tf_op jit(solution)/shard_map/dot_general | solution.py:69
  179.4 9.8 %collective-permute-done.24.refs_3_ = bf16[1,3,128,1024]{3,2,1,0:T(8,128)(2,1)} collective-permute-done((bf16[1,3,128,1024]{3,2,1,0:T(8,128)(2,1)}, bf16[1,3,128,1024]{3,2,1,0:T(8,128)(2,1)}, u32[]{:S(2)}, u32[]{:S(2)}) %collective-permute-start.24) | collective-permute-done | bytes 786464 | tf_op jit(solution)/shard_map/ppermute | solution.py:464
  189.2 8.4 %collective-permute-done.25.refs_4_ = bf16[1,3,128,1024]{3,2,1,0:T(8,128)(2,1)} collective-permute-done((bf16[1,3,128,1024]{3,2,1,0:T(8,128)(2,1)}, bf16[1,3,128,1024]{3,2,1,0:T(8,128)(2,1)}, u32[]{:S(2)}, u32[]{:S(2)}) %collective-permute-start.25) | collective-permute-done | bytes 786464 | tf_op jit(solution)/shard_map/ppermute | solution.py:464
  198.3 4.7 fusion.19
  203.0 2.5 fusion.15
  205.5 7.6 %assemble.5 = bf16[4096,1024]{1,0:T(8,128)(2,1)} custom-call(s32[33]{0:T(128)} %pad_add_fusion.1.table_ref, bf16[1024,1024]{1,0:T(8,128)(2,1)} %refs_0_.5, bf16[1,3,128,1024]{3,2,1,0:T(8,128)(2,1)} %maximum_bitcast_fusion.1.refs_1_, bf16[1,3,128,1024]{3,2,1,0:T(8,128)(2,1)} %collective-permute-done.19.refs_2_, ...), custom_call_target="tpu_custom_call" | custom-call | tf_op jit(solution)/shard_map/assemble/pallas_call | solution.py:225
  213.1 5.1 %add_convert_fusion.1 = bf16[2,4,128,1024]{3,2,1,0:T(8,128)(2,1)} fusion(f32[2,4,128,1024]{3,2,1,0:T(8,128)} %bitcast.200, bf16[4,4,128,1024]{3,2,1,0:T(8,128)(2,1)} %collective-permute-done.30), kind=kLoop, calls=%fused_computation.19 | loop fusion | flops 3145728 | bytes 8388608 | tf_op jit(solution)/shard_map/convert_element_type | solution.py:316
  219.1 7.2 %fusion.82 = f32[512,4096]{1,0:T(8,128)} fusion(bf16[4096,1024]{1,0:T(8,128)(2,1)S(1)} %copy-done.12, bf16[512,1024]{1,0:T(8,128)(2,1)S(1)} %copy-done.20, pred[512]{0:T(512)(128)(4,1)S(1)} %broadcast_select_fusion.3), kind=kOutput, calls=%fused_computation.265 | convolution fusion | flops 4295491584 | bytes 17826304 | tf_op jit(solution)/shard_map/dot_general | solution.py:65
  226.3 5.0 convert_reduce_fusion
  231.4 4.4 convolution_convert_fusion
  235.8 2.7 fusion.16
  242.3 7.1 %fusion.92 = f32[512,1024]{1,0:T(8,128)S(1)} fusion(bf16[512,4096]{1,0:T(8,128)(2,1)S(1)} %copy-done.1, bf16[1024,4096]{1,0:T(8,128)(2,1)} %get-tuple-element.164), kind=kOutput, calls=%fused_computation.275 | convolution fusion | flops 4294967296 | bytes 14680064 | tf_op jit(solution)/shard_map/dot_general | solution.py:65
  249.5 15.1 %collective-permute-done.32 = bf16[2,4,128,1024]{3,2,1,0:T(8,128)(2,1)S(1)} collective-permute-done((bf16[2,4,128,1024]{3,2,1,0:T(8,128)(2,1)S(1)}, bf16[2,4,128,1024]{3,2,1,0:T(8,128)(2,1)S(1)}, u32[]{:S(2)}, u32[]{:S(2)}) %collective-permute-start.32) | collective-permute-done | bytes 2097184 | tf_op jit(solution)/shard_map/ppermute | solution.py:317
  264.6 3.5 add_convert_fusion.4
  268.1 3.7 add_convert_fusion
  278.7 3.3 fusion.22
  289.2 19.0 %attend_back.2 = bf16[512,1536]{1,0:T(8,128)(2,1)} custom-call(s32[512,1]{1,0:T(8,128)} %fusion.35.refs_0_, s32[1,512]{1,0:T(1,128)} %broadcast_select_fusion.2.refs_1_, bf16[512,3072]{1,0:T(8,128)(2,1)} %convolution_convert_fusion.2.refs_2_.refs_3_.refs_4_, bf16[512,3072]{1,0:T(8,128)(2,1)} %convolution_convert_fusion.2.refs_2_.refs_3_.refs_4_, ...), custom_call_target="tpu_custom_call" | custom-call | tf_op jit(solution)/shard_map/attend_back/pallas_call | solution.py:167
  308.3 10.4 %collective-permute-done.36 = bf16[2,4,32,1024]{3,2,1,0:T(8,128)(2,1)S(1)} collective-permute-done((bf16[2,4,32,1024]{3,2,1,0:T(8,128)(2,1)}, bf16[2,4,32,1024]{3,2,1,0:T(8,128)(2,1)S(1)}, u32[]{:S(2)}, u32[]{:S(2)}) %collective-permute-start.36) | collective-permute-done | bytes 524320 | tf_op jit(solution)/shard_map/ppermute | solution.py:317
  318.7 3.4 fusion.10
  324.8 2.9 add_convert_fusion.3
  327.7 18.8 %attend_back.3 = bf16[512,1536]{1,0:T(8,128)(2,1)} custom-call(s32[512,1]{1,0:T(8,128)} %fusion.35.refs_0_, s32[1,512]{1,0:T(1,128)} %broadcast_select_fusion.2.refs_1_, bf16[512,3072]{1,0:T(8,128)(2,1)} %convolution_convert_fusion.2.refs_2_.refs_3_.refs_4_, bf16[512,3072]{1,0:T(8,128)(2,1)} %convolution_convert_fusion.2.refs_2_.refs_3_.refs_4_, ...), custom_call_target="tpu_custom_call" | custom-call | tf_op jit(solution)/shard_map/attend_back/pallas_call | solution.py:167
  351.3 3.5 convolution_convert_fusion.1
  354.8 8.9 %select_convert_fusion = bf16[512,1024]{1,0:T(8,128)(2,1)} fusion(f32[512,1024]{1,0:T(8,128)S(1)} %copy-done.7, bf16[512,4096]{1,0:T(8,128)(2,1)S(1)} %copy-done.19, bf16[4096,1024]{1,0:T(8,128)(2,1)} %assemble.5, pred[512]{0:T(512)(128)(4,1)S(1)} %broadcast_select_fusion.3), kind=kOutput, calls=%fused_computation.35 | convolution fusion | flops 4296540160 | bytes 15729152 | tf_op jit(solution)/shard_map/dot_general | solution.py:659
  363.8 4.3 fusion.57
  375.6 2.7 fusion.53
  380.2 5.8 %fusion.93 = f32[512,1024]{1,0:T(8,128)S(1)} fusion(bf16[512,3072]{1,0:T(8,128)(2,1)S(1)} %slice_dynamic-update-slice_fusion, bf16[1024,3072]{1,0:T(8,128)(2,1)} %assemble.3), kind=kOutput, calls=%fused_computation.276 | convolution fusion | flops 3221225472 | bytes 11534336 | tf_op jit(solution)/shard_map/dot_general | solution.py:65
  386.1 2.7 fusion.51
  390.1 3.1 add_convert_fusion.2
  401.2 4.2 collective-permute-start.44
  405.7 3.6 collective-permute-start.50
  413.0 10.7 %collective-permute-start.45 = (bf16[32,4096]{1,0:T(8,128)(2,1)}, bf16[32,4096]{1,0:T(8,128)(2,1)S(1)}, u32[]{:S(2)}, u32[]{:S(2)}) collective-permute-start(bf16[32,4096]{1,0:T(8,128)(2,1)} %get-tuple-element.222), channel_id=1, source_target_pairs={{0,2},{1,3},{2,0},{3,1},{4,6},{5,7},{6,4},{7,5},{8,10},{9,11},{10,... | collective-permute-start | bytes 786440 | tf_op jit(solution)/shard_map/ppermute | solution.py:298
  426.0 3.5 collective-permute-start.47
  434.8 2.6 add_convert_fusion.7
  443.1 6.1 %collective-permute-done.64 = bf16[1,32,1024]{2,1,0:T(8,128)(2,1)S(1)} collective-permute-done((bf16[1,32,1024]{2,1,0:T(8,128)(2,1)S(1)}, bf16[1,32,1024]{2,1,0:T(8,128)(2,1)S(1)}, u32[]{:S(2)}, u32[]{:S(2)}) %collective-permute-start.64) | collective-permute-done | bytes 65568 | tf_op jit(solution)/shard_map/ppermute | solution.py:326
  450.3 2.7 collective-permute-done.57
  455.2 2.6 collective-permute-start.59
  459.1 5.7 %collective-permute-done.58 = bf16[32,3072]{1,0:T(8,128)(2,1)S(1)} collective-permute-done((bf16[32,3072]{1,0:T(8,128)(2,1)S(1)}, bf16[32,3072]{1,0:T(8,128)(2,1)S(1)}, u32[]{:S(2)}, u32[]{:S(2)}) %collective-permute-start.58) | collective-permute-done | bytes 196640 | tf_op jit(solution)/shard_map/ppermute | solution.py:298
  465.7 3.7 collective-permute-done.59
  473.5 4.1 collective-permute-done.52
  481.0 4.0 collective-permute-done.53
  485.3 2.9 collective-permute-start.54
  493.3 2.6 collective-permute-start.56
  500.6 3.8 finish.7
  504.5 3.8 finish.6
  508.3 3.3 finish.4
  (368 shorter events, 126.2 us)
Async XLA Ops:
  5.8 12.8 %collective-permute-start = (bf16[32,3584]{1,0:T(8,128)(2,1)S(1)}, bf16[32,3584]{1,0:T(8,128)(2,1)S(1)}, u32[]{:S(2)}, u32[]{:S(2)}) collective-permute-start(bf16[32,3584]{1,0:T(8,128)(2,1)S(1)} %pad_maximum_fusion.8), channel_id=1, source_target_pairs={{0,1},{1,2},{2,3},{3,0},{4,5},{5,6},{6,7},{7,4},{8,9},{9,10},{10,1... | collective-permute-start | bytes 688136 | tf_op jit(solution)/shard_map/ppermute | solution.py:298
  8.9 17.6 %collective-permute-start.1 = (bf16[32,3584]{1,0:T(8,128)(2,1)S(1)}, bf16[32,3584]{1,0:T(8,128)(2,1)S(1)}, u32[]{:S(2)}, u32[]{:S(2)}) collective-permute-start(bf16[32,3584]{1,0:T(8,128)(2,1)S(1)} %pad_maximum_fusion.8), channel_id=1, source_target_pairs={{0,2},{1,3},{2,0},{3,1},{4,6},{5,7},{6,4},{7,5},{8,10},{9,11},{10,... | collective-permute-start | bytes 688136 | tf_op jit(solution)/shard_map/ppermute | solution.py:298
  11.5 15.0 %collective-permute-start.2 = (bf16[32,3584]{1,0:T(8,128)(2,1)S(1)}, bf16[32,3584]{1,0:T(8,128)(2,1)S(1)}, u32[]{:S(2)}, u32[]{:S(2)}) collective-permute-start(bf16[32,3584]{1,0:T(8,128)(2,1)S(1)} %pad_maximum_fusion.8), channel_id=1, source_target_pairs={{0,3},{1,0},{2,1},{3,2},{4,7},{5,4},{6,5},{7,6},{8,11},{9,8},{10,9... | collective-permute-start | bytes 688136 | tf_op jit(solution)/shard_map/ppermute | solution.py:298
  27.4 15.4 %collective-permute-start.5 = (bf16[32,5120]{1,0:T(8,128)(2,1)}, bf16[32,5120]{1,0:T(8,128)(2,1)}, u32[]{:S(2)}, u32[]{:S(2)}) collective-permute-start(bf16[32,5120]{1,0:T(8,128)(2,1)} %pad_maximum_fusion.6), channel_id=1, source_target_pairs={{0,1},{1,2},{2,3},{3,0},{4,5},{5,6},{6,7},{7,4},{8,9},{9,10},{10,1... | collective-permute-start | bytes 983048 | tf_op jit(solution)/shard_map/ppermute | solution.py:298
  32.8 22.4 %collective-permute-start.6 = (bf16[32,5120]{1,0:T(8,128)(2,1)}, bf16[32,5120]{1,0:T(8,128)(2,1)}, u32[]{:S(2)}, u32[]{:S(2)}) collective-permute-start(bf16[32,5120]{1,0:T(8,128)(2,1)} %pad_maximum_fusion.6), channel_id=1, source_target_pairs={{0,2},{1,3},{2,0},{3,1},{4,6},{5,7},{6,4},{7,5},{8,10},{9,11},{10,... | collective-permute-start | bytes 983048 | tf_op jit(solution)/shard_map/ppermute | solution.py:298
  34.4 20.8 %collective-permute-start.7 = (bf16[32,5120]{1,0:T(8,128)(2,1)}, bf16[32,5120]{1,0:T(8,128)(2,1)}, u32[]{:S(2)}, u32[]{:S(2)}) collective-permute-start(bf16[32,5120]{1,0:T(8,128)(2,1)} %pad_maximum_fusion.6), channel_id=1, source_target_pairs={{0,3},{1,0},{2,1},{3,2},{4,7},{5,4},{6,5},{7,6},{8,11},{9,8},{10,9... | collective-permute-start | bytes 983048 | tf_op jit(solution)/shard_map/ppermute | solution.py:298
  35.2 20.0 %collective-permute-start.4 = (bf16[1,3,32,3072]{3,2,1,0:T(8,128)(2,1)}, bf16[1,3,32,3072]{3,2,1,0:T(8,128)(2,1)}, u32[]{:S(2)}, u32[]{:S(2)}) collective-permute-start(bf16[1,3,32,3072]{3,2,1,0:T(8,128)(2,1)} %maximum_bitcast_fusion.2.refs_1_), channel_id=1, source_target_pairs={{0,8},{4,20},{8,0},{12,28},{16,24},{20,4},{24,16},{28,12},{1,9},{5... | collective-permute-start | bytes 1769480 | tf_op jit(solution)/shard_map/ppermute | solution.py:464
  36.7 20.5 %collective-permute-start.3 = (bf16[1,3,32,3072]{3,2,1,0:T(8,128)(2,1)}, bf16[1,3,32,3072]{3,2,1,0:T(8,128)(2,1)}, u32[]{:S(2)}, u32[]{:S(2)}) collective-permute-start(bf16[1,3,32,3072]{3,2,1,0:T(8,128)(2,1)} %maximum_bitcast_fusion.2.refs_1_), channel_id=1, source_target_pairs={{0,16},{4,12},{8,24},{12,4},{16,0},{20,28},{24,8},{28,20},{1,17},{... | collective-permute-start | bytes 1769480 | tf_op jit(solution)/shard_map/ppermute | solution.py:464
  42.9 25.8 %collective-permute-start.14 = (bf16[1,3,32,3072]{3,2,1,0:T(8,128)(2,1)}, bf16[1,3,32,3072]{3,2,1,0:T(8,128)(2,1)}, u32[]{:S(2)}, u32[]{:S(2)}) collective-permute-start(bf16[1,3,32,3072]{3,2,1,0:T(8,128)(2,1)} %maximum_bitcast_fusion.2.refs_1_), channel_id=1, source_target_pairs={{0,4},{4,0},{8,12},{12,8},{16,20},{20,16},{24,28},{28,24},{1,5},{5... | collective-permute-start | bytes 1769480 | tf_op jit(solution)/shard_map/ppermute | solution.py:294
  55.2 10.1 %collective-permute-start.8 = (bf16[1,3,32,3072]{3,2,1,0:T(8,128)(2,1)}, bf16[1,3,32,3072]{3,2,1,0:T(8,128)(2,1)S(1)}, u32[]{:S(2)}, u32[]{:S(2)}) collective-permute-start(bf16[1,3,32,3072]{3,2,1,0:T(8,128)(2,1)} %collective-permute-done.4.refs_2_), channel_id=1, source_target_pairs={{0,16},{4,12},{8,24},{12,4},{16,0},{20,28},{24,8},{28,20},{1,17},{... | collective-permute-start | bytes 1769480 | tf_op jit(solution)/shard_map/ppermute | solution.py:464
  57.1 13.1 %collective-permute-start.15 = (bf16[1,3,32,3072]{3,2,1,0:T(8,128)(2,1)}, bf16[1,3,32,3072]{3,2,1,0:T(8,128)(2,1)}, u32[]{:S(2)}, u32[]{:S(2)}) collective-permute-start(bf16[1,3,32,3072]{3,2,1,0:T(8,128)(2,1)} %collective-permute-done.4.refs_2_), channel_id=1, source_target_pairs={{0,4},{4,0},{8,12},{12,8},{16,20},{20,16},{24,28},{28,24},{1,5},{5... | collective-permute-start | bytes 1769480 | tf_op jit(solution)/shard_map/ppermute | solution.py:294
  67.1 24.4 %collective-permute-start.13 = (bf16[1,3,32,5120]{3,2,1,0:T(8,128)(2,1)S(1)}, bf16[1,3,32,5120]{3,2,1,0:T(8,128)(2,1)}, u32[]{:S(2)}, u32[]{:S(2)}) collective-permute-start(bf16[1,3,32,5120]{3,2,1,0:T(8,128)(2,1)S(1)} %maximum_bitcast_fusion.refs_2_), channel_id=1, source_target_pairs={{0,8},{4,20},{8,0},{12,28},{16,24},{20,4},{24,16},{28,12},{1,9},{5... | collective-permute-start | bytes 2949128 | tf_op jit(solution)/shard_map/ppermute | solution.py:464
  68.7 48.2 %collective-permute-start.12 = (bf16[1,3,32,5120]{3,2,1,0:T(8,128)(2,1)S(1)}, bf16[1,3,32,5120]{3,2,1,0:T(8,128)(2,1)}, u32[]{:S(2)}, u32[]{:S(2)}) collective-permute-start(bf16[1,3,32,5120]{3,2,1,0:T(8,128)(2,1)S(1)} %maximum_bitcast_fusion.refs_2_), channel_id=1, source_target_pairs={{0,16},{4,12},{8,24},{12,4},{16,0},{20,28},{24,8},{28,20},{1,17},{... | collective-permute-start | bytes 2949128 | tf_op jit(solution)/shard_map/ppermute | solution.py:464
  91.5 25.4 %collective-permute-start.18 = (bf16[1,3,32,5120]{3,2,1,0:T(8,128)(2,1)}, bf16[1,3,32,5120]{3,2,1,0:T(8,128)(2,1)}, u32[]{:S(2)}, u32[]{:S(2)}) collective-permute-start(bf16[1,3,32,5120]{3,2,1,0:T(8,128)(2,1)} %collective-permute-done.13.refs_3_), channel_id=1, source_target_pairs={{0,16},{4,12},{8,24},{12,4},{16,0},{20,28},{24,8},{28,20},{1,17},{... | collective-permute-start | bytes 2949128 | tf_op jit(solution)/shard_map/ppermute | solution.py:464
  93.5 24.0 %collective-permute-start.10 = (bf16[128,1024]{1,0:T(8,128)(2,1)S(1)}, bf16[128,1024]{1,0:T(8,128)(2,1)}, u32[]{:S(2)}, u32[]{:S(2)}) collective-permute-start(bf16[128,1024]{1,0:T(8,128)(2,1)S(1)} %constant_dynamic-slice_fusion.4), channel_id=1, source_target_pairs={{0,2},{1,3},{2,0},{3,1},{4,6},{5,7},{6,4},{7,5},{8,10},{9,11},{10,... | collective-permute-start | bytes 786440 | tf_op jit(solution)/shard_map/ppermute | solution.py:298
  100.6 40.0 %collective-permute-start.20 = (bf16[1,3,32,5120]{3,2,1,0:T(8,128)(2,1)S(1)}, bf16[1,3,32,5120]{3,2,1,0:T(8,128)(2,1)}, u32[]{:S(2)}, u32[]{:S(2)}) collective-permute-start(bf16[1,3,32,5120]{3,2,1,0:T(8,128)(2,1)S(1)} %maximum_bitcast_fusion.refs_2_), channel_id=1, source_target_pairs={{0,4},{4,0},{8,12},{12,8},{16,20},{20,16},{24,28},{28,24},{1,5},{5... | collective-permute-start | bytes 2949128 | tf_op jit(solution)/shard_map/ppermute | solution.py:294
  100.6 40.0 %collective-permute-start.21 = (bf16[1,3,32,5120]{3,2,1,0:T(8,128)(2,1)}, bf16[1,3,32,5120]{3,2,1,0:T(8,128)(2,1)}, u32[]{:S(2)}, u32[]{:S(2)}) collective-permute-start(bf16[1,3,32,5120]{3,2,1,0:T(8,128)(2,1)} %collective-permute-done.13.refs_3_), channel_id=1, source_target_pairs={{0,4},{4,0},{8,12},{12,8},{16,20},{20,16},{24,28},{28,24},{1,5},{5... | collective-permute-start | bytes 2949128 | tf_op jit(solution)/shard_map/ppermute | solution.py:294
  116.9 23.7 %collective-permute-start.22 = (bf16[1,3,32,5120]{3,2,1,0:T(8,128)(2,1)}, bf16[1,3,32,5120]{3,2,1,0:T(8,128)(2,1)}, u32[]{:S(2)}, u32[]{:S(2)}) collective-permute-start(bf16[1,3,32,5120]{3,2,1,0:T(8,128)(2,1)} %collective-permute-done.12.refs_4_), channel_id=1, source_target_pairs={{0,4},{4,0},{8,12},{12,8},{16,20},{20,16},{24,28},{28,24},{1,5},{5... | collective-permute-start | bytes 2949128 | tf_op jit(solution)/shard_map/ppermute | solution.py:294
  117.0 23.6 %collective-permute-start.23 = (bf16[1,3,32,5120]{3,2,1,0:T(8,128)(2,1)}, bf16[1,3,32,5120]{3,2,1,0:T(8,128)(2,1)}, u32[]{:S(2)}, u32[]{:S(2)}) collective-permute-start(bf16[1,3,32,5120]{3,2,1,0:T(8,128)(2,1)} %collective-permute-done.18.refs_5_), channel_id=1, source_target_pairs={{0,4},{4,0},{8,12},{12,8},{16,20},{20,16},{24,28},{28,24},{1,5},{5... | collective-permute-start | bytes 2949128 | tf_op jit(solution)/shard_map/ppermute | solution.py:294
  117.5 9.9 %collective-permute-start.11 = (bf16[128,1024]{1,0:T(8,128)(2,1)S(1)}, bf16[128,1024]{1,0:T(8,128)(2,1)S(1)}, u32[]{:S(2)}, u32[]{:S(2)}) collective-permute-start(bf16[128,1024]{1,0:T(8,128)(2,1)S(1)} %constant_dynamic-slice_fusion.4), channel_id=1, source_target_pairs={{0,3},{1,0},{2,1},{3,2},{4,7},{5,4},{6,5},{7,6},{8,11},{9,8},{10,9... | collective-permute-start | bytes 786440 | tf_op jit(solution)/shard_map/ppermute | solution.py:298
  127.4 9.6 %collective-permute-start.9 = (bf16[128,1024]{1,0:T(8,128)(2,1)S(1)}, bf16[128,1024]{1,0:T(8,128)(2,1)}, u32[]{:S(2)}, u32[]{:S(2)}) collective-permute-start(bf16[128,1024]{1,0:T(8,128)(2,1)S(1)} %constant_dynamic-slice_fusion.4), channel_id=1, source_target_pairs={{0,1},{1,2},{2,3},{3,0},{4,5},{5,6},{6,7},{7,4},{8,9},{9,10},{10,1... | collective-permute-start | bytes 786440 | tf_op jit(solution)/shard_map/ppermute | solution.py:298
  139.1 26.3 %collective-permute-start.19 = (bf16[1,3,128,1024]{3,2,1,0:T(8,128)(2,1)}, bf16[1,3,128,1024]{3,2,1,0:T(8,128)(2,1)}, u32[]{:S(2)}, u32[]{:S(2)}) collective-permute-start(bf16[1,3,128,1024]{3,2,1,0:T(8,128)(2,1)} %maximum_bitcast_fusion.1.refs_1_), channel_id=1, source_target_pairs={{0,8},{4,20},{8,0},{12,28},{16,24},{20,4},{24,16},{28,12},{1,9},{5... | collective-permute-start | bytes 2359304 | tf_op jit(solution)/shard_map/ppermute | solution.py:464
  176.9 36.2 %collective-permute-start.30 = (bf16[4,4,128,1024]{3,2,1,0:T(8,128)(2,1)}, bf16[4,4,128,1024]{3,2,1,0:T(8,128)(2,1)}, u32[]{:S(2)}, u32[]{:S(2)}) collective-permute-start(bf16[4,4,128,1024]{3,2,1,0:T(8,128)(2,1)} %bitcast.24), channel_id=1, source_target_pairs={{0,4},{4,0},{8,12},{12,8},{16,20},{20,16},{24,28},{28,24},{1,5},{5... | collective-permute-start | bytes 12582920 | tf_op jit(solution)/shard_map/ppermute | solution.py:294
  176.9 12.3 %collective-permute-start.24 = (bf16[1,3,128,1024]{3,2,1,0:T(8,128)(2,1)}, bf16[1,3,128,1024]{3,2,1,0:T(8,128)(2,1)}, u32[]{:S(2)}, u32[]{:S(2)}) collective-permute-start(bf16[1,3,128,1024]{3,2,1,0:T(8,128)(2,1)} %maximum_bitcast_fusion.1.refs_1_), channel_id=1, source_target_pairs={{0,16},{4,12},{8,24},{12,4},{16,0},{20,28},{24,8},{28,20},{1,17},{... | collective-permute-start | bytes 2359304 | tf_op jit(solution)/shard_map/ppermute | solution.py:464
  177.6 20.0 %collective-permute-start.25 = (bf16[1,3,128,1024]{3,2,1,0:T(8,128)(2,1)}, bf16[1,3,128,1024]{3,2,1,0:T(8,128)(2,1)}, u32[]{:S(2)}, u32[]{:S(2)}) collective-permute-start(bf16[1,3,128,1024]{3,2,1,0:T(8,128)(2,1)} %collective-permute-done.19.refs_2_), channel_id=1, source_target_pairs={{0,16},{4,12},{8,24},{12,4},{16,0},{20,28},{24,8},{28,20},{1,17},{... | collective-permute-start | bytes 2359304 | tf_op jit(solution)/shard_map/ppermute | solution.py:464
  178.9 26.6 %collective-permute-start.26 = (bf16[1,3,128,1024]{3,2,1,0:T(8,128)(2,1)}, bf16[1,3,128,1024]{3,2,1,0:T(8,128)(2,1)}, u32[]{:S(2)}, u32[]{:S(2)}) collective-permute-start(bf16[1,3,128,1024]{3,2,1,0:T(8,128)(2,1)} %maximum_bitcast_fusion.1.refs_1_), channel_id=1, source_target_pairs={{0,4},{4,0},{8,12},{12,8},{16,20},{20,16},{24,28},{28,24},{1,5},{5... | collective-permute-start | bytes 2359304 | tf_op jit(solution)/shard_map/ppermute | solution.py:294
  178.9 26.6 %collective-permute-start.27 = (bf16[1,3,128,1024]{3,2,1,0:T(8,128)(2,1)}, bf16[1,3,128,1024]{3,2,1,0:T(8,128)(2,1)}, u32[]{:S(2)}, u32[]{:S(2)}) collective-permute-start(bf16[1,3,128,1024]{3,2,1,0:T(8,128)(2,1)} %collective-permute-done.19.refs_2_), channel_id=1, source_target_pairs={{0,4},{4,0},{8,12},{12,8},{16,20},{20,16},{24,28},{28,24},{1,5},{5... | collective-permute-start | bytes 2359304 | tf_op jit(solution)/shard_map/ppermute | solution.py:294
  197.6 7.9 %collective-permute-start.28 = (bf16[1,3,128,1024]{3,2,1,0:T(8,128)(2,1)}, bf16[1,3,128,1024]{3,2,1,0:T(8,128)(2,1)}, u32[]{:S(2)}, u32[]{:S(2)}) collective-permute-start(bf16[1,3,128,1024]{3,2,1,0:T(8,128)(2,1)} %collective-permute-done.24.refs_3_), channel_id=1, source_target_pairs={{0,4},{4,0},{8,12},{12,8},{16,20},{20,16},{24,28},{28,24},{1,5},{5... | collective-permute-start | bytes 2359304 | tf_op jit(solution)/shard_map/ppermute | solution.py:294
  197.6 7.9 %collective-permute-start.29 = (bf16[1,3,128,1024]{3,2,1,0:T(8,128)(2,1)}, bf16[1,3,128,1024]{3,2,1,0:T(8,128)(2,1)}, u32[]{:S(2)}, u32[]{:S(2)}) collective-permute-start(bf16[1,3,128,1024]{3,2,1,0:T(8,128)(2,1)} %collective-permute-done.25.refs_4_), channel_id=1, source_target_pairs={{0,4},{4,0},{8,12},{12,8},{16,20},{20,16},{24,28},{28,24},{1,5},{5... | collective-permute-start | bytes 2359304 | tf_op jit(solution)/shard_map/ppermute | solution.py:294
  235.8 28.8 %collective-permute-start.31 = (bf16[4,4,32,4096]{3,2,1,0:T(8,128)(2,1)}, bf16[4,4,32,4096]{3,2,1,0:T(8,128)(2,1)}, u32[]{:S(2)}, u32[]{:S(2)}) collective-permute-start(bf16[4,4,32,4096]{3,2,1,0:T(8,128)(2,1)} %bitcast.26), channel_id=1, source_target_pairs={{0,4},{4,0},{8,12},{12,8},{16,20},{20,16},{24,28},{28,24},{1,5},{5... | collective-permute-start | bytes 12582920 | tf_op jit(solution)/shard_map/ppermute | solution.py:294
  238.5 26.1 %collective-permute-start.32 = (bf16[2,4,128,1024]{3,2,1,0:T(8,128)(2,1)S(1)}, bf16[2,4,128,1024]{3,2,1,0:T(8,128)(2,1)S(1)}, u32[]{:S(2)}, u32[]{:S(2)}) collective-permute-start(bf16[2,4,128,1024]{3,2,1,0:T(8,128)(2,1)S(1)} %copy-done.25), channel_id=1, source_target_pairs={{0,8},{4,20},{8,0},{12,28},{16,24},{20,4},{24,16},{28,12},{1,9},{5... | collective-permute-start | bytes 6291464 | tf_op jit(solution)/shard_map/ppermute | solution.py:317
  275.5 10.0 %collective-permute-start.33 = (bf16[4,4,32,1024]{3,2,1,0:T(8,128)(2,1)S(1)}, bf16[4,4,32,1024]{3,2,1,0:T(8,128)(2,1)S(1)}, u32[]{:S(2)}, u32[]{:S(2)}) collective-permute-start(bf16[4,4,32,1024]{3,2,1,0:T(8,128)(2,1)S(1)} %bitcast.232), channel_id=1, source_target_pairs={{0,4},{4,0},{8,12},{12,8},{16,20},{20,16},{24,28},{28,24},{1,5},{5... | collective-permute-start | bytes 3145736 | tf_op jit(solution)/shard_map/ppermute | solution.py:294
  275.5 43.2 %collective-permute-start.35 = (bf16[2,4,32,4096]{3,2,1,0:T(8,128)(2,1)}, bf16[2,4,32,4096]{3,2,1,0:T(8,128)(2,1)}, u32[]{:S(2)}, u32[]{:S(2)}) collective-permute-start(bf16[2,4,32,4096]{3,2,1,0:T(8,128)(2,1)} %add_convert_fusion), channel_id=1, source_target_pairs={{0,8},{4,20},{8,0},{12,28},{16,24},{20,4},{24,16},{28,12},{1,9},{5... | collective-permute-start | bytes 6291464 | tf_op jit(solution)/shard_map/ppermute | solution.py:317
  282.0 26.4 %collective-permute-start.34 = (bf16[1,4,128,1024]{3,2,1,0:T(8,128)(2,1)}, bf16[1,4,128,1024]{3,2,1,0:T(8,128)(2,1)}, u32[]{:S(2)}, u32[]{:S(2)}) collective-permute-start(bf16[1,4,128,1024]{3,2,1,0:T(8,128)(2,1)} %add_convert_fusion.4), channel_id=1, source_target_pairs={{0,16},{4,12},{8,24},{12,4},{16,0},{20,28},{24,8},{28,20},{1,17},{... | collective-permute-start | bytes 3145736 | tf_op jit(solution)/shard_map/ppermute | solution.py:317
  286.6 32.1 %collective-permute-start.36 = (bf16[2,4,32,1024]{3,2,1,0:T(8,128)(2,1)}, bf16[2,4,32,1024]{3,2,1,0:T(8,128)(2,1)S(1)}, u32[]{:S(2)}, u32[]{:S(2)}) collective-permute-start(bf16[2,4,32,1024]{3,2,1,0:T(8,128)(2,1)} %add_convert_fusion.8), channel_id=1, source_target_pairs={{0,8},{4,20},{8,0},{12,28},{16,24},{20,4},{24,16},{28,12},{1,9},{5... | collective-permute-start | bytes 1572872 | tf_op jit(solution)/shard_map/ppermute | solution.py:317
  354.8 34.0 %collective-permute-start.37 = (bf16[4,4,32,3072]{3,2,1,0:T(8,128)(2,1)}, bf16[4,4,32,3072]{3,2,1,0:T(8,128)(2,1)}, u32[]{:S(2)}, u32[]{:S(2)}) collective-permute-start(bf16[4,4,32,3072]{3,2,1,0:T(8,128)(2,1)} %bitcast.41), channel_id=1, source_target_pairs={{0,4},{4,0},{8,12},{12,8},{16,20},{20,16},{24,28},{28,24},{1,5},{5... | collective-permute-start | bytes 9437192 | tf_op jit(solution)/shard_map/ppermute | solution.py:294
  371.0 24.2 %collective-permute-start.41 = (bf16[1,4,32,4096]{3,2,1,0:T(8,128)(2,1)}, bf16[1,4,32,4096]{3,2,1,0:T(8,128)(2,1)S(1)}, u32[]{:S(2)}, u32[]{:S(2)}) collective-permute-start(bf16[1,4,32,4096]{3,2,1,0:T(8,128)(2,1)} %add_convert_fusion.3), channel_id=1, source_target_pairs={{0,16},{4,12},{8,24},{12,4},{16,0},{20,28},{24,8},{28,20},{1,17},{... | collective-permute-start | bytes 3145736 | tf_op jit(solution)/shard_map/ppermute | solution.py:317
  371.8 21.4 %collective-permute-start.38 = (bf16[128,1024]{1,0:T(8,128)(2,1)}, bf16[128,1024]{1,0:T(8,128)(2,1)S(1)}, u32[]{:S(2)}, u32[]{:S(2)}) collective-permute-start(bf16[128,1024]{1,0:T(8,128)(2,1)} %get-tuple-element.206), channel_id=1, source_target_pairs={{0,1},{1,2},{2,3},{3,0},{4,5},{5,6},{6,7},{7,4},{8,9},{9,10},{10,1... | collective-permute-start | bytes 786440 | tf_op jit(solution)/shard_map/ppermute | solution.py:298
  371.8 21.6 %collective-permute-start.39 = (bf16[128,1024]{1,0:T(8,128)(2,1)}, bf16[128,1024]{1,0:T(8,128)(2,1)S(1)}, u32[]{:S(2)}, u32[]{:S(2)}) collective-permute-start(bf16[128,1024]{1,0:T(8,128)(2,1)} %get-tuple-element.207), channel_id=1, source_target_pairs={{0,2},{1,3},{2,0},{3,1},{4,6},{5,7},{6,4},{7,5},{8,10},{9,11},{10,... | collective-permute-start | bytes 786440 | tf_op jit(solution)/shard_map/ppermute | solution.py:298
  373.8 19.5 %collective-permute-start.40 = (bf16[128,1024]{1,0:T(8,128)(2,1)}, bf16[128,1024]{1,0:T(8,128)(2,1)S(1)}, u32[]{:S(2)}, u32[]{:S(2)}) collective-permute-start(bf16[128,1024]{1,0:T(8,128)(2,1)} %get-tuple-element.208), channel_id=1, source_target_pairs={{0,3},{1,0},{2,1},{3,2},{4,7},{5,4},{6,5},{7,6},{8,11},{9,8},{10,9... | collective-permute-start | bytes 786440 | tf_op jit(solution)/shard_map/ppermute | solution.py:298
  399.6 34.3 %collective-permute-start.43 = (bf16[2,4,32,3072]{3,2,1,0:T(8,128)(2,1)}, bf16[2,4,32,3072]{3,2,1,0:T(8,128)(2,1)}, u32[]{:S(2)}, u32[]{:S(2)}) collective-permute-start(bf16[2,4,32,3072]{3,2,1,0:T(8,128)(2,1)} %add_convert_fusion.2), channel_id=1, source_target_pairs={{0,8},{4,20},{8,0},{12,28},{16,24},{20,4},{24,16},{28,12},{1,9},{5... | collective-permute-start | bytes 4718600 | tf_op jit(solution)/shard_map/ppermute | solution.py:317
  401.2 29.7 %collective-permute-start.44 = (bf16[32,4096]{1,0:T(8,128)(2,1)}, bf16[32,4096]{1,0:T(8,128)(2,1)}, u32[]{:S(2)}, u32[]{:S(2)}) collective-permute-start(bf16[32,4096]{1,0:T(8,128)(2,1)} %get-tuple-element.221), channel_id=1, source_target_pairs={{0,1},{1,2},{2,3},{3,0},{4,5},{5,6},{6,7},{7,4},{8,9},{9,10},{10,1... | collective-permute-start | bytes 786440 | tf_op jit(solution)/shard_map/ppermute | solution.py:298
  405.5 18.2 %collective-permute-start.49 = (bf16[32,1024]{1,0:T(8,128)(2,1)S(1)}, bf16[32,1024]{1,0:T(8,128)(2,1)S(1)}, u32[]{:S(2)}, u32[]{:S(2)}) collective-permute-start(bf16[32,1024]{1,0:T(8,128)(2,1)S(1)} %get-tuple-element.226), channel_id=1, source_target_pairs={{0,2},{1,3},{2,0},{3,1},{4,6},{5,7},{6,4},{7,5},{8,10},{9,11},{10,... | collective-permute-start | bytes 196616 | tf_op jit(solution)/shard_map/ppermute | solution.py:298
  405.7 20.4 %collective-permute-start.50 = (bf16[32,1024]{1,0:T(8,128)(2,1)S(1)}, bf16[32,1024]{1,0:T(8,128)(2,1)S(1)}, u32[]{:S(2)}, u32[]{:S(2)}) collective-permute-start(bf16[32,1024]{1,0:T(8,128)(2,1)S(1)} %get-tuple-element.227), channel_id=1, source_target_pairs={{0,3},{1,0},{2,1},{3,2},{4,7},{5,4},{6,5},{7,6},{8,11},{9,8},{10,9... | collective-permute-start | bytes 196616 | tf_op jit(solution)/shard_map/ppermute | solution.py:298
  413.0 18.2 %collective-permute-start.45 = (bf16[32,4096]{1,0:T(8,128)(2,1)}, bf16[32,4096]{1,0:T(8,128)(2,1)S(1)}, u32[]{:S(2)}, u32[]{:S(2)}) collective-permute-start(bf16[32,4096]{1,0:T(8,128)(2,1)} %get-tuple-element.222), channel_id=1, source_target_pairs={{0,2},{1,3},{2,0},{3,1},{4,6},{5,7},{6,4},{7,5},{8,10},{9,11},{10,... | collective-permute-start | bytes 786440 | tf_op jit(solution)/shard_map/ppermute | solution.py:298
  423.7 9.0 %collective-permute-start.46 = (bf16[32,4096]{1,0:T(8,128)(2,1)}, bf16[32,4096]{1,0:T(8,128)(2,1)S(1)}, u32[]{:S(2)}, u32[]{:S(2)}) collective-permute-start(bf16[32,4096]{1,0:T(8,128)(2,1)} %get-tuple-element.223), channel_id=1, source_target_pairs={{0,3},{1,0},{2,1},{3,2},{4,7},{5,4},{6,5},{7,6},{8,11},{9,8},{10,9... | collective-permute-start | bytes 786440 | tf_op jit(solution)/shard_map/ppermute | solution.py:298
  426.0 7.9 %collective-permute-start.47 = (bf16[1,128,1024]{2,1,0:T(8,128)(2,1)S(1)}, bf16[1,128,1024]{2,1,0:T(8,128)(2,1)S(1)}, u32[]{:S(2)}, u32[]{:S(2)}) collective-permute-start(bf16[1,128,1024]{2,1,0:T(8,128)(2,1)S(1)} %fusion.40), channel_id=1, source_target_pairs={{0,8},{4,20},{8,0},{12,28},{16,24},{20,4},{24,16},{28,12},{1,9},{5... | collective-permute-start | bytes 786440 | tf_op jit(solution)/shard_map/ppermute | solution.py:326
  438.6 11.7 %collective-permute-start.67 = (bf16[1,32,4096]{2,1,0:T(8,128)(2,1)S(1)}, bf16[1,32,4096]{2,1,0:T(8,128)(2,1)S(1)}, u32[]{:S(2)}, u32[]{:S(2)}) collective-permute-start(bf16[1,32,4096]{2,1,0:T(8,128)(2,1)S(1)} %fusion.41), channel_id=1, source_target_pairs={{0,8},{4,20},{8,0},{12,28},{16,24},{20,4},{24,16},{28,12},{1,9},{5... | collective-permute-start | bytes 786440 | tf_op jit(solution)/shard_map/ppermute | solution.py:326
  440.7 12.3 %collective-permute-start.57 = (bf16[1,4,32,3072]{3,2,1,0:T(8,128)(2,1)}, bf16[1,4,32,3072]{3,2,1,0:T(8,128)(2,1)}, u32[]{:S(2)}, u32[]{:S(2)}) collective-permute-start(bf16[1,4,32,3072]{3,2,1,0:T(8,128)(2,1)} %add_convert_fusion.7), channel_id=1, source_target_pairs={{0,16},{4,12},{8,24},{12,4},{16,0},{20,28},{24,8},{28,20},{1,17},{... | collective-permute-start | bytes 2359304 | tf_op jit(solution)/shard_map/ppermute | solution.py:317
  441.7 30.2 %collective-permute-start.70 = (bf16[2,128,1024]{2,1,0:T(8,128)(2,1)}, bf16[2,128,1024]{2,1,0:T(8,128)(2,1)}, u32[]{:S(2)}, u32[]{:S(2)}) collective-permute-start(bf16[2,128,1024]{2,1,0:T(8,128)(2,1)} %pad_maximum_fusion.3), channel_id=1, source_target_pairs={{0,16},{4,12},{8,24},{12,4},{16,0},{20,28},{24,8},{28,20},{1,17},{... | collective-permute-start | bytes 1572872 | tf_op jit(solution)/shard_map/ppermute | solution.py:326
  443.0 14.7 %collective-permute-start.51 = (f32[4,64,256]{2,0,1:T(4,128)S(1)}, f32[4,64,256]{2,0,1:T(4,128)S(1)}, u32[]{:S(2)}, u32[]{:S(2)}) collective-permute-start(f32[4,64,256]{2,0,1:T(4,128)S(1)} %select_maximum_fusion), channel_id=1, source_target_pairs={{0,4},{4,0},{8,12},{12,8},{16,20},{20,16},{24,28},{28,24},{1,5},{5... | collective-permute-start | bytes 786440 | tf_op jit(solution)/shard_map/ppermute | solution.py:337
  449.3 22.4 %collective-permute-start.65 = (bf16[2,32,1024]{2,1,0:T(8,128)(2,1)S(1)}, bf16[2,32,1024]{2,1,0:T(8,128)(2,1)S(1)}, u32[]{:S(2)}, u32[]{:S(2)}) collective-permute-start(bf16[2,32,1024]{2,1,0:T(8,128)(2,1)S(1)} %pad_maximum_fusion.9), channel_id=1, source_target_pairs={{0,16},{4,12},{8,24},{12,4},{16,0},{20,28},{24,8},{28,20},{1,17},{... | collective-permute-start | bytes 393224 | tf_op jit(solution)/shard_map/ppermute | solution.py:326
  455.1 9.7 %collective-permute-start.58 = (bf16[32,3072]{1,0:T(8,128)(2,1)S(1)}, bf16[32,3072]{1,0:T(8,128)(2,1)S(1)}, u32[]{:S(2)}, u32[]{:S(2)}) collective-permute-start(bf16[32,3072]{1,0:T(8,128)(2,1)S(1)} %get-tuple-element.270), channel_id=1, source_target_pairs={{0,1},{1,2},{2,3},{3,0},{4,5},{5,6},{6,7},{7,4},{8,9},{9,10},{10,1... | collective-permute-start | bytes 589832 | tf_op jit(solution)/shard_map/ppermute | solution.py:298
  455.2 14.3 %collective-permute-start.59 = (bf16[32,3072]{1,0:T(8,128)(2,1)S(1)}, bf16[32,3072]{1,0:T(8,128)(2,1)S(1)}, u32[]{:S(2)}, u32[]{:S(2)}) collective-permute-start(bf16[32,3072]{1,0:T(8,128)(2,1)S(1)} %get-tuple-element.272), channel_id=1, source_target_pairs={{0,2},{1,3},{2,0},{3,1},{4,6},{5,7},{6,4},{7,5},{8,10},{9,11},{10,... | collective-permute-start | bytes 589832 | tf_op jit(solution)/shard_map/ppermute | solution.py:298
  457.7 13.4 %collective-permute-start.60 = (bf16[32,3072]{1,0:T(8,128)(2,1)S(1)}, bf16[32,3072]{1,0:T(8,128)(2,1)S(1)}, u32[]{:S(2)}, u32[]{:S(2)}) collective-permute-start(bf16[32,3072]{1,0:T(8,128)(2,1)S(1)} %get-tuple-element.271), channel_id=1, source_target_pairs={{0,3},{1,0},{2,1},{3,2},{4,7},{5,4},{6,5},{7,6},{8,11},{9,8},{10,9... | collective-permute-start | bytes 589832 | tf_op jit(solution)/shard_map/ppermute | solution.py:298
  464.8 16.0 %collective-permute-start.68 = (bf16[2,32,4096]{2,1,0:T(8,128)(2,1)S(1)}, bf16[2,32,4096]{2,1,0:T(8,128)(2,1)S(1)}, u32[]{:S(2)}, u32[]{:S(2)}) collective-permute-start(bf16[2,32,4096]{2,1,0:T(8,128)(2,1)S(1)} %pad_maximum_fusion.4), channel_id=1, source_target_pairs={{0,16},{4,12},{8,24},{12,4},{16,0},{20,28},{24,8},{28,20},{1,17},{... | collective-permute-start | bytes 1572872 | tf_op jit(solution)/shard_map/ppermute | solution.py:326
  469.5 8.1 %collective-permute-start.52 = (f32[4,64,256]{2,0,1:T(4,128)S(1)}, f32[4,64,256]{2,0,1:T(4,128)S(1)}, u32[]{:S(2)}, u32[]{:S(2)}) collective-permute-start(f32[4,64,256]{2,0,1:T(4,128)S(1)} %fusion.80), channel_id=1, source_target_pairs={{0,8},{4,12},{8,0},{12,4},{16,24},{20,28},{24,16},{28,20},{1,9},{5... | collective-permute-start | bytes 786440 | tf_op jit(solution)/shard_map/ppermute | solution.py:337
  471.2 8.5 %collective-permute-start.61 = (bf16[1,32,3072]{2,1,0:T(8,128)(2,1)S(1)}, bf16[1,32,3072]{2,1,0:T(8,128)(2,1)S(1)}, u32[]{:S(2)}, u32[]{:S(2)}) collective-permute-start(bf16[1,32,3072]{2,1,0:T(8,128)(2,1)S(1)} %fusion.50), channel_id=1, source_target_pairs={{0,8},{4,20},{8,0},{12,28},{16,24},{20,4},{24,16},{28,12},{1,9},{5... | collective-permute-start | bytes 589832 | tf_op jit(solution)/shard_map/ppermute | solution.py:326
  471.7 17.7 %collective-permute-start.66 = (bf16[4,32,1024]{2,1,0:T(8,128)(2,1)S(1)}, bf16[4,32,1024]{2,1,0:T(8,128)(2,1)S(1)}, u32[]{:S(2)}, u32[]{:S(2)}) collective-permute-start(bf16[4,32,1024]{2,1,0:T(8,128)(2,1)S(1)} %pad_maximum_fusion.7.refs_0_), channel_id=1, source_target_pairs={{0,4},{4,0},{8,12},{12,8},{16,20},{20,16},{24,28},{28,24},{1,5},{5... | collective-permute-start | bytes 786440 | tf_op jit(solution)/shard_map/ppermute | solution.py:294
  473.0 27.6 %collective-permute-start.71 = (bf16[4,128,1024]{2,1,0:T(8,128)(2,1)S(1)}, bf16[4,128,1024]{2,1,0:T(8,128)(2,1)}, u32[]{:S(2)}, u32[]{:S(2)}) collective-permute-start(bf16[4,128,1024]{2,1,0:T(8,128)(2,1)S(1)} %pad_maximum_fusion.1.refs_0_), channel_id=1, source_target_pairs={{0,4},{4,0},{8,12},{12,8},{16,20},{20,16},{24,28},{28,24},{1,5},{5... | collective-permute-start | bytes 3145736 | tf_op jit(solution)/shard_map/ppermute | solution.py:294
  479.7 9.5 %collective-permute-start.62 = (bf16[2,32,3072]{2,1,0:T(8,128)(2,1)S(1)}, bf16[2,32,3072]{2,1,0:T(8,128)(2,1)S(1)}, u32[]{:S(2)}, u32[]{:S(2)}) collective-permute-start(bf16[2,32,3072]{2,1,0:T(8,128)(2,1)S(1)} %pad_maximum_fusion.5), channel_id=1, source_target_pairs={{0,16},{4,12},{8,24},{12,4},{16,0},{20,28},{24,8},{28,20},{1,17},{... | collective-permute-start | bytes 1179656 | tf_op jit(solution)/shard_map/ppermute | solution.py:326
  480.9 23.6 %collective-permute-start.69 = (bf16[4,32,4096]{2,1,0:T(8,128)(2,1)S(1)}, bf16[4,32,4096]{2,1,0:T(8,128)(2,1)}, u32[]{:S(2)}, u32[]{:S(2)}) collective-permute-start(bf16[4,32,4096]{2,1,0:T(8,128)(2,1)S(1)} %pad_maximum_fusion.refs_0_), channel_id=1, source_target_pairs={{0,4},{4,0},{8,12},{12,8},{16,20},{20,16},{24,28},{28,24},{1,5},{5... | collective-permute-start | bytes 3145736 | tf_op jit(solution)/shard_map/ppermute | solution.py:294
  485.3 7.9 %collective-permute-start.54 = (f32[64,256]{1,0:T(8,128)S(1)}, f32[64,256]{1,0:T(8,128)S(1)}, u32[]{:S(2)}, u32[]{:S(2)}) collective-permute-start(f32[64,256]{1,0:T(8,128)S(1)} %bitcast.211), channel_id=1, source_target_pairs={{0,1},{1,2},{2,3},{3,0},{4,5},{5,6},{6,7},{7,4},{8,9},{9,10},{10,1... | collective-permute-start | bytes 196616 | tf_op jit(solution)/shard_map/ppermute | solution.py:298
  489.3 19.0 %collective-permute-start.63 = (bf16[4,32,3072]{2,1,0:T(8,128)(2,1)S(1)}, bf16[4,32,3072]{2,1,0:T(8,128)(2,1)}, u32[]{:S(2)}, u32[]{:S(2)}) collective-permute-start(bf16[4,32,3072]{2,1,0:T(8,128)(2,1)S(1)} %pad_maximum_fusion.2.refs_0_), channel_id=1, source_target_pairs={{0,4},{4,0},{8,12},{12,8},{16,20},{20,16},{24,28},{28,24},{1,5},{5... | collective-permute-start | bytes 2359304 | tf_op jit(solution)/shard_map/ppermute | solution.py:294
  (68 other events, 1995.4 us)

commit v6 on v5

--- a/solution.py
+++ b/solution.py
@@ -137,7 +137,7 @@
     ]
 
 
-def attend(projected, segment):
+def attend(projected, segment, start, count):
     rows = projected.shape[0]
     pairs = HEADS // 2
     windows = key_windows(rows)
@@ -147,10 +147,10 @@
 
     return pl.pallas_call(
         body,
-        grid=(pairs,),
-        in_specs=pair_specs(rows, pairs),
+        grid=(count,),
+        in_specs=pair_specs(rows, pairs, start),
         out_specs=pl.BlockSpec((rows, 2 * HDIM), lambda i: (0, i)),
-        out_shape=jax.ShapeDtypeStruct((rows, HEADS * HDIM), jnp.bfloat16),
+        out_shape=jax.ShapeDtypeStruct((rows, 2 * HDIM * count), jnp.bfloat16),
         name="attend",
     )(segment[:, None], segment[None, :], projected, projected, projected)
 
@@ -298,6 +298,13 @@
     return lax.ppermute(block, "fsdp", [(i, (i + step) % n_line) for i in range(n_line)])
 
 
+def plane_hops(block, n_dp):
+    across = (1 << n_dp.bit_length() - 1) - 2
+    both = [(i, i ^ across) for i in range(n_dp)]
+    hops = [hop_pairs(n_dp, stage) for stage in range(n_dp.bit_length() - 2)] + [both]
+    return [lax.ppermute(block, "dp", pairs) for pairs in hops]
+
+
 def add_up(terms):
     total = terms[0].astype(jnp.float32)
     for term in terms[1:]:
@@ -320,12 +327,9 @@
     total = add_up([grad(0, 1)[0]] + [term[0] for term in terms]).astype(jnp.bfloat16)
     sends = yield [total[step] for step in range(n_line)]
     arrived = yield [ahead(sends[step], n_line, step) for step in range(1, n_line)]
-    parts = [add_up([sends[0]] + arrived).astype(jnp.bfloat16)[None]]
-    for stage in range(n_dp.bit_length() - 2):
-        (send,) = yield [jnp.concatenate(parts) if len(parts) > 1 else parts[0]]
-        (got,) = yield [lax.ppermute(send, "dp", hop_pairs(n_dp, stage))]
-        parts = parts + [got]
-    (send,) = yield [jnp.concatenate(parts)]
+    (near,) = yield [add_up([sends[0]] + arrived).astype(jnp.bfloat16)[None]]
+    got = yield plane_hops(near, n_dp)
+    (send,) = yield [jnp.concatenate([near] + got)]
     (got,) = yield [swap_core(send, n_dp)]
     return [send, got]
 
@@ -435,7 +439,7 @@
     def pass_one(self, gate):
         return gate
 
-    pass_two = pass_three = pass_four = pass_one
+    pass_two = pass_three = pass_one
 
     def rows(self, block):
         return block
@@ -463,12 +467,31 @@
     def hop(self, block, stage):
         return lax.ppermute(block, "dp", hop_pairs(self.n_dp, stage))
 
-    def fan(self, gate, columns):
+    def settle(self, gate):
+        self.line, gate = lax.optimization_barrier((self.line, gate))
+        return gate
+
+    def near(self, gate, columns):
         self.line, gate = lax.optimization_barrier((self.line, gate))
         near = jnp.stack([item[:, :columns] for item in self.line])[None]
         near, gate = lax.optimization_barrier((near, gate))
+        self.cores = [swap_core(near, self.n_dp)]
+        return (near, gate)
+
+    def fan(self, gate, columns):
+        near, gate = self.near(gate, columns)
         self.parts = [near, self.hop(near, 0), self.hop(near, 1)]
-        self.cores = [swap_core(near, self.n_dp)]
+        return gate
+
+    def fan_wide(self, gate, columns):
+        near, gate = self.near(gate, columns)
+        self.parts = [near] + plane_hops(near, self.n_dp)
+        return gate
+
+    def close_wide(self, gate):
+        late, gate = lax.optimization_barrier((self.parts[1:], gate))
+        self.cores += [swap_core(item, self.n_dp) for item in late]
+        self.parts = self.parts[:1] + late
         return gate
 
     def forward(self, gate):
@@ -529,7 +552,7 @@
         two = Gather(unit_two, n_dp, n_line)
         two.line = one.forward(two.line)
         two.line = one.close(two.line)
-        table, unit_three = two.fan((self.got_table, unit_three), unit_two.shape[1])
+        table, unit_three = two.fan_wide((self.got_table, unit_three), unit_two.shape[1])
         three = Gather(unit_three, n_dp, n_line)
         (full_qkv,) = assemble([w_qkv], one.parts + one.cores, table, n_line, size)
         self.one = full_qkv
@@ -542,16 +565,13 @@
         return self.one
 
     def pass_one(self, gate):
-        return self.two[1].forward(gate)
+        return self.three[1].settle(gate)
 
     def pass_two(self, gate):
-        return self.three[1].fan(self.two[1].close(gate), self.three[2][1])
+        return self.three[1].fan_wide(self.two[1].close_wide(gate), self.three[2][1])
 
     def pass_three(self, gate):
-        return self.three[1].forward(gate)
-
-    def pass_four(self, gate):
-        return self.three[1].close(gate)
+        return self.three[1].close_wide(gate)
 
     def second(self):
         owns, got = self.two
@@ -640,8 +660,11 @@
     hidden_in = patches.astype(f32) + jnp.dot(place, full_table, precision=highest)
     normed_one = layer_norm(hidden_in, gain_one, bias_one).astype(bf16)
     projected = jnp.dot(normed_one, full_qkv, preferred_element_type=f32).astype(bf16)
-    projected = plan.pass_one(projected)
-    attn_rows = plan.pass_two(attend(projected, segment))
+    half = HEADS // 4
+    rows_a = attend(projected, segment, 0, half)
+    rows_a, projected = plan.pass_one((rows_a, projected))
+    rows_b = attend(projected, segment, half, half)
+    attn_rows = plan.pass_two(jnp.concatenate([rows_a, rows_b], axis=1))
     full_out, full_fc1 = plan.second()
     hidden_mid = hidden_in + jnp.dot(attn_rows, full_out, preferred_element_type=f32)
     normed_two = layer_norm(hidden_mid, gain_two, bias_two).astype(bf16)
@@ -650,46 +673,45 @@
     bell = jnp.exp(-0.5 * pre_act * pre_act) * (0.5 / jnp.pi) ** 0.5
     activated = (pre_act * share).astype(bf16)
     slope = (share + pre_act * bell).astype(bf16)
-    activated, slope = plan.pass_three((activated, slope))
     grad_out = jnp.where(valid[:, None], cotangent, jnp.zeros_like(cotangent))
     run_fc2 = plan.total(plan.wide_columns(activated), grad_out)
     activated, slope = tick((activated, slope), [run_fc2])
-    activated, slope = plan.pass_four((activated, slope))
+    activated, slope = plan.pass_three((activated, slope))
     full_fc2 = tick(plan.third(), [run_fc2])
-    branch_out = jnp.dot(activated, full_fc2, preferred_element_type=f32)
-    block_out = jnp.where(valid[:, None], hidden_mid + branch_out, 0.0).astype(bf16)
 
     grad_pre = (times_t(grad_out, full_fc2) * slope.astype(f32)).astype(bf16)
     grad_fc1_bias = jnp.sum(grad_pre.astype(f32), axis=0)
     run_fc1 = plan.total(plan.rows(normed_two), grad_pre)
     grad_pre = tick(grad_pre, [run_fc1])
     grad_norm_two = times_t(grad_pre, full_fc1)
-    grad_norm_two = tick(grad_norm_two, [run_fc1, run_fc2])
     _, pull_two = jax.vjp(layer_norm, hidden_mid, gain_two, bias_two)
     back_mid, grad_gain_two, grad_bias_two = pull_two(grad_norm_two)
     grad_mid = grad_out.astype(f32) + back_mid
-    grad_branch = grad_mid.astype(bf16)
+    grad_branch = tick(grad_mid.astype(bf16), [run_fc1])
     run_out = plan.total(plan.rows(attn_rows), grad_branch)
-    grad_branch = tick(grad_branch, [run_out])
     grad_attn = times_t(grad_branch, full_out).astype(bf16)
-    grad_attn = tick(grad_attn, [run_out])
-    half = HEADS // 4
-    back_a = attend_back(projected, grad_attn, segment, 0, half)
-    back_a, grad_attn = tick((back_a, grad_attn), [run_fc2, run_fc1, run_out])
-    back_b = attend_back(projected, grad_attn, segment, half, half)
-    side = back_a.shape[1] // 3
+    grad_attn = tick(grad_attn, [run_out, run_fc2])
+    fourth = HEADS // 8
+    backs = []
+    for group in ([run_out], [run_fc2], [run_fc1, run_out], [run_fc2, run_out]):
+        back = attend_back(projected, grad_attn, segment, len(backs) * fourth, fourth)
+        back, grad_attn = tick((back, grad_attn), group)
+        backs.append(back)
+    side = backs[0].shape[1] // 3
     grad_proj = jnp.concatenate(
-        [part[:, i * side : (i + 1) * side] for i in range(3) for part in (back_a, back_b)], axis=1
+        [part[:, i * side : (i + 1) * side] for i in range(3) for part in backs], axis=1
     )
     run_qkv = plan.total(plan.rows(normed_one), grad_proj)
     grad_proj = tick(grad_proj, [run_qkv])
     grad_norm_one = tick(times_t(grad_proj, full_qkv), [run_qkv])
-    grad_norm_one = tick(grad_norm_one, [run_fc2, run_fc1, run_out])
+    grad_norm_one, activated = tick((grad_norm_one, activated), [run_fc1, run_fc2])
     _, pull_one = jax.vjp(layer_norm, hidden_in, gain_one, bias_one)
     back_in, grad_gain_one, grad_bias_one = pull_one(grad_norm_one)
     grad_in = grad_mid + back_in
     grad_table = jnp.dot(place.T, grad_in, precision=highest)
-    grad_table, block_out = tick((grad_table, block_out), [run_qkv, run_fc1, run_fc2, run_out])
+    branch_out = jnp.dot(activated, full_fc2, preferred_element_type=f32)
+    block_out = jnp.where(valid[:, None], hidden_mid + branch_out, 0.0).astype(bf16)
+    grad_table, block_out = tick((grad_table, block_out), [run_qkv, run_fc1])
 
     def split(block):
         return block.reshape(-1, n_line, shard).transpose(1, 0, 2)

time: 520 us -> 516 us (level)
  starting transfers between devices: 99.1 us -> 87.4 us
  Pallas kernels: 94.8 us -> 101 us
  local copies, waits for them, and re-layouts: 23.7 us -> 29.1 us
    ppermute x0 -> x18, waiting for transfers between devices: none -> 59.6 us  [plane_hops(): return [lax.ppermute(block, 'dp', pairs) for pairs in hops]]
    ppermute x9 -> x3, waiting for transfers between devices: 33.5 us -> 9.14 us  [hop(): return lax.ppermute(block, 'dp', hop_pairs(self.n_dp, stage))]
    ppermute x0 -> x18, starting transfers between devices: none -> 20.2 us  [plane_hops(): return [lax.ppermute(block, 'dp', pairs) for pairs in hops]]
    ppermute x16 -> x8, waiting for transfers between devices: 39.5 us -> 20.2 us  [reduce_steps(): got, = (yield [lax.ppermute(send, 'dp', hop_pairs(n_dp, stage))])]
    ppermute x24, starting transfers between devices: 63 us -> 51.2 us  [ahead(): lax.ppermute(block, 'fsdp', [(i, (i + step) % n_line) for i in range(n_li...]
    ppermute x16 -> x8, starting transfers between devices: 17.4 us -> 6.77 us  [reduce_steps(): got, = (yield [lax.ppermute(send, 'dp', hop_pairs(n_dp, stage))])]
    ppermute x24, waiting for transfers between devices: 49.5 us -> 39.7 us  [ahead(): lax.ppermute(block, 'fsdp', [(i, (i + step) % n_line) for i in range(n_li...]
    ppermute x9 -> x3, starting transfers between devices: 12.4 us -> 3.52 us  [hop(): return lax.ppermute(block, 'dp', hop_pairs(self.n_dp, stage))]
  transfers between devices with their start and end apart: 72 -> 76, of which waited for: 28 -> 23; matrix products, arithmetic and copies ran while one was open for 22% -> 23% of each run, Pallas kernels for 13% -> 16%
where the time goes in v6:
time: 516 us; the launch traced here: 510 us
  waiting for transfers between devices  131 us (25%)
  matrix products  103 us (20%)
  Pallas kernels  101 us (20%)
  starting transfers between devices  87.4 us (17%)
  other arithmetic  57.5 us (11%)
  local copies, waits for them, and re-layouts  29.1 us (6%)
    ppermute x18, waiting for transfers between devices, plane_hops(): return [lax.ppermute(block, 'dp', pairs) for pairs in hops]  59.6 us
    ppermute x24, starting transfers between devices, ahead(): lax.ppermute(block, 'fsdp', [(i, (i + step) % n_line) for i in range(n_li...  51.2 us
    pallas_call x4, Pallas kernels, attend_back(): pl.pallas_call(body, grid=(count,), in_specs=pair_specs(rows, pairs, star...  41.6 us
    dot_general x16, matrix products, t_times(): lax.dot_general(left, right, (((0,), (0,)), ((), ())), preferred_element_...  40.7 us
    ppermute x24, waiting for transfers between devices, ahead(): lax.ppermute(block, 'fsdp', [(i, (i + step) % n_line) for i in range(n_li...  39.7 us
    convert_element_type x8, other arithmetic, reduce_steps(): send, = (yield [total.astype(jnp.bfloat16)])  23.5 us
    pallas_call x3, Pallas kernels, assemble(): pl.pallas_call(body, in_specs=[pl.BlockSpec(memory_space=pltpu.SMEM)] + [...  22.8 us
    dot_general x4, matrix products, times_t(): lax.dot_general(left, right, (((1,), (1,)), ((), ())), preferred_element_...  20.7 us
  transfers between devices with their start and end apart: 76, of which 23 were waited for; matrix products, arithmetic and copies ran while one was open for 23% of the time, Pallas kernels for 16%

profile of v6, /device:TPU:0, one launch (start us, length us, event | category | flops | bytes accessed | tf_op | source)
XLA Modules:
  0.0 510.5 jit_solution(8735538851854415293)
XLA Ops:
  5.8 3.1 collective-permute-start
  8.9 2.6 collective-permute-start.1
  19.9 6.6 %collective-permute-done.1 = bf16[32,3584]{1,0:T(8,128)(2,1)S(1)} collective-permute-done((bf16[32,3584]{1,0:T(8,128)(2,1)S(1)}, bf16[32,3584]{1,0:T(8,128)(2,1)S(1)}, u32[]{:S(2)}, u32[]{:S(2)}) %collective-permute-start.1) | collective-permute-done | bytes 229408 | tf_op jit(solution)/shard_map/ppermute | solution.py:298
  30.4 5.4 %collective-permute-start.5 = (bf16[32,5120]{1,0:T(8,128)(2,1)}, bf16[32,5120]{1,0:T(8,128)(2,1)}, u32[]{:S(2)}, u32[]{:S(2)}) collective-permute-start(bf16[32,5120]{1,0:T(8,128)(2,1)} %pad_maximum_fusion.3), channel_id=1, source_target_pairs={{0,1},{1,2},{2,3},{3,0},{4,5},{5,6},{6,7},{7,4},{8,9},{9,10},{10,1... | collective-permute-start | bytes 983048 | tf_op jit(solution)/shard_map/ppermute | solution.py:298
  40.3 5.6 %collective-permute-done.5 = bf16[32,5120]{1,0:T(8,128)(2,1)} collective-permute-done((bf16[32,5120]{1,0:T(8,128)(2,1)}, bf16[32,5120]{1,0:T(8,128)(2,1)}, u32[]{:S(2)}, u32[]{:S(2)}) %collective-permute-start.5) | collective-permute-done | bytes 327712 | tf_op jit(solution)/shard_map/ppermute | solution.py:298
  45.9 11.8 %collective-permute-done.6 = bf16[32,5120]{1,0:T(8,128)(2,1)} collective-permute-done((bf16[32,5120]{1,0:T(8,128)(2,1)}, bf16[32,5120]{1,0:T(8,128)(2,1)}, u32[]{:S(2)}, u32[]{:S(2)}) %collective-permute-start.6) | collective-permute-done | bytes 327712 | tf_op jit(solution)/shard_map/ppermute | solution.py:298
  58.6 9.1 %collective-permute-done.8.refs_4_ = bf16[1,3,32,3072]{3,2,1,0:T(8,128)(2,1)S(1)} collective-permute-done((bf16[1,3,32,3072]{3,2,1,0:T(8,128)(2,1)}, bf16[1,3,32,3072]{3,2,1,0:T(8,128)(2,1)S(1)}, u32[]{:S(2)}, u32[]{:S(2)}) %collective-permute-start.8) | collective-permute-done | bytes 589856 | tf_op jit(solution)/shard_map/ppermute | solution.py:468
  69.5 7.5 %collective-permute-start.9 = (bf16[128,1024]{1,0:T(8,128)(2,1)S(1)}, bf16[128,1024]{1,0:T(8,128)(2,1)}, u32[]{:S(2)}, u32[]{:S(2)}) collective-permute-start(bf16[128,1024]{1,0:T(8,128)(2,1)S(1)} %constant_dynamic-slice_fusion.4), channel_id=1, source_target_pairs={{0,1},{1,2},{2,3},{3,0},{4,5},{5,6},{6,7},{7,4},{8,9},{9,10},{10,1... | collective-permute-start | bytes 786440 | tf_op jit(solution)/shard_map/ppermute | solution.py:298
  77.1 2.4 collective-permute-start.10
  82.2 6.2 %assemble.3 = bf16[1024,3072]{1,0:T(8,128)(2,1)} custom-call(s32[33]{0:T(128)} %pad_add_fusion.1.table_ref, bf16[256,3072]{1,0:T(8,128)(2,1)} %refs_0_.3, bf16[1,3,32,3072]{3,2,1,0:T(8,128)(2,1)} %maximum_bitcast_fusion.2.refs_1_, bf16[1,3,32,3072]{3,2,1,0:T(8,128)(2,1)} %collective-permute-done.4.refs_2_, ...), custom_call_target="tpu_custom_call" | custom-call | tf_op jit(solution)/shard_map/assemble/pallas_call | solution.py:225
  88.4 2.3 collective-permute-start.18
  90.8 7.8 %convolution_convert_fusion.2.refs_2_.refs_3_.refs_4_ = bf16[512,3072]{1,0:T(8,128)(2,1)} fusion(bf16[1024,3072]{1,0:T(8,128)(2,1)} %assemble.3, f32[512,1024]{1,0:T(8,128)S(1)} %get-tuple-element.318, f32[1024]{0:T(1024)S(1)} %bitcast.224, f32[1024]{0:T(1024)S(1)} %bitcast.212, f32[512]{0:T(512)S(1)} %fusion.73, f32[512]{0:T(512)S(1)} %broadcast_multiply_fusion.1), kind=kOutput, calls=%fused_computation.13 | convolution fusion | flops 3225419776 | bytes 11546624 | tf_op jit(solution)/shard_map/dot_general | solution.py:662
  98.5 8.8 %attend.2 = bf16[512,512]{1,0:T(8,128)(2,1)} custom-call(s32[512,1]{1,0:T(8,128)} %fusion.35.refs_0_, s32[1,512]{1,0:T(1,128)} %broadcast_select_fusion.2.refs_1_, bf16[512,3072]{1,0:T(8,128)(2,1)} %convolution_convert_fusion.2.refs_2_.refs_3_.refs_4_, bf16[512,3072]{1,0:T(8,128)(2,1)} %convolution_convert_fusion.2.refs_2_.refs_3_.refs_4_, ...), custom_call_target="tpu_custom_call" | custom-call | tf_op jit(solution)/shard_map/attend/pallas_call | solution.py:148
  107.4 8.9 %attend.3 = bf16[512,512]{1,0:T(8,128)(2,1)} custom-call(s32[512,1]{1,0:T(8,128)} %fusion.35.refs_0_, s32[1,512]{1,0:T(1,128)} %broadcast_select_fusion.2.refs_1_, bf16[512,3072]{1,0:T(8,128)(2,1)} %convolution_convert_fusion.2.refs_2_.refs_3_.refs_4_, bf16[512,3072]{1,0:T(8,128)(2,1)} %convolution_convert_fusion.2.refs_2_.refs_3_.refs_4_, ...), custom_call_target="tpu_custom_call" | custom-call | tf_op jit(solution)/shard_map/attend/pallas_call | solution.py:148
  116.3 2.3 pad_maximum_fusion
  118.6 6.7 %collective-permute-done.18.refs_5_ = bf16[1,3,32,5120]{3,2,1,0:T(8,128)(2,1)} collective-permute-done((bf16[1,3,32,5120]{3,2,1,0:T(8,128)(2,1)S(1)}, bf16[1,3,32,5120]{3,2,1,0:T(8,128)(2,1)}, u32[]{:S(2)}, u32[]{:S(2)}) %collective-permute-start.18) | collective-permute-done | bytes 983072 | tf_op jit(solution)/shard_map/ppermute | solution.py:305
  131.0 9.0 %assemble.4 = (bf16[1024,1024]{1,0:T(8,128)(2,1)}, bf16[1024,4096]{1,0:T(8,128)(2,1)}) custom-call(s32[33]{0:T(128)} %pad_add_fusion.1.table_ref, bf16[256,1024]{1,0:T(8,128)(2,1)} %refs_0_.4, bf16[256,4096]{1,0:T(8,128)(2,1)} %refs_1_.1, bf16[1,3,32,5120]{3,2,1,0:T(8,128)(2,1)} %copy-done.15, bf16[1,3,32,5120]{3,2,1,0:T(8,128)(2,1)} %collective-permute-done.16.refs_3_, ...), custom_call_target="tpu_custom_call" | custom-call | tf_op jit(solution)/shard_map/assemble/pallas_call | solution.py:225
  140.1 3.1 fusion.91
  144.1 11.5 %fusion.4 = (bf16[512,4096]{1,0:T(8,128)(2,1)}, bf16[512,4096]{1,0:T(8,128)(2,1)}) fusion(f32[4096]{0:T(1024)S(1)} %bitcast.216, bf16[1024,4096]{1,0:T(8,128)(2,1)S(1)} %copy-done.54, f32[512,1024]{1,0:T(8,128)S(1)} %get-tuple-element.320, f32[1024]{0:T(1024)S(1)} %bitcast.222, f32[1024]{0:T(1024)S(1)} %bitcast.217, f32[512]{0:T(512)S(1)} %fusion.74, ...), kind=kOutput, calls=%fused_computation.6 | convolution fusion | flops 4322754560 | bytes 18903040 | tf_op jit(solution)/shard_map/dot_general | solution.py:671
  155.6 5.5 %column_order.1 = bf16[512,4096]{1,0:T(8,128)(2,1)} custom-call(s32[32]{0:T(128)} %add.443.table_ref, bf16[512,4096]{1,0:T(8,128)(2,1)} %get-tuple-element.247.in_ref), custom_call_target="tpu_custom_call" | custom-call | tf_op jit(solution)/shard_map/column_order/pallas_call | solution.py:245
  161.1 6.0 %convolution_convert_fusion.3 = bf16[2048,1024]{1,0:T(8,128)(2,1)} fusion(bf16[512,4096]{1,0:T(8,128)(2,1)} %column_order.1, bf16[512,1024]{1,0:T(8,128)(2,1)S(1)} %copy-done.14, pred[512]{0:T(512)(128)(4,1)S(1)} %broadcast_select_fusion.3), kind=kOutput, calls=%fused_computation.20 | convolution fusion | flops 2150105088 | bytes 7340544 | tf_op jit(solution)/shard_map/dot_general | solution.py:69
  171.2 16.2 %collective-permute-done.19.refs_2_ = bf16[1,3,128,1024]{3,2,1,0:T(8,128)(2,1)} collective-permute-done((bf16[1,3,128,1024]{3,2,1,0:T(8,128)(2,1)}, bf16[1,3,128,1024]{3,2,1,0:T(8,128)(2,1)}, u32[]{:S(2)}, u32[]{:S(2)}) %collective-permute-start.19) | collective-permute-done | bytes 786464 | tf_op jit(solution)/shard_map/ppermute | solution.py:305
  187.6 18.0 %collective-permute-done.21.refs_4_ = bf16[1,3,128,1024]{3,2,1,0:T(8,128)(2,1)} collective-permute-done((bf16[1,3,128,1024]{3,2,1,0:T(8,128)(2,1)}, bf16[1,3,128,1024]{3,2,1,0:T(8,128)(2,1)}, u32[]{:S(2)}, u32[]{:S(2)}) %collective-permute-start.21) | collective-permute-done | bytes 786464 | tf_op jit(solution)/shard_map/ppermute | solution.py:305
  206.2 2.5 fusion.17
  208.6 4.6 fusion.19
  213.3 2.5 fusion.15
  215.8 7.6 %assemble.5 = bf16[4096,1024]{1,0:T(8,128)(2,1)} custom-call(s32[33]{0:T(128)} %pad_add_fusion.1.table_ref, bf16[1024,1024]{1,0:T(8,128)(2,1)} %refs_0_.5, bf16[1,3,128,1024]{3,2,1,0:T(8,128)(2,1)} %maximum_bitcast_fusion.1.refs_1_, bf16[1,3,128,1024]{3,2,1,0:T(8,128)(2,1)} %collective-permute-done.19.refs_2_, ...), custom_call_target="tpu_custom_call" | custom-call | tf_op jit(solution)/shard_map/assemble/pallas_call | solution.py:225
  223.4 5.1 add_convert_fusion.1
  229.4 4.8 fusion.82
  234.2 3.7 convert_reduce_fusion
  237.8 5.8 %convolution_convert_fusion = bf16[512,4096]{1,0:T(8,128)(2,1)} fusion(bf16[512,4096]{1,0:T(8,128)(2,1)S(1)} %get-tuple-element.192, bf16[512,1024]{1,0:T(8,128)(2,1)} %fusion.15), kind=kOutput, calls=%fused_computation.11 | convolution fusion | flops 2149580800 | bytes 8912896 | tf_op jit(solution)/shard_map/dot_general | solution.py:69
  244.2 2.3 fusion.16
  248.3 3.3 fusion.22
  252.1 7.9 %multiply_reduce_fusion = (f32[1024]{0:T(1024)S(1)}, f32[512]{0:T(512)S(1)}, f32[1024]{0:T(1024)S(1)}, f32[512,1024]{1,0:T(8,128)S(1)}) fusion(f32[512,1024]{1,0:T(8,128)S(1)} %copy-done.8, f32[512]{0:T(512)S(1)} %fusion.74, f32[512]{0:T(512)S(1)} %broadcast_multiply_fusion, f32[1024]{0:T(1024)S(1)} %bitcast.219, ...), kind=kOutput, calls=%fused_computation.33 | convolution fusion | flops 4299159040 | bytes 16795648 | tf_op jit(solution)/shard_map/dot_general | solution.py:65
  264.0 3.6 add_convert_fusion
  267.6 2.3 convolution_convert_fusion.4.refs_5_
  269.9 7.9 %collective-permute-done.32 = bf16[2,4,128,1024]{3,2,1,0:T(8,128)(2,1)S(1)} collective-permute-done((bf16[2,4,128,1024]{3,2,1,0:T(8,128)(2,1)}, bf16[2,4,128,1024]{3,2,1,0:T(8,128)(2,1)S(1)}, u32[]{:S(2)}, u32[]{:S(2)}) %collective-permute-start.32) | collective-permute-done | bytes 2097184 | tf_op jit(solution)/shard_map/ppermute | solution.py:324
  284.1 10.4 %attend_back.4 = bf16[512,768]{1,0:T(8,128)(2,1)} custom-call(s32[512,1]{1,0:T(8,128)} %fusion.35.refs_0_, s32[1,512]{1,0:T(1,128)} %broadcast_select_fusion.2.refs_1_, bf16[512,3072]{1,0:T(8,128)(2,1)} %convolution_convert_fusion.2.refs_2_.refs_3_.refs_4_, bf16[512,3072]{1,0:T(8,128)(2,1)} %convolution_convert_fusion.2.refs_2_.refs_3_.refs_4_, ...), custom_call_target="tpu_custom_call" | custom-call | tf_op jit(solution)/shard_map/attend_back/pallas_call | solution.py:167
  299.4 10.6 %attend_back.5 = bf16[512,768]{1,0:T(8,128)(2,1)} custom-call(s32[512,1]{1,0:T(8,128)} %fusion.35.refs_0_, s32[1,512]{1,0:T(1,128)} %broadcast_select_fusion.2.refs_1_, bf16[512,3072]{1,0:T(8,128)(2,1)} %convolution_convert_fusion.2.refs_2_.refs_3_.refs_4_, bf16[512,3072]{1,0:T(8,128)(2,1)} %convolution_convert_fusion.2.refs_2_.refs_3_.refs_4_, ...), custom_call_target="tpu_custom_call" | custom-call | tf_op jit(solution)/shard_map/attend_back/pallas_call | solution.py:167
  310.0 8.5 %collective-permute-done.34 = bf16[1,4,128,1024]{3,2,1,0:T(8,128)(2,1)} collective-permute-done((bf16[1,4,128,1024]{3,2,1,0:T(8,128)(2,1)S(1)}, bf16[1,4,128,1024]{3,2,1,0:T(8,128)(2,1)}, u32[]{:S(2)}, u32[]{:S(2)}) %collective-permute-start.34) | collective-permute-done | bytes 1048608 | tf_op jit(solution)/shard_map/ppermute | solution.py:324
  319.1 2.6 fusion.10
  322.7 10.3 %attend_back.6 = bf16[512,768]{1,0:T(8,128)(2,1)} custom-call(s32[512,1]{1,0:T(8,128)} %fusion.35.refs_0_, s32[1,512]{1,0:T(1,128)} %broadcast_select_fusion.2.refs_1_, bf16[512,3072]{1,0:T(8,128)(2,1)} %convolution_convert_fusion.2.refs_2_.refs_3_.refs_4_, bf16[512,3072]{1,0:T(8,128)(2,1)} %convolution_convert_fusion.2.refs_2_.refs_3_.refs_4_, ...), custom_call_target="tpu_custom_call" | custom-call | tf_op jit(solution)/shard_map/attend_back/pallas_call | solution.py:167
  338.3 3.6 add_convert_fusion.3
  345.0 10.3 %attend_back.7 = bf16[512,768]{1,0:T(8,128)(2,1)} custom-call(s32[512,1]{1,0:T(8,128)} %fusion.35.refs_0_, s32[1,512]{1,0:T(1,128)} %broadcast_select_fusion.2.refs_1_, bf16[512,3072]{1,0:T(8,128)(2,1)} %convolution_convert_fusion.2.refs_2_.refs_3_.refs_4_, bf16[512,3072]{1,0:T(8,128)(2,1)} %convolution_convert_fusion.2.refs_2_.refs_3_.refs_4_, ...), custom_call_target="tpu_custom_call" | custom-call | tf_op jit(solution)/shard_map/attend_back/pallas_call | solution.py:167
  361.3 3.5 convolution_convert_fusion.1
  364.9 3.1 fusion.55
  369.9 3.5 collective-permute-start.66
  376.2 5.8 %fusion.92 = f32[512,1024]{1,0:T(8,128)S(1)} fusion(bf16[512,3072]{1,0:T(8,128)(2,1)S(1)} %slice_dynamic-update-slice_fusion, bf16[1024,3072]{1,0:T(8,128)(2,1)} %assemble.3), kind=kOutput, calls=%fused_computation.281 | convolution fusion | flops 3221225472 | bytes 11534336 | tf_op jit(solution)/shard_map/dot_general | solution.py:65
  393.5 3.0 add_convert_fusion.2
  398.8 3.4 collective-permute-done.45
  402.2 2.2 fusion.9
  412.6 2.2 collective-permute-start.48
  415.6 3.5 fusion.83
  419.7 9.0 %select_convert_fusion = bf16[512,1024]{1,0:T(8,128)(2,1)} fusion(f32[512,1024]{1,0:T(8,128)S(1)} %copy-done.9, bf16[512,4096]{1,0:T(8,128)(2,1)S(1)} %copy-done.13, bf16[4096,1024]{1,0:T(8,128)(2,1)} %assemble.5, pred[512]{0:T(512)(128)(4,1)S(1)} %broadcast_select_fusion.3), kind=kOutput, calls=%fused_computation.35 | convolution fusion | flops 4296540160 | bytes 15729152 | tf_op jit(solution)/shard_map/dot_general | solution.py:712
  431.0 2.6 add_convert_fusion.7
  440.4 5.6 %collective-permute-done.71 = bf16[1,32,4096]{2,1,0:T(8,128)(2,1)S(1)} collective-permute-done((bf16[1,32,4096]{2,1,0:T(8,128)(2,1)S(1)}, bf16[1,32,4096]{2,1,0:T(8,128)(2,1)S(1)}, u32[]{:S(2)}, u32[]{:S(2)}) %collective-permute-start.71) | collective-permute-done | bytes 262176 | tf_op jit(solution)/shard_map/ppermute | solution.py:305
  446.7 3.7 collective-permute-done.56
  452.3 6.1 %collective-permute-start.59 = (bf16[32,3072]{1,0:T(8,128)(2,1)S(1)}, bf16[32,3072]{1,0:T(8,128)(2,1)S(1)}, u32[]{:S(2)}, u32[]{:S(2)}) collective-permute-start(bf16[32,3072]{1,0:T(8,128)(2,1)S(1)} %get-tuple-element.293), channel_id=1, source_target_pairs={{0,3},{1,0},{2,1},{3,2},{4,7},{5,4},{6,5},{7,6},{8,11},{9,8},{10,9... | collective-permute-start | bytes 589832 | tf_op jit(solution)/shard_map/ppermute | solution.py:298
  463.0 13.6 %collective-permute-done.58 = bf16[32,3072]{1,0:T(8,128)(2,1)S(1)} collective-permute-done((bf16[32,3072]{1,0:T(8,128)(2,1)S(1)}, bf16[32,3072]{1,0:T(8,128)(2,1)S(1)}, u32[]{:S(2)}, u32[]{:S(2)}) %collective-permute-start.58) | collective-permute-done | bytes 196640 | tf_op jit(solution)/shard_map/ppermute | solution.py:298
  481.5 3.8 collective-permute-done.62
  485.6 3.3 collective-permute-done.61
  496.5 3.8 finish.7
  503.1 3.8 finish.6
  507.0 3.3 finish.4
  (376 shorter events, 133.1 us)
Async XLA Ops:
  5.8 14.1 %collective-permute-start = (bf16[32,3584]{1,0:T(8,128)(2,1)S(1)}, bf16[32,3584]{1,0:T(8,128)(2,1)S(1)}, u32[]{:S(2)}, u32[]{:S(2)}) collective-permute-start(bf16[32,3584]{1,0:T(8,128)(2,1)S(1)} %pad_maximum_fusion.5), channel_id=1, source_target_pairs={{0,1},{1,2},{2,3},{3,0},{4,5},{5,6},{6,7},{7,4},{8,9},{9,10},{10,1... | collective-permute-start | bytes 688136 | tf_op jit(solution)/shard_map/ppermute | solution.py:298
  8.9 17.6 %collective-permute-start.1 = (bf16[32,3584]{1,0:T(8,128)(2,1)S(1)}, bf16[32,3584]{1,0:T(8,128)(2,1)S(1)}, u32[]{:S(2)}, u32[]{:S(2)}) collective-permute-start(bf16[32,3584]{1,0:T(8,128)(2,1)S(1)} %pad_maximum_fusion.5), channel_id=1, source_target_pairs={{0,2},{1,3},{2,0},{3,1},{4,6},{5,7},{6,4},{7,5},{8,10},{9,11},{10,... | collective-permute-start | bytes 688136 | tf_op jit(solution)/shard_map/ppermute | solution.py:298
  11.5 15.0 %collective-permute-start.2 = (bf16[32,3584]{1,0:T(8,128)(2,1)S(1)}, bf16[32,3584]{1,0:T(8,128)(2,1)S(1)}, u32[]{:S(2)}, u32[]{:S(2)}) collective-permute-start(bf16[32,3584]{1,0:T(8,128)(2,1)S(1)} %pad_maximum_fusion.5), channel_id=1, source_target_pairs={{0,3},{1,0},{2,1},{3,2},{4,7},{5,4},{6,5},{7,6},{8,11},{9,8},{10,9... | collective-permute-start | bytes 688136 | tf_op jit(solution)/shard_map/ppermute | solution.py:298
  27.4 31.2 %collective-permute-start.3 = (bf16[1,3,32,3072]{3,2,1,0:T(8,128)(2,1)}, bf16[1,3,32,3072]{3,2,1,0:T(8,128)(2,1)}, u32[]{:S(2)}, u32[]{:S(2)}) collective-permute-start(bf16[1,3,32,3072]{3,2,1,0:T(8,128)(2,1)} %maximum_bitcast_fusion.2.refs_1_), channel_id=1, source_target_pairs={{0,16},{4,12},{8,24},{12,4},{16,0},{20,28},{24,8},{28,20},{1,17},{... | collective-permute-start | bytes 1769480 | tf_op jit(solution)/shard_map/ppermute | solution.py:468
  28.9 28.7 %collective-permute-start.4 = (bf16[1,3,32,3072]{3,2,1,0:T(8,128)(2,1)}, bf16[1,3,32,3072]{3,2,1,0:T(8,128)(2,1)}, u32[]{:S(2)}, u32[]{:S(2)}) collective-permute-start(bf16[1,3,32,3072]{3,2,1,0:T(8,128)(2,1)} %maximum_bitcast_fusion.2.refs_1_), channel_id=1, source_target_pairs={{0,8},{4,20},{8,0},{12,28},{16,24},{20,4},{24,16},{28,12},{1,9},{5... | collective-permute-start | bytes 1769480 | tf_op jit(solution)/shard_map/ppermute | solution.py:468
  30.4 15.4 %collective-permute-start.5 = (bf16[32,5120]{1,0:T(8,128)(2,1)}, bf16[32,5120]{1,0:T(8,128)(2,1)}, u32[]{:S(2)}, u32[]{:S(2)}) collective-permute-start(bf16[32,5120]{1,0:T(8,128)(2,1)} %pad_maximum_fusion.3), channel_id=1, source_target_pairs={{0,1},{1,2},{2,3},{3,0},{4,5},{5,6},{6,7},{7,4},{8,9},{9,10},{10,1... | collective-permute-start | bytes 983048 | tf_op jit(solution)/shard_map/ppermute | solution.py:298
  35.8 21.8 %collective-permute-start.6 = (bf16[32,5120]{1,0:T(8,128)(2,1)}, bf16[32,5120]{1,0:T(8,128)(2,1)}, u32[]{:S(2)}, u32[]{:S(2)}) collective-permute-start(bf16[32,5120]{1,0:T(8,128)(2,1)} %pad_maximum_fusion.3), channel_id=1, source_target_pairs={{0,2},{1,3},{2,0},{3,1},{4,6},{5,7},{6,4},{7,5},{8,10},{9,11},{10,... | collective-permute-start | bytes 983048 | tf_op jit(solution)/shard_map/ppermute | solution.py:298
  37.4 20.2 %collective-permute-start.7 = (bf16[32,5120]{1,0:T(8,128)(2,1)}, bf16[32,5120]{1,0:T(8,128)(2,1)}, u32[]{:S(2)}, u32[]{:S(2)}) collective-permute-start(bf16[32,5120]{1,0:T(8,128)(2,1)} %pad_maximum_fusion.3), channel_id=1, source_target_pairs={{0,3},{1,0},{2,1},{3,2},{4,7},{5,4},{6,5},{7,6},{8,11},{9,8},{10,9... | collective-permute-start | bytes 983048 | tf_op jit(solution)/shard_map/ppermute | solution.py:298
  45.9 31.3 %collective-permute-start.12 = (bf16[1,3,32,3072]{3,2,1,0:T(8,128)(2,1)}, bf16[1,3,32,3072]{3,2,1,0:T(8,128)(2,1)S(1)}, u32[]{:S(2)}, u32[]{:S(2)}) collective-permute-start(bf16[1,3,32,3072]{3,2,1,0:T(8,128)(2,1)} %maximum_bitcast_fusion.2.refs_1_), channel_id=1, source_target_pairs={{0,4},{4,0},{8,12},{12,8},{16,20},{20,16},{24,28},{28,24},{1,5},{5... | collective-permute-start | bytes 1769480 | tf_op jit(solution)/shard_map/ppermute | solution.py:294
  57.6 10.1 %collective-permute-start.8 = (bf16[1,3,32,3072]{3,2,1,0:T(8,128)(2,1)}, bf16[1,3,32,3072]{3,2,1,0:T(8,128)(2,1)S(1)}, u32[]{:S(2)}, u32[]{:S(2)}) collective-permute-start(bf16[1,3,32,3072]{3,2,1,0:T(8,128)(2,1)} %collective-permute-done.4.refs_2_), channel_id=1, source_target_pairs={{0,16},{4,12},{8,24},{12,4},{16,0},{20,28},{24,8},{28,20},{1,17},{... | collective-permute-start | bytes 1769480 | tf_op jit(solution)/shard_map/ppermute | solution.py:468
  58.5 21.0 %collective-permute-start.13 = (bf16[1,3,32,3072]{3,2,1,0:T(8,128)(2,1)}, bf16[1,3,32,3072]{3,2,1,0:T(8,128)(2,1)S(1)}, u32[]{:S(2)}, u32[]{:S(2)}) collective-permute-start(bf16[1,3,32,3072]{3,2,1,0:T(8,128)(2,1)} %collective-permute-done.4.refs_2_), channel_id=1, source_target_pairs={{0,4},{4,0},{8,12},{12,8},{16,20},{20,16},{24,28},{28,24},{1,5},{5... | collective-permute-start | bytes 1769480 | tf_op jit(solution)/shard_map/ppermute | solution.py:294
  67.7 12.4 %collective-permute-start.14 = (bf16[1,3,32,3072]{3,2,1,0:T(8,128)(2,1)}, bf16[1,3,32,3072]{3,2,1,0:T(8,128)(2,1)S(1)}, u32[]{:S(2)}, u32[]{:S(2)}) collective-permute-start(bf16[1,3,32,3072]{3,2,1,0:T(8,128)(2,1)} %collective-permute-done.3.refs_3_), channel_id=1, source_target_pairs={{0,4},{4,0},{8,12},{12,8},{16,20},{20,16},{24,28},{28,24},{1,5},{5... | collective-permute-start | bytes 1769480 | tf_op jit(solution)/shard_map/ppermute | solution.py:294
  67.7 12.9 %collective-permute-start.15 = (bf16[1,3,32,3072]{3,2,1,0:T(8,128)(2,1)S(1)}, bf16[1,3,32,3072]{3,2,1,0:T(8,128)(2,1)S(1)}, u32[]{:S(2)}, u32[]{:S(2)}) collective-permute-start(bf16[1,3,32,3072]{3,2,1,0:T(8,128)(2,1)S(1)} %collective-permute-done.8.refs_4_), channel_id=1, source_target_pairs={{0,4},{4,0},{8,12},{12,8},{16,20},{20,16},{24,28},{28,24},{1,5},{5... | collective-permute-start | bytes 1769480 | tf_op jit(solution)/shard_map/ppermute | solution.py:294
  69.5 18.9 %collective-permute-start.9 = (bf16[128,1024]{1,0:T(8,128)(2,1)S(1)}, bf16[128,1024]{1,0:T(8,128)(2,1)}, u32[]{:S(2)}, u32[]{:S(2)}) collective-permute-start(bf16[128,1024]{1,0:T(8,128)(2,1)S(1)} %constant_dynamic-slice_fusion.4), channel_id=1, source_target_pairs={{0,1},{1,2},{2,3},{3,0},{4,5},{5,6},{6,7},{7,4},{8,9},{9,10},{10,1... | collective-permute-start | bytes 786440 | tf_op jit(solution)/shard_map/ppermute | solution.py:298
  77.1 30.2 %collective-permute-start.10 = (bf16[128,1024]{1,0:T(8,128)(2,1)S(1)}, bf16[128,1024]{1,0:T(8,128)(2,1)}, u32[]{:S(2)}, u32[]{:S(2)}) collective-permute-start(bf16[128,1024]{1,0:T(8,128)(2,1)S(1)} %constant_dynamic-slice_fusion.4), channel_id=1, source_target_pairs={{0,2},{1,3},{2,0},{3,1},{4,6},{5,7},{6,4},{7,5},{8,10},{9,11},{10,... | collective-permute-start | bytes 786440 | tf_op jit(solution)/shard_map/ppermute | solution.py:298
  79.5 27.9 %collective-permute-start.11 = (bf16[128,1024]{1,0:T(8,128)(2,1)S(1)}, bf16[128,1024]{1,0:T(8,128)(2,1)}, u32[]{:S(2)}, u32[]{:S(2)}) collective-permute-start(bf16[128,1024]{1,0:T(8,128)(2,1)S(1)} %constant_dynamic-slice_fusion.4), channel_id=1, source_target_pairs={{0,3},{1,0},{2,1},{3,2},{4,7},{5,4},{6,5},{7,6},{8,11},{9,8},{10,9... | collective-permute-start | bytes 786440 | tf_op jit(solution)/shard_map/ppermute | solution.py:298
  80.1 38.5 %collective-permute-start.16 = (bf16[1,3,32,5120]{3,2,1,0:T(8,128)(2,1)S(1)}, bf16[1,3,32,5120]{3,2,1,0:T(8,128)(2,1)}, u32[]{:S(2)}, u32[]{:S(2)}) collective-permute-start(bf16[1,3,32,5120]{3,2,1,0:T(8,128)(2,1)S(1)} %maximum_bitcast_fusion.refs_2_), channel_id=1, source_target_pairs={{0,8},{4,20},{8,0},{12,28},{16,24},{20,4},{24,16},{28,12},{1,9},{5... | collective-permute-start | bytes 2949128 | tf_op jit(solution)/shard_map/ppermute | solution.py:305
  81.7 36.9 %collective-permute-start.17 = (bf16[1,3,32,5120]{3,2,1,0:T(8,128)(2,1)S(1)}, bf16[1,3,32,5120]{3,2,1,0:T(8,128)(2,1)}, u32[]{:S(2)}, u32[]{:S(2)}) collective-permute-start(bf16[1,3,32,5120]{3,2,1,0:T(8,128)(2,1)S(1)} %maximum_bitcast_fusion.refs_2_), channel_id=1, source_target_pairs={{0,16},{4,12},{8,24},{12,4},{16,0},{20,28},{24,8},{28,20},{1,17},{... | collective-permute-start | bytes 2949128 | tf_op jit(solution)/shard_map/ppermute | solution.py:305
  88.4 36.9 %collective-permute-start.18 = (bf16[1,3,32,5120]{3,2,1,0:T(8,128)(2,1)S(1)}, bf16[1,3,32,5120]{3,2,1,0:T(8,128)(2,1)}, u32[]{:S(2)}, u32[]{:S(2)}) collective-permute-start(bf16[1,3,32,5120]{3,2,1,0:T(8,128)(2,1)S(1)} %maximum_bitcast_fusion.refs_2_), channel_id=1, source_target_pairs={{0,24},{4,28},{8,16},{12,20},{16,8},{20,12},{24,0},{28,4},{1,25},{... | collective-permute-start | bytes 2949128 | tf_op jit(solution)/shard_map/ppermute | solution.py:305
  107.4 21.7 %collective-permute-start.22 = (bf16[1,3,32,5120]{3,2,1,0:T(8,128)(2,1)S(1)}, bf16[1,3,32,5120]{3,2,1,0:T(8,128)(2,1)}, u32[]{:S(2)}, u32[]{:S(2)}) collective-permute-start(bf16[1,3,32,5120]{3,2,1,0:T(8,128)(2,1)S(1)} %maximum_bitcast_fusion.refs_2_), channel_id=1, source_target_pairs={{0,4},{4,0},{8,12},{12,8},{16,20},{20,16},{24,28},{28,24},{1,5},{5... | collective-permute-start | bytes 2949128 | tf_op jit(solution)/shard_map/ppermute | solution.py:294
  167.1 56.2 %collective-permute-start.30 = (bf16[4,4,128,1024]{3,2,1,0:T(8,128)(2,1)}, bf16[4,4,128,1024]{3,2,1,0:T(8,128)(2,1)}, u32[]{:S(2)}, u32[]{:S(2)}) collective-permute-start(bf16[4,4,128,1024]{3,2,1,0:T(8,128)(2,1)} %bitcast.24), channel_id=1, source_target_pairs={{0,4},{4,0},{8,12},{12,8},{16,20},{20,16},{24,28},{28,24},{1,5},{5... | collective-permute-start | bytes 12582920 | tf_op jit(solution)/shard_map/ppermute | solution.py:294
  167.5 19.9 %collective-permute-start.19 = (bf16[1,3,128,1024]{3,2,1,0:T(8,128)(2,1)}, bf16[1,3,128,1024]{3,2,1,0:T(8,128)(2,1)}, u32[]{:S(2)}, u32[]{:S(2)}) collective-permute-start(bf16[1,3,128,1024]{3,2,1,0:T(8,128)(2,1)} %maximum_bitcast_fusion.1.refs_1_), channel_id=1, source_target_pairs={{0,8},{4,20},{8,0},{12,28},{16,24},{20,4},{24,16},{28,12},{1,9},{5... | collective-permute-start | bytes 2359304 | tf_op jit(solution)/shard_map/ppermute | solution.py:305
  168.0 19.6 %collective-permute-start.20 = (bf16[1,3,128,1024]{3,2,1,0:T(8,128)(2,1)}, bf16[1,3,128,1024]{3,2,1,0:T(8,128)(2,1)}, u32[]{:S(2)}, u32[]{:S(2)}) collective-permute-start(bf16[1,3,128,1024]{3,2,1,0:T(8,128)(2,1)} %maximum_bitcast_fusion.1.refs_1_), channel_id=1, source_target_pairs={{0,16},{4,12},{8,24},{12,4},{16,0},{20,28},{24,8},{28,20},{1,17},{... | collective-permute-start | bytes 2359304 | tf_op jit(solution)/shard_map/ppermute | solution.py:305
  169.8 35.9 %collective-permute-start.21 = (bf16[1,3,128,1024]{3,2,1,0:T(8,128)(2,1)}, bf16[1,3,128,1024]{3,2,1,0:T(8,128)(2,1)}, u32[]{:S(2)}, u32[]{:S(2)}) collective-permute-start(bf16[1,3,128,1024]{3,2,1,0:T(8,128)(2,1)} %maximum_bitcast_fusion.1.refs_1_), channel_id=1, source_target_pairs={{0,24},{4,28},{8,16},{12,20},{16,8},{20,12},{24,0},{28,4},{1,25},{... | collective-permute-start | bytes 2359304 | tf_op jit(solution)/shard_map/ppermute | solution.py:305
  171.2 44.6 %collective-permute-start.26 = (bf16[1,3,128,1024]{3,2,1,0:T(8,128)(2,1)}, bf16[1,3,128,1024]{3,2,1,0:T(8,128)(2,1)}, u32[]{:S(2)}, u32[]{:S(2)}) collective-permute-start(bf16[1,3,128,1024]{3,2,1,0:T(8,128)(2,1)} %maximum_bitcast_fusion.1.refs_1_), channel_id=1, source_target_pairs={{0,4},{4,0},{8,12},{12,8},{16,20},{20,16},{24,28},{28,24},{1,5},{5... | collective-permute-start | bytes 2359304 | tf_op jit(solution)/shard_map/ppermute | solution.py:294
  205.7 10.1 %collective-permute-start.27 = (bf16[1,3,128,1024]{3,2,1,0:T(8,128)(2,1)}, bf16[1,3,128,1024]{3,2,1,0:T(8,128)(2,1)}, u32[]{:S(2)}, u32[]{:S(2)}) collective-permute-start(bf16[1,3,128,1024]{3,2,1,0:T(8,128)(2,1)} %collective-permute-done.19.refs_2_), channel_id=1, source_target_pairs={{0,4},{4,0},{8,12},{12,8},{16,20},{20,16},{24,28},{28,24},{1,5},{5... | collective-permute-start | bytes 2359304 | tf_op jit(solution)/shard_map/ppermute | solution.py:294
  205.7 10.1 %collective-permute-start.28 = (bf16[1,3,128,1024]{3,2,1,0:T(8,128)(2,1)}, bf16[1,3,128,1024]{3,2,1,0:T(8,128)(2,1)}, u32[]{:S(2)}, u32[]{:S(2)}) collective-permute-start(bf16[1,3,128,1024]{3,2,1,0:T(8,128)(2,1)} %collective-permute-done.20.refs_3_), channel_id=1, source_target_pairs={{0,4},{4,0},{8,12},{12,8},{16,20},{20,16},{24,28},{28,24},{1,5},{5... | collective-permute-start | bytes 2359304 | tf_op jit(solution)/shard_map/ppermute | solution.py:294
  206.2 9.6 %collective-permute-start.29 = (bf16[1,3,128,1024]{3,2,1,0:T(8,128)(2,1)}, bf16[1,3,128,1024]{3,2,1,0:T(8,128)(2,1)}, u32[]{:S(2)}, u32[]{:S(2)}) collective-permute-start(bf16[1,3,128,1024]{3,2,1,0:T(8,128)(2,1)} %collective-permute-done.21.refs_4_), channel_id=1, source_target_pairs={{0,4},{4,0},{8,12},{12,8},{16,20},{20,16},{24,28},{28,24},{1,5},{5... | collective-permute-start | bytes 2359304 | tf_op jit(solution)/shard_map/ppermute | solution.py:294
  243.7 20.4 %collective-permute-start.31 = (bf16[4,4,32,4096]{3,2,1,0:T(8,128)(2,1)}, bf16[4,4,32,4096]{3,2,1,0:T(8,128)(2,1)}, u32[]{:S(2)}, u32[]{:S(2)}) collective-permute-start(bf16[4,4,32,4096]{3,2,1,0:T(8,128)(2,1)} %bitcast.26), channel_id=1, source_target_pairs={{0,4},{4,0},{8,12},{12,8},{16,20},{20,16},{24,28},{28,24},{1,5},{5... | collective-permute-start | bytes 12582920 | tf_op jit(solution)/shard_map/ppermute | solution.py:294
  251.6 26.2 %collective-permute-start.32 = (bf16[2,4,128,1024]{3,2,1,0:T(8,128)(2,1)}, bf16[2,4,128,1024]{3,2,1,0:T(8,128)(2,1)S(1)}, u32[]{:S(2)}, u32[]{:S(2)}) collective-permute-start(bf16[2,4,128,1024]{3,2,1,0:T(8,128)(2,1)} %add_convert_fusion.1), channel_id=1, source_target_pairs={{0,8},{4,20},{8,0},{12,28},{16,24},{20,4},{24,16},{28,12},{1,9},{5... | collective-permute-start | bytes 6291464 | tf_op jit(solution)/shard_map/ppermute | solution.py:324
  281.4 16.1 %collective-permute-start.33 = (bf16[4,4,32,1024]{3,2,1,0:T(8,128)(2,1)}, bf16[4,4,32,1024]{3,2,1,0:T(8,128)(2,1)}, u32[]{:S(2)}, u32[]{:S(2)}) collective-permute-start(bf16[4,4,32,1024]{3,2,1,0:T(8,128)(2,1)} %bitcast.29), channel_id=1, source_target_pairs={{0,4},{4,0},{8,12},{12,8},{16,20},{20,16},{24,28},{28,24},{1,5},{5... | collective-permute-start | bytes 3145736 | tf_op jit(solution)/shard_map/ppermute | solution.py:294
  281.4 56.9 %collective-permute-start.35 = (bf16[2,4,32,4096]{3,2,1,0:T(8,128)(2,1)}, bf16[2,4,32,4096]{3,2,1,0:T(8,128)(2,1)}, u32[]{:S(2)}, u32[]{:S(2)}) collective-permute-start(bf16[2,4,32,4096]{3,2,1,0:T(8,128)(2,1)} %add_convert_fusion), channel_id=1, source_target_pairs={{0,8},{4,20},{8,0},{12,28},{16,24},{20,4},{24,16},{28,12},{1,9},{5... | collective-permute-start | bytes 6291464 | tf_op jit(solution)/shard_map/ppermute | solution.py:324
  294.5 24.1 %collective-permute-start.34 = (bf16[1,4,128,1024]{3,2,1,0:T(8,128)(2,1)S(1)}, bf16[1,4,128,1024]{3,2,1,0:T(8,128)(2,1)}, u32[]{:S(2)}, u32[]{:S(2)}) collective-permute-start(bf16[1,4,128,1024]{3,2,1,0:T(8,128)(2,1)S(1)} %add_convert_fusion.4), channel_id=1, source_target_pairs={{0,16},{4,12},{8,24},{12,4},{16,0},{20,28},{24,8},{28,20},{1,17},{... | collective-permute-start | bytes 3145736 | tf_op jit(solution)/shard_map/ppermute | solution.py:324
  318.5 19.8 %collective-permute-start.36 = (bf16[2,4,32,1024]{3,2,1,0:T(8,128)(2,1)}, bf16[2,4,32,1024]{3,2,1,0:T(8,128)(2,1)}, u32[]{:S(2)}, u32[]{:S(2)}) collective-permute-start(bf16[2,4,32,1024]{3,2,1,0:T(8,128)(2,1)} %add_convert_fusion.8), channel_id=1, source_target_pairs={{0,8},{4,20},{8,0},{12,28},{16,24},{20,4},{24,16},{28,12},{1,9},{5... | collective-permute-start | bytes 1572872 | tf_op jit(solution)/shard_map/ppermute | solution.py:324
  333.0 23.5 %collective-permute-start.37 = (bf16[128,1024]{1,0:T(8,128)(2,1)}, bf16[128,1024]{1,0:T(8,128)(2,1)S(1)}, u32[]{:S(2)}, u32[]{:S(2)}) collective-permute-start(bf16[128,1024]{1,0:T(8,128)(2,1)} %get-tuple-element.221), channel_id=1, source_target_pairs={{0,1},{1,2},{2,3},{3,0},{4,5},{5,6},{6,7},{7,4},{8,9},{9,10},{10,1... | collective-permute-start | bytes 786440 | tf_op jit(solution)/shard_map/ppermute | solution.py:298
  335.0 21.5 %collective-permute-start.38 = (bf16[128,1024]{1,0:T(8,128)(2,1)}, bf16[128,1024]{1,0:T(8,128)(2,1)}, u32[]{:S(2)}, u32[]{:S(2)}) collective-permute-start(bf16[128,1024]{1,0:T(8,128)(2,1)} %get-tuple-element.222), channel_id=1, source_target_pairs={{0,2},{1,3},{2,0},{3,1},{4,6},{5,7},{6,4},{7,5},{8,10},{9,11},{10,... | collective-permute-start | bytes 786440 | tf_op jit(solution)/shard_map/ppermute | solution.py:298
  335.6 20.9 %collective-permute-start.39 = (bf16[128,1024]{1,0:T(8,128)(2,1)}, bf16[128,1024]{1,0:T(8,128)(2,1)}, u32[]{:S(2)}, u32[]{:S(2)}) collective-permute-start(bf16[128,1024]{1,0:T(8,128)(2,1)} %get-tuple-element.223), channel_id=1, source_target_pairs={{0,3},{1,0},{2,1},{3,2},{4,7},{5,4},{6,5},{7,6},{8,11},{9,8},{10,9... | collective-permute-start | bytes 786440 | tf_op jit(solution)/shard_map/ppermute | solution.py:298
  343.8 12.7 %collective-permute-start.40 = (bf16[1,4,32,1024]{3,2,1,0:T(8,128)(2,1)}, bf16[1,4,32,1024]{3,2,1,0:T(8,128)(2,1)}, u32[]{:S(2)}, u32[]{:S(2)}) collective-permute-start(bf16[1,4,32,1024]{3,2,1,0:T(8,128)(2,1)} %add_convert_fusion.11), channel_id=1, source_target_pairs={{0,16},{4,12},{8,24},{12,4},{16,0},{20,28},{24,8},{28,20},{1,17},{... | collective-permute-start | bytes 786440 | tf_op jit(solution)/shard_map/ppermute | solution.py:324
  364.8 28.7 %collective-permute-start.41 = (bf16[4,4,32,3072]{3,2,1,0:T(8,128)(2,1)}, bf16[4,4,32,3072]{3,2,1,0:T(8,128)(2,1)}, u32[]{:S(2)}, u32[]{:S(2)}) collective-permute-start(bf16[4,4,32,3072]{3,2,1,0:T(8,128)(2,1)} %bitcast.50), channel_id=1, source_target_pairs={{0,4},{4,0},{8,12},{12,8},{16,20},{20,16},{24,28},{28,24},{1,5},{5... | collective-permute-start | bytes 9437192 | tf_op jit(solution)/shard_map/ppermute | solution.py:294
  368.1 34.1 %collective-permute-start.42 = (bf16[1,4,32,4096]{3,2,1,0:T(8,128)(2,1)S(1)}, bf16[1,4,32,4096]{3,2,1,0:T(8,128)(2,1)S(1)}, u32[]{:S(2)}, u32[]{:S(2)}) collective-permute-start(bf16[1,4,32,4096]{3,2,1,0:T(8,128)(2,1)S(1)} %copy-done.26), channel_id=1, source_target_pairs={{0,16},{4,12},{8,24},{12,4},{16,0},{20,28},{24,8},{28,20},{1,17},{... | collective-permute-start | bytes 3145736 | tf_op jit(solution)/shard_map/ppermute | solution.py:324
  369.9 14.0 %collective-permute-start.66 = (bf16[32,1024]{1,0:T(8,128)(2,1)S(1)}, bf16[32,1024]{1,0:T(8,128)(2,1)S(1)}, u32[]{:S(2)}, u32[]{:S(2)}) collective-permute-start(bf16[32,1024]{1,0:T(8,128)(2,1)S(1)} %copy-done.49), channel_id=1, source_target_pairs={{0,3},{1,0},{2,1},{3,2},{4,7},{5,4},{6,5},{7,6},{8,11},{9,8},{10,9... | collective-permute-start | bytes 196616 | tf_op jit(solution)/shard_map/ppermute | solution.py:298
  373.4 10.5 %collective-permute-start.65 = (bf16[32,1024]{1,0:T(8,128)(2,1)S(1)}, bf16[32,1024]{1,0:T(8,128)(2,1)S(1)}, u32[]{:S(2)}, u32[]{:S(2)}) collective-permute-start(bf16[32,1024]{1,0:T(8,128)(2,1)S(1)} %copy-done.48), channel_id=1, source_target_pairs={{0,2},{1,3},{2,0},{3,1},{4,6},{5,7},{6,4},{7,5},{8,10},{9,11},{10,... | collective-permute-start | bytes 196616 | tf_op jit(solution)/shard_map/ppermute | solution.py:298
  390.9 11.3 %collective-permute-start.45 = (bf16[1,128,1024]{2,1,0:T(8,128)(2,1)S(1)}, bf16[1,128,1024]{2,1,0:T(8,128)(2,1)S(1)}, u32[]{:S(2)}, u32[]{:S(2)}) collective-permute-start(bf16[1,128,1024]{2,1,0:T(8,128)(2,1)S(1)} %fusion.40), channel_id=1, source_target_pairs={{0,24},{4,28},{8,16},{12,20},{16,8},{20,12},{24,0},{28,4},{1,25},{... | collective-permute-start | bytes 786440 | tf_op jit(solution)/shard_map/ppermute | solution.py:305
  409.2 21.8 %collective-permute-start.46 = (bf16[2,4,32,3072]{3,2,1,0:T(8,128)(2,1)}, bf16[2,4,32,3072]{3,2,1,0:T(8,128)(2,1)}, u32[]{:S(2)}, u32[]{:S(2)}) collective-permute-start(bf16[2,4,32,3072]{3,2,1,0:T(8,128)(2,1)} %add_convert_fusion.2), channel_id=1, source_target_pairs={{0,8},{4,20},{8,0},{12,28},{16,24},{20,4},{24,16},{28,12},{1,9},{5... | collective-permute-start | bytes 4718600 | tf_op jit(solution)/shard_map/ppermute | solution.py:324
  410.6 19.5 %collective-permute-start.47 = (bf16[32,4096]{1,0:T(8,128)(2,1)}, bf16[32,4096]{1,0:T(8,128)(2,1)S(1)}, u32[]{:S(2)}, u32[]{:S(2)}) collective-permute-start(bf16[32,4096]{1,0:T(8,128)(2,1)} %get-tuple-element.249), channel_id=1, source_target_pairs={{0,1},{1,2},{2,3},{3,0},{4,5},{5,6},{6,7},{7,4},{8,9},{9,10},{10,1... | collective-permute-start | bytes 786440 | tf_op jit(solution)/shard_map/ppermute | solution.py:298
  412.6 18.4 %collective-permute-start.48 = (bf16[32,4096]{1,0:T(8,128)(2,1)}, bf16[32,4096]{1,0:T(8,128)(2,1)}, u32[]{:S(2)}, u32[]{:S(2)}) collective-permute-start(bf16[32,4096]{1,0:T(8,128)(2,1)} %get-tuple-element.250), channel_id=1, source_target_pairs={{0,2},{1,3},{2,0},{3,1},{4,6},{5,7},{6,4},{7,5},{8,10},{9,11},{10,... | collective-permute-start | bytes 786440 | tf_op jit(solution)/shard_map/ppermute | solution.py:298
  414.7 16.2 %collective-permute-start.49 = (bf16[32,4096]{1,0:T(8,128)(2,1)}, bf16[32,4096]{1,0:T(8,128)(2,1)}, u32[]{:S(2)}, u32[]{:S(2)}) collective-permute-start(bf16[32,4096]{1,0:T(8,128)(2,1)} %get-tuple-element.251), channel_id=1, source_target_pairs={{0,3},{1,0},{2,1},{3,2},{4,7},{5,4},{6,5},{7,6},{8,11},{9,8},{10,9... | collective-permute-start | bytes 786440 | tf_op jit(solution)/shard_map/ppermute | solution.py:298
  415.5 76.9 %collective-permute-start.75 = (bf16[4,128,1024]{2,1,0:T(8,128)(2,1)S(1)}, bf16[4,128,1024]{2,1,0:T(8,128)(2,1)}, u32[]{:S(2)}, u32[]{:S(2)}) collective-permute-start(bf16[4,128,1024]{2,1,0:T(8,128)(2,1)S(1)} %pad_maximum_fusion.1.refs_0_), channel_id=1, source_target_pairs={{0,4},{4,0},{8,12},{12,8},{16,20},{20,16},{24,28},{28,24},{1,5},{5... | collective-permute-start | bytes 3145736 | tf_op jit(solution)/shard_map/ppermute | solution.py:294
  435.4 15.0 %collective-permute-start.56 = (bf16[1,4,32,3072]{3,2,1,0:T(8,128)(2,1)}, bf16[1,4,32,3072]{3,2,1,0:T(8,128)(2,1)S(1)}, u32[]{:S(2)}, u32[]{:S(2)}) collective-permute-start(bf16[1,4,32,3072]{3,2,1,0:T(8,128)(2,1)} %add_convert_fusion.7), channel_id=1, source_target_pairs={{0,16},{4,12},{8,24},{12,4},{16,0},{20,28},{24,8},{28,20},{1,17},{... | collective-permute-start | bytes 2359304 | tf_op jit(solution)/shard_map/ppermute | solution.py:324
  436.8 9.2 %collective-permute-start.71 = (bf16[1,32,4096]{2,1,0:T(8,128)(2,1)S(1)}, bf16[1,32,4096]{2,1,0:T(8,128)(2,1)S(1)}, u32[]{:S(2)}, u32[]{:S(2)}) collective-permute-start(bf16[1,32,4096]{2,1,0:T(8,128)(2,1)S(1)} %fusion.41), channel_id=1, source_target_pairs={{0,8},{4,20},{8,0},{12,28},{16,24},{20,4},{24,16},{28,12},{1,9},{5... | collective-permute-start | bytes 786440 | tf_op jit(solution)/shard_map/ppermute | solution.py:305
  438.4 21.3 %collective-permute-start.72 = (bf16[1,32,4096]{2,1,0:T(8,128)(2,1)S(1)}, bf16[1,32,4096]{2,1,0:T(8,128)(2,1)S(1)}, u32[]{:S(2)}, u32[]{:S(2)}) collective-permute-start(bf16[1,32,4096]{2,1,0:T(8,128)(2,1)S(1)} %fusion.41), channel_id=1, source_target_pairs={{0,16},{4,12},{8,24},{12,4},{16,0},{20,28},{24,8},{28,20},{1,17},{... | collective-permute-start | bytes 786440 | tf_op jit(solution)/shard_map/ppermute | solution.py:305
  439.7 20.7 %collective-permute-start.51 = (f32[4,64,256]{2,0,1:T(4,128)S(1)}, f32[4,64,256]{2,0,1:T(4,128)S(1)}, u32[]{:S(2)}, u32[]{:S(2)}) collective-permute-start(f32[4,64,256]{2,0,1:T(4,128)S(1)} %fusion.80), channel_id=1, source_target_pairs={{0,8},{4,12},{8,0},{12,4},{16,24},{20,28},{24,16},{28,20},{1,9},{5... | collective-permute-start | bytes 786440 | tf_op jit(solution)/shard_map/ppermute | solution.py:341
  452.3 10.1 %collective-permute-start.59 = (bf16[32,3072]{1,0:T(8,128)(2,1)S(1)}, bf16[32,3072]{1,0:T(8,128)(2,1)S(1)}, u32[]{:S(2)}, u32[]{:S(2)}) collective-permute-start(bf16[32,3072]{1,0:T(8,128)(2,1)S(1)} %get-tuple-element.293), channel_id=1, source_target_pairs={{0,3},{1,0},{2,1},{3,2},{4,7},{5,4},{6,5},{7,6},{8,11},{9,8},{10,9... | collective-permute-start | bytes 589832 | tf_op jit(solution)/shard_map/ppermute | solution.py:298
  458.5 18.2 %collective-permute-start.58 = (bf16[32,3072]{1,0:T(8,128)(2,1)S(1)}, bf16[32,3072]{1,0:T(8,128)(2,1)S(1)}, u32[]{:S(2)}, u32[]{:S(2)}) collective-permute-start(bf16[32,3072]{1,0:T(8,128)(2,1)S(1)} %get-tuple-element.294), channel_id=1, source_target_pairs={{0,2},{1,3},{2,0},{3,1},{4,6},{5,7},{6,4},{7,5},{8,10},{9,11},{10,... | collective-permute-start | bytes 589832 | tf_op jit(solution)/shard_map/ppermute | solution.py:298
  459.7 17.0 %collective-permute-start.57 = (bf16[32,3072]{1,0:T(8,128)(2,1)S(1)}, bf16[32,3072]{1,0:T(8,128)(2,1)S(1)}, u32[]{:S(2)}, u32[]{:S(2)}) collective-permute-start(bf16[32,3072]{1,0:T(8,128)(2,1)S(1)} %get-tuple-element.292), channel_id=1, source_target_pairs={{0,1},{1,2},{2,3},{3,0},{4,5},{5,6},{6,7},{7,4},{8,9},{9,10},{10,1... | collective-permute-start | bytes 589832 | tf_op jit(solution)/shard_map/ppermute | solution.py:298
  460.4 18.7 %collective-permute-start.73 = (bf16[1,32,4096]{2,1,0:T(8,128)(2,1)S(1)}, bf16[1,32,4096]{2,1,0:T(8,128)(2,1)S(1)}, u32[]{:S(2)}, u32[]{:S(2)}) collective-permute-start(bf16[1,32,4096]{2,1,0:T(8,128)(2,1)S(1)} %fusion.41), channel_id=1, source_target_pairs={{0,24},{4,28},{8,16},{12,20},{16,8},{20,12},{24,0},{28,4},{1,25},{... | collective-permute-start | bytes 786440 | tf_op jit(solution)/shard_map/ppermute | solution.py:305
  462.4 18.6 %collective-permute-start.52 = (f32[4,64,256]{2,0,1:T(4,128)S(1)}, f32[4,64,256]{2,0,1:T(4,128)S(1)}, u32[]{:S(2)}, u32[]{:S(2)}) collective-permute-start(f32[4,64,256]{2,0,1:T(4,128)S(1)} %add.479), channel_id=1, source_target_pairs={{0,16},{4,20},{8,24},{12,28},{16,0},{20,4},{24,8},{28,12},{1,17},{... | collective-permute-start | bytes 786440 | tf_op jit(solution)/shard_map/ppermute | solution.py:341
  477.4 11.5 %collective-permute-start.61 = (bf16[1,32,3072]{2,1,0:T(8,128)(2,1)S(1)}, bf16[1,32,3072]{2,1,0:T(8,128)(2,1)S(1)}, u32[]{:S(2)}, u32[]{:S(2)}) collective-permute-start(bf16[1,32,3072]{2,1,0:T(8,128)(2,1)S(1)} %fusion.50), channel_id=1, source_target_pairs={{0,16},{4,12},{8,24},{12,4},{16,0},{20,28},{24,8},{28,20},{1,17},{... | collective-permute-start | bytes 589832 | tf_op jit(solution)/shard_map/ppermute | solution.py:305
  479.1 9.8 %collective-permute-start.60 = (bf16[1,32,3072]{2,1,0:T(8,128)(2,1)S(1)}, bf16[1,32,3072]{2,1,0:T(8,128)(2,1)S(1)}, u32[]{:S(2)}, u32[]{:S(2)}) collective-permute-start(bf16[1,32,3072]{2,1,0:T(8,128)(2,1)S(1)} %fusion.50), channel_id=1, source_target_pairs={{0,8},{4,20},{8,0},{12,28},{16,24},{20,4},{24,16},{28,12},{1,9},{5... | collective-permute-start | bytes 589832 | tf_op jit(solution)/shard_map/ppermute | solution.py:305
  481.1 9.3 %collective-permute-start.70 = (bf16[4,32,1024]{2,1,0:T(8,128)(2,1)S(1)}, bf16[4,32,1024]{2,1,0:T(8,128)(2,1)S(1)}, u32[]{:S(2)}, u32[]{:S(2)}) collective-permute-start(bf16[4,32,1024]{2,1,0:T(8,128)(2,1)S(1)} %copy-done.30), channel_id=1, source_target_pairs={{0,4},{4,0},{8,12},{12,8},{16,20},{20,16},{24,28},{28,24},{1,5},{5... | collective-permute-start | bytes 786440 | tf_op jit(solution)/shard_map/ppermute | solution.py:294
  485.3 16.8 %collective-permute-start.74 = (bf16[4,32,4096]{2,1,0:T(8,128)(2,1)}, bf16[4,32,4096]{2,1,0:T(8,128)(2,1)S(1)}, u32[]{:S(2)}, u32[]{:S(2)}) collective-permute-start(bf16[4,32,4096]{2,1,0:T(8,128)(2,1)} %constant_dynamic-update-slice_fusion.refs_0_), channel_id=1, source_target_pairs={{0,4},{4,0},{8,12},{12,8},{16,20},{20,16},{24,28},{28,24},{1,5},{5... | collective-permute-start | bytes 3145736 | tf_op jit(solution)/shard_map/ppermute | solution.py:294
  489.0 18.0 %collective-permute-start.63 = (bf16[4,32,3072]{2,1,0:T(8,128)(2,1)S(1)}, bf16[4,32,3072]{2,1,0:T(8,128)(2,1)}, u32[]{:S(2)}, u32[]{:S(2)}) collective-permute-start(bf16[4,32,3072]{2,1,0:T(8,128)(2,1)S(1)} %pad_maximum_fusion.2.refs_0_), channel_id=1, source_target_pairs={{0,4},{4,0},{8,12},{12,8},{16,20},{20,16},{24,28},{28,24},{1,5},{5... | collective-permute-start | bytes 2359304 | tf_op jit(solution)/shard_map/ppermute | solution.py:294
  489.6 10.7 %collective-permute-start.55 = (f32[64,256]{1,0:T(8,128)S(1)}, f32[64,256]{1,0:T(8,128)S(1)}, u32[]{:S(2)}, u32[]{:S(2)}) collective-permute-start(f32[64,256]{1,0:T(8,128)S(1)} %bitcast.210), channel_id=1, source_target_pairs={{0,3},{1,0},{2,1},{3,2},{4,7},{5,4},{6,5},{7,6},{8,11},{9,8},{10,9... | collective-permute-start | bytes 196616 | tf_op jit(solution)/shard_map/ppermute | solution.py:298
  490.3 10.0 %collective-permute-start.54 = (f32[64,256]{1,0:T(8,128)}, f32[64,256]{1,0:T(8,128)S(1)}, u32[]{:S(2)}, u32[]{:S(2)}) collective-permute-start(f32[64,256]{1,0:T(8,128)} %bitcast.192), channel_id=1, source_target_pairs={{0,2},{1,3},{2,0},{3,1},{4,6},{5,7},{6,4},{7,5},{8,10},{9,11},{10,... | collective-permute-start | bytes 196616 | tf_op jit(solution)/shard_map/ppermute | solution.py:298
  (68 other events, 689.4 us)

commit v7 on v6

--- a/solution.py
+++ b/solution.py
@@ -439,7 +439,7 @@
     def pass_one(self, gate):
         return gate
 
-    pass_two = pass_three = pass_one
+    pass_two = pass_three = pass_four = pass_five = pass_one
 
     def rows(self, block):
         return block
@@ -466,10 +466,6 @@
 
     def hop(self, block, stage):
         return lax.ppermute(block, "dp", hop_pairs(self.n_dp, stage))
-
-    def settle(self, gate):
-        self.line, gate = lax.optimization_barrier((self.line, gate))
-        return gate
 
     def near(self, gate, columns):
         self.line, gate = lax.optimization_barrier((self.line, gate))
@@ -552,12 +548,12 @@
         two = Gather(unit_two, n_dp, n_line)
         two.line = one.forward(two.line)
         two.line = one.close(two.line)
-        table, unit_three = two.fan_wide((self.got_table, unit_three), unit_two.shape[1])
-        three = Gather(unit_three, n_dp, n_line)
+        table = two.fan_wide(self.got_table, unit_two.shape[1])
         (full_qkv,) = assemble([w_qkv], one.parts + one.cores, table, n_line, size)
         self.one = full_qkv
         self.two = ([w_out, w_fc1], two)
-        self.three = (w_fc2, three, unit_three.shape)
+        self.w_fc2 = w_fc2
+        self.unit_three = unit_three
         far = jnp.concatenate([far[:, :, i * shard : (i + 1) * shard] for i in range(fold)], axis=1)
         return jnp.take(jnp.concatenate([padded[None], far]), self.unline, axis=0)
 
@@ -565,21 +561,31 @@
         return self.one
 
     def pass_one(self, gate):
-        return self.three[1].settle(gate)
+        unit, gate = lax.optimization_barrier((self.unit_three, gate))
+        self.three = Gather(unit, self.n_dp, self.n_line)
+        return gate
 
     def pass_two(self, gate):
-        return self.three[1].fan_wide(self.two[1].close_wide(gate), self.three[2][1])
+        return self.two[1].close_wide(gate)
 
     def pass_three(self, gate):
-        return self.three[1].close_wide(gate)
+        return self.three.fan(gate, self.unit_three.shape[1])
+
+    def pass_four(self, gate):
+        return self.three.forward(gate)
+
+    def pass_five(self, gate):
+        return self.three.close(gate)
 
     def second(self):
         owns, got = self.two
         return assemble(owns, got.parts + got.cores, self.got_table, self.n_line, self.unit)
 
     def third(self):
-        own, got, unit = self.three
-        return assemble([own], got.parts + got.cores, self.got_table, self.n_line, unit[0])[0]
+        got = self.three
+        return assemble(
+            [self.w_fc2], got.parts + got.cores, self.got_table, self.n_line, self.unit_three.shape[0]
+        )[0]
 
     def rows(self, block):
         return jnp.dot(block, self.order, preferred_element_type=jnp.float32).astype(jnp.bfloat16)
@@ -661,22 +667,22 @@
     normed_one = layer_norm(hidden_in, gain_one, bias_one).astype(bf16)
     projected = jnp.dot(normed_one, full_qkv, preferred_element_type=f32).astype(bf16)
     half = HEADS // 4
-    rows_a = attend(projected, segment, 0, half)
-    rows_a, projected = plan.pass_one((rows_a, projected))
-    rows_b = attend(projected, segment, half, half)
-    attn_rows = plan.pass_two(jnp.concatenate([rows_a, rows_b], axis=1))
+    projected = plan.pass_one(projected)
+    attn_rows = plan.pass_two(attend(projected, segment, 0, 2 * half))
     full_out, full_fc1 = plan.second()
+    attn_rows, full_out = plan.pass_three((attn_rows, full_out))
     hidden_mid = hidden_in + jnp.dot(attn_rows, full_out, preferred_element_type=f32)
     normed_two = layer_norm(hidden_mid, gain_two, bias_two).astype(bf16)
+    normed_two = plan.pass_four(normed_two)
     pre_act = jnp.dot(normed_two, full_fc1, preferred_element_type=f32) + full_bias
     share = 0.5 * (1.0 + lax.erf(pre_act * 0.5**0.5))
     bell = jnp.exp(-0.5 * pre_act * pre_act) * (0.5 / jnp.pi) ** 0.5
     activated = (pre_act * share).astype(bf16)
     slope = (share + pre_act * bell).astype(bf16)
+    activated, slope = plan.pass_five((activated, slope))
     grad_out = jnp.where(valid[:, None], cotangent, jnp.zeros_like(cotangent))
     run_fc2 = plan.total(plan.wide_columns(activated), grad_out)
     activated, slope = tick((activated, slope), [run_fc2])
-    activated, slope = plan.pass_three((activated, slope))
     full_fc2 = tick(plan.third(), [run_fc2])
 
     grad_pre = (times_t(grad_out, full_fc2) * slope.astype(f32)).astype(bf16)
@@ -693,7 +699,8 @@
     grad_attn = tick(grad_attn, [run_out, run_fc2])
     fourth = HEADS // 8
     backs = []
-    for group in ([run_out], [run_fc2], [run_fc1, run_out], [run_fc2, run_out]):
+    every = [run_fc2, run_fc1, run_out]
+    for group in ([run_out], [], every, every):
         back = attend_back(projected, grad_attn, segment, len(backs) * fourth, fourth)
         back, grad_attn = tick((back, grad_attn), group)
         backs.append(back)
@@ -704,14 +711,14 @@
     run_qkv = plan.total(plan.rows(normed_one), grad_proj)
     grad_proj = tick(grad_proj, [run_qkv])
     grad_norm_one = tick(times_t(grad_proj, full_qkv), [run_qkv])
-    grad_norm_one, activated = tick((grad_norm_one, activated), [run_fc1, run_fc2])
     _, pull_one = jax.vjp(layer_norm, hidden_in, gain_one, bias_one)
     back_in, grad_gain_one, grad_bias_one = pull_one(grad_norm_one)
     grad_in = grad_mid + back_in
     grad_table = jnp.dot(place.T, grad_in, precision=highest)
+    grad_table, activated = tick((grad_table, activated), [run_qkv] + every)
     branch_out = jnp.dot(activated, full_fc2, preferred_element_type=f32)
     block_out = jnp.where(valid[:, None], hidden_mid + branch_out, 0.0).astype(bf16)
-    grad_table, block_out = tick((grad_table, block_out), [run_qkv, run_fc1])
+    block_out = tick(block_out, [run_qkv] + every)
 
     def split(block):
         return block.reshape(-1, n_line, shard).transpose(1, 0, 2)

time: 516 us -> 534 us (1.035)
  matrix products: 103 us -> 115 us
  waiting for transfers between devices: 131 us -> 123 us
  starting transfers between devices: 87.4 us -> 95.3 us
    ppermute x18 -> x15, waiting for transfers between devices: 59.6 us -> 28.7 us  [plane_hops(): return [lax.ppermute(block, 'dp', pairs) for pairs in hops]]
    ppermute x24, waiting for transfers between devices: 39.7 us -> 55.5 us  [ahead(): lax.ppermute(block, 'fsdp', [(i, (i + step) % n_line) for i in range(n_li...]
    ppermute x3 -> x6, waiting for transfers between devices: 9.14 us -> 24.2 us  [hop(): return lax.ppermute(block, 'dp', hop_pairs(self.n_dp, stage))]
    ppermute x8, waiting for transfers between devices: 20.2 us -> 12.2 us  [reduce_steps(): got, = (yield [lax.ppermute(send, 'dp', hop_pairs(n_dp, stage))])]
    dot_general x4, matrix products: 20.7 us -> 28.3 us  [times_t(): lax.dot_general(left, right, (((1,), (1,)), ((), ())), preferred_element_...]
    ppermute x24, starting transfers between devices: 51.2 us -> 58.1 us  [ahead(): lax.ppermute(block, 'fsdp', [(i, (i + step) % n_line) for i in range(n_li...]
    unnamed x134 -> x167, local copies, waits for them, and re-layouts: 14.8 us -> 11.7 us
    pallas_call x2 -> x1, Pallas kernels: 17.7 us -> 15.8 us  [attend(): pl.pallas_call(body, grid=(count,), in_specs=pair_specs(rows, pairs, star...]
  transfers between devices with their start and end apart: 76 -> 76, of which waited for: 23 -> 23; matrix products, arithmetic and copies ran while one was open for 23% -> 26% of each run, Pallas kernels for 16% -> 17%
where the time goes in v7:
time: 534 us; the launch traced here: 525 us
  waiting for transfers between devices  123 us (23%)
  matrix products  115 us (22%)
  Pallas kernels  98.9 us (19%)
  starting transfers between devices  95.3 us (18%)
  other arithmetic  58.8 us (11%)
  local copies, waits for them, and re-layouts  31.2 us (6%)
    ppermute x24, starting transfers between devices, ahead(): lax.ppermute(block, 'fsdp', [(i, (i + step) % n_line) for i in range(n_li...  58.1 us
    ppermute x24, waiting for transfers between devices, ahead(): lax.ppermute(block, 'fsdp', [(i, (i + step) % n_line) for i in range(n_li...  55.5 us
    dot_general x16, matrix products, t_times(): lax.dot_general(left, right, (((0,), (0,)), ((), ())), preferred_element_...  42.8 us
    pallas_call x4, Pallas kernels, attend_back(): pl.pallas_call(body, grid=(count,), in_specs=pair_specs(rows, pairs, star...  41.6 us
    ppermute x15, waiting for transfers between devices, plane_hops(): return [lax.ppermute(block, 'dp', pairs) for pairs in hops]  28.7 us
    dot_general x4, matrix products, times_t(): lax.dot_general(left, right, (((1,), (1,)), ((), ())), preferred_element_...  28.3 us
    ppermute x6, waiting for transfers between devices, hop(): return lax.ppermute(block, 'dp', hop_pairs(self.n_dp, stage))  24.2 us
    pallas_call x3, Pallas kernels, assemble(): pl.pallas_call(body, in_specs=[pl.BlockSpec(memory_space=pltpu.SMEM)] + [...  23 us
  transfers between devices with their start and end apart: 76, of which 23 were waited for; matrix products, arithmetic and copies ran while one was open for 26% of the time, Pallas kernels for 17%

profile of v7, /device:TPU:0, one launch (start us, length us, event | category | flops | bytes accessed | tf_op | source)
XLA Modules:
  0.0 524.9 jit_solution(7092884171813960084)
XLA Ops:
  5.8 3.1 collective-permute-start
  8.9 2.6 collective-permute-start.1
  21.0 5.5 %collective-permute-done.1 = bf16[32,3584]{1,0:T(8,128)(2,1)S(1)} collective-permute-done((bf16[32,3584]{1,0:T(8,128)(2,1)S(1)}, bf16[32,3584]{1,0:T(8,128)(2,1)S(1)}, u32[]{:S(2)}, u32[]{:S(2)}) %collective-permute-start.1) | collective-permute-done | bytes 229408 | tf_op jit(solution)/shard_map/ppermute | solution.py:298
  30.5 5.4 %collective-permute-start.5 = (bf16[32,5120]{1,0:T(8,128)(2,1)}, bf16[32,5120]{1,0:T(8,128)(2,1)}, u32[]{:S(2)}, u32[]{:S(2)}) collective-permute-start(bf16[32,5120]{1,0:T(8,128)(2,1)} %pad_maximum_fusion.3), channel_id=1, source_target_pairs={{0,1},{1,2},{2,3},{3,0},{4,5},{5,6},{6,7},{7,4},{8,9},{9,10},{10,1... | collective-permute-start | bytes 983048 | tf_op jit(solution)/shard_map/ppermute | solution.py:298
  40.3 5.6 %collective-permute-done.5 = bf16[32,5120]{1,0:T(8,128)(2,1)} collective-permute-done((bf16[32,5120]{1,0:T(8,128)(2,1)}, bf16[32,5120]{1,0:T(8,128)(2,1)}, u32[]{:S(2)}, u32[]{:S(2)}) %collective-permute-start.5) | collective-permute-done | bytes 327712 | tf_op jit(solution)/shard_map/ppermute | solution.py:298
  45.9 11.8 %collective-permute-done.6 = bf16[32,5120]{1,0:T(8,128)(2,1)} collective-permute-done((bf16[32,5120]{1,0:T(8,128)(2,1)}, bf16[32,5120]{1,0:T(8,128)(2,1)}, u32[]{:S(2)}, u32[]{:S(2)}) %collective-permute-start.6) | collective-permute-done | bytes 327712 | tf_op jit(solution)/shard_map/ppermute | solution.py:298
  59.1 8.6 %collective-permute-done.8.refs_4_ = bf16[1,3,32,3072]{3,2,1,0:T(8,128)(2,1)S(1)} collective-permute-done((bf16[1,3,32,3072]{3,2,1,0:T(8,128)(2,1)}, bf16[1,3,32,3072]{3,2,1,0:T(8,128)(2,1)S(1)}, u32[]{:S(2)}, u32[]{:S(2)}) %collective-permute-start.8) | collective-permute-done | bytes 589856 | tf_op jit(solution)/shard_map/ppermute | solution.py:468
  70.7 2.4 collective-permute-start.18
  74.0 6.2 %assemble.3 = bf16[1024,3072]{1,0:T(8,128)(2,1)} custom-call(s32[33]{0:T(128)} %pad_add_fusion.1.table_ref, bf16[256,3072]{1,0:T(8,128)(2,1)} %refs_0_.3, bf16[1,3,32,3072]{3,2,1,0:T(8,128)(2,1)} %maximum_bitcast_fusion.2.refs_1_, bf16[1,3,32,3072]{3,2,1,0:T(8,128)(2,1)} %collective-permute-done.4.refs_2_, ...), custom_call_target="tpu_custom_call" | custom-call | tf_op jit(solution)/shard_map/assemble/pallas_call | solution.py:225
  80.3 7.8 %convolution_convert_fusion.2.refs_2_.refs_3_.refs_4_ = bf16[512,3072]{1,0:T(8,128)(2,1)} fusion(bf16[1024,3072]{1,0:T(8,128)(2,1)} %assemble.3, f32[512,1024]{1,0:T(8,128)S(1)} %get-tuple-element.341, f32[1024]{0:T(1024)S(1)} %bitcast.223, f32[1024]{0:T(1024)S(1)} %bitcast.216, f32[512]{0:T(512)S(1)} %fusion.70, f32[512]{0:T(512)S(1)} %broadcast_multiply_fusion.1), kind=kOutput, calls=%fused_computation.13 | convolution fusion | flops 3225419776 | bytes 11546624 | tf_op jit(solution)/shard_map/dot_general | solution.py:668
  88.1 15.8 %attend.1 = bf16[512,1024]{1,0:T(8,128)(2,1)} custom-call(s32[512,1]{1,0:T(8,128)} %fusion.32.refs_0_, s32[1,512]{1,0:T(1,128)} %broadcast_select_fusion.2.refs_1_, bf16[512,3072]{1,0:T(8,128)(2,1)} %convolution_convert_fusion.2.refs_2_.refs_3_.refs_4_, bf16[512,3072]{1,0:T(8,128)(2,1)} %convolution_convert_fusion.2.refs_2_.refs_3_.refs_4_, ...), custom_call_target="tpu_custom_call" | custom-call | tf_op jit(solution)/shard_map/attend/pallas_call | solution.py:148
  103.9 11.2 %collective-permute-done.18.refs_5_ = bf16[1,3,32,5120]{3,2,1,0:T(8,128)(2,1)} collective-permute-done((bf16[1,3,32,5120]{3,2,1,0:T(8,128)(2,1)S(1)}, bf16[1,3,32,5120]{3,2,1,0:T(8,128)(2,1)}, u32[]{:S(2)}, u32[]{:S(2)}) %collective-permute-start.18) | collective-permute-done | bytes 983072 | tf_op jit(solution)/shard_map/ppermute | solution.py:305
  115.8 7.5 %collective-permute-start.13 = (bf16[128,1024]{1,0:T(8,128)(2,1)S(1)}, bf16[128,1024]{1,0:T(8,128)(2,1)}, u32[]{:S(2)}, u32[]{:S(2)}) collective-permute-start(bf16[128,1024]{1,0:T(8,128)(2,1)S(1)} %copy-done.44), channel_id=1, source_target_pairs={{0,1},{1,2},{2,3},{3,0},{4,5},{5,6},{6,7},{7,4},{8,9},{9,10},{10,1... | collective-permute-start | bytes 786440 | tf_op jit(solution)/shard_map/ppermute | solution.py:298
  129.1 9.2 %assemble.4 = (bf16[1024,1024]{1,0:T(8,128)(2,1)}, bf16[1024,4096]{1,0:T(8,128)(2,1)}) custom-call(s32[33]{0:T(128)} %pad_add_fusion.1.table_ref, bf16[256,1024]{1,0:T(8,128)(2,1)} %refs_0_.4, bf16[256,4096]{1,0:T(8,128)(2,1)} %refs_1_.1, bf16[1,3,32,5120]{3,2,1,0:T(8,128)(2,1)} %copy-done.16, bf16[1,3,32,5120]{3,2,1,0:T(8,128)(2,1)} %collective-permute-done.16.refs_3_, ...), custom_call_target="tpu_custom_call" | custom-call | tf_op jit(solution)/shard_map/assemble/pallas_call | solution.py:225
  138.3 5.1 collective-permute-done.14
  147.2 2.9 fusion.86
  151.5 13.9 %collective-permute-done.23.refs_2_ = bf16[1,3,128,1024]{3,2,1,0:T(8,128)(2,1)} collective-permute-done((bf16[1,3,128,1024]{3,2,1,0:T(8,128)(2,1)}, bf16[1,3,128,1024]{3,2,1,0:T(8,128)(2,1)}, u32[]{:S(2)}, u32[]{:S(2)}) %collective-permute-start.23) | collective-permute-done | bytes 786464 | tf_op jit(solution)/shard_map/ppermute | solution.py:468
  166.4 9.5 %fusion.4 = (bf16[512,4096]{1,0:T(8,128)(2,1)}, bf16[512,4096]{1,0:T(8,128)(2,1)}) fusion(f32[4096]{0:T(1024)S(1)} %bitcast.221, bf16[512,1024]{1,0:T(8,128)(2,1)S(1)} %add_convert_fusion.5, bf16[1024,4096]{1,0:T(8,128)(2,1)S(1)} %bitcast.230), kind=kOutput, calls=%fused_computation.6 | convolution fusion | flops 4320133120 | bytes 17842176 | tf_op jit(solution)/shard_map/dot_general | solution.py:677
  177.6 5.4 %column_order.1 = bf16[512,4096]{1,0:T(8,128)(2,1)} custom-call(s32[32]{0:T(128)} %add.443.table_ref, bf16[512,4096]{1,0:T(8,128)(2,1)} %get-tuple-element.270.in_ref), custom_call_target="tpu_custom_call" | custom-call | tf_op jit(solution)/shard_map/column_order/pallas_call | solution.py:245
  183.0 6.1 %convolution_convert_fusion.3 = bf16[2048,1024]{1,0:T(8,128)(2,1)} fusion(bf16[512,4096]{1,0:T(8,128)(2,1)} %column_order.1, bf16[512,1024]{1,0:T(8,128)(2,1)S(1)} %copy-done.13, pred[512]{0:T(512)(128)(4,1)S(1)} %copy-done.66), kind=kOutput, calls=%fused_computation.20 | convolution fusion | flops 2150105088 | bytes 7340544 | tf_op jit(solution)/shard_map/dot_general | solution.py:69
  190.4 3.5 fusion.15
  193.9 4.5 fusion.19
  201.1 7.6 %assemble.5 = bf16[4096,1024]{1,0:T(8,128)(2,1)} custom-call(s32[33]{0:T(128)} %pad_add_fusion.1.table_ref, bf16[1024,1024]{1,0:T(8,128)(2,1)} %refs_0_.5, bf16[1,3,128,1024]{3,2,1,0:T(8,128)(2,1)} %maximum_bitcast_fusion.1.refs_1_, bf16[1,3,128,1024]{3,2,1,0:T(8,128)(2,1)} %collective-permute-done.23.refs_2_, ...), custom_call_target="tpu_custom_call" | custom-call | tf_op jit(solution)/shard_map/assemble/pallas_call | solution.py:225
  208.7 4.9 add_convert_fusion.1
  213.7 10.0 %convert_reduce_fusion = (f32[4096]{0:T(1024)}, bf16[512,4096]{1,0:T(8,128)(2,1)S(1)}) fusion(bf16[512,4096]{1,0:T(8,128)(2,1)} %get-tuple-element.201, bf16[4096,1024]{1,0:T(8,128)(2,1)} %assemble.5, bf16[512,1024]{1,0:T(8,128)(2,1)S(1)} %copy-done.13, pred[512]{0:T(512)(128)(4,1)S(1)} %copy-done.66), kind=kOutput, calls=%fused_computation.7 | convolution fusion | flops 4305973248 | bytes 17842688 | tf_op jit(solution)/shard_map/dot_general | solution.py:65
  223.7 2.4 convolution_convert_fusion
  228.7 3.3 fusion.25
  232.5 10.2 %multiply_reduce_fusion = (f32[1024]{0:T(1024)}, f32[512]{0:T(512)S(1)}, f32[1024]{0:T(1024)}, f32[512,1024]{1,0:T(8,128)}) fusion(f32[512,1024]{1,0:T(8,128)S(1)} %copy-done.5, f32[512]{0:T(512)S(1)} %fusion.71, f32[512]{0:T(512)S(1)} %broadcast_multiply_fusion, f32[1024]{0:T(1024)S(1)} %bitcast.214, bf16[512,4096]{1,0:T(8,128)(2,1)S(1)} %get-tuple-element.202, ...), kind=kOutput, calls=%fused_computation.33 | convolution fusion | flops 4299159040 | bytes 16795648 | tf_op jit(solution)/shard_map/dot_general | solution.py:65
  242.7 2.4 fusion.80
  250.9 2.4 convolution_convert_fusion.4.refs_5_
  253.3 5.0 collective-permute-done.32
  258.8 3.2 add_convert_fusion.4
  263.8 2.5 fusion.17
  266.3 3.1 fusion.22
  270.9 10.3 %attend_back.4 = bf16[512,768]{1,0:T(8,128)(2,1)} custom-call(s32[512,1]{1,0:T(8,128)} %fusion.32.refs_0_, s32[1,512]{1,0:T(1,128)} %broadcast_select_fusion.2.refs_1_, bf16[512,3072]{1,0:T(8,128)(2,1)} %convolution_convert_fusion.2.refs_2_.refs_3_.refs_4_, bf16[512,3072]{1,0:T(8,128)(2,1)} %convolution_convert_fusion.2.refs_2_.refs_3_.refs_4_, ...), custom_call_target="tpu_custom_call" | custom-call | tf_op jit(solution)/shard_map/attend_back/pallas_call | solution.py:167
  284.7 3.0 fusion.58
  289.8 10.3 %attend_back.5 = bf16[512,768]{1,0:T(8,128)(2,1)} custom-call(s32[512,1]{1,0:T(8,128)} %fusion.32.refs_0_, s32[1,512]{1,0:T(1,128)} %broadcast_select_fusion.2.refs_1_, bf16[512,3072]{1,0:T(8,128)(2,1)} %convolution_convert_fusion.2.refs_2_.refs_3_.refs_4_, bf16[512,3072]{1,0:T(8,128)(2,1)} %convolution_convert_fusion.2.refs_2_.refs_3_.refs_4_, ...), custom_call_target="tpu_custom_call" | custom-call | tf_op jit(solution)/shard_map/attend_back/pallas_call | solution.py:167
  300.1 10.7 %attend_back.6 = bf16[512,768]{1,0:T(8,128)(2,1)} custom-call(s32[512,1]{1,0:T(8,128)} %fusion.32.refs_0_, s32[1,512]{1,0:T(1,128)} %broadcast_select_fusion.2.refs_1_, bf16[512,3072]{1,0:T(8,128)(2,1)} %convolution_convert_fusion.2.refs_2_.refs_3_.refs_4_, bf16[512,3072]{1,0:T(8,128)(2,1)} %convolution_convert_fusion.2.refs_2_.refs_3_.refs_4_, ...), custom_call_target="tpu_custom_call" | custom-call | tf_op jit(solution)/shard_map/attend_back/pallas_call | solution.py:167
  310.8 3.2 fusion.10
  315.1 3.1 add_convert_fusion.3
  321.0 3.0 fusion.54
  327.0 6.2 %collective-permute-start.37 = (bf16[128,1024]{1,0:T(8,128)(2,1)}, bf16[128,1024]{1,0:T(8,128)(2,1)S(1)}, u32[]{:S(2)}, u32[]{:S(2)}) collective-permute-start(bf16[128,1024]{1,0:T(8,128)(2,1)} %get-tuple-element.229), channel_id=1, source_target_pairs={{0,1},{1,2},{2,3},{3,0},{4,5},{5,6},{6,7},{7,4},{8,9},{9,10},{10,1... | collective-permute-start | bytes 786440 | tf_op jit(solution)/shard_map/ppermute | solution.py:298
  337.7 10.3 %attend_back.7 = bf16[512,768]{1,0:T(8,128)(2,1)} custom-call(s32[512,1]{1,0:T(8,128)} %fusion.32.refs_0_, s32[1,512]{1,0:T(1,128)} %broadcast_select_fusion.2.refs_1_, bf16[512,3072]{1,0:T(8,128)(2,1)} %convolution_convert_fusion.2.refs_2_.refs_3_.refs_4_, bf16[512,3072]{1,0:T(8,128)(2,1)} %convolution_convert_fusion.2.refs_2_.refs_3_.refs_4_, ...), custom_call_target="tpu_custom_call" | custom-call | tf_op jit(solution)/shard_map/attend_back/pallas_call | solution.py:167
  350.5 3.1 fusion.9
  360.2 3.5 convolution_convert_fusion.1
  368.7 6.2 %collective-permute-start.50 = (bf16[32,1024]{1,0:T(8,128)(2,1)}, bf16[32,1024]{1,0:T(8,128)(2,1)}, u32[]{:S(2)}, u32[]{:S(2)}) collective-permute-start(bf16[32,1024]{1,0:T(8,128)(2,1)} %get-tuple-element.253), channel_id=1, source_target_pairs={{0,1},{1,2},{2,3},{3,0},{4,5},{5,6},{6,7},{7,4},{8,9},{9,10},{10,1... | collective-permute-start | bytes 196616 | tf_op jit(solution)/shard_map/ppermute | solution.py:298
  374.9 2.5 collective-permute-start.51
  377.5 2.7 fusion.50
  382.1 5.6 %fusion.87 = f32[512,1024]{1,0:T(8,128)S(1)} fusion(bf16[512,3072]{1,0:T(8,128)(2,1)S(1)} %slice_dynamic-update-slice_fusion, bf16[1024,3072]{1,0:T(8,128)(2,1)} %assemble.3), kind=kOutput, calls=%fused_computation.272 | convolution fusion | flops 3221225472 | bytes 11534336 | tf_op jit(solution)/shard_map/dot_general | solution.py:65
  387.7 3.2 add_convert_fusion.2
  406.1 3.7 fusion.88
  409.8 8.8 %collective-permute-done.46 = bf16[1,128,1024]{2,1,0:T(8,128)(2,1)S(1)} collective-permute-done((bf16[1,128,1024]{2,1,0:T(8,128)(2,1)}, bf16[1,128,1024]{2,1,0:T(8,128)(2,1)S(1)}, u32[]{:S(2)}, u32[]{:S(2)}) %collective-permute-start.46) | collective-permute-done | bytes 262176 | tf_op jit(solution)/shard_map/ppermute | solution.py:305
  418.6 4.0 collective-permute-done.48
  422.6 2.6 add_convert_fusion.7
  440.2 10.2 %select_convert_fusion = bf16[512,1024]{1,0:T(8,128)(2,1)} fusion(f32[512,1024]{1,0:T(8,128)S(1)} %copy-done.6, bf16[512,4096]{1,0:T(8,128)(2,1)} %get-tuple-element.270.in_ref, bf16[4096,1024]{1,0:T(8,128)(2,1)} %assemble.5, pred[512]{0:T(512)(128)(4,1)S(1)} %copy-done.68), kind=kOutput, calls=%fused_computation.35 | convolution fusion | flops 4296540160 | bytes 15729152 | tf_op jit(solution)/shard_map/dot_general | solution.py:719
  451.1 7.2 %collective-permute-done.53 = bf16[1,4,32,3072]{3,2,1,0:T(8,128)(2,1)S(1)} collective-permute-done((bf16[1,4,32,3072]{3,2,1,0:T(8,128)(2,1)S(1)}, bf16[1,4,32,3072]{3,2,1,0:T(8,128)(2,1)S(1)}, u32[]{:S(2)}, u32[]{:S(2)}) %collective-permute-start.53) | collective-permute-done | bytes 786464 | tf_op jit(solution)/shard_map/ppermute | solution.py:324
  461.9 5.1 collective-permute-start.69
  470.8 14.6 %collective-permute-done.68 = bf16[32,3072]{1,0:T(8,128)(2,1)S(1)} collective-permute-done((bf16[32,3072]{1,0:T(8,128)(2,1)S(1)}, bf16[32,3072]{1,0:T(8,128)(2,1)S(1)}, u32[]{:S(2)}, u32[]{:S(2)}) %collective-permute-start.68) | collective-permute-done | bytes 196640 | tf_op jit(solution)/shard_map/ppermute | solution.py:298
  489.8 4.0 collective-permute-done.72
  493.8 4.6 collective-permute-done.71
  504.8 3.9 collective-permute-done.65
  510.7 3.8 finish.7
  517.6 3.8 finish.6
  521.4 3.3 finish.4
  (408 shorter events, 145.5 us)
Async XLA Ops:
  5.8 15.2 %collective-permute-start = (bf16[32,3584]{1,0:T(8,128)(2,1)S(1)}, bf16[32,3584]{1,0:T(8,128)(2,1)S(1)}, u32[]{:S(2)}, u32[]{:S(2)}) collective-permute-start(bf16[32,3584]{1,0:T(8,128)(2,1)S(1)} %pad_maximum_fusion.5), channel_id=1, source_target_pairs={{0,1},{1,2},{2,3},{3,0},{4,5},{5,6},{6,7},{7,4},{8,9},{9,10},{10,1... | collective-permute-start | bytes 688136 | tf_op jit(solution)/shard_map/ppermute | solution.py:298
  8.9 17.6 %collective-permute-start.1 = (bf16[32,3584]{1,0:T(8,128)(2,1)S(1)}, bf16[32,3584]{1,0:T(8,128)(2,1)S(1)}, u32[]{:S(2)}, u32[]{:S(2)}) collective-permute-start(bf16[32,3584]{1,0:T(8,128)(2,1)S(1)} %pad_maximum_fusion.5), channel_id=1, source_target_pairs={{0,2},{1,3},{2,0},{3,1},{4,6},{5,7},{6,4},{7,5},{8,10},{9,11},{10,... | collective-permute-start | bytes 688136 | tf_op jit(solution)/shard_map/ppermute | solution.py:298
  11.5 15.0 %collective-permute-start.2 = (bf16[32,3584]{1,0:T(8,128)(2,1)S(1)}, bf16[32,3584]{1,0:T(8,128)(2,1)S(1)}, u32[]{:S(2)}, u32[]{:S(2)}) collective-permute-start(bf16[32,3584]{1,0:T(8,128)(2,1)S(1)} %pad_maximum_fusion.5), channel_id=1, source_target_pairs={{0,3},{1,0},{2,1},{3,2},{4,7},{5,4},{6,5},{7,6},{8,11},{9,8},{10,9... | collective-permute-start | bytes 688136 | tf_op jit(solution)/shard_map/ppermute | solution.py:298
  27.4 31.7 %collective-permute-start.3 = (bf16[1,3,32,3072]{3,2,1,0:T(8,128)(2,1)}, bf16[1,3,32,3072]{3,2,1,0:T(8,128)(2,1)}, u32[]{:S(2)}, u32[]{:S(2)}) collective-permute-start(bf16[1,3,32,3072]{3,2,1,0:T(8,128)(2,1)} %maximum_bitcast_fusion.2.refs_1_), channel_id=1, source_target_pairs={{0,16},{4,12},{8,24},{12,4},{16,0},{20,28},{24,8},{28,20},{1,17},{... | collective-permute-start | bytes 1769480 | tf_op jit(solution)/shard_map/ppermute | solution.py:468
  29.0 28.7 %collective-permute-start.4 = (bf16[1,3,32,3072]{3,2,1,0:T(8,128)(2,1)}, bf16[1,3,32,3072]{3,2,1,0:T(8,128)(2,1)}, u32[]{:S(2)}, u32[]{:S(2)}) collective-permute-start(bf16[1,3,32,3072]{3,2,1,0:T(8,128)(2,1)} %maximum_bitcast_fusion.2.refs_1_), channel_id=1, source_target_pairs={{0,8},{4,20},{8,0},{12,28},{16,24},{20,4},{24,16},{28,12},{1,9},{5... | collective-permute-start | bytes 1769480 | tf_op jit(solution)/shard_map/ppermute | solution.py:468
  30.5 15.4 %collective-permute-start.5 = (bf16[32,5120]{1,0:T(8,128)(2,1)}, bf16[32,5120]{1,0:T(8,128)(2,1)}, u32[]{:S(2)}, u32[]{:S(2)}) collective-permute-start(bf16[32,5120]{1,0:T(8,128)(2,1)} %pad_maximum_fusion.3), channel_id=1, source_target_pairs={{0,1},{1,2},{2,3},{3,0},{4,5},{5,6},{6,7},{7,4},{8,9},{9,10},{10,1... | collective-permute-start | bytes 983048 | tf_op jit(solution)/shard_map/ppermute | solution.py:298
  35.8 21.8 %collective-permute-start.6 = (bf16[32,5120]{1,0:T(8,128)(2,1)}, bf16[32,5120]{1,0:T(8,128)(2,1)}, u32[]{:S(2)}, u32[]{:S(2)}) collective-permute-start(bf16[32,5120]{1,0:T(8,128)(2,1)} %pad_maximum_fusion.3), channel_id=1, source_target_pairs={{0,2},{1,3},{2,0},{3,1},{4,6},{5,7},{6,4},{7,5},{8,10},{9,11},{10,... | collective-permute-start | bytes 983048 | tf_op jit(solution)/shard_map/ppermute | solution.py:298
  37.4 20.2 %collective-permute-start.7 = (bf16[32,5120]{1,0:T(8,128)(2,1)}, bf16[32,5120]{1,0:T(8,128)(2,1)}, u32[]{:S(2)}, u32[]{:S(2)}) collective-permute-start(bf16[32,5120]{1,0:T(8,128)(2,1)} %pad_maximum_fusion.3), channel_id=1, source_target_pairs={{0,3},{1,0},{2,1},{3,2},{4,7},{5,4},{6,5},{7,6},{8,11},{9,8},{10,9... | collective-permute-start | bytes 983048 | tf_op jit(solution)/shard_map/ppermute | solution.py:298
  45.9 24.3 %collective-permute-start.9 = (bf16[1,3,32,3072]{3,2,1,0:T(8,128)(2,1)}, bf16[1,3,32,3072]{3,2,1,0:T(8,128)(2,1)S(1)}, u32[]{:S(2)}, u32[]{:S(2)}) collective-permute-start(bf16[1,3,32,3072]{3,2,1,0:T(8,128)(2,1)} %maximum_bitcast_fusion.2.refs_1_), channel_id=1, source_target_pairs={{0,4},{4,0},{8,12},{12,8},{16,20},{20,16},{24,28},{28,24},{1,5},{5... | collective-permute-start | bytes 1769480 | tf_op jit(solution)/shard_map/ppermute | solution.py:294
  57.7 10.1 %collective-permute-start.8 = (bf16[1,3,32,3072]{3,2,1,0:T(8,128)(2,1)}, bf16[1,3,32,3072]{3,2,1,0:T(8,128)(2,1)S(1)}, u32[]{:S(2)}, u32[]{:S(2)}) collective-permute-start(bf16[1,3,32,3072]{3,2,1,0:T(8,128)(2,1)} %collective-permute-done.4.refs_2_), channel_id=1, source_target_pairs={{0,16},{4,12},{8,24},{12,4},{16,0},{20,28},{24,8},{28,20},{1,17},{... | collective-permute-start | bytes 1769480 | tf_op jit(solution)/shard_map/ppermute | solution.py:468
  58.8 11.9 %collective-permute-start.10 = (bf16[1,3,32,3072]{3,2,1,0:T(8,128)(2,1)}, bf16[1,3,32,3072]{3,2,1,0:T(8,128)(2,1)S(1)}, u32[]{:S(2)}, u32[]{:S(2)}) collective-permute-start(bf16[1,3,32,3072]{3,2,1,0:T(8,128)(2,1)} %collective-permute-done.4.refs_2_), channel_id=1, source_target_pairs={{0,4},{4,0},{8,12},{12,8},{16,20},{20,16},{24,28},{28,24},{1,5},{5... | collective-permute-start | bytes 1769480 | tf_op jit(solution)/shard_map/ppermute | solution.py:294
  69.6 34.3 %collective-permute-start.16 = (bf16[1,3,32,5120]{3,2,1,0:T(8,128)(2,1)S(1)}, bf16[1,3,32,5120]{3,2,1,0:T(8,128)(2,1)}, u32[]{:S(2)}, u32[]{:S(2)}) collective-permute-start(bf16[1,3,32,5120]{3,2,1,0:T(8,128)(2,1)S(1)} %maximum_bitcast_fusion.refs_2_), channel_id=1, source_target_pairs={{0,8},{4,20},{8,0},{12,28},{16,24},{20,4},{24,16},{28,12},{1,9},{5... | collective-permute-start | bytes 2949128 | tf_op jit(solution)/shard_map/ppermute | solution.py:305
  70.2 33.7 %collective-permute-start.17 = (bf16[1,3,32,5120]{3,2,1,0:T(8,128)(2,1)S(1)}, bf16[1,3,32,5120]{3,2,1,0:T(8,128)(2,1)}, u32[]{:S(2)}, u32[]{:S(2)}) collective-permute-start(bf16[1,3,32,5120]{3,2,1,0:T(8,128)(2,1)S(1)} %maximum_bitcast_fusion.refs_2_), channel_id=1, source_target_pairs={{0,16},{4,12},{8,24},{12,4},{16,0},{20,28},{24,8},{28,20},{1,17},{... | collective-permute-start | bytes 2949128 | tf_op jit(solution)/shard_map/ppermute | solution.py:305
  70.7 44.4 %collective-permute-start.18 = (bf16[1,3,32,5120]{3,2,1,0:T(8,128)(2,1)S(1)}, bf16[1,3,32,5120]{3,2,1,0:T(8,128)(2,1)}, u32[]{:S(2)}, u32[]{:S(2)}) collective-permute-start(bf16[1,3,32,5120]{3,2,1,0:T(8,128)(2,1)S(1)} %maximum_bitcast_fusion.refs_2_), channel_id=1, source_target_pairs={{0,24},{4,28},{8,16},{12,20},{16,8},{20,12},{24,0},{28,4},{1,25},{... | collective-permute-start | bytes 2949128 | tf_op jit(solution)/shard_map/ppermute | solution.py:305
  73.2 50.1 %collective-permute-start.19 = (bf16[1,3,32,5120]{3,2,1,0:T(8,128)(2,1)S(1)}, bf16[1,3,32,5120]{3,2,1,0:T(8,128)(2,1)}, u32[]{:S(2)}, u32[]{:S(2)}) collective-permute-start(bf16[1,3,32,5120]{3,2,1,0:T(8,128)(2,1)S(1)} %maximum_bitcast_fusion.refs_2_), channel_id=1, source_target_pairs={{0,4},{4,0},{8,12},{12,8},{16,20},{20,16},{24,28},{28,24},{1,5},{5... | collective-permute-start | bytes 2949128 | tf_op jit(solution)/shard_map/ppermute | solution.py:294
  115.1 10.5 %collective-permute-start.20 = (bf16[1,3,32,5120]{3,2,1,0:T(8,128)(2,1)}, bf16[1,3,32,5120]{3,2,1,0:T(8,128)(2,1)}, u32[]{:S(2)}, u32[]{:S(2)}) collective-permute-start(bf16[1,3,32,5120]{3,2,1,0:T(8,128)(2,1)} %collective-permute-done.16.refs_3_), channel_id=1, source_target_pairs={{0,4},{4,0},{8,12},{12,8},{16,20},{20,16},{24,28},{28,24},{1,5},{5... | collective-permute-start | bytes 2949128 | tf_op jit(solution)/shard_map/ppermute | solution.py:294
  115.2 13.8 %collective-permute-start.21 = (bf16[1,3,32,5120]{3,2,1,0:T(8,128)(2,1)}, bf16[1,3,32,5120]{3,2,1,0:T(8,128)(2,1)}, u32[]{:S(2)}, u32[]{:S(2)}) collective-permute-start(bf16[1,3,32,5120]{3,2,1,0:T(8,128)(2,1)} %collective-permute-done.17.refs_4_), channel_id=1, source_target_pairs={{0,4},{4,0},{8,12},{12,8},{16,20},{20,16},{24,28},{28,24},{1,5},{5... | collective-permute-start | bytes 2949128 | tf_op jit(solution)/shard_map/ppermute | solution.py:294
  115.6 13.5 %collective-permute-start.22 = (bf16[1,3,32,5120]{3,2,1,0:T(8,128)(2,1)}, bf16[1,3,32,5120]{3,2,1,0:T(8,128)(2,1)}, u32[]{:S(2)}, u32[]{:S(2)}) collective-permute-start(bf16[1,3,32,5120]{3,2,1,0:T(8,128)(2,1)} %collective-permute-done.18.refs_5_), channel_id=1, source_target_pairs={{0,4},{4,0},{8,12},{12,8},{16,20},{20,16},{24,28},{28,24},{1,5},{5... | collective-permute-start | bytes 2949128 | tf_op jit(solution)/shard_map/ppermute | solution.py:294
  115.8 22.5 %collective-permute-start.13 = (bf16[128,1024]{1,0:T(8,128)(2,1)S(1)}, bf16[128,1024]{1,0:T(8,128)(2,1)}, u32[]{:S(2)}, u32[]{:S(2)}) collective-permute-start(bf16[128,1024]{1,0:T(8,128)(2,1)S(1)} %copy-done.44), channel_id=1, source_target_pairs={{0,1},{1,2},{2,3},{3,0},{4,5},{5,6},{6,7},{7,4},{8,9},{9,10},{10,1... | collective-permute-start | bytes 786440 | tf_op jit(solution)/shard_map/ppermute | solution.py:298
  123.3 20.1 %collective-permute-start.14 = (bf16[128,1024]{1,0:T(8,128)(2,1)S(1)}, bf16[128,1024]{1,0:T(8,128)(2,1)}, u32[]{:S(2)}, u32[]{:S(2)}) collective-permute-start(bf16[128,1024]{1,0:T(8,128)(2,1)S(1)} %copy-done.44), channel_id=1, source_target_pairs={{0,2},{1,3},{2,0},{3,1},{4,6},{5,7},{6,4},{7,5},{8,10},{9,11},{10,... | collective-permute-start | bytes 786440 | tf_op jit(solution)/shard_map/ppermute | solution.py:298
  125.6 17.8 %collective-permute-start.15 = (bf16[128,1024]{1,0:T(8,128)(2,1)S(1)}, bf16[128,1024]{1,0:T(8,128)(2,1)}, u32[]{:S(2)}, u32[]{:S(2)}) collective-permute-start(bf16[128,1024]{1,0:T(8,128)(2,1)S(1)} %copy-done.44), channel_id=1, source_target_pairs={{0,3},{1,0},{2,1},{3,2},{4,7},{5,4},{6,5},{7,6},{8,11},{9,8},{10,9... | collective-permute-start | bytes 786440 | tf_op jit(solution)/shard_map/ppermute | solution.py:298
  145.6 30.3 %collective-permute-start.24 = (bf16[1,3,128,1024]{3,2,1,0:T(8,128)(2,1)}, bf16[1,3,128,1024]{3,2,1,0:T(8,128)(2,1)}, u32[]{:S(2)}, u32[]{:S(2)}) collective-permute-start(bf16[1,3,128,1024]{3,2,1,0:T(8,128)(2,1)} %maximum_bitcast_fusion.1.refs_1_), channel_id=1, source_target_pairs={{0,16},{4,12},{8,24},{12,4},{16,0},{20,28},{24,8},{28,20},{1,17},{... | collective-permute-start | bytes 2359304 | tf_op jit(solution)/shard_map/ppermute | solution.py:468
  146.7 18.7 %collective-permute-start.23 = (bf16[1,3,128,1024]{3,2,1,0:T(8,128)(2,1)}, bf16[1,3,128,1024]{3,2,1,0:T(8,128)(2,1)}, u32[]{:S(2)}, u32[]{:S(2)}) collective-permute-start(bf16[1,3,128,1024]{3,2,1,0:T(8,128)(2,1)} %maximum_bitcast_fusion.1.refs_1_), channel_id=1, source_target_pairs={{0,8},{4,20},{8,0},{12,28},{16,24},{20,4},{24,16},{28,12},{1,9},{5... | collective-permute-start | bytes 2359304 | tf_op jit(solution)/shard_map/ppermute | solution.py:468
  165.3 12.3 %collective-permute-start.25 = (bf16[1,3,128,1024]{3,2,1,0:T(8,128)(2,1)}, bf16[1,3,128,1024]{3,2,1,0:T(8,128)(2,1)}, u32[]{:S(2)}, u32[]{:S(2)}) collective-permute-start(bf16[1,3,128,1024]{3,2,1,0:T(8,128)(2,1)} %collective-permute-done.23.refs_2_), channel_id=1, source_target_pairs={{0,16},{4,12},{8,24},{12,4},{16,0},{20,28},{24,8},{28,20},{1,17},{... | collective-permute-start | bytes 2359304 | tf_op jit(solution)/shard_map/ppermute | solution.py:468
  189.1 19.6 %collective-permute-start.30 = (bf16[4,4,128,1024]{3,2,1,0:T(8,128)(2,1)}, bf16[4,4,128,1024]{3,2,1,0:T(8,128)(2,1)}, u32[]{:S(2)}, u32[]{:S(2)}) collective-permute-start(bf16[4,4,128,1024]{3,2,1,0:T(8,128)(2,1)} %bitcast.24), channel_id=1, source_target_pairs={{0,4},{4,0},{8,12},{12,8},{16,20},{20,16},{24,28},{28,24},{1,5},{5... | collective-permute-start | bytes 12582920 | tf_op jit(solution)/shard_map/ppermute | solution.py:294
  189.1 9.3 %collective-permute-start.26 = (bf16[1,3,128,1024]{3,2,1,0:T(8,128)(2,1)}, bf16[1,3,128,1024]{3,2,1,0:T(8,128)(2,1)}, u32[]{:S(2)}, u32[]{:S(2)}) collective-permute-start(bf16[1,3,128,1024]{3,2,1,0:T(8,128)(2,1)} %maximum_bitcast_fusion.1.refs_1_), channel_id=1, source_target_pairs={{0,4},{4,0},{8,12},{12,8},{16,20},{20,16},{24,28},{28,24},{1,5},{5... | collective-permute-start | bytes 2359304 | tf_op jit(solution)/shard_map/ppermute | solution.py:294
  189.6 9.2 %collective-permute-start.27 = (bf16[1,3,128,1024]{3,2,1,0:T(8,128)(2,1)}, bf16[1,3,128,1024]{3,2,1,0:T(8,128)(2,1)}, u32[]{:S(2)}, u32[]{:S(2)}) collective-permute-start(bf16[1,3,128,1024]{3,2,1,0:T(8,128)(2,1)} %collective-permute-done.23.refs_2_), channel_id=1, source_target_pairs={{0,4},{4,0},{8,12},{12,8},{16,20},{20,16},{24,28},{28,24},{1,5},{5... | collective-permute-start | bytes 2359304 | tf_op jit(solution)/shard_map/ppermute | solution.py:294
  189.7 10.3 %collective-permute-start.28 = (bf16[1,3,128,1024]{3,2,1,0:T(8,128)(2,1)}, bf16[1,3,128,1024]{3,2,1,0:T(8,128)(2,1)}, u32[]{:S(2)}, u32[]{:S(2)}) collective-permute-start(bf16[1,3,128,1024]{3,2,1,0:T(8,128)(2,1)} %collective-permute-done.24.refs_3_), channel_id=1, source_target_pairs={{0,4},{4,0},{8,12},{12,8},{16,20},{20,16},{24,28},{28,24},{1,5},{5... | collective-permute-start | bytes 2359304 | tf_op jit(solution)/shard_map/ppermute | solution.py:294
  190.2 11.0 %collective-permute-start.29 = (bf16[1,3,128,1024]{3,2,1,0:T(8,128)(2,1)}, bf16[1,3,128,1024]{3,2,1,0:T(8,128)(2,1)}, u32[]{:S(2)}, u32[]{:S(2)}) collective-permute-start(bf16[1,3,128,1024]{3,2,1,0:T(8,128)(2,1)} %collective-permute-done.25.refs_4_), channel_id=1, source_target_pairs={{0,4},{4,0},{8,12},{12,8},{16,20},{20,16},{24,28},{28,24},{1,5},{5... | collective-permute-start | bytes 2359304 | tf_op jit(solution)/shard_map/ppermute | solution.py:294
  226.2 21.6 %collective-permute-start.31 = (bf16[4,4,32,4096]{3,2,1,0:T(8,128)(2,1)S(1)}, bf16[4,4,32,4096]{3,2,1,0:T(8,128)(2,1)S(1)}, u32[]{:S(2)}, u32[]{:S(2)}) collective-permute-start(bf16[4,4,32,4096]{3,2,1,0:T(8,128)(2,1)S(1)} %bitcast.199), channel_id=1, source_target_pairs={{0,4},{4,0},{8,12},{12,8},{16,20},{20,16},{24,28},{28,24},{1,5},{5... | collective-permute-start | bytes 12582920 | tf_op jit(solution)/shard_map/ppermute | solution.py:294
  231.9 26.4 %collective-permute-start.32 = (bf16[2,4,128,1024]{3,2,1,0:T(8,128)(2,1)}, bf16[2,4,128,1024]{3,2,1,0:T(8,128)(2,1)}, u32[]{:S(2)}, u32[]{:S(2)}) collective-permute-start(bf16[2,4,128,1024]{3,2,1,0:T(8,128)(2,1)} %add_convert_fusion.1), channel_id=1, source_target_pairs={{0,8},{4,20},{8,0},{12,28},{16,24},{20,4},{24,16},{28,12},{1,9},{5... | collective-permute-start | bytes 6291464 | tf_op jit(solution)/shard_map/ppermute | solution.py:324
  258.3 52.5 %collective-permute-start.35 = (bf16[2,4,32,4096]{3,2,1,0:T(8,128)(2,1)}, bf16[2,4,32,4096]{3,2,1,0:T(8,128)(2,1)}, u32[]{:S(2)}, u32[]{:S(2)}) collective-permute-start(bf16[2,4,32,4096]{3,2,1,0:T(8,128)(2,1)} %add_convert_fusion), channel_id=1, source_target_pairs={{0,8},{4,20},{8,0},{12,28},{16,24},{20,4},{24,16},{28,12},{1,9},{5... | collective-permute-start | bytes 6291464 | tf_op jit(solution)/shard_map/ppermute | solution.py:324
  263.8 17.4 %collective-permute-start.33 = (bf16[4,4,32,1024]{3,2,1,0:T(8,128)(2,1)}, bf16[4,4,32,1024]{3,2,1,0:T(8,128)(2,1)}, u32[]{:S(2)}, u32[]{:S(2)}) collective-permute-start(bf16[4,4,32,1024]{3,2,1,0:T(8,128)(2,1)} %bitcast.29), channel_id=1, source_target_pairs={{0,4},{4,0},{8,12},{12,8},{16,20},{20,16},{24,28},{28,24},{1,5},{5... | collective-permute-start | bytes 3145736 | tf_op jit(solution)/shard_map/ppermute | solution.py:294
  269.4 41.4 %collective-permute-start.34 = (bf16[1,4,128,1024]{3,2,1,0:T(8,128)(2,1)}, bf16[1,4,128,1024]{3,2,1,0:T(8,128)(2,1)}, u32[]{:S(2)}, u32[]{:S(2)}) collective-permute-start(bf16[1,4,128,1024]{3,2,1,0:T(8,128)(2,1)} %add_convert_fusion.4), channel_id=1, source_target_pairs={{0,16},{4,12},{8,24},{12,4},{16,0},{20,28},{24,8},{28,20},{1,17},{... | collective-permute-start | bytes 3145736 | tf_op jit(solution)/shard_map/ppermute | solution.py:324
  283.2 27.6 %collective-permute-start.36 = (bf16[2,4,32,1024]{3,2,1,0:T(8,128)(2,1)}, bf16[2,4,32,1024]{3,2,1,0:T(8,128)(2,1)}, u32[]{:S(2)}, u32[]{:S(2)}) collective-permute-start(bf16[2,4,32,1024]{3,2,1,0:T(8,128)(2,1)} %add_convert_fusion.8), channel_id=1, source_target_pairs={{0,8},{4,20},{8,0},{12,28},{16,24},{20,4},{24,16},{28,12},{1,9},{5... | collective-permute-start | bytes 1572872 | tf_op jit(solution)/shard_map/ppermute | solution.py:324
  320.0 30.5 %collective-permute-start.40 = (bf16[1,4,32,4096]{3,2,1,0:T(8,128)(2,1)}, bf16[1,4,32,4096]{3,2,1,0:T(8,128)(2,1)}, u32[]{:S(2)}, u32[]{:S(2)}) collective-permute-start(bf16[1,4,32,4096]{3,2,1,0:T(8,128)(2,1)} %add_convert_fusion.3), channel_id=1, source_target_pairs={{0,16},{4,12},{8,24},{12,4},{16,0},{20,28},{24,8},{28,20},{1,17},{... | collective-permute-start | bytes 3145736 | tf_op jit(solution)/shard_map/ppermute | solution.py:324
  327.0 21.9 %collective-permute-start.37 = (bf16[128,1024]{1,0:T(8,128)(2,1)}, bf16[128,1024]{1,0:T(8,128)(2,1)S(1)}, u32[]{:S(2)}, u32[]{:S(2)}) collective-permute-start(bf16[128,1024]{1,0:T(8,128)(2,1)} %get-tuple-element.229), channel_id=1, source_target_pairs={{0,1},{1,2},{2,3},{3,0},{4,5},{5,6},{6,7},{7,4},{8,9},{9,10},{10,1... | collective-permute-start | bytes 786440 | tf_op jit(solution)/shard_map/ppermute | solution.py:298
  333.3 17.2 %collective-permute-start.38 = (bf16[128,1024]{1,0:T(8,128)(2,1)}, bf16[128,1024]{1,0:T(8,128)(2,1)}, u32[]{:S(2)}, u32[]{:S(2)}) collective-permute-start(bf16[128,1024]{1,0:T(8,128)(2,1)} %get-tuple-element.230), channel_id=1, source_target_pairs={{0,2},{1,3},{2,0},{3,1},{4,6},{5,7},{6,4},{7,5},{8,10},{9,11},{10,... | collective-permute-start | bytes 786440 | tf_op jit(solution)/shard_map/ppermute | solution.py:298
  333.6 16.9 %collective-permute-start.39 = (bf16[128,1024]{1,0:T(8,128)(2,1)}, bf16[128,1024]{1,0:T(8,128)(2,1)}, u32[]{:S(2)}, u32[]{:S(2)}) collective-permute-start(bf16[128,1024]{1,0:T(8,128)(2,1)} %get-tuple-element.231), channel_id=1, source_target_pairs={{0,3},{1,0},{2,1},{3,2},{4,7},{5,4},{6,5},{7,6},{8,11},{9,8},{10,9... | collective-permute-start | bytes 786440 | tf_op jit(solution)/shard_map/ppermute | solution.py:298
  335.7 14.8 %collective-permute-start.41 = (bf16[1,4,32,1024]{3,2,1,0:T(8,128)(2,1)}, bf16[1,4,32,1024]{3,2,1,0:T(8,128)(2,1)}, u32[]{:S(2)}, u32[]{:S(2)}) collective-permute-start(bf16[1,4,32,1024]{3,2,1,0:T(8,128)(2,1)} %add_convert_fusion.11), channel_id=1, source_target_pairs={{0,16},{4,12},{8,24},{12,4},{16,0},{20,28},{24,8},{28,20},{1,17},{... | collective-permute-start | bytes 786440 | tf_op jit(solution)/shard_map/ppermute | solution.py:324
  363.7 24.0 %collective-permute-start.42 = (bf16[4,4,32,3072]{3,2,1,0:T(8,128)(2,1)}, bf16[4,4,32,3072]{3,2,1,0:T(8,128)(2,1)}, u32[]{:S(2)}, u32[]{:S(2)}) collective-permute-start(bf16[4,4,32,3072]{3,2,1,0:T(8,128)(2,1)} %bitcast.58), channel_id=1, source_target_pairs={{0,4},{4,0},{8,12},{12,8},{16,20},{20,16},{24,28},{28,24},{1,5},{5... | collective-permute-start | bytes 9437192 | tf_op jit(solution)/shard_map/ppermute | solution.py:294
  366.3 36.2 %collective-permute-start.44 = (bf16[1,128,1024]{2,1,0:T(8,128)(2,1)}, bf16[1,128,1024]{2,1,0:T(8,128)(2,1)}, u32[]{:S(2)}, u32[]{:S(2)}) collective-permute-start(bf16[1,128,1024]{2,1,0:T(8,128)(2,1)} %fusion.37), channel_id=1, source_target_pairs={{0,8},{4,20},{8,0},{12,28},{16,24},{20,4},{24,16},{28,12},{1,9},{5... | collective-permute-start | bytes 786440 | tf_op jit(solution)/shard_map/ppermute | solution.py:305
  367.8 36.8 %collective-permute-start.45 = (bf16[1,128,1024]{2,1,0:T(8,128)(2,1)}, bf16[1,128,1024]{2,1,0:T(8,128)(2,1)}, u32[]{:S(2)}, u32[]{:S(2)}) collective-permute-start(bf16[1,128,1024]{2,1,0:T(8,128)(2,1)} %fusion.37), channel_id=1, source_target_pairs={{0,16},{4,12},{8,24},{12,4},{16,0},{20,28},{24,8},{28,20},{1,17},{... | collective-permute-start | bytes 786440 | tf_op jit(solution)/shard_map/ppermute | solution.py:305
  368.7 29.0 %collective-permute-start.50 = (bf16[32,1024]{1,0:T(8,128)(2,1)}, bf16[32,1024]{1,0:T(8,128)(2,1)}, u32[]{:S(2)}, u32[]{:S(2)}) collective-permute-start(bf16[32,1024]{1,0:T(8,128)(2,1)} %get-tuple-element.253), channel_id=1, source_target_pairs={{0,1},{1,2},{2,3},{3,0},{4,5},{5,6},{6,7},{7,4},{8,9},{9,10},{10,1... | collective-permute-start | bytes 196616 | tf_op jit(solution)/shard_map/ppermute | solution.py:298
  374.9 23.6 %collective-permute-start.51 = (bf16[32,1024]{1,0:T(8,128)(2,1)}, bf16[32,1024]{1,0:T(8,128)(2,1)}, u32[]{:S(2)}, u32[]{:S(2)}) collective-permute-start(bf16[32,1024]{1,0:T(8,128)(2,1)} %get-tuple-element.254), channel_id=1, source_target_pairs={{0,2},{1,3},{2,0},{3,1},{4,6},{5,7},{6,4},{7,5},{8,10},{9,11},{10,... | collective-permute-start | bytes 196616 | tf_op jit(solution)/shard_map/ppermute | solution.py:298
  391.8 30.8 %collective-permute-start.43 = (bf16[2,4,32,3072]{3,2,1,0:T(8,128)(2,1)}, bf16[2,4,32,3072]{3,2,1,0:T(8,128)(2,1)}, u32[]{:S(2)}, u32[]{:S(2)}) collective-permute-start(bf16[2,4,32,3072]{3,2,1,0:T(8,128)(2,1)} %add_convert_fusion.2), channel_id=1, source_target_pairs={{0,8},{4,20},{8,0},{12,28},{16,24},{20,4},{24,16},{28,12},{1,9},{5... | collective-permute-start | bytes 4718600 | tf_op jit(solution)/shard_map/ppermute | solution.py:324
  398.6 20.0 %collective-permute-start.46 = (bf16[1,128,1024]{2,1,0:T(8,128)(2,1)}, bf16[1,128,1024]{2,1,0:T(8,128)(2,1)S(1)}, u32[]{:S(2)}, u32[]{:S(2)}) collective-permute-start(bf16[1,128,1024]{2,1,0:T(8,128)(2,1)} %fusion.37), channel_id=1, source_target_pairs={{0,24},{4,28},{8,16},{12,20},{16,8},{20,12},{24,0},{28,4},{1,25},{... | collective-permute-start | bytes 786440 | tf_op jit(solution)/shard_map/ppermute | solution.py:305
  402.2 16.4 %collective-permute-start.47 = (bf16[32,4096]{1,0:T(8,128)(2,1)}, bf16[32,4096]{1,0:T(8,128)(2,1)S(1)}, u32[]{:S(2)}, u32[]{:S(2)}) collective-permute-start(bf16[32,4096]{1,0:T(8,128)(2,1)} %get-tuple-element.250), channel_id=1, source_target_pairs={{0,1},{1,2},{2,3},{3,0},{4,5},{5,6},{6,7},{7,4},{8,9},{9,10},{10,1... | collective-permute-start | bytes 786440 | tf_op jit(solution)/shard_map/ppermute | solution.py:298
  402.5 20.1 %collective-permute-start.48 = (bf16[32,4096]{1,0:T(8,128)(2,1)}, bf16[32,4096]{1,0:T(8,128)(2,1)S(1)}, u32[]{:S(2)}, u32[]{:S(2)}) collective-permute-start(bf16[32,4096]{1,0:T(8,128)(2,1)} %get-tuple-element.251), channel_id=1, source_target_pairs={{0,2},{1,3},{2,0},{3,1},{4,6},{5,7},{6,4},{7,5},{8,10},{9,11},{10,... | collective-permute-start | bytes 786440 | tf_op jit(solution)/shard_map/ppermute | solution.py:298
  404.6 18.1 %collective-permute-start.49 = (bf16[32,4096]{1,0:T(8,128)(2,1)}, bf16[32,4096]{1,0:T(8,128)(2,1)S(1)}, u32[]{:S(2)}, u32[]{:S(2)}) collective-permute-start(bf16[32,4096]{1,0:T(8,128)(2,1)} %get-tuple-element.252), channel_id=1, source_target_pairs={{0,3},{1,0},{2,1},{3,2},{4,7},{5,4},{6,5},{7,6},{8,11},{9,8},{10,9... | collective-permute-start | bytes 786440 | tf_op jit(solution)/shard_map/ppermute | solution.py:298
  435.6 14.9 %collective-permute-start.55 = (bf16[1,32,4096]{2,1,0:T(8,128)(2,1)S(1)}, bf16[1,32,4096]{2,1,0:T(8,128)(2,1)S(1)}, u32[]{:S(2)}, u32[]{:S(2)}) collective-permute-start(bf16[1,32,4096]{2,1,0:T(8,128)(2,1)S(1)} %copy-done.35), channel_id=1, source_target_pairs={{0,8},{4,20},{8,0},{12,28},{16,24},{20,4},{24,16},{28,12},{1,9},{5... | collective-permute-start | bytes 786440 | tf_op jit(solution)/shard_map/ppermute | solution.py:305
  436.2 14.9 %collective-permute-start.56 = (bf16[1,32,4096]{2,1,0:T(8,128)(2,1)S(1)}, bf16[1,32,4096]{2,1,0:T(8,128)(2,1)S(1)}, u32[]{:S(2)}, u32[]{:S(2)}) collective-permute-start(bf16[1,32,4096]{2,1,0:T(8,128)(2,1)S(1)} %copy-done.35), channel_id=1, source_target_pairs={{0,16},{4,12},{8,24},{12,4},{16,0},{20,28},{24,8},{28,20},{1,17},{... | collective-permute-start | bytes 786440 | tf_op jit(solution)/shard_map/ppermute | solution.py:305
  437.2 13.9 %collective-permute-start.57 = (bf16[1,32,4096]{2,1,0:T(8,128)(2,1)S(1)}, bf16[1,32,4096]{2,1,0:T(8,128)(2,1)S(1)}, u32[]{:S(2)}, u32[]{:S(2)}) collective-permute-start(bf16[1,32,4096]{2,1,0:T(8,128)(2,1)S(1)} %copy-done.35), channel_id=1, source_target_pairs={{0,24},{4,28},{8,16},{12,20},{16,8},{20,12},{24,0},{28,4},{1,25},{... | collective-permute-start | bytes 786440 | tf_op jit(solution)/shard_map/ppermute | solution.py:305
  439.2 19.1 %collective-permute-start.53 = (bf16[1,4,32,3072]{3,2,1,0:T(8,128)(2,1)S(1)}, bf16[1,4,32,3072]{3,2,1,0:T(8,128)(2,1)S(1)}, u32[]{:S(2)}, u32[]{:S(2)}) collective-permute-start(bf16[1,4,32,3072]{3,2,1,0:T(8,128)(2,1)S(1)} %copy-done.37), channel_id=1, source_target_pairs={{0,16},{4,12},{8,24},{12,4},{16,0},{20,28},{24,8},{28,20},{1,17},{... | collective-permute-start | bytes 2359304 | tf_op jit(solution)/shard_map/ppermute | solution.py:324
  440.2 18.1 %collective-permute-start.54 = (bf16[4,128,1024]{2,1,0:T(8,128)(2,1)S(1)}, bf16[4,128,1024]{2,1,0:T(8,128)(2,1)S(1)}, u32[]{:S(2)}, u32[]{:S(2)}) collective-permute-start(bf16[4,128,1024]{2,1,0:T(8,128)(2,1)S(1)} %copy-done.10), channel_id=1, source_target_pairs={{0,4},{4,0},{8,12},{12,8},{16,20},{20,16},{24,28},{28,24},{1,5},{5... | collective-permute-start | bytes 3145736 | tf_op jit(solution)/shard_map/ppermute | solution.py:294
  450.5 18.2 %collective-permute-start.62 = (f32[4,64,256]{2,0,1:T(4,128)S(1)}, f32[4,64,256]{2,0,1:T(4,128)S(1)}, u32[]{:S(2)}, u32[]{:S(2)}) collective-permute-start(f32[4,64,256]{2,0,1:T(4,128)S(1)} %fusion.77), channel_id=1, source_target_pairs={{0,8},{4,12},{8,0},{12,4},{16,24},{20,28},{24,16},{28,20},{1,9},{5... | collective-permute-start | bytes 786440 | tf_op jit(solution)/shard_map/ppermute | solution.py:341
  461.9 9.0 %collective-permute-start.69 = (bf16[32,3072]{1,0:T(8,128)(2,1)S(1)}, bf16[32,3072]{1,0:T(8,128)(2,1)S(1)}, u32[]{:S(2)}, u32[]{:S(2)}) collective-permute-start(bf16[32,3072]{1,0:T(8,128)(2,1)S(1)} %get-tuple-element.288), channel_id=1, source_target_pairs={{0,3},{1,0},{2,1},{3,2},{4,7},{5,4},{6,5},{7,6},{8,11},{9,8},{10,9... | collective-permute-start | bytes 589832 | tf_op jit(solution)/shard_map/ppermute | solution.py:298
  467.0 18.4 %collective-permute-start.68 = (bf16[32,3072]{1,0:T(8,128)(2,1)S(1)}, bf16[32,3072]{1,0:T(8,128)(2,1)S(1)}, u32[]{:S(2)}, u32[]{:S(2)}) collective-permute-start(bf16[32,3072]{1,0:T(8,128)(2,1)S(1)} %get-tuple-element.287), channel_id=1, source_target_pairs={{0,2},{1,3},{2,0},{3,1},{4,6},{5,7},{6,4},{7,5},{8,10},{9,11},{10,... | collective-permute-start | bytes 589832 | tf_op jit(solution)/shard_map/ppermute | solution.py:298
  468.6 16.7 %collective-permute-start.67 = (bf16[32,3072]{1,0:T(8,128)(2,1)S(1)}, bf16[32,3072]{1,0:T(8,128)(2,1)S(1)}, u32[]{:S(2)}, u32[]{:S(2)}) collective-permute-start(bf16[32,3072]{1,0:T(8,128)(2,1)S(1)} %get-tuple-element.286), channel_id=1, source_target_pairs={{0,1},{1,2},{2,3},{3,0},{4,5},{5,6},{6,7},{7,4},{8,9},{9,10},{10,1... | collective-permute-start | bytes 589832 | tf_op jit(solution)/shard_map/ppermute | solution.py:298
  468.7 20.3 %collective-permute-start.63 = (f32[4,64,256]{2,0,1:T(4,128)S(1)}, f32[4,64,256]{2,0,1:T(4,128)S(1)}, u32[]{:S(2)}, u32[]{:S(2)}) collective-permute-start(f32[4,64,256]{2,0,1:T(4,128)S(1)} %add.485), channel_id=1, source_target_pairs={{0,16},{4,20},{8,24},{12,28},{16,0},{20,4},{24,8},{28,12},{1,17},{... | collective-permute-start | bytes 786440 | tf_op jit(solution)/shard_map/ppermute | solution.py:341
  486.6 11.8 %collective-permute-start.71 = (bf16[1,32,3072]{2,1,0:T(8,128)(2,1)S(1)}, bf16[1,32,3072]{2,1,0:T(8,128)(2,1)}, u32[]{:S(2)}, u32[]{:S(2)}) collective-permute-start(bf16[1,32,3072]{2,1,0:T(8,128)(2,1)S(1)} %fusion.47), channel_id=1, source_target_pairs={{0,16},{4,12},{8,24},{12,4},{16,0},{20,28},{24,8},{28,20},{1,17},{... | collective-permute-start | bytes 589832 | tf_op jit(solution)/shard_map/ppermute | solution.py:305
  487.7 10.8 %collective-permute-start.70 = (bf16[1,32,3072]{2,1,0:T(8,128)(2,1)S(1)}, bf16[1,32,3072]{2,1,0:T(8,128)(2,1)}, u32[]{:S(2)}, u32[]{:S(2)}) collective-permute-start(bf16[1,32,3072]{2,1,0:T(8,128)(2,1)S(1)} %fusion.47), channel_id=1, source_target_pairs={{0,8},{4,20},{8,0},{12,28},{16,24},{20,4},{24,16},{28,12},{1,9},{5... | collective-permute-start | bytes 589832 | tf_op jit(solution)/shard_map/ppermute | solution.py:305
  489.1 27.5 %collective-permute-start.75 = (bf16[4,32,4096]{2,1,0:T(8,128)(2,1)S(1)}, bf16[4,32,4096]{2,1,0:T(8,128)(2,1)S(1)}, u32[]{:S(2)}, u32[]{:S(2)}) collective-permute-start(bf16[4,32,4096]{2,1,0:T(8,128)(2,1)S(1)} %pad_maximum_fusion.1.refs_0_), channel_id=1, source_target_pairs={{0,4},{4,0},{8,12},{12,8},{16,20},{20,16},{24,28},{28,24},{1,5},{5... | collective-permute-start | bytes 3145736 | tf_op jit(solution)/shard_map/ppermute | solution.py:294
  499.7 21.8 %collective-permute-start.73 = (bf16[4,32,3072]{2,1,0:T(8,128)(2,1)S(1)}, bf16[4,32,3072]{2,1,0:T(8,128)(2,1)}, u32[]{:S(2)}, u32[]{:S(2)}) collective-permute-start(bf16[4,32,3072]{2,1,0:T(8,128)(2,1)S(1)} %pad_maximum_fusion.2.refs_0_), channel_id=1, source_target_pairs={{0,4},{4,0},{8,12},{12,8},{16,20},{20,16},{24,28},{28,24},{1,5},{5... | collective-permute-start | bytes 2359304 | tf_op jit(solution)/shard_map/ppermute | solution.py:294
  (86 other events, 1493.7 us)

commit v8 on v4

--- a/solution.py
+++ b/solution.py
@@ -298,6 +298,13 @@
     return lax.ppermute(block, "fsdp", [(i, (i + step) % n_line) for i in range(n_line)])
 
 
+def plane_hops(block, n_dp):
+    across = (1 << n_dp.bit_length() - 1) - 2
+    both = [(i, i ^ across) for i in range(n_dp)]
+    hops = [hop_pairs(n_dp, stage) for stage in range(n_dp.bit_length() - 2)] + [both]
+    return [lax.ppermute(block, "dp", pairs) for pairs in hops]
+
+
 def add_up(terms):
     total = terms[0].astype(jnp.float32)
     for term in terms[1:]:
@@ -320,12 +327,10 @@
         add_up([term[step] for term in terms]).astype(jnp.bfloat16) for step in range(1, n_line)
     ]
     arrived = yield [ahead(send, n_line, step + 1) for step, send in enumerate(sends)]
-    parts = [add_up([term[0] for term in terms] + arrived).astype(jnp.bfloat16)[None]]
-    for stage in range(n_dp.bit_length() - 2):
-        (send,) = yield [jnp.concatenate(parts) if len(parts) > 1 else parts[0]]
-        (got,) = yield [lax.ppermute(send, "dp", hop_pairs(n_dp, stage))]
-        parts = parts + [got]
-    (send,) = yield [jnp.concatenate(parts)]
+    total = add_up([term[0] for term in terms] + arrived)
+    (near,) = yield [total.astype(jnp.bfloat16)[None]]
+    got = yield plane_hops(near, n_dp)
+    (send,) = yield [jnp.concatenate([near] + got)]
     (got,) = yield [swap_core(send, n_dp)]
     return [send, got]
 
@@ -467,9 +472,9 @@
     def hop(self, block, stage):
         return lax.ppermute(block, "dp", hop_pairs(self.n_dp, stage))
 
-    def fan(self, gate, rows):
+    def fan(self, gate, columns):
         self.line, gate = lax.optimization_barrier((self.line, gate))
-        near = jnp.stack([item[:rows] for item in self.line])[None]
+        near = jnp.stack([item[:, :columns] for item in self.line])[None]
         near, gate = lax.optimization_barrier((near, gate))
         self.parts = [near, self.hop(near, 0), self.hop(near, 1)]
         self.cores = [swap_core(near, self.n_dp)]
@@ -519,30 +524,25 @@
         n_dp = self.n_dp
         n_line = self.n_line
         shard = smalls.shape[1]
+        size = self.unit
         wide = w_qkv.shape[1] + w_out.shape[1]
-        fold = wide // shard
-        small_rows = -(-smalls.shape[0] // (16 * fold)) * 16
-        padded = jnp.pad(smalls, ((0, small_rows * fold - smalls.shape[0]), (0, 0)))
-        packed = jnp.concatenate(
-            [padded[i * small_rows : (i + 1) * small_rows] for i in range(fold)], axis=1
-        )
-        unit_one = jnp.concatenate(
-            [jnp.concatenate([self.pick(w_qkv), self.pick(w_out)], axis=1), packed]
-        )
+        fold = -(-smalls.shape[0] // size)
+        padded = jnp.pad(smalls, ((0, size * fold - smalls.shape[0]), (0, 0)))
+        packed = [padded[i * size : (i + 1) * size] for i in range(fold)]
+        unit_one = jnp.concatenate([self.pick(w_qkv), self.pick(w_out)] + packed, axis=1)
         unit_two, unit_three = (self.pick(w_fc1), self.pick(w_fc2))
-        size = self.unit
         one = Gather(unit_one, n_dp, n_line)
-        unit_two = one.fan(unit_two, size)
-        far = jnp.stack([item[size:] for item in one.line])
+        unit_two = one.fan(unit_two, wide)
+        far = jnp.stack([item[:, wide:] for item in one.line])
         two = Gather(unit_two, n_dp, n_line)
         two.line = one.forward(two.line)
         two.line = one.close(two.line)
-        table, unit_three = two.fan((self.got_table, unit_three), size)
+        table, unit_three = two.fan((self.got_table, unit_three), unit_two.shape[1])
         three = Gather(unit_three, n_dp, n_line)
         full_qkv, full_out = assemble([w_qkv, w_out], one.parts + one.cores, table, n_line, size)
         self.one = (full_qkv, full_out)
         self.two = (w_fc1, two)
-        self.three = (w_fc2, three, unit_three.shape[0])
+        self.three = (w_fc2, three, unit_three.shape)
         far = jnp.concatenate([far[:, :, i * shard : (i + 1) * shard] for i in range(fold)], axis=1)
         return jnp.take(jnp.concatenate([padded[None], far]), self.unline, axis=0)
 
@@ -553,7 +553,7 @@
         return self.two[1].forward(gate)
 
     def pass_two(self, gate):
-        return self.three[1].fan(self.two[1].close(gate), self.three[2])
+        return self.three[1].fan(self.two[1].close(gate), self.three[2][1])
 
     def pass_three(self, gate):
         return self.three[1].forward(gate)
@@ -567,7 +567,7 @@
 
     def third(self):
         own, got, unit = self.three
-        return assemble([own], got.parts + got.cores, self.got_table, self.n_line, unit)[0]
+        return assemble([own], got.parts + got.cores, self.got_table, self.n_line, unit[0])[0]
 
     def rows(self, block):
         return jnp.dot(block, self.order, preferred_element_type=jnp.float32).astype(jnp.bfloat16)
@@ -668,8 +668,6 @@
     run_fc2 = plan.total([(plan.wide_columns(activated), grad_out)])
     activated = tick(activated, [run_fc2])
     full_fc2, activated = tick((plan.third(), activated), [run_fc2])
-    branch_out = jnp.dot(activated, full_fc2, preferred_element_type=f32)
-    block_out = jnp.where(valid[:, None], hidden_mid + branch_out, 0.0).astype(bf16)
 
     grad_pre = (times_t(grad_out, full_fc2) * slope.astype(f32)).astype(bf16)
     grad_fc1_bias = jnp.sum(grad_pre.astype(f32), axis=0)
@@ -694,12 +692,15 @@
     )
     run_qkv = plan.total([(plan.rows(normed_one), grad_proj)])
     grad_proj = tick(grad_proj, [run_qkv])
-    grad_norm_one = times_t(grad_proj, full_qkv)
-    grad_norm_one = tick(grad_norm_one, [run_fc2, run_fc1, run_out, run_qkv])
+    grad_norm_one = tick(times_t(grad_proj, full_qkv), [run_qkv])
     _, pull_one = jax.vjp(layer_norm, hidden_in, gain_one, bias_one)
     back_in, grad_gain_one, grad_bias_one = pull_one(grad_norm_one)
     grad_in = grad_mid + back_in
     grad_table = jnp.dot(place.T, grad_in, precision=highest)
+    grad_table, activated = tick((grad_table, activated), [run_qkv])
+    branch_out = jnp.dot(activated, full_fc2, preferred_element_type=f32)
+    block_out = jnp.where(valid[:, None], hidden_mid + branch_out, 0.0).astype(bf16)
+    block_out = tick(block_out, [run_qkv, run_fc2, run_fc1, run_out])
 
     def split(block):
         return block.reshape(-1, n_line, shard).transpose(1, 0, 2)

time: 490 us -> 471 us (0.961)
  waiting for transfers between devices: 112 us -> 98.3 us
  starting transfers between devices: 89.1 us -> 82 us
    ppermute x0 -> x12, waiting for transfers between devices: none -> 16.1 us  [plane_hops(): return [lax.ppermute(block, 'dp', pairs) for pairs in hops]]
    ppermute x24, waiting for transfers between devices: 56.7 us -> 41.2 us  [ahead(): lax.ppermute(block, 'fsdp', [(i, (i + step) % n_line) for i in range(n_li...]
    ppermute x0 -> x12, starting transfers between devices: none -> 14.6 us  [plane_hops(): return [lax.ppermute(block, 'dp', pairs) for pairs in hops]]
    ppermute x24, starting transfers between devices: 58.5 us -> 44.4 us  [ahead(): lax.ppermute(block, 'fsdp', [(i, (i + step) % n_line) for i in range(n_li...]
    ppermute x16 -> x8, waiting for transfers between devices: 29.8 us -> 18.8 us  [reduce_steps(): got, = (yield [lax.ppermute(send, 'dp', hop_pairs(n_dp, stage))])]
    ppermute x16 -> x8, starting transfers between devices: 17.6 us -> 9.65 us  [reduce_steps(): got, = (yield [lax.ppermute(send, 'dp', hop_pairs(n_dp, stage))])]
    unnamed x205 -> x166, local copies, waits for them, and re-layouts: 17.7 us -> 15.5 us
  transfers between devices with their start and end apart: 72 -> 76, of which waited for: 20 -> 23; matrix products, arithmetic and copies ran while one was open for 23% -> 24% of each run, Pallas kernels for 18% -> 18%
where the time goes in v8:
time: 471 us; the launch traced here: 464 us
  waiting for transfers between devices  98.3 us (21%)
  matrix products  96.4 us (20%)
  Pallas kernels  94.9 us (20%)
  starting transfers between devices  82 us (17%)
  other arithmetic  57.4 us (12%)
  local copies, waits for them, and re-layouts  33.1 us (7%)
    ppermute x24, starting transfers between devices, ahead(): lax.ppermute(block, 'fsdp', [(i, (i + step) % n_line) for i in range(n_li...  44.4 us
    ppermute x24, waiting for transfers between devices, ahead(): lax.ppermute(block, 'fsdp', [(i, (i + step) % n_line) for i in range(n_li...  41.2 us
    pallas_call x2, Pallas kernels, attend_back(): pl.pallas_call(body, grid=(count,), in_specs=pair_specs(rows, pairs, star...  37.7 us
    dot_general x8, matrix products, t_times(): lax.dot_general(left, right, (((0,), (0,)), ((), ())), preferred_element_...  27.3 us
    dot_general x4, matrix products, times_t(): lax.dot_general(left, right, (((1,), (1,)), ((), ())), preferred_element_...  27 us
    convert_element_type x8, other arithmetic, reduce_steps(): add_up([term[half:] for term in terms]).astype(jnp.bfloat16)  23.3 us
    pallas_call x3, Pallas kernels, assemble(): pl.pallas_call(body, in_specs=[pl.BlockSpec(memory_space=pltpu.SMEM)] + [...  22.9 us
    ppermute x8, waiting for transfers between devices, reduce_steps(): got, = (yield [lax.ppermute(send, 'dp', hop_pairs(n_dp, stage))])  18.8 us
  transfers between devices with their start and end apart: 76, of which 23 were waited for; matrix products, arithmetic and copies ran while one was open for 24% of the time, Pallas kernels for 18%

profile of v8, /device:TPU:0, one launch (start us, length us, event | category | flops | bytes accessed | tf_op | source)
XLA Modules:
  0.0 464.3 jit_solution(15043881789351712069)
XLA Ops:
  6.6 3.1 collective-permute-start
  9.7 2.6 collective-permute-start.1
  19.7 11.8 %collective-permute-done.1 = bf16[32,4608]{1,0:T(8,128)(2,1)S(1)} collective-permute-done((bf16[32,4608]{1,0:T(8,128)(2,1)S(1)}, bf16[32,4608]{1,0:T(8,128)(2,1)S(1)}, u32[]{:S(2)}, u32[]{:S(2)}) %collective-permute-start.1) | collective-permute-done | bytes 294944 | tf_op jit(solution)/shard_map/ppermute | solution.py:298
  35.6 6.8 %collective-permute-start.5 = (bf16[32,4096]{1,0:T(8,128)(2,1)S(1)}, bf16[32,4096]{1,0:T(8,128)(2,1)S(1)}, u32[]{:S(2)}, u32[]{:S(2)}) collective-permute-start(bf16[32,4096]{1,0:T(8,128)(2,1)S(1)} %constant_dynamic-slice_fusion.5), channel_id=1, source_target_pairs={{0,1},{1,2},{2,3},{3,0},{4,5},{5,6},{6,7},{7,4},{8,9},{9,10},{10,1... | collective-permute-start | bytes 786440 | tf_op jit(solution)/shard_map/ppermute | solution.py:298
  45.6 5.1 %collective-permute-done.5 = bf16[32,4096]{1,0:T(8,128)(2,1)S(1)} collective-permute-done((bf16[32,4096]{1,0:T(8,128)(2,1)S(1)}, bf16[32,4096]{1,0:T(8,128)(2,1)S(1)}, u32[]{:S(2)}, u32[]{:S(2)}) %collective-permute-start.5) | collective-permute-done | bytes 262176 | tf_op jit(solution)/shard_map/ppermute | solution.py:298
  50.7 9.0 %collective-permute-done.6 = bf16[32,4096]{1,0:T(8,128)(2,1)S(1)} collective-permute-done((bf16[32,4096]{1,0:T(8,128)(2,1)S(1)}, bf16[32,4096]{1,0:T(8,128)(2,1)S(1)}, u32[]{:S(2)}, u32[]{:S(2)}) %collective-permute-start.6) | collective-permute-done | bytes 262176 | tf_op jit(solution)/shard_map/ppermute | solution.py:298
  62.1 9.8 %collective-permute-done.8.refs_5_ = bf16[1,3,32,4096]{3,2,1,0:T(8,128)(2,1)S(1)} collective-permute-done((bf16[1,3,32,4096]{3,2,1,0:T(8,128)(2,1)}, bf16[1,3,32,4096]{3,2,1,0:T(8,128)(2,1)S(1)}, u32[]{:S(2)}, u32[]{:S(2)}) %collective-permute-start.8) | collective-permute-done | bytes 786464 | tf_op jit(solution)/shard_map/ppermute | solution.py:473
  75.7 7.7 %assemble.3 = (bf16[1024,3072]{1,0:T(8,128)(2,1)}, bf16[1024,1024]{1,0:T(8,128)(2,1)}) custom-call(s32[33]{0:T(128)} %pad_add_fusion.1.table_ref, bf16[256,3072]{1,0:T(8,128)(2,1)} %refs_0_.3, bf16[256,1024]{1,0:T(8,128)(2,1)} %refs_1_.1, bf16[1,3,32,4096]{3,2,1,0:T(8,128)(2,1)} %maximum_bitcast_fusion.refs_2_, ...), custom_call_target="tpu_custom_call" | custom-call | tf_op jit(solution)/shard_map/assemble/pallas_call | solution.py:225
  83.4 7.8 %convolution_convert_fusion.4.refs_2_.refs_3_.refs_4_ = bf16[512,3072]{1,0:T(8,128)(2,1)} fusion(bf16[1024,3072]{1,0:T(8,128)(2,1)} %get-tuple-element.151, f32[512,1024]{1,0:T(8,128)S(1)} %get-tuple-element.287, f32[1024]{0:T(1024)S(1)} %bitcast.299, f32[1024]{0:T(1024)S(1)} %bitcast.291, f32[512]{0:T(512)S(1)} %fusion.86, f32[512]{0:T(512)S(1)} %broadcast_multiply_fusion.1), kind=kOutput, calls=%fused_computation.15 | convolution fusion | flops 3225419776 | bytes 11546624 | tf_op jit(solution)/shard_map/dot_general | solution.py:654
  94.1 6.0 %collective-permute-start.9 = (bf16[128,1024]{1,0:T(8,128)(2,1)S(1)}, bf16[128,1024]{1,0:T(8,128)(2,1)S(1)}, u32[]{:S(2)}, u32[]{:S(2)}) collective-permute-start(bf16[128,1024]{1,0:T(8,128)(2,1)S(1)} %copy-done.38), channel_id=1, source_target_pairs={{0,1},{1,2},{2,3},{3,0},{4,5},{5,6},{6,7},{7,4},{8,9},{9,10},{10,1... | collective-permute-start | bytes 786440 | tf_op jit(solution)/shard_map/ppermute | solution.py:298
  100.1 2.4 collective-permute-start.10
  106.8 15.8 %attend.1 = bf16[512,1024]{1,0:T(8,128)(2,1)} custom-call(s32[512,1]{1,0:T(8,128)} %fusion.59.refs_0_, s32[1,512]{1,0:T(1,128)} %broadcast_select_fusion.2.refs_1_, bf16[512,3072]{1,0:T(8,128)(2,1)} %convolution_convert_fusion.4.refs_2_.refs_3_.refs_4_, bf16[512,3072]{1,0:T(8,128)(2,1)} %convolution_convert_fusion.4.refs_2_.refs_3_.refs_4_, ...), custom_call_target="tpu_custom_call" | custom-call | tf_op jit(solution)/shard_map/attend/pallas_call | solution.py:148
  126.5 3.3 fusion.103
  131.9 5.7 %collective-permute-done.19.refs_2_ = bf16[1,3,128,1024]{3,2,1,0:T(8,128)(2,1)} collective-permute-done((bf16[1,3,128,1024]{3,2,1,0:T(8,128)(2,1)}, bf16[1,3,128,1024]{3,2,1,0:T(8,128)(2,1)}, u32[]{:S(2)}, u32[]{:S(2)}) %collective-permute-start.19) | collective-permute-done | bytes 786464 | tf_op jit(solution)/shard_map/ppermute | solution.py:473
  140.5 7.6 %assemble.4 = bf16[1024,4096]{1,0:T(8,128)(2,1)} custom-call(s32[33]{0:T(128)} %pad_add_fusion.1.table_ref, bf16[256,4096]{1,0:T(8,128)(2,1)} %refs_0_.4, bf16[1,3,32,4096]{3,2,1,0:T(8,128)(2,1)} %copy-done.20, bf16[1,3,32,4096]{3,2,1,0:T(8,128)(2,1)} %collective-permute-done.13.refs_2_, bf16[1,3,32,4096]{3,2,1,0:T(8,128)(2,1)} %collective-permute-done.12.refs_3_, ...), custom_call_target="tpu_custom_call" | custom-call | tf_op jit(solution)/shard_map/assemble/pallas_call | solution.py:225
  148.0 10.4 %multiply_convert_fusion.1 = (bf16[512,4096]{1,0:T(8,128)(2,1)}, f32[512,4096]{1,0:T(8,128)}) fusion(f32[4096]{0:T(1024)S(1)} %bitcast.296, bf16[512,1024]{1,0:T(8,128)(2,1)S(1)} %copy-done.28, bf16[1024,4096]{1,0:T(8,128)(2,1)} %assemble.4), kind=kOutput, calls=%fused_computation.9 | convolution fusion | flops 4307550208 | bytes 22036480 | tf_op jit(solution)/shard_map/dot_general | solution.py:661
  158.5 5.5 %column_order.1 = bf16[512,4096]{1,0:T(8,128)(2,1)} custom-call(s32[32]{0:T(128)} %add.550.table_ref, bf16[512,4096]{1,0:T(8,128)(2,1)} %get-tuple-element.218.in_ref), custom_call_target="tpu_custom_call" | custom-call | tf_op jit(solution)/shard_map/column_order/pallas_call | solution.py:245
  164.0 6.0 %convolution_convert_fusion.6 = bf16[2048,1024]{1,0:T(8,128)(2,1)} fusion(bf16[512,4096]{1,0:T(8,128)(2,1)} %column_order.1, bf16[512,1024]{1,0:T(8,128)(2,1)S(1)} %copy-done.18, pred[512]{0:T(512)(128)(4,1)S(1)} %copy-done.67), kind=kOutput, calls=%fused_computation.25 | convolution fusion | flops 2150105088 | bytes 7340544 | tf_op jit(solution)/shard_map/dot_general | solution.py:69
  171.3 3.7 fusion.22
  174.9 2.4 convolution_convert_fusion.5
  182.7 7.6 %assemble.5 = bf16[4096,1024]{1,0:T(8,128)(2,1)} custom-call(s32[33]{0:T(128)} %pad_add_fusion.1.table_ref, bf16[1024,1024]{1,0:T(8,128)(2,1)} %refs_0_.5, bf16[1,3,128,1024]{3,2,1,0:T(8,128)(2,1)} %maximum_bitcast_fusion.2.refs_1_, bf16[1,3,128,1024]{3,2,1,0:T(8,128)(2,1)} %collective-permute-done.19.refs_2_, ...), custom_call_target="tpu_custom_call" | custom-call | tf_op jit(solution)/shard_map/assemble/pallas_call | solution.py:225
  190.3 3.4 fusion.6
  193.7 11.7 %convert_reduce_fusion = (f32[4096]{0:T(1024)}, bf16[512,4096]{1,0:T(8,128)(2,1)S(1)}) fusion(f32[512,4096]{1,0:T(8,128)} %get-tuple-element.291, f32[4096]{0:T(1024)S(1)} %bitcast.297, bf16[4096,1024]{1,0:T(8,128)(2,1)} %assemble.5, bf16[512,1024]{1,0:T(8,128)(2,1)S(1)} %copy-done.18, pred[512]{0:T(512)(128)(4,1)S(1)} %copy-done.67), kind=kOutput, calls=%fused_computation.7 | convolution fusion | flops 4326944768 | bytes 22053376 | tf_op jit(solution)/shard_map/dot_general | solution.py:65
  205.4 5.7 %convolution_convert_fusion.1 = bf16[512,4096]{1,0:T(8,128)(2,1)} fusion(bf16[512,4096]{1,0:T(8,128)(2,1)S(1)} %get-tuple-element.175, bf16[512,1024]{1,0:T(8,128)(2,1)} %fusion.22), kind=kOutput, calls=%fused_computation.12 | convolution fusion | flops 2149580800 | bytes 8912896 | tf_op jit(solution)/shard_map/dot_general | solution.py:69
  212.1 6.8 %multiply_reduce_fusion = (f32[1024]{0:T(1024)}, f32[512]{0:T(512)S(1)}, f32[1024]{0:T(1024)}, f32[512,1024]{1,0:T(8,128)}) fusion(f32[512,1024]{1,0:T(8,128)S(1)} %copy-done.1, f32[512]{0:T(512)S(1)} %fusion.87, f32[512]{0:T(512)S(1)} %broadcast_multiply_fusion, f32[1024]{0:T(1024)S(1)} %bitcast.289, bf16[512,4096]{1,0:T(8,128)(2,1)S(1)} %get-tuple-element.175, ...), kind=kOutput, calls=%fused_computation.38 | convolution fusion | flops 4299159040 | bytes 16795648 | tf_op jit(solution)/shard_map/dot_general | solution.py:65
  218.9 2.4 fusion.97
  221.3 2.5 convolution_convert_fusion
  227.8 3.8 fusion.5
  236.4 2.7 convolution_convert_fusion.7.refs_5_
  240.9 3.2 fusion.16
  245.6 18.8 %attend_back.2 = bf16[512,1536]{1,0:T(8,128)(2,1)} custom-call(s32[512,1]{1,0:T(8,128)} %fusion.59.refs_0_, s32[1,512]{1,0:T(1,128)} %broadcast_select_fusion.2.refs_1_, bf16[512,3072]{1,0:T(8,128)(2,1)} %convolution_convert_fusion.4.refs_2_.refs_3_.refs_4_, bf16[512,3072]{1,0:T(8,128)(2,1)} %convolution_convert_fusion.4.refs_2_.refs_3_.refs_4_, ...), custom_call_target="tpu_custom_call" | custom-call | tf_op jit(solution)/shard_map/attend_back/pallas_call | solution.py:167
  266.2 4.2 collective-permute-done.33
  271.4 3.1 fusion.46
  274.6 3.0 fusion.14
  280.9 2.1 collective-permute-start.36
  285.5 2.5 fusion.24
  287.9 18.9 %attend_back.3 = bf16[512,1536]{1,0:T(8,128)(2,1)} custom-call(s32[512,1]{1,0:T(8,128)} %fusion.59.refs_0_, s32[1,512]{1,0:T(1,128)} %broadcast_select_fusion.2.refs_1_, bf16[512,3072]{1,0:T(8,128)(2,1)} %convolution_convert_fusion.4.refs_2_.refs_3_.refs_4_, bf16[512,3072]{1,0:T(8,128)(2,1)} %convolution_convert_fusion.4.refs_2_.refs_3_.refs_4_, ...), custom_call_target="tpu_custom_call" | custom-call | tf_op jit(solution)/shard_map/attend_back/pallas_call | solution.py:167
  306.9 3.2 fusion.39
  315.0 3.5 convolution_convert_fusion.3
  320.0 3.7 convolution_convert_fusion.2
  326.7 5.8 %fusion.104 = f32[512,1024]{1,0:T(8,128)S(1)} fusion(bf16[512,3072]{1,0:T(8,128)(2,1)S(1)} %copy-done.8, bf16[1024,3072]{1,0:T(8,128)(2,1)} %get-tuple-element.151), kind=kOutput, calls=%fused_computation.305 | convolution fusion | flops 3221225472 | bytes 11534336 | tf_op jit(solution)/shard_map/dot_general | solution.py:65
  332.6 3.9 fusion.10
  339.2 2.4 fusion.96
  344.5 13.6 %collective-permute-done.42 = bf16[2,4,32,3072]{3,2,1,0:T(8,128)(2,1)} collective-permute-done((bf16[2,4,32,3072]{3,2,1,0:T(8,128)(2,1)}, bf16[2,4,32,3072]{3,2,1,0:T(8,128)(2,1)}, u32[]{:S(2)}, u32[]{:S(2)}) %collective-permute-start.42) | collective-permute-done | bytes 1572896 | tf_op jit(solution)/shard_map/ppermute | solution.py:322
  358.1 2.8 fusion.21
  366.8 2.8 collective-permute-done.44
  369.6 2.1 collective-permute-start.48
  373.0 4.1 collective-permute-done.46
  377.1 3.7 collective-permute-done.52
  380.9 2.3 collective-permute-start.43
  383.2 10.1 %select_convert_fusion = bf16[512,1024]{1,0:T(8,128)(2,1)} fusion(f32[512,1024]{1,0:T(8,128)S(1)} %copy-done.2, bf16[512,4096]{1,0:T(8,128)(2,1)} %get-tuple-element.218.in_ref, bf16[4096,1024]{1,0:T(8,128)(2,1)} %assemble.5, pred[512]{0:T(512)(128)(4,1)S(1)} %copy-done.68), kind=kOutput, calls=%fused_computation.40 | convolution fusion | flops 4296540160 | bytes 15729152 | tf_op jit(solution)/shard_map/dot_general | solution.py:701
  403.2 2.0 collective-permute-start.66
  406.3 3.0 collective-permute-done.66
  409.3 2.1 collective-permute-start.59
  412.3 4.3 collective-permute-start.57
  417.6 10.8 %collective-permute-done.58 = bf16[32,3072]{1,0:T(8,128)(2,1)S(1)} collective-permute-done((bf16[32,3072]{1,0:T(8,128)(2,1)S(1)}, bf16[32,3072]{1,0:T(8,128)(2,1)S(1)}, u32[]{:S(2)}, u32[]{:S(2)}) %collective-permute-start.58) | collective-permute-done | bytes 196640 | tf_op jit(solution)/shard_map/ppermute | solution.py:298
  435.6 3.1 collective-permute-done.62
  438.7 2.2 collective-permute-done.61
  440.9 2.6 collective-permute-start.69
  446.1 2.2 collective-permute-done.68
  451.1 2.1 finish.5
  453.2 3.8 finish.7
  457.0 3.3 finish.4
  460.3 3.8 finish.6
  (406 shorter events, 117.6 us)
Async XLA Ops:
  6.6 13.1 %collective-permute-start = (bf16[32,4608]{1,0:T(8,128)(2,1)S(1)}, bf16[32,4608]{1,0:T(8,128)(2,1)S(1)}, u32[]{:S(2)}, u32[]{:S(2)}) collective-permute-start(bf16[32,4608]{1,0:T(8,128)(2,1)S(1)} %pad_maximum_fusion.2), channel_id=1, source_target_pairs={{0,1},{1,2},{2,3},{3,0},{4,5},{5,6},{6,7},{7,4},{8,9},{9,10},{10,1... | collective-permute-start | bytes 884744 | tf_op jit(solution)/shard_map/ppermute | solution.py:298
  9.7 21.8 %collective-permute-start.1 = (bf16[32,4608]{1,0:T(8,128)(2,1)S(1)}, bf16[32,4608]{1,0:T(8,128)(2,1)S(1)}, u32[]{:S(2)}, u32[]{:S(2)}) collective-permute-start(bf16[32,4608]{1,0:T(8,128)(2,1)S(1)} %pad_maximum_fusion.2), channel_id=1, source_target_pairs={{0,2},{1,3},{2,0},{3,1},{4,6},{5,7},{6,4},{7,5},{8,10},{9,11},{10,... | collective-permute-start | bytes 884744 | tf_op jit(solution)/shard_map/ppermute | solution.py:298
  12.3 19.2 %collective-permute-start.2 = (bf16[32,4608]{1,0:T(8,128)(2,1)S(1)}, bf16[32,4608]{1,0:T(8,128)(2,1)S(1)}, u32[]{:S(2)}, u32[]{:S(2)}) collective-permute-start(bf16[32,4608]{1,0:T(8,128)(2,1)S(1)} %pad_maximum_fusion.2), channel_id=1, source_target_pairs={{0,3},{1,0},{2,1},{3,2},{4,7},{5,4},{6,5},{7,6},{8,11},{9,8},{10,9... | collective-permute-start | bytes 884744 | tf_op jit(solution)/shard_map/ppermute | solution.py:298
  32.6 29.6 %collective-permute-start.3 = (bf16[1,3,32,4096]{3,2,1,0:T(8,128)(2,1)}, bf16[1,3,32,4096]{3,2,1,0:T(8,128)(2,1)}, u32[]{:S(2)}, u32[]{:S(2)}) collective-permute-start(bf16[1,3,32,4096]{3,2,1,0:T(8,128)(2,1)} %maximum_bitcast_fusion.refs_2_), channel_id=1, source_target_pairs={{0,16},{4,12},{8,24},{12,4},{16,0},{20,28},{24,8},{28,20},{1,17},{... | collective-permute-start | bytes 2359304 | tf_op jit(solution)/shard_map/ppermute | solution.py:473
  34.1 25.5 %collective-permute-start.4 = (bf16[1,3,32,4096]{3,2,1,0:T(8,128)(2,1)}, bf16[1,3,32,4096]{3,2,1,0:T(8,128)(2,1)}, u32[]{:S(2)}, u32[]{:S(2)}) collective-permute-start(bf16[1,3,32,4096]{3,2,1,0:T(8,128)(2,1)} %maximum_bitcast_fusion.refs_2_), channel_id=1, source_target_pairs={{0,8},{4,20},{8,0},{12,28},{16,24},{20,4},{24,16},{28,12},{1,9},{5... | collective-permute-start | bytes 2359304 | tf_op jit(solution)/shard_map/ppermute | solution.py:473
  35.6 15.1 %collective-permute-start.5 = (bf16[32,4096]{1,0:T(8,128)(2,1)S(1)}, bf16[32,4096]{1,0:T(8,128)(2,1)S(1)}, u32[]{:S(2)}, u32[]{:S(2)}) collective-permute-start(bf16[32,4096]{1,0:T(8,128)(2,1)S(1)} %constant_dynamic-slice_fusion.5), channel_id=1, source_target_pairs={{0,1},{1,2},{2,3},{3,0},{4,5},{5,6},{6,7},{7,4},{8,9},{9,10},{10,1... | collective-permute-start | bytes 786440 | tf_op jit(solution)/shard_map/ppermute | solution.py:298
  42.4 17.3 %collective-permute-start.6 = (bf16[32,4096]{1,0:T(8,128)(2,1)S(1)}, bf16[32,4096]{1,0:T(8,128)(2,1)S(1)}, u32[]{:S(2)}, u32[]{:S(2)}) collective-permute-start(bf16[32,4096]{1,0:T(8,128)(2,1)S(1)} %constant_dynamic-slice_fusion.5), channel_id=1, source_target_pairs={{0,2},{1,3},{2,0},{3,1},{4,6},{5,7},{6,4},{7,5},{8,10},{9,11},{10,... | collective-permute-start | bytes 786440 | tf_op jit(solution)/shard_map/ppermute | solution.py:298
  44.0 15.7 %collective-permute-start.7 = (bf16[32,4096]{1,0:T(8,128)(2,1)S(1)}, bf16[32,4096]{1,0:T(8,128)(2,1)S(1)}, u32[]{:S(2)}, u32[]{:S(2)}) collective-permute-start(bf16[32,4096]{1,0:T(8,128)(2,1)S(1)} %constant_dynamic-slice_fusion.5), channel_id=1, source_target_pairs={{0,3},{1,0},{2,1},{3,2},{4,7},{5,4},{6,5},{7,6},{8,11},{9,8},{10,9... | collective-permute-start | bytes 786440 | tf_op jit(solution)/shard_map/ppermute | solution.py:298
  50.7 23.1 %collective-permute-start.14 = (bf16[1,3,32,4096]{3,2,1,0:T(8,128)(2,1)}, bf16[1,3,32,4096]{3,2,1,0:T(8,128)(2,1)}, u32[]{:S(2)}, u32[]{:S(2)}) collective-permute-start(bf16[1,3,32,4096]{3,2,1,0:T(8,128)(2,1)} %maximum_bitcast_fusion.refs_2_), channel_id=1, source_target_pairs={{0,4},{4,0},{8,12},{12,8},{16,20},{20,16},{24,28},{28,24},{1,5},{5... | collective-permute-start | bytes 2359304 | tf_op jit(solution)/shard_map/ppermute | solution.py:294
  59.7 12.3 %collective-permute-start.8 = (bf16[1,3,32,4096]{3,2,1,0:T(8,128)(2,1)}, bf16[1,3,32,4096]{3,2,1,0:T(8,128)(2,1)S(1)}, u32[]{:S(2)}, u32[]{:S(2)}) collective-permute-start(bf16[1,3,32,4096]{3,2,1,0:T(8,128)(2,1)} %collective-permute-done.4.refs_3_), channel_id=1, source_target_pairs={{0,16},{4,12},{8,24},{12,4},{16,0},{20,28},{24,8},{28,20},{1,17},{... | collective-permute-start | bytes 2359304 | tf_op jit(solution)/shard_map/ppermute | solution.py:473
  62.1 12.3 %collective-permute-start.15 = (bf16[1,3,32,4096]{3,2,1,0:T(8,128)(2,1)}, bf16[1,3,32,4096]{3,2,1,0:T(8,128)(2,1)}, u32[]{:S(2)}, u32[]{:S(2)}) collective-permute-start(bf16[1,3,32,4096]{3,2,1,0:T(8,128)(2,1)} %collective-permute-done.4.refs_3_), channel_id=1, source_target_pairs={{0,4},{4,0},{8,12},{12,8},{16,20},{20,16},{24,28},{28,24},{1,5},{5... | collective-permute-start | bytes 2359304 | tf_op jit(solution)/shard_map/ppermute | solution.py:294
  73.2 49.4 %collective-permute-start.12 = (bf16[1,3,32,4096]{3,2,1,0:T(8,128)(2,1)S(1)}, bf16[1,3,32,4096]{3,2,1,0:T(8,128)(2,1)}, u32[]{:S(2)}, u32[]{:S(2)}) collective-permute-start(bf16[1,3,32,4096]{3,2,1,0:T(8,128)(2,1)S(1)} %maximum_bitcast_fusion.1.refs_1_), channel_id=1, source_target_pairs={{0,16},{4,12},{8,24},{12,4},{16,0},{20,28},{24,8},{28,20},{1,17},{... | collective-permute-start | bytes 2359304 | tf_op jit(solution)/shard_map/ppermute | solution.py:473
  73.8 19.0 %collective-permute-start.13 = (bf16[1,3,32,4096]{3,2,1,0:T(8,128)(2,1)S(1)}, bf16[1,3,32,4096]{3,2,1,0:T(8,128)(2,1)}, u32[]{:S(2)}, u32[]{:S(2)}) collective-permute-start(bf16[1,3,32,4096]{3,2,1,0:T(8,128)(2,1)S(1)} %maximum_bitcast_fusion.1.refs_1_), channel_id=1, source_target_pairs={{0,8},{4,20},{8,0},{12,28},{16,24},{20,4},{24,16},{28,12},{1,9},{5... | collective-permute-start | bytes 2359304 | tf_op jit(solution)/shard_map/ppermute | solution.py:473
  92.8 29.9 %collective-permute-start.18 = (bf16[1,3,32,4096]{3,2,1,0:T(8,128)(2,1)}, bf16[1,3,32,4096]{3,2,1,0:T(8,128)(2,1)}, u32[]{:S(2)}, u32[]{:S(2)}) collective-permute-start(bf16[1,3,32,4096]{3,2,1,0:T(8,128)(2,1)} %collective-permute-done.13.refs_2_), channel_id=1, source_target_pairs={{0,16},{4,12},{8,24},{12,4},{16,0},{20,28},{24,8},{28,20},{1,17},{... | collective-permute-start | bytes 2359304 | tf_op jit(solution)/shard_map/ppermute | solution.py:473
  94.1 29.1 %collective-permute-start.9 = (bf16[128,1024]{1,0:T(8,128)(2,1)S(1)}, bf16[128,1024]{1,0:T(8,128)(2,1)S(1)}, u32[]{:S(2)}, u32[]{:S(2)}) collective-permute-start(bf16[128,1024]{1,0:T(8,128)(2,1)S(1)} %copy-done.38), channel_id=1, source_target_pairs={{0,1},{1,2},{2,3},{3,0},{4,5},{5,6},{6,7},{7,4},{8,9},{9,10},{10,1... | collective-permute-start | bytes 786440 | tf_op jit(solution)/shard_map/ppermute | solution.py:298
  100.1 23.1 %collective-permute-start.10 = (bf16[128,1024]{1,0:T(8,128)(2,1)S(1)}, bf16[128,1024]{1,0:T(8,128)(2,1)}, u32[]{:S(2)}, u32[]{:S(2)}) collective-permute-start(bf16[128,1024]{1,0:T(8,128)(2,1)S(1)} %copy-done.38), channel_id=1, source_target_pairs={{0,2},{1,3},{2,0},{3,1},{4,6},{5,7},{6,4},{7,5},{8,10},{9,11},{10,... | collective-permute-start | bytes 786440 | tf_op jit(solution)/shard_map/ppermute | solution.py:298
  102.5 20.7 %collective-permute-start.11 = (bf16[128,1024]{1,0:T(8,128)(2,1)S(1)}, bf16[128,1024]{1,0:T(8,128)(2,1)}, u32[]{:S(2)}, u32[]{:S(2)}) collective-permute-start(bf16[128,1024]{1,0:T(8,128)(2,1)S(1)} %copy-done.38), channel_id=1, source_target_pairs={{0,3},{1,0},{2,1},{3,2},{4,7},{5,4},{6,5},{7,6},{8,11},{9,8},{10,9... | collective-permute-start | bytes 786440 | tf_op jit(solution)/shard_map/ppermute | solution.py:298
  122.6 16.4 %collective-permute-start.22 = (bf16[1,3,32,4096]{3,2,1,0:T(8,128)(2,1)S(1)}, bf16[1,3,32,4096]{3,2,1,0:T(8,128)(2,1)S(1)}, u32[]{:S(2)}, u32[]{:S(2)}) collective-permute-start(bf16[1,3,32,4096]{3,2,1,0:T(8,128)(2,1)S(1)} %maximum_bitcast_fusion.1.refs_1_), channel_id=1, source_target_pairs={{0,4},{4,0},{8,12},{12,8},{16,20},{20,16},{24,28},{28,24},{1,5},{5... | collective-permute-start | bytes 2359304 | tf_op jit(solution)/shard_map/ppermute | solution.py:294
  122.7 17.7 %collective-permute-start.23 = (bf16[1,3,32,4096]{3,2,1,0:T(8,128)(2,1)}, bf16[1,3,32,4096]{3,2,1,0:T(8,128)(2,1)}, u32[]{:S(2)}, u32[]{:S(2)}) collective-permute-start(bf16[1,3,32,4096]{3,2,1,0:T(8,128)(2,1)} %collective-permute-done.13.refs_2_), channel_id=1, source_target_pairs={{0,4},{4,0},{8,12},{12,8},{16,20},{20,16},{24,28},{28,24},{1,5},{5... | collective-permute-start | bytes 2359304 | tf_op jit(solution)/shard_map/ppermute | solution.py:294
  125.2 12.3 %collective-permute-start.19 = (bf16[1,3,128,1024]{3,2,1,0:T(8,128)(2,1)}, bf16[1,3,128,1024]{3,2,1,0:T(8,128)(2,1)}, u32[]{:S(2)}, u32[]{:S(2)}) collective-permute-start(bf16[1,3,128,1024]{3,2,1,0:T(8,128)(2,1)} %maximum_bitcast_fusion.2.refs_1_), channel_id=1, source_target_pairs={{0,8},{4,20},{8,0},{12,28},{16,24},{20,4},{24,16},{28,12},{1,9},{5... | collective-permute-start | bytes 2359304 | tf_op jit(solution)/shard_map/ppermute | solution.py:473
  125.7 14.7 %collective-permute-start.24 = (bf16[1,3,32,4096]{3,2,1,0:T(8,128)(2,1)}, bf16[1,3,32,4096]{3,2,1,0:T(8,128)(2,1)}, u32[]{:S(2)}, u32[]{:S(2)}) collective-permute-start(bf16[1,3,32,4096]{3,2,1,0:T(8,128)(2,1)} %collective-permute-done.12.refs_3_), channel_id=1, source_target_pairs={{0,4},{4,0},{8,12},{12,8},{16,20},{20,16},{24,28},{28,24},{1,5},{5... | collective-permute-start | bytes 2359304 | tf_op jit(solution)/shard_map/ppermute | solution.py:294
  126.5 13.9 %collective-permute-start.25 = (bf16[1,3,32,4096]{3,2,1,0:T(8,128)(2,1)}, bf16[1,3,32,4096]{3,2,1,0:T(8,128)(2,1)}, u32[]{:S(2)}, u32[]{:S(2)}) collective-permute-start(bf16[1,3,32,4096]{3,2,1,0:T(8,128)(2,1)} %collective-permute-done.18.refs_4_), channel_id=1, source_target_pairs={{0,4},{4,0},{8,12},{12,8},{16,20},{20,16},{24,28},{28,24},{1,5},{5... | collective-permute-start | bytes 2359304 | tf_op jit(solution)/shard_map/ppermute | solution.py:294
  137.5 21.0 %collective-permute-start.20 = (bf16[1,3,128,1024]{3,2,1,0:T(8,128)(2,1)}, bf16[1,3,128,1024]{3,2,1,0:T(8,128)(2,1)}, u32[]{:S(2)}, u32[]{:S(2)}) collective-permute-start(bf16[1,3,128,1024]{3,2,1,0:T(8,128)(2,1)} %maximum_bitcast_fusion.2.refs_1_), channel_id=1, source_target_pairs={{0,16},{4,12},{8,24},{12,4},{16,0},{20,28},{24,8},{28,20},{1,17},{... | collective-permute-start | bytes 2359304 | tf_op jit(solution)/shard_map/ppermute | solution.py:473
  139.9 18.6 %collective-permute-start.21 = (bf16[1,3,128,1024]{3,2,1,0:T(8,128)(2,1)}, bf16[1,3,128,1024]{3,2,1,0:T(8,128)(2,1)}, u32[]{:S(2)}, u32[]{:S(2)}) collective-permute-start(bf16[1,3,128,1024]{3,2,1,0:T(8,128)(2,1)} %collective-permute-done.19.refs_2_), channel_id=1, source_target_pairs={{0,16},{4,12},{8,24},{12,4},{16,0},{20,28},{24,8},{28,20},{1,17},{... | collective-permute-start | bytes 2359304 | tf_op jit(solution)/shard_map/ppermute | solution.py:473
  170.0 20.3 %collective-permute-start.30 = (bf16[4,4,128,1024]{3,2,1,0:T(8,128)(2,1)}, bf16[4,4,128,1024]{3,2,1,0:T(8,128)(2,1)}, u32[]{:S(2)}, u32[]{:S(2)}) collective-permute-start(bf16[4,4,128,1024]{3,2,1,0:T(8,128)(2,1)} %bitcast.24), channel_id=1, source_target_pairs={{0,4},{4,0},{8,12},{12,8},{16,20},{20,16},{24,28},{28,24},{1,5},{5... | collective-permute-start | bytes 12582920 | tf_op jit(solution)/shard_map/ppermute | solution.py:294
  170.2 9.9 %collective-permute-start.26 = (bf16[1,3,128,1024]{3,2,1,0:T(8,128)(2,1)}, bf16[1,3,128,1024]{3,2,1,0:T(8,128)(2,1)S(1)}, u32[]{:S(2)}, u32[]{:S(2)}) collective-permute-start(bf16[1,3,128,1024]{3,2,1,0:T(8,128)(2,1)} %maximum_bitcast_fusion.2.refs_1_), channel_id=1, source_target_pairs={{0,4},{4,0},{8,12},{12,8},{16,20},{20,16},{24,28},{28,24},{1,5},{5... | collective-permute-start | bytes 2359304 | tf_op jit(solution)/shard_map/ppermute | solution.py:294
  170.7 10.2 %collective-permute-start.27 = (bf16[1,3,128,1024]{3,2,1,0:T(8,128)(2,1)}, bf16[1,3,128,1024]{3,2,1,0:T(8,128)(2,1)S(1)}, u32[]{:S(2)}, u32[]{:S(2)}) collective-permute-start(bf16[1,3,128,1024]{3,2,1,0:T(8,128)(2,1)} %collective-permute-done.19.refs_2_), channel_id=1, source_target_pairs={{0,4},{4,0},{8,12},{12,8},{16,20},{20,16},{24,28},{28,24},{1,5},{5... | collective-permute-start | bytes 2359304 | tf_op jit(solution)/shard_map/ppermute | solution.py:294
  170.7 11.0 %collective-permute-start.28 = (bf16[1,3,128,1024]{3,2,1,0:T(8,128)(2,1)}, bf16[1,3,128,1024]{3,2,1,0:T(8,128)(2,1)S(1)}, u32[]{:S(2)}, u32[]{:S(2)}) collective-permute-start(bf16[1,3,128,1024]{3,2,1,0:T(8,128)(2,1)} %collective-permute-done.20.refs_3_), channel_id=1, source_target_pairs={{0,4},{4,0},{8,12},{12,8},{16,20},{20,16},{24,28},{28,24},{1,5},{5... | collective-permute-start | bytes 2359304 | tf_op jit(solution)/shard_map/ppermute | solution.py:294
  171.2 11.5 %collective-permute-start.29 = (bf16[1,3,128,1024]{3,2,1,0:T(8,128)(2,1)}, bf16[1,3,128,1024]{3,2,1,0:T(8,128)(2,1)}, u32[]{:S(2)}, u32[]{:S(2)}) collective-permute-start(bf16[1,3,128,1024]{3,2,1,0:T(8,128)(2,1)} %collective-permute-done.21.refs_4_), channel_id=1, source_target_pairs={{0,4},{4,0},{8,12},{12,8},{16,20},{20,16},{24,28},{28,24},{1,5},{5... | collective-permute-start | bytes 2359304 | tf_op jit(solution)/shard_map/ppermute | solution.py:294
  211.1 15.2 %collective-permute-start.31 = (bf16[4,4,32,4096]{3,2,1,0:T(8,128)(2,1)}, bf16[4,4,32,4096]{3,2,1,0:T(8,128)(2,1)}, u32[]{:S(2)}, u32[]{:S(2)}) collective-permute-start(bf16[4,4,32,4096]{3,2,1,0:T(8,128)(2,1)} %bitcast.26), channel_id=1, source_target_pairs={{0,4},{4,0},{8,12},{12,8},{16,20},{20,16},{24,28},{28,24},{1,5},{5... | collective-permute-start | bytes 12582920 | tf_op jit(solution)/shard_map/ppermute | solution.py:294
  211.6 27.6 %collective-permute-start.32 = (bf16[2,4,128,1024]{3,2,1,0:T(8,128)(2,1)S(1)}, bf16[2,4,128,1024]{3,2,1,0:T(8,128)(2,1)}, u32[]{:S(2)}, u32[]{:S(2)}) collective-permute-start(bf16[2,4,128,1024]{3,2,1,0:T(8,128)(2,1)S(1)} %fusion.6), channel_id=1, source_target_pairs={{0,8},{4,20},{8,0},{12,28},{16,24},{20,4},{24,16},{28,12},{1,9},{5... | collective-permute-start | bytes 6291464 | tf_op jit(solution)/shard_map/ppermute | solution.py:322
  231.6 39.8 %collective-permute-start.34 = (bf16[2,4,32,4096]{3,2,1,0:T(8,128)(2,1)}, bf16[2,4,32,4096]{3,2,1,0:T(8,128)(2,1)}, u32[]{:S(2)}, u32[]{:S(2)}) collective-permute-start(bf16[2,4,32,4096]{3,2,1,0:T(8,128)(2,1)} %fusion.5), channel_id=1, source_target_pairs={{0,8},{4,20},{8,0},{12,28},{16,24},{20,4},{24,16},{28,12},{1,9},{5... | collective-permute-start | bytes 6291464 | tf_op jit(solution)/shard_map/ppermute | solution.py:322
  244.1 26.3 %collective-permute-start.33 = (bf16[1,4,128,1024]{3,2,1,0:T(8,128)(2,1)}, bf16[1,4,128,1024]{3,2,1,0:T(8,128)(2,1)}, u32[]{:S(2)}, u32[]{:S(2)}) collective-permute-start(bf16[1,4,128,1024]{3,2,1,0:T(8,128)(2,1)} %fusion.16), channel_id=1, source_target_pairs={{0,16},{4,12},{8,24},{12,4},{16,0},{20,28},{24,8},{28,20},{1,17},{... | collective-permute-start | bytes 3145736 | tf_op jit(solution)/shard_map/ppermute | solution.py:322
  245.5 24.9 %collective-permute-start.35 = (bf16[4,4,32,1024]{3,2,1,0:T(8,128)(2,1)}, bf16[4,4,32,1024]{3,2,1,0:T(8,128)(2,1)}, u32[]{:S(2)}, u32[]{:S(2)}) collective-permute-start(bf16[4,4,32,1024]{3,2,1,0:T(8,128)(2,1)} %bitcast.29), channel_id=1, source_target_pairs={{0,4},{4,0},{8,12},{12,8},{16,20},{20,16},{24,28},{28,24},{1,5},{5... | collective-permute-start | bytes 3145736 | tf_op jit(solution)/shard_map/ppermute | solution.py:294
  278.9 28.0 %collective-permute-start.39 = (bf16[1,4,32,4096]{3,2,1,0:T(8,128)(2,1)}, bf16[1,4,32,4096]{3,2,1,0:T(8,128)(2,1)}, u32[]{:S(2)}, u32[]{:S(2)}) collective-permute-start(bf16[1,4,32,4096]{3,2,1,0:T(8,128)(2,1)} %fusion.14), channel_id=1, source_target_pairs={{0,16},{4,12},{8,24},{12,4},{16,0},{20,28},{24,8},{28,20},{1,17},{... | collective-permute-start | bytes 3145736 | tf_op jit(solution)/shard_map/ppermute | solution.py:322
  280.4 26.5 %collective-permute-start.40 = (bf16[2,4,32,1024]{3,2,1,0:T(8,128)(2,1)S(1)}, bf16[2,4,32,1024]{3,2,1,0:T(8,128)(2,1)}, u32[]{:S(2)}, u32[]{:S(2)}) collective-permute-start(bf16[2,4,32,1024]{3,2,1,0:T(8,128)(2,1)S(1)} %fusion.26), channel_id=1, source_target_pairs={{0,8},{4,20},{8,0},{12,28},{16,24},{20,4},{24,16},{28,12},{1,9},{5... | collective-permute-start | bytes 1572872 | tf_op jit(solution)/shard_map/ppermute | solution.py:322
  280.9 25.9 %collective-permute-start.36 = (bf16[128,1024]{1,0:T(8,128)(2,1)}, bf16[128,1024]{1,0:T(8,128)(2,1)S(1)}, u32[]{:S(2)}, u32[]{:S(2)}) collective-permute-start(bf16[128,1024]{1,0:T(8,128)(2,1)} %get-tuple-element.194), channel_id=1, source_target_pairs={{0,1},{1,2},{2,3},{3,0},{4,5},{5,6},{6,7},{7,4},{8,9},{9,10},{10,1... | collective-permute-start | bytes 786440 | tf_op jit(solution)/shard_map/ppermute | solution.py:298
  283.1 23.7 %collective-permute-start.37 = (bf16[128,1024]{1,0:T(8,128)(2,1)}, bf16[128,1024]{1,0:T(8,128)(2,1)S(1)}, u32[]{:S(2)}, u32[]{:S(2)}) collective-permute-start(bf16[128,1024]{1,0:T(8,128)(2,1)} %get-tuple-element.195), channel_id=1, source_target_pairs={{0,2},{1,3},{2,0},{3,1},{4,6},{5,7},{6,4},{7,5},{8,10},{9,11},{10,... | collective-permute-start | bytes 786440 | tf_op jit(solution)/shard_map/ppermute | solution.py:298
  283.6 23.3 %collective-permute-start.38 = (bf16[128,1024]{1,0:T(8,128)(2,1)}, bf16[128,1024]{1,0:T(8,128)(2,1)}, u32[]{:S(2)}, u32[]{:S(2)}) collective-permute-start(bf16[128,1024]{1,0:T(8,128)(2,1)} %get-tuple-element.196), channel_id=1, source_target_pairs={{0,3},{1,0},{2,1},{3,2},{4,7},{5,4},{6,5},{7,6},{8,11},{9,8},{10,9... | collective-permute-start | bytes 786440 | tf_op jit(solution)/shard_map/ppermute | solution.py:298
  318.6 14.0 %collective-permute-start.41 = (bf16[4,4,32,3072]{3,2,1,0:T(8,128)(2,1)}, bf16[4,4,32,3072]{3,2,1,0:T(8,128)(2,1)}, u32[]{:S(2)}, u32[]{:S(2)}) collective-permute-start(bf16[4,4,32,3072]{3,2,1,0:T(8,128)(2,1)} %bitcast.55), channel_id=1, source_target_pairs={{0,4},{4,0},{8,12},{12,8},{16,20},{20,16},{24,28},{28,24},{1,5},{5... | collective-permute-start | bytes 9437192 | tf_op jit(solution)/shard_map/ppermute | solution.py:294
  337.3 20.8 %collective-permute-start.42 = (bf16[2,4,32,3072]{3,2,1,0:T(8,128)(2,1)}, bf16[2,4,32,3072]{3,2,1,0:T(8,128)(2,1)}, u32[]{:S(2)}, u32[]{:S(2)}) collective-permute-start(bf16[2,4,32,3072]{3,2,1,0:T(8,128)(2,1)} %fusion.10), channel_id=1, source_target_pairs={{0,8},{4,20},{8,0},{12,28},{16,24},{20,4},{24,16},{28,12},{1,9},{5... | collective-permute-start | bytes 4718600 | tf_op jit(solution)/shard_map/ppermute | solution.py:322
  361.1 8.5 %collective-permute-start.44 = (bf16[1,128,1024]{2,1,0:T(8,128)(2,1)S(1)}, bf16[1,128,1024]{2,1,0:T(8,128)(2,1)S(1)}, u32[]{:S(2)}, u32[]{:S(2)}) collective-permute-start(bf16[1,128,1024]{2,1,0:T(8,128)(2,1)S(1)} %fusion.64), channel_id=1, source_target_pairs={{0,8},{4,20},{8,0},{12,28},{16,24},{20,4},{24,16},{28,12},{1,9},{5... | collective-permute-start | bytes 786440 | tf_op jit(solution)/shard_map/ppermute | solution.py:305
  362.9 8.8 %collective-permute-start.45 = (bf16[1,128,1024]{2,1,0:T(8,128)(2,1)S(1)}, bf16[1,128,1024]{2,1,0:T(8,128)(2,1)}, u32[]{:S(2)}, u32[]{:S(2)}) collective-permute-start(bf16[1,128,1024]{2,1,0:T(8,128)(2,1)S(1)} %fusion.64), channel_id=1, source_target_pairs={{0,16},{4,12},{8,24},{12,4},{16,0},{20,28},{24,8},{28,20},{1,17},{... | collective-permute-start | bytes 786440 | tf_op jit(solution)/shard_map/ppermute | solution.py:305
  364.5 12.7 %collective-permute-start.46 = (bf16[1,128,1024]{2,1,0:T(8,128)(2,1)S(1)}, bf16[1,128,1024]{2,1,0:T(8,128)(2,1)}, u32[]{:S(2)}, u32[]{:S(2)}) collective-permute-start(bf16[1,128,1024]{2,1,0:T(8,128)(2,1)S(1)} %fusion.64), channel_id=1, source_target_pairs={{0,24},{4,28},{8,16},{12,20},{16,8},{20,12},{24,0},{28,4},{1,25},{... | collective-permute-start | bytes 786440 | tf_op jit(solution)/shard_map/ppermute | solution.py:305
  364.8 16.1 %collective-permute-start.52 = (f32[4,64,256]{2,0,1:T(4,128)S(1)}, f32[4,64,256]{2,0,1:T(4,128)S(1)}, u32[]{:S(2)}, u32[]{:S(2)}) collective-permute-start(f32[4,64,256]{2,0,1:T(4,128)S(1)} %fusion.93), channel_id=1, source_target_pairs={{0,8},{4,12},{8,0},{12,4},{16,24},{20,28},{24,16},{28,20},{1,9},{5... | collective-permute-start | bytes 786440 | tf_op jit(solution)/shard_map/ppermute | solution.py:342
  366.6 26.9 %collective-permute-start.47 = (bf16[32,4096]{1,0:T(8,128)(2,1)}, bf16[32,4096]{1,0:T(8,128)(2,1)S(1)}, u32[]{:S(2)}, u32[]{:S(2)}) collective-permute-start(bf16[32,4096]{1,0:T(8,128)(2,1)} %get-tuple-element.221), channel_id=1, source_target_pairs={{0,1},{1,2},{2,3},{3,0},{4,5},{5,6},{6,7},{7,4},{8,9},{9,10},{10,1... | collective-permute-start | bytes 786440 | tf_op jit(solution)/shard_map/ppermute | solution.py:298
  369.6 23.9 %collective-permute-start.48 = (bf16[32,4096]{1,0:T(8,128)(2,1)}, bf16[32,4096]{1,0:T(8,128)(2,1)S(1)}, u32[]{:S(2)}, u32[]{:S(2)}) collective-permute-start(bf16[32,4096]{1,0:T(8,128)(2,1)} %get-tuple-element.222), channel_id=1, source_target_pairs={{0,2},{1,3},{2,0},{3,1},{4,6},{5,7},{6,4},{7,5},{8,10},{9,11},{10,... | collective-permute-start | bytes 786440 | tf_op jit(solution)/shard_map/ppermute | solution.py:298
  371.8 21.8 %collective-permute-start.49 = (bf16[32,4096]{1,0:T(8,128)(2,1)}, bf16[32,4096]{1,0:T(8,128)(2,1)S(1)}, u32[]{:S(2)}, u32[]{:S(2)}) collective-permute-start(bf16[32,4096]{1,0:T(8,128)(2,1)} %get-tuple-element.223), channel_id=1, source_target_pairs={{0,3},{1,0},{2,1},{3,2},{4,7},{5,4},{6,5},{7,6},{8,11},{9,8},{10,9... | collective-permute-start | bytes 786440 | tf_op jit(solution)/shard_map/ppermute | solution.py:298
  377.1 16.4 %collective-permute-start.50 = (bf16[1,4,32,1024]{3,2,1,0:T(8,128)(2,1)}, bf16[1,4,32,1024]{3,2,1,0:T(8,128)(2,1)S(1)}, u32[]{:S(2)}, u32[]{:S(2)}) collective-permute-start(bf16[1,4,32,1024]{3,2,1,0:T(8,128)(2,1)} %fusion.38), channel_id=1, source_target_pairs={{0,16},{4,12},{8,24},{12,4},{16,0},{20,28},{24,8},{28,20},{1,17},{... | collective-permute-start | bytes 786440 | tf_op jit(solution)/shard_map/ppermute | solution.py:322
  380.9 12.7 %collective-permute-start.43 = (bf16[1,4,32,3072]{3,2,1,0:T(8,128)(2,1)}, bf16[1,4,32,3072]{3,2,1,0:T(8,128)(2,1)S(1)}, u32[]{:S(2)}, u32[]{:S(2)}) collective-permute-start(bf16[1,4,32,3072]{3,2,1,0:T(8,128)(2,1)} %fusion.21), channel_id=1, source_target_pairs={{0,16},{4,12},{8,24},{12,4},{16,0},{20,28},{24,8},{28,20},{1,17},{... | collective-permute-start | bytes 2359304 | tf_op jit(solution)/shard_map/ppermute | solution.py:322
  393.4 11.9 %collective-permute-start.53 = (f32[4,64,256]{2,0,1:T(4,128)S(1)}, f32[4,64,256]{2,0,1:T(4,128)S(1)}, u32[]{:S(2)}, u32[]{:S(2)}) collective-permute-start(f32[4,64,256]{2,0,1:T(4,128)S(1)} %add.620), channel_id=1, source_target_pairs={{0,16},{4,20},{8,24},{12,28},{16,0},{20,4},{24,8},{28,12},{1,17},{... | collective-permute-start | bytes 786440 | tf_op jit(solution)/shard_map/ppermute | solution.py:342
  399.5 30.5 %collective-permute-start.71 = (bf16[1,32,4096]{2,1,0:T(8,128)(2,1)S(1)}, bf16[1,32,4096]{2,1,0:T(8,128)(2,1)S(1)}, u32[]{:S(2)}, u32[]{:S(2)}) collective-permute-start(bf16[1,32,4096]{2,1,0:T(8,128)(2,1)S(1)} %fusion.65), channel_id=1, source_target_pairs={{0,8},{4,20},{8,0},{12,28},{16,24},{20,4},{24,16},{28,12},{1,9},{5... | collective-permute-start | bytes 786440 | tf_op jit(solution)/shard_map/ppermute | solution.py:305
  401.2 30.6 %collective-permute-start.72 = (bf16[1,32,4096]{2,1,0:T(8,128)(2,1)S(1)}, bf16[1,32,4096]{2,1,0:T(8,128)(2,1)S(1)}, u32[]{:S(2)}, u32[]{:S(2)}) collective-permute-start(bf16[1,32,4096]{2,1,0:T(8,128)(2,1)S(1)} %fusion.65), channel_id=1, source_target_pairs={{0,16},{4,12},{8,24},{12,4},{16,0},{20,28},{24,8},{28,20},{1,17},{... | collective-permute-start | bytes 786440 | tf_op jit(solution)/shard_map/ppermute | solution.py:305
  412.3 16.2 %collective-permute-start.58 = (bf16[32,3072]{1,0:T(8,128)(2,1)S(1)}, bf16[32,3072]{1,0:T(8,128)(2,1)S(1)}, u32[]{:S(2)}, u32[]{:S(2)}) collective-permute-start(bf16[32,3072]{1,0:T(8,128)(2,1)S(1)} %get-tuple-element.237), channel_id=1, source_target_pairs={{0,2},{1,3},{2,0},{3,1},{4,6},{5,7},{6,4},{7,5},{8,10},{9,11},{10,... | collective-permute-start | bytes 589832 | tf_op jit(solution)/shard_map/ppermute | solution.py:298
  412.3 16.2 %collective-permute-start.57 = (bf16[32,3072]{1,0:T(8,128)(2,1)S(1)}, bf16[32,3072]{1,0:T(8,128)(2,1)S(1)}, u32[]{:S(2)}, u32[]{:S(2)}) collective-permute-start(bf16[32,3072]{1,0:T(8,128)(2,1)S(1)} %get-tuple-element.236), channel_id=1, source_target_pairs={{0,1},{1,2},{2,3},{3,0},{4,5},{5,6},{6,7},{7,4},{8,9},{9,10},{10,1... | collective-permute-start | bytes 589832 | tf_op jit(solution)/shard_map/ppermute | solution.py:298
  417.5 15.4 %collective-permute-start.73 = (bf16[1,32,4096]{2,1,0:T(8,128)(2,1)S(1)}, bf16[1,32,4096]{2,1,0:T(8,128)(2,1)S(1)}, u32[]{:S(2)}, u32[]{:S(2)}) collective-permute-start(bf16[1,32,4096]{2,1,0:T(8,128)(2,1)S(1)} %fusion.65), channel_id=1, source_target_pairs={{0,24},{4,28},{8,16},{12,20},{16,8},{20,12},{24,0},{28,4},{1,25},{... | collective-permute-start | bytes 786440 | tf_op jit(solution)/shard_map/ppermute | solution.py:305
  428.5 15.2 %collective-permute-start.55 = (f32[64,256]{1,0:T(8,128)S(1)}, f32[64,256]{1,0:T(8,128)S(1)}, u32[]{:S(2)}, u32[]{:S(2)}) collective-permute-start(f32[64,256]{1,0:T(8,128)S(1)} %bitcast.286), channel_id=1, source_target_pairs={{0,2},{1,3},{2,0},{3,1},{4,6},{5,7},{6,4},{7,5},{8,10},{9,11},{10,... | collective-permute-start | bytes 196616 | tf_op jit(solution)/shard_map/ppermute | solution.py:298
  430.0 8.7 %collective-permute-start.62 = (bf16[1,32,3072]{2,1,0:T(8,128)(2,1)S(1)}, bf16[1,32,3072]{2,1,0:T(8,128)(2,1)S(1)}, u32[]{:S(2)}, u32[]{:S(2)}) collective-permute-start(bf16[1,32,3072]{2,1,0:T(8,128)(2,1)S(1)} %fusion.68), channel_id=1, source_target_pairs={{0,24},{4,28},{8,16},{12,20},{16,8},{20,12},{24,0},{28,4},{1,25},{... | collective-permute-start | bytes 589832 | tf_op jit(solution)/shard_map/ppermute | solution.py:305
  431.9 9.1 %collective-permute-start.61 = (bf16[1,32,3072]{2,1,0:T(8,128)(2,1)S(1)}, bf16[1,32,3072]{2,1,0:T(8,128)(2,1)S(1)}, u32[]{:S(2)}, u32[]{:S(2)}) collective-permute-start(bf16[1,32,3072]{2,1,0:T(8,128)(2,1)S(1)} %fusion.68), channel_id=1, source_target_pairs={{0,16},{4,12},{8,24},{12,4},{16,0},{20,28},{24,8},{28,20},{1,17},{... | collective-permute-start | bytes 589832 | tf_op jit(solution)/shard_map/ppermute | solution.py:305
  433.0 10.6 %collective-permute-start.60 = (bf16[1,32,3072]{2,1,0:T(8,128)(2,1)S(1)}, bf16[1,32,3072]{2,1,0:T(8,128)(2,1)S(1)}, u32[]{:S(2)}, u32[]{:S(2)}) collective-permute-start(bf16[1,32,3072]{2,1,0:T(8,128)(2,1)S(1)} %fusion.68), channel_id=1, source_target_pairs={{0,8},{4,20},{8,0},{12,28},{16,24},{20,4},{24,16},{28,12},{1,9},{5... | collective-permute-start | bytes 589832 | tf_op jit(solution)/shard_map/ppermute | solution.py:305
  433.8 10.4 %collective-permute-start.54 = (f32[64,256]{1,0:T(8,128)S(1)}, f32[64,256]{1,0:T(8,128)S(1)}, u32[]{:S(2)}, u32[]{:S(2)}) collective-permute-start(f32[64,256]{1,0:T(8,128)S(1)} %bitcast.285), channel_id=1, source_target_pairs={{0,1},{1,2},{2,3},{3,0},{4,5},{5,6},{6,7},{7,4},{8,9},{9,10},{10,1... | collective-permute-start | bytes 196616 | tf_op jit(solution)/shard_map/ppermute | solution.py:298
  438.7 14.5 %collective-permute-start.75 = (bf16[4,128,1024]{2,1,0:T(8,128)(2,1)S(1)}, bf16[4,128,1024]{2,1,0:T(8,128)(2,1)}, u32[]{:S(2)}, u32[]{:S(2)}) collective-permute-start(bf16[4,128,1024]{2,1,0:T(8,128)(2,1)S(1)} %pad_maximum_fusion.refs_0_), channel_id=1, source_target_pairs={{0,4},{4,0},{8,12},{12,8},{16,20},{20,16},{24,28},{28,24},{1,5},{5... | collective-permute-start | bytes 3145736 | tf_op jit(solution)/shard_map/ppermute | solution.py:294
  443.6 16.7 %collective-permute-start.74 = (bf16[4,32,4096]{2,1,0:T(8,128)(2,1)S(1)}, bf16[4,32,4096]{2,1,0:T(8,128)(2,1)}, u32[]{:S(2)}, u32[]{:S(2)}) collective-permute-start(bf16[4,32,4096]{2,1,0:T(8,128)(2,1)S(1)} %constant_dynamic-update-slice_fusion.refs_0_), channel_id=1, source_target_pairs={{0,4},{4,0},{8,12},{12,8},{16,20},{20,16},{24,28},{28,24},{1,5},{5... | collective-permute-start | bytes 3145736 | tf_op jit(solution)/shard_map/ppermute | solution.py:294
  446.1 10.9 %collective-permute-start.63 = (bf16[4,32,3072]{2,1,0:T(8,128)(2,1)S(1)}, bf16[4,32,3072]{2,1,0:T(8,128)(2,1)}, u32[]{:S(2)}, u32[]{:S(2)}) collective-permute-start(bf16[4,32,3072]{2,1,0:T(8,128)(2,1)S(1)} %pad_maximum_fusion.1.refs_0_), channel_id=1, source_target_pairs={{0,4},{4,0},{8,12},{12,8},{16,20},{20,16},{24,28},{28,24},{1,5},{5... | collective-permute-start | bytes 2359304 | tf_op jit(solution)/shard_map/ppermute | solution.py:294
  (93 other events, 1420.6 us)

commit v9 on v8

--- a/solution.py
+++ b/solution.py
@@ -692,15 +692,16 @@
     )
     run_qkv = plan.total([(plan.rows(normed_one), grad_proj)])
     grad_proj = tick(grad_proj, [run_qkv])
-    grad_norm_one = tick(times_t(grad_proj, full_qkv), [run_qkv])
+    every = [run_fc2, run_fc1, run_out]
+    grad_norm_one = tick(times_t(grad_proj, full_qkv), [run_qkv, run_fc2])
     _, pull_one = jax.vjp(layer_norm, hidden_in, gain_one, bias_one)
     back_in, grad_gain_one, grad_bias_one = pull_one(grad_norm_one)
     grad_in = grad_mid + back_in
     grad_table = jnp.dot(place.T, grad_in, precision=highest)
-    grad_table, activated = tick((grad_table, activated), [run_qkv])
+    grad_table, activated = tick((grad_table, activated), [run_qkv] + every)
     branch_out = jnp.dot(activated, full_fc2, preferred_element_type=f32)
     block_out = jnp.where(valid[:, None], hidden_mid + branch_out, 0.0).astype(bf16)
-    block_out = tick(block_out, [run_qkv, run_fc2, run_fc1, run_out])
+    block_out = tick(block_out, [run_qkv] + every)
 
     def split(block):
         return block.reshape(-1, n_line, shard).transpose(1, 0, 2)

time: 471 us -> 472 us (level)
    ppermute x24, waiting for transfers between devices: 41.2 us -> 54.1 us  [ahead(): lax.ppermute(block, 'fsdp', [(i, (i + step) % n_line) for i in range(n_li...]
    ppermute x12, waiting for transfers between devices: 16.1 us -> 6.52 us  [plane_hops(): return [lax.ppermute(block, 'dp', pairs) for pairs in hops]]
    unnamed x166 -> x174, local copies, waits for them, and re-layouts: 15.5 us -> 17 us
  transfers between devices with their start and end apart: 76 -> 76, of which waited for: 23 -> 23; matrix products, arithmetic and copies ran while one was open for 24% -> 25% of each run, Pallas kernels for 18% -> 19%
where the time goes in v9:
time: 472 us; the launch traced here: 466 us
  waiting for transfers between devices  97.6 us (21%)
  matrix products  95.5 us (20%)
  Pallas kernels  95 us (20%)
  starting transfers between devices  79 us (17%)
  other arithmetic  60.6 us (13%)
  local copies, waits for them, and re-layouts  35.8 us (8%)
    ppermute x24, waiting for transfers between devices, ahead(): lax.ppermute(block, 'fsdp', [(i, (i + step) % n_line) for i in range(n_li...  54.1 us
    ppermute x24, starting transfers between devices, ahead(): lax.ppermute(block, 'fsdp', [(i, (i + step) % n_line) for i in range(n_li...  41.8 us
    pallas_call x2, Pallas kernels, attend_back(): pl.pallas_call(body, grid=(count,), in_specs=pair_specs(rows, pairs, star...  37.7 us
    dot_general x4, matrix products, times_t(): lax.dot_general(left, right, (((1,), (1,)), ((), ())), preferred_element_...  27.7 us
    dot_general x8, matrix products, t_times(): lax.dot_general(left, right, (((0,), (0,)), ((), ())), preferred_element_...  25.7 us
    convert_element_type x8, other arithmetic, reduce_steps(): add_up([term[half:] for term in terms]).astype(jnp.bfloat16)  23.5 us
    pallas_call x3, Pallas kernels, assemble(): pl.pallas_call(body, in_specs=[pl.BlockSpec(memory_space=pltpu.SMEM)] + [...  22.9 us
    unnamed x174, local copies, waits for them, and re-layouts  17 us
  transfers between devices with their start and end apart: 76, of which 23 were waited for; matrix products, arithmetic and copies ran while one was open for 25% of the time, Pallas kernels for 19%

profile of v9, /device:TPU:0, one launch (start us, length us, event | category | flops | bytes accessed | tf_op | source)
XLA Modules:
  0.0 465.7 jit_solution(9605744542997947054)
XLA Ops:
  6.6 3.1 collective-permute-start
  9.7 2.6 collective-permute-start.1
  19.7 11.8 %collective-permute-done.1 = bf16[32,4608]{1,0:T(8,128)(2,1)S(1)} collective-permute-done((bf16[32,4608]{1,0:T(8,128)(2,1)S(1)}, bf16[32,4608]{1,0:T(8,128)(2,1)S(1)}, u32[]{:S(2)}, u32[]{:S(2)}) %collective-permute-start.1) | collective-permute-done | bytes 294944 | tf_op jit(solution)/shard_map/ppermute | solution.py:298
  35.6 6.8 %collective-permute-start.5 = (bf16[32,4096]{1,0:T(8,128)(2,1)S(1)}, bf16[32,4096]{1,0:T(8,128)(2,1)S(1)}, u32[]{:S(2)}, u32[]{:S(2)}) collective-permute-start(bf16[32,4096]{1,0:T(8,128)(2,1)S(1)} %constant_dynamic-slice_fusion.5), channel_id=1, source_target_pairs={{0,1},{1,2},{2,3},{3,0},{4,5},{5,6},{6,7},{7,4},{8,9},{9,10},{10,1... | collective-permute-start | bytes 786440 | tf_op jit(solution)/shard_map/ppermute | solution.py:298
  45.6 5.1 %collective-permute-done.5 = bf16[32,4096]{1,0:T(8,128)(2,1)S(1)} collective-permute-done((bf16[32,4096]{1,0:T(8,128)(2,1)S(1)}, bf16[32,4096]{1,0:T(8,128)(2,1)S(1)}, u32[]{:S(2)}, u32[]{:S(2)}) %collective-permute-start.5) | collective-permute-done | bytes 262176 | tf_op jit(solution)/shard_map/ppermute | solution.py:298
  50.7 9.0 %collective-permute-done.6 = bf16[32,4096]{1,0:T(8,128)(2,1)S(1)} collective-permute-done((bf16[32,4096]{1,0:T(8,128)(2,1)S(1)}, bf16[32,4096]{1,0:T(8,128)(2,1)S(1)}, u32[]{:S(2)}, u32[]{:S(2)}) %collective-permute-start.6) | collective-permute-done | bytes 262176 | tf_op jit(solution)/shard_map/ppermute | solution.py:298
  62.1 9.8 %collective-permute-done.8.refs_5_ = bf16[1,3,32,4096]{3,2,1,0:T(8,128)(2,1)S(1)} collective-permute-done((bf16[1,3,32,4096]{3,2,1,0:T(8,128)(2,1)}, bf16[1,3,32,4096]{3,2,1,0:T(8,128)(2,1)S(1)}, u32[]{:S(2)}, u32[]{:S(2)}) %collective-permute-start.8) | collective-permute-done | bytes 786464 | tf_op jit(solution)/shard_map/ppermute | solution.py:473
  75.7 7.7 %assemble.3 = (bf16[1024,3072]{1,0:T(8,128)(2,1)}, bf16[1024,1024]{1,0:T(8,128)(2,1)}) custom-call(s32[33]{0:T(128)} %pad_add_fusion.1.table_ref, bf16[256,3072]{1,0:T(8,128)(2,1)} %refs_0_.3, bf16[256,1024]{1,0:T(8,128)(2,1)} %refs_1_.1, bf16[1,3,32,4096]{3,2,1,0:T(8,128)(2,1)} %maximum_bitcast_fusion.refs_2_, ...), custom_call_target="tpu_custom_call" | custom-call | tf_op jit(solution)/shard_map/assemble/pallas_call | solution.py:225
  83.4 7.8 %convolution_convert_fusion.4.refs_2_.refs_3_.refs_4_ = bf16[512,3072]{1,0:T(8,128)(2,1)} fusion(bf16[1024,3072]{1,0:T(8,128)(2,1)} %get-tuple-element.160, f32[512,1024]{1,0:T(8,128)S(1)} %get-tuple-element.305, f32[1024]{0:T(1024)S(1)} %bitcast.299, f32[1024]{0:T(1024)S(1)} %bitcast.291, f32[512]{0:T(512)S(1)} %fusion.86, f32[512]{0:T(512)S(1)} %broadcast_multiply_fusion.1), kind=kOutput, calls=%fused_computation.15 | convolution fusion | flops 3225419776 | bytes 11546624 | tf_op jit(solution)/shard_map/dot_general | solution.py:654
  94.1 6.0 %collective-permute-start.9 = (bf16[128,1024]{1,0:T(8,128)(2,1)S(1)}, bf16[128,1024]{1,0:T(8,128)(2,1)S(1)}, u32[]{:S(2)}, u32[]{:S(2)}) collective-permute-start(bf16[128,1024]{1,0:T(8,128)(2,1)S(1)} %copy-done.40), channel_id=1, source_target_pairs={{0,1},{1,2},{2,3},{3,0},{4,5},{5,6},{6,7},{7,4},{8,9},{9,10},{10,1... | collective-permute-start | bytes 786440 | tf_op jit(solution)/shard_map/ppermute | solution.py:298
  100.1 2.4 collective-permute-start.10
  106.8 15.8 %attend.1 = bf16[512,1024]{1,0:T(8,128)(2,1)} custom-call(s32[512,1]{1,0:T(8,128)} %fusion.59.refs_0_, s32[1,512]{1,0:T(1,128)} %broadcast_select_fusion.2.refs_1_, bf16[512,3072]{1,0:T(8,128)(2,1)} %convolution_convert_fusion.4.refs_2_.refs_3_.refs_4_, bf16[512,3072]{1,0:T(8,128)(2,1)} %convolution_convert_fusion.4.refs_2_.refs_3_.refs_4_, ...), custom_call_target="tpu_custom_call" | custom-call | tf_op jit(solution)/shard_map/attend/pallas_call | solution.py:148
  123.2 2.0 maximum_bitcast_fusion.2.refs_1_
  126.6 3.3 fusion.103
  131.9 5.6 %collective-permute-done.19.refs_2_ = bf16[1,3,128,1024]{3,2,1,0:T(8,128)(2,1)} collective-permute-done((bf16[1,3,128,1024]{3,2,1,0:T(8,128)(2,1)}, bf16[1,3,128,1024]{3,2,1,0:T(8,128)(2,1)}, u32[]{:S(2)}, u32[]{:S(2)}) %collective-permute-start.19) | collective-permute-done | bytes 786464 | tf_op jit(solution)/shard_map/ppermute | solution.py:473
  140.5 7.5 %assemble.4 = bf16[1024,4096]{1,0:T(8,128)(2,1)} custom-call(s32[33]{0:T(128)} %pad_add_fusion.1.table_ref, bf16[256,4096]{1,0:T(8,128)(2,1)} %refs_0_.4, bf16[1,3,32,4096]{3,2,1,0:T(8,128)(2,1)} %copy-done.18, bf16[1,3,32,4096]{3,2,1,0:T(8,128)(2,1)} %collective-permute-done.13.refs_2_, bf16[1,3,32,4096]{3,2,1,0:T(8,128)(2,1)} %collective-permute-done.12.refs_3_, ...), custom_call_target="tpu_custom_call" | custom-call | tf_op jit(solution)/shard_map/assemble/pallas_call | solution.py:225
  148.0 10.4 %multiply_convert_fusion.1 = (bf16[512,4096]{1,0:T(8,128)(2,1)}, f32[512,4096]{1,0:T(8,128)}) fusion(f32[4096]{0:T(1024)S(1)} %bitcast.296, bf16[512,1024]{1,0:T(8,128)(2,1)S(1)} %copy-done.27, bf16[1024,4096]{1,0:T(8,128)(2,1)} %assemble.4), kind=kOutput, calls=%fused_computation.9 | convolution fusion | flops 4307550208 | bytes 22036480 | tf_op jit(solution)/shard_map/dot_general | solution.py:661
  158.5 5.5 %column_order.1 = bf16[512,4096]{1,0:T(8,128)(2,1)} custom-call(s32[32]{0:T(128)} %add.550.table_ref, bf16[512,4096]{1,0:T(8,128)(2,1)} %get-tuple-element.240.in_ref), custom_call_target="tpu_custom_call" | custom-call | tf_op jit(solution)/shard_map/column_order/pallas_call | solution.py:245
  164.0 6.0 %convolution_convert_fusion.6 = bf16[2048,1024]{1,0:T(8,128)(2,1)} fusion(bf16[512,4096]{1,0:T(8,128)(2,1)} %column_order.1, bf16[512,1024]{1,0:T(8,128)(2,1)S(1)} %copy-done.16, pred[512]{0:T(512)(128)(4,1)S(1)} %copy-done.70), kind=kOutput, calls=%fused_computation.25 | convolution fusion | flops 2150105088 | bytes 7340544 | tf_op jit(solution)/shard_map/dot_general | solution.py:69
  171.2 3.7 fusion.22
  174.9 2.5 convolution_convert_fusion.5
  182.6 7.6 %assemble.5 = bf16[4096,1024]{1,0:T(8,128)(2,1)} custom-call(s32[33]{0:T(128)} %pad_add_fusion.1.table_ref, bf16[1024,1024]{1,0:T(8,128)(2,1)} %refs_0_.5, bf16[1,3,128,1024]{3,2,1,0:T(8,128)(2,1)} %maximum_bitcast_fusion.2.refs_1_, bf16[1,3,128,1024]{3,2,1,0:T(8,128)(2,1)} %collective-permute-done.19.refs_2_, ...), custom_call_target="tpu_custom_call" | custom-call | tf_op jit(solution)/shard_map/assemble/pallas_call | solution.py:225
  190.3 3.4 fusion.6
  193.7 11.7 %convert_reduce_fusion = (f32[4096]{0:T(1024)}, bf16[512,4096]{1,0:T(8,128)(2,1)S(1)}) fusion(f32[512,4096]{1,0:T(8,128)} %get-tuple-element.309, f32[4096]{0:T(1024)S(1)} %bitcast.297, bf16[4096,1024]{1,0:T(8,128)(2,1)} %assemble.5, bf16[512,1024]{1,0:T(8,128)(2,1)S(1)} %copy-done.16, pred[512]{0:T(512)(128)(4,1)S(1)} %copy-done.70), kind=kOutput, calls=%fused_computation.7 | convolution fusion | flops 4326944768 | bytes 22053376 | tf_op jit(solution)/shard_map/dot_general | solution.py:65
  205.3 5.7 %convolution_convert_fusion.1 = bf16[512,4096]{1,0:T(8,128)(2,1)} fusion(bf16[512,4096]{1,0:T(8,128)(2,1)S(1)} %get-tuple-element.184, bf16[512,1024]{1,0:T(8,128)(2,1)} %fusion.22), kind=kOutput, calls=%fused_computation.12 | convolution fusion | flops 2149580800 | bytes 8912896 | tf_op jit(solution)/shard_map/dot_general | solution.py:69
  212.1 6.8 %multiply_reduce_fusion = (f32[1024]{0:T(1024)}, f32[512]{0:T(512)S(1)}, f32[1024]{0:T(1024)}, f32[512,1024]{1,0:T(8,128)}) fusion(f32[512,1024]{1,0:T(8,128)S(1)} %copy-done.1, f32[512]{0:T(512)S(1)} %fusion.87, f32[512]{0:T(512)S(1)} %broadcast_multiply_fusion, f32[1024]{0:T(1024)S(1)} %bitcast.289, bf16[512,4096]{1,0:T(8,128)(2,1)S(1)} %get-tuple-element.184, ...), kind=kOutput, calls=%fused_computation.38 | convolution fusion | flops 4299159040 | bytes 16795648 | tf_op jit(solution)/shard_map/dot_general | solution.py:65
  218.9 2.4 fusion.97
  221.3 2.5 convolution_convert_fusion
  223.8 2.0 copy-done.5
  227.8 3.9 fusion.5
  234.5 2.0 copy-done.75
  236.5 2.7 convolution_convert_fusion.7.refs_5_
  240.9 3.2 fusion.16
  245.6 18.8 %attend_back.2 = bf16[512,1536]{1,0:T(8,128)(2,1)} custom-call(s32[512,1]{1,0:T(8,128)} %fusion.59.refs_0_, s32[1,512]{1,0:T(1,128)} %broadcast_select_fusion.2.refs_1_, bf16[512,3072]{1,0:T(8,128)(2,1)} %convolution_convert_fusion.4.refs_2_.refs_3_.refs_4_, bf16[512,3072]{1,0:T(8,128)(2,1)} %convolution_convert_fusion.4.refs_2_.refs_3_.refs_4_, ...), custom_call_target="tpu_custom_call" | custom-call | tf_op jit(solution)/shard_map/attend_back/pallas_call | solution.py:167
  266.2 4.2 collective-permute-done.33
  271.4 3.2 fusion.46
  274.6 3.0 fusion.14
  277.6 2.1 fusion.26
  281.7 2.1 collective-permute-start.36
  284.4 1.9 collective-permute-start.38
  286.3 2.5 fusion.24
  288.7 18.9 %attend_back.3 = bf16[512,1536]{1,0:T(8,128)(2,1)} custom-call(s32[512,1]{1,0:T(8,128)} %fusion.59.refs_0_, s32[1,512]{1,0:T(1,128)} %broadcast_select_fusion.2.refs_1_, bf16[512,3072]{1,0:T(8,128)(2,1)} %convolution_convert_fusion.4.refs_2_.refs_3_.refs_4_, bf16[512,3072]{1,0:T(8,128)(2,1)} %convolution_convert_fusion.4.refs_2_.refs_3_.refs_4_, ...), custom_call_target="tpu_custom_call" | custom-call | tf_op jit(solution)/shard_map/attend_back/pallas_call | solution.py:167
  307.7 3.2 fusion.39
  310.9 2.0 fusion.38
  315.9 3.7 convolution_convert_fusion.3
  325.7 6.5 %fusion.104 = f32[512,1024]{1,0:T(8,128)S(1)} fusion(bf16[512,3072]{1,0:T(8,128)(2,1)} %copy-done.7, bf16[1024,3072]{1,0:T(8,128)(2,1)} %get-tuple-element.160), kind=kOutput, calls=%fused_computation.305 | convolution fusion | flops 3221225472 | bytes 11534336 | tf_op jit(solution)/shard_map/dot_general | solution.py:65
  336.4 2.0 collective-permute-start.48
  340.3 3.2 fusion.10
  353.3 3.9 collective-permute-done.48
  357.2 2.5 collective-permute-done.50
  359.8 9.3 %collective-permute-done.45 = bf16[2,4,32,3072]{3,2,1,0:T(8,128)(2,1)} collective-permute-done((bf16[2,4,32,3072]{3,2,1,0:T(8,128)(2,1)}, bf16[2,4,32,3072]{3,2,1,0:T(8,128)(2,1)}, u32[]{:S(2)}, u32[]{:S(2)}) %collective-permute-start.45) | collective-permute-done | bytes 1572896 | tf_op jit(solution)/shard_map/ppermute | solution.py:322
  370.8 2.6 fusion.21
  373.5 2.4 fusion.65
  383.1 2.7 collective-permute-done.55
  390.6 10.1 %select_convert_fusion = bf16[512,1024]{1,0:T(8,128)(2,1)} fusion(f32[512,1024]{1,0:T(8,128)S(1)} %copy-done.2, bf16[512,4096]{1,0:T(8,128)(2,1)} %get-tuple-element.240.in_ref, bf16[4096,1024]{1,0:T(8,128)(2,1)} %assemble.5, pred[512]{0:T(512)(128)(4,1)S(1)} %copy-done.72), kind=kOutput, calls=%fused_computation.40 | convolution fusion | flops 4296540160 | bytes 15729152 | tf_op jit(solution)/shard_map/dot_general | solution.py:702
  400.7 4.0 finish.7
  408.2 2.3 pad_maximum_fusion.1.refs_0_
  416.4 4.2 collective-permute-done.66
  421.5 11.5 %collective-permute-done.65 = bf16[32,3072]{1,0:T(8,128)(2,1)S(1)} collective-permute-done((bf16[32,3072]{1,0:T(8,128)(2,1)S(1)}, bf16[32,3072]{1,0:T(8,128)(2,1)S(1)}, u32[]{:S(2)}, u32[]{:S(2)}) %collective-permute-start.65) | collective-permute-done | bytes 196640 | tf_op jit(solution)/shard_map/ppermute | solution.py:298
  438.0 5.1 %collective-permute-done.69 = bf16[1,32,3072]{2,1,0:T(8,128)(2,1)S(1)} collective-permute-done((bf16[1,32,3072]{2,1,0:T(8,128)(2,1)S(1)}, bf16[1,32,3072]{2,1,0:T(8,128)(2,1)S(1)}, u32[]{:S(2)}, u32[]{:S(2)}) %collective-permute-start.69) | collective-permute-done | bytes 196640 | tf_op jit(solution)/shard_map/ppermute | solution.py:305
  448.5 3.3 collective-permute-done.61
  454.4 2.1 finish.5
  457.5 3.8 finish.6
  462.2 3.2 finish.4
  (414 shorter events, 124.9 us)
Async XLA Ops:
  6.6 13.1 %collective-permute-start = (bf16[32,4608]{1,0:T(8,128)(2,1)S(1)}, bf16[32,4608]{1,0:T(8,128)(2,1)S(1)}, u32[]{:S(2)}, u32[]{:S(2)}) collective-permute-start(bf16[32,4608]{1,0:T(8,128)(2,1)S(1)} %pad_maximum_fusion.3), channel_id=1, source_target_pairs={{0,1},{1,2},{2,3},{3,0},{4,5},{5,6},{6,7},{7,4},{8,9},{9,10},{10,1... | collective-permute-start | bytes 884744 | tf_op jit(solution)/shard_map/ppermute | solution.py:298
  9.7 21.8 %collective-permute-start.1 = (bf16[32,4608]{1,0:T(8,128)(2,1)S(1)}, bf16[32,4608]{1,0:T(8,128)(2,1)S(1)}, u32[]{:S(2)}, u32[]{:S(2)}) collective-permute-start(bf16[32,4608]{1,0:T(8,128)(2,1)S(1)} %pad_maximum_fusion.3), channel_id=1, source_target_pairs={{0,2},{1,3},{2,0},{3,1},{4,6},{5,7},{6,4},{7,5},{8,10},{9,11},{10,... | collective-permute-start | bytes 884744 | tf_op jit(solution)/shard_map/ppermute | solution.py:298
  12.3 19.2 %collective-permute-start.2 = (bf16[32,4608]{1,0:T(8,128)(2,1)S(1)}, bf16[32,4608]{1,0:T(8,128)(2,1)S(1)}, u32[]{:S(2)}, u32[]{:S(2)}) collective-permute-start(bf16[32,4608]{1,0:T(8,128)(2,1)S(1)} %pad_maximum_fusion.3), channel_id=1, source_target_pairs={{0,3},{1,0},{2,1},{3,2},{4,7},{5,4},{6,5},{7,6},{8,11},{9,8},{10,9... | collective-permute-start | bytes 884744 | tf_op jit(solution)/shard_map/ppermute | solution.py:298
  32.6 29.6 %collective-permute-start.3 = (bf16[1,3,32,4096]{3,2,1,0:T(8,128)(2,1)}, bf16[1,3,32,4096]{3,2,1,0:T(8,128)(2,1)}, u32[]{:S(2)}, u32[]{:S(2)}) collective-permute-start(bf16[1,3,32,4096]{3,2,1,0:T(8,128)(2,1)} %maximum_bitcast_fusion.refs_2_), channel_id=1, source_target_pairs={{0,16},{4,12},{8,24},{12,4},{16,0},{20,28},{24,8},{28,20},{1,17},{... | collective-permute-start | bytes 2359304 | tf_op jit(solution)/shard_map/ppermute | solution.py:473
  34.1 25.5 %collective-permute-start.4 = (bf16[1,3,32,4096]{3,2,1,0:T(8,128)(2,1)}, bf16[1,3,32,4096]{3,2,1,0:T(8,128)(2,1)}, u32[]{:S(2)}, u32[]{:S(2)}) collective-permute-start(bf16[1,3,32,4096]{3,2,1,0:T(8,128)(2,1)} %maximum_bitcast_fusion.refs_2_), channel_id=1, source_target_pairs={{0,8},{4,20},{8,0},{12,28},{16,24},{20,4},{24,16},{28,12},{1,9},{5... | collective-permute-start | bytes 2359304 | tf_op jit(solution)/shard_map/ppermute | solution.py:473
  35.6 15.1 %collective-permute-start.5 = (bf16[32,4096]{1,0:T(8,128)(2,1)S(1)}, bf16[32,4096]{1,0:T(8,128)(2,1)S(1)}, u32[]{:S(2)}, u32[]{:S(2)}) collective-permute-start(bf16[32,4096]{1,0:T(8,128)(2,1)S(1)} %constant_dynamic-slice_fusion.5), channel_id=1, source_target_pairs={{0,1},{1,2},{2,3},{3,0},{4,5},{5,6},{6,7},{7,4},{8,9},{9,10},{10,1... | collective-permute-start | bytes 786440 | tf_op jit(solution)/shard_map/ppermute | solution.py:298
  42.4 17.3 %collective-permute-start.6 = (bf16[32,4096]{1,0:T(8,128)(2,1)S(1)}, bf16[32,4096]{1,0:T(8,128)(2,1)S(1)}, u32[]{:S(2)}, u32[]{:S(2)}) collective-permute-start(bf16[32,4096]{1,0:T(8,128)(2,1)S(1)} %constant_dynamic-slice_fusion.5), channel_id=1, source_target_pairs={{0,2},{1,3},{2,0},{3,1},{4,6},{5,7},{6,4},{7,5},{8,10},{9,11},{10,... | collective-permute-start | bytes 786440 | tf_op jit(solution)/shard_map/ppermute | solution.py:298
  44.0 15.7 %collective-permute-start.7 = (bf16[32,4096]{1,0:T(8,128)(2,1)S(1)}, bf16[32,4096]{1,0:T(8,128)(2,1)S(1)}, u32[]{:S(2)}, u32[]{:S(2)}) collective-permute-start(bf16[32,4096]{1,0:T(8,128)(2,1)S(1)} %constant_dynamic-slice_fusion.5), channel_id=1, source_target_pairs={{0,3},{1,0},{2,1},{3,2},{4,7},{5,4},{6,5},{7,6},{8,11},{9,8},{10,9... | collective-permute-start | bytes 786440 | tf_op jit(solution)/shard_map/ppermute | solution.py:298
  50.7 23.1 %collective-permute-start.14 = (bf16[1,3,32,4096]{3,2,1,0:T(8,128)(2,1)}, bf16[1,3,32,4096]{3,2,1,0:T(8,128)(2,1)}, u32[]{:S(2)}, u32[]{:S(2)}) collective-permute-start(bf16[1,3,32,4096]{3,2,1,0:T(8,128)(2,1)} %maximum_bitcast_fusion.refs_2_), channel_id=1, source_target_pairs={{0,4},{4,0},{8,12},{12,8},{16,20},{20,16},{24,28},{28,24},{1,5},{5... | collective-permute-start | bytes 2359304 | tf_op jit(solution)/shard_map/ppermute | solution.py:294
  59.7 12.3 %collective-permute-start.8 = (bf16[1,3,32,4096]{3,2,1,0:T(8,128)(2,1)}, bf16[1,3,32,4096]{3,2,1,0:T(8,128)(2,1)S(1)}, u32[]{:S(2)}, u32[]{:S(2)}) collective-permute-start(bf16[1,3,32,4096]{3,2,1,0:T(8,128)(2,1)} %collective-permute-done.4.refs_3_), channel_id=1, source_target_pairs={{0,16},{4,12},{8,24},{12,4},{16,0},{20,28},{24,8},{28,20},{1,17},{... | collective-permute-start | bytes 2359304 | tf_op jit(solution)/shard_map/ppermute | solution.py:473
  62.1 12.3 %collective-permute-start.15 = (bf16[1,3,32,4096]{3,2,1,0:T(8,128)(2,1)}, bf16[1,3,32,4096]{3,2,1,0:T(8,128)(2,1)}, u32[]{:S(2)}, u32[]{:S(2)}) collective-permute-start(bf16[1,3,32,4096]{3,2,1,0:T(8,128)(2,1)} %collective-permute-done.4.refs_3_), channel_id=1, source_target_pairs={{0,4},{4,0},{8,12},{12,8},{16,20},{20,16},{24,28},{28,24},{1,5},{5... | collective-permute-start | bytes 2359304 | tf_op jit(solution)/shard_map/ppermute | solution.py:294
  73.2 49.4 %collective-permute-start.12 = (bf16[1,3,32,4096]{3,2,1,0:T(8,128)(2,1)S(1)}, bf16[1,3,32,4096]{3,2,1,0:T(8,128)(2,1)}, u32[]{:S(2)}, u32[]{:S(2)}) collective-permute-start(bf16[1,3,32,4096]{3,2,1,0:T(8,128)(2,1)S(1)} %maximum_bitcast_fusion.1.refs_1_), channel_id=1, source_target_pairs={{0,16},{4,12},{8,24},{12,4},{16,0},{20,28},{24,8},{28,20},{1,17},{... | collective-permute-start | bytes 2359304 | tf_op jit(solution)/shard_map/ppermute | solution.py:473
  73.8 19.0 %collective-permute-start.13 = (bf16[1,3,32,4096]{3,2,1,0:T(8,128)(2,1)S(1)}, bf16[1,3,32,4096]{3,2,1,0:T(8,128)(2,1)}, u32[]{:S(2)}, u32[]{:S(2)}) collective-permute-start(bf16[1,3,32,4096]{3,2,1,0:T(8,128)(2,1)S(1)} %maximum_bitcast_fusion.1.refs_1_), channel_id=1, source_target_pairs={{0,8},{4,20},{8,0},{12,28},{16,24},{20,4},{24,16},{28,12},{1,9},{5... | collective-permute-start | bytes 2359304 | tf_op jit(solution)/shard_map/ppermute | solution.py:473
  92.8 29.9 %collective-permute-start.18 = (bf16[1,3,32,4096]{3,2,1,0:T(8,128)(2,1)}, bf16[1,3,32,4096]{3,2,1,0:T(8,128)(2,1)}, u32[]{:S(2)}, u32[]{:S(2)}) collective-permute-start(bf16[1,3,32,4096]{3,2,1,0:T(8,128)(2,1)} %collective-permute-done.13.refs_2_), channel_id=1, source_target_pairs={{0,16},{4,12},{8,24},{12,4},{16,0},{20,28},{24,8},{28,20},{1,17},{... | collective-permute-start | bytes 2359304 | tf_op jit(solution)/shard_map/ppermute | solution.py:473
  94.1 29.1 %collective-permute-start.9 = (bf16[128,1024]{1,0:T(8,128)(2,1)S(1)}, bf16[128,1024]{1,0:T(8,128)(2,1)S(1)}, u32[]{:S(2)}, u32[]{:S(2)}) collective-permute-start(bf16[128,1024]{1,0:T(8,128)(2,1)S(1)} %copy-done.40), channel_id=1, source_target_pairs={{0,1},{1,2},{2,3},{3,0},{4,5},{5,6},{6,7},{7,4},{8,9},{9,10},{10,1... | collective-permute-start | bytes 786440 | tf_op jit(solution)/shard_map/ppermute | solution.py:298
  100.1 23.1 %collective-permute-start.10 = (bf16[128,1024]{1,0:T(8,128)(2,1)S(1)}, bf16[128,1024]{1,0:T(8,128)(2,1)}, u32[]{:S(2)}, u32[]{:S(2)}) collective-permute-start(bf16[128,1024]{1,0:T(8,128)(2,1)S(1)} %copy-done.40), channel_id=1, source_target_pairs={{0,2},{1,3},{2,0},{3,1},{4,6},{5,7},{6,4},{7,5},{8,10},{9,11},{10,... | collective-permute-start | bytes 786440 | tf_op jit(solution)/shard_map/ppermute | solution.py:298
  102.5 20.7 %collective-permute-start.11 = (bf16[128,1024]{1,0:T(8,128)(2,1)S(1)}, bf16[128,1024]{1,0:T(8,128)(2,1)}, u32[]{:S(2)}, u32[]{:S(2)}) collective-permute-start(bf16[128,1024]{1,0:T(8,128)(2,1)S(1)} %copy-done.40), channel_id=1, source_target_pairs={{0,3},{1,0},{2,1},{3,2},{4,7},{5,4},{6,5},{7,6},{8,11},{9,8},{10,9... | collective-permute-start | bytes 786440 | tf_op jit(solution)/shard_map/ppermute | solution.py:298
  122.6 16.5 %collective-permute-start.22 = (bf16[1,3,32,4096]{3,2,1,0:T(8,128)(2,1)S(1)}, bf16[1,3,32,4096]{3,2,1,0:T(8,128)(2,1)S(1)}, u32[]{:S(2)}, u32[]{:S(2)}) collective-permute-start(bf16[1,3,32,4096]{3,2,1,0:T(8,128)(2,1)S(1)} %maximum_bitcast_fusion.1.refs_1_), channel_id=1, source_target_pairs={{0,4},{4,0},{8,12},{12,8},{16,20},{20,16},{24,28},{28,24},{1,5},{5... | collective-permute-start | bytes 2359304 | tf_op jit(solution)/shard_map/ppermute | solution.py:294
  122.7 17.8 %collective-permute-start.23 = (bf16[1,3,32,4096]{3,2,1,0:T(8,128)(2,1)}, bf16[1,3,32,4096]{3,2,1,0:T(8,128)(2,1)}, u32[]{:S(2)}, u32[]{:S(2)}) collective-permute-start(bf16[1,3,32,4096]{3,2,1,0:T(8,128)(2,1)} %collective-permute-done.13.refs_2_), channel_id=1, source_target_pairs={{0,4},{4,0},{8,12},{12,8},{16,20},{20,16},{24,28},{28,24},{1,5},{5... | collective-permute-start | bytes 2359304 | tf_op jit(solution)/shard_map/ppermute | solution.py:294
  125.2 12.3 %collective-permute-start.19 = (bf16[1,3,128,1024]{3,2,1,0:T(8,128)(2,1)}, bf16[1,3,128,1024]{3,2,1,0:T(8,128)(2,1)}, u32[]{:S(2)}, u32[]{:S(2)}) collective-permute-start(bf16[1,3,128,1024]{3,2,1,0:T(8,128)(2,1)} %maximum_bitcast_fusion.2.refs_1_), channel_id=1, source_target_pairs={{0,8},{4,20},{8,0},{12,28},{16,24},{20,4},{24,16},{28,12},{1,9},{5... | collective-permute-start | bytes 2359304 | tf_op jit(solution)/shard_map/ppermute | solution.py:473
  125.8 14.7 %collective-permute-start.24 = (bf16[1,3,32,4096]{3,2,1,0:T(8,128)(2,1)}, bf16[1,3,32,4096]{3,2,1,0:T(8,128)(2,1)}, u32[]{:S(2)}, u32[]{:S(2)}) collective-permute-start(bf16[1,3,32,4096]{3,2,1,0:T(8,128)(2,1)} %collective-permute-done.12.refs_3_), channel_id=1, source_target_pairs={{0,4},{4,0},{8,12},{12,8},{16,20},{20,16},{24,28},{28,24},{1,5},{5... | collective-permute-start | bytes 2359304 | tf_op jit(solution)/shard_map/ppermute | solution.py:294
  126.6 13.9 %collective-permute-start.25 = (bf16[1,3,32,4096]{3,2,1,0:T(8,128)(2,1)}, bf16[1,3,32,4096]{3,2,1,0:T(8,128)(2,1)}, u32[]{:S(2)}, u32[]{:S(2)}) collective-permute-start(bf16[1,3,32,4096]{3,2,1,0:T(8,128)(2,1)} %collective-permute-done.18.refs_4_), channel_id=1, source_target_pairs={{0,4},{4,0},{8,12},{12,8},{16,20},{20,16},{24,28},{28,24},{1,5},{5... | collective-permute-start | bytes 2359304 | tf_op jit(solution)/shard_map/ppermute | solution.py:294
  137.5 20.9 %collective-permute-start.20 = (bf16[1,3,128,1024]{3,2,1,0:T(8,128)(2,1)}, bf16[1,3,128,1024]{3,2,1,0:T(8,128)(2,1)}, u32[]{:S(2)}, u32[]{:S(2)}) collective-permute-start(bf16[1,3,128,1024]{3,2,1,0:T(8,128)(2,1)} %maximum_bitcast_fusion.2.refs_1_), channel_id=1, source_target_pairs={{0,16},{4,12},{8,24},{12,4},{16,0},{20,28},{24,8},{28,20},{1,17},{... | collective-permute-start | bytes 2359304 | tf_op jit(solution)/shard_map/ppermute | solution.py:473
  140.0 18.5 %collective-permute-start.21 = (bf16[1,3,128,1024]{3,2,1,0:T(8,128)(2,1)}, bf16[1,3,128,1024]{3,2,1,0:T(8,128)(2,1)}, u32[]{:S(2)}, u32[]{:S(2)}) collective-permute-start(bf16[1,3,128,1024]{3,2,1,0:T(8,128)(2,1)} %collective-permute-done.19.refs_2_), channel_id=1, source_target_pairs={{0,16},{4,12},{8,24},{12,4},{16,0},{20,28},{24,8},{28,20},{1,17},{... | collective-permute-start | bytes 2359304 | tf_op jit(solution)/shard_map/ppermute | solution.py:473
  170.0 20.3 %collective-permute-start.30 = (bf16[4,4,128,1024]{3,2,1,0:T(8,128)(2,1)}, bf16[4,4,128,1024]{3,2,1,0:T(8,128)(2,1)}, u32[]{:S(2)}, u32[]{:S(2)}) collective-permute-start(bf16[4,4,128,1024]{3,2,1,0:T(8,128)(2,1)} %bitcast.24), channel_id=1, source_target_pairs={{0,4},{4,0},{8,12},{12,8},{16,20},{20,16},{24,28},{28,24},{1,5},{5... | collective-permute-start | bytes 12582920 | tf_op jit(solution)/shard_map/ppermute | solution.py:294
  170.1 9.9 %collective-permute-start.26 = (bf16[1,3,128,1024]{3,2,1,0:T(8,128)(2,1)}, bf16[1,3,128,1024]{3,2,1,0:T(8,128)(2,1)S(1)}, u32[]{:S(2)}, u32[]{:S(2)}) collective-permute-start(bf16[1,3,128,1024]{3,2,1,0:T(8,128)(2,1)} %maximum_bitcast_fusion.2.refs_1_), channel_id=1, source_target_pairs={{0,4},{4,0},{8,12},{12,8},{16,20},{20,16},{24,28},{28,24},{1,5},{5... | collective-permute-start | bytes 2359304 | tf_op jit(solution)/shard_map/ppermute | solution.py:294
  170.6 10.2 %collective-permute-start.27 = (bf16[1,3,128,1024]{3,2,1,0:T(8,128)(2,1)}, bf16[1,3,128,1024]{3,2,1,0:T(8,128)(2,1)S(1)}, u32[]{:S(2)}, u32[]{:S(2)}) collective-permute-start(bf16[1,3,128,1024]{3,2,1,0:T(8,128)(2,1)} %collective-permute-done.19.refs_2_), channel_id=1, source_target_pairs={{0,4},{4,0},{8,12},{12,8},{16,20},{20,16},{24,28},{28,24},{1,5},{5... | collective-permute-start | bytes 2359304 | tf_op jit(solution)/shard_map/ppermute | solution.py:294
  170.7 11.0 %collective-permute-start.28 = (bf16[1,3,128,1024]{3,2,1,0:T(8,128)(2,1)}, bf16[1,3,128,1024]{3,2,1,0:T(8,128)(2,1)S(1)}, u32[]{:S(2)}, u32[]{:S(2)}) collective-permute-start(bf16[1,3,128,1024]{3,2,1,0:T(8,128)(2,1)} %collective-permute-done.20.refs_3_), channel_id=1, source_target_pairs={{0,4},{4,0},{8,12},{12,8},{16,20},{20,16},{24,28},{28,24},{1,5},{5... | collective-permute-start | bytes 2359304 | tf_op jit(solution)/shard_map/ppermute | solution.py:294
  171.2 11.5 %collective-permute-start.29 = (bf16[1,3,128,1024]{3,2,1,0:T(8,128)(2,1)}, bf16[1,3,128,1024]{3,2,1,0:T(8,128)(2,1)}, u32[]{:S(2)}, u32[]{:S(2)}) collective-permute-start(bf16[1,3,128,1024]{3,2,1,0:T(8,128)(2,1)} %collective-permute-done.21.refs_4_), channel_id=1, source_target_pairs={{0,4},{4,0},{8,12},{12,8},{16,20},{20,16},{24,28},{28,24},{1,5},{5... | collective-permute-start | bytes 2359304 | tf_op jit(solution)/shard_map/ppermute | solution.py:294
  211.1 15.2 %collective-permute-start.31 = (bf16[4,4,32,4096]{3,2,1,0:T(8,128)(2,1)}, bf16[4,4,32,4096]{3,2,1,0:T(8,128)(2,1)}, u32[]{:S(2)}, u32[]{:S(2)}) collective-permute-start(bf16[4,4,32,4096]{3,2,1,0:T(8,128)(2,1)} %bitcast.26), channel_id=1, source_target_pairs={{0,4},{4,0},{8,12},{12,8},{16,20},{20,16},{24,28},{28,24},{1,5},{5... | collective-permute-start | bytes 12582920 | tf_op jit(solution)/shard_map/ppermute | solution.py:294
  211.6 27.6 %collective-permute-start.32 = (bf16[2,4,128,1024]{3,2,1,0:T(8,128)(2,1)S(1)}, bf16[2,4,128,1024]{3,2,1,0:T(8,128)(2,1)}, u32[]{:S(2)}, u32[]{:S(2)}) collective-permute-start(bf16[2,4,128,1024]{3,2,1,0:T(8,128)(2,1)S(1)} %fusion.6), channel_id=1, source_target_pairs={{0,8},{4,20},{8,0},{12,28},{16,24},{20,4},{24,16},{28,12},{1,9},{5... | collective-permute-start | bytes 6291464 | tf_op jit(solution)/shard_map/ppermute | solution.py:322
  231.7 39.7 %collective-permute-start.34 = (bf16[2,4,32,4096]{3,2,1,0:T(8,128)(2,1)}, bf16[2,4,32,4096]{3,2,1,0:T(8,128)(2,1)}, u32[]{:S(2)}, u32[]{:S(2)}) collective-permute-start(bf16[2,4,32,4096]{3,2,1,0:T(8,128)(2,1)} %fusion.5), channel_id=1, source_target_pairs={{0,8},{4,20},{8,0},{12,28},{16,24},{20,4},{24,16},{28,12},{1,9},{5... | collective-permute-start | bytes 6291464 | tf_op jit(solution)/shard_map/ppermute | solution.py:322
  244.1 26.3 %collective-permute-start.33 = (bf16[1,4,128,1024]{3,2,1,0:T(8,128)(2,1)}, bf16[1,4,128,1024]{3,2,1,0:T(8,128)(2,1)}, u32[]{:S(2)}, u32[]{:S(2)}) collective-permute-start(bf16[1,4,128,1024]{3,2,1,0:T(8,128)(2,1)} %fusion.16), channel_id=1, source_target_pairs={{0,16},{4,12},{8,24},{12,4},{16,0},{20,28},{24,8},{28,20},{1,17},{... | collective-permute-start | bytes 3145736 | tf_op jit(solution)/shard_map/ppermute | solution.py:322
  245.6 24.9 %collective-permute-start.35 = (bf16[4,4,32,1024]{3,2,1,0:T(8,128)(2,1)}, bf16[4,4,32,1024]{3,2,1,0:T(8,128)(2,1)}, u32[]{:S(2)}, u32[]{:S(2)}) collective-permute-start(bf16[4,4,32,1024]{3,2,1,0:T(8,128)(2,1)} %bitcast.29), channel_id=1, source_target_pairs={{0,4},{4,0},{8,12},{12,8},{16,20},{20,16},{24,28},{28,24},{1,5},{5... | collective-permute-start | bytes 3145736 | tf_op jit(solution)/shard_map/ppermute | solution.py:294
  279.7 27.9 %collective-permute-start.39 = (bf16[1,4,32,4096]{3,2,1,0:T(8,128)(2,1)}, bf16[1,4,32,4096]{3,2,1,0:T(8,128)(2,1)S(1)}, u32[]{:S(2)}, u32[]{:S(2)}) collective-permute-start(bf16[1,4,32,4096]{3,2,1,0:T(8,128)(2,1)} %fusion.14), channel_id=1, source_target_pairs={{0,16},{4,12},{8,24},{12,4},{16,0},{20,28},{24,8},{28,20},{1,17},{... | collective-permute-start | bytes 3145736 | tf_op jit(solution)/shard_map/ppermute | solution.py:322
  281.2 26.4 %collective-permute-start.40 = (bf16[2,4,32,1024]{3,2,1,0:T(8,128)(2,1)}, bf16[2,4,32,1024]{3,2,1,0:T(8,128)(2,1)}, u32[]{:S(2)}, u32[]{:S(2)}) collective-permute-start(bf16[2,4,32,1024]{3,2,1,0:T(8,128)(2,1)} %fusion.26), channel_id=1, source_target_pairs={{0,8},{4,20},{8,0},{12,28},{16,24},{20,4},{24,16},{28,12},{1,9},{5... | collective-permute-start | bytes 1572872 | tf_op jit(solution)/shard_map/ppermute | solution.py:322
  281.7 25.9 %collective-permute-start.36 = (bf16[128,1024]{1,0:T(8,128)(2,1)}, bf16[128,1024]{1,0:T(8,128)(2,1)}, u32[]{:S(2)}, u32[]{:S(2)}) collective-permute-start(bf16[128,1024]{1,0:T(8,128)(2,1)} %get-tuple-element.203), channel_id=1, source_target_pairs={{0,1},{1,2},{2,3},{3,0},{4,5},{5,6},{6,7},{7,4},{8,9},{9,10},{10,1... | collective-permute-start | bytes 786440 | tf_op jit(solution)/shard_map/ppermute | solution.py:298
  283.9 23.7 %collective-permute-start.37 = (bf16[128,1024]{1,0:T(8,128)(2,1)}, bf16[128,1024]{1,0:T(8,128)(2,1)}, u32[]{:S(2)}, u32[]{:S(2)}) collective-permute-start(bf16[128,1024]{1,0:T(8,128)(2,1)} %get-tuple-element.204), channel_id=1, source_target_pairs={{0,2},{1,3},{2,0},{3,1},{4,6},{5,7},{6,4},{7,5},{8,10},{9,11},{10,... | collective-permute-start | bytes 786440 | tf_op jit(solution)/shard_map/ppermute | solution.py:298
  284.4 23.3 %collective-permute-start.38 = (bf16[128,1024]{1,0:T(8,128)(2,1)}, bf16[128,1024]{1,0:T(8,128)(2,1)}, u32[]{:S(2)}, u32[]{:S(2)}) collective-permute-start(bf16[128,1024]{1,0:T(8,128)(2,1)} %get-tuple-element.205), channel_id=1, source_target_pairs={{0,3},{1,0},{2,1},{3,2},{4,7},{5,4},{6,5},{7,6},{8,11},{9,8},{10,9... | collective-permute-start | bytes 786440 | tf_op jit(solution)/shard_map/ppermute | solution.py:298
  319.6 20.7 %collective-permute-start.41 = (bf16[4,4,32,3072]{3,2,1,0:T(8,128)(2,1)}, bf16[4,4,32,3072]{3,2,1,0:T(8,128)(2,1)}, u32[]{:S(2)}, u32[]{:S(2)}) collective-permute-start(bf16[4,4,32,3072]{3,2,1,0:T(8,128)(2,1)} %bitcast.55), channel_id=1, source_target_pairs={{0,4},{4,0},{8,12},{12,8},{16,20},{20,16},{24,28},{28,24},{1,5},{5... | collective-permute-start | bytes 9437192 | tf_op jit(solution)/shard_map/ppermute | solution.py:294
  322.2 14.2 %collective-permute-start.42 = (bf16[1,128,1024]{2,1,0:T(8,128)(2,1)S(1)}, bf16[1,128,1024]{2,1,0:T(8,128)(2,1)S(1)}, u32[]{:S(2)}, u32[]{:S(2)}) collective-permute-start(bf16[1,128,1024]{2,1,0:T(8,128)(2,1)S(1)} %fusion.64), channel_id=1, source_target_pairs={{0,8},{4,20},{8,0},{12,28},{16,24},{20,4},{24,16},{28,12},{1,9},{5... | collective-permute-start | bytes 786440 | tf_op jit(solution)/shard_map/ppermute | solution.py:305
  323.9 14.5 %collective-permute-start.43 = (bf16[1,128,1024]{2,1,0:T(8,128)(2,1)S(1)}, bf16[1,128,1024]{2,1,0:T(8,128)(2,1)S(1)}, u32[]{:S(2)}, u32[]{:S(2)}) collective-permute-start(bf16[1,128,1024]{2,1,0:T(8,128)(2,1)S(1)} %fusion.64), channel_id=1, source_target_pairs={{0,16},{4,12},{8,24},{12,4},{16,0},{20,28},{24,8},{28,20},{1,17},{... | collective-permute-start | bytes 786440 | tf_op jit(solution)/shard_map/ppermute | solution.py:305
  325.5 14.8 %collective-permute-start.44 = (bf16[1,128,1024]{2,1,0:T(8,128)(2,1)S(1)}, bf16[1,128,1024]{2,1,0:T(8,128)(2,1)S(1)}, u32[]{:S(2)}, u32[]{:S(2)}) collective-permute-start(bf16[1,128,1024]{2,1,0:T(8,128)(2,1)S(1)} %fusion.64), channel_id=1, source_target_pairs={{0,24},{4,28},{8,16},{12,20},{16,8},{20,12},{24,0},{28,4},{1,25},{... | collective-permute-start | bytes 786440 | tf_op jit(solution)/shard_map/ppermute | solution.py:305
  335.8 14.7 %collective-permute-start.47 = (bf16[32,4096]{1,0:T(8,128)(2,1)}, bf16[32,4096]{1,0:T(8,128)(2,1)}, u32[]{:S(2)}, u32[]{:S(2)}) collective-permute-start(bf16[32,4096]{1,0:T(8,128)(2,1)} %get-tuple-element.229), channel_id=1, source_target_pairs={{0,1},{1,2},{2,3},{3,0},{4,5},{5,6},{6,7},{7,4},{8,9},{9,10},{10,1... | collective-permute-start | bytes 786440 | tf_op jit(solution)/shard_map/ppermute | solution.py:298
  336.4 20.8 %collective-permute-start.48 = (bf16[32,4096]{1,0:T(8,128)(2,1)}, bf16[32,4096]{1,0:T(8,128)(2,1)}, u32[]{:S(2)}, u32[]{:S(2)}) collective-permute-start(bf16[32,4096]{1,0:T(8,128)(2,1)} %get-tuple-element.230), channel_id=1, source_target_pairs={{0,2},{1,3},{2,0},{3,1},{4,6},{5,7},{6,4},{7,5},{8,10},{9,11},{10,... | collective-permute-start | bytes 786440 | tf_op jit(solution)/shard_map/ppermute | solution.py:298
  338.4 18.8 %collective-permute-start.49 = (bf16[32,4096]{1,0:T(8,128)(2,1)}, bf16[32,4096]{1,0:T(8,128)(2,1)}, u32[]{:S(2)}, u32[]{:S(2)}) collective-permute-start(bf16[32,4096]{1,0:T(8,128)(2,1)} %get-tuple-element.231), channel_id=1, source_target_pairs={{0,3},{1,0},{2,1},{3,2},{4,7},{5,4},{6,5},{7,6},{8,11},{9,8},{10,9... | collective-permute-start | bytes 786440 | tf_op jit(solution)/shard_map/ppermute | solution.py:298
  345.5 23.6 %collective-permute-start.45 = (bf16[2,4,32,3072]{3,2,1,0:T(8,128)(2,1)}, bf16[2,4,32,3072]{3,2,1,0:T(8,128)(2,1)}, u32[]{:S(2)}, u32[]{:S(2)}) collective-permute-start(bf16[2,4,32,3072]{3,2,1,0:T(8,128)(2,1)} %fusion.10), channel_id=1, source_target_pairs={{0,8},{4,20},{8,0},{12,28},{16,24},{20,4},{24,16},{28,12},{1,9},{5... | collective-permute-start | bytes 4718600 | tf_op jit(solution)/shard_map/ppermute | solution.py:322
  347.0 12.7 %collective-permute-start.46 = (bf16[4,128,1024]{2,1,0:T(8,128)(2,1)}, bf16[4,128,1024]{2,1,0:T(8,128)(2,1)}, u32[]{:S(2)}, u32[]{:S(2)}) collective-permute-start(bf16[4,128,1024]{2,1,0:T(8,128)(2,1)} %pad_maximum_fusion.refs_0_), channel_id=1, source_target_pairs={{0,4},{4,0},{8,12},{12,8},{16,20},{20,16},{24,28},{28,24},{1,5},{5... | collective-permute-start | bytes 3145736 | tf_op jit(solution)/shard_map/ppermute | solution.py:294
  377.8 11.0 %collective-permute-start.59 = (f32[4,64,256]{2,0,1:T(4,128)S(1)}, f32[4,64,256]{2,0,1:T(4,128)S(1)}, u32[]{:S(2)}, u32[]{:S(2)}) collective-permute-start(f32[4,64,256]{2,0,1:T(4,128)S(1)} %fusion.93), channel_id=1, source_target_pairs={{0,8},{4,12},{8,0},{12,4},{16,24},{20,28},{24,16},{28,20},{1,9},{5... | collective-permute-start | bytes 786440 | tf_op jit(solution)/shard_map/ppermute | solution.py:342
  381.2 25.1 %collective-permute-start.52 = (bf16[1,32,4096]{2,1,0:T(8,128)(2,1)}, bf16[1,32,4096]{2,1,0:T(8,128)(2,1)}, u32[]{:S(2)}, u32[]{:S(2)}) collective-permute-start(bf16[1,32,4096]{2,1,0:T(8,128)(2,1)} %fusion.65), channel_id=1, source_target_pairs={{0,8},{4,20},{8,0},{12,28},{16,24},{20,4},{24,16},{28,12},{1,9},{5... | collective-permute-start | bytes 786440 | tf_op jit(solution)/shard_map/ppermute | solution.py:305
  381.5 24.7 %collective-permute-start.53 = (bf16[1,32,4096]{2,1,0:T(8,128)(2,1)}, bf16[1,32,4096]{2,1,0:T(8,128)(2,1)}, u32[]{:S(2)}, u32[]{:S(2)}) collective-permute-start(bf16[1,32,4096]{2,1,0:T(8,128)(2,1)} %fusion.65), channel_id=1, source_target_pairs={{0,16},{4,12},{8,24},{12,4},{16,0},{20,28},{24,8},{28,20},{1,17},{... | collective-permute-start | bytes 786440 | tf_op jit(solution)/shard_map/ppermute | solution.py:305
  385.8 20.5 %collective-permute-start.54 = (bf16[1,32,4096]{2,1,0:T(8,128)(2,1)}, bf16[1,32,4096]{2,1,0:T(8,128)(2,1)}, u32[]{:S(2)}, u32[]{:S(2)}) collective-permute-start(bf16[1,32,4096]{2,1,0:T(8,128)(2,1)} %fusion.65), channel_id=1, source_target_pairs={{0,24},{4,28},{8,16},{12,20},{16,8},{20,12},{24,0},{28,4},{1,25},{... | collective-permute-start | bytes 786440 | tf_op jit(solution)/shard_map/ppermute | solution.py:305
  387.1 19.1 %collective-permute-start.51 = (bf16[1,4,32,3072]{3,2,1,0:T(8,128)(2,1)}, bf16[1,4,32,3072]{3,2,1,0:T(8,128)(2,1)}, u32[]{:S(2)}, u32[]{:S(2)}) collective-permute-start(bf16[1,4,32,3072]{3,2,1,0:T(8,128)(2,1)} %fusion.21), channel_id=1, source_target_pairs={{0,16},{4,12},{8,24},{12,4},{16,0},{20,28},{24,8},{28,20},{1,17},{... | collective-permute-start | bytes 2359304 | tf_op jit(solution)/shard_map/ppermute | solution.py:322
  388.7 17.0 %collective-permute-start.57 = (bf16[32,1024]{1,0:T(8,128)(2,1)}, bf16[32,1024]{1,0:T(8,128)(2,1)}, u32[]{:S(2)}, u32[]{:S(2)}) collective-permute-start(bf16[32,1024]{1,0:T(8,128)(2,1)} %get-tuple-element.245), channel_id=1, source_target_pairs={{0,3},{1,0},{2,1},{3,2},{4,7},{5,4},{6,5},{7,6},{8,11},{9,8},{10,9... | collective-permute-start | bytes 196616 | tf_op jit(solution)/shard_map/ppermute | solution.py:298
  405.7 9.6 %collective-permute-start.60 = (f32[4,64,256]{2,0,1:T(4,128)S(1)}, f32[4,64,256]{2,0,1:T(4,128)S(1)}, u32[]{:S(2)}, u32[]{:S(2)}) collective-permute-start(f32[4,64,256]{2,0,1:T(4,128)S(1)} %add.626), channel_id=1, source_target_pairs={{0,16},{4,20},{8,24},{12,28},{16,0},{20,4},{24,8},{28,12},{1,17},{... | collective-permute-start | bytes 786440 | tf_op jit(solution)/shard_map/ppermute | solution.py:342
  411.5 24.8 %collective-permute-start.71 = (bf16[1,32,1024]{2,1,0:T(8,128)(2,1)S(1)}, bf16[1,32,1024]{2,1,0:T(8,128)(2,1)S(1)}, u32[]{:S(2)}, u32[]{:S(2)}) collective-permute-start(bf16[1,32,1024]{2,1,0:T(8,128)(2,1)S(1)} %fusion.77), channel_id=1, source_target_pairs={{0,8},{4,20},{8,0},{12,28},{16,24},{20,4},{24,16},{28,12},{1,9},{5... | collective-permute-start | bytes 196616 | tf_op jit(solution)/shard_map/ppermute | solution.py:305
  411.9 26.0 %collective-permute-start.72 = (bf16[1,32,1024]{2,1,0:T(8,128)(2,1)S(1)}, bf16[1,32,1024]{2,1,0:T(8,128)(2,1)S(1)}, u32[]{:S(2)}, u32[]{:S(2)}) collective-permute-start(bf16[1,32,1024]{2,1,0:T(8,128)(2,1)S(1)} %fusion.77), channel_id=1, source_target_pairs={{0,16},{4,12},{8,24},{12,4},{16,0},{20,28},{24,8},{28,20},{1,17},{... | collective-permute-start | bytes 196616 | tf_op jit(solution)/shard_map/ppermute | solution.py:305
  414.5 18.5 %collective-permute-start.65 = (bf16[32,3072]{1,0:T(8,128)(2,1)S(1)}, bf16[32,3072]{1,0:T(8,128)(2,1)S(1)}, u32[]{:S(2)}, u32[]{:S(2)}) collective-permute-start(bf16[32,3072]{1,0:T(8,128)(2,1)S(1)} %get-tuple-element.257), channel_id=1, source_target_pairs={{0,2},{1,3},{2,0},{3,1},{4,6},{5,7},{6,4},{7,5},{8,10},{9,11},{10,... | collective-permute-start | bytes 589832 | tf_op jit(solution)/shard_map/ppermute | solution.py:298
  415.3 17.7 %collective-permute-start.64 = (bf16[32,3072]{1,0:T(8,128)(2,1)S(1)}, bf16[32,3072]{1,0:T(8,128)(2,1)S(1)}, u32[]{:S(2)}, u32[]{:S(2)}) collective-permute-start(bf16[32,3072]{1,0:T(8,128)(2,1)S(1)} %get-tuple-element.256), channel_id=1, source_target_pairs={{0,1},{1,2},{2,3},{3,0},{4,5},{5,6},{6,7},{7,4},{8,9},{9,10},{10,1... | collective-permute-start | bytes 589832 | tf_op jit(solution)/shard_map/ppermute | solution.py:298
  420.6 25.3 %collective-permute-start.73 = (bf16[1,32,1024]{2,1,0:T(8,128)(2,1)S(1)}, bf16[1,32,1024]{2,1,0:T(8,128)(2,1)S(1)}, u32[]{:S(2)}, u32[]{:S(2)}) collective-permute-start(bf16[1,32,1024]{2,1,0:T(8,128)(2,1)S(1)} %fusion.77), channel_id=1, source_target_pairs={{0,24},{4,28},{8,16},{12,20},{16,8},{20,12},{24,0},{28,4},{1,25},{... | collective-permute-start | bytes 196616 | tf_op jit(solution)/shard_map/ppermute | solution.py:305
  435.0 10.8 %collective-permute-start.68 = (bf16[1,32,3072]{2,1,0:T(8,128)(2,1)S(1)}, bf16[1,32,3072]{2,1,0:T(8,128)(2,1)S(1)}, u32[]{:S(2)}, u32[]{:S(2)}) collective-permute-start(bf16[1,32,3072]{2,1,0:T(8,128)(2,1)S(1)} %fusion.68), channel_id=1, source_target_pairs={{0,16},{4,12},{8,24},{12,4},{16,0},{20,28},{24,8},{28,20},{1,17},{... | collective-permute-start | bytes 589832 | tf_op jit(solution)/shard_map/ppermute | solution.py:305
  436.2 9.6 %collective-permute-start.67 = (bf16[1,32,3072]{2,1,0:T(8,128)(2,1)S(1)}, bf16[1,32,3072]{2,1,0:T(8,128)(2,1)S(1)}, u32[]{:S(2)}, u32[]{:S(2)}) collective-permute-start(bf16[1,32,3072]{2,1,0:T(8,128)(2,1)S(1)} %fusion.68), channel_id=1, source_target_pairs={{0,8},{4,20},{8,0},{12,28},{16,24},{20,4},{24,16},{28,12},{1,9},{5... | collective-permute-start | bytes 589832 | tf_op jit(solution)/shard_map/ppermute | solution.py:305
  445.8 10.6 %collective-permute-start.75 = (bf16[4,32,4096]{2,1,0:T(8,128)(2,1)}, bf16[4,32,4096]{2,1,0:T(8,128)(2,1)S(1)}, u32[]{:S(2)}, u32[]{:S(2)}) collective-permute-start(bf16[4,32,4096]{2,1,0:T(8,128)(2,1)} %pad_maximum_fusion.1.refs_0_), channel_id=1, source_target_pairs={{0,4},{4,0},{8,12},{12,8},{16,20},{20,16},{24,28},{28,24},{1,5},{5... | collective-permute-start | bytes 3145736 | tf_op jit(solution)/shard_map/ppermute | solution.py:294
  445.9 15.3 %collective-permute-start.70 = (bf16[4,32,3072]{2,1,0:T(8,128)(2,1)S(1)}, bf16[4,32,3072]{2,1,0:T(8,128)(2,1)S(1)}, u32[]{:S(2)}, u32[]{:S(2)}) collective-permute-start(bf16[4,32,3072]{2,1,0:T(8,128)(2,1)S(1)} %pad_maximum_fusion.2.refs_0_), channel_id=1, source_target_pairs={{0,4},{4,0},{8,12},{12,8},{16,20},{20,16},{24,28},{28,24},{1,5},{5... | collective-permute-start | bytes 2359304 | tf_op jit(solution)/shard_map/ppermute | solution.py:294
  (97 other events, 1338.3 us)

commit v10 on v9

--- a/solution.py
+++ b/solution.py
@@ -698,10 +698,10 @@
     back_in, grad_gain_one, grad_bias_one = pull_one(grad_norm_one)
     grad_in = grad_mid + back_in
     grad_table = jnp.dot(place.T, grad_in, precision=highest)
-    grad_table, activated = tick((grad_table, activated), [run_qkv] + every)
+    grad_table, activated = lax.optimization_barrier((grad_table, activated))
     branch_out = jnp.dot(activated, full_fc2, preferred_element_type=f32)
     block_out = jnp.where(valid[:, None], hidden_mid + branch_out, 0.0).astype(bf16)
-    block_out = tick(block_out, [run_qkv] + every)
+    grad_table, block_out = tick((grad_table, block_out), [run_qkv] + every)
 
     def split(block):
         return block.reshape(-1, n_line, shard).transpose(1, 0, 2)
@@ -714,6 +714,7 @@
         ],
         axis=1,
     )
+    rows_small = tick(rows_small, [run_qkv])
     run_small = plan.total_small(rows_small)
     (sum_fc2,) = run_fc2.result()
     (sum_fc1,) = run_fc1.result()

time: 472 us -> 477 us (1.011)
  local copies, waits for them, and re-layouts: 35.8 us -> 42.5 us
    ppermute x24, waiting for transfers between devices: 54.1 us -> 43.7 us  [ahead(): lax.ppermute(block, 'fsdp', [(i, (i + step) % n_line) for i in range(n_li...]
    ppermute x8, waiting for transfers between devices: 17 us -> 26.4 us  [reduce_steps(): got, = (yield [lax.ppermute(send, 'dp', hop_pairs(n_dp, stage))])]
  transfers between devices with their start and end apart: 76 -> 76, of which waited for: 23 -> 22; matrix products, arithmetic and copies ran while one was open for 25% -> 25% of each run, Pallas kernels for 19% -> 18%
where the time goes in v10:
time: 477 us; the launch traced here: 471 us
  waiting for transfers between devices  101 us (21%)
  Pallas kernels  94.9 us (20%)
  matrix products  91.6 us (19%)
  starting transfers between devices  78.8 us (17%)
  other arithmetic  60.4 us (13%)
  local copies, waits for them, and re-layouts  42.5 us (9%)
    ppermute x24, starting transfers between devices, ahead(): lax.ppermute(block, 'fsdp', [(i, (i + step) % n_line) for i in range(n_li...  43.9 us
    ppermute x24, waiting for transfers between devices, ahead(): lax.ppermute(block, 'fsdp', [(i, (i + step) % n_line) for i in range(n_li...  43.7 us
    pallas_call x2, Pallas kernels, attend_back(): pl.pallas_call(body, grid=(count,), in_specs=pair_specs(rows, pairs, star...  37.7 us
    dot_general x4, matrix products, times_t(): lax.dot_general(left, right, (((1,), (1,)), ((), ())), preferred_element_...  27.7 us
    ppermute x8, waiting for transfers between devices, reduce_steps(): got, = (yield [lax.ppermute(send, 'dp', hop_pairs(n_dp, stage))])  26.4 us
    dot_general x8, matrix products, t_times(): lax.dot_general(left, right, (((0,), (0,)), ((), ())), preferred_element_...  25.7 us
    convert_element_type x8, other arithmetic, reduce_steps(): add_up([term[half:] for term in terms]).astype(jnp.bfloat16)  23.3 us
    pallas_call x3, Pallas kernels, assemble(): pl.pallas_call(body, in_specs=[pl.BlockSpec(memory_space=pltpu.SMEM)] + [...  22.9 us
  transfers between devices with their start and end apart: 76, of which 22 were waited for; matrix products, arithmetic and copies ran while one was open for 25% of the time, Pallas kernels for 18%

profile of v10, /device:TPU:0, one launch (start us, length us, event | category | flops | bytes accessed | tf_op | source)
XLA Modules:
  0.0 470.8 jit_solution(4537318035140310477)
XLA Ops:
  6.6 3.1 collective-permute-start
  9.7 2.6 collective-permute-start.1
  19.7 11.8 %collective-permute-done.1 = bf16[32,4608]{1,0:T(8,128)(2,1)S(1)} collective-permute-done((bf16[32,4608]{1,0:T(8,128)(2,1)S(1)}, bf16[32,4608]{1,0:T(8,128)(2,1)S(1)}, u32[]{:S(2)}, u32[]{:S(2)}) %collective-permute-start.1) | collective-permute-done | bytes 294944 | tf_op jit(solution)/shard_map/ppermute | solution.py:298
  35.6 6.8 %collective-permute-start.5 = (bf16[32,4096]{1,0:T(8,128)(2,1)S(1)}, bf16[32,4096]{1,0:T(8,128)(2,1)S(1)}, u32[]{:S(2)}, u32[]{:S(2)}) collective-permute-start(bf16[32,4096]{1,0:T(8,128)(2,1)S(1)} %constant_dynamic-slice_fusion.5), channel_id=1, source_target_pairs={{0,1},{1,2},{2,3},{3,0},{4,5},{5,6},{6,7},{7,4},{8,9},{9,10},{10,1... | collective-permute-start | bytes 786440 | tf_op jit(solution)/shard_map/ppermute | solution.py:298
  45.6 5.1 %collective-permute-done.5 = bf16[32,4096]{1,0:T(8,128)(2,1)S(1)} collective-permute-done((bf16[32,4096]{1,0:T(8,128)(2,1)S(1)}, bf16[32,4096]{1,0:T(8,128)(2,1)S(1)}, u32[]{:S(2)}, u32[]{:S(2)}) %collective-permute-start.5) | collective-permute-done | bytes 262176 | tf_op jit(solution)/shard_map/ppermute | solution.py:298
  50.7 9.0 %collective-permute-done.6 = bf16[32,4096]{1,0:T(8,128)(2,1)S(1)} collective-permute-done((bf16[32,4096]{1,0:T(8,128)(2,1)S(1)}, bf16[32,4096]{1,0:T(8,128)(2,1)S(1)}, u32[]{:S(2)}, u32[]{:S(2)}) %collective-permute-start.6) | collective-permute-done | bytes 262176 | tf_op jit(solution)/shard_map/ppermute | solution.py:298
  62.1 9.8 %collective-permute-done.8.refs_5_ = bf16[1,3,32,4096]{3,2,1,0:T(8,128)(2,1)S(1)} collective-permute-done((bf16[1,3,32,4096]{3,2,1,0:T(8,128)(2,1)}, bf16[1,3,32,4096]{3,2,1,0:T(8,128)(2,1)S(1)}, u32[]{:S(2)}, u32[]{:S(2)}) %collective-permute-start.8) | collective-permute-done | bytes 786464 | tf_op jit(solution)/shard_map/ppermute | solution.py:473
  75.6 7.7 %assemble.3 = (bf16[1024,3072]{1,0:T(8,128)(2,1)}, bf16[1024,1024]{1,0:T(8,128)(2,1)}) custom-call(s32[33]{0:T(128)} %pad_add_fusion.1.table_ref, bf16[256,3072]{1,0:T(8,128)(2,1)} %refs_0_.3, bf16[256,1024]{1,0:T(8,128)(2,1)} %refs_1_.1, bf16[1,3,32,4096]{3,2,1,0:T(8,128)(2,1)} %maximum_bitcast_fusion.refs_2_, ...), custom_call_target="tpu_custom_call" | custom-call | tf_op jit(solution)/shard_map/assemble/pallas_call | solution.py:225
  83.4 7.8 %convolution_convert_fusion.4.refs_2_.refs_3_.refs_4_ = bf16[512,3072]{1,0:T(8,128)(2,1)} fusion(bf16[1024,3072]{1,0:T(8,128)(2,1)} %get-tuple-element.154, f32[512,1024]{1,0:T(8,128)S(1)} %get-tuple-element.293, f32[1024]{0:T(1024)S(1)} %bitcast.300, f32[1024]{0:T(1024)S(1)} %bitcast.292, f32[512]{0:T(512)S(1)} %fusion.86, f32[512]{0:T(512)S(1)} %broadcast_multiply_fusion.1), kind=kOutput, calls=%fused_computation.15 | convolution fusion | flops 3225419776 | bytes 11546624 | tf_op jit(solution)/shard_map/dot_general | solution.py:654
  94.7 6.0 %collective-permute-start.9 = (bf16[128,1024]{1,0:T(8,128)(2,1)S(1)}, bf16[128,1024]{1,0:T(8,128)(2,1)S(1)}, u32[]{:S(2)}, u32[]{:S(2)}) collective-permute-start(bf16[128,1024]{1,0:T(8,128)(2,1)S(1)} %copy-done.38), channel_id=1, source_target_pairs={{0,1},{1,2},{2,3},{3,0},{4,5},{5,6},{6,7},{7,4},{8,9},{9,10},{10,1... | collective-permute-start | bytes 786440 | tf_op jit(solution)/shard_map/ppermute | solution.py:298
  100.7 2.4 collective-permute-start.10
  107.5 15.8 %attend.1 = bf16[512,1024]{1,0:T(8,128)(2,1)} custom-call(s32[512,1]{1,0:T(8,128)} %fusion.59.refs_0_, s32[1,512]{1,0:T(1,128)} %broadcast_select_fusion.2.refs_1_, bf16[512,3072]{1,0:T(8,128)(2,1)} %convolution_convert_fusion.4.refs_2_.refs_3_.refs_4_, bf16[512,3072]{1,0:T(8,128)(2,1)} %convolution_convert_fusion.4.refs_2_.refs_3_.refs_4_, ...), custom_call_target="tpu_custom_call" | custom-call | tf_op jit(solution)/shard_map/attend/pallas_call | solution.py:148
  123.9 2.0 maximum_bitcast_fusion.2.refs_1_
  126.9 3.3 fusion.102
  132.3 5.9 %collective-permute-done.19.refs_2_ = bf16[1,3,128,1024]{3,2,1,0:T(8,128)(2,1)} collective-permute-done((bf16[1,3,128,1024]{3,2,1,0:T(8,128)(2,1)}, bf16[1,3,128,1024]{3,2,1,0:T(8,128)(2,1)}, u32[]{:S(2)}, u32[]{:S(2)}) %collective-permute-start.19) | collective-permute-done | bytes 786464 | tf_op jit(solution)/shard_map/ppermute | solution.py:473
  141.1 7.5 %assemble.4 = bf16[1024,4096]{1,0:T(8,128)(2,1)} custom-call(s32[33]{0:T(128)} %pad_add_fusion.1.table_ref, bf16[256,4096]{1,0:T(8,128)(2,1)} %refs_0_.4, bf16[1,3,32,4096]{3,2,1,0:T(8,128)(2,1)} %copy-done.19, bf16[1,3,32,4096]{3,2,1,0:T(8,128)(2,1)} %collective-permute-done.13.refs_2_, bf16[1,3,32,4096]{3,2,1,0:T(8,128)(2,1)} %collective-permute-done.12.refs_3_, ...), custom_call_target="tpu_custom_call" | custom-call | tf_op jit(solution)/shard_map/assemble/pallas_call | solution.py:225
  148.7 10.4 %multiply_convert_fusion.1 = (bf16[512,4096]{1,0:T(8,128)(2,1)}, f32[512,4096]{1,0:T(8,128)}) fusion(f32[4096]{0:T(1024)S(1)} %bitcast.297, bf16[512,1024]{1,0:T(8,128)(2,1)S(1)} %copy-done.26, bf16[1024,4096]{1,0:T(8,128)(2,1)} %assemble.4), kind=kOutput, calls=%fused_computation.9 | convolution fusion | flops 4307550208 | bytes 22036480 | tf_op jit(solution)/shard_map/dot_general | solution.py:661
  159.2 5.5 %column_order.1 = bf16[512,4096]{1,0:T(8,128)(2,1)} custom-call(s32[32]{0:T(128)} %add.550.table_ref, bf16[512,4096]{1,0:T(8,128)(2,1)} %get-tuple-element.222.in_ref), custom_call_target="tpu_custom_call" | custom-call | tf_op jit(solution)/shard_map/column_order/pallas_call | solution.py:245
  164.7 6.0 %convolution_convert_fusion.6 = bf16[2048,1024]{1,0:T(8,128)(2,1)} fusion(bf16[512,4096]{1,0:T(8,128)(2,1)} %column_order.1, bf16[512,1024]{1,0:T(8,128)(2,1)S(1)} %copy-done.17, pred[512]{0:T(512)(128)(4,1)S(1)} %copy-done.69), kind=kOutput, calls=%fused_computation.25 | convolution fusion | flops 2150105088 | bytes 7340544 | tf_op jit(solution)/shard_map/dot_general | solution.py:69
  171.9 3.7 fusion.22
  175.6 2.5 convolution_convert_fusion.5
  183.3 7.6 %assemble.5 = bf16[4096,1024]{1,0:T(8,128)(2,1)} custom-call(s32[33]{0:T(128)} %pad_add_fusion.1.table_ref, bf16[1024,1024]{1,0:T(8,128)(2,1)} %refs_0_.5, bf16[1,3,128,1024]{3,2,1,0:T(8,128)(2,1)} %maximum_bitcast_fusion.2.refs_1_, bf16[1,3,128,1024]{3,2,1,0:T(8,128)(2,1)} %collective-permute-done.19.refs_2_, ...), custom_call_target="tpu_custom_call" | custom-call | tf_op jit(solution)/shard_map/assemble/pallas_call | solution.py:225
  191.0 3.4 fusion.6
  194.3 11.7 %convert_reduce_fusion = (f32[4096]{0:T(1024)}, bf16[512,4096]{1,0:T(8,128)(2,1)S(1)}) fusion(f32[512,4096]{1,0:T(8,128)} %get-tuple-element.297, f32[4096]{0:T(1024)S(1)} %bitcast.298, bf16[4096,1024]{1,0:T(8,128)(2,1)} %assemble.5, bf16[512,1024]{1,0:T(8,128)(2,1)S(1)} %copy-done.17, pred[512]{0:T(512)(128)(4,1)S(1)} %copy-done.69), kind=kOutput, calls=%fused_computation.7 | convolution fusion | flops 4326944768 | bytes 22053376 | tf_op jit(solution)/shard_map/dot_general | solution.py:65
  206.0 5.7 %convolution_convert_fusion.1 = bf16[512,4096]{1,0:T(8,128)(2,1)} fusion(bf16[512,4096]{1,0:T(8,128)(2,1)S(1)} %get-tuple-element.178, bf16[512,1024]{1,0:T(8,128)(2,1)} %fusion.22), kind=kOutput, calls=%fused_computation.12 | convolution fusion | flops 2149580800 | bytes 8912896 | tf_op jit(solution)/shard_map/dot_general | solution.py:69
  212.7 6.8 %multiply_reduce_fusion = (f32[1024]{0:T(1024)}, f32[512]{0:T(512)S(1)}, f32[1024]{0:T(1024)}, f32[512,1024]{1,0:T(8,128)}) fusion(f32[512,1024]{1,0:T(8,128)S(1)} %copy-done.1, f32[512]{0:T(512)S(1)} %fusion.87, f32[512]{0:T(512)S(1)} %broadcast_multiply_fusion, f32[1024]{0:T(1024)S(1)} %bitcast.290, bf16[512,4096]{1,0:T(8,128)(2,1)S(1)} %get-tuple-element.178, ...), kind=kOutput, calls=%fused_computation.38 | convolution fusion | flops 4299159040 | bytes 16795648 | tf_op jit(solution)/shard_map/dot_general | solution.py:65
  219.6 2.4 fusion.96
  222.0 2.5 convolution_convert_fusion
  224.5 2.0 copy-done.5
  228.4 3.9 fusion.5
  235.1 2.0 copy-done.73
  237.1 2.7 convolution_convert_fusion.7.refs_5_
  241.6 3.2 fusion.16
  245.8 18.8 %attend_back.2 = bf16[512,1536]{1,0:T(8,128)(2,1)} custom-call(s32[512,1]{1,0:T(8,128)} %fusion.59.refs_0_, s32[1,512]{1,0:T(1,128)} %broadcast_select_fusion.2.refs_1_, bf16[512,3072]{1,0:T(8,128)(2,1)} %convolution_convert_fusion.4.refs_2_.refs_3_.refs_4_, bf16[512,3072]{1,0:T(8,128)(2,1)} %convolution_convert_fusion.4.refs_2_.refs_3_.refs_4_, ...), custom_call_target="tpu_custom_call" | custom-call | tf_op jit(solution)/shard_map/attend_back/pallas_call | solution.py:167
  266.4 4.6 collective-permute-done.33
  272.0 3.2 fusion.46
  275.2 3.0 fusion.14
  278.3 2.1 fusion.26
  281.9 2.0 collective-permute-start.36
  286.3 2.5 fusion.24
  288.8 18.9 %attend_back.3 = bf16[512,1536]{1,0:T(8,128)(2,1)} custom-call(s32[512,1]{1,0:T(8,128)} %fusion.59.refs_0_, s32[1,512]{1,0:T(1,128)} %broadcast_select_fusion.2.refs_1_, bf16[512,3072]{1,0:T(8,128)(2,1)} %convolution_convert_fusion.4.refs_2_.refs_3_.refs_4_, bf16[512,3072]{1,0:T(8,128)(2,1)} %convolution_convert_fusion.4.refs_2_.refs_3_.refs_4_, ...), custom_call_target="tpu_custom_call" | custom-call | tf_op jit(solution)/shard_map/attend_back/pallas_call | solution.py:167
  307.7 3.2 fusion.39
  310.9 2.0 fusion.38
  316.0 3.7 convolution_convert_fusion.3
  325.7 6.5 %fusion.103 = f32[512,1024]{1,0:T(8,128)S(1)} fusion(bf16[512,3072]{1,0:T(8,128)(2,1)} %copy-done.6, bf16[1024,3072]{1,0:T(8,128)(2,1)} %get-tuple-element.154), kind=kOutput, calls=%fused_computation.303 | convolution fusion | flops 3221225472 | bytes 11534336 | tf_op jit(solution)/shard_map/dot_general | solution.py:65
  332.3 1.9 convolution_convert_fusion.2
  338.4 2.0 collective-permute-start.49
  341.4 3.1 fusion.10
  350.3 2.1 fusion.104
  354.0 5.5 %select_convert_fusion = bf16[512,1024]{1,0:T(8,128)(2,1)} fusion(f32[512,1024]{1,0:T(8,128)S(1)} %copy-done.2, bf16[512,4096]{1,0:T(8,128)(2,1)S(1)} %copy-done.13, bf16[4096,1024]{1,0:T(8,128)(2,1)S(1)} %bitcast.271, pred[512]{0:T(512)(128)(4,1)S(1)} %copy-done.70), kind=kOutput, calls=%fused_computation.40 | convolution fusion | flops 4296540160 | bytes 15729152 | tf_op jit(solution)/shard_map/dot_general | solution.py:702
  360.2 12.9 %collective-permute-done.45 = bf16[2,4,32,3072]{3,2,1,0:T(8,128)(2,1)} collective-permute-done((bf16[2,4,32,3072]{3,2,1,0:T(8,128)(2,1)}, bf16[2,4,32,3072]{3,2,1,0:T(8,128)(2,1)}, u32[]{:S(2)}, u32[]{:S(2)}) %collective-permute-start.45) | collective-permute-done | bytes 1572896 | tf_op jit(solution)/shard_map/ppermute | solution.py:322
  375.0 2.6 fusion.21
  398.4 7.8 %collective-permute-done.51 = bf16[1,4,32,3072]{3,2,1,0:T(8,128)(2,1)S(1)} collective-permute-done((bf16[1,4,32,3072]{3,2,1,0:T(8,128)(2,1)}, bf16[1,4,32,3072]{3,2,1,0:T(8,128)(2,1)S(1)}, u32[]{:S(2)}, u32[]{:S(2)}) %collective-permute-start.51) | collective-permute-done | bytes 786464 | tf_op jit(solution)/shard_map/ppermute | solution.py:322
  408.8 2.5 collective-permute-start.60
  412.2 4.5 collective-permute-done.60
  417.5 11.7 %collective-permute-done.59 = bf16[32,3072]{1,0:T(8,128)(2,1)S(1)} collective-permute-done((bf16[32,3072]{1,0:T(8,128)(2,1)S(1)}, bf16[32,3072]{1,0:T(8,128)(2,1)S(1)}, u32[]{:S(2)}, u32[]{:S(2)}) %collective-permute-start.59) | collective-permute-done | bytes 196640 | tf_op jit(solution)/shard_map/ppermute | solution.py:298
  431.6 1.9 collective-permute-start.63
  439.5 3.6 collective-permute-done.63
  447.5 3.8 collective-permute-done.54
  452.8 2.0 collective-permute-start.55
  454.8 3.8 finish.7
  458.6 2.1 finish.5
  460.7 3.8 finish.6
  467.3 3.2 finish.4
  (416 shorter events, 128.8 us)
Async XLA Ops:
  6.6 13.1 %collective-permute-start = (bf16[32,4608]{1,0:T(8,128)(2,1)S(1)}, bf16[32,4608]{1,0:T(8,128)(2,1)S(1)}, u32[]{:S(2)}, u32[]{:S(2)}) collective-permute-start(bf16[32,4608]{1,0:T(8,128)(2,1)S(1)} %pad_maximum_fusion.2), channel_id=1, source_target_pairs={{0,1},{1,2},{2,3},{3,0},{4,5},{5,6},{6,7},{7,4},{8,9},{9,10},{10,1... | collective-permute-start | bytes 884744 | tf_op jit(solution)/shard_map/ppermute | solution.py:298
  9.7 21.8 %collective-permute-start.1 = (bf16[32,4608]{1,0:T(8,128)(2,1)S(1)}, bf16[32,4608]{1,0:T(8,128)(2,1)S(1)}, u32[]{:S(2)}, u32[]{:S(2)}) collective-permute-start(bf16[32,4608]{1,0:T(8,128)(2,1)S(1)} %pad_maximum_fusion.2), channel_id=1, source_target_pairs={{0,2},{1,3},{2,0},{3,1},{4,6},{5,7},{6,4},{7,5},{8,10},{9,11},{10,... | collective-permute-start | bytes 884744 | tf_op jit(solution)/shard_map/ppermute | solution.py:298
  12.3 19.2 %collective-permute-start.2 = (bf16[32,4608]{1,0:T(8,128)(2,1)S(1)}, bf16[32,4608]{1,0:T(8,128)(2,1)S(1)}, u32[]{:S(2)}, u32[]{:S(2)}) collective-permute-start(bf16[32,4608]{1,0:T(8,128)(2,1)S(1)} %pad_maximum_fusion.2), channel_id=1, source_target_pairs={{0,3},{1,0},{2,1},{3,2},{4,7},{5,4},{6,5},{7,6},{8,11},{9,8},{10,9... | collective-permute-start | bytes 884744 | tf_op jit(solution)/shard_map/ppermute | solution.py:298
  32.6 29.6 %collective-permute-start.3 = (bf16[1,3,32,4096]{3,2,1,0:T(8,128)(2,1)}, bf16[1,3,32,4096]{3,2,1,0:T(8,128)(2,1)}, u32[]{:S(2)}, u32[]{:S(2)}) collective-permute-start(bf16[1,3,32,4096]{3,2,1,0:T(8,128)(2,1)} %maximum_bitcast_fusion.refs_2_), channel_id=1, source_target_pairs={{0,16},{4,12},{8,24},{12,4},{16,0},{20,28},{24,8},{28,20},{1,17},{... | collective-permute-start | bytes 2359304 | tf_op jit(solution)/shard_map/ppermute | solution.py:473
  34.1 25.5 %collective-permute-start.4 = (bf16[1,3,32,4096]{3,2,1,0:T(8,128)(2,1)}, bf16[1,3,32,4096]{3,2,1,0:T(8,128)(2,1)}, u32[]{:S(2)}, u32[]{:S(2)}) collective-permute-start(bf16[1,3,32,4096]{3,2,1,0:T(8,128)(2,1)} %maximum_bitcast_fusion.refs_2_), channel_id=1, source_target_pairs={{0,8},{4,20},{8,0},{12,28},{16,24},{20,4},{24,16},{28,12},{1,9},{5... | collective-permute-start | bytes 2359304 | tf_op jit(solution)/shard_map/ppermute | solution.py:473
  35.6 15.1 %collective-permute-start.5 = (bf16[32,4096]{1,0:T(8,128)(2,1)S(1)}, bf16[32,4096]{1,0:T(8,128)(2,1)S(1)}, u32[]{:S(2)}, u32[]{:S(2)}) collective-permute-start(bf16[32,4096]{1,0:T(8,128)(2,1)S(1)} %constant_dynamic-slice_fusion.5), channel_id=1, source_target_pairs={{0,1},{1,2},{2,3},{3,0},{4,5},{5,6},{6,7},{7,4},{8,9},{9,10},{10,1... | collective-permute-start | bytes 786440 | tf_op jit(solution)/shard_map/ppermute | solution.py:298
  42.4 17.3 %collective-permute-start.6 = (bf16[32,4096]{1,0:T(8,128)(2,1)S(1)}, bf16[32,4096]{1,0:T(8,128)(2,1)S(1)}, u32[]{:S(2)}, u32[]{:S(2)}) collective-permute-start(bf16[32,4096]{1,0:T(8,128)(2,1)S(1)} %constant_dynamic-slice_fusion.5), channel_id=1, source_target_pairs={{0,2},{1,3},{2,0},{3,1},{4,6},{5,7},{6,4},{7,5},{8,10},{9,11},{10,... | collective-permute-start | bytes 786440 | tf_op jit(solution)/shard_map/ppermute | solution.py:298
  43.9 15.7 %collective-permute-start.7 = (bf16[32,4096]{1,0:T(8,128)(2,1)S(1)}, bf16[32,4096]{1,0:T(8,128)(2,1)S(1)}, u32[]{:S(2)}, u32[]{:S(2)}) collective-permute-start(bf16[32,4096]{1,0:T(8,128)(2,1)S(1)} %constant_dynamic-slice_fusion.5), channel_id=1, source_target_pairs={{0,3},{1,0},{2,1},{3,2},{4,7},{5,4},{6,5},{7,6},{8,11},{9,8},{10,9... | collective-permute-start | bytes 786440 | tf_op jit(solution)/shard_map/ppermute | solution.py:298
  50.6 23.1 %collective-permute-start.14 = (bf16[1,3,32,4096]{3,2,1,0:T(8,128)(2,1)}, bf16[1,3,32,4096]{3,2,1,0:T(8,128)(2,1)}, u32[]{:S(2)}, u32[]{:S(2)}) collective-permute-start(bf16[1,3,32,4096]{3,2,1,0:T(8,128)(2,1)} %maximum_bitcast_fusion.refs_2_), channel_id=1, source_target_pairs={{0,4},{4,0},{8,12},{12,8},{16,20},{20,16},{24,28},{28,24},{1,5},{5... | collective-permute-start | bytes 2359304 | tf_op jit(solution)/shard_map/ppermute | solution.py:294
  59.6 12.3 %collective-permute-start.8 = (bf16[1,3,32,4096]{3,2,1,0:T(8,128)(2,1)}, bf16[1,3,32,4096]{3,2,1,0:T(8,128)(2,1)S(1)}, u32[]{:S(2)}, u32[]{:S(2)}) collective-permute-start(bf16[1,3,32,4096]{3,2,1,0:T(8,128)(2,1)} %collective-permute-done.4.refs_3_), channel_id=1, source_target_pairs={{0,16},{4,12},{8,24},{12,4},{16,0},{20,28},{24,8},{28,20},{1,17},{... | collective-permute-start | bytes 2359304 | tf_op jit(solution)/shard_map/ppermute | solution.py:473
  62.0 12.3 %collective-permute-start.15 = (bf16[1,3,32,4096]{3,2,1,0:T(8,128)(2,1)}, bf16[1,3,32,4096]{3,2,1,0:T(8,128)(2,1)}, u32[]{:S(2)}, u32[]{:S(2)}) collective-permute-start(bf16[1,3,32,4096]{3,2,1,0:T(8,128)(2,1)} %collective-permute-done.4.refs_3_), channel_id=1, source_target_pairs={{0,4},{4,0},{8,12},{12,8},{16,20},{20,16},{24,28},{28,24},{1,5},{5... | collective-permute-start | bytes 2359304 | tf_op jit(solution)/shard_map/ppermute | solution.py:294
  73.2 19.9 %collective-permute-start.13 = (bf16[1,3,32,4096]{3,2,1,0:T(8,128)(2,1)S(1)}, bf16[1,3,32,4096]{3,2,1,0:T(8,128)(2,1)}, u32[]{:S(2)}, u32[]{:S(2)}) collective-permute-start(bf16[1,3,32,4096]{3,2,1,0:T(8,128)(2,1)S(1)} %maximum_bitcast_fusion.1.refs_1_), channel_id=1, source_target_pairs={{0,8},{4,20},{8,0},{12,28},{16,24},{20,4},{24,16},{28,12},{1,9},{5... | collective-permute-start | bytes 2359304 | tf_op jit(solution)/shard_map/ppermute | solution.py:473
  73.8 49.5 %collective-permute-start.12 = (bf16[1,3,32,4096]{3,2,1,0:T(8,128)(2,1)S(1)}, bf16[1,3,32,4096]{3,2,1,0:T(8,128)(2,1)}, u32[]{:S(2)}, u32[]{:S(2)}) collective-permute-start(bf16[1,3,32,4096]{3,2,1,0:T(8,128)(2,1)S(1)} %maximum_bitcast_fusion.1.refs_1_), channel_id=1, source_target_pairs={{0,16},{4,12},{8,24},{12,4},{16,0},{20,28},{24,8},{28,20},{1,17},{... | collective-permute-start | bytes 2359304 | tf_op jit(solution)/shard_map/ppermute | solution.py:473
  93.0 30.3 %collective-permute-start.18 = (bf16[1,3,32,4096]{3,2,1,0:T(8,128)(2,1)}, bf16[1,3,32,4096]{3,2,1,0:T(8,128)(2,1)}, u32[]{:S(2)}, u32[]{:S(2)}) collective-permute-start(bf16[1,3,32,4096]{3,2,1,0:T(8,128)(2,1)} %collective-permute-done.13.refs_2_), channel_id=1, source_target_pairs={{0,16},{4,12},{8,24},{12,4},{16,0},{20,28},{24,8},{28,20},{1,17},{... | collective-permute-start | bytes 2359304 | tf_op jit(solution)/shard_map/ppermute | solution.py:473
  94.7 29.1 %collective-permute-start.9 = (bf16[128,1024]{1,0:T(8,128)(2,1)S(1)}, bf16[128,1024]{1,0:T(8,128)(2,1)S(1)}, u32[]{:S(2)}, u32[]{:S(2)}) collective-permute-start(bf16[128,1024]{1,0:T(8,128)(2,1)S(1)} %copy-done.38), channel_id=1, source_target_pairs={{0,1},{1,2},{2,3},{3,0},{4,5},{5,6},{6,7},{7,4},{8,9},{9,10},{10,1... | collective-permute-start | bytes 786440 | tf_op jit(solution)/shard_map/ppermute | solution.py:298
  100.7 23.1 %collective-permute-start.10 = (bf16[128,1024]{1,0:T(8,128)(2,1)S(1)}, bf16[128,1024]{1,0:T(8,128)(2,1)}, u32[]{:S(2)}, u32[]{:S(2)}) collective-permute-start(bf16[128,1024]{1,0:T(8,128)(2,1)S(1)} %copy-done.38), channel_id=1, source_target_pairs={{0,2},{1,3},{2,0},{3,1},{4,6},{5,7},{6,4},{7,5},{8,10},{9,11},{10,... | collective-permute-start | bytes 786440 | tf_op jit(solution)/shard_map/ppermute | solution.py:298
  103.2 20.7 %collective-permute-start.11 = (bf16[128,1024]{1,0:T(8,128)(2,1)S(1)}, bf16[128,1024]{1,0:T(8,128)(2,1)}, u32[]{:S(2)}, u32[]{:S(2)}) collective-permute-start(bf16[128,1024]{1,0:T(8,128)(2,1)S(1)} %copy-done.38), channel_id=1, source_target_pairs={{0,3},{1,0},{2,1},{3,2},{4,7},{5,4},{6,5},{7,6},{8,11},{9,8},{10,9... | collective-permute-start | bytes 786440 | tf_op jit(solution)/shard_map/ppermute | solution.py:298
  123.3 16.0 %collective-permute-start.22 = (bf16[1,3,32,4096]{3,2,1,0:T(8,128)(2,1)S(1)}, bf16[1,3,32,4096]{3,2,1,0:T(8,128)(2,1)S(1)}, u32[]{:S(2)}, u32[]{:S(2)}) collective-permute-start(bf16[1,3,32,4096]{3,2,1,0:T(8,128)(2,1)S(1)} %maximum_bitcast_fusion.1.refs_1_), channel_id=1, source_target_pairs={{0,4},{4,0},{8,12},{12,8},{16,20},{20,16},{24,28},{28,24},{1,5},{5... | collective-permute-start | bytes 2359304 | tf_op jit(solution)/shard_map/ppermute | solution.py:294
  123.4 17.8 %collective-permute-start.23 = (bf16[1,3,32,4096]{3,2,1,0:T(8,128)(2,1)}, bf16[1,3,32,4096]{3,2,1,0:T(8,128)(2,1)}, u32[]{:S(2)}, u32[]{:S(2)}) collective-permute-start(bf16[1,3,32,4096]{3,2,1,0:T(8,128)(2,1)} %collective-permute-done.13.refs_2_), channel_id=1, source_target_pairs={{0,4},{4,0},{8,12},{12,8},{16,20},{20,16},{24,28},{28,24},{1,5},{5... | collective-permute-start | bytes 2359304 | tf_op jit(solution)/shard_map/ppermute | solution.py:294
  125.9 12.3 %collective-permute-start.19 = (bf16[1,3,128,1024]{3,2,1,0:T(8,128)(2,1)}, bf16[1,3,128,1024]{3,2,1,0:T(8,128)(2,1)}, u32[]{:S(2)}, u32[]{:S(2)}) collective-permute-start(bf16[1,3,128,1024]{3,2,1,0:T(8,128)(2,1)} %maximum_bitcast_fusion.2.refs_1_), channel_id=1, source_target_pairs={{0,8},{4,20},{8,0},{12,28},{16,24},{20,4},{24,16},{28,12},{1,9},{5... | collective-permute-start | bytes 2359304 | tf_op jit(solution)/shard_map/ppermute | solution.py:473
  126.4 14.7 %collective-permute-start.24 = (bf16[1,3,32,4096]{3,2,1,0:T(8,128)(2,1)}, bf16[1,3,32,4096]{3,2,1,0:T(8,128)(2,1)}, u32[]{:S(2)}, u32[]{:S(2)}) collective-permute-start(bf16[1,3,32,4096]{3,2,1,0:T(8,128)(2,1)} %collective-permute-done.12.refs_3_), channel_id=1, source_target_pairs={{0,4},{4,0},{8,12},{12,8},{16,20},{20,16},{24,28},{28,24},{1,5},{5... | collective-permute-start | bytes 2359304 | tf_op jit(solution)/shard_map/ppermute | solution.py:294
  126.8 14.3 %collective-permute-start.25 = (bf16[1,3,32,4096]{3,2,1,0:T(8,128)(2,1)}, bf16[1,3,32,4096]{3,2,1,0:T(8,128)(2,1)}, u32[]{:S(2)}, u32[]{:S(2)}) collective-permute-start(bf16[1,3,32,4096]{3,2,1,0:T(8,128)(2,1)} %collective-permute-done.18.refs_4_), channel_id=1, source_target_pairs={{0,4},{4,0},{8,12},{12,8},{16,20},{20,16},{24,28},{28,24},{1,5},{5... | collective-permute-start | bytes 2359304 | tf_op jit(solution)/shard_map/ppermute | solution.py:294
  138.2 20.9 %collective-permute-start.20 = (bf16[1,3,128,1024]{3,2,1,0:T(8,128)(2,1)}, bf16[1,3,128,1024]{3,2,1,0:T(8,128)(2,1)}, u32[]{:S(2)}, u32[]{:S(2)}) collective-permute-start(bf16[1,3,128,1024]{3,2,1,0:T(8,128)(2,1)} %maximum_bitcast_fusion.2.refs_1_), channel_id=1, source_target_pairs={{0,16},{4,12},{8,24},{12,4},{16,0},{20,28},{24,8},{28,20},{1,17},{... | collective-permute-start | bytes 2359304 | tf_op jit(solution)/shard_map/ppermute | solution.py:473
  140.2 19.0 %collective-permute-start.21 = (bf16[1,3,128,1024]{3,2,1,0:T(8,128)(2,1)}, bf16[1,3,128,1024]{3,2,1,0:T(8,128)(2,1)}, u32[]{:S(2)}, u32[]{:S(2)}) collective-permute-start(bf16[1,3,128,1024]{3,2,1,0:T(8,128)(2,1)} %collective-permute-done.19.refs_2_), channel_id=1, source_target_pairs={{0,16},{4,12},{8,24},{12,4},{16,0},{20,28},{24,8},{28,20},{1,17},{... | collective-permute-start | bytes 2359304 | tf_op jit(solution)/shard_map/ppermute | solution.py:473
  170.6 20.3 %collective-permute-start.30 = (bf16[4,4,128,1024]{3,2,1,0:T(8,128)(2,1)}, bf16[4,4,128,1024]{3,2,1,0:T(8,128)(2,1)}, u32[]{:S(2)}, u32[]{:S(2)}) collective-permute-start(bf16[4,4,128,1024]{3,2,1,0:T(8,128)(2,1)} %bitcast.24), channel_id=1, source_target_pairs={{0,4},{4,0},{8,12},{12,8},{16,20},{20,16},{24,28},{28,24},{1,5},{5... | collective-permute-start | bytes 12582920 | tf_op jit(solution)/shard_map/ppermute | solution.py:294
  171.4 11.1 %collective-permute-start.28 = (bf16[1,3,128,1024]{3,2,1,0:T(8,128)(2,1)}, bf16[1,3,128,1024]{3,2,1,0:T(8,128)(2,1)S(1)}, u32[]{:S(2)}, u32[]{:S(2)}) collective-permute-start(bf16[1,3,128,1024]{3,2,1,0:T(8,128)(2,1)} %collective-permute-done.20.refs_3_), channel_id=1, source_target_pairs={{0,4},{4,0},{8,12},{12,8},{16,20},{20,16},{24,28},{28,24},{1,5},{5... | collective-permute-start | bytes 2359304 | tf_op jit(solution)/shard_map/ppermute | solution.py:294
  171.8 11.5 %collective-permute-start.29 = (bf16[1,3,128,1024]{3,2,1,0:T(8,128)(2,1)}, bf16[1,3,128,1024]{3,2,1,0:T(8,128)(2,1)}, u32[]{:S(2)}, u32[]{:S(2)}) collective-permute-start(bf16[1,3,128,1024]{3,2,1,0:T(8,128)(2,1)} %collective-permute-done.21.refs_4_), channel_id=1, source_target_pairs={{0,4},{4,0},{8,12},{12,8},{16,20},{20,16},{24,28},{28,24},{1,5},{5... | collective-permute-start | bytes 2359304 | tf_op jit(solution)/shard_map/ppermute | solution.py:294
  211.7 15.2 %collective-permute-start.31 = (bf16[4,4,32,4096]{3,2,1,0:T(8,128)(2,1)}, bf16[4,4,32,4096]{3,2,1,0:T(8,128)(2,1)}, u32[]{:S(2)}, u32[]{:S(2)}) collective-permute-start(bf16[4,4,32,4096]{3,2,1,0:T(8,128)(2,1)} %bitcast.26), channel_id=1, source_target_pairs={{0,4},{4,0},{8,12},{12,8},{16,20},{20,16},{24,28},{28,24},{1,5},{5... | collective-permute-start | bytes 12582920 | tf_op jit(solution)/shard_map/ppermute | solution.py:294
  212.2 27.6 %collective-permute-start.32 = (bf16[2,4,128,1024]{3,2,1,0:T(8,128)(2,1)S(1)}, bf16[2,4,128,1024]{3,2,1,0:T(8,128)(2,1)}, u32[]{:S(2)}, u32[]{:S(2)}) collective-permute-start(bf16[2,4,128,1024]{3,2,1,0:T(8,128)(2,1)S(1)} %fusion.6), channel_id=1, source_target_pairs={{0,8},{4,20},{8,0},{12,28},{16,24},{20,4},{24,16},{28,12},{1,9},{5... | collective-permute-start | bytes 6291464 | tf_op jit(solution)/shard_map/ppermute | solution.py:322
  232.3 39.7 %collective-permute-start.34 = (bf16[2,4,32,4096]{3,2,1,0:T(8,128)(2,1)}, bf16[2,4,32,4096]{3,2,1,0:T(8,128)(2,1)}, u32[]{:S(2)}, u32[]{:S(2)}) collective-permute-start(bf16[2,4,32,4096]{3,2,1,0:T(8,128)(2,1)} %fusion.5), channel_id=1, source_target_pairs={{0,8},{4,20},{8,0},{12,28},{16,24},{20,4},{24,16},{28,12},{1,9},{5... | collective-permute-start | bytes 6291464 | tf_op jit(solution)/shard_map/ppermute | solution.py:322
  244.8 26.3 %collective-permute-start.33 = (bf16[1,4,128,1024]{3,2,1,0:T(8,128)(2,1)}, bf16[1,4,128,1024]{3,2,1,0:T(8,128)(2,1)}, u32[]{:S(2)}, u32[]{:S(2)}) collective-permute-start(bf16[1,4,128,1024]{3,2,1,0:T(8,128)(2,1)} %fusion.16), channel_id=1, source_target_pairs={{0,16},{4,12},{8,24},{12,4},{16,0},{20,28},{24,8},{28,20},{1,17},{... | collective-permute-start | bytes 3145736 | tf_op jit(solution)/shard_map/ppermute | solution.py:322
  245.8 25.3 %collective-permute-start.35 = (bf16[4,4,32,1024]{3,2,1,0:T(8,128)(2,1)}, bf16[4,4,32,1024]{3,2,1,0:T(8,128)(2,1)}, u32[]{:S(2)}, u32[]{:S(2)}) collective-permute-start(bf16[4,4,32,1024]{3,2,1,0:T(8,128)(2,1)} %bitcast.29), channel_id=1, source_target_pairs={{0,4},{4,0},{8,12},{12,8},{16,20},{20,16},{24,28},{28,24},{1,5},{5... | collective-permute-start | bytes 3145736 | tf_op jit(solution)/shard_map/ppermute | solution.py:294
  280.4 27.3 %collective-permute-start.39 = (bf16[1,4,32,4096]{3,2,1,0:T(8,128)(2,1)}, bf16[1,4,32,4096]{3,2,1,0:T(8,128)(2,1)S(1)}, u32[]{:S(2)}, u32[]{:S(2)}) collective-permute-start(bf16[1,4,32,4096]{3,2,1,0:T(8,128)(2,1)} %fusion.14), channel_id=1, source_target_pairs={{0,16},{4,12},{8,24},{12,4},{16,0},{20,28},{24,8},{28,20},{1,17},{... | collective-permute-start | bytes 3145736 | tf_op jit(solution)/shard_map/ppermute | solution.py:322
  281.4 26.3 %collective-permute-start.40 = (bf16[2,4,32,1024]{3,2,1,0:T(8,128)(2,1)}, bf16[2,4,32,1024]{3,2,1,0:T(8,128)(2,1)}, u32[]{:S(2)}, u32[]{:S(2)}) collective-permute-start(bf16[2,4,32,1024]{3,2,1,0:T(8,128)(2,1)} %fusion.26), channel_id=1, source_target_pairs={{0,8},{4,20},{8,0},{12,28},{16,24},{20,4},{24,16},{28,12},{1,9},{5... | collective-permute-start | bytes 1572872 | tf_op jit(solution)/shard_map/ppermute | solution.py:322
  281.9 25.7 %collective-permute-start.36 = (bf16[128,1024]{1,0:T(8,128)(2,1)}, bf16[128,1024]{1,0:T(8,128)(2,1)}, u32[]{:S(2)}, u32[]{:S(2)}) collective-permute-start(bf16[128,1024]{1,0:T(8,128)(2,1)} %get-tuple-element.197), channel_id=1, source_target_pairs={{0,1},{1,2},{2,3},{3,0},{4,5},{5,6},{6,7},{7,4},{8,9},{9,10},{10,1... | collective-permute-start | bytes 786440 | tf_op jit(solution)/shard_map/ppermute | solution.py:298
  283.9 23.7 %collective-permute-start.37 = (bf16[128,1024]{1,0:T(8,128)(2,1)}, bf16[128,1024]{1,0:T(8,128)(2,1)}, u32[]{:S(2)}, u32[]{:S(2)}) collective-permute-start(bf16[128,1024]{1,0:T(8,128)(2,1)} %get-tuple-element.198), channel_id=1, source_target_pairs={{0,2},{1,3},{2,0},{3,1},{4,6},{5,7},{6,4},{7,5},{8,10},{9,11},{10,... | collective-permute-start | bytes 786440 | tf_op jit(solution)/shard_map/ppermute | solution.py:298
  284.4 23.3 %collective-permute-start.38 = (bf16[128,1024]{1,0:T(8,128)(2,1)}, bf16[128,1024]{1,0:T(8,128)(2,1)}, u32[]{:S(2)}, u32[]{:S(2)}) collective-permute-start(bf16[128,1024]{1,0:T(8,128)(2,1)} %get-tuple-element.199), channel_id=1, source_target_pairs={{0,3},{1,0},{2,1},{3,2},{4,7},{5,4},{6,5},{7,6},{8,11},{9,8},{10,9... | collective-permute-start | bytes 786440 | tf_op jit(solution)/shard_map/ppermute | solution.py:298
  319.6 21.8 %collective-permute-start.41 = (bf16[4,4,32,3072]{3,2,1,0:T(8,128)(2,1)}, bf16[4,4,32,3072]{3,2,1,0:T(8,128)(2,1)}, u32[]{:S(2)}, u32[]{:S(2)}) collective-permute-start(bf16[4,4,32,3072]{3,2,1,0:T(8,128)(2,1)} %bitcast.55), channel_id=1, source_target_pairs={{0,4},{4,0},{8,12},{12,8},{16,20},{20,16},{24,28},{28,24},{1,5},{5... | collective-permute-start | bytes 9437192 | tf_op jit(solution)/shard_map/ppermute | solution.py:294
  322.2 14.3 %collective-permute-start.42 = (bf16[1,128,1024]{2,1,0:T(8,128)(2,1)S(1)}, bf16[1,128,1024]{2,1,0:T(8,128)(2,1)S(1)}, u32[]{:S(2)}, u32[]{:S(2)}) collective-permute-start(bf16[1,128,1024]{2,1,0:T(8,128)(2,1)S(1)} %fusion.64), channel_id=1, source_target_pairs={{0,8},{4,20},{8,0},{12,28},{16,24},{20,4},{24,16},{28,12},{1,9},{5... | collective-permute-start | bytes 786440 | tf_op jit(solution)/shard_map/ppermute | solution.py:305
  323.7 14.7 %collective-permute-start.43 = (bf16[1,128,1024]{2,1,0:T(8,128)(2,1)S(1)}, bf16[1,128,1024]{2,1,0:T(8,128)(2,1)S(1)}, u32[]{:S(2)}, u32[]{:S(2)}) collective-permute-start(bf16[1,128,1024]{2,1,0:T(8,128)(2,1)S(1)} %fusion.64), channel_id=1, source_target_pairs={{0,16},{4,12},{8,24},{12,4},{16,0},{20,28},{24,8},{28,20},{1,17},{... | collective-permute-start | bytes 786440 | tf_op jit(solution)/shard_map/ppermute | solution.py:305
  324.7 15.7 %collective-permute-start.44 = (bf16[1,128,1024]{2,1,0:T(8,128)(2,1)S(1)}, bf16[1,128,1024]{2,1,0:T(8,128)(2,1)S(1)}, u32[]{:S(2)}, u32[]{:S(2)}) collective-permute-start(bf16[1,128,1024]{2,1,0:T(8,128)(2,1)S(1)} %fusion.64), channel_id=1, source_target_pairs={{0,24},{4,28},{8,16},{12,20},{16,8},{20,12},{24,0},{28,4},{1,25},{... | collective-permute-start | bytes 786440 | tf_op jit(solution)/shard_map/ppermute | solution.py:305
  335.8 18.1 %collective-permute-start.47 = (bf16[32,4096]{1,0:T(8,128)(2,1)S(1)}, bf16[32,4096]{1,0:T(8,128)(2,1)S(1)}, u32[]{:S(2)}, u32[]{:S(2)}) collective-permute-start(bf16[32,4096]{1,0:T(8,128)(2,1)S(1)} %copy-done.48), channel_id=1, source_target_pairs={{0,1},{1,2},{2,3},{3,0},{4,5},{5,6},{6,7},{7,4},{8,9},{9,10},{10,1... | collective-permute-start | bytes 786440 | tf_op jit(solution)/shard_map/ppermute | solution.py:298
  336.6 23.7 %collective-permute-start.48 = (bf16[32,4096]{1,0:T(8,128)(2,1)}, bf16[32,4096]{1,0:T(8,128)(2,1)}, u32[]{:S(2)}, u32[]{:S(2)}) collective-permute-start(bf16[32,4096]{1,0:T(8,128)(2,1)} %get-tuple-element.226), channel_id=1, source_target_pairs={{0,2},{1,3},{2,0},{3,1},{4,6},{5,7},{6,4},{7,5},{8,10},{9,11},{10,... | collective-permute-start | bytes 786440 | tf_op jit(solution)/shard_map/ppermute | solution.py:298
  338.4 21.8 %collective-permute-start.49 = (bf16[32,4096]{1,0:T(8,128)(2,1)}, bf16[32,4096]{1,0:T(8,128)(2,1)}, u32[]{:S(2)}, u32[]{:S(2)}) collective-permute-start(bf16[32,4096]{1,0:T(8,128)(2,1)} %get-tuple-element.227), channel_id=1, source_target_pairs={{0,3},{1,0},{2,1},{3,2},{4,7},{5,4},{6,5},{7,6},{8,11},{9,8},{10,9... | collective-permute-start | bytes 786440 | tf_op jit(solution)/shard_map/ppermute | solution.py:298
  340.4 19.8 %collective-permute-start.50 = (bf16[1,4,32,1024]{3,2,1,0:T(8,128)(2,1)}, bf16[1,4,32,1024]{3,2,1,0:T(8,128)(2,1)}, u32[]{:S(2)}, u32[]{:S(2)}) collective-permute-start(bf16[1,4,32,1024]{3,2,1,0:T(8,128)(2,1)} %fusion.38), channel_id=1, source_target_pairs={{0,16},{4,12},{8,24},{12,4},{16,0},{20,28},{24,8},{28,20},{1,17},{... | collective-permute-start | bytes 786440 | tf_op jit(solution)/shard_map/ppermute | solution.py:322
  352.4 20.8 %collective-permute-start.45 = (bf16[2,4,32,3072]{3,2,1,0:T(8,128)(2,1)}, bf16[2,4,32,3072]{3,2,1,0:T(8,128)(2,1)}, u32[]{:S(2)}, u32[]{:S(2)}) collective-permute-start(bf16[2,4,32,3072]{3,2,1,0:T(8,128)(2,1)} %fusion.10), channel_id=1, source_target_pairs={{0,8},{4,20},{8,0},{12,28},{16,24},{20,4},{24,16},{28,12},{1,9},{5... | collective-permute-start | bytes 4718600 | tf_op jit(solution)/shard_map/ppermute | solution.py:322
  380.1 14.0 %collective-permute-start.72 = (bf16[1,32,4096]{2,1,0:T(8,128)(2,1)S(1)}, bf16[1,32,4096]{2,1,0:T(8,128)(2,1)}, u32[]{:S(2)}, u32[]{:S(2)}) collective-permute-start(bf16[1,32,4096]{2,1,0:T(8,128)(2,1)S(1)} %fusion.65), channel_id=1, source_target_pairs={{0,8},{4,20},{8,0},{12,28},{16,24},{20,4},{24,16},{28,12},{1,9},{5... | collective-permute-start | bytes 786440 | tf_op jit(solution)/shard_map/ppermute | solution.py:305
  381.5 15.2 %collective-permute-start.73 = (bf16[1,32,4096]{2,1,0:T(8,128)(2,1)S(1)}, bf16[1,32,4096]{2,1,0:T(8,128)(2,1)}, u32[]{:S(2)}, u32[]{:S(2)}) collective-permute-start(bf16[1,32,4096]{2,1,0:T(8,128)(2,1)S(1)} %fusion.65), channel_id=1, source_target_pairs={{0,16},{4,12},{8,24},{12,4},{16,0},{20,28},{24,8},{28,20},{1,17},{... | collective-permute-start | bytes 786440 | tf_op jit(solution)/shard_map/ppermute | solution.py:305
  388.8 19.3 %collective-permute-start.74 = (bf16[1,32,4096]{2,1,0:T(8,128)(2,1)S(1)}, bf16[1,32,4096]{2,1,0:T(8,128)(2,1)S(1)}, u32[]{:S(2)}, u32[]{:S(2)}) collective-permute-start(bf16[1,32,4096]{2,1,0:T(8,128)(2,1)S(1)} %fusion.65), channel_id=1, source_target_pairs={{0,24},{4,28},{8,16},{12,20},{16,8},{20,12},{24,0},{28,4},{1,25},{... | collective-permute-start | bytes 786440 | tf_op jit(solution)/shard_map/ppermute | solution.py:305
  390.2 16.1 %collective-permute-start.51 = (bf16[1,4,32,3072]{3,2,1,0:T(8,128)(2,1)}, bf16[1,4,32,3072]{3,2,1,0:T(8,128)(2,1)S(1)}, u32[]{:S(2)}, u32[]{:S(2)}) collective-permute-start(bf16[1,4,32,3072]{3,2,1,0:T(8,128)(2,1)} %fusion.21), channel_id=1, source_target_pairs={{0,16},{4,12},{8,24},{12,4},{16,0},{20,28},{24,8},{28,20},{1,17},{... | collective-permute-start | bytes 2359304 | tf_op jit(solution)/shard_map/ppermute | solution.py:322
  393.0 38.6 %collective-permute-start.70 = (bf16[1,32,1024]{2,1,0:T(8,128)(2,1)S(1)}, bf16[1,32,1024]{2,1,0:T(8,128)(2,1)S(1)}, u32[]{:S(2)}, u32[]{:S(2)}) collective-permute-start(bf16[1,32,1024]{2,1,0:T(8,128)(2,1)S(1)} %fusion.77), channel_id=1, source_target_pairs={{0,24},{4,28},{8,16},{12,20},{16,8},{20,12},{24,0},{28,4},{1,25},{... | collective-permute-start | bytes 196616 | tf_op jit(solution)/shard_map/ppermute | solution.py:305
  394.1 39.5 %collective-permute-start.69 = (bf16[1,32,1024]{2,1,0:T(8,128)(2,1)S(1)}, bf16[1,32,1024]{2,1,0:T(8,128)(2,1)S(1)}, u32[]{:S(2)}, u32[]{:S(2)}) collective-permute-start(bf16[1,32,1024]{2,1,0:T(8,128)(2,1)S(1)} %fusion.77), channel_id=1, source_target_pairs={{0,16},{4,12},{8,24},{12,4},{16,0},{20,28},{24,8},{28,20},{1,17},{... | collective-permute-start | bytes 196616 | tf_op jit(solution)/shard_map/ppermute | solution.py:305
  411.3 17.9 %collective-permute-start.59 = (bf16[32,3072]{1,0:T(8,128)(2,1)S(1)}, bf16[32,3072]{1,0:T(8,128)(2,1)S(1)}, u32[]{:S(2)}, u32[]{:S(2)}) collective-permute-start(bf16[32,3072]{1,0:T(8,128)(2,1)S(1)} %get-tuple-element.243), channel_id=1, source_target_pairs={{0,2},{1,3},{2,0},{3,1},{4,6},{5,7},{6,4},{7,5},{8,10},{9,11},{10,... | collective-permute-start | bytes 589832 | tf_op jit(solution)/shard_map/ppermute | solution.py:298
  411.4 17.9 %collective-permute-start.58 = (bf16[32,3072]{1,0:T(8,128)(2,1)S(1)}, bf16[32,3072]{1,0:T(8,128)(2,1)S(1)}, u32[]{:S(2)}, u32[]{:S(2)}) collective-permute-start(bf16[32,3072]{1,0:T(8,128)(2,1)S(1)} %get-tuple-element.242), channel_id=1, source_target_pairs={{0,1},{1,2},{2,3},{3,0},{4,5},{5,6},{6,7},{7,4},{8,9},{9,10},{10,1... | collective-permute-start | bytes 589832 | tf_op jit(solution)/shard_map/ppermute | solution.py:298
  416.7 17.9 %collective-permute-start.68 = (bf16[1,32,1024]{2,1,0:T(8,128)(2,1)S(1)}, bf16[1,32,1024]{2,1,0:T(8,128)(2,1)S(1)}, u32[]{:S(2)}, u32[]{:S(2)}) collective-permute-start(bf16[1,32,1024]{2,1,0:T(8,128)(2,1)S(1)} %fusion.77), channel_id=1, source_target_pairs={{0,8},{4,20},{8,0},{12,28},{16,24},{20,4},{24,16},{28,12},{1,9},{5... | collective-permute-start | bytes 196616 | tf_op jit(solution)/shard_map/ppermute | solution.py:305
  429.2 31.5 %collective-permute-start.75 = (bf16[4,32,4096]{2,1,0:T(8,128)(2,1)}, bf16[4,32,4096]{2,1,0:T(8,128)(2,1)}, u32[]{:S(2)}, u32[]{:S(2)}) collective-permute-start(bf16[4,32,4096]{2,1,0:T(8,128)(2,1)} %constant_dynamic-update-slice_fusion.refs_0_), channel_id=1, source_target_pairs={{0,4},{4,0},{8,12},{12,8},{16,20},{20,16},{24,28},{28,24},{1,5},{5... | collective-permute-start | bytes 3145736 | tf_op jit(solution)/shard_map/ppermute | solution.py:294
  431.6 11.5 %collective-permute-start.63 = (bf16[1,32,3072]{2,1,0:T(8,128)(2,1)}, bf16[1,32,3072]{2,1,0:T(8,128)(2,1)S(1)}, u32[]{:S(2)}, u32[]{:S(2)}) collective-permute-start(bf16[1,32,3072]{2,1,0:T(8,128)(2,1)} %fusion.68), channel_id=1, source_target_pairs={{0,24},{4,28},{8,16},{12,20},{16,8},{20,12},{24,0},{28,4},{1,25},{... | collective-permute-start | bytes 589832 | tf_op jit(solution)/shard_map/ppermute | solution.py:305
  433.6 12.0 %collective-permute-start.62 = (bf16[1,32,3072]{2,1,0:T(8,128)(2,1)}, bf16[1,32,3072]{2,1,0:T(8,128)(2,1)S(1)}, u32[]{:S(2)}, u32[]{:S(2)}) collective-permute-start(bf16[1,32,3072]{2,1,0:T(8,128)(2,1)} %fusion.68), channel_id=1, source_target_pairs={{0,16},{4,12},{8,24},{12,4},{16,0},{20,28},{24,8},{28,20},{1,17},{... | collective-permute-start | bytes 589832 | tf_op jit(solution)/shard_map/ppermute | solution.py:305
  435.2 11.2 %collective-permute-start.61 = (bf16[1,32,3072]{2,1,0:T(8,128)(2,1)}, bf16[1,32,3072]{2,1,0:T(8,128)(2,1)S(1)}, u32[]{:S(2)}, u32[]{:S(2)}) collective-permute-start(bf16[1,32,3072]{2,1,0:T(8,128)(2,1)} %fusion.68), channel_id=1, source_target_pairs={{0,8},{4,20},{8,0},{12,28},{16,24},{20,4},{24,16},{28,12},{1,9},{5... | collective-permute-start | bytes 589832 | tf_op jit(solution)/shard_map/ppermute | solution.py:305
  438.5 14.2 %collective-permute-start.71 = (bf16[4,32,1024]{2,1,0:T(8,128)(2,1)S(1)}, bf16[4,32,1024]{2,1,0:T(8,128)(2,1)S(1)}, u32[]{:S(2)}, u32[]{:S(2)}) collective-permute-start(bf16[4,32,1024]{2,1,0:T(8,128)(2,1)S(1)} %pad_maximum_fusion.3.refs_0_), channel_id=1, source_target_pairs={{0,4},{4,0},{8,12},{12,8},{16,20},{20,16},{24,28},{28,24},{1,5},{5... | collective-permute-start | bytes 786440 | tf_op jit(solution)/shard_map/ppermute | solution.py:294
  447.5 18.9 %collective-permute-start.64 = (bf16[4,32,3072]{2,1,0:T(8,128)(2,1)S(1)}, bf16[4,32,3072]{2,1,0:T(8,128)(2,1)S(1)}, u32[]{:S(2)}, u32[]{:S(2)}) collective-permute-start(bf16[4,32,3072]{2,1,0:T(8,128)(2,1)S(1)} %pad_maximum_fusion.1.refs_0_), channel_id=1, source_target_pairs={{0,4},{4,0},{8,12},{12,8},{16,20},{20,16},{24,28},{28,24},{1,5},{5... | collective-permute-start | bytes 2359304 | tf_op jit(solution)/shard_map/ppermute | solution.py:294
  451.7 12.8 %collective-permute-start.57 = (f32[64,256]{1,0:T(8,128)S(1)}, f32[64,256]{1,0:T(8,128)S(1)}, u32[]{:S(2)}, u32[]{:S(2)}) collective-permute-start(f32[64,256]{1,0:T(8,128)S(1)} %bitcast.286), channel_id=1, source_target_pairs={{0,3},{1,0},{2,1},{3,2},{4,7},{5,4},{6,5},{7,6},{8,11},{9,8},{10,9... | collective-permute-start | bytes 196616 | tf_op jit(solution)/shard_map/ppermute | solution.py:298
  451.8 12.7 %collective-permute-start.56 = (f32[64,256]{1,0:T(8,128)S(1)}, f32[64,256]{1,0:T(8,128)S(1)}, u32[]{:S(2)}, u32[]{:S(2)}) collective-permute-start(f32[64,256]{1,0:T(8,128)S(1)} %bitcast.287), channel_id=1, source_target_pairs={{0,2},{1,3},{2,0},{3,1},{4,6},{5,7},{6,4},{7,5},{8,10},{9,11},{10,... | collective-permute-start | bytes 196616 | tf_op jit(solution)/shard_map/ppermute | solution.py:298
  452.8 11.8 %collective-permute-start.55 = (f32[64,256]{1,0:T(8,128)S(1)}, f32[64,256]{1,0:T(8,128)S(1)}, u32[]{:S(2)}, u32[]{:S(2)}) collective-permute-start(f32[64,256]{1,0:T(8,128)S(1)} %bitcast.288), channel_id=1, source_target_pairs={{0,1},{1,2},{2,3},{3,0},{4,5},{5,6},{6,7},{7,4},{8,9},{9,10},{10,1... | collective-permute-start | bytes 196616 | tf_op jit(solution)/shard_map/ppermute | solution.py:298
  (97 other events, 1382.0 us)

commit v11 on v9

--- a/solution.py
+++ b/solution.py
@@ -715,8 +715,8 @@
         axis=1,
     )
     run_small = plan.total_small(rows_small)
-    (sum_fc2,) = run_fc2.result()
-    (sum_fc1,) = run_fc1.result()
+    (sum_fc2,) = tick(run_fc2.result(), [run_qkv])
+    (sum_fc1,) = tick(run_fc1.result(), [run_qkv])
     (sum_out,) = run_out.result()
     (sum_qkv,) = run_qkv.result()
     small = run_small.result()

time: 472 us -> 467 us (0.989)
  waiting for transfers between devices: 97.6 us -> 83.4 us
  starting transfers between devices: 79 us -> 87.5 us
    ppermute x24, waiting for transfers between devices: 54.1 us -> 46.4 us  [ahead(): lax.ppermute(block, 'fsdp', [(i, (i + step) % n_line) for i in range(n_li...]
    ppermute x12, waiting for transfers between devices: 6.52 us -> 0.03 us  [plane_hops(): return [lax.ppermute(block, 'dp', pairs) for pairs in hops]]
    ppermute x24, starting transfers between devices: 41.8 us -> 47.6 us  [ahead(): lax.ppermute(block, 'fsdp', [(i, (i + step) % n_line) for i in range(n_li...]
    unnamed x174 -> x184, local copies, waits for them, and re-layouts: 17 us -> 18.4 us
  transfers between devices with their start and end apart: 76 -> 76, of which waited for: 23 -> 21; matrix products, arithmetic and copies ran while one was open for 25% -> 25% of each run, Pallas kernels for 19% -> 19%
where the time goes in v11:
time: 467 us; the launch traced here: 460 us
  matrix products  95.5 us (20%)
  Pallas kernels  95 us (20%)
  starting transfers between devices  87.5 us (19%)
  waiting for transfers between devices  83.4 us (18%)
  other arithmetic  59.8 us (13%)
  local copies, waits for them, and re-layouts  37.1 us (8%)
    ppermute x24, starting transfers between devices, ahead(): lax.ppermute(block, 'fsdp', [(i, (i + step) % n_line) for i in range(n_li...  47.6 us
    ppermute x24, waiting for transfers between devices, ahead(): lax.ppermute(block, 'fsdp', [(i, (i + step) % n_line) for i in range(n_li...  46.4 us
    pallas_call x2, Pallas kernels, attend_back(): pl.pallas_call(body, grid=(count,), in_specs=pair_specs(rows, pairs, star...  37.7 us
    dot_general x4, matrix products, times_t(): lax.dot_general(left, right, (((1,), (1,)), ((), ())), preferred_element_...  27.7 us
    dot_general x8, matrix products, t_times(): lax.dot_general(left, right, (((0,), (0,)), ((), ())), preferred_element_...  25.7 us
    convert_element_type x8, other arithmetic, reduce_steps(): add_up([term[half:] for term in terms]).astype(jnp.bfloat16)  23.3 us
    pallas_call x3, Pallas kernels, assemble(): pl.pallas_call(body, in_specs=[pl.BlockSpec(memory_space=pltpu.SMEM)] + [...  22.8 us
    unnamed x184, local copies, waits for them, and re-layouts  18.4 us
  transfers between devices with their start and end apart: 76, of which 21 were waited for; matrix products, arithmetic and copies ran while one was open for 25% of the time, Pallas kernels for 19%

profile of v11, /device:TPU:0, one launch (start us, length us, event | category | flops | bytes accessed | tf_op | source)
XLA Modules:
  0.0 460.4 jit_solution(6288111047061613621)
XLA Ops:
  6.6 3.1 collective-permute-start
  9.7 2.6 collective-permute-start.1
  19.7 11.8 %collective-permute-done.1 = bf16[32,4608]{1,0:T(8,128)(2,1)S(1)} collective-permute-done((bf16[32,4608]{1,0:T(8,128)(2,1)S(1)}, bf16[32,4608]{1,0:T(8,128)(2,1)S(1)}, u32[]{:S(2)}, u32[]{:S(2)}) %collective-permute-start.1) | collective-permute-done | bytes 294944 | tf_op jit(solution)/shard_map/ppermute | solution.py:298
  35.6 6.8 %collective-permute-start.5 = (bf16[32,4096]{1,0:T(8,128)(2,1)S(1)}, bf16[32,4096]{1,0:T(8,128)(2,1)S(1)}, u32[]{:S(2)}, u32[]{:S(2)}) collective-permute-start(bf16[32,4096]{1,0:T(8,128)(2,1)S(1)} %constant_dynamic-slice_fusion.5), channel_id=1, source_target_pairs={{0,1},{1,2},{2,3},{3,0},{4,5},{5,6},{6,7},{7,4},{8,9},{9,10},{10,1... | collective-permute-start | bytes 786440 | tf_op jit(solution)/shard_map/ppermute | solution.py:298
  45.6 5.1 %collective-permute-done.5 = bf16[32,4096]{1,0:T(8,128)(2,1)S(1)} collective-permute-done((bf16[32,4096]{1,0:T(8,128)(2,1)S(1)}, bf16[32,4096]{1,0:T(8,128)(2,1)S(1)}, u32[]{:S(2)}, u32[]{:S(2)}) %collective-permute-start.5) | collective-permute-done | bytes 262176 | tf_op jit(solution)/shard_map/ppermute | solution.py:298
  50.7 9.0 %collective-permute-done.6 = bf16[32,4096]{1,0:T(8,128)(2,1)S(1)} collective-permute-done((bf16[32,4096]{1,0:T(8,128)(2,1)S(1)}, bf16[32,4096]{1,0:T(8,128)(2,1)S(1)}, u32[]{:S(2)}, u32[]{:S(2)}) %collective-permute-start.6) | collective-permute-done | bytes 262176 | tf_op jit(solution)/shard_map/ppermute | solution.py:298
  62.1 9.8 %collective-permute-done.8.refs_5_ = bf16[1,3,32,4096]{3,2,1,0:T(8,128)(2,1)S(1)} collective-permute-done((bf16[1,3,32,4096]{3,2,1,0:T(8,128)(2,1)}, bf16[1,3,32,4096]{3,2,1,0:T(8,128)(2,1)S(1)}, u32[]{:S(2)}, u32[]{:S(2)}) %collective-permute-start.8) | collective-permute-done | bytes 786464 | tf_op jit(solution)/shard_map/ppermute | solution.py:473
  75.7 7.7 %assemble.3 = (bf16[1024,3072]{1,0:T(8,128)(2,1)}, bf16[1024,1024]{1,0:T(8,128)(2,1)}) custom-call(s32[33]{0:T(128)} %pad_add_fusion.1.table_ref, bf16[256,3072]{1,0:T(8,128)(2,1)} %refs_0_.3, bf16[256,1024]{1,0:T(8,128)(2,1)} %refs_1_.1, bf16[1,3,32,4096]{3,2,1,0:T(8,128)(2,1)} %maximum_bitcast_fusion.refs_2_, ...), custom_call_target="tpu_custom_call" | custom-call | tf_op jit(solution)/shard_map/assemble/pallas_call | solution.py:225
  83.4 7.8 %convolution_convert_fusion.4.refs_2_.refs_3_.refs_4_ = bf16[512,3072]{1,0:T(8,128)(2,1)} fusion(bf16[1024,3072]{1,0:T(8,128)(2,1)} %get-tuple-element.172, f32[512,1024]{1,0:T(8,128)S(1)} %get-tuple-element.329, f32[1024]{0:T(1024)S(1)} %bitcast.298, f32[1024]{0:T(1024)S(1)} %bitcast.290, f32[512]{0:T(512)S(1)} %fusion.86, f32[512]{0:T(512)S(1)} %broadcast_multiply_fusion.1), kind=kOutput, calls=%fused_computation.15 | convolution fusion | flops 3225419776 | bytes 11546624 | tf_op jit(solution)/shard_map/dot_general | solution.py:654
  94.1 6.0 %collective-permute-start.9 = (bf16[128,1024]{1,0:T(8,128)(2,1)S(1)}, bf16[128,1024]{1,0:T(8,128)(2,1)S(1)}, u32[]{:S(2)}, u32[]{:S(2)}) collective-permute-start(bf16[128,1024]{1,0:T(8,128)(2,1)S(1)} %copy-done.43), channel_id=1, source_target_pairs={{0,1},{1,2},{2,3},{3,0},{4,5},{5,6},{6,7},{7,4},{8,9},{9,10},{10,1... | collective-permute-start | bytes 786440 | tf_op jit(solution)/shard_map/ppermute | solution.py:298
  100.1 2.4 collective-permute-start.10
  106.8 15.8 %attend.1 = bf16[512,1024]{1,0:T(8,128)(2,1)} custom-call(s32[512,1]{1,0:T(8,128)} %fusion.59.refs_0_, s32[1,512]{1,0:T(1,128)} %broadcast_select_fusion.2.refs_1_, bf16[512,3072]{1,0:T(8,128)(2,1)} %convolution_convert_fusion.4.refs_2_.refs_3_.refs_4_, bf16[512,3072]{1,0:T(8,128)(2,1)} %convolution_convert_fusion.4.refs_2_.refs_3_.refs_4_, ...), custom_call_target="tpu_custom_call" | custom-call | tf_op jit(solution)/shard_map/attend/pallas_call | solution.py:148
  123.2 2.0 maximum_bitcast_fusion.2.refs_1_
  126.5 3.3 fusion.103
  131.9 5.6 %collective-permute-done.19.refs_2_ = bf16[1,3,128,1024]{3,2,1,0:T(8,128)(2,1)} collective-permute-done((bf16[1,3,128,1024]{3,2,1,0:T(8,128)(2,1)}, bf16[1,3,128,1024]{3,2,1,0:T(8,128)(2,1)}, u32[]{:S(2)}, u32[]{:S(2)}) %collective-permute-start.19) | collective-permute-done | bytes 786464 | tf_op jit(solution)/shard_map/ppermute | solution.py:473
  140.4 7.5 %assemble.4 = bf16[1024,4096]{1,0:T(8,128)(2,1)} custom-call(s32[33]{0:T(128)} %pad_add_fusion.1.table_ref, bf16[256,4096]{1,0:T(8,128)(2,1)} %refs_0_.4, bf16[1,3,32,4096]{3,2,1,0:T(8,128)(2,1)} %copy-done.19, bf16[1,3,32,4096]{3,2,1,0:T(8,128)(2,1)} %collective-permute-done.13.refs_2_, bf16[1,3,32,4096]{3,2,1,0:T(8,128)(2,1)} %collective-permute-done.12.refs_3_, ...), custom_call_target="tpu_custom_call" | custom-call | tf_op jit(solution)/shard_map/assemble/pallas_call | solution.py:225
  148.0 10.4 %multiply_convert_fusion.1 = (bf16[512,4096]{1,0:T(8,128)(2,1)}, f32[512,4096]{1,0:T(8,128)}) fusion(f32[4096]{0:T(1024)S(1)} %bitcast.295, bf16[512,1024]{1,0:T(8,128)(2,1)S(1)} %copy-done.28, bf16[1024,4096]{1,0:T(8,128)(2,1)} %assemble.4), kind=kOutput, calls=%fused_computation.9 | convolution fusion | flops 4307550208 | bytes 22036480 | tf_op jit(solution)/shard_map/dot_general | solution.py:661
  158.5 5.5 %column_order.1 = bf16[512,4096]{1,0:T(8,128)(2,1)} custom-call(s32[32]{0:T(128)} %add.550.table_ref, bf16[512,4096]{1,0:T(8,128)(2,1)} %get-tuple-element.252.in_ref), custom_call_target="tpu_custom_call" | custom-call | tf_op jit(solution)/shard_map/column_order/pallas_call | solution.py:245
  164.0 6.0 %convolution_convert_fusion.6 = bf16[2048,1024]{1,0:T(8,128)(2,1)} fusion(bf16[512,4096]{1,0:T(8,128)(2,1)} %column_order.1, bf16[512,1024]{1,0:T(8,128)(2,1)S(1)} %copy-done.17, pred[512]{0:T(512)(128)(4,1)S(1)} %copy-done.75), kind=kOutput, calls=%fused_computation.25 | convolution fusion | flops 2150105088 | bytes 7340544 | tf_op jit(solution)/shard_map/dot_general | solution.py:69
  171.2 3.7 fusion.22
  174.9 2.5 convolution_convert_fusion.5
  182.6 7.6 %assemble.5 = bf16[4096,1024]{1,0:T(8,128)(2,1)} custom-call(s32[33]{0:T(128)} %pad_add_fusion.1.table_ref, bf16[1024,1024]{1,0:T(8,128)(2,1)} %refs_0_.5, bf16[1,3,128,1024]{3,2,1,0:T(8,128)(2,1)} %maximum_bitcast_fusion.2.refs_1_, bf16[1,3,128,1024]{3,2,1,0:T(8,128)(2,1)} %collective-permute-done.19.refs_2_, ...), custom_call_target="tpu_custom_call" | custom-call | tf_op jit(solution)/shard_map/assemble/pallas_call | solution.py:225
  190.3 3.4 fusion.6
  193.6 11.7 %convert_reduce_fusion = (f32[4096]{0:T(1024)}, bf16[512,4096]{1,0:T(8,128)(2,1)S(1)}) fusion(f32[512,4096]{1,0:T(8,128)} %get-tuple-element.333, f32[4096]{0:T(1024)S(1)} %bitcast.296, bf16[4096,1024]{1,0:T(8,128)(2,1)} %assemble.5, bf16[512,1024]{1,0:T(8,128)(2,1)S(1)} %copy-done.17, pred[512]{0:T(512)(128)(4,1)S(1)} %copy-done.75), kind=kOutput, calls=%fused_computation.7 | convolution fusion | flops 4326944768 | bytes 22053376 | tf_op jit(solution)/shard_map/dot_general | solution.py:65
  205.3 5.7 %convolution_convert_fusion.1 = bf16[512,4096]{1,0:T(8,128)(2,1)} fusion(bf16[512,4096]{1,0:T(8,128)(2,1)S(1)} %get-tuple-element.196, bf16[512,1024]{1,0:T(8,128)(2,1)} %fusion.22), kind=kOutput, calls=%fused_computation.12 | convolution fusion | flops 2149580800 | bytes 8912896 | tf_op jit(solution)/shard_map/dot_general | solution.py:69
  212.0 6.8 %multiply_reduce_fusion = (f32[1024]{0:T(1024)}, f32[512]{0:T(512)S(1)}, f32[1024]{0:T(1024)}, f32[512,1024]{1,0:T(8,128)}) fusion(f32[512,1024]{1,0:T(8,128)S(1)} %copy-done.1, f32[512]{0:T(512)S(1)} %fusion.87, f32[512]{0:T(512)S(1)} %broadcast_multiply_fusion, f32[1024]{0:T(1024)S(1)} %bitcast.288, bf16[512,4096]{1,0:T(8,128)(2,1)S(1)} %get-tuple-element.196, ...), kind=kOutput, calls=%fused_computation.38 | convolution fusion | flops 4299159040 | bytes 16795648 | tf_op jit(solution)/shard_map/dot_general | solution.py:65
  218.9 2.4 fusion.97
  221.3 2.5 convolution_convert_fusion
  223.8 2.0 copy-done.5
  227.7 3.9 fusion.5
  236.4 2.7 convolution_convert_fusion.7.refs_5_
  240.9 3.2 fusion.16
  245.5 18.8 %attend_back.2 = bf16[512,1536]{1,0:T(8,128)(2,1)} custom-call(s32[512,1]{1,0:T(8,128)} %fusion.59.refs_0_, s32[1,512]{1,0:T(1,128)} %broadcast_select_fusion.2.refs_1_, bf16[512,3072]{1,0:T(8,128)(2,1)} %convolution_convert_fusion.4.refs_2_.refs_3_.refs_4_, bf16[512,3072]{1,0:T(8,128)(2,1)} %convolution_convert_fusion.4.refs_2_.refs_3_.refs_4_, ...), custom_call_target="tpu_custom_call" | custom-call | tf_op jit(solution)/shard_map/attend_back/pallas_call | solution.py:167
  266.1 4.2 collective-permute-done.33
  271.4 3.2 fusion.46
  274.6 3.0 fusion.14
  277.6 2.1 fusion.26
  281.7 2.2 collective-permute-start.36
  286.2 2.5 fusion.24
  288.7 18.9 %attend_back.3 = bf16[512,1536]{1,0:T(8,128)(2,1)} custom-call(s32[512,1]{1,0:T(8,128)} %fusion.59.refs_0_, s32[1,512]{1,0:T(1,128)} %broadcast_select_fusion.2.refs_1_, bf16[512,3072]{1,0:T(8,128)(2,1)} %convolution_convert_fusion.4.refs_2_.refs_3_.refs_4_, bf16[512,3072]{1,0:T(8,128)(2,1)} %convolution_convert_fusion.4.refs_2_.refs_3_.refs_4_, ...), custom_call_target="tpu_custom_call" | custom-call | tf_op jit(solution)/shard_map/attend_back/pallas_call | solution.py:167
  307.6 3.2 fusion.39
  310.8 2.0 fusion.38
  315.8 3.7 convolution_convert_fusion.3
  325.6 6.5 %fusion.104 = f32[512,1024]{1,0:T(8,128)S(1)} fusion(bf16[512,3072]{1,0:T(8,128)(2,1)} %copy-done.7, bf16[1024,3072]{1,0:T(8,128)(2,1)} %get-tuple-element.172), kind=kOutput, calls=%fused_computation.305 | convolution fusion | flops 3221225472 | bytes 11534336 | tf_op jit(solution)/shard_map/dot_general | solution.py:65
  336.3 2.0 collective-permute-start.48
  340.1 3.2 fusion.10
  353.2 3.9 collective-permute-done.48
  357.1 2.5 collective-permute-done.50
  359.6 9.3 %collective-permute-done.45 = bf16[2,4,32,3072]{3,2,1,0:T(8,128)(2,1)} collective-permute-done((bf16[2,4,32,3072]{3,2,1,0:T(8,128)(2,1)}, bf16[2,4,32,3072]{3,2,1,0:T(8,128)(2,1)}, u32[]{:S(2)}, u32[]{:S(2)}) %collective-permute-start.45) | collective-permute-done | bytes 1572896 | tf_op jit(solution)/shard_map/ppermute | solution.py:322
  370.6 2.6 fusion.21
  373.3 2.4 fusion.65
  382.8 2.9 collective-permute-done.55
  390.5 10.1 %select_convert_fusion = bf16[512,1024]{1,0:T(8,128)(2,1)} fusion(f32[512,1024]{1,0:T(8,128)S(1)} %copy-done.2, bf16[512,4096]{1,0:T(8,128)(2,1)} %get-tuple-element.252.in_ref, bf16[4096,1024]{1,0:T(8,128)(2,1)} %assemble.5, pred[512]{0:T(512)(128)(4,1)S(1)} %copy-done.77), kind=kOutput, calls=%fused_computation.40 | convolution fusion | flops 4296540160 | bytes 15729152 | tf_op jit(solution)/shard_map/dot_general | solution.py:702
  400.6 4.0 finish.5
  412.5 2.4 collective-permute-start.67
  418.1 2.4 collective-permute-done.65
  422.0 5.4 %collective-permute-done.66 = bf16[32,3072]{1,0:T(8,128)(2,1)S(1)} collective-permute-done((bf16[32,3072]{1,0:T(8,128)(2,1)S(1)}, bf16[32,3072]{1,0:T(8,128)(2,1)S(1)}, u32[]{:S(2)}, u32[]{:S(2)}) %collective-permute-start.66) | collective-permute-done | bytes 196640 | tf_op jit(solution)/shard_map/ppermute | solution.py:298
  432.2 2.4 collective-permute-start.74
  435.8 3.6 collective-permute-start.63
  439.4 3.9 finish.4
  443.3 2.0 collective-permute-start.62
  446.1 3.6 collective-permute-done.62
  453.9 2.1 finish.7
  456.9 3.2 finish.6
  (424 shorter events, 128.1 us)
Async XLA Ops:
  6.6 13.1 %collective-permute-start = (bf16[32,4608]{1,0:T(8,128)(2,1)S(1)}, bf16[32,4608]{1,0:T(8,128)(2,1)S(1)}, u32[]{:S(2)}, u32[]{:S(2)}) collective-permute-start(bf16[32,4608]{1,0:T(8,128)(2,1)S(1)} %pad_maximum_fusion.3), channel_id=1, source_target_pairs={{0,1},{1,2},{2,3},{3,0},{4,5},{5,6},{6,7},{7,4},{8,9},{9,10},{10,1... | collective-permute-start | bytes 884744 | tf_op jit(solution)/shard_map/ppermute | solution.py:298
  9.7 21.8 %collective-permute-start.1 = (bf16[32,4608]{1,0:T(8,128)(2,1)S(1)}, bf16[32,4608]{1,0:T(8,128)(2,1)S(1)}, u32[]{:S(2)}, u32[]{:S(2)}) collective-permute-start(bf16[32,4608]{1,0:T(8,128)(2,1)S(1)} %pad_maximum_fusion.3), channel_id=1, source_target_pairs={{0,2},{1,3},{2,0},{3,1},{4,6},{5,7},{6,4},{7,5},{8,10},{9,11},{10,... | collective-permute-start | bytes 884744 | tf_op jit(solution)/shard_map/ppermute | solution.py:298
  12.3 19.2 %collective-permute-start.2 = (bf16[32,4608]{1,0:T(8,128)(2,1)S(1)}, bf16[32,4608]{1,0:T(8,128)(2,1)S(1)}, u32[]{:S(2)}, u32[]{:S(2)}) collective-permute-start(bf16[32,4608]{1,0:T(8,128)(2,1)S(1)} %pad_maximum_fusion.3), channel_id=1, source_target_pairs={{0,3},{1,0},{2,1},{3,2},{4,7},{5,4},{6,5},{7,6},{8,11},{9,8},{10,9... | collective-permute-start | bytes 884744 | tf_op jit(solution)/shard_map/ppermute | solution.py:298
  32.6 29.6 %collective-permute-start.3 = (bf16[1,3,32,4096]{3,2,1,0:T(8,128)(2,1)}, bf16[1,3,32,4096]{3,2,1,0:T(8,128)(2,1)}, u32[]{:S(2)}, u32[]{:S(2)}) collective-permute-start(bf16[1,3,32,4096]{3,2,1,0:T(8,128)(2,1)} %maximum_bitcast_fusion.refs_2_), channel_id=1, source_target_pairs={{0,16},{4,12},{8,24},{12,4},{16,0},{20,28},{24,8},{28,20},{1,17},{... | collective-permute-start | bytes 2359304 | tf_op jit(solution)/shard_map/ppermute | solution.py:473
  34.1 25.5 %collective-permute-start.4 = (bf16[1,3,32,4096]{3,2,1,0:T(8,128)(2,1)}, bf16[1,3,32,4096]{3,2,1,0:T(8,128)(2,1)}, u32[]{:S(2)}, u32[]{:S(2)}) collective-permute-start(bf16[1,3,32,4096]{3,2,1,0:T(8,128)(2,1)} %maximum_bitcast_fusion.refs_2_), channel_id=1, source_target_pairs={{0,8},{4,20},{8,0},{12,28},{16,24},{20,4},{24,16},{28,12},{1,9},{5... | collective-permute-start | bytes 2359304 | tf_op jit(solution)/shard_map/ppermute | solution.py:473
  35.6 15.1 %collective-permute-start.5 = (bf16[32,4096]{1,0:T(8,128)(2,1)S(1)}, bf16[32,4096]{1,0:T(8,128)(2,1)S(1)}, u32[]{:S(2)}, u32[]{:S(2)}) collective-permute-start(bf16[32,4096]{1,0:T(8,128)(2,1)S(1)} %constant_dynamic-slice_fusion.5), channel_id=1, source_target_pairs={{0,1},{1,2},{2,3},{3,0},{4,5},{5,6},{6,7},{7,4},{8,9},{9,10},{10,1... | collective-permute-start | bytes 786440 | tf_op jit(solution)/shard_map/ppermute | solution.py:298
  42.4 17.3 %collective-permute-start.6 = (bf16[32,4096]{1,0:T(8,128)(2,1)S(1)}, bf16[32,4096]{1,0:T(8,128)(2,1)S(1)}, u32[]{:S(2)}, u32[]{:S(2)}) collective-permute-start(bf16[32,4096]{1,0:T(8,128)(2,1)S(1)} %constant_dynamic-slice_fusion.5), channel_id=1, source_target_pairs={{0,2},{1,3},{2,0},{3,1},{4,6},{5,7},{6,4},{7,5},{8,10},{9,11},{10,... | collective-permute-start | bytes 786440 | tf_op jit(solution)/shard_map/ppermute | solution.py:298
  44.0 15.7 %collective-permute-start.7 = (bf16[32,4096]{1,0:T(8,128)(2,1)S(1)}, bf16[32,4096]{1,0:T(8,128)(2,1)S(1)}, u32[]{:S(2)}, u32[]{:S(2)}) collective-permute-start(bf16[32,4096]{1,0:T(8,128)(2,1)S(1)} %constant_dynamic-slice_fusion.5), channel_id=1, source_target_pairs={{0,3},{1,0},{2,1},{3,2},{4,7},{5,4},{6,5},{7,6},{8,11},{9,8},{10,9... | collective-permute-start | bytes 786440 | tf_op jit(solution)/shard_map/ppermute | solution.py:298
  50.7 23.1 %collective-permute-start.14 = (bf16[1,3,32,4096]{3,2,1,0:T(8,128)(2,1)}, bf16[1,3,32,4096]{3,2,1,0:T(8,128)(2,1)}, u32[]{:S(2)}, u32[]{:S(2)}) collective-permute-start(bf16[1,3,32,4096]{3,2,1,0:T(8,128)(2,1)} %maximum_bitcast_fusion.refs_2_), channel_id=1, source_target_pairs={{0,4},{4,0},{8,12},{12,8},{16,20},{20,16},{24,28},{28,24},{1,5},{5... | collective-permute-start | bytes 2359304 | tf_op jit(solution)/shard_map/ppermute | solution.py:294
  59.7 12.3 %collective-permute-start.8 = (bf16[1,3,32,4096]{3,2,1,0:T(8,128)(2,1)}, bf16[1,3,32,4096]{3,2,1,0:T(8,128)(2,1)S(1)}, u32[]{:S(2)}, u32[]{:S(2)}) collective-permute-start(bf16[1,3,32,4096]{3,2,1,0:T(8,128)(2,1)} %collective-permute-done.4.refs_3_), channel_id=1, source_target_pairs={{0,16},{4,12},{8,24},{12,4},{16,0},{20,28},{24,8},{28,20},{1,17},{... | collective-permute-start | bytes 2359304 | tf_op jit(solution)/shard_map/ppermute | solution.py:473
  62.1 12.3 %collective-permute-start.15 = (bf16[1,3,32,4096]{3,2,1,0:T(8,128)(2,1)}, bf16[1,3,32,4096]{3,2,1,0:T(8,128)(2,1)}, u32[]{:S(2)}, u32[]{:S(2)}) collective-permute-start(bf16[1,3,32,4096]{3,2,1,0:T(8,128)(2,1)} %collective-permute-done.4.refs_3_), channel_id=1, source_target_pairs={{0,4},{4,0},{8,12},{12,8},{16,20},{20,16},{24,28},{28,24},{1,5},{5... | collective-permute-start | bytes 2359304 | tf_op jit(solution)/shard_map/ppermute | solution.py:294
  73.2 49.4 %collective-permute-start.12 = (bf16[1,3,32,4096]{3,2,1,0:T(8,128)(2,1)S(1)}, bf16[1,3,32,4096]{3,2,1,0:T(8,128)(2,1)}, u32[]{:S(2)}, u32[]{:S(2)}) collective-permute-start(bf16[1,3,32,4096]{3,2,1,0:T(8,128)(2,1)S(1)} %maximum_bitcast_fusion.1.refs_1_), channel_id=1, source_target_pairs={{0,16},{4,12},{8,24},{12,4},{16,0},{20,28},{24,8},{28,20},{1,17},{... | collective-permute-start | bytes 2359304 | tf_op jit(solution)/shard_map/ppermute | solution.py:473
  73.8 19.0 %collective-permute-start.13 = (bf16[1,3,32,4096]{3,2,1,0:T(8,128)(2,1)S(1)}, bf16[1,3,32,4096]{3,2,1,0:T(8,128)(2,1)}, u32[]{:S(2)}, u32[]{:S(2)}) collective-permute-start(bf16[1,3,32,4096]{3,2,1,0:T(8,128)(2,1)S(1)} %maximum_bitcast_fusion.1.refs_1_), channel_id=1, source_target_pairs={{0,8},{4,20},{8,0},{12,28},{16,24},{20,4},{24,16},{28,12},{1,9},{5... | collective-permute-start | bytes 2359304 | tf_op jit(solution)/shard_map/ppermute | solution.py:473
  92.8 29.8 %collective-permute-start.18 = (bf16[1,3,32,4096]{3,2,1,0:T(8,128)(2,1)}, bf16[1,3,32,4096]{3,2,1,0:T(8,128)(2,1)}, u32[]{:S(2)}, u32[]{:S(2)}) collective-permute-start(bf16[1,3,32,4096]{3,2,1,0:T(8,128)(2,1)} %collective-permute-done.13.refs_2_), channel_id=1, source_target_pairs={{0,16},{4,12},{8,24},{12,4},{16,0},{20,28},{24,8},{28,20},{1,17},{... | collective-permute-start | bytes 2359304 | tf_op jit(solution)/shard_map/ppermute | solution.py:473
  94.1 29.1 %collective-permute-start.9 = (bf16[128,1024]{1,0:T(8,128)(2,1)S(1)}, bf16[128,1024]{1,0:T(8,128)(2,1)S(1)}, u32[]{:S(2)}, u32[]{:S(2)}) collective-permute-start(bf16[128,1024]{1,0:T(8,128)(2,1)S(1)} %copy-done.43), channel_id=1, source_target_pairs={{0,1},{1,2},{2,3},{3,0},{4,5},{5,6},{6,7},{7,4},{8,9},{9,10},{10,1... | collective-permute-start | bytes 786440 | tf_op jit(solution)/shard_map/ppermute | solution.py:298
  100.1 23.1 %collective-permute-start.10 = (bf16[128,1024]{1,0:T(8,128)(2,1)S(1)}, bf16[128,1024]{1,0:T(8,128)(2,1)}, u32[]{:S(2)}, u32[]{:S(2)}) collective-permute-start(bf16[128,1024]{1,0:T(8,128)(2,1)S(1)} %copy-done.43), channel_id=1, source_target_pairs={{0,2},{1,3},{2,0},{3,1},{4,6},{5,7},{6,4},{7,5},{8,10},{9,11},{10,... | collective-permute-start | bytes 786440 | tf_op jit(solution)/shard_map/ppermute | solution.py:298
  102.5 20.6 %collective-permute-start.11 = (bf16[128,1024]{1,0:T(8,128)(2,1)S(1)}, bf16[128,1024]{1,0:T(8,128)(2,1)}, u32[]{:S(2)}, u32[]{:S(2)}) collective-permute-start(bf16[128,1024]{1,0:T(8,128)(2,1)S(1)} %copy-done.43), channel_id=1, source_target_pairs={{0,3},{1,0},{2,1},{3,2},{4,7},{5,4},{6,5},{7,6},{8,11},{9,8},{10,9... | collective-permute-start | bytes 786440 | tf_op jit(solution)/shard_map/ppermute | solution.py:298
  122.6 16.4 %collective-permute-start.22 = (bf16[1,3,32,4096]{3,2,1,0:T(8,128)(2,1)S(1)}, bf16[1,3,32,4096]{3,2,1,0:T(8,128)(2,1)S(1)}, u32[]{:S(2)}, u32[]{:S(2)}) collective-permute-start(bf16[1,3,32,4096]{3,2,1,0:T(8,128)(2,1)S(1)} %maximum_bitcast_fusion.1.refs_1_), channel_id=1, source_target_pairs={{0,4},{4,0},{8,12},{12,8},{16,20},{20,16},{24,28},{28,24},{1,5},{5... | collective-permute-start | bytes 2359304 | tf_op jit(solution)/shard_map/ppermute | solution.py:294
  122.7 17.8 %collective-permute-start.23 = (bf16[1,3,32,4096]{3,2,1,0:T(8,128)(2,1)}, bf16[1,3,32,4096]{3,2,1,0:T(8,128)(2,1)}, u32[]{:S(2)}, u32[]{:S(2)}) collective-permute-start(bf16[1,3,32,4096]{3,2,1,0:T(8,128)(2,1)} %collective-permute-done.13.refs_2_), channel_id=1, source_target_pairs={{0,4},{4,0},{8,12},{12,8},{16,20},{20,16},{24,28},{28,24},{1,5},{5... | collective-permute-start | bytes 2359304 | tf_op jit(solution)/shard_map/ppermute | solution.py:294
  125.2 12.3 %collective-permute-start.19 = (bf16[1,3,128,1024]{3,2,1,0:T(8,128)(2,1)}, bf16[1,3,128,1024]{3,2,1,0:T(8,128)(2,1)}, u32[]{:S(2)}, u32[]{:S(2)}) collective-permute-start(bf16[1,3,128,1024]{3,2,1,0:T(8,128)(2,1)} %maximum_bitcast_fusion.2.refs_1_), channel_id=1, source_target_pairs={{0,8},{4,20},{8,0},{12,28},{16,24},{20,4},{24,16},{28,12},{1,9},{5... | collective-permute-start | bytes 2359304 | tf_op jit(solution)/shard_map/ppermute | solution.py:473
  125.7 14.7 %collective-permute-start.24 = (bf16[1,3,32,4096]{3,2,1,0:T(8,128)(2,1)}, bf16[1,3,32,4096]{3,2,1,0:T(8,128)(2,1)}, u32[]{:S(2)}, u32[]{:S(2)}) collective-permute-start(bf16[1,3,32,4096]{3,2,1,0:T(8,128)(2,1)} %collective-permute-done.12.refs_3_), channel_id=1, source_target_pairs={{0,4},{4,0},{8,12},{12,8},{16,20},{20,16},{24,28},{28,24},{1,5},{5... | collective-permute-start | bytes 2359304 | tf_op jit(solution)/shard_map/ppermute | solution.py:294
  126.5 13.9 %collective-permute-start.25 = (bf16[1,3,32,4096]{3,2,1,0:T(8,128)(2,1)}, bf16[1,3,32,4096]{3,2,1,0:T(8,128)(2,1)}, u32[]{:S(2)}, u32[]{:S(2)}) collective-permute-start(bf16[1,3,32,4096]{3,2,1,0:T(8,128)(2,1)} %collective-permute-done.18.refs_4_), channel_id=1, source_target_pairs={{0,4},{4,0},{8,12},{12,8},{16,20},{20,16},{24,28},{28,24},{1,5},{5... | collective-permute-start | bytes 2359304 | tf_op jit(solution)/shard_map/ppermute | solution.py:294
  137.5 20.9 %collective-permute-start.20 = (bf16[1,3,128,1024]{3,2,1,0:T(8,128)(2,1)}, bf16[1,3,128,1024]{3,2,1,0:T(8,128)(2,1)}, u32[]{:S(2)}, u32[]{:S(2)}) collective-permute-start(bf16[1,3,128,1024]{3,2,1,0:T(8,128)(2,1)} %maximum_bitcast_fusion.2.refs_1_), channel_id=1, source_target_pairs={{0,16},{4,12},{8,24},{12,4},{16,0},{20,28},{24,8},{28,20},{1,17},{... | collective-permute-start | bytes 2359304 | tf_op jit(solution)/shard_map/ppermute | solution.py:473
  139.9 18.5 %collective-permute-start.21 = (bf16[1,3,128,1024]{3,2,1,0:T(8,128)(2,1)}, bf16[1,3,128,1024]{3,2,1,0:T(8,128)(2,1)}, u32[]{:S(2)}, u32[]{:S(2)}) collective-permute-start(bf16[1,3,128,1024]{3,2,1,0:T(8,128)(2,1)} %collective-permute-done.19.refs_2_), channel_id=1, source_target_pairs={{0,16},{4,12},{8,24},{12,4},{16,0},{20,28},{24,8},{28,20},{1,17},{... | collective-permute-start | bytes 2359304 | tf_op jit(solution)/shard_map/ppermute | solution.py:473
  169.9 20.3 %collective-permute-start.30 = (bf16[4,4,128,1024]{3,2,1,0:T(8,128)(2,1)}, bf16[4,4,128,1024]{3,2,1,0:T(8,128)(2,1)}, u32[]{:S(2)}, u32[]{:S(2)}) collective-permute-start(bf16[4,4,128,1024]{3,2,1,0:T(8,128)(2,1)} %bitcast.24), channel_id=1, source_target_pairs={{0,4},{4,0},{8,12},{12,8},{16,20},{20,16},{24,28},{28,24},{1,5},{5... | collective-permute-start | bytes 12582920 | tf_op jit(solution)/shard_map/ppermute | solution.py:294
  170.6 10.2 %collective-permute-start.27 = (bf16[1,3,128,1024]{3,2,1,0:T(8,128)(2,1)}, bf16[1,3,128,1024]{3,2,1,0:T(8,128)(2,1)S(1)}, u32[]{:S(2)}, u32[]{:S(2)}) collective-permute-start(bf16[1,3,128,1024]{3,2,1,0:T(8,128)(2,1)} %collective-permute-done.19.refs_2_), channel_id=1, source_target_pairs={{0,4},{4,0},{8,12},{12,8},{16,20},{20,16},{24,28},{28,24},{1,5},{5... | collective-permute-start | bytes 2359304 | tf_op jit(solution)/shard_map/ppermute | solution.py:294
  170.7 11.0 %collective-permute-start.28 = (bf16[1,3,128,1024]{3,2,1,0:T(8,128)(2,1)}, bf16[1,3,128,1024]{3,2,1,0:T(8,128)(2,1)S(1)}, u32[]{:S(2)}, u32[]{:S(2)}) collective-permute-start(bf16[1,3,128,1024]{3,2,1,0:T(8,128)(2,1)} %collective-permute-done.20.refs_3_), channel_id=1, source_target_pairs={{0,4},{4,0},{8,12},{12,8},{16,20},{20,16},{24,28},{28,24},{1,5},{5... | collective-permute-start | bytes 2359304 | tf_op jit(solution)/shard_map/ppermute | solution.py:294
  171.1 11.5 %collective-permute-start.29 = (bf16[1,3,128,1024]{3,2,1,0:T(8,128)(2,1)}, bf16[1,3,128,1024]{3,2,1,0:T(8,128)(2,1)}, u32[]{:S(2)}, u32[]{:S(2)}) collective-permute-start(bf16[1,3,128,1024]{3,2,1,0:T(8,128)(2,1)} %collective-permute-done.21.refs_4_), channel_id=1, source_target_pairs={{0,4},{4,0},{8,12},{12,8},{16,20},{20,16},{24,28},{28,24},{1,5},{5... | collective-permute-start | bytes 2359304 | tf_op jit(solution)/shard_map/ppermute | solution.py:294
  211.0 15.2 %collective-permute-start.31 = (bf16[4,4,32,4096]{3,2,1,0:T(8,128)(2,1)}, bf16[4,4,32,4096]{3,2,1,0:T(8,128)(2,1)}, u32[]{:S(2)}, u32[]{:S(2)}) collective-permute-start(bf16[4,4,32,4096]{3,2,1,0:T(8,128)(2,1)} %bitcast.26), channel_id=1, source_target_pairs={{0,4},{4,0},{8,12},{12,8},{16,20},{20,16},{24,28},{28,24},{1,5},{5... | collective-permute-start | bytes 12582920 | tf_op jit(solution)/shard_map/ppermute | solution.py:294
  211.5 27.6 %collective-permute-start.32 = (bf16[2,4,128,1024]{3,2,1,0:T(8,128)(2,1)S(1)}, bf16[2,4,128,1024]{3,2,1,0:T(8,128)(2,1)}, u32[]{:S(2)}, u32[]{:S(2)}) collective-permute-start(bf16[2,4,128,1024]{3,2,1,0:T(8,128)(2,1)S(1)} %fusion.6), channel_id=1, source_target_pairs={{0,8},{4,20},{8,0},{12,28},{16,24},{20,4},{24,16},{28,12},{1,9},{5... | collective-permute-start | bytes 6291464 | tf_op jit(solution)/shard_map/ppermute | solution.py:322
  231.6 39.8 %collective-permute-start.34 = (bf16[2,4,32,4096]{3,2,1,0:T(8,128)(2,1)}, bf16[2,4,32,4096]{3,2,1,0:T(8,128)(2,1)}, u32[]{:S(2)}, u32[]{:S(2)}) collective-permute-start(bf16[2,4,32,4096]{3,2,1,0:T(8,128)(2,1)} %fusion.5), channel_id=1, source_target_pairs={{0,8},{4,20},{8,0},{12,28},{16,24},{20,4},{24,16},{28,12},{1,9},{5... | collective-permute-start | bytes 6291464 | tf_op jit(solution)/shard_map/ppermute | solution.py:322
  244.0 26.3 %collective-permute-start.33 = (bf16[1,4,128,1024]{3,2,1,0:T(8,128)(2,1)}, bf16[1,4,128,1024]{3,2,1,0:T(8,128)(2,1)}, u32[]{:S(2)}, u32[]{:S(2)}) collective-permute-start(bf16[1,4,128,1024]{3,2,1,0:T(8,128)(2,1)} %fusion.16), channel_id=1, source_target_pairs={{0,16},{4,12},{8,24},{12,4},{16,0},{20,28},{24,8},{28,20},{1,17},{... | collective-permute-start | bytes 3145736 | tf_op jit(solution)/shard_map/ppermute | solution.py:322
  245.5 24.9 %collective-permute-start.35 = (bf16[4,4,32,1024]{3,2,1,0:T(8,128)(2,1)}, bf16[4,4,32,1024]{3,2,1,0:T(8,128)(2,1)}, u32[]{:S(2)}, u32[]{:S(2)}) collective-permute-start(bf16[4,4,32,1024]{3,2,1,0:T(8,128)(2,1)} %bitcast.29), channel_id=1, source_target_pairs={{0,4},{4,0},{8,12},{12,8},{16,20},{20,16},{24,28},{28,24},{1,5},{5... | collective-permute-start | bytes 3145736 | tf_op jit(solution)/shard_map/ppermute | solution.py:294
  279.7 27.9 %collective-permute-start.39 = (bf16[1,4,32,4096]{3,2,1,0:T(8,128)(2,1)}, bf16[1,4,32,4096]{3,2,1,0:T(8,128)(2,1)S(1)}, u32[]{:S(2)}, u32[]{:S(2)}) collective-permute-start(bf16[1,4,32,4096]{3,2,1,0:T(8,128)(2,1)} %fusion.14), channel_id=1, source_target_pairs={{0,16},{4,12},{8,24},{12,4},{16,0},{20,28},{24,8},{28,20},{1,17},{... | collective-permute-start | bytes 3145736 | tf_op jit(solution)/shard_map/ppermute | solution.py:322
  281.1 26.4 %collective-permute-start.40 = (bf16[2,4,32,1024]{3,2,1,0:T(8,128)(2,1)}, bf16[2,4,32,1024]{3,2,1,0:T(8,128)(2,1)}, u32[]{:S(2)}, u32[]{:S(2)}) collective-permute-start(bf16[2,4,32,1024]{3,2,1,0:T(8,128)(2,1)} %fusion.26), channel_id=1, source_target_pairs={{0,8},{4,20},{8,0},{12,28},{16,24},{20,4},{24,16},{28,12},{1,9},{5... | collective-permute-start | bytes 1572872 | tf_op jit(solution)/shard_map/ppermute | solution.py:322
  281.7 25.9 %collective-permute-start.36 = (bf16[128,1024]{1,0:T(8,128)(2,1)}, bf16[128,1024]{1,0:T(8,128)(2,1)}, u32[]{:S(2)}, u32[]{:S(2)}) collective-permute-start(bf16[128,1024]{1,0:T(8,128)(2,1)} %get-tuple-element.215), channel_id=1, source_target_pairs={{0,1},{1,2},{2,3},{3,0},{4,5},{5,6},{6,7},{7,4},{8,9},{9,10},{10,1... | collective-permute-start | bytes 786440 | tf_op jit(solution)/shard_map/ppermute | solution.py:298
  283.8 23.7 %collective-permute-start.37 = (bf16[128,1024]{1,0:T(8,128)(2,1)}, bf16[128,1024]{1,0:T(8,128)(2,1)}, u32[]{:S(2)}, u32[]{:S(2)}) collective-permute-start(bf16[128,1024]{1,0:T(8,128)(2,1)} %get-tuple-element.216), channel_id=1, source_target_pairs={{0,2},{1,3},{2,0},{3,1},{4,6},{5,7},{6,4},{7,5},{8,10},{9,11},{10,... | collective-permute-start | bytes 786440 | tf_op jit(solution)/shard_map/ppermute | solution.py:298
  284.3 23.3 %collective-permute-start.38 = (bf16[128,1024]{1,0:T(8,128)(2,1)}, bf16[128,1024]{1,0:T(8,128)(2,1)}, u32[]{:S(2)}, u32[]{:S(2)}) collective-permute-start(bf16[128,1024]{1,0:T(8,128)(2,1)} %get-tuple-element.217), channel_id=1, source_target_pairs={{0,3},{1,0},{2,1},{3,2},{4,7},{5,4},{6,5},{7,6},{8,11},{9,8},{10,9... | collective-permute-start | bytes 786440 | tf_op jit(solution)/shard_map/ppermute | solution.py:298
  319.5 20.6 %collective-permute-start.41 = (bf16[4,4,32,3072]{3,2,1,0:T(8,128)(2,1)}, bf16[4,4,32,3072]{3,2,1,0:T(8,128)(2,1)}, u32[]{:S(2)}, u32[]{:S(2)}) collective-permute-start(bf16[4,4,32,3072]{3,2,1,0:T(8,128)(2,1)} %bitcast.55), channel_id=1, source_target_pairs={{0,4},{4,0},{8,12},{12,8},{16,20},{20,16},{24,28},{28,24},{1,5},{5... | collective-permute-start | bytes 9437192 | tf_op jit(solution)/shard_map/ppermute | solution.py:294
  322.1 14.2 %collective-permute-start.42 = (bf16[1,128,1024]{2,1,0:T(8,128)(2,1)S(1)}, bf16[1,128,1024]{2,1,0:T(8,128)(2,1)S(1)}, u32[]{:S(2)}, u32[]{:S(2)}) collective-permute-start(bf16[1,128,1024]{2,1,0:T(8,128)(2,1)S(1)} %fusion.64), channel_id=1, source_target_pairs={{0,8},{4,20},{8,0},{12,28},{16,24},{20,4},{24,16},{28,12},{1,9},{5... | collective-permute-start | bytes 786440 | tf_op jit(solution)/shard_map/ppermute | solution.py:305
  323.8 14.5 %collective-permute-start.43 = (bf16[1,128,1024]{2,1,0:T(8,128)(2,1)S(1)}, bf16[1,128,1024]{2,1,0:T(8,128)(2,1)S(1)}, u32[]{:S(2)}, u32[]{:S(2)}) collective-permute-start(bf16[1,128,1024]{2,1,0:T(8,128)(2,1)S(1)} %fusion.64), channel_id=1, source_target_pairs={{0,16},{4,12},{8,24},{12,4},{16,0},{20,28},{24,8},{28,20},{1,17},{... | collective-permute-start | bytes 786440 | tf_op jit(solution)/shard_map/ppermute | solution.py:305
  325.4 14.8 %collective-permute-start.44 = (bf16[1,128,1024]{2,1,0:T(8,128)(2,1)S(1)}, bf16[1,128,1024]{2,1,0:T(8,128)(2,1)S(1)}, u32[]{:S(2)}, u32[]{:S(2)}) collective-permute-start(bf16[1,128,1024]{2,1,0:T(8,128)(2,1)S(1)} %fusion.64), channel_id=1, source_target_pairs={{0,24},{4,28},{8,16},{12,20},{16,8},{20,12},{24,0},{28,4},{1,25},{... | collective-permute-start | bytes 786440 | tf_op jit(solution)/shard_map/ppermute | solution.py:305
  335.7 14.6 %collective-permute-start.47 = (bf16[32,4096]{1,0:T(8,128)(2,1)}, bf16[32,4096]{1,0:T(8,128)(2,1)}, u32[]{:S(2)}, u32[]{:S(2)}) collective-permute-start(bf16[32,4096]{1,0:T(8,128)(2,1)} %get-tuple-element.241), channel_id=1, source_target_pairs={{0,1},{1,2},{2,3},{3,0},{4,5},{5,6},{6,7},{7,4},{8,9},{9,10},{10,1... | collective-permute-start | bytes 786440 | tf_op jit(solution)/shard_map/ppermute | solution.py:298
  336.3 20.8 %collective-permute-start.48 = (bf16[32,4096]{1,0:T(8,128)(2,1)}, bf16[32,4096]{1,0:T(8,128)(2,1)}, u32[]{:S(2)}, u32[]{:S(2)}) collective-permute-start(bf16[32,4096]{1,0:T(8,128)(2,1)} %get-tuple-element.242), channel_id=1, source_target_pairs={{0,2},{1,3},{2,0},{3,1},{4,6},{5,7},{6,4},{7,5},{8,10},{9,11},{10,... | collective-permute-start | bytes 786440 | tf_op jit(solution)/shard_map/ppermute | solution.py:298
  338.3 18.8 %collective-permute-start.49 = (bf16[32,4096]{1,0:T(8,128)(2,1)}, bf16[32,4096]{1,0:T(8,128)(2,1)}, u32[]{:S(2)}, u32[]{:S(2)}) collective-permute-start(bf16[32,4096]{1,0:T(8,128)(2,1)} %get-tuple-element.243), channel_id=1, source_target_pairs={{0,3},{1,0},{2,1},{3,2},{4,7},{5,4},{6,5},{7,6},{8,11},{9,8},{10,9... | collective-permute-start | bytes 786440 | tf_op jit(solution)/shard_map/ppermute | solution.py:298
  345.3 23.6 %collective-permute-start.45 = (bf16[2,4,32,3072]{3,2,1,0:T(8,128)(2,1)}, bf16[2,4,32,3072]{3,2,1,0:T(8,128)(2,1)}, u32[]{:S(2)}, u32[]{:S(2)}) collective-permute-start(bf16[2,4,32,3072]{3,2,1,0:T(8,128)(2,1)} %fusion.10), channel_id=1, source_target_pairs={{0,8},{4,20},{8,0},{12,28},{16,24},{20,4},{24,16},{28,12},{1,9},{5... | collective-permute-start | bytes 4718600 | tf_op jit(solution)/shard_map/ppermute | solution.py:322
  346.8 12.7 %collective-permute-start.46 = (bf16[4,128,1024]{2,1,0:T(8,128)(2,1)}, bf16[4,128,1024]{2,1,0:T(8,128)(2,1)}, u32[]{:S(2)}, u32[]{:S(2)}) collective-permute-start(bf16[4,128,1024]{2,1,0:T(8,128)(2,1)} %pad_maximum_fusion.refs_0_), channel_id=1, source_target_pairs={{0,4},{4,0},{8,12},{12,8},{16,20},{20,16},{24,28},{28,24},{1,5},{5... | collective-permute-start | bytes 3145736 | tf_op jit(solution)/shard_map/ppermute | solution.py:294
  377.6 11.0 %collective-permute-start.59 = (f32[4,64,256]{2,0,1:T(4,128)S(1)}, f32[4,64,256]{2,0,1:T(4,128)S(1)}, u32[]{:S(2)}, u32[]{:S(2)}) collective-permute-start(f32[4,64,256]{2,0,1:T(4,128)S(1)} %fusion.93), channel_id=1, source_target_pairs={{0,8},{4,12},{8,0},{12,4},{16,24},{20,28},{24,16},{28,20},{1,9},{5... | collective-permute-start | bytes 786440 | tf_op jit(solution)/shard_map/ppermute | solution.py:342
  380.9 25.2 %collective-permute-start.52 = (bf16[1,32,4096]{2,1,0:T(8,128)(2,1)}, bf16[1,32,4096]{2,1,0:T(8,128)(2,1)}, u32[]{:S(2)}, u32[]{:S(2)}) collective-permute-start(bf16[1,32,4096]{2,1,0:T(8,128)(2,1)} %fusion.65), channel_id=1, source_target_pairs={{0,8},{4,20},{8,0},{12,28},{16,24},{20,4},{24,16},{28,12},{1,9},{5... | collective-permute-start | bytes 786440 | tf_op jit(solution)/shard_map/ppermute | solution.py:305
  381.3 24.9 %collective-permute-start.53 = (bf16[1,32,4096]{2,1,0:T(8,128)(2,1)}, bf16[1,32,4096]{2,1,0:T(8,128)(2,1)}, u32[]{:S(2)}, u32[]{:S(2)}) collective-permute-start(bf16[1,32,4096]{2,1,0:T(8,128)(2,1)} %fusion.65), channel_id=1, source_target_pairs={{0,16},{4,12},{8,24},{12,4},{16,0},{20,28},{24,8},{28,20},{1,17},{... | collective-permute-start | bytes 786440 | tf_op jit(solution)/shard_map/ppermute | solution.py:305
  385.8 20.4 %collective-permute-start.54 = (bf16[1,32,4096]{2,1,0:T(8,128)(2,1)}, bf16[1,32,4096]{2,1,0:T(8,128)(2,1)}, u32[]{:S(2)}, u32[]{:S(2)}) collective-permute-start(bf16[1,32,4096]{2,1,0:T(8,128)(2,1)} %fusion.65), channel_id=1, source_target_pairs={{0,24},{4,28},{8,16},{12,20},{16,8},{20,12},{24,0},{28,4},{1,25},{... | collective-permute-start | bytes 786440 | tf_op jit(solution)/shard_map/ppermute | solution.py:305
  387.1 19.1 %collective-permute-start.51 = (bf16[1,4,32,3072]{3,2,1,0:T(8,128)(2,1)}, bf16[1,4,32,3072]{3,2,1,0:T(8,128)(2,1)}, u32[]{:S(2)}, u32[]{:S(2)}) collective-permute-start(bf16[1,4,32,3072]{3,2,1,0:T(8,128)(2,1)} %fusion.21), channel_id=1, source_target_pairs={{0,16},{4,12},{8,24},{12,4},{16,0},{20,28},{24,8},{28,20},{1,17},{... | collective-permute-start | bytes 2359304 | tf_op jit(solution)/shard_map/ppermute | solution.py:322
  388.6 17.1 %collective-permute-start.57 = (bf16[32,1024]{1,0:T(8,128)(2,1)}, bf16[32,1024]{1,0:T(8,128)(2,1)}, u32[]{:S(2)}, u32[]{:S(2)}) collective-permute-start(bf16[32,1024]{1,0:T(8,128)(2,1)} %get-tuple-element.257), channel_id=1, source_target_pairs={{0,3},{1,0},{2,1},{3,2},{4,7},{5,4},{6,5},{7,6},{8,11},{9,8},{10,9... | collective-permute-start | bytes 196616 | tf_op jit(solution)/shard_map/ppermute | solution.py:298
  411.0 16.4 %collective-permute-start.66 = (bf16[32,3072]{1,0:T(8,128)(2,1)S(1)}, bf16[32,3072]{1,0:T(8,128)(2,1)S(1)}, u32[]{:S(2)}, u32[]{:S(2)}) collective-permute-start(bf16[32,3072]{1,0:T(8,128)(2,1)S(1)} %get-tuple-element.271), channel_id=1, source_target_pairs={{0,2},{1,3},{2,0},{3,1},{4,6},{5,7},{6,4},{7,5},{8,10},{9,11},{10,... | collective-permute-start | bytes 589832 | tf_op jit(solution)/shard_map/ppermute | solution.py:298
  412.5 14.9 %collective-permute-start.67 = (bf16[32,3072]{1,0:T(8,128)(2,1)S(1)}, bf16[32,3072]{1,0:T(8,128)(2,1)S(1)}, u32[]{:S(2)}, u32[]{:S(2)}) collective-permute-start(bf16[32,3072]{1,0:T(8,128)(2,1)S(1)} %get-tuple-element.272), channel_id=1, source_target_pairs={{0,3},{1,0},{2,1},{3,2},{4,7},{5,4},{6,5},{7,6},{8,11},{9,8},{10,9... | collective-permute-start | bytes 589832 | tf_op jit(solution)/shard_map/ppermute | solution.py:298
  416.4 18.3 %collective-permute-start.64 = (bf16[4,32,4096]{2,1,0:T(8,128)(2,1)S(1)}, bf16[4,32,4096]{2,1,0:T(8,128)(2,1)S(1)}, u32[]{:S(2)}, u32[]{:S(2)}) collective-permute-start(bf16[4,32,4096]{2,1,0:T(8,128)(2,1)S(1)} %pad_maximum_fusion.1.refs_0_), channel_id=1, source_target_pairs={{0,4},{4,0},{8,12},{12,8},{16,20},{20,16},{24,28},{28,24},{1,5},{5... | collective-permute-start | bytes 3145736 | tf_op jit(solution)/shard_map/ppermute | solution.py:294
  416.4 15.2 %collective-permute-start.72 = (bf16[1,32,1024]{2,1,0:T(8,128)(2,1)S(1)}, bf16[1,32,1024]{2,1,0:T(8,128)(2,1)S(1)}, u32[]{:S(2)}, u32[]{:S(2)}) collective-permute-start(bf16[1,32,1024]{2,1,0:T(8,128)(2,1)S(1)} %fusion.77), channel_id=1, source_target_pairs={{0,8},{4,20},{8,0},{12,28},{16,24},{20,4},{24,16},{28,12},{1,9},{5... | collective-permute-start | bytes 196616 | tf_op jit(solution)/shard_map/ppermute | solution.py:305
  420.4 11.8 %collective-permute-start.73 = (bf16[1,32,1024]{2,1,0:T(8,128)(2,1)S(1)}, bf16[1,32,1024]{2,1,0:T(8,128)(2,1)S(1)}, u32[]{:S(2)}, u32[]{:S(2)}) collective-permute-start(bf16[1,32,1024]{2,1,0:T(8,128)(2,1)S(1)} %fusion.77), channel_id=1, source_target_pairs={{0,16},{4,12},{8,24},{12,4},{16,0},{20,28},{24,8},{28,20},{1,17},{... | collective-permute-start | bytes 196616 | tf_op jit(solution)/shard_map/ppermute | solution.py:305
  428.7 14.6 %collective-permute-start.68 = (bf16[1,32,3072]{2,1,0:T(8,128)(2,1)S(1)}, bf16[1,32,3072]{2,1,0:T(8,128)(2,1)S(1)}, u32[]{:S(2)}, u32[]{:S(2)}) collective-permute-start(bf16[1,32,3072]{2,1,0:T(8,128)(2,1)S(1)} %fusion.68), channel_id=1, source_target_pairs={{0,8},{4,20},{8,0},{12,28},{16,24},{20,4},{24,16},{28,12},{1,9},{5... | collective-permute-start | bytes 589832 | tf_op jit(solution)/shard_map/ppermute | solution.py:305
  430.2 15.1 %collective-permute-start.69 = (bf16[1,32,3072]{2,1,0:T(8,128)(2,1)S(1)}, bf16[1,32,3072]{2,1,0:T(8,128)(2,1)S(1)}, u32[]{:S(2)}, u32[]{:S(2)}) collective-permute-start(bf16[1,32,3072]{2,1,0:T(8,128)(2,1)S(1)} %fusion.68), channel_id=1, source_target_pairs={{0,16},{4,12},{8,24},{12,4},{16,0},{20,28},{24,8},{28,20},{1,17},{... | collective-permute-start | bytes 589832 | tf_op jit(solution)/shard_map/ppermute | solution.py:305
  431.7 13.7 %collective-permute-start.70 = (bf16[1,32,3072]{2,1,0:T(8,128)(2,1)S(1)}, bf16[1,32,3072]{2,1,0:T(8,128)(2,1)S(1)}, u32[]{:S(2)}, u32[]{:S(2)}) collective-permute-start(bf16[1,32,3072]{2,1,0:T(8,128)(2,1)S(1)} %fusion.68), channel_id=1, source_target_pairs={{0,24},{4,28},{8,16},{12,20},{16,8},{20,12},{24,0},{28,4},{1,25},{... | collective-permute-start | bytes 589832 | tf_op jit(solution)/shard_map/ppermute | solution.py:305
  432.2 13.3 %collective-permute-start.74 = (bf16[1,32,1024]{2,1,0:T(8,128)(2,1)S(1)}, bf16[1,32,1024]{2,1,0:T(8,128)(2,1)S(1)}, u32[]{:S(2)}, u32[]{:S(2)}) collective-permute-start(bf16[1,32,1024]{2,1,0:T(8,128)(2,1)S(1)} %fusion.77), channel_id=1, source_target_pairs={{0,24},{4,28},{8,16},{12,20},{16,8},{20,12},{24,0},{28,4},{1,25},{... | collective-permute-start | bytes 196616 | tf_op jit(solution)/shard_map/ppermute | solution.py:305
  435.8 10.4 %collective-permute-start.63 = (f32[64,256]{1,0:T(8,128)}, f32[64,256]{1,0:T(8,128)S(1)}, u32[]{:S(2)}, u32[]{:S(2)}) collective-permute-start(f32[64,256]{1,0:T(8,128)} %bitcast.264), channel_id=1, source_target_pairs={{0,3},{1,0},{2,1},{3,2},{4,7},{5,4},{6,5},{7,6},{8,11},{9,8},{10,9... | collective-permute-start | bytes 196616 | tf_op jit(solution)/shard_map/ppermute | solution.py:298
  445.5 10.6 %collective-permute-start.71 = (bf16[4,32,3072]{2,1,0:T(8,128)(2,1)S(1)}, bf16[4,32,3072]{2,1,0:T(8,128)(2,1)S(1)}, u32[]{:S(2)}, u32[]{:S(2)}) collective-permute-start(bf16[4,32,3072]{2,1,0:T(8,128)(2,1)S(1)} %pad_maximum_fusion.2.refs_0_), channel_id=1, source_target_pairs={{0,4},{4,0},{8,12},{12,8},{16,20},{20,16},{24,28},{28,24},{1,5},{5... | collective-permute-start | bytes 2359304 | tf_op jit(solution)/shard_map/ppermute | solution.py:294
  (102 other events, 1390.6 us)

commit v12 on v11

--- a/solution.py
+++ b/solution.py
@@ -714,6 +714,7 @@
         ],
         axis=1,
     )
+    rows_small, block_out = lax.optimization_barrier((rows_small, block_out))
     run_small = plan.total_small(rows_small)
     (sum_fc2,) = tick(run_fc2.result(), [run_qkv])
     (sum_fc1,) = tick(run_fc1.result(), [run_qkv])

time: 467 us -> 471 us (level)
  other arithmetic: 59.8 us -> 64.9 us
    ppermute x24, waiting for transfers between devices: 46.4 us -> 38.9 us  [ahead(): lax.ppermute(block, 'fsdp', [(i, (i + step) % n_line) for i in range(n_li...]
    ppermute x12, waiting for transfers between devices: 0.03 us -> 6.71 us  [plane_hops(): return [lax.ppermute(block, 'dp', pairs) for pairs in hops]]
    unnamed x184 -> x170, local copies, waits for them, and re-layouts: 18.4 us -> 16.8 us
  transfers between devices with their start and end apart: 76 -> 76, of which waited for: 21 -> 23; matrix products, arithmetic and copies ran while one was open for 25% -> 26% of each run, Pallas kernels for 19% -> 19%
where the time goes in v12:
time: 471 us; the launch traced here: 465 us
  matrix products  95.1 us (20%)
  Pallas kernels  94.8 us (20%)
  starting transfers between devices  84.4 us (18%)
  waiting for transfers between devices  84.3 us (18%)
  other arithmetic  64.9 us (14%)
  local copies, waits for them, and re-layouts  39 us (8%)
    ppermute x24, starting transfers between devices, ahead(): lax.ppermute(block, 'fsdp', [(i, (i + step) % n_line) for i in range(n_li...  48.7 us
    ppermute x24, waiting for transfers between devices, ahead(): lax.ppermute(block, 'fsdp', [(i, (i + step) % n_line) for i in range(n_li...  38.9 us
    pallas_call x2, Pallas kernels, attend_back(): pl.pallas_call(body, grid=(count,), in_specs=pair_specs(rows, pairs, star...  37.7 us
    dot_general x4, matrix products, times_t(): lax.dot_general(left, right, (((1,), (1,)), ((), ())), preferred_element_...  27.7 us
    dot_general x8, matrix products, t_times(): lax.dot_general(left, right, (((0,), (0,)), ((), ())), preferred_element_...  25.7 us
    convert_element_type x8, other arithmetic, reduce_steps(): add_up([term[half:] for term in terms]).astype(jnp.bfloat16)  23.5 us
    pallas_call x3, Pallas kernels, assemble(): pl.pallas_call(body, in_specs=[pl.BlockSpec(memory_space=pltpu.SMEM)] + [...  22.9 us
    ppermute x9, waiting for transfers between devices, hop(): return lax.ppermute(block, 'dp', hop_pairs(self.n_dp, stage))  17.5 us
  transfers between devices with their start and end apart: 76, of which 23 were waited for; matrix products, arithmetic and copies ran while one was open for 26% of the time, Pallas kernels for 19%

profile of v12, /device:TPU:0, one launch (start us, length us, event | category | flops | bytes accessed | tf_op | source)
XLA Modules:
  0.0 464.6 jit_solution(3363975345774854450)
XLA Ops:
  6.6 3.1 collective-permute-start
  9.7 2.6 collective-permute-start.1
  19.7 11.8 %collective-permute-done.1 = bf16[32,4608]{1,0:T(8,128)(2,1)S(1)} collective-permute-done((bf16[32,4608]{1,0:T(8,128)(2,1)S(1)}, bf16[32,4608]{1,0:T(8,128)(2,1)S(1)}, u32[]{:S(2)}, u32[]{:S(2)}) %collective-permute-start.1) | collective-permute-done | bytes 294944 | tf_op jit(solution)/shard_map/ppermute | solution.py:298
  35.6 6.8 %collective-permute-start.5 = (bf16[32,4096]{1,0:T(8,128)(2,1)S(1)}, bf16[32,4096]{1,0:T(8,128)(2,1)S(1)}, u32[]{:S(2)}, u32[]{:S(2)}) collective-permute-start(bf16[32,4096]{1,0:T(8,128)(2,1)S(1)} %constant_dynamic-slice_fusion.5), channel_id=1, source_target_pairs={{0,1},{1,2},{2,3},{3,0},{4,5},{5,6},{6,7},{7,4},{8,9},{9,10},{10,1... | collective-permute-start | bytes 786440 | tf_op jit(solution)/shard_map/ppermute | solution.py:298
  45.6 5.1 %collective-permute-done.5 = bf16[32,4096]{1,0:T(8,128)(2,1)S(1)} collective-permute-done((bf16[32,4096]{1,0:T(8,128)(2,1)S(1)}, bf16[32,4096]{1,0:T(8,128)(2,1)S(1)}, u32[]{:S(2)}, u32[]{:S(2)}) %collective-permute-start.5) | collective-permute-done | bytes 262176 | tf_op jit(solution)/shard_map/ppermute | solution.py:298
  50.7 9.0 %collective-permute-done.6 = bf16[32,4096]{1,0:T(8,128)(2,1)S(1)} collective-permute-done((bf16[32,4096]{1,0:T(8,128)(2,1)S(1)}, bf16[32,4096]{1,0:T(8,128)(2,1)S(1)}, u32[]{:S(2)}, u32[]{:S(2)}) %collective-permute-start.6) | collective-permute-done | bytes 262176 | tf_op jit(solution)/shard_map/ppermute | solution.py:298
  62.1 9.8 %collective-permute-done.8.refs_5_ = bf16[1,3,32,4096]{3,2,1,0:T(8,128)(2,1)S(1)} collective-permute-done((bf16[1,3,32,4096]{3,2,1,0:T(8,128)(2,1)}, bf16[1,3,32,4096]{3,2,1,0:T(8,128)(2,1)S(1)}, u32[]{:S(2)}, u32[]{:S(2)}) %collective-permute-start.8) | collective-permute-done | bytes 786464 | tf_op jit(solution)/shard_map/ppermute | solution.py:473
  75.6 7.7 %assemble.3 = (bf16[1024,3072]{1,0:T(8,128)(2,1)}, bf16[1024,1024]{1,0:T(8,128)(2,1)}) custom-call(s32[33]{0:T(128)} %pad_add_fusion.1.table_ref, bf16[256,3072]{1,0:T(8,128)(2,1)} %refs_0_.3, bf16[256,1024]{1,0:T(8,128)(2,1)} %refs_1_.1, bf16[1,3,32,4096]{3,2,1,0:T(8,128)(2,1)} %maximum_bitcast_fusion.refs_2_, ...), custom_call_target="tpu_custom_call" | custom-call | tf_op jit(solution)/shard_map/assemble/pallas_call | solution.py:225
  83.4 7.8 %convolution_convert_fusion.4.refs_2_.refs_3_.refs_4_ = bf16[512,3072]{1,0:T(8,128)(2,1)} fusion(bf16[1024,3072]{1,0:T(8,128)(2,1)} %get-tuple-element.173, f32[512,1024]{1,0:T(8,128)S(1)} %get-tuple-element.333, f32[1024]{0:T(1024)S(1)} %bitcast.298, f32[1024]{0:T(1024)S(1)} %bitcast.290, f32[512]{0:T(512)S(1)} %fusion.86, f32[512]{0:T(512)S(1)} %broadcast_multiply_fusion.1), kind=kOutput, calls=%fused_computation.15 | convolution fusion | flops 3225419776 | bytes 11546624 | tf_op jit(solution)/shard_map/dot_general | solution.py:654
  94.7 6.0 %collective-permute-start.14 = (bf16[128,1024]{1,0:T(8,128)(2,1)S(1)}, bf16[128,1024]{1,0:T(8,128)(2,1)S(1)}, u32[]{:S(2)}, u32[]{:S(2)}) collective-permute-start(bf16[128,1024]{1,0:T(8,128)(2,1)S(1)} %copy-done.37), channel_id=1, source_target_pairs={{0,1},{1,2},{2,3},{3,0},{4,5},{5,6},{6,7},{7,4},{8,9},{9,10},{10,1... | collective-permute-start | bytes 786440 | tf_op jit(solution)/shard_map/ppermute | solution.py:298
  100.7 2.4 collective-permute-start.15
  107.5 15.8 %attend.1 = bf16[512,1024]{1,0:T(8,128)(2,1)} custom-call(s32[512,1]{1,0:T(8,128)} %fusion.59.refs_0_, s32[1,512]{1,0:T(1,128)} %broadcast_select_fusion.2.refs_1_, bf16[512,3072]{1,0:T(8,128)(2,1)} %convolution_convert_fusion.4.refs_2_.refs_3_.refs_4_, bf16[512,3072]{1,0:T(8,128)(2,1)} %convolution_convert_fusion.4.refs_2_.refs_3_.refs_4_, ...), custom_call_target="tpu_custom_call" | custom-call | tf_op jit(solution)/shard_map/attend/pallas_call | solution.py:148
  123.9 2.0 maximum_bitcast_fusion.2.refs_1_
  127.0 3.3 fusion.102
  132.3 5.9 %collective-permute-done.19.refs_2_ = bf16[1,3,128,1024]{3,2,1,0:T(8,128)(2,1)} collective-permute-done((bf16[1,3,128,1024]{3,2,1,0:T(8,128)(2,1)}, bf16[1,3,128,1024]{3,2,1,0:T(8,128)(2,1)}, u32[]{:S(2)}, u32[]{:S(2)}) %collective-permute-start.19) | collective-permute-done | bytes 786464 | tf_op jit(solution)/shard_map/ppermute | solution.py:473
  141.2 7.6 %assemble.4 = bf16[1024,4096]{1,0:T(8,128)(2,1)} custom-call(s32[33]{0:T(128)} %pad_add_fusion.1.table_ref, bf16[256,4096]{1,0:T(8,128)(2,1)} %refs_0_.4, bf16[1,3,32,4096]{3,2,1,0:T(8,128)(2,1)} %copy-done.18, bf16[1,3,32,4096]{3,2,1,0:T(8,128)(2,1)} %collective-permute-done.9.refs_2_, bf16[1,3,32,4096]{3,2,1,0:T(8,128)(2,1)} %collective-permute-done.17.refs_3_, ...), custom_call_target="tpu_custom_call" | custom-call | tf_op jit(solution)/shard_map/assemble/pallas_call | solution.py:225
  148.8 10.4 %multiply_convert_fusion.1 = (bf16[512,4096]{1,0:T(8,128)(2,1)}, f32[512,4096]{1,0:T(8,128)}) fusion(f32[4096]{0:T(1024)S(1)} %bitcast.295, bf16[512,1024]{1,0:T(8,128)(2,1)S(1)} %copy-done.26, bf16[1024,4096]{1,0:T(8,128)(2,1)} %assemble.4), kind=kOutput, calls=%fused_computation.9 | convolution fusion | flops 4307550208 | bytes 22036480 | tf_op jit(solution)/shard_map/dot_general | solution.py:661
  159.3 5.5 %column_order.1 = bf16[512,4096]{1,0:T(8,128)(2,1)} custom-call(s32[32]{0:T(128)} %add.550.table_ref, bf16[512,4096]{1,0:T(8,128)(2,1)} %get-tuple-element.255.in_ref), custom_call_target="tpu_custom_call" | custom-call | tf_op jit(solution)/shard_map/column_order/pallas_call | solution.py:245
  164.7 6.0 %convolution_convert_fusion.6 = bf16[2048,1024]{1,0:T(8,128)(2,1)} fusion(bf16[512,4096]{1,0:T(8,128)(2,1)} %column_order.1, bf16[512,1024]{1,0:T(8,128)(2,1)S(1)} %copy-done.17, pred[512]{0:T(512)(128)(4,1)S(1)} %copy-done.68), kind=kOutput, calls=%fused_computation.25 | convolution fusion | flops 2150105088 | bytes 7340544 | tf_op jit(solution)/shard_map/dot_general | solution.py:69
  172.0 3.7 fusion.22
  175.6 2.5 convolution_convert_fusion.5
  183.4 7.6 %assemble.5 = bf16[4096,1024]{1,0:T(8,128)(2,1)} custom-call(s32[33]{0:T(128)} %pad_add_fusion.1.table_ref, bf16[1024,1024]{1,0:T(8,128)(2,1)} %refs_0_.5, bf16[1,3,128,1024]{3,2,1,0:T(8,128)(2,1)} %maximum_bitcast_fusion.2.refs_1_, bf16[1,3,128,1024]{3,2,1,0:T(8,128)(2,1)} %collective-permute-done.19.refs_2_, ...), custom_call_target="tpu_custom_call" | custom-call | tf_op jit(solution)/shard_map/assemble/pallas_call | solution.py:225
  191.0 3.4 fusion.6
  194.4 11.7 %convert_reduce_fusion = (f32[4096]{0:T(1024)}, bf16[512,4096]{1,0:T(8,128)(2,1)S(1)}) fusion(f32[512,4096]{1,0:T(8,128)} %get-tuple-element.337, f32[4096]{0:T(1024)S(1)} %bitcast.296, bf16[4096,1024]{1,0:T(8,128)(2,1)} %assemble.5, bf16[512,1024]{1,0:T(8,128)(2,1)S(1)} %copy-done.17, pred[512]{0:T(512)(128)(4,1)S(1)} %copy-done.68), kind=kOutput, calls=%fused_computation.7 | convolution fusion | flops 4326944768 | bytes 22053376 | tf_op jit(solution)/shard_map/dot_general | solution.py:65
  206.1 5.7 %convolution_convert_fusion.1 = bf16[512,4096]{1,0:T(8,128)(2,1)} fusion(bf16[512,4096]{1,0:T(8,128)(2,1)S(1)} %get-tuple-element.198, bf16[512,1024]{1,0:T(8,128)(2,1)} %fusion.22), kind=kOutput, calls=%fused_computation.12 | convolution fusion | flops 2149580800 | bytes 8912896 | tf_op jit(solution)/shard_map/dot_general | solution.py:69
  212.8 6.8 %multiply_reduce_fusion.1 = (f32[1024]{0:T(1024)}, f32[512]{0:T(512)S(1)}, f32[1024]{0:T(1024)}, f32[512,1024]{1,0:T(8,128)}) fusion(f32[512,1024]{1,0:T(8,128)S(1)} %copy-done.1, f32[512]{0:T(512)S(1)} %fusion.87, f32[512]{0:T(512)S(1)} %broadcast_multiply_fusion, f32[1024]{0:T(1024)S(1)} %bitcast.288, bf16[512,4096]{1,0:T(8,128)(2,1)S(1)} %get-tuple-element.198, ...), kind=kOutput, calls=%fused_computation.41 | convolution fusion | flops 4299159040 | bytes 16795648 | tf_op jit(solution)/shard_map/dot_general | solution.py:65
  219.6 2.4 fusion.96
  222.0 2.5 convolution_convert_fusion
  228.5 3.8 fusion.5
  237.1 2.7 convolution_convert_fusion.7.refs_5_
  241.6 3.2 fusion.16
  245.8 18.8 %attend_back.2 = bf16[512,1536]{1,0:T(8,128)(2,1)} custom-call(s32[512,1]{1,0:T(8,128)} %fusion.59.refs_0_, s32[1,512]{1,0:T(1,128)} %broadcast_select_fusion.2.refs_1_, bf16[512,3072]{1,0:T(8,128)(2,1)} %convolution_convert_fusion.4.refs_2_.refs_3_.refs_4_, bf16[512,3072]{1,0:T(8,128)(2,1)} %convolution_convert_fusion.4.refs_2_.refs_3_.refs_4_, ...), custom_call_target="tpu_custom_call" | custom-call | tf_op jit(solution)/shard_map/attend_back/pallas_call | solution.py:167
  266.5 4.7 %collective-permute-done.33 = bf16[1,4,128,1024]{3,2,1,0:T(8,128)(2,1)} collective-permute-done((bf16[1,4,128,1024]{3,2,1,0:T(8,128)(2,1)}, bf16[1,4,128,1024]{3,2,1,0:T(8,128)(2,1)}, u32[]{:S(2)}, u32[]{:S(2)}) %collective-permute-start.33) | collective-permute-done | bytes 1048608 | tf_op jit(solution)/shard_map/ppermute | solution.py:322
  272.1 3.1 fusion.46
  275.3 3.0 fusion.14
  278.3 2.1 fusion.26
  286.3 2.5 fusion.24
  288.8 18.9 %attend_back.3 = bf16[512,1536]{1,0:T(8,128)(2,1)} custom-call(s32[512,1]{1,0:T(8,128)} %fusion.59.refs_0_, s32[1,512]{1,0:T(1,128)} %broadcast_select_fusion.2.refs_1_, bf16[512,3072]{1,0:T(8,128)(2,1)} %convolution_convert_fusion.4.refs_2_.refs_3_.refs_4_, bf16[512,3072]{1,0:T(8,128)(2,1)} %convolution_convert_fusion.4.refs_2_.refs_3_.refs_4_, ...), custom_call_target="tpu_custom_call" | custom-call | tf_op jit(solution)/shard_map/attend_back/pallas_call | solution.py:167
  307.7 3.2 fusion.39
  315.9 3.7 convolution_convert_fusion.3
  325.7 6.5 %fusion.103 = f32[512,1024]{1,0:T(8,128)S(1)} fusion(bf16[512,3072]{1,0:T(8,128)(2,1)} %copy-done.6, bf16[1024,3072]{1,0:T(8,128)(2,1)} %get-tuple-element.173), kind=kOutput, calls=%fused_computation.303 | convolution fusion | flops 3221225472 | bytes 11534336 | tf_op jit(solution)/shard_map/dot_general | solution.py:65
  338.4 2.0 collective-permute-start.49
  340.4 3.2 fusion.10
  349.5 4.1 fusion.94
  354.8 2.1 fusion.104
  357.2 5.7 %collective-permute-done.50 = bf16[1,4,32,1024]{3,2,1,0:T(8,128)(2,1)S(1)} collective-permute-done((bf16[1,4,32,1024]{3,2,1,0:T(8,128)(2,1)S(1)}, bf16[1,4,32,1024]{3,2,1,0:T(8,128)(2,1)S(1)}, u32[]{:S(2)}, u32[]{:S(2)}) %collective-permute-start.50) | collective-permute-done | bytes 262176 | tf_op jit(solution)/shard_map/ppermute | solution.py:322
  362.9 4.5 collective-permute-done.45
  369.2 2.8 fusion.21
  380.3 9.0 %select_convert_fusion = bf16[512,1024]{1,0:T(8,128)(2,1)} fusion(f32[512,1024]{1,0:T(8,128)S(1)} %copy-done.2, bf16[512,4096]{1,0:T(8,128)(2,1)S(1)} %copy-done.13, bf16[4096,1024]{1,0:T(8,128)(2,1)} %assemble.5, pred[512]{0:T(512)(128)(4,1)S(1)} %copy-done.70), kind=kOutput, calls=%fused_computation.38 | convolution fusion | flops 4296540160 | bytes 15729152 | tf_op jit(solution)/shard_map/dot_general | solution.py:702
  391.0 2.9 collective-permute-start.57
  396.3 2.6 fusion.55
  398.9 2.2 pad_maximum_fusion.1.refs_0_
  405.4 3.8 finish.5
  409.3 2.0 collective-permute-start.65
  411.3 2.3 collective-permute-start.66
  415.1 3.1 collective-permute-done.72
  420.1 6.6 %collective-permute-done.66 = bf16[32,3072]{1,0:T(8,128)(2,1)S(1)} collective-permute-done((bf16[32,3072]{1,0:T(8,128)(2,1)}, bf16[32,3072]{1,0:T(8,128)(2,1)S(1)}, u32[]{:S(2)}, u32[]{:S(2)}) %collective-permute-start.66) | collective-permute-done | bytes 196640 | tf_op jit(solution)/shard_map/ppermute | solution.py:298
  435.9 2.3 collective-permute-done.60
  438.3 3.8 finish.4
  442.2 3.6 collective-permute-done.69
  446.2 5.6 %collective-permute-start.63 = (f32[64,256]{1,0:T(8,128)S(1)}, f32[64,256]{1,0:T(8,128)S(1)}, u32[]{:S(2)}, u32[]{:S(2)}) collective-permute-start(f32[64,256]{1,0:T(8,128)S(1)} %bitcast.284), channel_id=1, source_target_pairs={{0,3},{1,0},{2,1},{3,2},{4,7},{5,4},{6,5},{7,6},{8,11},{9,8},{10,9... | collective-permute-start | bytes 196616 | tf_op jit(solution)/shard_map/ppermute | solution.py:298
  453.2 2.1 finish.7
  455.3 3.0 collective-permute-done.62
  461.0 3.2 finish.6
  (411 shorter events, 129.2 us)
Async XLA Ops:
  6.6 13.1 %collective-permute-start = (bf16[32,4608]{1,0:T(8,128)(2,1)S(1)}, bf16[32,4608]{1,0:T(8,128)(2,1)S(1)}, u32[]{:S(2)}, u32[]{:S(2)}) collective-permute-start(bf16[32,4608]{1,0:T(8,128)(2,1)S(1)} %pad_maximum_fusion.3), channel_id=1, source_target_pairs={{0,1},{1,2},{2,3},{3,0},{4,5},{5,6},{6,7},{7,4},{8,9},{9,10},{10,1... | collective-permute-start | bytes 884744 | tf_op jit(solution)/shard_map/ppermute | solution.py:298
  9.7 21.8 %collective-permute-start.1 = (bf16[32,4608]{1,0:T(8,128)(2,1)S(1)}, bf16[32,4608]{1,0:T(8,128)(2,1)S(1)}, u32[]{:S(2)}, u32[]{:S(2)}) collective-permute-start(bf16[32,4608]{1,0:T(8,128)(2,1)S(1)} %pad_maximum_fusion.3), channel_id=1, source_target_pairs={{0,2},{1,3},{2,0},{3,1},{4,6},{5,7},{6,4},{7,5},{8,10},{9,11},{10,... | collective-permute-start | bytes 884744 | tf_op jit(solution)/shard_map/ppermute | solution.py:298
  12.3 19.2 %collective-permute-start.2 = (bf16[32,4608]{1,0:T(8,128)(2,1)S(1)}, bf16[32,4608]{1,0:T(8,128)(2,1)S(1)}, u32[]{:S(2)}, u32[]{:S(2)}) collective-permute-start(bf16[32,4608]{1,0:T(8,128)(2,1)S(1)} %pad_maximum_fusion.3), channel_id=1, source_target_pairs={{0,3},{1,0},{2,1},{3,2},{4,7},{5,4},{6,5},{7,6},{8,11},{9,8},{10,9... | collective-permute-start | bytes 884744 | tf_op jit(solution)/shard_map/ppermute | solution.py:298
  32.6 29.6 %collective-permute-start.3 = (bf16[1,3,32,4096]{3,2,1,0:T(8,128)(2,1)}, bf16[1,3,32,4096]{3,2,1,0:T(8,128)(2,1)}, u32[]{:S(2)}, u32[]{:S(2)}) collective-permute-start(bf16[1,3,32,4096]{3,2,1,0:T(8,128)(2,1)} %maximum_bitcast_fusion.refs_2_), channel_id=1, source_target_pairs={{0,16},{4,12},{8,24},{12,4},{16,0},{20,28},{24,8},{28,20},{1,17},{... | collective-permute-start | bytes 2359304 | tf_op jit(solution)/shard_map/ppermute | solution.py:473
  34.1 25.5 %collective-permute-start.4 = (bf16[1,3,32,4096]{3,2,1,0:T(8,128)(2,1)}, bf16[1,3,32,4096]{3,2,1,0:T(8,128)(2,1)}, u32[]{:S(2)}, u32[]{:S(2)}) collective-permute-start(bf16[1,3,32,4096]{3,2,1,0:T(8,128)(2,1)} %maximum_bitcast_fusion.refs_2_), channel_id=1, source_target_pairs={{0,8},{4,20},{8,0},{12,28},{16,24},{20,4},{24,16},{28,12},{1,9},{5... | collective-permute-start | bytes 2359304 | tf_op jit(solution)/shard_map/ppermute | solution.py:473
  35.6 15.1 %collective-permute-start.5 = (bf16[32,4096]{1,0:T(8,128)(2,1)S(1)}, bf16[32,4096]{1,0:T(8,128)(2,1)S(1)}, u32[]{:S(2)}, u32[]{:S(2)}) collective-permute-start(bf16[32,4096]{1,0:T(8,128)(2,1)S(1)} %constant_dynamic-slice_fusion.5), channel_id=1, source_target_pairs={{0,1},{1,2},{2,3},{3,0},{4,5},{5,6},{6,7},{7,4},{8,9},{9,10},{10,1... | collective-permute-start | bytes 786440 | tf_op jit(solution)/shard_map/ppermute | solution.py:298
  42.4 17.3 %collective-permute-start.6 = (bf16[32,4096]{1,0:T(8,128)(2,1)S(1)}, bf16[32,4096]{1,0:T(8,128)(2,1)S(1)}, u32[]{:S(2)}, u32[]{:S(2)}) collective-permute-start(bf16[32,4096]{1,0:T(8,128)(2,1)S(1)} %constant_dynamic-slice_fusion.5), channel_id=1, source_target_pairs={{0,2},{1,3},{2,0},{3,1},{4,6},{5,7},{6,4},{7,5},{8,10},{9,11},{10,... | collective-permute-start | bytes 786440 | tf_op jit(solution)/shard_map/ppermute | solution.py:298
  43.9 15.7 %collective-permute-start.7 = (bf16[32,4096]{1,0:T(8,128)(2,1)S(1)}, bf16[32,4096]{1,0:T(8,128)(2,1)S(1)}, u32[]{:S(2)}, u32[]{:S(2)}) collective-permute-start(bf16[32,4096]{1,0:T(8,128)(2,1)S(1)} %constant_dynamic-slice_fusion.5), channel_id=1, source_target_pairs={{0,3},{1,0},{2,1},{3,2},{4,7},{5,4},{6,5},{7,6},{8,11},{9,8},{10,9... | collective-permute-start | bytes 786440 | tf_op jit(solution)/shard_map/ppermute | solution.py:298
  50.6 23.1 %collective-permute-start.10 = (bf16[1,3,32,4096]{3,2,1,0:T(8,128)(2,1)}, bf16[1,3,32,4096]{3,2,1,0:T(8,128)(2,1)}, u32[]{:S(2)}, u32[]{:S(2)}) collective-permute-start(bf16[1,3,32,4096]{3,2,1,0:T(8,128)(2,1)} %maximum_bitcast_fusion.refs_2_), channel_id=1, source_target_pairs={{0,4},{4,0},{8,12},{12,8},{16,20},{20,16},{24,28},{28,24},{1,5},{5... | collective-permute-start | bytes 2359304 | tf_op jit(solution)/shard_map/ppermute | solution.py:294
  59.6 12.3 %collective-permute-start.8 = (bf16[1,3,32,4096]{3,2,1,0:T(8,128)(2,1)}, bf16[1,3,32,4096]{3,2,1,0:T(8,128)(2,1)S(1)}, u32[]{:S(2)}, u32[]{:S(2)}) collective-permute-start(bf16[1,3,32,4096]{3,2,1,0:T(8,128)(2,1)} %collective-permute-done.4.refs_3_), channel_id=1, source_target_pairs={{0,16},{4,12},{8,24},{12,4},{16,0},{20,28},{24,8},{28,20},{1,17},{... | collective-permute-start | bytes 2359304 | tf_op jit(solution)/shard_map/ppermute | solution.py:473
  62.0 12.3 %collective-permute-start.11 = (bf16[1,3,32,4096]{3,2,1,0:T(8,128)(2,1)}, bf16[1,3,32,4096]{3,2,1,0:T(8,128)(2,1)}, u32[]{:S(2)}, u32[]{:S(2)}) collective-permute-start(bf16[1,3,32,4096]{3,2,1,0:T(8,128)(2,1)} %collective-permute-done.4.refs_3_), channel_id=1, source_target_pairs={{0,4},{4,0},{8,12},{12,8},{16,20},{20,16},{24,28},{28,24},{1,5},{5... | collective-permute-start | bytes 2359304 | tf_op jit(solution)/shard_map/ppermute | solution.py:294
  73.2 19.9 %collective-permute-start.9 = (bf16[1,3,32,4096]{3,2,1,0:T(8,128)(2,1)S(1)}, bf16[1,3,32,4096]{3,2,1,0:T(8,128)(2,1)}, u32[]{:S(2)}, u32[]{:S(2)}) collective-permute-start(bf16[1,3,32,4096]{3,2,1,0:T(8,128)(2,1)S(1)} %maximum_bitcast_fusion.1.refs_1_), channel_id=1, source_target_pairs={{0,8},{4,20},{8,0},{12,28},{16,24},{20,4},{24,16},{28,12},{1,9},{5... | collective-permute-start | bytes 2359304 | tf_op jit(solution)/shard_map/ppermute | solution.py:473
  73.8 49.6 %collective-permute-start.17 = (bf16[1,3,32,4096]{3,2,1,0:T(8,128)(2,1)S(1)}, bf16[1,3,32,4096]{3,2,1,0:T(8,128)(2,1)}, u32[]{:S(2)}, u32[]{:S(2)}) collective-permute-start(bf16[1,3,32,4096]{3,2,1,0:T(8,128)(2,1)S(1)} %maximum_bitcast_fusion.1.refs_1_), channel_id=1, source_target_pairs={{0,16},{4,12},{8,24},{12,4},{16,0},{20,28},{24,8},{28,20},{1,17},{... | collective-permute-start | bytes 2359304 | tf_op jit(solution)/shard_map/ppermute | solution.py:473
  93.0 30.4 %collective-permute-start.18 = (bf16[1,3,32,4096]{3,2,1,0:T(8,128)(2,1)}, bf16[1,3,32,4096]{3,2,1,0:T(8,128)(2,1)}, u32[]{:S(2)}, u32[]{:S(2)}) collective-permute-start(bf16[1,3,32,4096]{3,2,1,0:T(8,128)(2,1)} %collective-permute-done.9.refs_2_), channel_id=1, source_target_pairs={{0,16},{4,12},{8,24},{12,4},{16,0},{20,28},{24,8},{28,20},{1,17},{... | collective-permute-start | bytes 2359304 | tf_op jit(solution)/shard_map/ppermute | solution.py:473
  94.7 29.2 %collective-permute-start.14 = (bf16[128,1024]{1,0:T(8,128)(2,1)S(1)}, bf16[128,1024]{1,0:T(8,128)(2,1)S(1)}, u32[]{:S(2)}, u32[]{:S(2)}) collective-permute-start(bf16[128,1024]{1,0:T(8,128)(2,1)S(1)} %copy-done.37), channel_id=1, source_target_pairs={{0,1},{1,2},{2,3},{3,0},{4,5},{5,6},{6,7},{7,4},{8,9},{9,10},{10,1... | collective-permute-start | bytes 786440 | tf_op jit(solution)/shard_map/ppermute | solution.py:298
  100.7 23.2 %collective-permute-start.15 = (bf16[128,1024]{1,0:T(8,128)(2,1)S(1)}, bf16[128,1024]{1,0:T(8,128)(2,1)}, u32[]{:S(2)}, u32[]{:S(2)}) collective-permute-start(bf16[128,1024]{1,0:T(8,128)(2,1)S(1)} %copy-done.37), channel_id=1, source_target_pairs={{0,2},{1,3},{2,0},{3,1},{4,6},{5,7},{6,4},{7,5},{8,10},{9,11},{10,... | collective-permute-start | bytes 786440 | tf_op jit(solution)/shard_map/ppermute | solution.py:298
  103.2 20.8 %collective-permute-start.16 = (bf16[128,1024]{1,0:T(8,128)(2,1)S(1)}, bf16[128,1024]{1,0:T(8,128)(2,1)}, u32[]{:S(2)}, u32[]{:S(2)}) collective-permute-start(bf16[128,1024]{1,0:T(8,128)(2,1)S(1)} %copy-done.37), channel_id=1, source_target_pairs={{0,3},{1,0},{2,1},{3,2},{4,7},{5,4},{6,5},{7,6},{8,11},{9,8},{10,9... | collective-permute-start | bytes 786440 | tf_op jit(solution)/shard_map/ppermute | solution.py:298
  123.3 16.0 %collective-permute-start.22 = (bf16[1,3,32,4096]{3,2,1,0:T(8,128)(2,1)S(1)}, bf16[1,3,32,4096]{3,2,1,0:T(8,128)(2,1)S(1)}, u32[]{:S(2)}, u32[]{:S(2)}) collective-permute-start(bf16[1,3,32,4096]{3,2,1,0:T(8,128)(2,1)S(1)} %maximum_bitcast_fusion.1.refs_1_), channel_id=1, source_target_pairs={{0,4},{4,0},{8,12},{12,8},{16,20},{20,16},{24,28},{28,24},{1,5},{5... | collective-permute-start | bytes 2359304 | tf_op jit(solution)/shard_map/ppermute | solution.py:294
  123.4 17.7 %collective-permute-start.23 = (bf16[1,3,32,4096]{3,2,1,0:T(8,128)(2,1)}, bf16[1,3,32,4096]{3,2,1,0:T(8,128)(2,1)}, u32[]{:S(2)}, u32[]{:S(2)}) collective-permute-start(bf16[1,3,32,4096]{3,2,1,0:T(8,128)(2,1)} %collective-permute-done.9.refs_2_), channel_id=1, source_target_pairs={{0,4},{4,0},{8,12},{12,8},{16,20},{20,16},{24,28},{28,24},{1,5},{5... | collective-permute-start | bytes 2359304 | tf_op jit(solution)/shard_map/ppermute | solution.py:294
  125.9 12.3 %collective-permute-start.19 = (bf16[1,3,128,1024]{3,2,1,0:T(8,128)(2,1)}, bf16[1,3,128,1024]{3,2,1,0:T(8,128)(2,1)}, u32[]{:S(2)}, u32[]{:S(2)}) collective-permute-start(bf16[1,3,128,1024]{3,2,1,0:T(8,128)(2,1)} %maximum_bitcast_fusion.2.refs_1_), channel_id=1, source_target_pairs={{0,8},{4,20},{8,0},{12,28},{16,24},{20,4},{24,16},{28,12},{1,9},{5... | collective-permute-start | bytes 2359304 | tf_op jit(solution)/shard_map/ppermute | solution.py:473
  126.5 14.7 %collective-permute-start.24 = (bf16[1,3,32,4096]{3,2,1,0:T(8,128)(2,1)}, bf16[1,3,32,4096]{3,2,1,0:T(8,128)(2,1)}, u32[]{:S(2)}, u32[]{:S(2)}) collective-permute-start(bf16[1,3,32,4096]{3,2,1,0:T(8,128)(2,1)} %collective-permute-done.17.refs_3_), channel_id=1, source_target_pairs={{0,4},{4,0},{8,12},{12,8},{16,20},{20,16},{24,28},{28,24},{1,5},{5... | collective-permute-start | bytes 2359304 | tf_op jit(solution)/shard_map/ppermute | solution.py:294
  126.8 14.3 %collective-permute-start.25 = (bf16[1,3,32,4096]{3,2,1,0:T(8,128)(2,1)}, bf16[1,3,32,4096]{3,2,1,0:T(8,128)(2,1)}, u32[]{:S(2)}, u32[]{:S(2)}) collective-permute-start(bf16[1,3,32,4096]{3,2,1,0:T(8,128)(2,1)} %collective-permute-done.18.refs_4_), channel_id=1, source_target_pairs={{0,4},{4,0},{8,12},{12,8},{16,20},{20,16},{24,28},{28,24},{1,5},{5... | collective-permute-start | bytes 2359304 | tf_op jit(solution)/shard_map/ppermute | solution.py:294
  138.2 21.0 %collective-permute-start.20 = (bf16[1,3,128,1024]{3,2,1,0:T(8,128)(2,1)}, bf16[1,3,128,1024]{3,2,1,0:T(8,128)(2,1)}, u32[]{:S(2)}, u32[]{:S(2)}) collective-permute-start(bf16[1,3,128,1024]{3,2,1,0:T(8,128)(2,1)} %maximum_bitcast_fusion.2.refs_1_), channel_id=1, source_target_pairs={{0,16},{4,12},{8,24},{12,4},{16,0},{20,28},{24,8},{28,20},{1,17},{... | collective-permute-start | bytes 2359304 | tf_op jit(solution)/shard_map/ppermute | solution.py:473
  140.2 19.0 %collective-permute-start.21 = (bf16[1,3,128,1024]{3,2,1,0:T(8,128)(2,1)}, bf16[1,3,128,1024]{3,2,1,0:T(8,128)(2,1)}, u32[]{:S(2)}, u32[]{:S(2)}) collective-permute-start(bf16[1,3,128,1024]{3,2,1,0:T(8,128)(2,1)} %collective-permute-done.19.refs_2_), channel_id=1, source_target_pairs={{0,16},{4,12},{8,24},{12,4},{16,0},{20,28},{24,8},{28,20},{1,17},{... | collective-permute-start | bytes 2359304 | tf_op jit(solution)/shard_map/ppermute | solution.py:473
  170.7 20.3 %collective-permute-start.30 = (bf16[4,4,128,1024]{3,2,1,0:T(8,128)(2,1)}, bf16[4,4,128,1024]{3,2,1,0:T(8,128)(2,1)}, u32[]{:S(2)}, u32[]{:S(2)}) collective-permute-start(bf16[4,4,128,1024]{3,2,1,0:T(8,128)(2,1)} %bitcast.24), channel_id=1, source_target_pairs={{0,4},{4,0},{8,12},{12,8},{16,20},{20,16},{24,28},{28,24},{1,5},{5... | collective-permute-start | bytes 12582920 | tf_op jit(solution)/shard_map/ppermute | solution.py:294
  170.9 9.8 %collective-permute-start.26 = (bf16[1,3,128,1024]{3,2,1,0:T(8,128)(2,1)}, bf16[1,3,128,1024]{3,2,1,0:T(8,128)(2,1)S(1)}, u32[]{:S(2)}, u32[]{:S(2)}) collective-permute-start(bf16[1,3,128,1024]{3,2,1,0:T(8,128)(2,1)} %maximum_bitcast_fusion.2.refs_1_), channel_id=1, source_target_pairs={{0,4},{4,0},{8,12},{12,8},{16,20},{20,16},{24,28},{28,24},{1,5},{5... | collective-permute-start | bytes 2359304 | tf_op jit(solution)/shard_map/ppermute | solution.py:294
  171.4 10.2 %collective-permute-start.27 = (bf16[1,3,128,1024]{3,2,1,0:T(8,128)(2,1)}, bf16[1,3,128,1024]{3,2,1,0:T(8,128)(2,1)S(1)}, u32[]{:S(2)}, u32[]{:S(2)}) collective-permute-start(bf16[1,3,128,1024]{3,2,1,0:T(8,128)(2,1)} %collective-permute-done.19.refs_2_), channel_id=1, source_target_pairs={{0,4},{4,0},{8,12},{12,8},{16,20},{20,16},{24,28},{28,24},{1,5},{5... | collective-permute-start | bytes 2359304 | tf_op jit(solution)/shard_map/ppermute | solution.py:294
  171.5 11.0 %collective-permute-start.28 = (bf16[1,3,128,1024]{3,2,1,0:T(8,128)(2,1)}, bf16[1,3,128,1024]{3,2,1,0:T(8,128)(2,1)S(1)}, u32[]{:S(2)}, u32[]{:S(2)}) collective-permute-start(bf16[1,3,128,1024]{3,2,1,0:T(8,128)(2,1)} %collective-permute-done.20.refs_3_), channel_id=1, source_target_pairs={{0,4},{4,0},{8,12},{12,8},{16,20},{20,16},{24,28},{28,24},{1,5},{5... | collective-permute-start | bytes 2359304 | tf_op jit(solution)/shard_map/ppermute | solution.py:294
  171.9 11.5 %collective-permute-start.29 = (bf16[1,3,128,1024]{3,2,1,0:T(8,128)(2,1)}, bf16[1,3,128,1024]{3,2,1,0:T(8,128)(2,1)}, u32[]{:S(2)}, u32[]{:S(2)}) collective-permute-start(bf16[1,3,128,1024]{3,2,1,0:T(8,128)(2,1)} %collective-permute-done.21.refs_4_), channel_id=1, source_target_pairs={{0,4},{4,0},{8,12},{12,8},{16,20},{20,16},{24,28},{28,24},{1,5},{5... | collective-permute-start | bytes 2359304 | tf_op jit(solution)/shard_map/ppermute | solution.py:294
  211.8 15.2 %collective-permute-start.31 = (bf16[4,4,32,4096]{3,2,1,0:T(8,128)(2,1)}, bf16[4,4,32,4096]{3,2,1,0:T(8,128)(2,1)}, u32[]{:S(2)}, u32[]{:S(2)}) collective-permute-start(bf16[4,4,32,4096]{3,2,1,0:T(8,128)(2,1)} %bitcast.26), channel_id=1, source_target_pairs={{0,4},{4,0},{8,12},{12,8},{16,20},{20,16},{24,28},{28,24},{1,5},{5... | collective-permute-start | bytes 12582920 | tf_op jit(solution)/shard_map/ppermute | solution.py:294
  212.3 27.6 %collective-permute-start.32 = (bf16[2,4,128,1024]{3,2,1,0:T(8,128)(2,1)S(1)}, bf16[2,4,128,1024]{3,2,1,0:T(8,128)(2,1)}, u32[]{:S(2)}, u32[]{:S(2)}) collective-permute-start(bf16[2,4,128,1024]{3,2,1,0:T(8,128)(2,1)S(1)} %fusion.6), channel_id=1, source_target_pairs={{0,8},{4,20},{8,0},{12,28},{16,24},{20,4},{24,16},{28,12},{1,9},{5... | collective-permute-start | bytes 6291464 | tf_op jit(solution)/shard_map/ppermute | solution.py:322
  232.3 39.8 %collective-permute-start.34 = (bf16[2,4,32,4096]{3,2,1,0:T(8,128)(2,1)}, bf16[2,4,32,4096]{3,2,1,0:T(8,128)(2,1)}, u32[]{:S(2)}, u32[]{:S(2)}) collective-permute-start(bf16[2,4,32,4096]{3,2,1,0:T(8,128)(2,1)} %fusion.5), channel_id=1, source_target_pairs={{0,8},{4,20},{8,0},{12,28},{16,24},{20,4},{24,16},{28,12},{1,9},{5... | collective-permute-start | bytes 6291464 | tf_op jit(solution)/shard_map/ppermute | solution.py:322
  244.8 26.3 %collective-permute-start.33 = (bf16[1,4,128,1024]{3,2,1,0:T(8,128)(2,1)}, bf16[1,4,128,1024]{3,2,1,0:T(8,128)(2,1)}, u32[]{:S(2)}, u32[]{:S(2)}) collective-permute-start(bf16[1,4,128,1024]{3,2,1,0:T(8,128)(2,1)} %fusion.16), channel_id=1, source_target_pairs={{0,16},{4,12},{8,24},{12,4},{16,0},{20,28},{24,8},{28,20},{1,17},{... | collective-permute-start | bytes 3145736 | tf_op jit(solution)/shard_map/ppermute | solution.py:322
  245.8 25.3 %collective-permute-start.35 = (bf16[4,4,32,1024]{3,2,1,0:T(8,128)(2,1)}, bf16[4,4,32,1024]{3,2,1,0:T(8,128)(2,1)}, u32[]{:S(2)}, u32[]{:S(2)}) collective-permute-start(bf16[4,4,32,1024]{3,2,1,0:T(8,128)(2,1)} %bitcast.29), channel_id=1, source_target_pairs={{0,4},{4,0},{8,12},{12,8},{16,20},{20,16},{24,28},{28,24},{1,5},{5... | collective-permute-start | bytes 3145736 | tf_op jit(solution)/shard_map/ppermute | solution.py:294
  280.4 27.3 %collective-permute-start.39 = (bf16[1,4,32,4096]{3,2,1,0:T(8,128)(2,1)}, bf16[1,4,32,4096]{3,2,1,0:T(8,128)(2,1)S(1)}, u32[]{:S(2)}, u32[]{:S(2)}) collective-permute-start(bf16[1,4,32,4096]{3,2,1,0:T(8,128)(2,1)} %fusion.14), channel_id=1, source_target_pairs={{0,16},{4,12},{8,24},{12,4},{16,0},{20,28},{24,8},{28,20},{1,17},{... | collective-permute-start | bytes 3145736 | tf_op jit(solution)/shard_map/ppermute | solution.py:322
  281.4 26.3 %collective-permute-start.40 = (bf16[2,4,32,1024]{3,2,1,0:T(8,128)(2,1)}, bf16[2,4,32,1024]{3,2,1,0:T(8,128)(2,1)}, u32[]{:S(2)}, u32[]{:S(2)}) collective-permute-start(bf16[2,4,32,1024]{3,2,1,0:T(8,128)(2,1)} %fusion.26), channel_id=1, source_target_pairs={{0,8},{4,20},{8,0},{12,28},{16,24},{20,4},{24,16},{28,12},{1,9},{5... | collective-permute-start | bytes 1572872 | tf_op jit(solution)/shard_map/ppermute | solution.py:322
  282.0 25.7 %collective-permute-start.36 = (bf16[128,1024]{1,0:T(8,128)(2,1)}, bf16[128,1024]{1,0:T(8,128)(2,1)}, u32[]{:S(2)}, u32[]{:S(2)}) collective-permute-start(bf16[128,1024]{1,0:T(8,128)(2,1)} %get-tuple-element.217), channel_id=1, source_target_pairs={{0,1},{1,2},{2,3},{3,0},{4,5},{5,6},{6,7},{7,4},{8,9},{9,10},{10,1... | collective-permute-start | bytes 786440 | tf_op jit(solution)/shard_map/ppermute | solution.py:298
  284.0 23.7 %collective-permute-start.37 = (bf16[128,1024]{1,0:T(8,128)(2,1)}, bf16[128,1024]{1,0:T(8,128)(2,1)}, u32[]{:S(2)}, u32[]{:S(2)}) collective-permute-start(bf16[128,1024]{1,0:T(8,128)(2,1)} %get-tuple-element.218), channel_id=1, source_target_pairs={{0,2},{1,3},{2,0},{3,1},{4,6},{5,7},{6,4},{7,5},{8,10},{9,11},{10,... | collective-permute-start | bytes 786440 | tf_op jit(solution)/shard_map/ppermute | solution.py:298
  284.5 23.2 %collective-permute-start.38 = (bf16[128,1024]{1,0:T(8,128)(2,1)}, bf16[128,1024]{1,0:T(8,128)(2,1)}, u32[]{:S(2)}, u32[]{:S(2)}) collective-permute-start(bf16[128,1024]{1,0:T(8,128)(2,1)} %get-tuple-element.219), channel_id=1, source_target_pairs={{0,3},{1,0},{2,1},{3,2},{4,7},{5,4},{6,5},{7,6},{8,11},{9,8},{10,9... | collective-permute-start | bytes 786440 | tf_op jit(solution)/shard_map/ppermute | solution.py:298
  319.6 20.8 %collective-permute-start.41 = (bf16[4,4,32,3072]{3,2,1,0:T(8,128)(2,1)}, bf16[4,4,32,3072]{3,2,1,0:T(8,128)(2,1)}, u32[]{:S(2)}, u32[]{:S(2)}) collective-permute-start(bf16[4,4,32,3072]{3,2,1,0:T(8,128)(2,1)} %bitcast.55), channel_id=1, source_target_pairs={{0,4},{4,0},{8,12},{12,8},{16,20},{20,16},{24,28},{28,24},{1,5},{5... | collective-permute-start | bytes 9437192 | tf_op jit(solution)/shard_map/ppermute | solution.py:294
  322.2 14.4 %collective-permute-start.42 = (bf16[1,128,1024]{2,1,0:T(8,128)(2,1)S(1)}, bf16[1,128,1024]{2,1,0:T(8,128)(2,1)S(1)}, u32[]{:S(2)}, u32[]{:S(2)}) collective-permute-start(bf16[1,128,1024]{2,1,0:T(8,128)(2,1)S(1)} %fusion.64), channel_id=1, source_target_pairs={{0,8},{4,20},{8,0},{12,28},{16,24},{20,4},{24,16},{28,12},{1,9},{5... | collective-permute-start | bytes 786440 | tf_op jit(solution)/shard_map/ppermute | solution.py:305
  323.8 14.7 %collective-permute-start.43 = (bf16[1,128,1024]{2,1,0:T(8,128)(2,1)S(1)}, bf16[1,128,1024]{2,1,0:T(8,128)(2,1)S(1)}, u32[]{:S(2)}, u32[]{:S(2)}) collective-permute-start(bf16[1,128,1024]{2,1,0:T(8,128)(2,1)S(1)} %fusion.64), channel_id=1, source_target_pairs={{0,16},{4,12},{8,24},{12,4},{16,0},{20,28},{24,8},{28,20},{1,17},{... | collective-permute-start | bytes 786440 | tf_op jit(solution)/shard_map/ppermute | solution.py:305
  324.7 15.7 %collective-permute-start.44 = (bf16[1,128,1024]{2,1,0:T(8,128)(2,1)S(1)}, bf16[1,128,1024]{2,1,0:T(8,128)(2,1)S(1)}, u32[]{:S(2)}, u32[]{:S(2)}) collective-permute-start(bf16[1,128,1024]{2,1,0:T(8,128)(2,1)S(1)} %fusion.64), channel_id=1, source_target_pairs={{0,24},{4,28},{8,16},{12,20},{16,8},{20,12},{24,0},{28,4},{1,25},{... | collective-permute-start | bytes 786440 | tf_op jit(solution)/shard_map/ppermute | solution.py:305
  335.8 17.8 %collective-permute-start.47 = (bf16[32,4096]{1,0:T(8,128)(2,1)}, bf16[32,4096]{1,0:T(8,128)(2,1)}, u32[]{:S(2)}, u32[]{:S(2)}) collective-permute-start(bf16[32,4096]{1,0:T(8,128)(2,1)} %get-tuple-element.243), channel_id=1, source_target_pairs={{0,1},{1,2},{2,3},{3,0},{4,5},{5,6},{6,7},{7,4},{8,9},{9,10},{10,1... | collective-permute-start | bytes 786440 | tf_op jit(solution)/shard_map/ppermute | solution.py:298
  336.6 20.6 %collective-permute-start.48 = (bf16[32,4096]{1,0:T(8,128)(2,1)}, bf16[32,4096]{1,0:T(8,128)(2,1)}, u32[]{:S(2)}, u32[]{:S(2)}) collective-permute-start(bf16[32,4096]{1,0:T(8,128)(2,1)} %get-tuple-element.244), channel_id=1, source_target_pairs={{0,2},{1,3},{2,0},{3,1},{4,6},{5,7},{6,4},{7,5},{8,10},{9,11},{10,... | collective-permute-start | bytes 786440 | tf_op jit(solution)/shard_map/ppermute | solution.py:298
  338.4 18.8 %collective-permute-start.49 = (bf16[32,4096]{1,0:T(8,128)(2,1)}, bf16[32,4096]{1,0:T(8,128)(2,1)}, u32[]{:S(2)}, u32[]{:S(2)}) collective-permute-start(bf16[32,4096]{1,0:T(8,128)(2,1)} %get-tuple-element.245), channel_id=1, source_target_pairs={{0,3},{1,0},{2,1},{3,2},{4,7},{5,4},{6,5},{7,6},{8,11},{9,8},{10,9... | collective-permute-start | bytes 786440 | tf_op jit(solution)/shard_map/ppermute | solution.py:298
  343.8 23.6 %collective-permute-start.45 = (bf16[2,4,32,3072]{3,2,1,0:T(8,128)(2,1)}, bf16[2,4,32,3072]{3,2,1,0:T(8,128)(2,1)}, u32[]{:S(2)}, u32[]{:S(2)}) collective-permute-start(bf16[2,4,32,3072]{3,2,1,0:T(8,128)(2,1)} %fusion.10), channel_id=1, source_target_pairs={{0,8},{4,20},{8,0},{12,28},{16,24},{20,4},{24,16},{28,12},{1,9},{5... | collective-permute-start | bytes 4718600 | tf_op jit(solution)/shard_map/ppermute | solution.py:322
  346.2 16.8 %collective-permute-start.46 = (bf16[4,128,1024]{2,1,0:T(8,128)(2,1)S(1)}, bf16[4,128,1024]{2,1,0:T(8,128)(2,1)}, u32[]{:S(2)}, u32[]{:S(2)}) collective-permute-start(bf16[4,128,1024]{2,1,0:T(8,128)(2,1)S(1)} %pad_maximum_fusion.refs_0_), channel_id=1, source_target_pairs={{0,4},{4,0},{8,12},{12,8},{16,20},{20,16},{24,28},{28,24},{1,5},{5... | collective-permute-start | bytes 3145736 | tf_op jit(solution)/shard_map/ppermute | solution.py:294
  374.5 21.8 %collective-permute-start.52 = (bf16[1,32,4096]{2,1,0:T(8,128)(2,1)S(1)}, bf16[1,32,4096]{2,1,0:T(8,128)(2,1)}, u32[]{:S(2)}, u32[]{:S(2)}) collective-permute-start(bf16[1,32,4096]{2,1,0:T(8,128)(2,1)S(1)} %fusion.65), channel_id=1, source_target_pairs={{0,8},{4,20},{8,0},{12,28},{16,24},{20,4},{24,16},{28,12},{1,9},{5... | collective-permute-start | bytes 786440 | tf_op jit(solution)/shard_map/ppermute | solution.py:305
  376.0 20.3 %collective-permute-start.53 = (bf16[1,32,4096]{2,1,0:T(8,128)(2,1)S(1)}, bf16[1,32,4096]{2,1,0:T(8,128)(2,1)}, u32[]{:S(2)}, u32[]{:S(2)}) collective-permute-start(bf16[1,32,4096]{2,1,0:T(8,128)(2,1)S(1)} %fusion.65), channel_id=1, source_target_pairs={{0,16},{4,12},{8,24},{12,4},{16,0},{20,28},{24,8},{28,20},{1,17},{... | collective-permute-start | bytes 786440 | tf_op jit(solution)/shard_map/ppermute | solution.py:305
  377.0 19.3 %collective-permute-start.54 = (bf16[1,32,4096]{2,1,0:T(8,128)(2,1)S(1)}, bf16[1,32,4096]{2,1,0:T(8,128)(2,1)}, u32[]{:S(2)}, u32[]{:S(2)}) collective-permute-start(bf16[1,32,4096]{2,1,0:T(8,128)(2,1)S(1)} %fusion.65), channel_id=1, source_target_pairs={{0,24},{4,28},{8,16},{12,20},{16,8},{20,12},{24,0},{28,4},{1,25},{... | collective-permute-start | bytes 786440 | tf_op jit(solution)/shard_map/ppermute | solution.py:305
  378.0 18.4 %collective-permute-start.51 = (bf16[1,4,32,3072]{3,2,1,0:T(8,128)(2,1)}, bf16[1,4,32,3072]{3,2,1,0:T(8,128)(2,1)}, u32[]{:S(2)}, u32[]{:S(2)}) collective-permute-start(bf16[1,4,32,3072]{3,2,1,0:T(8,128)(2,1)} %fusion.21), channel_id=1, source_target_pairs={{0,16},{4,12},{8,24},{12,4},{16,0},{20,28},{24,8},{28,20},{1,17},{... | collective-permute-start | bytes 2359304 | tf_op jit(solution)/shard_map/ppermute | solution.py:322
  379.7 11.2 %collective-permute-start.56 = (bf16[32,1024]{1,0:T(8,128)(2,1)}, bf16[32,1024]{1,0:T(8,128)(2,1)S(1)}, u32[]{:S(2)}, u32[]{:S(2)}) collective-permute-start(bf16[32,1024]{1,0:T(8,128)(2,1)} %get-tuple-element.259), channel_id=1, source_target_pairs={{0,2},{1,3},{2,0},{3,1},{4,6},{5,7},{6,4},{7,5},{8,10},{9,11},{10,... | collective-permute-start | bytes 196616 | tf_op jit(solution)/shard_map/ppermute | solution.py:298
  403.9 23.8 %collective-permute-start.59 = (f32[4,64,256]{2,0,1:T(4,128)S(1)}, f32[4,64,256]{2,0,1:T(4,128)}, u32[]{:S(2)}, u32[]{:S(2)}) collective-permute-start(f32[4,64,256]{2,0,1:T(4,128)S(1)} %pad_add_fusion.3), channel_id=1, source_target_pairs={{0,8},{4,12},{8,0},{12,4},{16,24},{20,28},{24,16},{28,20},{1,9},{5... | collective-permute-start | bytes 786440 | tf_op jit(solution)/shard_map/ppermute | solution.py:342
  409.3 9.9 %collective-permute-start.65 = (bf16[32,3072]{1,0:T(8,128)(2,1)}, bf16[32,3072]{1,0:T(8,128)(2,1)S(1)}, u32[]{:S(2)}, u32[]{:S(2)}) collective-permute-start(bf16[32,3072]{1,0:T(8,128)(2,1)} %get-tuple-element.274), channel_id=1, source_target_pairs={{0,1},{1,2},{2,3},{3,0},{4,5},{5,6},{6,7},{7,4},{8,9},{9,10},{10,1... | collective-permute-start | bytes 589832 | tf_op jit(solution)/shard_map/ppermute | solution.py:298
  411.3 15.4 %collective-permute-start.66 = (bf16[32,3072]{1,0:T(8,128)(2,1)}, bf16[32,3072]{1,0:T(8,128)(2,1)S(1)}, u32[]{:S(2)}, u32[]{:S(2)}) collective-permute-start(bf16[32,3072]{1,0:T(8,128)(2,1)} %get-tuple-element.275), channel_id=1, source_target_pairs={{0,2},{1,3},{2,0},{3,1},{4,6},{5,7},{6,4},{7,5},{8,10},{9,11},{10,... | collective-permute-start | bytes 589832 | tf_op jit(solution)/shard_map/ppermute | solution.py:298
  413.6 14.1 %collective-permute-start.67 = (bf16[32,3072]{1,0:T(8,128)(2,1)}, bf16[32,3072]{1,0:T(8,128)(2,1)S(1)}, u32[]{:S(2)}, u32[]{:S(2)}) collective-permute-start(bf16[32,3072]{1,0:T(8,128)(2,1)} %get-tuple-element.276), channel_id=1, source_target_pairs={{0,3},{1,0},{2,1},{3,2},{4,7},{5,4},{6,5},{7,6},{8,11},{9,8},{10,9... | collective-permute-start | bytes 589832 | tf_op jit(solution)/shard_map/ppermute | solution.py:298
  418.2 20.1 %collective-permute-start.64 = (bf16[4,32,4096]{2,1,0:T(8,128)(2,1)}, bf16[4,32,4096]{2,1,0:T(8,128)(2,1)}, u32[]{:S(2)}, u32[]{:S(2)}) collective-permute-start(bf16[4,32,4096]{2,1,0:T(8,128)(2,1)} %pad_maximum_fusion.1.refs_0_), channel_id=1, source_target_pairs={{0,4},{4,0},{8,12},{12,8},{16,20},{20,16},{24,28},{28,24},{1,5},{5... | collective-permute-start | bytes 3145736 | tf_op jit(solution)/shard_map/ppermute | solution.py:294
  419.1 13.5 %collective-permute-start.73 = (bf16[1,32,1024]{2,1,0:T(8,128)(2,1)S(1)}, bf16[1,32,1024]{2,1,0:T(8,128)(2,1)S(1)}, u32[]{:S(2)}, u32[]{:S(2)}) collective-permute-start(bf16[1,32,1024]{2,1,0:T(8,128)(2,1)S(1)} %fusion.77), channel_id=1, source_target_pairs={{0,16},{4,12},{8,24},{12,4},{16,0},{20,28},{24,8},{28,20},{1,17},{... | collective-permute-start | bytes 196616 | tf_op jit(solution)/shard_map/ppermute | solution.py:305
  431.1 11.1 %collective-permute-start.68 = (bf16[1,32,3072]{2,1,0:T(8,128)(2,1)S(1)}, bf16[1,32,3072]{2,1,0:T(8,128)(2,1)S(1)}, u32[]{:S(2)}, u32[]{:S(2)}) collective-permute-start(bf16[1,32,3072]{2,1,0:T(8,128)(2,1)S(1)} %fusion.68), channel_id=1, source_target_pairs={{0,8},{4,20},{8,0},{12,28},{16,24},{20,4},{24,16},{28,12},{1,9},{5... | collective-permute-start | bytes 589832 | tf_op jit(solution)/shard_map/ppermute | solution.py:305
  432.7 13.1 %collective-permute-start.69 = (bf16[1,32,3072]{2,1,0:T(8,128)(2,1)S(1)}, bf16[1,32,3072]{2,1,0:T(8,128)(2,1)S(1)}, u32[]{:S(2)}, u32[]{:S(2)}) collective-permute-start(bf16[1,32,3072]{2,1,0:T(8,128)(2,1)S(1)} %fusion.68), channel_id=1, source_target_pairs={{0,16},{4,12},{8,24},{12,4},{16,0},{20,28},{24,8},{28,20},{1,17},{... | collective-permute-start | bytes 589832 | tf_op jit(solution)/shard_map/ppermute | solution.py:305
  433.7 12.1 %collective-permute-start.70 = (bf16[1,32,3072]{2,1,0:T(8,128)(2,1)S(1)}, bf16[1,32,3072]{2,1,0:T(8,128)(2,1)S(1)}, u32[]{:S(2)}, u32[]{:S(2)}) collective-permute-start(bf16[1,32,3072]{2,1,0:T(8,128)(2,1)S(1)} %fusion.68), channel_id=1, source_target_pairs={{0,24},{4,28},{8,16},{12,20},{16,8},{20,12},{24,0},{28,4},{1,25},{... | collective-permute-start | bytes 589832 | tf_op jit(solution)/shard_map/ppermute | solution.py:305
  438.2 14.2 %collective-permute-start.75 = (bf16[4,32,1024]{2,1,0:T(8,128)(2,1)}, bf16[4,32,1024]{2,1,0:T(8,128)(2,1)S(1)}, u32[]{:S(2)}, u32[]{:S(2)}) collective-permute-start(bf16[4,32,1024]{2,1,0:T(8,128)(2,1)} %constant_dynamic-update-slice_fusion.refs_0_), channel_id=1, source_target_pairs={{0,4},{4,0},{8,12},{12,8},{16,20},{20,16},{24,28},{28,24},{1,5},{5... | collective-permute-start | bytes 786440 | tf_op jit(solution)/shard_map/ppermute | solution.py:294
  445.9 14.3 %collective-permute-start.71 = (bf16[4,32,3072]{2,1,0:T(8,128)(2,1)S(1)}, bf16[4,32,3072]{2,1,0:T(8,128)(2,1)S(1)}, u32[]{:S(2)}, u32[]{:S(2)}) collective-permute-start(bf16[4,32,3072]{2,1,0:T(8,128)(2,1)S(1)} %pad_maximum_fusion.2.refs_0_), channel_id=1, source_target_pairs={{0,4},{4,0},{8,12},{12,8},{16,20},{20,16},{24,28},{28,24},{1,5},{5... | collective-permute-start | bytes 2359304 | tf_op jit(solution)/shard_map/ppermute | solution.py:294
  (95 other events, 1375.2 us)
